TPU v7x, 32 devices: a whole 2x2x4 slice. The times are simulated.
32 devices in a mesh: clip: 4 (over x, core), seq: 4 (over z), head: 2 (over y).
Axes of the slice: x: 2, y: 2, z: 4, core: 2. Of those that a mesh axis runs over, the one named last changes fastest.
Arguments:
- tokens: bfloat16 [8, 8, 196, 768], P(('clip', 'head'), 'seq'), may hold values from -6 to 6
- cotangent: bfloat16 [8, 8, 196, 768], P(('clip', 'head'), 'seq'), may hold values from -6 to 6
- time_qkv: bfloat16 [2, 768, 3, 768], P(None, ('clip', 'seq'), None, 'head'), may hold values from -0.21875 to 0.21875
- time_out: bfloat16 [2, 768, 768], P(None, 'head', ('clip', 'seq')), may hold values from -0.4375 to 0.4375
- time_mix: bfloat16 [2, 768, 768], P(None, ('clip', 'seq', 'head')), may hold values from -0.21875 to 0.21875
- space_qkv: bfloat16 [2, 768, 3, 768], P(None, ('clip', 'seq'), None, 'head'), may hold values from -0.21875 to 0.21875
- space_out: bfloat16 [2, 768, 768], P(None, 'head', ('clip', 'seq')), may hold values from -1 to 1
- mlp_in: bfloat16 [2, 768, 3072], P(None, ('clip', 'seq'), 'head'), may hold values from -0.21875 to 0.21875
- mlp_out: bfloat16 [2, 3072, 768], P(None, 'head', ('clip', 'seq')), may hold values from -0.21875 to 0.21875
- norm_gain: float32 [2, 3, 768], P(None, None, ('clip', 'seq', 'head')), may hold values from 0.25 to 1.75
- norm_bias: float32 [2, 3, 768], P(None, None, ('clip', 'seq', 'head')), may hold values from -3 to 3
Outputs:
- output: bfloat16 [8, 8, 196, 768], P(('clip', 'head'), 'seq')
- tokens_grad: float32 [8, 8, 196, 768], P(('clip', 'head'), 'seq')
- time_qkv_grad: float32 [2, 768, 3, 768], P(None, ('clip', 'seq'), None, 'head')
- time_out_grad: float32 [2, 768, 768], P(None, 'head', ('clip', 'seq'))
- time_mix_grad: float32 [2, 768, 768], P(None, ('clip', 'seq', 'head'))
- space_qkv_grad: float32 [2, 768, 3, 768], P(None, ('clip', 'seq'), None, 'head')
- space_out_grad: float32 [2, 768, 768], P(None, 'head', ('clip', 'seq'))
- mlp_in_grad: float32 [2, 768, 3072], P(None, ('clip', 'seq'), 'head')
- mlp_out_grad: float32 [2, 3072, 768], P(None, 'head', ('clip', 'seq'))
- norm_gain_grad: float32 [2, 3, 768], P(None, None, ('clip', 'seq', 'head'))
- norm_bias_grad: float32 [2, 3, 768], P(None, None, ('clip', 'seq', 'head'))
All inputs are finite; a program needn't handle non-finite values.
Results may differ from a plain program's by a relative error of at most 0.024.
Values may be sent and summed in bfloat16 or wider, within the bound.
No kernel may reach another device: no remote copies, remote signals or barrier semaphores. Data moves between devices by JAX's collectives and lax.ppermute only.
A program may use at most 256 MiB of HBM per device.

v0:
```python
import math

import jax
import jax.numpy as jnp
from jax import lax
from jax.sharding import PartitionSpec as P

HEAD_DIM = 64


norm_eps = 1e-06
half_root = 0.7071067811865476
inv_root_tau = 0.3989422804014327
time_forms = ("cfphe,cgphe->cphfg", "cphfg,cgphe->cfphe", "cphfg,cfphe->cgphe")
space_forms = ("cfphe,cfqhe->cfhpq", "cfhpq,cfqhe->cfphe", "cfhpq,cfphe->cfqhe")


def matmul(form, left, right):
    return jnp.einsum(form, left, right, preferred_element_type=jnp.float32)


def norm_forward(values, gain_row, bias_row):
    centred = values - jnp.mean(values, axis=-1, keepdims=True)
    inverse_spread = lax.rsqrt(jnp.mean(centred * centred, axis=-1, keepdims=True) + norm_eps)
    normed = centred * inverse_spread
    return (normed * gain_row + bias_row, normed, inverse_spread)


def norm_backward(upstream, normed, inverse_spread, gain_row):
    scaled = upstream * gain_row
    mean_scaled = jnp.mean(scaled, axis=-1, keepdims=True)
    mean_cross = jnp.mean(scaled * normed, axis=-1, keepdims=True)
    lead_axes = tuple(range(upstream.ndim - 1))
    change = inverse_spread * (scaled - mean_scaled - normed * mean_cross)
    return (change, jnp.sum(upstream * normed, axis=lead_axes), jnp.sum(upstream, axis=lead_axes))


def gelu_value(hidden):
    return 0.5 * hidden * (1.0 + lax.erf(hidden * half_root))


def gelu_slope(hidden):
    return (
        0.5 * (1.0 + lax.erf(hidden * half_root))
        + hidden * jnp.exp(-0.5 * hidden * hidden) * inv_root_tau
    )


def attend(packed, forms, scale):
    queries = packed[:, :, :, 0]
    key_rows = packed[:, :, :, 1]
    value_rows = packed[:, :, :, 2]
    scores = matmul(forms[0], queries, key_rows) * scale
    row_peak = jnp.max(scores, axis=-1, keepdims=True)
    exponent = jnp.exp(scores - row_peak)
    row_total = jnp.sum(exponent, axis=-1, keepdims=True)
    weights_soft = (exponent / row_total).astype(jnp.bfloat16)
    mixed = matmul(forms[1], weights_soft, value_rows).astype(jnp.bfloat16)
    return (mixed, row_peak + jnp.log(row_total))


def attend_back(packed, grad_mixed, log_total, forms, scale):
    queries = packed[:, :, :, 0]
    key_rows = packed[:, :, :, 1]
    value_rows = packed[:, :, :, 2]
    weights_soft = jnp.exp(matmul(forms[0], queries, key_rows) * scale - log_total)
    grad_values = matmul(forms[2], weights_soft.astype(jnp.bfloat16), grad_mixed)
    grad_weights = matmul(forms[0], grad_mixed, value_rows)
    grad_scores = (
        weights_soft * (grad_weights - jnp.sum(weights_soft * grad_weights, axis=-1, keepdims=True))
    ).astype(jnp.bfloat16)
    grad_queries = matmul(forms[1], grad_scores, key_rows) * scale
    grad_keys = matmul(forms[2], grad_scores, queries) * scale
    return jnp.stack((grad_queries, grad_keys, grad_values), axis=3).astype(jnp.bfloat16)


def with_heads(values, head_count):
    return values.reshape(values.shape[:3] + (head_count, HEAD_DIM))


def forward_layer(residual, split_set, whole_set, scale):
    time_qkv, time_out, space_qkv, space_out, mlp_in, mlp_out = split_set
    time_mix, gains, biases = whole_set
    width_local = time_out.shape[0]
    head_count = width_local // HEAD_DIM
    normed_one, hat_one, spread_one = norm_forward(residual, gains[0], biases[0])
    place_rows = lax.all_to_all(
        normed_one.astype(jnp.bfloat16), "seq", split_axis=2, concat_axis=1, tiled=True
    )
    packed_one = matmul("cfpd,dge->cfpge", place_rows, time_qkv).astype(jnp.bfloat16)
    packed_one = packed_one.reshape(packed_one.shape[:4] + (head_count, HEAD_DIM))
    mixed_one, total_one = attend(packed_one, time_forms, scale)
    mixed_one = mixed_one.reshape(mixed_one.shape[:3] + (width_local,))
    frame_mixed = lax.all_to_all(mixed_one, "seq", split_axis=1, concat_axis=2, tiled=True)
    summed_one = matmul("cfpe,ed->cfpd", frame_mixed, time_out).astype(jnp.bfloat16)
    residual = residual + matmul("cfpk,kd->cfpd", summed_one, time_mix)
    normed_two, hat_two, spread_two = norm_forward(residual, gains[1], biases[1])
    frame_rows = normed_two.astype(jnp.bfloat16)
    packed_two = matmul("cfpd,dge->cfpge", frame_rows, space_qkv).astype(jnp.bfloat16)
    packed_two = packed_two.reshape(packed_two.shape[:4] + (head_count, HEAD_DIM))
    mixed_two, total_two = attend(packed_two, space_forms, scale)
    flat_two = mixed_two.reshape(mixed_two.shape[:3] + (width_local,))
    residual = residual + matmul("cfpe,ed->cfpd", flat_two, space_out)
    normed_three, hat_three, spread_three = norm_forward(residual, gains[2], biases[2])
    mlp_rows = normed_three.astype(jnp.bfloat16)
    hidden = matmul("cfpd,du->cfpu", mlp_rows, mlp_in)
    activated = gelu_value(hidden).astype(jnp.bfloat16)
    residual = residual + matmul("cfpu,ud->cfpd", activated, mlp_out)
    stored = (
        hat_one,
        spread_one,
        place_rows,
        packed_one,
        total_one,
        frame_mixed,
        summed_one,
        hat_two,
        spread_two,
        frame_rows,
        packed_two,
        total_two,
        flat_two,
        hat_three,
        spread_three,
        mlp_rows,
        hidden,
        activated,
    )
    return (residual, stored)


def backward_layer(gradient, stored, split_set, whole_set, scale):
    time_qkv, time_out, space_qkv, space_out, mlp_in, mlp_out = split_set
    time_mix, gains, biases = whole_set
    (
        hat_one,
        spread_one,
        place_rows,
        packed_one,
        total_one,
        frame_mixed,
        summed_one,
        hat_two,
        spread_two,
        frame_rows,
        packed_two,
        total_two,
        flat_two,
        hat_three,
        spread_three,
        mlp_rows,
        hidden,
        activated,
    ) = stored
    width_local = time_out.shape[0]
    head_count = width_local // HEAD_DIM
    grad_mlp = gradient.astype(jnp.bfloat16)
    grad_mlp_out = matmul("cfpu,cfpd->ud", activated, grad_mlp)
    grad_hidden = (matmul("cfpd,ud->cfpu", grad_mlp, mlp_out) * gelu_slope(hidden)).astype(
        jnp.bfloat16
    )
    grad_mlp_in = matmul("cfpd,cfpu->du", mlp_rows, grad_hidden)
    change, gain_three, bias_three = norm_backward(
        matmul("cfpu,du->cfpd", grad_hidden, mlp_in), hat_three, spread_three, gains[2]
    )
    gradient = gradient + change
    grad_space = gradient.astype(jnp.bfloat16)
    grad_space_out = matmul("cfpe,cfpd->ed", flat_two, grad_space)
    grad_mixed_two = with_heads(
        matmul("cfpd,ed->cfpe", grad_space, space_out).astype(jnp.bfloat16), head_count
    )
    grad_packed_two = attend_back(packed_two, grad_mixed_two, total_two, space_forms, scale)
    grad_packed_two = grad_packed_two.reshape(grad_packed_two.shape[:4] + (width_local,))
    grad_space_qkv = matmul("cfpd,cfpge->dge", frame_rows, grad_packed_two)
    change, gain_two, bias_two = norm_backward(
        matmul("cfpge,dge->cfpd", grad_packed_two, space_qkv), hat_two, spread_two, gains[1]
    )
    gradient = gradient + change
    grad_time = gradient.astype(jnp.bfloat16)
    grad_time_mix = matmul("cfpk,cfpd->kd", summed_one, grad_time)
    grad_summed = matmul("cfpd,kd->cfpk", grad_time, time_mix).astype(jnp.bfloat16)
    grad_time_out = matmul("cfpe,cfpd->ed", frame_mixed, grad_summed)
    grad_frame_mixed = matmul("cfpd,ed->cfpe", grad_summed, time_out).astype(jnp.bfloat16)
    grad_place_mixed = lax.all_to_all(
        grad_frame_mixed, "seq", split_axis=2, concat_axis=1, tiled=True
    )
    grad_packed_one = attend_back(
        packed_one, with_heads(grad_place_mixed, head_count), total_one, time_forms, scale
    )
    grad_packed_one = grad_packed_one.reshape(grad_packed_one.shape[:4] + (width_local,))
    grad_time_qkv = matmul("cfpd,cfpge->dge", place_rows, grad_packed_one)
    place_grad = matmul("cfpge,dge->cfpd", grad_packed_one, time_qkv)
    frame_grad = lax.all_to_all(
        place_grad.astype(jnp.bfloat16), "seq", split_axis=1, concat_axis=2, tiled=True
    ).astype(place_grad.dtype)
    change, gain_one, bias_one = norm_backward(frame_grad, hat_one, spread_one, gains[0])
    gradient = gradient + change
    split_grads = (
        grad_time_qkv,
        grad_time_out,
        grad_space_qkv,
        grad_space_out,
        grad_mlp_in,
        grad_mlp_out,
    )
    whole_grads = (
        grad_time_mix,
        jnp.stack((gain_one, gain_two, gain_three)),
        jnp.stack((bias_one, bias_two, bias_three)),
    )
    return (gradient, split_grads, whole_grads)


def on_device(
    tokens,
    cotangent,
    time_qkv,
    time_out,
    time_mix,
    space_qkv,
    space_out,
    mlp_in,
    mlp_out,
    norm_gain,
    norm_bias,
):
    scale = 1.0 / math.sqrt(HEAD_DIM)
    layer_count = time_qkv.shape[0]
    full_gain, full_bias = (
        lax.all_gather(norm_gain, ("clip", "seq", "head"), axis=2, tiled=True),
        lax.all_gather(norm_bias, ("clip", "seq", "head"), axis=2, tiled=True),
    )
    residual = tokens.astype(jnp.float32)
    saved_split = []
    saved_whole = []
    saved_state = []
    for layer_index in range(layer_count):
        split_set = (
            lax.all_gather(
                lax.all_gather(time_qkv[layer_index], ("clip", "seq"), axis=0, tiled=True),
                "head",
                axis=2,
                tiled=True,
            ),
            lax.all_gather(
                lax.all_gather(time_out[layer_index], ("clip", "seq"), axis=1, tiled=True),
                "head",
                axis=0,
                tiled=True,
            ),
            lax.all_gather(
                lax.all_gather(space_qkv[layer_index], ("clip", "seq"), axis=0, tiled=True),
                "head",
                axis=2,
                tiled=True,
            ),
            lax.all_gather(
                lax.all_gather(space_out[layer_index], ("clip", "seq"), axis=1, tiled=True),
                "head",
                axis=0,
                tiled=True,
            ),
            lax.all_gather(
                lax.all_gather(mlp_in[layer_index], ("clip", "seq"), axis=0, tiled=True),
                "head",
                axis=1,
                tiled=True,
            ),
            lax.all_gather(
                lax.all_gather(mlp_out[layer_index], ("clip", "seq"), axis=1, tiled=True),
                "head",
                axis=0,
                tiled=True,
            ),
        )
        fetch_mix_full = lax.all_gather(
            time_mix[layer_index], ("clip", "seq", "head"), axis=0, tiled=True
        )
        whole_set = (fetch_mix_full, full_gain[layer_index], full_bias[layer_index])
        residual, stored = forward_layer(residual, split_set, whole_set, scale)
        saved_split.append(split_set)
        saved_whole.append(whole_set)
        saved_state.append(stored)
    output = residual.astype(jnp.bfloat16)
    gradient = cotangent.astype(jnp.float32)
    split_results = [None] * layer_count
    whole_results = [None] * layer_count
    for layer_index in reversed(range(layer_count)):
        split_set = (
            lax.all_gather(
                lax.all_gather(time_qkv[layer_index], ("clip", "seq"), axis=0, tiled=True),
                "head",
                axis=2,
                tiled=True,
            ),
            lax.all_gather(
                lax.all_gather(time_out[layer_index], ("clip", "seq"), axis=1, tiled=True),
                "head",
                axis=0,
                tiled=True,
            ),
            lax.all_gather(
                lax.all_gather(space_qkv[layer_index], ("clip", "seq"), axis=0, tiled=True),
                "head",
                axis=2,
                tiled=True,
            ),
            lax.all_gather(
                lax.all_gather(space_out[layer_index], ("clip", "seq"), axis=1, tiled=True),
                "head",
                axis=0,
                tiled=True,
            ),
            lax.all_gather(
                lax.all_gather(mlp_in[layer_index], ("clip", "seq"), axis=0, tiled=True),
                "head",
                axis=1,
                tiled=True,
            ),
            lax.all_gather(
                lax.all_gather(mlp_out[layer_index], ("clip", "seq"), axis=1, tiled=True),
                "head",
                axis=0,
                tiled=True,
            ),
        )
        mix_full = lax.all_gather(
            time_mix[layer_index], ("clip", "seq", "head"), axis=0, tiled=True
        )
        whole_set = (mix_full, full_gain[layer_index], full_bias[layer_index])
        gradient, split_grads, whole_grads = backward_layer(
            gradient, saved_state[layer_index], split_set, whole_set, scale
        )
        head_sums = (
            lax.psum_scatter(
                split_grads[0].astype(jnp.bfloat16), "head", scatter_dimension=2, tiled=True
            ).astype(jnp.float32),
            lax.psum_scatter(
                split_grads[1].astype(jnp.bfloat16), "head", scatter_dimension=0, tiled=True
            ).astype(jnp.float32),
            lax.psum_scatter(
                split_grads[2].astype(jnp.bfloat16), "head", scatter_dimension=2, tiled=True
            ).astype(jnp.float32),
            lax.psum_scatter(
                split_grads[3].astype(jnp.bfloat16), "head", scatter_dimension=0, tiled=True
            ).astype(jnp.float32),
            lax.psum_scatter(
                split_grads[4].astype(jnp.bfloat16), "head", scatter_dimension=1, tiled=True
            ).astype(jnp.float32),
            lax.psum_scatter(
                split_grads[5].astype(jnp.bfloat16), "head", scatter_dimension=0, tiled=True
            ).astype(jnp.float32),
        )
        split_results[layer_index] = (
            lax.psum_scatter(head_sums[0], ("clip", "seq"), scatter_dimension=0, tiled=True),
            lax.psum_scatter(head_sums[1], ("clip", "seq"), scatter_dimension=1, tiled=True),
            lax.psum_scatter(head_sums[2], ("clip", "seq"), scatter_dimension=0, tiled=True),
            lax.psum_scatter(head_sums[3], ("clip", "seq"), scatter_dimension=1, tiled=True),
            lax.psum_scatter(head_sums[4], ("clip", "seq"), scatter_dimension=0, tiled=True),
            lax.psum_scatter(head_sums[5], ("clip", "seq"), scatter_dimension=1, tiled=True),
        )
        whole_results[layer_index] = (
            lax.psum_scatter(
                whole_grads[0], ("clip", "seq", "head"), scatter_dimension=0, tiled=True
            ),
            lax.psum_scatter(
                whole_grads[1], ("clip", "seq", "head"), scatter_dimension=1, tiled=True
            ),
            lax.psum_scatter(
                whole_grads[2], ("clip", "seq", "head"), scatter_dimension=1, tiled=True
            ),
        )

    def stack_layers(results, member):
        return jnp.stack([result[member] for result in results])

    return (
        output,
        gradient,
        stack_layers(split_results, 0),
        stack_layers(split_results, 1),
        stack_layers(whole_results, 0),
        stack_layers(split_results, 2),
        stack_layers(split_results, 3),
        stack_layers(split_results, 4),
        stack_layers(split_results, 5),
        stack_layers(whole_results, 1),
        stack_layers(whole_results, 2),
    )


def solution(mesh):
    in_specs = (
        P(("clip", "head"), "seq", None, None),
        P(("clip", "head"), "seq", None, None),
        P(None, ("clip", "seq"), None, "head"),
        P(None, "head", ("clip", "seq")),
        P(None, ("clip", "seq", "head"), None),
        P(None, ("clip", "seq"), None, "head"),
        P(None, "head", ("clip", "seq")),
        P(None, ("clip", "seq"), "head"),
        P(None, "head", ("clip", "seq")),
        P(None, None, ("clip", "seq", "head")),
        P(None, None, ("clip", "seq", "head")),
    )
    out_specs = (
        P(("clip", "head"), "seq", None, None),
        P(("clip", "head"), "seq", None, None),
        P(None, ("clip", "seq"), None, "head"),
        P(None, "head", ("clip", "seq")),
        P(None, ("clip", "seq", "head"), None),
        P(None, ("clip", "seq"), None, "head"),
        P(None, "head", ("clip", "seq")),
        P(None, ("clip", "seq"), "head"),
        P(None, "head", ("clip", "seq")),
        P(None, None, ("clip", "seq", "head")),
        P(None, None, ("clip", "seq", "head")),
    )
    return jax.shard_map(
        on_device, mesh=mesh, in_specs=in_specs, out_specs=out_specs, check_vma=False
    )
```

profile of v0, /device:TPU:0, one launch (start us, length us, event | category | flops | bytes accessed | tf_op | source)
XLA Modules:
  0.0 2757.3 jit_solution(5865487013776124863)
XLA Ops:
  14.5 39.4 %all-gather.49.cloned.1.call-done = bf16[1,768,3,384]{3,1,2,0:T(8,128)(2,1)} async-done(((bf16[1,48,3,384]{3,1,2,0:T(8,128)(2,1)}), bf16[1,768,3,384]{3,1,2,0:T(8,128)(2,1)}) %all-gather.49.cloned.1.call-update) | async-done | bytes 1769488 | tf_op jit(solution)/shard_map/all_gather | solution.py:240
  97.5 39.3 %all-gather.7 = bf16[1,384,768]{1,2,0:T(8,128)(2,1)S(1)} all-gather(bf16[1,384,48]{1,2,0:T(8,128)(2,1)S(1)} %get-tuple-element.106), channel_id=9, replica_groups=mesh['clip'=4,'seq'=4,'head'=2] {'clip','seq'}, dimensions={2}, use_global_device_ids=true | all-gather | bytes 626688 | tf_op jit(solution)/shard_map/all_gather | solution.py:258
  143.0 43.6 %all-gather.67.cloned.1.call-done = bf16[1,1536,768]{1,2,0:T(8,128)(2,1)} async-done(((bf16[1,1536,48]{1,2,0:T(8,128)(2,1)}), bf16[1,1536,768]{1,2,0:T(8,128)(2,1)}) %all-gather.67.cloned.1.call-update) | async-done | bytes 2359312 | tf_op jit(solution)/shard_map/all_gather | solution.py:270
  191.1 37.4 %all-gather.71.cloned.1.call-done = bf16[1,768,3,384]{3,1,2,0:T(8,128)(2,1)} async-done(((bf16[1,48,3,384]{3,1,2,0:T(8,128)(2,1)}), bf16[1,768,3,384]{3,1,2,0:T(8,128)(2,1)}) %all-gather.71.cloned.1.call-update) | async-done | bytes 1769488 | tf_op jit(solution)/shard_map/all_gather | solution.py:240
  229.1 37.4 %all-gather.15 = bf16[1,384,768]{1,2,0:T(8,128)(2,1)S(1)} all-gather(bf16[1,384,48]{1,2,0:T(8,128)(2,1)S(1)} %get-tuple-element.109), channel_id=17, replica_groups=mesh['clip'=4,'seq'=4,'head'=2] {'clip','seq'}, dimensions={2}, use_global_device_ids=true | all-gather | bytes 626688 | tf_op jit(solution)/shard_map/all_gather | solution.py:246
  271.6 72.0 %all_gather.111 = f32[2,3,768]{1,0,2:T(2,128)S(1)} all-gather(f32[2,3,24]{1,0,2:T(2,128)S(1)} %copy.296), channel_id=1, replica_groups=mesh['clip'=4,'seq'=4,'head'=2] {'clip','seq','head'}, dimensions={2}, use_global_device_ids=true | all-gather | bytes 19008 | tf_op jit(solution)/shard_map/all_gather | solution.py:231
  343.6 70.0 %all_gather.110 = f32[2,3,768]{1,0,2:T(2,128)S(1)} all-gather(f32[2,3,24]{1,0,2:T(2,128)S(1)} %copy.295), channel_id=1, replica_groups=mesh['clip'=4,'seq'=4,'head'=2] {'clip','seq','head'}, dimensions={2}, use_global_device_ids=true | all-gather | bytes 19008 | tf_op jit(solution)/shard_map/all_gather | solution.py:230
  444.8 46.8 %all-gather.20 = bf16[1,384,768]{1,2,0:T(8,128)(2,1)S(1)} all-gather(bf16[1,384,48]{1,2,0:T(8,128)(2,1)S(1)} %get-tuple-element.105), channel_id=22, replica_groups=mesh['clip'=4,'seq'=4,'head'=2] {'clip','seq'}, dimensions={2}, use_global_device_ids=true | all-gather | bytes 626688 | tf_op jit(solution)/shard_map/all_gather | solution.py:258
  556.3 51.8 %all-gather.65.cloned.1.call-done = bf16[1,768,3072]{2,1,0:T(8,128)(2,1)} async-done(((bf16[1,768,1536]{2,1,0:T(8,128)(2,1)}), bf16[1,768,3072]{2,1,0:T(8,128)(2,1)}) %all-gather.65.cloned.1.call-update) | async-done | bytes 4718608 | tf_op jit(solution)/shard_map/all_gather | solution.py:263
  614.9 57.3 %all-gather.69.cloned.1.call-done = bf16[1,3072,768]{2,1,0:T(8,128)(2,1)} async-done(((bf16[1,1536,768]{2,1,0:T(8,128)(2,1)}), bf16[1,3072,768]{2,1,0:T(8,128)(2,1)}) %all-gather.69.cloned.1.call-update) | async-done | bytes 4718608 | tf_op jit(solution)/shard_map/all_gather | solution.py:269
  801.1 54.9 %all-gather.77.cloned.1.call-done = bf16[1,768,768]{2,1,0:T(8,128)(2,1)} async-done(((bf16[1,24,768]{2,1,0:T(8,128)(2,1)}), bf16[1,768,768]{2,1,0:T(8,128)(2,1)}) %all-gather.77.cloned.1.call-update) | async-done | bytes 1179664 | tf_op jit(solution)/shard_map/all_gather | solution.py:276
  859.7 46.1 %all-gather.81.cloned.1.call-done = bf16[1,768,3,768]{3,1,2,0:T(8,128)(2,1)} async-done(((bf16[1,768,3,384]{3,1,2,0:T(8,128)(2,1)}), bf16[1,768,3,768]{3,1,2,0:T(8,128)(2,1)}) %all-gather.81.cloned.1.call-update) | async-done | bytes 3538960 | tf_op jit(solution)/shard_map/all_gather | solution.py:251
  933.8 60.4 %all-gather.87.cloned.1.call-done = bf16[1,768,3072]{2,1,0:T(8,128)(2,1)} async-done(((bf16[1,768,1536]{2,1,0:T(8,128)(2,1)}), bf16[1,768,3072]{2,1,0:T(8,128)(2,1)}) %all-gather.87.cloned.1.call-update) | async-done | bytes 4718608 | tf_op jit(solution)/shard_map/all_gather | solution.py:263
  1001.2 57.2 %all-gather.91.cloned.1.call-done = bf16[1,3072,768]{2,1,0:T(8,128)(2,1)} async-done(((bf16[1,1536,768]{2,1,0:T(8,128)(2,1)}), bf16[1,3072,768]{2,1,0:T(8,128)(2,1)}) %all-gather.91.cloned.1.call-update) | async-done | bytes 4718608 | tf_op jit(solution)/shard_map/all_gather | solution.py:269
  1464.3 48.4 %reduce-scatter.81.cloned.1.call-done = bf16[1536,768]{1,0:T(8,128)(2,1)} async-done(((bf16[3072,768]{1,0:T(8,128)(2,1)}), bf16[1536,768]{1,0:T(8,128)(2,1)}) %reduce-scatter.81.cloned.1.call-update) | async-done | bytes 2359312 | tf_op jit(solution)/shard_map/reduce_scatter | solution.py:350
  1517.4 57.8 %reduce-scatter.79.cloned.1.call-done = bf16[1536,768]{1,0:T(8,128)(2,1)} async-done(((bf16[3072,768]{1,0:T(8,128)(2,1)}), bf16[1536,768]{1,0:T(8,128)(2,1)}) %reduce-scatter.79.cloned.1.call-update) | async-done | bytes 2359312 | tf_op jit(solution)/shard_map/reduce_scatter | solution.py:350
  1579.8 57.5 %reduce-scatter.75.cloned.1.call-done = bf16[768,1536]{1,0:T(8,128)(2,1)} async-done(((bf16[768,3072]{1,0:T(8,128)(2,1)}), bf16[768,1536]{1,0:T(8,128)(2,1)}) %reduce-scatter.75.cloned.1.call-update) | async-done | bytes 2359312 | tf_op jit(solution)/shard_map/reduce_scatter | solution.py:347
  1641.9 57.9 %reduce-scatter.71.cloned.1.call-done = bf16[768,1536]{1,0:T(8,128)(2,1)} async-done(((bf16[768,3072]{1,0:T(8,128)(2,1)}), bf16[768,1536]{1,0:T(8,128)(2,1)}) %reduce-scatter.71.cloned.1.call-update) | async-done | bytes 2359312 | tf_op jit(solution)/shard_map/reduce_scatter | solution.py:347
  1736.1 37.9 %all-reduce.4 = (f32[3,768]{1,0:T(4,128)S(1)}, f32[3,768]{1,0:T(4,128)S(1)}, f32[3,768]{1,0:T(4,128)S(1)}, f32[3,768]{1,0:T(4,128)S(1)}) all-reduce(f32[3,768]{1,0:T(4,128)S(1)} %pad_maximum_fusion.14, f32[3,768]{1,0:T(4,128)S(1)} %pad_maximum_fusion.13, ...), channel_id=55, replica_groups=mesh['clip'=4,'seq'=4,'head'=2] {'clip','seq','head'}, use_global_device_ids=true, to_apply=%region_69.0.clone | all-reduce | flops 9216 | bytes 73728
  1778.7 43.5 %reduce-scatter.89.cloned.1.call-done = f32[48,384]{1,0:T(8,128)} async-done(((f32[768,384]{1,0:T(8,128)}), f32[48,384]{1,0:T(8,128)}) %reduce-scatter.89.cloned.1.call-update) | async-done | bytes 73744
  1823.3 102.1 %reduce-scatter.61.cloned.1.call-done = f32[24,768]{1,0:T(8,128)} async-done(((f32[768,768]{1,0:T(8,128)}), f32[24,768]{1,0:T(8,128)}) %reduce-scatter.61.cloned.1.call-update) | async-done | bytes 73744 | tf_op jit(solution)/shard_map/reduce_scatter | solution.py:363
  1925.4 104.1 %reduce-scatter.59.cloned.1.call-done = f32[24,768]{1,0:T(8,128)} async-done(((f32[768,768]{1,0:T(8,128)}), f32[24,768]{1,0:T(8,128)}) %reduce-scatter.59.cloned.1.call-update) | async-done | bytes 73744 | tf_op jit(solution)/shard_map/reduce_scatter | solution.py:363
  2031.1 59.1 %reduce-scatter.95.cloned.1.call-done = f32[48,384]{1,0:T(8,128)} async-done(((f32[768,384]{1,0:T(8,128)}), f32[48,384]{1,0:T(8,128)}) %reduce-scatter.95.cloned.1.call-update) | async-done | bytes 73744
  2091.3 59.6 %reduce-scatter.87.cloned.1.call-done = f32[48,384]{1,0:T(8,128)} async-done(((f32[768,384]{1,0:T(8,128)}), f32[48,384]{1,0:T(8,128)}) %reduce-scatter.87.cloned.1.call-update) | async-done | bytes 73744
  2153.4 68.5 %reduce-scatter.65.cloned.1.call-done = f32[48,3,384]{2,0,1:T(8,128)} async-done(((f32[768,3,384]{2,0,1:T(8,128)}), f32[48,3,384]{2,0,1:T(8,128)}) %reduce-scatter.65.cloned.1.call-update) | async-done | bytes 221200 | tf_op jit(solution)/shard_map/reduce_scatter | solution.py:357
  2221.9 70.9 %reduce-scatter.63.cloned.1.call-done = f32[48,3,384]{2,0,1:T(8,128)} async-done(((f32[768,3,384]{2,0,1:T(8,128)}), f32[48,3,384]{2,0,1:T(8,128)}) %reduce-scatter.63.cloned.1.call-update) | async-done | bytes 221200 | tf_op jit(solution)/shard_map/reduce_scatter | solution.py:357
  2294.6 68.9 %reduce-scatter.53.cloned.1.call-done = f32[48,3,384]{2,0,1:T(8,128)} async-done(((f32[768,3,384]{2,0,1:T(8,128)}), f32[48,3,384]{2,0,1:T(8,128)}) %reduce-scatter.53.cloned.1.call-update) | async-done | bytes 221200 | tf_op jit(solution)/shard_map/reduce_scatter | solution.py:355
  2363.5 70.8 %reduce-scatter.51.cloned.1.call-done = f32[48,3,384]{2,0,1:T(8,128)} async-done(((f32[768,3,384]{2,0,1:T(8,128)}), f32[48,3,384]{2,0,1:T(8,128)}) %reduce-scatter.51.cloned.1.call-update) | async-done | bytes 221200 | tf_op jit(solution)/shard_map/reduce_scatter | solution.py:355
  2436.2 76.4 %reduce-scatter.101.cloned.1.call-done = f32[48,1536]{1,0:T(8,128)} async-done(((f32[768,1536]{1,0:T(8,128)}), f32[48,1536]{1,0:T(8,128)}) %reduce-scatter.101.cloned.1.call-update) | async-done | bytes 294928
  2514.0 77.4 %reduce-scatter.99.cloned.1.call-done = f32[48,1536]{1,0:T(8,128)} async-done(((f32[768,1536]{1,0:T(8,128)}), f32[48,1536]{1,0:T(8,128)}) %reduce-scatter.99.cloned.1.call-update) | async-done | bytes 294928
  2593.8 76.0 %reduce-scatter.77.cloned.1.call-done = f32[48,1536]{1,0:T(8,128)} async-done(((f32[768,1536]{1,0:T(8,128)}), f32[48,1536]{1,0:T(8,128)}) %reduce-scatter.77.cloned.1.call-update) | async-done | bytes 294928 | tf_op jit(solution)/shard_map/reduce_scatter | solution.py:359
  2669.8 78.9 %reduce-scatter.73.cloned.1.call-done = f32[48,1536]{1,0:T(8,128)} async-done(((f32[768,1536]{1,0:T(8,128)}), f32[48,1536]{1,0:T(8,128)}) %reduce-scatter.73.cloned.1.call-update) | async-done | bytes 294928 | tf_op jit(solution)/shard_map/reduce_scatter | solution.py:359
  (711 shorter events, 811.0 us)
Async XLA Ops:
  14.4 478.5 %all-gather.51.cloned.1.call-start = ((), (), s32[]{:S(2)}) async-start(), calls=%async_computation.51 | async-start | bytes 5308416 | tf_op jit(solution)/shard_map/all_gather | solution.py:239
  54.0 461.5 %all-gather.85.cloned.1.call-start = ((), (), s32[]{:S(2)}) async-start(), calls=%async_computation.68 | async-start | bytes 2506752 | tf_op jit(solution)/shard_map/all_gather | solution.py:264
  54.7 476.8 %all-gather.53.cloned.1.call-start = ((), (), s32[]{:S(2)}) async-start(), calls=%async_computation.52 | async-start | bytes 1769472 | tf_op jit(solution)/shard_map/all_gather | solution.py:245
  93.1 440.6 %all-gather.55.cloned.1.call-start = ((), (), s32[]{:S(2)}) async-start(), calls=%async_computation.53 | async-start | bytes 1216512 | tf_op jit(solution)/shard_map/all_gather | solution.py:276
  93.8 442.5 %all-gather.59.cloned.1.call-start = ((), (), s32[]{:S(2)}) async-start(), calls=%async_computation.55 | async-start | bytes 5308416 | tf_op jit(solution)/shard_map/all_gather | solution.py:251
  97.4 455.9 %all-gather.61.cloned.1.call-start = ((), (), s32[]{:S(2)}) async-start(), calls=%async_computation.56 | async-start | bytes 1769472 | tf_op jit(solution)/shard_map/all_gather | solution.py:257
  137.9 470.2 %all-gather.65.cloned.1.call-start = ((), (), s32[]{:S(2)}) async-start(), calls=%async_computation.58 | async-start | bytes 7077888 | tf_op jit(solution)/shard_map/all_gather | solution.py:263
  142.9 529.2 %all-gather.69.cloned.1.call-start = ((), (), s32[]{:S(2)}) async-start(), calls=%async_computation.60 | async-start | bytes 7077888 | tf_op jit(solution)/shard_map/all_gather | solution.py:269
  191.0 532.0 %all-gather.73.cloned.1.call-start = ((), (), s32[]{:S(2)}) async-start(), calls=%async_computation.62 | async-start | bytes 5308416 | tf_op jit(solution)/shard_map/all_gather | solution.py:239
  228.5 545.9 %all-gather.89.cloned.1.call-start = ((), (), s32[]{:S(2)}) async-start(), calls=%async_computation.70 | async-start | bytes 2506752 | tf_op jit(solution)/shard_map/all_gather | solution.py:270
  229.1 569.8 %all-gather.75.cloned.1.call-start = ((), (), s32[]{:S(2)}) async-start(), calls=%async_computation.63 | async-start | bytes 1769472 | tf_op jit(solution)/shard_map/all_gather | solution.py:245
  267.7 588.2 %all-gather.77.cloned.1.call-start = ((), (), s32[]{:S(2)}) async-start(), calls=%async_computation.64 | async-start | bytes 1216512 | tf_op jit(solution)/shard_map/all_gather | solution.py:276
  268.3 637.5 %all-gather.81.cloned.1.call-start = ((), (), s32[]{:S(2)}) async-start(), calls=%async_computation.66 | async-start | bytes 5308416 | tf_op jit(solution)/shard_map/all_gather | solution.py:251
  444.8 485.2 %all-gather.83.cloned.1.call-start = ((), (), s32[]{:S(2)}) async-start(), calls=%async_computation.67 | async-start | bytes 1769472 | tf_op jit(solution)/shard_map/all_gather | solution.py:257
  515.0 479.2 %all-gather.87.cloned.1.call-start = ((), (), s32[]{:S(2)}) async-start(), calls=%async_computation.69 | async-start | bytes 7077888 | tf_op jit(solution)/shard_map/all_gather | solution.py:263
  747.7 310.7 %all-gather.91.cloned.1.call-start = ((), (), s32[]{:S(2)}) async-start(), calls=%async_computation.71 | async-start | bytes 7077888 | tf_op jit(solution)/shard_map/all_gather | solution.py:269
  1353.4 284.0 %reduce-scatter.75.cloned.1.call-start = ((), (), s32[]{:S(2)}) async-start(), calls=%async_computation.46 | async-start | bytes 7077888 | tf_op jit(solution)/shard_map/reduce_scatter | solution.py:347
  1360.9 338.9 %reduce-scatter.71.cloned.1.call-start = ((), (), s32[]{:S(2)}) async-start(), calls=%async_computation.44 | async-start | bytes 7077888 | tf_op jit(solution)/shard_map/reduce_scatter | solution.py:347
  1368.4 409.2 %reduce-scatter.97.cloned.1.call-start = ((), (), s32[]{:S(2)}) async-start(), calls=%async_computation.79 | async-start | bytes 1253376
  1370.8 451.4 %reduce-scatter.89.cloned.1.call-start = ((), (), s32[]{:S(2)}) async-start(), calls=%async_computation.75 | async-start | bytes 1253376
  1373.5 551.9 %reduce-scatter.61.cloned.1.call-start = ((), (), s32[]{:S(2)}) async-start(), calls=%async_computation.39 | async-start | bytes 2433024 | tf_op jit(solution)/shard_map/reduce_scatter | solution.py:363
  1375.8 653.8 %reduce-scatter.59.cloned.1.call-start = ((), (), s32[]{:S(2)}) async-start(), calls=%async_computation.38 | async-start | bytes 2433024 | tf_op jit(solution)/shard_map/reduce_scatter | solution.py:363
  1379.5 710.7 %reduce-scatter.95.cloned.1.call-start = ((), (), s32[]{:S(2)}) async-start(), calls=%async_computation.78 | async-start | bytes 1253376
  1381.9 769.0 %reduce-scatter.87.cloned.1.call-start = ((), (), s32[]{:S(2)}) async-start(), calls=%async_computation.74 | async-start | bytes 1253376
  1384.3 837.5 %reduce-scatter.65.cloned.1.call-start = ((), (), s32[]{:S(2)}) async-start(), calls=%async_computation.41 | async-start | bytes 3760128 | tf_op jit(solution)/shard_map/reduce_scatter | solution.py:357
  1398.2 894.6 %reduce-scatter.63.cloned.1.call-start = ((), (), s32[]{:S(2)}) async-start(), calls=%async_computation.40 | async-start | bytes 3760128 | tf_op jit(solution)/shard_map/reduce_scatter | solution.py:357
  1412.5 951.0 %reduce-scatter.53.cloned.1.call-start = ((), (), s32[]{:S(2)}) async-start(), calls=%async_computation.35 | async-start | bytes 3760128 | tf_op jit(solution)/shard_map/reduce_scatter | solution.py:355
  1426.3 1008.0 %reduce-scatter.51.cloned.1.call-start = ((), (), s32[]{:S(2)}) async-start(), calls=%async_computation.34 | async-start | bytes 3760128 | tf_op jit(solution)/shard_map/reduce_scatter | solution.py:355
  1464.2 1048.3 %reduce-scatter.101.cloned.1.call-start = ((), (), s32[]{:S(2)}) async-start(), calls=%async_computation.81 | async-start | bytes 5013504
  1517.3 1074.1 %reduce-scatter.99.cloned.1.call-start = ((), (), s32[]{:S(2)}) async-start(), calls=%async_computation.80 | async-start | bytes 5013504
  1579.8 1090.0 %reduce-scatter.77.cloned.1.call-start = ((), (), s32[]{:S(2)}) async-start(), calls=%async_computation.47 | async-start | bytes 5013504 | tf_op jit(solution)/shard_map/reduce_scatter | solution.py:359
  1641.9 1106.8 %reduce-scatter.73.cloned.1.call-start = ((), (), s32[]{:S(2)}) async-start(), calls=%async_computation.45 | async-start | bytes 5013504 | tf_op jit(solution)/shard_map/reduce_scatter | solution.py:359
  (174 other events, 6834.5 us)
Sparse Core Ops, SparseCore 0:
  272.9 61.6 all-gather.50
  411.2 58.0 all-gather.54
  470.8 48.2 all-gather.58
  545.4 62.6 all-gather.64
  609.5 62.6 all-gather.68
  673.6 49.3 all-gather.72
  725.7 48.6 all-gather.88
  801.7 54.1 all-gather.76
  857.5 48.2 all-gather.80
  931.5 62.6 all-gather.86
  995.7 62.6 all-gather.90
  1252.8 47.6 reduce-scatter.92
  1302.8 47.6 reduce-scatter.90
  1352.8 47.6 reduce-scatter.84
  1452.7 59.9 reduce-scatter.80
  1515.1 59.9 reduce-scatter.78
  1577.3 59.9 reduce-scatter.74
  1639.8 59.9 reduce-scatter.70
  1703.4 58.2 reduce-scatter.96
  1765.2 56.9 reduce-scatter.88
  1827.3 98.0 reduce-scatter.60
  1931.5 97.9 reduce-scatter.58
  2033.0 57.1 reduce-scatter.94
  2093.8 57.0 reduce-scatter.86
  2154.8 67.0 reduce-scatter.64
  2225.8 66.9 reduce-scatter.62
  2296.5 66.9 reduce-scatter.52
  2367.4 66.9 reduce-scatter.50
  2438.1 74.4 reduce-scatter.100
  2516.8 74.6 reduce-scatter.98
  2595.2 74.5 reduce-scatter.76
  2674.0 74.6 reduce-scatter.72
  (16 shorter events, 516.7 us)
where the time goes:
time: 2770 us; the launch traced here: 2760 us
  waiting for transfers between devices  1810 us (65%)
  blocking collectives  361 us (13%)
  local copies, waits for them, and re-layouts  274 us (10%)
  matrix products  208 us (8%)
  other arithmetic  54.9 us (2%)
  starting transfers between devices  31.8 us (1%)
    unnamed x58, waiting for transfers between devices  344 us
    dot_general x66, matrix products, matmul(): return jnp.einsum(form, left, right, preferred_element_type=jnp.float32)  208 us
    reduce_scatter x2, waiting for transfers between devices, on_device(): lax.psum_scatter(whole_grads[0], ('clip', 'seq', 'head'), scatter_dimensi...  206 us
    reduce_scatter x2, waiting for transfers between devices, on_device(): lax.psum_scatter(head_sums[4], ('clip', 'seq'), scatter_dimension=0, tile...  155 us
    unnamed x340, local copies, waits for them, and re-layouts  149 us
    reduce_scatter x2, waiting for transfers between devices, on_device(): lax.psum_scatter(head_sums[0], ('clip', 'seq'), scatter_dimension=0, tile...  140 us
    reduce_scatter x2, waiting for transfers between devices, on_device(): lax.psum_scatter(head_sums[2], ('clip', 'seq'), scatter_dimension=0, tile...  139 us
    reduce_scatter x2, waiting for transfers between devices, on_device(): lax.psum_scatter(split_grads[4].astype(jnp.bfloat16), 'head', scatter_dim...  115 us
  transfers between devices with their start and end apart: 55, of which 39 were waited for; matrix products, arithmetic and copies ran while one was open for 17% of the time, Pallas kernels for 0%

commit v1 on v0

v1 whole, which is shorter than its diff:
```python
import functools
import math

import jax
import jax.numpy as jnp
from jax import lax
from jax.experimental import pallas as pl
from jax.experimental.pallas import tpu as pltpu
from jax.sharding import PartitionSpec as P

HEAD_DIM = 64
NORM_EPS = 1e-06
HALF_ROOT = 0.7071067811865476
INV_ROOT_TAU = 0.3989422804014327
LOG2E = 1.4426950408889634
FAR = -1e30
LANES = 128
VMEM = 56 * 1024 * 1024
ALL = ("clip", "seq", "head")
BF16 = jnp.bfloat16
F32 = jnp.float32


def round_up(value, step):
    return -(-value // step) * step


def nn(a, b):
    return lax.dot_general(a, b, (((1,), (0,)), ((), ())), preferred_element_type=F32)


def nt(a, b):
    return lax.dot_general(a, b, (((1,), (1,)), ((), ())), preferred_element_type=F32)


def tn(a, b):
    return lax.dot_general(a, b, (((0,), (0,)), ((), ())), preferred_element_type=F32)


def norm_parts(x):
    mean = jnp.mean(x, axis=-1, keepdims=True)
    centred = x - mean
    spread = lax.rsqrt(jnp.mean(centred * centred, axis=-1, keepdims=True) + NORM_EPS)
    return centred * spread, spread


def norm_rounded(x, gain, bias):
    hat, _ = norm_parts(x)
    return (hat * gain + bias).astype(BF16)


def norm_back(u, x, gain):
    hat, spread = norm_parts(x)
    scaled = u * gain
    mean_scaled = jnp.mean(scaled, axis=-1, keepdims=True)
    mean_cross = jnp.mean(scaled * hat, axis=-1, keepdims=True)
    change = spread * (scaled - mean_scaled - hat * mean_cross)
    sums = jnp.concatenate(
        (jnp.sum(u * hat, axis=0, keepdims=True), jnp.sum(u, axis=0, keepdims=True)), axis=0
    )
    return change, sums


class Rows:
    def __init__(self, frames, places, ways):
        self.frames = frames
        self.places = places
        self.ways = ways
        self.frame_rows = round_up(places, 16)
        self.rows = frames * self.frame_rows
        self.block = places // ways
        self.chunk = round_up(frames * self.block, 8)
        self.time_rows = ways * self.chunk

    def split(self, r):
        way = jnp.zeros_like(r)
        for k in range(1, self.ways):
            way = way + (r >= k * self.chunk).astype(jnp.int32)
        rest = r - way * self.chunk
        frame = jnp.zeros_like(r)
        for k in range(1, self.frames):
            frame = frame + (rest >= k * self.block).astype(jnp.int32)
        real = rest < self.frames * self.block
        return way, frame, rest - frame * self.block, real

    def to_time(self):
        r = lax.broadcasted_iota(jnp.int32, (self.time_rows, 1), 0)
        way, frame, place, real = self.split(r)
        source = jnp.where(real, frame * self.frame_rows + way * self.block + place, -1)
        c = lax.broadcasted_iota(jnp.int32, (self.time_rows, self.rows), 1)
        return jnp.where(c == source, 1.0, 0.0).astype(BF16)

    def time_bias(self):
        def label(r):
            _, _, place, real = self.split(r)
            return jnp.where(real, place, -1)

        a = label(lax.broadcasted_iota(jnp.int32, (self.time_rows, 1), 0))
        b = label(lax.broadcasted_iota(jnp.int32, (1, self.time_rows), 1))
        return jnp.where(a == b, 0.0, FAR).astype(F32)

    def space_bias(self):
        a = lax.broadcasted_iota(jnp.int32, (self.frame_rows, 1), 0)
        return jnp.where(a < self.places, 0.0, FAR).astype(F32)


def lane_masks(rows):
    lane = lax.broadcasted_iota(jnp.int32, (rows, LANES), 1)
    return lane < HEAD_DIM


def one_of(value, low, half):
    zero = jnp.zeros_like(value)
    return jnp.where(low, value, zero) if half == 0 else jnp.where(low, zero, value)


def pair_forward(q, k, v, bias, rate):
    low = lane_masks(q.shape[0])
    mixed, logs = [], []
    for half in range(2):
        s = nt(k, one_of(q, low, half)) + bias
        peak = jnp.max(s, axis=0, keepdims=True)
        e = jnp.exp2((s - peak) * rate)
        total = jnp.sum(e, axis=0, keepdims=True)
        soft = (e * (1.0 / total)).astype(BF16)
        mixed.append(tn(soft, v))
        logs.append(peak * rate + jnp.log2(total))
    return jnp.where(low, mixed[0], mixed[1]).astype(BF16), logs


def pair_backward(q, k, v, do, logs, bias, rate, scale):
    low = lane_masks(q.shape[0])
    dq, dk, dv = [], [], []
    for half in range(2):
        s = nt(k, one_of(q, low, half)) + bias
        soft = jnp.exp2(s * rate - logs[half])
        dp = nt(v, one_of(do, low, half))
        ds = (soft * (dp - jnp.sum(soft * dp, axis=0, keepdims=True))).astype(BF16)
        dv.append(nn(soft.astype(BF16), do))
        dk.append(nn(ds, q))
        dq.append(tn(ds, k))
    return (
        (jnp.where(low, dq[0], dq[1]) * scale).astype(BF16),
        (jnp.where(low, dk[0], dk[1]) * scale).astype(BF16),
        jnp.where(low, dv[0], dv[1]).astype(BF16),
    )


def call(body, grid, ins, outs, scratch, args, flops=0):
    specs = [spec for spec in ins]
    moved = sum(math.prod(o.shape) * o.dtype.itemsize for o, _ in outs)
    moved += sum(math.prod(a.shape) * a.dtype.itemsize for a in args)
    return pl.pallas_call(
        body,
        out_shape=[shape for shape, _ in outs],
        grid=grid,
        in_specs=specs,
        out_specs=[spec for _, spec in outs],
        scratch_shapes=scratch,
        compiler_params=pltpu.CompilerParams(vmem_limit_bytes=VMEM),
        cost_estimate=pl.CostEstimate(flops=flops, bytes_accessed=moved, transcendentals=0),
    )(*args)


def whole(shape):
    zeros = (0,) * len(shape)
    return pl.BlockSpec(shape, lambda *_: zeros)


def made(shape, dtype, block=None, index=None):
    spec = whole(shape) if block is None else pl.BlockSpec(block, index)
    return jax.ShapeDtypeStruct(shape, dtype), spec


def slabs(count, first, width, depth):
    return pl.BlockSpec((count, 1, depth, width), lambda h, *_: (first // count, h, 0, 0))


def send_first(rows, x, gb):
    def body(x_ref, gb_ref, out_ref):
        a = norm_rounded(x_ref[...], gb_ref[0:1], gb_ref[3:4])
        out_ref[...] = nn(rows.to_time(), a).astype(BF16)

    d = x.shape[1]
    return call(
        body, (1,), [whole(x.shape), whole(gb.shape)], [made((rows.time_rows, d), BF16)], [], (x, gb)
    )[0]


def time_forward(rows, a, w, head_shares):
    t, d = a.shape
    width = w.shape[3]
    pairs = width // LANES
    rate = LOG2E / math.sqrt(HEAD_DIM)

    def body(a_ref, w_ref, qkv_ref, out_ref, log_ref, bias_ref):
        @pl.when(pl.program_id(0) == 0)
        def _():
            bias_ref[...] = rows.time_bias()

        act = a_ref[...]
        for g in range(3):
            qkv_ref[g] = nn(act, w_ref[g, 0]).astype(BF16)

        @pl.loop(0, pairs)
        def _(i):
            lanes = pl.ds(pl.multiple_of(i * LANES, LANES), LANES)
            mixed, logs = pair_forward(
                qkv_ref[0, :, lanes], qkv_ref[1, :, lanes], qkv_ref[2, :, lanes], bias_ref[...], rate
            )
            out_ref[:, lanes] = mixed
            log_ref[0, i] = jnp.concatenate(logs, axis=0)

    return call(
        body,
        (head_shares,),
        [whole(a.shape), slabs(3, 0, width, d)],
        [
            made((3, t, d), BF16, (3, t, width), lambda h: (0, 0, h)),
            made((t, d), BF16, (t, width), lambda h: (0, h)),
            made((head_shares, pairs, 2, t), F32, (1, pairs, 2, t), lambda h: (h, 0, 0, 0)),
        ],
        [pltpu.VMEM((t, t), F32)],
        (a, w),
        flops=2 * t * d * 3 * d,
    )


def middle_forward(rows, back, x, w, mix, gb):
    t, d = x.shape
    width = w.shape[3]
    shares = w.shape[1]

    def body(back_ref, x_ref, to_ref, sq_ref, mix_ref, gb_ref, o1_ref, y1_ref, x1_ref, qkv_ref):
        o1 = tn(rows.to_time(), back_ref[...]).astype(BF16)
        o1_ref[...] = o1
        y1 = jnp.zeros((t, d), F32)
        for h in range(shares):
            y1 = y1 + nt(o1[:, h * width : (h + 1) * width], to_ref[0, h])
        y1 = y1.astype(BF16)
        y1_ref[...] = y1
        x1 = x_ref[...] + nn(y1, mix_ref[...])
        x1_ref[...] = x1
        a2 = norm_rounded(x1, gb_ref[1:2], gb_ref[4:5])
        for g in range(3):
            for h in range(shares):
                qkv_ref[g, :, h * width : (h + 1) * width] = nn(a2, sq_ref[g, h]).astype(BF16)

    return call(
        body,
        (1,),
        [
            whole(back.shape),
            whole(x.shape),
            pl.BlockSpec((1, shares, d, width), lambda i: (6, 0, 0, 0)),
            pl.BlockSpec((3, shares, d, width), lambda i: (1, 0, 0, 0)),
            whole(mix.shape),
            whole(gb.shape),
        ],
        [made((t, d), BF16), made((t, d), BF16), made((t, d), F32), made((3, t, d), BF16)],
        [],
        (back, x, w, w, mix, gb),
        flops=2 * t * d * 5 * d,
    )


def space_forward(rows, qkv, x1, w):
    t, d = x1.shape
    width = w.shape[3]
    shares = w.shape[1]
    pairs = width // LANES
    rate = LOG2E / math.sqrt(HEAD_DIM)
    n = rows.frame_rows

    def body(qkv_ref, x1_ref, w_ref, o2_ref, x2_ref, log_ref):
        bias = rows.space_bias()

        @pl.loop(0, pairs)
        def _(i):
            lanes = pl.ds(pl.multiple_of(i * LANES, LANES), LANES)
            for f in range(rows.frames):
                at = slice(f * n, (f + 1) * n)
                mixed, logs = pair_forward(
                    qkv_ref[0, at, lanes], qkv_ref[1, at, lanes], qkv_ref[2, at, lanes], bias, rate
                )
                o2_ref[at, lanes] = mixed
                log_ref[0, i, f] = jnp.concatenate(logs, axis=0)

        @pl.when(pl.program_id(0) == 0)
        def _():
            x2_ref[...] = x1_ref[...]

        x2_ref[...] += nt(o2_ref[...], w_ref[0, 0])

    return call(
        body,
        (shares,),
        [
            pl.BlockSpec((3, t, width), lambda h: (0, 0, h)),
            whole(x1.shape),
            slabs(1, 7, width, d),
        ],
        [
            made((t, d), BF16, (t, width), lambda h: (0, h)),
            made((t, d), F32),
            made(
                (shares, pairs, rows.frames, 2, n),
                F32,
                (1, pairs, rows.frames, 2, n),
                lambda h: (h, 0, 0, 0, 0),
            ),
        ],
        [],
        (qkv, x1, w),
        flops=2 * t * d * d,
    )


def ff_slab(first, per_share, depth, width):
    return pl.BlockSpec(
        (1, 1, depth, width), lambda j: (first + j % per_share, j // per_share, 0, 0)
    )


def mlp_forward(rows, x2, w, gb, gb_next):
    t, d = x2.shape
    width = w.shape[3]
    shares = w.shape[1]
    per_share = (w.shape[0] - 9) // 2
    steps = shares * per_share
    last = gb_next is None

    def body(x2_ref, wi_ref, wo_ref, gb_ref, *rest):
        if last:
            x3_ref, a3_ref = rest
        else:
            gn_ref, x3_ref, send_ref, a3_ref = rest
        j = pl.program_id(0)

        @pl.when(j == 0)
        def _():
            a3_ref[...] = norm_rounded(x2_ref[...], gb_ref[2:3], gb_ref[5:6])
            x3_ref[...] = x2_ref[...]

        hid = nn(a3_ref[...], wi_ref[0, 0])
        act = (0.5 * hid * (1.0 + lax.erf(hid * HALF_ROOT))).astype(BF16)
        x3_ref[...] += nt(act, wo_ref[0, 0])

        if not last:

            @pl.when(j == steps - 1)
            def _():
                a = norm_rounded(x3_ref[...], gn_ref[0:1], gn_ref[3:4])
                send_ref[...] = nn(rows.to_time(), a).astype(BF16)

    ins = [
        whole(x2.shape),
        ff_slab(8, per_share, d, width),
        ff_slab(8 + per_share, per_share, d, width),
        whole(gb.shape),
    ]
    outs = [made((t, d), F32)]
    args = [x2, w, w, gb]
    if not last:
        ins.append(whole(gb_next.shape))
        outs.append(made((rows.time_rows, d), BF16))
        args.append(gb_next)
    return call(
        body, (steps,), ins, outs, [pltpu.VMEM((t, d), BF16)], tuple(args), flops=4 * t * d * width * steps
    )


def mlp_backward(rows, grad, x2, w, gb):
    t, d = x2.shape
    width = w.shape[3]
    shares = w.shape[1]
    per_share = (w.shape[0] - 9) // 2
    steps = shares * per_share

    def body(g_ref, x2_ref, wi_ref, wo_ref, gb_ref, go_ref, gi_ref, gw_ref, sums_ref, a3_ref, a3t_ref, e3_ref, e3t_ref, u_ref):
        j = pl.program_id(0)

        @pl.when(j == 0)
        def _():
            hat, _ = norm_parts(x2_ref[...])
            a3 = hat * gb_ref[2:3] + gb_ref[5:6]
            a3_ref[...] = a3.astype(BF16)
            a3t_ref[...] = a3.T.astype(BF16)
            g = g_ref[...]
            e3_ref[...] = g.astype(BF16)
            e3t_ref[...] = g.T.astype(BF16)
            u_ref[...] = jnp.zeros((t, d), F32)

        hid = nn(a3_ref[...], wi_ref[0, 0])
        phi = 0.5 * (1.0 + lax.erf(hid * HALF_ROOT))
        act = (hid * phi).astype(BF16)
        slope = phi + hid * jnp.exp(-0.5 * hid * hid) * INV_ROOT_TAU
        dhid = (nn(e3_ref[...], wo_ref[0, 0]) * slope).astype(BF16)
        gw_ref[0, 0] = nn(e3t_ref[...], act).astype(BF16)
        gi_ref[0, 0] = nn(a3t_ref[...], dhid).astype(BF16)
        u_ref[...] += nt(dhid, wi_ref[0, 0])

        @pl.when(j == steps - 1)
        def _():
            change, sums = norm_back(u_ref[...], x2_ref[...], gb_ref[2:3])
            go_ref[...] = g_ref[...] + change
            sums_ref[...] = sums

    slab_out = lambda: made(
        (per_share, shares, d, width),
        BF16,
        (1, 1, d, width),
        lambda j: (j % per_share, j // per_share, 0, 0),
    )
    return call(
        body,
        (steps,),
        [
            whole(grad.shape),
            whole(x2.shape),
            ff_slab(8, per_share, d, width),
            ff_slab(8 + per_share, per_share, d, width),
            whole(gb.shape),
        ],
        [made((t, d), F32), slab_out(), slab_out(), made((2, d), F32)],
        [
            pltpu.VMEM((t, d), BF16),
            pltpu.VMEM((d, t), BF16),
            pltpu.VMEM((t, d), BF16),
            pltpu.VMEM((d, t), BF16),
            pltpu.VMEM((t, d), F32),
        ],
        (grad, x2, w, w, gb),
        flops=10 * t * d * width * steps,
    )


def space_backward(rows, grad, x1, qkv, o2, logs, w, gb):
    t, d = x1.shape
    width = w.shape[3]
    shares = w.shape[1]
    pairs = width // LANES
    scale = 1.0 / math.sqrt(HEAD_DIM)
    rate = LOG2E * scale
    n = rows.frame_rows

    def body(g_ref, x1_ref, qkv_ref, o2_ref, log_ref, wo_ref, wq_ref, gb_ref, go_ref, gw_ref, gq_ref, sums_ref, e2_ref, e2t_ref, a2t_ref, do_ref, dqkv_ref, u_ref):
        h = pl.program_id(0)

        @pl.when(h == 0)
        def _():
            g = g_ref[...]
            e2_ref[...] = g.astype(BF16)
            e2t_ref[...] = g.T.astype(BF16)
            hat, _ = norm_parts(x1_ref[...])
            a2t_ref[...] = (hat * gb_ref[1:2] + gb_ref[4:5]).T.astype(BF16)
            u_ref[...] = jnp.zeros((t, d), F32)

        bias = rows.space_bias()
        gw_ref[0, 0] = nn(e2t_ref[...], o2_ref[...]).astype(BF16)
        do_ref[...] = nn(e2_ref[...], wo_ref[0, 0]).astype(BF16)

        @pl.loop(0, pairs)
        def _(i):
            lanes = pl.ds(pl.multiple_of(i * LANES, LANES), LANES)
            for f in range(rows.frames):
                at = slice(f * n, (f + 1) * n)
                log = log_ref[0, i, f]
                grads = pair_backward(
                    qkv_ref[0, at, lanes],
                    qkv_ref[1, at, lanes],
                    qkv_ref[2, at, lanes],
                    do_ref[at, lanes],
                    (log[0:1], log[1:2]),
                    bias,
                    rate,
                    scale,
                )
                for part in range(3):
                    dqkv_ref[part, at, lanes] = grads[part]

        for part in range(3):
            gq_ref[part, 0] = nn(a2t_ref[...], dqkv_ref[part]).astype(BF16)
            u_ref[...] += nt(dqkv_ref[part], wq_ref[part, 0])

        @pl.when(h == shares - 1)
        def _():
            change, sums = norm_back(u_ref[...], x1_ref[...], gb_ref[1:2])
            go_ref[...] = g_ref[...] + change
            sums_ref[...] = sums

    return call(
        body,
        (shares,),
        [
            whole(grad.shape),
            whole(x1.shape),
            pl.BlockSpec((3, t, width), lambda h: (0, 0, h)),
            pl.BlockSpec((t, width), lambda h: (0, h)),
            pl.BlockSpec((1,) + logs.shape[1:], lambda h: (h, 0, 0, 0, 0)),
            slabs(1, 7, width, d),
            slabs(3, 3, width, d),
            whole(gb.shape),
        ],
        [
            made((t, d), F32),
            made((1, shares, d, width), BF16, (1, 1, d, width), lambda h: (0, h, 0, 0)),
            made((3, shares, d, width), BF16, (3, 1, d, width), lambda h: (0, h, 0, 0)),
            made((2, d), F32),
        ],
        [
            pltpu.VMEM((t, d), BF16),
            pltpu.VMEM((d, t), BF16),
            pltpu.VMEM((d, t), BF16),
            pltpu.VMEM((t, width), BF16),
            pltpu.VMEM((3, t, width), BF16),
            pltpu.VMEM((t, d), F32),
        ],
        (grad, x1, qkv, o2, logs, w, w, gb),
        flops=2 * t * d * d * 8,
    )


def middle_backward(rows, grad, y1, o1, w, mix):
    t, d = grad.shape
    width = w.shape[3]
    shares = w.shape[1]

    def body(g_ref, y1_ref, o1_ref, to_ref, mix_ref, send_ref, gm_ref, gt_ref):
        e1 = g_ref[...].astype(BF16)
        gm_ref[...] = tn(y1_ref[...], e1).astype(BF16)
        dy = nt(e1, mix_ref[...])
        dy1 = dy.astype(BF16)
        send = rows.to_time()
        for h in range(shares):
            lanes = slice(h * width, (h + 1) * width)
            gt_ref[0, h] = tn(dy1, o1_ref[:, lanes]).astype(BF16)
            do1 = nn(dy1, to_ref[0, h]).astype(BF16)
            send_ref[:, lanes] = nn(send, do1).astype(BF16)

    return call(
        body,
        (1,),
        [
            whole(grad.shape),
            whole(y1.shape),
            whole(o1.shape),
            pl.BlockSpec((1, shares, d, width), lambda i: (6, 0, 0, 0)),
            whole(mix.shape),
        ],
        [
            made((rows.time_rows, d), BF16),
            made((d, d), BF16),
            made((1, shares, d, width), BF16),
        ],
        [],
        (grad, y1, o1, w, mix),
        flops=8 * t * d * d,
    )


def time_backward(rows, do1, a, qkv, logs, w):
    t, d = a.shape
    width = w.shape[3]
    shares = w.shape[1]
    pairs = width // LANES
    scale = 1.0 / math.sqrt(HEAD_DIM)
    rate = LOG2E * scale

    def body(do_ref, a_ref, qkv_ref, log_ref, w_ref, out_ref, gq_ref, bias_ref, dqkv_ref, at_ref, u_ref):
        h = pl.program_id(0)

        @pl.when(h == 0)
        def _():
            bias_ref[...] = rows.time_bias()
            at_ref[...] = a_ref[...].T
            u_ref[...] = jnp.zeros((t, d), F32)

        @pl.loop(0, pairs)
        def _(i):
            lanes = pl.ds(pl.multiple_of(i * LANES, LANES), LANES)
            log = log_ref[0, i]
            grads = pair_backward(
                qkv_ref[0, :, lanes],
                qkv_ref[1, :, lanes],
                qkv_ref[2, :, lanes],
                do_ref[:, lanes],
                (log[0:1], log[1:2]),
                bias_ref[...],
                rate,
                scale,
            )
            for part in range(3):
                dqkv_ref[part, :, lanes] = grads[part]

        for part in range(3):
            gq_ref[part, 0] = nn(at_ref[...], dqkv_ref[part]).astype(BF16)
            u_ref[...] += nt(dqkv_ref[part], w_ref[part, 0])

        @pl.when(h == shares - 1)
        def _():
            out_ref[...] = u_ref[...].astype(BF16)

    return call(
        body,
        (shares,),
        [
            pl.BlockSpec((t, width), lambda h: (0, h)),
            whole(a.shape),
            pl.BlockSpec((3, t, width), lambda h: (0, 0, h)),
            pl.BlockSpec((1,) + logs.shape[1:], lambda h: (h, 0, 0, 0)),
            slabs(3, 0, width, d),
        ],
        [
            made((t, d), BF16),
            made((3, shares, d, width), BF16, (3, 1, d, width), lambda h: (0, h, 0, 0)),
        ],
        [
            pltpu.VMEM((t, t), F32),
            pltpu.VMEM((3, t, width), BF16),
            pltpu.VMEM((d, t), BF16),
            pltpu.VMEM((t, d), F32),
        ],
        (do1, a, qkv, logs, w),
        flops=2 * t * d * d * 6,
    )


def first_norm_back(rows, back, x, grad, gb):
    t, d = x.shape

    def body(back_ref, x_ref, g_ref, gb_ref, go_ref, sums_ref):
        u = tn(rows.to_time(), back_ref[...])
        change, sums = norm_back(u, x_ref[...], gb_ref[0:1])
        go_ref[...] = g_ref[...] + change
        sums_ref[...] = sums

    return call(
        body,
        (1,),
        [whole(back.shape), whole(x.shape), whole(grad.shape), whole(gb.shape)],
        [made((t, d), F32), made((2, d), F32)],
        [],
        (back, x, grad, gb),
    )


def swap_places(rows_array):
    return lax.all_to_all(rows_array, "seq", split_axis=0, concat_axis=0, tiled=True)


def pack_layer(time_qkv, time_out, time_mix, space_qkv, space_out, mlp_in, mlp_out):
    width = time_qkv.shape[2]
    r = time_qkv.shape[0]
    halves = time_mix.shape[1] // width

    def columns(a):
        return a.reshape(r, -1, width).transpose(1, 0, 2)

    mix = time_mix.reshape(-1, halves, width).transpose(1, 0, 2).reshape(1, r, width)
    return jnp.concatenate(
        (
            columns(time_qkv),
            columns(space_qkv),
            time_out.T[None],
            space_out.T[None],
            columns(mlp_in),
            columns(mlp_out.T),
            mix,
        ),
        axis=0,
    )


def gather_slabs(pack):
    full = lax.all_gather(pack, ("head", "clip", "seq"), axis=1, tiled=True)
    return full.reshape(pack.shape[0], lax.axis_size("head"), -1, pack.shape[2])


def mix_whole(slab, shards):
    shares, depth, width = slab.shape
    part = slab.reshape(shares, shards, shares, depth // (shards * shares), width)
    return part.transpose(1, 0, 3, 2, 4).reshape(depth, shares * width)


def mix_slab(whole_grad, shards, shares):
    depth, full = whole_grad.shape
    width = full // shares
    part = whole_grad.reshape(shards, shares, depth // (shards * shares), shares, width)
    return part.transpose(1, 0, 3, 2, 4).reshape(1, shares, depth, width)


def added(a, b):
    return (a.astype(F32) + b.astype(F32)).astype(BF16)


def picked(a, index, axis):
    return lax.dynamic_index_in_dim(a, index, axis, keepdims=False)


def fold(a, axis, name, bit):
    size = lax.axis_size(name)
    mine = (lax.axis_index(name) >> bit) & 1
    sent = lax.ppermute(
        picked(a, 1 - mine, axis), name, [(i, i ^ (1 << bit)) for i in range(size)]
    )
    return added(picked(a, mine, axis), sent)


def reduce_slabs(g, head_first):
    ns, shares, depth, width = g.shape
    clips, ways = lax.axis_size("clip"), lax.axis_size("seq")
    r = depth // (clips * ways)
    a = g.reshape(ns, shares, clips // 2, 2, ways, r, width)
    a = fold(a, 3, "clip", 0)

    def by_head(a):
        return fold(a, 1, "head", 0)

    def by_clip(a, axis):
        bits = int(math.log2(clips)) - 1
        for bit in range(bits):
            shape = a.shape
            a = a.reshape(shape[:axis] + (shape[axis] // 2, 2) + shape[axis + 1 :])
            a = fold(a, axis + 1, "clip", bit + 1)
        return a.reshape(a.shape[:axis] + a.shape[axis + 1 :])

    if head_first:
        a = by_clip(by_head(a), 1)
    else:
        a = by_head(by_clip(a, 2))
    a = a.transpose(1, 0, 2, 3)
    parts = lax.all_to_all(a, "seq", split_axis=0, concat_axis=0, tiled=True)
    return jnp.sum(parts.astype(F32), axis=0)


def gather_norms(gain, bias):
    layers, norms, part = gain.shape
    both = jnp.concatenate((gain, bias), axis=1).reshape(1, -1)
    count = lax.axis_size("clip") * lax.axis_size("seq") * lax.axis_size("head")
    width = round_up(both.shape[1], 128)
    padded = jnp.pad(both, ((0, 0), (0, width - both.shape[1])))
    every = lax.all_to_all(
        jnp.broadcast_to(padded, (count, width)), ALL, split_axis=0, concat_axis=0, tiled=True
    )[:, : both.shape[1]]
    return every.reshape(count, layers * 2 * norms, part).transpose(1, 0, 2).reshape(layers, 2 * norms, -1)


def reduce_norms(sums):
    count = lax.axis_size("clip") * lax.axis_size("seq") * lax.axis_size("head")
    rows, features = sums.shape
    part = features // count
    a = sums.reshape(rows, count, part).transpose(1, 0, 2).reshape(count, rows * part)
    width = round_up(rows * part, 128)
    a = jnp.pad(a, ((0, 0), (0, width - rows * part)))
    every = lax.all_to_all(a, ALL, split_axis=0, concat_axis=0, tiled=True)
    return jnp.sum(every, axis=0)[: rows * part].reshape(rows, part)


def on_device(
    tokens,
    cotangent,
    time_qkv,
    time_out,
    time_mix,
    space_qkv,
    space_out,
    mlp_in,
    mlp_out,
    norm_gain,
    norm_bias,
):
    layers = time_qkv.shape[0]
    clips, frames, places, d = tokens.shape
    ways = lax.axis_size("seq")
    shards = lax.axis_size("clip") * ways
    rows = Rows(clips * frames, places, ways)
    shares = lax.axis_size("head")

    def as_rows(a):
        a = a.astype(F32).reshape(rows.frames, places, d)
        a = jnp.pad(a, ((0, 0), (0, rows.frame_rows - places), (0, 0)))
        return a.reshape(rows.rows, d)

    def from_rows(a):
        a = a.reshape(rows.frames, rows.frame_rows, d)[:, :places]
        return a.reshape(tokens.shape)

    gbs = gather_norms(norm_gain, norm_bias)
    gb = [gbs[l] for l in range(layers)]
    weights = [
        gather_slabs(
            pack_layer(
                time_qkv[l], time_out[l], time_mix[l], space_qkv[l], space_out[l], mlp_in[l], mlp_out[l]
            )
        )
        for l in range(layers)
    ]
    mixes = [mix_whole(w[-1], shards) for w in weights]

    x = as_rows(tokens)
    send = send_first(rows, x, gb[0])
    kept = []
    for l in range(layers):
        w = weights[l]
        a1 = swap_places(send)
        qkv1, o1_time, log1 = time_forward(rows, a1, w, shares)
        back = swap_places(o1_time)
        o1, y1, x1, qkv2 = middle_forward(rows, back, x, w, mixes[l], gb[l])
        o2, x2, log2 = space_forward(rows, qkv2, x1, w)
        kept.append((x, a1, qkv1, log1, o1, y1, x1, qkv2, o2, log2, x2))
        if l + 1 < layers:
            x, send = mlp_forward(rows, x2, w, gb[l], gb[l + 1])
        else:
            (x,) = mlp_forward(rows, x2, w, gb[l], None)
    output = from_rows(x).astype(BF16)

    grad = as_rows(cotangent)
    results = [None] * layers
    norm_rows = [None] * layers
    for l in reversed(range(layers)):
        w = weights[l]
        x, a1, qkv1, log1, o1, y1, x1, qkv2, o2, log2, x2 = kept[l]
        grad, g_in, g_out, s3 = mlp_backward(rows, grad, x2, w, gb[l])
        grad, g_so, g_sq, s2 = space_backward(rows, grad, x1, qkv2, o2, log2, w, gb[l])
        do1, g_mix, g_to = middle_backward(rows, grad, y1, o1, w, mixes[l])
        da1, g_tq = time_backward(rows, swap_places(do1), a1, qkv1, log1, w)
        grad, s1 = first_norm_back(rows, swap_places(da1), x, grad, gb[l])
        results[l] = (
            reduce_slabs(g_in, True),
            reduce_slabs(g_out, False),
            reduce_slabs(jnp.concatenate((g_so, g_sq), axis=0), True),
            reduce_slabs(jnp.concatenate((g_to, mix_slab(g_mix, shards, shares)), axis=0), False),
            reduce_slabs(g_tq, True),
        )
        norm_rows[l] = jnp.concatenate((s1[0:1], s2[0:1], s3[0:1], s1[1:2], s2[1:2], s3[1:2]), axis=0)
    tokens_grad = from_rows(grad)
    norm_sums = reduce_norms(jnp.concatenate(norm_rows, axis=0)).reshape(layers, 2, 3, -1)

    def stacked(form):
        return jnp.stack([form(*results[l]) for l in range(layers)])

    def rows_of(a):
        return a.transpose(1, 0, 2)

    def flat(a):
        return rows_of(a).reshape(a.shape[1], -1)

    def mix_rows(a):
        r, width = a.shape
        return a.reshape(shares, r // shares, width).transpose(1, 0, 2).reshape(r // shares, -1)

    return (
        output,
        tokens_grad,
        stacked(lambda gi, go, s, t, q: rows_of(q)),
        stacked(lambda gi, go, s, t, q: t[0].T),
        stacked(lambda gi, go, s, t, q: mix_rows(t[1])),
        stacked(lambda gi, go, s, t, q: rows_of(s[1:])),
        stacked(lambda gi, go, s, t, q: s[0].T),
        stacked(lambda gi, go, s, t, q: flat(gi)),
        stacked(lambda gi, go, s, t, q: flat(go).T),
        norm_sums[:, 0],
        norm_sums[:, 1],
    )


def solution(mesh):
    token_spec = P(("clip", "head"), "seq", None, None)
    in_specs = (
        token_spec,
        token_spec,
        P(None, ("clip", "seq"), None, "head"),
        P(None, "head", ("clip", "seq")),
        P(None, ("clip", "seq", "head"), None),
        P(None, ("clip", "seq"), None, "head"),
        P(None, "head", ("clip", "seq")),
        P(None, ("clip", "seq"), "head"),
        P(None, "head", ("clip", "seq")),
        P(None, None, ("clip", "seq", "head")),
        P(None, None, ("clip", "seq", "head")),
    )
    return jax.shard_map(
        on_device, mesh=mesh, in_specs=in_specs, out_specs=in_specs, check_vma=False
    )
```

time: 2770 us -> 909 us (0.33)
  waiting for transfers between devices: 1810 us -> 334 us
  blocking collectives: 361 us -> 26.7 us
  Pallas kernels: 0 us -> 235 us
  matrix products: 208 us -> 0 us
  local copies, waits for them, and re-layouts: 274 us -> 108 us
  starting transfers between devices: 31.8 us -> 105 us
    reduce_scatter x16 -> x0, waiting for transfers between devices: 862 us -> none  [the longest x2 206 us: on_device(): lax.psum_scatter(whole_grads[0], ('clip', 'seq', 'head'), scatter_dimensi...]
    all_gather x22 -> x2, waiting for transfers between devices: 536 us -> 165 us  [gather_slabs(): full = lax.all_gather(pack, ('head', 'clip', 'seq'), axis=1, tiled=True)]
    unnamed x58 -> x2, waiting for transfers between devices: 344 us -> 0.03 us
    all_gather x6 -> x0, blocking collectives: 303 us -> none  [the longest x2 86.1 us: on_device(): lax.all_gather(space_out[layer_index], ('clip', 'seq'), axis=1, tiled=True)]
    pallas_call x0 -> x19, Pallas kernels: none -> 235 us  [call(): pl.pallas_call(body, out_shape=[shape for shape, _ in outs], grid=grid, i...]
    dot_general x66 -> x0, matrix products: 208 us -> none  [matmul(): return jnp.einsum(form, left, right, preferred_element_type=jnp.float32)]
    unnamed x340 -> x159, local copies, waits for them, and re-layouts: 149 us -> 26.3 us
    ppermute x0 -> x30, waiting for transfers between devices: none -> 94.8 us  [fold(): lax.ppermute(picked(a, 1 - mine, axis), name, [(i, i ^ 1 << bit) for i in...]
  transfers between devices with their start and end apart: 55 -> 51, of which waited for: 39 -> 21; matrix products, arithmetic and copies ran while one was open for 17% -> 18% of each run, Pallas kernels for 0% -> 16%
where the time goes in v1:
time: 909 us; the launch traced here: 902 us
  waiting for transfers between devices  334 us (37%)
  Pallas kernels  235 us (26%)
  local copies, waits for them, and re-layouts  108 us (12%)
  starting transfers between devices  105 us (12%)
  other arithmetic  78 us (9%)
  blocking collectives  26.7 us (3%)
  between operations  15.7 us (2%)
    pallas_call x19, Pallas kernels, call(): pl.pallas_call(body, out_shape=[shape for shape, _ in outs], grid=grid, i...  235 us
    all_gather x2, waiting for transfers between devices, gather_slabs(): full = lax.all_gather(pack, ('head', 'clip', 'seq'), axis=1, tiled=True)  165 us
    ppermute x30, waiting for transfers between devices, fold(): lax.ppermute(picked(a, 1 - mine, axis), name, [(i, i ^ 1 << bit) for i in...  94.8 us
    all_to_all x10, starting transfers between devices, reduce_slabs(): parts = lax.all_to_all(a, 'seq', split_axis=0, concat_axis=0, tiled=True)  41.7 us
    all_to_all x7, waiting for transfers between devices, swap_places(): lax.all_to_all(rows_array, 'seq', split_axis=0, concat_axis=0, tiled=True)  39 us
    convert_element_type x20, other arithmetic, added(): return (a.astype(F32) + b.astype(F32)).astype(BF16)  38.6 us
    all_to_all x7, starting transfers between devices, swap_places(): lax.all_to_all(rows_array, 'seq', split_axis=0, concat_axis=0, tiled=True)  30.5 us
    dynamic_slice x16, local copies, waits for them, and re-layouts, picked(): return lax.dynamic_index_in_dim(a, index, axis, keepdims=False)  28.8 us
  transfers between devices with their start and end apart: 51, of which 21 were waited for; matrix products, arithmetic and copies ran while one was open for 18% of the time, Pallas kernels for 16%

profile of v1, /device:TPU:0, one launch (start us, length us, event | category | flops | bytes accessed | tf_op | source)
XLA Modules:
  0.0 901.6 jit_solution(15639554946667645961)
XLA Ops:
  12.4 7.3 all-to-all-start
  21.1 6.0 all-to-all-done
  31.0 26.7 %all_to_all.156 = bf16[4,104,768]{2,1,0:T(8,128)(2,1)} all-to-all(bf16[4,104,768]{2,1,0:T(8,128)(2,1)} %bitcast.438), channel_id=1, replica_groups=mesh['clip'=4,'seq'=4,'head'=2] {'seq'}, dimensions={0} | all-to-all | bytes 1277952 | tf_op jit(solution)/shard_map/all_to_all | solution.py:649
  57.8 90.8 %all-gather.3.cloned.1.call-done = bf16[17,1536,384]{2,1,0:T(8,128)(2,1)} async-done(((bf16[17,48,384]{2,1,0:T(8,128)(2,1)}), bf16[17,1536,384]{2,1,0:T(8,128)(2,1)}) %all-gather.3.cloned.1.call-update) | async-done | bytes 20054032 | tf_op jit(solution)/shard_map/all_gather | solution.py:676
  148.5 12.0 %shard_map.195 = (bf16[3,416,768]{2,1,0:T(8,128)(2,1)}, bf16[416,768]{1,0:T(8,128)(2,1)}, f32[2,3,2,416]{3,2,1,0:T(2,128)}) custom-call(bf16[416,768]{1,0:T(8,128)(2,1)} %bitcast.409, bf16[17,2,768,384]{3,2,1,0:T(8,128)(2,1)} %bitcast.375), custom_call_target="tpu_custom_call" | custom-call | flops 1472200704 | bytes 23268864 | tf_op jit(solution)/shard_map/pallas_call | solution.py:153
  168.7 21.0 %all-to-all-done.2 = bf16[4,104,768]{2,1,0:T(8,128)(2,1)S(1)} async-done(((bf16[4,104,768]{2,1,0:T(8,128)(2,1)}), bf16[4,104,768]{2,1,0:T(8,128)(2,1)S(1)}, u32[]{:S(2)}, u32[]{:S(2)}) %all-to-all-start.2) | async-done | bytes 639008 | tf_op jit(solution)/shard_map/all_to_all | solution.py:649
  190.5 9.3 %shard_map.196 = (bf16[416,768]{1,0:T(8,128)(2,1)}, bf16[416,768]{1,0:T(8,128)(2,1)}, f32[416,768]{1,0:T(8,128)}, bf16[3,416,768]{2,1,0:T(8,128)(2,1)}) custom-call(bf16[416,768]{1,0:T(8,128)(2,1)} %bitcast.436, f32[416,768]{1,0:T(8,128)} %bitcast_convert_fusion.1.x_ref, bf16[17,2,768,384]{3,2,1,0:T(8,128)(2,1)} %bitcast.376, ...), custom_call_target="tpu_custom_call" | custom-call | flops 2453667840 | bytes 47695872 | tf_op jit(solution)/shard_map/pallas_call | solution.py:153
  199.9 9.9 %shard_map.197 = (bf16[416,768]{1,0:T(8,128)(2,1)}, f32[416,768]{1,0:T(8,128)}, f32[2,3,2,2,208]{4,3,2,1,0:T(2,128)}) custom-call(bf16[3,416,768]{2,1,0:T(8,128)(2,1)} %get-tuple-element.64.qkv_ref, f32[416,768]{1,0:T(8,128)} %get-tuple-element.65.x1_ref, bf16[17,2,768,384]{3,2,1,0:T(8,128)(2,1)} %bitcast.378), custom_call_target="tpu_custom_call" | custom-call | flops 490733568 | bytes 25185792 | tf_op jit(solution)/shard_map/pallas_call | solution.py:153
  209.8 13.2 %shard_map.198 = (f32[416,768]{1,0:T(8,128)}, bf16[416,768]{1,0:T(8,128)(2,1)}) custom-call(f32[416,768]{1,0:T(8,128)} %get-tuple-element.66.x2_ref, bf16[17,2,768,384]{3,2,1,0:T(8,128)(2,1)} %bitcast.379, bf16[17,2,768,384]{3,2,1,0:T(8,128)(2,1)} %bitcast.380, f32[6,768]{1,0:T(8,128)} %squeeze.185.gb_ref, f32[6,768]{1,0:T(8,128)} %squeeze.191.rest_0_.gb_ref), custom_call_target="tpu_custom_call" | custom-call | flops 3925868544 | bytes 43339776 | tf_op jit(solution)/shard_map/pallas_call | solution.py:153
  226.5 74.3 %all-gather.5.cloned.1.call-done = bf16[17,1536,384]{2,1,0:T(8,128)(2,1)} async-done(((bf16[17,48,384]{2,1,0:T(8,128)(2,1)}), bf16[17,1536,384]{2,1,0:T(8,128)(2,1)}) %all-gather.5.cloned.1.call-update) | async-done | bytes 20054032 | tf_op jit(solution)/shard_map/all_gather | solution.py:676
  301.7 12.0 %shard_map.199 = (bf16[3,416,768]{2,1,0:T(8,128)(2,1)}, bf16[416,768]{1,0:T(8,128)(2,1)}, f32[2,3,2,416]{3,2,1,0:T(2,128)}) custom-call(bf16[416,768]{1,0:T(8,128)(2,1)} %bitcast.411, bf16[17,2,768,384]{3,2,1,0:T(8,128)(2,1)} %bitcast.387), custom_call_target="tpu_custom_call" | custom-call | flops 1472200704 | bytes 23268864 | tf_op jit(solution)/shard_map/pallas_call | solution.py:153
  322.6 12.7 %all-to-all-done.4 = bf16[4,104,768]{2,1,0:T(8,128)(2,1)S(1)} async-done(((bf16[4,104,768]{2,1,0:T(8,128)(2,1)}), bf16[4,104,768]{2,1,0:T(8,128)(2,1)S(1)}, u32[]{:S(2)}, u32[]{:S(2)}) %all-to-all-start.4) | async-done | bytes 639008 | tf_op jit(solution)/shard_map/all_to_all | solution.py:649
  336.2 8.8 shard_map.200
  345.0 9.9 %shard_map.201 = (bf16[416,768]{1,0:T(8,128)(2,1)}, f32[416,768]{1,0:T(8,128)}, f32[2,3,2,2,208]{4,3,2,1,0:T(2,128)}) custom-call(bf16[3,416,768]{2,1,0:T(8,128)(2,1)} %get-tuple-element.70.qkv_ref, f32[416,768]{1,0:T(8,128)} %get-tuple-element.71.x1_ref, bf16[17,2,768,384]{3,2,1,0:T(8,128)(2,1)} %bitcast.390), custom_call_target="tpu_custom_call" | custom-call | flops 490733568 | bytes 25185792 | tf_op jit(solution)/shard_map/pallas_call | solution.py:153
  354.9 12.1 %shard_map.202 = f32[416,768]{1,0:T(8,128)} custom-call(f32[416,768]{1,0:T(8,128)} %get-tuple-element.72.x2_ref, bf16[17,2,768,384]{3,2,1,0:T(8,128)(2,1)} %bitcast.391, bf16[17,2,768,384]{3,2,1,0:T(8,128)(2,1)} %bitcast.392, f32[6,768]{1,0:T(8,128)} %squeeze.191.rest_0_.gb_ref), custom_call_target="tpu_custom_call" | custom-call | flops 3925868544 | bytes 42682368 | tf_op jit(solution)/shard_map/pallas_call | solution.py:153
  366.9 21.8 %shard_map.203 = (f32[416,768]{1,0:T(8,128)}, bf16[4,2,768,384]{3,2,1,0:T(8,128)(2,1)}, bf16[4,2,768,384]{3,2,1,0:T(8,128)(2,1)}, f32[2,768]{1,0:T(2,128)}) custom-call(f32[416,768]{1,0:T(8,128)} %bitcast_convert_fusion.g_ref, f32[416,768]{1,0:T(8,128)} %get-tuple-element.72.x2_ref, bf16[17,2,768,384]{3,2,1,0:T(8,128)(2,1)} %bitcast.393, ...), custom_call_target="tpu_custom_call" | custom-call | flops 9814671360 | bytes 53403648 | tf_op jit(solution)/shard_map/pallas_call | solution.py:153
  388.7 21.7 %shard_map.204 = (f32[416,768]{1,0:T(8,128)}, bf16[1,2,768,384]{3,2,1,0:T(8,128)(2,1)}, bf16[3,2,768,384]{3,2,1,0:T(8,128)(2,1)}, f32[2,768]{1,0:T(2,128)}) custom-call(f32[416,768]{1,0:T(8,128)} %get-tuple-element.73.g_ref, f32[416,768]{1,0:T(8,128)} %get-tuple-element.71.x1_ref, bf16[3,416,768]{2,1,0:T(8,128)(2,1)} %get-tuple-element.70.qkv_ref, ...), custom_call_target="tpu_custom_call" | custom-call | flops 3925868544 | bytes 51260928 | tf_op jit(solution)/shard_map/pallas_call | solution.py:153
  410.5 6.7 shard_map.205
  439.4 17.9 %shard_map.206 = (bf16[416,768]{1,0:T(8,128)(2,1)}, bf16[3,2,768,384]{3,2,1,0:T(8,128)(2,1)}) custom-call(bf16[416,768]{1,0:T(8,128)(2,1)} %bitcast.57.do_ref, bf16[416,768]{1,0:T(8,128)(2,1)} %bitcast.412, bf16[3,416,768]{2,1,0:T(8,128)(2,1)} %get-tuple-element.80.qkv_ref, f32[2,3,2,416]{3,2,1,0:T(2,128)} %get-tuple-element.81.log_ref, ...), custom_call_target="tpu_custom_call" | custom-call | flops 2944401408 | bytes 27446784 | tf_op jit(solution)/shard_map/pallas_call | solution.py:153
  457.4 5.5 all-to-all-start.6
  469.2 11.0 %collective-permute-done.10 = bf16[2,2,1,4,48,384]{5,4,3,2,1,0:T(8,128)(2,1)S(1)} collective-permute-done((bf16[2,2,1,4,48,384]{5,4,3,2,1,0:T(8,128)(2,1)S(1)}, bf16[2,2,1,4,48,384]{5,4,3,2,1,0:T(8,128)(2,1)S(1)}, u32[]{:S(2)}, u32[]{:S(2)}) %collective-permute-start.10) | collective-permute-done | bytes 589856 | tf_op jit(solution)/shard_map/ppermute | solution.py:704
  487.6 21.8 %shard_map.208 = (f32[416,768]{1,0:T(8,128)}, bf16[4,2,768,384]{3,2,1,0:T(8,128)(2,1)}, bf16[4,2,768,384]{3,2,1,0:T(8,128)(2,1)}, f32[2,768]{1,0:T(2,128)}) custom-call(f32[416,768]{1,0:T(8,128)} %get-tuple-element.83.g_ref, f32[416,768]{1,0:T(8,128)} %get-tuple-element.66.x2_ref, bf16[17,2,768,384]{3,2,1,0:T(8,128)(2,1)} %bitcast.381, ...), custom_call_target="tpu_custom_call" | custom-call | flops 9814671360 | bytes 53403648 | tf_op jit(solution)/shard_map/pallas_call | solution.py:153
  509.4 21.7 %shard_map.209 = (f32[416,768]{1,0:T(8,128)}, bf16[1,2,768,384]{3,2,1,0:T(8,128)(2,1)}, bf16[3,2,768,384]{3,2,1,0:T(8,128)(2,1)}, f32[2,768]{1,0:T(2,128)}) custom-call(f32[416,768]{1,0:T(8,128)} %get-tuple-element.84.g_ref, f32[416,768]{1,0:T(8,128)} %get-tuple-element.65.x1_ref, bf16[3,416,768]{2,1,0:T(8,128)(2,1)} %get-tuple-element.64.qkv_ref, ...), custom_call_target="tpu_custom_call" | custom-call | flops 3925868544 | bytes 51260928 | tf_op jit(solution)/shard_map/pallas_call | solution.py:153
  532.5 6.8 shard_map.210
  598.6 5.3 all-to-all-done.7
  604.0 18.0 %shard_map.211 = (bf16[416,768]{1,0:T(8,128)(2,1)}, bf16[3,2,768,384]{3,2,1,0:T(8,128)(2,1)}) custom-call(bf16[416,768]{1,0:T(8,128)(2,1)} %bitcast.61.do_ref, bf16[416,768]{1,0:T(8,128)(2,1)} %bitcast.410, bf16[3,416,768]{2,1,0:T(8,128)(2,1)} %get-tuple-element.91.qkv_ref, f32[2,3,2,416]{3,2,1,0:T(2,128)} %get-tuple-element.92.log_ref, ...), custom_call_target="tpu_custom_call" | custom-call | flops 2944401408 | bytes 27446784 | tf_op jit(solution)/shard_map/pallas_call | solution.py:153
  643.6 11.6 %collective-permute-done.4 = bf16[3,2,4,48,384]{4,3,0,2,1:T(8,128)(2,1)S(1)} collective-permute-done((bf16[3,2,4,48,384]{4,3,0,2,1:T(8,128)(2,1)S(1)}, bf16[3,2,4,48,384]{4,3,0,2,1:T(8,128)(2,1)S(1)}, u32[]{:S(2)}, u32[]{:S(2)}) %collective-permute-start.4) | collective-permute-done | bytes 884768 | tf_op jit(solution)/shard_map/ppermute | solution.py:704
  755.1 41.3 %collective-permute-done.1 = bf16[3,2,4,48,384]{4,3,0,2,1:T(8,128)(2,1)} collective-permute-done((bf16[3,2,4,48,384]{4,3,0,2,1:T(8,128)(2,1)}, bf16[3,2,4,48,384]{4,3,0,2,1:T(8,128)(2,1)}, u32[]{:S(2)}, u32[]{:S(2)}) %collective-permute-start.1) | collective-permute-done | bytes 884768 | tf_op jit(solution)/shard_map/ppermute | solution.py:704
  808.5 6.9 collective-permute-done.2
  828.0 5.9 all-to-all-done.9
  858.0 13.4 %collective-permute-done.26 = bf16[4,4,48,384]{3,2,0,1:T(8,128)(2,1)S(1)} collective-permute-done((bf16[4,4,48,384]{3,2,0,1:T(8,128)(2,1)S(1)}, bf16[4,4,48,384]{3,2,0,1:T(8,128)(2,1)S(1)}, u32[]{:S(2)}, u32[]{:S(2)}) %collective-permute-start.26) | collective-permute-done | bytes 589856 | tf_op jit(solution)/shard_map/ppermute | solution.py:704
  880.6 10.6 %all-to-all-done.17 = bf16[4,4,48,384]{3,2,1,0:T(8,128)(2,1)S(1)} async-done(((bf16[4,4,48,384]{3,2,1,0:T(8,128)(2,1)}), bf16[4,4,48,384]{3,2,1,0:T(8,128)(2,1)S(1)}, u32[]{:S(2)}, u32[]{:S(2)}) %all-to-all-start.17) | async-done | bytes 589856 | tf_op jit(solution)/shard_map/all_to_all | solution.py:733
  (412 shorter events, 311.8 us)
Async XLA Ops:
  7.2 141.3 %all-gather.3.cloned.1.call-start = ((), (), s32[]{:S(2)}) async-start(), calls=%async_computation.20 | async-start | bytes 20680704 | tf_op jit(solution)/shard_map/all_gather | solution.py:676
  10.6 290.1 %all-gather.5.cloned.1.call-start = ((), (), s32[]{:S(2)}) async-start(), calls=%async_computation.21 | async-start | bytes 20680704 | tf_op jit(solution)/shard_map/all_gather | solution.py:676
  160.5 29.1 %all-to-all-start.2 = ((bf16[4,104,768]{2,1,0:T(8,128)(2,1)}), bf16[4,104,768]{2,1,0:T(8,128)(2,1)S(1)}, u32[]{:S(2)}, u32[]{:S(2)}) async-start(bf16[4,104,768]{2,1,0:T(8,128)(2,1)} %bitcast.461), calls=%async_computation.2 | async-start | bytes 1277952 | tf_op jit(solution)/shard_map/all_to_all | solution.py:649
  223.0 77.8 %all-to-all-start.3 = ((bf16[4,104,768]{2,1,0:T(8,128)(2,1)}), bf16[4,104,768]{2,1,0:T(8,128)(2,1)S(1)}, u32[]{:S(2)}, u32[]{:S(2)}) async-start(bf16[4,104,768]{2,1,0:T(8,128)(2,1)} %bitcast.462), calls=%async_computation.3 | async-start | bytes 1277952 | tf_op jit(solution)/shard_map/all_to_all | solution.py:649
  417.2 22.2 %all-to-all-start.5 = ((bf16[4,104,768]{2,1,0:T(8,128)(2,1)}), bf16[4,104,768]{2,1,0:T(8,128)(2,1)}, u32[]{:S(2)}, u32[]{:S(2)}) async-start(bf16[4,104,768]{2,1,0:T(8,128)(2,1)} %bitcast.459), calls=%async_computation.5 | async-start | bytes 1277952 | tf_op jit(solution)/shard_map/all_to_all | solution.py:649
  426.5 36.4 %collective-permute-start.9 = (bf16[2,2,2,4,48,384]{5,4,3,2,1,0:T(8,128)(2,1)}, bf16[2,2,2,4,48,384]{5,4,3,2,1,0:T(8,128)(2,1)}, u32[]{:S(2)}, u32[]{:S(2)}) collective-permute-start(bf16[2,2,2,4,48,384]{5,4,3,2,1,0:T(8,128)(2,1)} %fusion.17), channel_id=1, source_target_pairs={{0,8},{8,0},{16,24},{24,16},{1,9},{9,1},{17,25},{25,17},{2,10},{10... | collective-permute-start | bytes 3538952 | tf_op jit(solution)/shard_map/ppermute | solution.py:704
  431.6 134.5 %collective-permute-start.15 = (bf16[4,2,2,4,48,384]{5,4,0,3,2,1:T(8,128)(2,1)}, bf16[4,2,2,4,48,384]{5,4,0,3,2,1:T(8,128)(2,1)}, u32[]{:S(2)}, u32[]{:S(2)}) collective-permute-start(bf16[4,2,2,4,48,384]{5,4,0,3,2,1:T(8,128)(2,1)} %bitcast.362), channel_id=1, source_target_pairs={{0,8},{8,0},{16,24},{24,16},{1,9},{9,1},{17,25},{25,17},{2,10},{10... | collective-permute-start | bytes 7077896 | tf_op jit(solution)/shard_map/ppermute | solution.py:704
  435.3 135.2 %collective-permute-start.21 = (bf16[4,2,2,4,48,384]{5,4,0,3,2,1:T(8,128)(2,1)}, bf16[4,2,2,4,48,384]{5,4,0,3,2,1:T(8,128)(2,1)}, u32[]{:S(2)}, u32[]{:S(2)}) collective-permute-start(bf16[4,2,2,4,48,384]{5,4,0,3,2,1:T(8,128)(2,1)} %bitcast.360), channel_id=1, source_target_pairs={{0,8},{8,0},{16,24},{24,16},{1,9},{9,1},{17,25},{25,17},{2,10},{10... | collective-permute-start | bytes 7077896 | tf_op jit(solution)/shard_map/ppermute | solution.py:704
  439.4 136.9 %collective-permute-start.27 = (bf16[4,2,2,4,48,384]{5,4,0,3,2,1:T(8,128)(2,1)}, bf16[4,2,2,4,48,384]{5,4,0,3,2,1:T(8,128)(2,1)}, u32[]{:S(2)}, u32[]{:S(2)}) collective-permute-start(bf16[4,2,2,4,48,384]{5,4,0,3,2,1:T(8,128)(2,1)} %bitcast.358), channel_id=1, source_target_pairs={{0,8},{8,0},{16,24},{24,16},{1,9},{9,1},{17,25},{25,17},{2,10},{10... | collective-permute-start | bytes 7077896 | tf_op jit(solution)/shard_map/ppermute | solution.py:704
  457.4 25.3 %all-to-all-start.6 = ((bf16[4,104,768]{2,1,0:T(8,128)(2,1)}), bf16[4,104,768]{2,1,0:T(8,128)(2,1)S(1)}, u32[]{:S(2)}, u32[]{:S(2)}) async-start(bf16[4,104,768]{2,1,0:T(8,128)(2,1)} %bitcast.460), calls=%async_computation.6 | async-start | bytes 1277952 | tf_op jit(solution)/shard_map/all_to_all | solution.py:649
  469.2 123.4 %collective-permute-start.3 = (bf16[3,2,2,4,48,384]{5,4,0,3,2,1:T(8,128)(2,1)}, bf16[3,2,2,4,48,384]{5,4,0,3,2,1:T(8,128)(2,1)}, u32[]{:S(2)}, u32[]{:S(2)}) collective-permute-start(bf16[3,2,2,4,48,384]{5,4,0,3,2,1:T(8,128)(2,1)} %bitcast.364), channel_id=1, source_target_pairs={{0,8},{8,0},{16,24},{24,16},{1,9},{9,1},{17,25},{25,17},{2,10},{10... | collective-permute-start | bytes 5308424 | tf_op jit(solution)/shard_map/ppermute | solution.py:704
  481.3 78.2 %collective-permute-start.11 = (bf16[2,4,48,384]{3,2,1,0:T(8,128)(2,1)}, bf16[2,4,48,384]{3,2,1,0:T(8,128)(2,1)}, u32[]{:S(2)}, u32[]{:S(2)}) collective-permute-start(bf16[2,4,48,384]{3,2,1,0:T(8,128)(2,1)} %dynamic-slice_bitcast_fusion.8), channel_id=1, source_target_pairs={{0,1},{1,0},{2,3},{3,2},{4,5},{5,4},{6,7},{7,6},{8,9},{9,8},{10,11... | collective-permute-start | bytes 884744 | tf_op jit(solution)/shard_map/ppermute | solution.py:704
  559.4 71.8 %collective-permute-start.6 = (bf16[2,2,2,4,48,384]{5,4,3,2,1,0:T(8,128)(2,1)}, bf16[2,2,2,4,48,384]{5,4,3,2,1,0:T(8,128)(2,1)}, u32[]{:S(2)}, u32[]{:S(2)}) collective-permute-start(bf16[2,2,2,4,48,384]{5,4,3,2,1,0:T(8,128)(2,1)} %fusion.21), channel_id=1, source_target_pairs={{0,8},{8,0},{16,24},{24,16},{1,9},{9,1},{17,25},{25,17},{2,10},{10... | collective-permute-start | bytes 3538952 | tf_op jit(solution)/shard_map/ppermute | solution.py:704
  566.0 152.7 %collective-permute-start.12 = (bf16[4,2,2,4,48,384]{5,4,0,3,2,1:T(8,128)(2,1)}, bf16[4,2,2,4,48,384]{5,4,0,3,2,1:T(8,128)(2,1)}, u32[]{:S(2)}, u32[]{:S(2)}) collective-permute-start(bf16[4,2,2,4,48,384]{5,4,0,3,2,1:T(8,128)(2,1)} %bitcast.443), channel_id=1, source_target_pairs={{0,8},{8,0},{16,24},{24,16},{1,9},{9,1},{17,25},{25,17},{2,10},{10... | collective-permute-start | bytes 7077896 | tf_op jit(solution)/shard_map/ppermute | solution.py:704
  570.4 62.8 %collective-permute-start.16 = (bf16[4,2,4,48,384]{4,3,0,2,1:T(8,128)(2,1)}, bf16[4,2,4,48,384]{4,3,0,2,1:T(8,128)(2,1)}, u32[]{:S(2)}, u32[]{:S(2)}) collective-permute-start(bf16[4,2,4,48,384]{4,3,0,2,1:T(8,128)(2,1)} %dynamic-slice_bitcast_fusion.2), channel_id=1, source_target_pairs={{0,1},{1,0},{2,3},{3,2},{4,5},{5,4},{6,7},{7,6},{8,9},{9,8},{10,11... | collective-permute-start | bytes 3538952 | tf_op jit(solution)/shard_map/ppermute | solution.py:704
  576.3 60.1 %collective-permute-start.22 = (bf16[4,2,4,48,384]{4,3,0,2,1:T(8,128)(2,1)}, bf16[4,2,4,48,384]{4,3,0,2,1:T(8,128)(2,1)}, u32[]{:S(2)}, u32[]{:S(2)}) collective-permute-start(bf16[4,2,4,48,384]{4,3,0,2,1:T(8,128)(2,1)} %dynamic-slice_bitcast_fusion), channel_id=1, source_target_pairs={{0,1},{1,0},{2,3},{3,2},{4,5},{5,4},{6,7},{7,6},{8,9},{9,8},{10,11... | collective-permute-start | bytes 3538952 | tf_op jit(solution)/shard_map/ppermute | solution.py:704
  581.2 22.8 %all-to-all-start.7 = ((bf16[4,104,768]{2,1,0:T(8,128)(2,1)}), bf16[4,104,768]{2,1,0:T(8,128)(2,1)}, u32[]{:S(2)}, u32[]{:S(2)}) async-start(bf16[4,104,768]{2,1,0:T(8,128)(2,1)} %bitcast.456), calls=%async_computation.7 | async-start | bytes 1277952 | tf_op jit(solution)/shard_map/all_to_all | solution.py:649
  592.6 46.8 %collective-permute-start.28 = (bf16[4,2,1,4,48,384]{5,4,0,3,2,1:T(8,128)(2,1)}, bf16[4,2,1,4,48,384]{5,4,0,3,2,1:T(8,128)(2,1)}, u32[]{:S(2)}, u32[]{:S(2)}) collective-permute-start(bf16[4,2,1,4,48,384]{5,4,0,3,2,1:T(8,128)(2,1)} %constant_dynamic-slice_fusion), channel_id=1, source_target_pairs={{0,16},{8,24},{16,0},{24,8},{1,17},{9,25},{17,1},{25,9},{2,18},{10... | collective-permute-start | bytes 3538952 | tf_op jit(solution)/shard_map/ppermute | solution.py:704
  622.0 38.1 %all-to-all-start.8 = ((bf16[4,104,768]{2,1,0:T(8,128)(2,1)}), bf16[4,104,768]{2,1,0:T(8,128)(2,1)}, u32[]{:S(2)}, u32[]{:S(2)}) async-start(bf16[4,104,768]{2,1,0:T(8,128)(2,1)} %bitcast.457), calls=%async_computation.8 | async-start | bytes 1277952 | tf_op jit(solution)/shard_map/all_to_all | solution.py:649
  631.2 98.0 %collective-permute-start.18 = (bf16[4,2,2,4,48,384]{5,4,0,3,2,1:T(8,128)(2,1)}, bf16[4,2,2,4,48,384]{5,4,0,3,2,1:T(8,128)(2,1)}, u32[]{:S(2)}, u32[]{:S(2)}) collective-permute-start(bf16[4,2,2,4,48,384]{5,4,0,3,2,1:T(8,128)(2,1)} %bitcast.361), channel_id=1, source_target_pairs={{0,8},{8,0},{16,24},{24,16},{1,9},{9,1},{17,25},{25,17},{2,10},{10... | collective-permute-start | bytes 7077896 | tf_op jit(solution)/shard_map/ppermute | solution.py:704
  633.2 21.9 %collective-permute-start.4 = (bf16[3,2,4,48,384]{4,3,0,2,1:T(8,128)(2,1)S(1)}, bf16[3,2,4,48,384]{4,3,0,2,1:T(8,128)(2,1)S(1)}, u32[]{:S(2)}, u32[]{:S(2)}) collective-permute-start(bf16[3,2,4,48,384]{4,3,0,2,1:T(8,128)(2,1)S(1)} %copy-done.46), channel_id=1, source_target_pairs={{0,1},{1,0},{2,3},{3,2},{4,5},{5,4},{6,7},{7,6},{8,9},{9,8},{10,11... | collective-permute-start | bytes 2654216 | tf_op jit(solution)/shard_map/ppermute | solution.py:704
  639.4 61.3 %collective-permute-start.17 = (bf16[4,1,4,48,384]{4,3,0,2,1:T(8,128)(2,1)}, bf16[4,1,4,48,384]{4,3,0,2,1:T(8,128)(2,1)}, u32[]{:S(2)}, u32[]{:S(2)}) collective-permute-start(bf16[4,1,4,48,384]{4,3,0,2,1:T(8,128)(2,1)} %constant_dynamic-slice_fusion.12), channel_id=1, source_target_pairs={{0,16},{8,24},{16,0},{24,8},{1,17},{9,25},{17,1},{25,9},{2,18},{10... | collective-permute-start | bytes 1769480 | tf_op jit(solution)/shard_map/ppermute | solution.py:704
  655.2 48.2 %collective-permute-start.23 = (bf16[4,1,4,48,384]{4,3,0,2,1:T(8,128)(2,1)}, bf16[4,1,4,48,384]{4,3,0,2,1:T(8,128)(2,1)}, u32[]{:S(2)}, u32[]{:S(2)}) collective-permute-start(bf16[4,1,4,48,384]{4,3,0,2,1:T(8,128)(2,1)} %constant_dynamic-slice_fusion.6), channel_id=1, source_target_pairs={{0,16},{8,24},{16,0},{24,8},{1,17},{9,25},{17,1},{25,9},{2,18},{10... | collective-permute-start | bytes 1769480 | tf_op jit(solution)/shard_map/ppermute | solution.py:704
  659.5 28.6 %collective-permute-start.8 = (bf16[2,4,48,384]{3,2,1,0:T(8,128)(2,1)}, bf16[2,4,48,384]{3,2,1,0:T(8,128)(2,1)}, u32[]{:S(2)}, u32[]{:S(2)}) collective-permute-start(bf16[2,4,48,384]{3,2,1,0:T(8,128)(2,1)} %dynamic-slice_bitcast_fusion.9), channel_id=1, source_target_pairs={{0,1},{1,0},{2,3},{3,2},{4,5},{5,4},{6,7},{7,6},{8,9},{9,8},{10,11... | collective-permute-start | bytes 884744 | tf_op jit(solution)/shard_map/ppermute | solution.py:704
  700.6 48.5 %collective-permute-start.24 = (bf16[4,2,2,4,48,384]{5,4,0,3,2,1:T(8,128)(2,1)}, bf16[4,2,2,4,48,384]{5,4,0,3,2,1:T(8,128)(2,1)}, u32[]{:S(2)}, u32[]{:S(2)}) collective-permute-start(bf16[4,2,2,4,48,384]{5,4,0,3,2,1:T(8,128)(2,1)} %bitcast.442), channel_id=1, source_target_pairs={{0,8},{8,0},{16,24},{24,16},{1,9},{9,1},{17,25},{25,17},{2,10},{10... | collective-permute-start | bytes 7077896 | tf_op jit(solution)/shard_map/ppermute | solution.py:704
  703.4 31.2 %collective-permute-start = (bf16[3,2,2,4,48,384]{5,4,0,3,2,1:T(8,128)(2,1)}, bf16[3,2,2,4,48,384]{5,4,0,3,2,1:T(8,128)(2,1)}, u32[]{:S(2)}, u32[]{:S(2)}) collective-permute-start(bf16[3,2,2,4,48,384]{5,4,0,3,2,1:T(8,128)(2,1)} %bitcast.444), channel_id=1, source_target_pairs={{0,8},{8,0},{16,24},{24,16},{1,9},{9,1},{17,25},{25,17},{2,10},{10... | collective-permute-start | bytes 5308424 | tf_op jit(solution)/shard_map/ppermute | solution.py:704
  724.3 79.2 %collective-permute-start.13 = (bf16[4,2,4,48,384]{4,3,0,2,1:T(8,128)(2,1)}, bf16[4,2,4,48,384]{4,3,0,2,1:T(8,128)(2,1)}, u32[]{:S(2)}, u32[]{:S(2)}) collective-permute-start(bf16[4,2,4,48,384]{4,3,0,2,1:T(8,128)(2,1)} %dynamic-slice_bitcast_fusion.3), channel_id=1, source_target_pairs={{0,1},{1,0},{2,3},{3,2},{4,5},{5,4},{6,7},{7,6},{8,9},{9,8},{10,11... | collective-permute-start | bytes 3538952 | tf_op jit(solution)/shard_map/ppermute | solution.py:704
  733.3 88.2 %collective-permute-start.19 = (bf16[4,2,4,48,384]{4,3,0,2,1:T(8,128)(2,1)}, bf16[4,2,4,48,384]{4,3,0,2,1:T(8,128)(2,1)}, u32[]{:S(2)}, u32[]{:S(2)}) collective-permute-start(bf16[4,2,4,48,384]{4,3,0,2,1:T(8,128)(2,1)} %dynamic-slice_bitcast_fusion.1), channel_id=1, source_target_pairs={{0,1},{1,0},{2,3},{3,2},{4,5},{5,4},{6,7},{7,6},{8,9},{9,8},{10,11... | collective-permute-start | bytes 3538952 | tf_op jit(solution)/shard_map/ppermute | solution.py:704
  738.5 58.0 %collective-permute-start.1 = (bf16[3,2,4,48,384]{4,3,0,2,1:T(8,128)(2,1)}, bf16[3,2,4,48,384]{4,3,0,2,1:T(8,128)(2,1)}, u32[]{:S(2)}, u32[]{:S(2)}) collective-permute-start(bf16[3,2,4,48,384]{4,3,0,2,1:T(8,128)(2,1)} %dynamic-slice_bitcast_fusion.5), channel_id=1, source_target_pairs={{0,1},{1,0},{2,3},{3,2},{4,5},{5,4},{6,7},{7,6},{8,9},{9,8},{10,11... | collective-permute-start | bytes 2654216 | tf_op jit(solution)/shard_map/ppermute | solution.py:704
  744.9 52.9 %all-to-all-start.16 = ((bf16[4,4,48,384]{3,2,1,0:T(8,128)(2,1)}), bf16[4,4,48,384]{3,2,1,0:T(8,128)(2,1)}, u32[]{:S(2)}, u32[]{:S(2)}) async-start(bf16[4,4,48,384]{3,2,1,0:T(8,128)(2,1)} %fusion.29), calls=%async_computation.16 | async-start | bytes 1179648 | tf_op jit(solution)/shard_map/all_to_all | solution.py:733
  752.6 93.1 %collective-permute-start.25 = (bf16[4,2,1,4,48,384]{5,4,0,3,2,1:T(8,128)(2,1)}, bf16[4,2,1,4,48,384]{5,4,0,3,2,1:T(8,128)(2,1)}, u32[]{:S(2)}, u32[]{:S(2)}) collective-permute-start(bf16[4,2,1,4,48,384]{5,4,0,3,2,1:T(8,128)(2,1)} %constant_dynamic-slice_fusion.3), channel_id=1, source_target_pairs={{0,16},{8,24},{16,0},{24,8},{1,17},{9,25},{17,1},{25,9},{2,18},{10... | collective-permute-start | bytes 3538952 | tf_op jit(solution)/shard_map/ppermute | solution.py:704
  824.2 24.1 %collective-permute-start.20 = (bf16[4,1,4,48,384]{4,3,0,2,1:T(8,128)(2,1)}, bf16[4,1,4,48,384]{4,3,0,2,1:T(8,128)(2,1)}, u32[]{:S(2)}, u32[]{:S(2)}) collective-permute-start(bf16[4,1,4,48,384]{4,3,0,2,1:T(8,128)(2,1)} %constant_dynamic-slice_fusion.9), channel_id=1, source_target_pairs={{0,16},{8,24},{16,0},{24,8},{1,17},{9,25},{17,1},{25,9},{2,18},{10... | collective-permute-start | bytes 1769480 | tf_op jit(solution)/shard_map/ppermute | solution.py:704
  (91 other events, 728.7 us)
Sparse Core Ops, SparseCore 0:
  11.1 137.3 all-gather.2
  151.6 149.1 all-gather.4

commit v2 on v1

--- a/solution.py
+++ b/solution.py
@@ -377,7 +377,7 @@
     per_share = (w.shape[0] - 9) // 2
     steps = shares * per_share
 
-    def body(g_ref, x2_ref, wi_ref, wo_ref, gb_ref, go_ref, gi_ref, gw_ref, sums_ref, a3_ref, a3t_ref, e3_ref, e3t_ref, u_ref):
+    def body(g_ref, x2_ref, wi_ref, wo_ref, gb_ref, go_ref, gw_ref, sums_ref, a3_ref, a3t_ref, e3_ref, e3t_ref, u_ref):
         j = pl.program_id(0)
 
         @pl.when(j == 0)
@@ -396,8 +396,8 @@
         act = (hid * phi).astype(BF16)
         slope = phi + hid * jnp.exp(-0.5 * hid * hid) * INV_ROOT_TAU
         dhid = (nn(e3_ref[...], wo_ref[0, 0]) * slope).astype(BF16)
-        gw_ref[0, 0] = nn(e3t_ref[...], act).astype(BF16)
-        gi_ref[0, 0] = nn(a3t_ref[...], dhid).astype(BF16)
+        gw_ref[1, 0, 0] = nn(e3t_ref[...], act).astype(BF16)
+        gw_ref[0, 0, 0] = nn(a3t_ref[...], dhid).astype(BF16)
         u_ref[...] += nt(dhid, wi_ref[0, 0])
 
         @pl.when(j == steps - 1)
@@ -406,13 +406,13 @@
             go_ref[...] = g_ref[...] + change
             sums_ref[...] = sums
 
-    slab_out = lambda: made(
-        (per_share, shares, d, width),
+    slab_out = made(
+        (2, per_share, shares, d, width),
         BF16,
-        (1, 1, d, width),
-        lambda j: (j % per_share, j // per_share, 0, 0),
-    )
-    return call(
+        (2, 1, 1, d, width),
+        lambda j: (0, j % per_share, j // per_share, 0, 0),
+    )
+    grad, slabs_grad, sums = call(
         body,
         (steps,),
         [
@@ -422,7 +422,7 @@
             ff_slab(8 + per_share, per_share, d, width),
             whole(gb.shape),
         ],
-        [made((t, d), F32), slab_out(), slab_out(), made((2, d), F32)],
+        [made((t, d), F32), slab_out, made((2, d), F32)],
         [
             pltpu.VMEM((t, d), BF16),
             pltpu.VMEM((d, t), BF16),
@@ -433,6 +433,7 @@
         (grad, x2, w, w, gb),
         flops=10 * t * d * width * steps,
     )
+    return grad, slabs_grad.reshape(2 * per_share, shares, d, width), sums
 
 
 def space_backward(rows, grad, x1, qkv, o2, logs, w, gb):
@@ -444,7 +445,7 @@
     rate = LOG2E * scale
     n = rows.frame_rows
 
-    def body(g_ref, x1_ref, qkv_ref, o2_ref, log_ref, wo_ref, wq_ref, gb_ref, go_ref, gw_ref, gq_ref, sums_ref, e2_ref, e2t_ref, a2t_ref, do_ref, dqkv_ref, u_ref):
+    def body(g_ref, x1_ref, qkv_ref, o2_ref, log_ref, wo_ref, wq_ref, gb_ref, go_ref, gq_ref, sums_ref, e2_ref, e2t_ref, a2t_ref, do_ref, dqkv_ref, u_ref):
         h = pl.program_id(0)
 
         @pl.when(h == 0)
@@ -457,7 +458,7 @@
             u_ref[...] = jnp.zeros((t, d), F32)
 
         bias = rows.space_bias()
-        gw_ref[0, 0] = nn(e2t_ref[...], o2_ref[...]).astype(BF16)
+        gq_ref[0, 0] = nn(e2t_ref[...], o2_ref[...]).astype(BF16)
         do_ref[...] = nn(e2_ref[...], wo_ref[0, 0]).astype(BF16)
 
         @pl.loop(0, pairs)
@@ -480,7 +481,7 @@
                     dqkv_ref[part, at, lanes] = grads[part]
 
         for part in range(3):
-            gq_ref[part, 0] = nn(a2t_ref[...], dqkv_ref[part]).astype(BF16)
+            gq_ref[part + 1, 0] = nn(a2t_ref[...], dqkv_ref[part]).astype(BF16)
             u_ref[...] += nt(dqkv_ref[part], wq_ref[part, 0])
 
         @pl.when(h == shares - 1)
@@ -504,8 +505,7 @@
         ],
         [
             made((t, d), F32),
-            made((1, shares, d, width), BF16, (1, 1, d, width), lambda h: (0, h, 0, 0)),
-            made((3, shares, d, width), BF16, (3, 1, d, width), lambda h: (0, h, 0, 0)),
+            made((4, shares, d, width), BF16, (4, 1, d, width), lambda h: (0, h, 0, 0)),
             made((2, d), F32),
         ],
         [
@@ -690,48 +690,89 @@
     return part.transpose(1, 0, 3, 2, 4).reshape(1, shares, depth, width)
 
 
-def added(a, b):
-    return (a.astype(F32) + b.astype(F32)).astype(BF16)
-
-
-def picked(a, index, axis):
-    return lax.dynamic_index_in_dim(a, index, axis, keepdims=False)
-
-
-def fold(a, axis, name, bit):
-    size = lax.axis_size(name)
-    mine = (lax.axis_index(name) >> bit) & 1
-    sent = lax.ppermute(
-        picked(a, 1 - mine, axis), name, [(i, i ^ (1 << bit)) for i in range(size)]
-    )
-    return added(picked(a, mine, axis), sent)
-
-
-def reduce_slabs(g, head_first):
+def total_of(terms):
+    result = terms[0].astype(F32)
+    for term in terms[1:]:
+        result = result + term.astype(F32)
+    return result
+
+
+class Part:
+    def __init__(self, terms, names):
+        self.terms = terms
+        self.names = list(names)
+
+    def axis_of(self, name):
+        if name == "h":
+            return "head", 0
+        return "clip", int(name[1:])
+
+    def picked(self, name, index):
+        axis = self.names.index(name)
+        return [lax.dynamic_index_in_dim(t, index, axis, keepdims=False) for t in self.terms]
+
+    def mine(self, name):
+        axis, bit = self.axis_of(name)
+        return (lax.axis_index(axis) >> bit) & 1
+
+    def to_send(self, name):
+        return total_of(self.picked(name, 1 - self.mine(name))).astype(BF16)
+
+    def take(self, name, sent):
+        axis, bit = self.axis_of(name)
+        size = lax.axis_size(axis)
+        got = lax.ppermute(sent, axis, [(i, i ^ (1 << bit)) for i in range(size)])
+        self.terms = self.picked(name, self.mine(name)) + [got]
+        self.names.remove(name)
+
+    def cut(self, first, last):
+        return Part([t[first:last] for t in self.terms], self.names)
+
+
+def reduction(g):
     ns, shares, depth, width = g.shape
     clips, ways = lax.axis_size("clip"), lax.axis_size("seq")
+    bits = int(math.log2(clips))
     r = depth // (clips * ways)
-    a = g.reshape(ns, shares, clips // 2, 2, ways, r, width)
-    a = fold(a, 3, "clip", 0)
-
-    def by_head(a):
-        return fold(a, 1, "head", 0)
-
-    def by_clip(a, axis):
-        bits = int(math.log2(clips)) - 1
-        for bit in range(bits):
-            shape = a.shape
-            a = a.reshape(shape[:axis] + (shape[axis] // 2, 2) + shape[axis + 1 :])
-            a = fold(a, axis + 1, "clip", bit + 1)
-        return a.reshape(a.shape[:axis] + a.shape[axis + 1 :])
-
-    if head_first:
-        a = by_clip(by_head(a), 1)
-    else:
-        a = by_head(by_clip(a, 2))
-    a = a.transpose(1, 0, 2, 3)
-    parts = lax.all_to_all(a, "seq", split_axis=0, concat_axis=0, tiled=True)
-    return jnp.sum(parts.astype(F32), axis=0)
+    chips = ["c%d" % b for b in reversed(range(1, bits))]
+    names = ["n", "h"] + chips + ["c0", "s", "r", "w"]
+    whole_part = Part([g.reshape((ns, shares) + (2,) * bits + (ways, r, width))], names)
+    (sent,) = yield (whole_part.to_send("c0"),)
+    whole_part.take("c0", sent)
+    half = (ns + 1) // 2
+    parts = (whole_part.cut(0, half), whole_part.cut(half, ns))
+    orders = (chips + ["h"], ["h"] + chips)
+    for step in range(bits):
+        sent = yield tuple(p.to_send(o[step]) for p, o in zip(parts, orders))
+        for p, o, one in zip(parts, orders, sent):
+            p.take(o[step], one)
+    both = [total_of(p.terms).astype(BF16).transpose(1, 0, 2, 3) for p in parts]
+    (sent,) = yield (jnp.concatenate(both, axis=1),)
+    got = lax.all_to_all(sent, "seq", split_axis=0, concat_axis=0, tiled=True)
+    yield jnp.sum(got.astype(F32), axis=0)
+
+
+class Line:
+    def __init__(self):
+        self.going = []
+        self.done = {}
+
+    def add(self, key, g):
+        way = reduction(g)
+        self.going.append([key, way, next(way)])
+
+    def move(self, x):
+        ready = [item[2] for item in self.going]
+        x, ready = lax.optimization_barrier((x, ready))
+        still = []
+        for (key, way, _), sent in zip(self.going, ready):
+            got = way.send(sent)
+            if isinstance(got, tuple):
+                still.append([key, way, got])
+            else:
+                self.done[key] = got
+        self.going = still
+        return x
 
 
 def gather_norms(gain, bias):
@@ -816,24 +857,28 @@
     output = from_rows(x).astype(BF16)
 
     grad = as_rows(cotangent)
-    results = [None] * layers
+    line = Line()
     norm_rows = [None] * layers
     for l in reversed(range(layers)):
         w = weights[l]
         x, a1, qkv1, log1, o1, y1, x1, qkv2, o2, log2, x2 = kept[l]
-        grad, g_in, g_out, s3 = mlp_backward(rows, grad, x2, w, gb[l])
-        grad, g_so, g_sq, s2 = space_backward(rows, grad, x1, qkv2, o2, log2, w, gb[l])
+        grad, g_ff, s3 = mlp_backward(rows, grad, x2, w, gb[l])
+        line.add(("ff", l), g_ff)
+        grad = line.move(grad)
+        grad, g_space, s2 = space_backward(rows, grad, x1, qkv2, o2, log2, w, gb[l])
+        line.add(("space", l), g_space)
+        grad = line.move(grad)
         do1, g_mix, g_to = middle_backward(rows, grad, y1, o1, w, mixes[l])
-        da1, g_tq = time_backward(rows, swap_places(do1), a1, qkv1, log1, w)
-        grad, s1 = first_norm_back(rows, swap_places(da1), x, grad, gb[l])
-        results[l] = (
-            reduce_slabs(g_in, True),
-            reduce_slabs(g_out, False),
-            reduce_slabs(jnp.concatenate((g_so, g_sq), axis=0), True),
-            reduce_slabs(jnp.concatenate((g_to, mix_slab(g_mix, shards, shares)), axis=0), False),
-            reduce_slabs(g_tq, True),
-        )
+        line.add(("out", l), jnp.concatenate((g_to, mix_slab(g_mix, shards, shares)), axis=0))
+        do1 = line.move(swap_places(do1))
+        da1, g_tq = time_backward(rows, do1, a1, qkv1, log1, w)
+        line.add(("time", l), g_tq)
+        da1 = line.move(swap_places(da1))
+        grad, s1 = first_norm_back(rows, da1, x, grad, gb[l])
         norm_rows[l] = jnp.concatenate((s1[0:1], s2[0:1], s3[0:1], s1[1:2], s2[1:2], s3[1:2]), axis=0)
+    while line.going:
+        line.move(())
+    results = [[line.done[(key, l)] for key in ("ff", "space", "out", "time")] for l in range(layers)]
     tokens_grad = from_rows(grad)
     norm_sums = reduce_norms(jnp.concatenate(norm_rows, axis=0)).reshape(layers, 2, 3, -1)
 
@@ -850,16 +895,17 @@
         r, width = a.shape
         return a.reshape(shares, r // shares, width).transpose(1, 0, 2).reshape(r // shares, -1)
 
+    per_share = mlp_in.shape[2] // time_qkv.shape[3]
     return (
         output,
         tokens_grad,
-        stacked(lambda gi, go, s, t, q: rows_of(q)),
-        stacked(lambda gi, go, s, t, q: t[0].T),
-        stacked(lambda gi, go, s, t, q: mix_rows(t[1])),
-        stacked(lambda gi, go, s, t, q: rows_of(s[1:])),
-        stacked(lambda gi, go, s, t, q: s[0].T),
-        stacked(lambda gi, go, s, t, q: flat(gi)),
-        stacked(lambda gi, go, s, t, q: flat(go).T),
+        stacked(lambda ff, s, t, q: rows_of(q)),
+        stacked(lambda ff, s, t, q: t[0].T),
+        stacked(lambda ff, s, t, q: mix_rows(t[1])),
+        stacked(lambda ff, s, t, q: rows_of(s[1:])),
+        stacked(lambda ff, s, t, q: s[0].T),
+        stacked(lambda ff, s, t, q: flat(ff[:per_share])),
+        stacked(lambda ff, s, t, q: flat(ff[per_share:]).T),
         norm_sums[:, 0],
         norm_sums[:, 1],
     )

time: 909 us -> 873 us (0.960)
  waiting for transfers between devices: 334 us -> 278 us
  other arithmetic: 78 us -> 99.4 us
    ppermute x30 -> x40, waiting for transfers between devices: 94.8 us -> 39.7 us  [take(): got = lax.ppermute(sent, axis, [(i, i ^ 1 << bit) for i in range(size)])]
    convert_element_type x20 -> x32, other arithmetic: 38.6 us -> 57.5 us  [to_send(): return total_of(self.picked(name, 1 - self.mine(name))).astype(BF16)]
    slice x0 -> x12, local copies, waits for them, and re-layouts: none -> 16.2 us  [cut(): return Part([t[first:last] for t in self.terms], self.names)]
    dynamic_slice x16 -> x6, local copies, waits for them, and re-layouts: 28.8 us -> 13.3 us  [picked(): lax.dynamic_index_in_dim(t, index, axis, keepdims=False)]
    ppermute x30 -> x40, starting transfers between devices: 19.7 us -> 34.5 us  [take(): got = lax.ppermute(sent, axis, [(i, i ^ 1 << bit) for i in range(size)])]
    all_to_all x10 -> x8, starting transfers between devices: 41.7 us -> 34.9 us  [reduction(): got = lax.all_to_all(sent, 'seq', split_axis=0, concat_axis=0, tiled=True)]
    all_to_all x10 -> x8, waiting for transfers between devices: 26.4 us -> 20.9 us  [reduction(): got = lax.all_to_all(sent, 'seq', split_axis=0, concat_axis=0, tiled=True)]
    squeeze x20 -> x6, local copies, waits for them, and re-layouts: 18.5 us -> 23.2 us  [picked(): lax.dynamic_index_in_dim(t, index, axis, keepdims=False)]
  transfers between devices with their start and end apart: 51 -> 59, of which waited for: 21 -> 20; matrix products, arithmetic and copies ran while one was open for 18% -> 19% of each run, Pallas kernels for 16% -> 21%
where the time goes in v2:
time: 873 us; the launch traced here: 866 us
  waiting for transfers between devices  278 us (32%)
  Pallas kernels  234 us (27%)
  starting transfers between devices  108 us (12%)
  local copies, waits for them, and re-layouts  102 us (12%)
  other arithmetic  99.4 us (11%)
  blocking collectives  27.8 us (3%)
  between operations  15.8 us (2%)
    pallas_call x19, Pallas kernels, call(): pl.pallas_call(body, out_shape=[shape for shape, _ in outs], grid=grid, i...  234 us
    all_gather x2, waiting for transfers between devices, gather_slabs(): full = lax.all_gather(pack, ('head', 'clip', 'seq'), axis=1, tiled=True)  163 us
    convert_element_type x32, other arithmetic, to_send(): return total_of(self.picked(name, 1 - self.mine(name))).astype(BF16)  57.5 us
    all_to_all x7, waiting for transfers between devices, swap_places(): lax.all_to_all(rows_array, 'seq', split_axis=0, concat_axis=0, tiled=True)  42.8 us
    ppermute x40, waiting for transfers between devices, take(): got = lax.ppermute(sent, axis, [(i, i ^ 1 << bit) for i in range(size)])  39.7 us
    all_to_all x8, starting transfers between devices, reduction(): got = lax.all_to_all(sent, 'seq', split_axis=0, concat_axis=0, tiled=True)  34.9 us
    ppermute x40, starting transfers between devices, take(): got = lax.ppermute(sent, axis, [(i, i ^ 1 << bit) for i in range(size)])  34.5 us
    all_to_all x7, starting transfers between devices, swap_places(): lax.all_to_all(rows_array, 'seq', split_axis=0, concat_axis=0, tiled=True)  29.1 us
  transfers between devices with their start and end apart: 59, of which 20 were waited for; matrix products, arithmetic and copies ran while one was open for 19% of the time, Pallas kernels for 21%

profile of v2, /device:TPU:0, one launch (start us, length us, event | category | flops | bytes accessed | tf_op | source)
XLA Modules:
  0.0 866.1 jit_solution(18053627385383832429)
XLA Ops:
  13.1 7.3 all-to-all-start
  21.8 6.0 all-to-all-done
  31.7 27.8 %all_to_all.150 = bf16[4,104,768]{2,1,0:T(8,128)(2,1)} all-to-all(bf16[4,104,768]{2,1,0:T(8,128)(2,1)} %bitcast.878), channel_id=1, replica_groups=mesh['clip'=4,'seq'=4,'head'=2] {'seq'}, dimensions={0} | all-to-all | bytes 1277952 | tf_op jit(solution)/shard_map/all_to_all | solution.py:649
  59.5 88.9 %all-gather.3.cloned.1.call-done = bf16[17,1536,384]{2,1,0:T(8,128)(2,1)} async-done(((bf16[17,48,384]{2,1,0:T(8,128)(2,1)}), bf16[17,1536,384]{2,1,0:T(8,128)(2,1)}) %all-gather.3.cloned.1.call-update) | async-done | bytes 20054032 | tf_op jit(solution)/shard_map/all_gather | solution.py:676
  148.4 12.0 %shard_map.195 = (bf16[3,416,768]{2,1,0:T(8,128)(2,1)}, bf16[416,768]{1,0:T(8,128)(2,1)}, f32[2,3,2,416]{3,2,1,0:T(2,128)}) custom-call(bf16[416,768]{1,0:T(8,128)(2,1)} %bitcast.841, bf16[17,2,768,384]{3,2,1,0:T(8,128)(2,1)} %bitcast.805), custom_call_target="tpu_custom_call" | custom-call | flops 1472200704 | bytes 23268864 | tf_op jit(solution)/shard_map/pallas_call | solution.py:153
  168.5 21.0 %all-to-all-done.2 = bf16[4,104,768]{2,1,0:T(8,128)(2,1)S(1)} async-done(((bf16[4,104,768]{2,1,0:T(8,128)(2,1)}), bf16[4,104,768]{2,1,0:T(8,128)(2,1)S(1)}, u32[]{:S(2)}, u32[]{:S(2)}) %all-to-all-start.2) | async-done | bytes 639008 | tf_op jit(solution)/shard_map/all_to_all | solution.py:649
  190.3 9.3 %shard_map.196 = (bf16[416,768]{1,0:T(8,128)(2,1)}, bf16[416,768]{1,0:T(8,128)(2,1)}, f32[416,768]{1,0:T(8,128)}, bf16[3,416,768]{2,1,0:T(8,128)(2,1)}) custom-call(bf16[416,768]{1,0:T(8,128)(2,1)} %bitcast.876, f32[416,768]{1,0:T(8,128)} %bitcast_convert_fusion.1.x_ref, bf16[17,2,768,384]{3,2,1,0:T(8,128)(2,1)} %bitcast.806, ...), custom_call_target="tpu_custom_call" | custom-call | flops 2453667840 | bytes 47695872 | tf_op jit(solution)/shard_map/pallas_call | solution.py:153
  199.7 9.9 %shard_map.197 = (bf16[416,768]{1,0:T(8,128)(2,1)}, f32[416,768]{1,0:T(8,128)}, f32[2,3,2,2,208]{4,3,2,1,0:T(2,128)}) custom-call(bf16[3,416,768]{2,1,0:T(8,128)(2,1)} %get-tuple-element.115.qkv_ref, f32[416,768]{1,0:T(8,128)} %get-tuple-element.116.x1_ref, bf16[17,2,768,384]{3,2,1,0:T(8,128)(2,1)} %bitcast.808), custom_call_target="tpu_custom_call" | custom-call | flops 490733568 | bytes 25185792 | tf_op jit(solution)/shard_map/pallas_call | solution.py:153
  209.5 13.3 %shard_map.198 = (f32[416,768]{1,0:T(8,128)}, bf16[416,768]{1,0:T(8,128)(2,1)}) custom-call(f32[416,768]{1,0:T(8,128)} %get-tuple-element.117.x2_ref, bf16[17,2,768,384]{3,2,1,0:T(8,128)(2,1)} %bitcast.809, bf16[17,2,768,384]{3,2,1,0:T(8,128)(2,1)} %bitcast.810, f32[6,768]{1,0:T(8,128)} %squeeze.259.gb_ref, f32[6,768]{1,0:T(8,128)} %squeeze.265.rest_0_.gb_ref), custom_call_target="tpu_custom_call" | custom-call | flops 3925868544 | bytes 43339776 | tf_op jit(solution)/shard_map/pallas_call | solution.py:153
  226.3 74.3 %all-gather.5.cloned.1.call-done = bf16[17,1536,384]{2,1,0:T(8,128)(2,1)} async-done(((bf16[17,48,384]{2,1,0:T(8,128)(2,1)}), bf16[17,1536,384]{2,1,0:T(8,128)(2,1)}) %all-gather.5.cloned.1.call-update) | async-done | bytes 20054032 | tf_op jit(solution)/shard_map/all_gather | solution.py:676
  301.5 12.0 %shard_map.199 = (bf16[3,416,768]{2,1,0:T(8,128)(2,1)}, bf16[416,768]{1,0:T(8,128)(2,1)}, f32[2,3,2,416]{3,2,1,0:T(2,128)}) custom-call(bf16[416,768]{1,0:T(8,128)(2,1)} %bitcast.843, bf16[17,2,768,384]{3,2,1,0:T(8,128)(2,1)} %bitcast.817), custom_call_target="tpu_custom_call" | custom-call | flops 1472200704 | bytes 23268864 | tf_op jit(solution)/shard_map/pallas_call | solution.py:153
  322.5 12.7 %all-to-all-done.4 = bf16[4,104,768]{2,1,0:T(8,128)(2,1)S(1)} async-done(((bf16[4,104,768]{2,1,0:T(8,128)(2,1)}), bf16[4,104,768]{2,1,0:T(8,128)(2,1)S(1)}, u32[]{:S(2)}, u32[]{:S(2)}) %all-to-all-start.4) | async-done | bytes 639008 | tf_op jit(solution)/shard_map/all_to_all | solution.py:649
  336.1 8.8 %shard_map.200 = (bf16[416,768]{1,0:T(8,128)(2,1)}, bf16[416,768]{1,0:T(8,128)(2,1)}, f32[416,768]{1,0:T(8,128)}, bf16[3,416,768]{2,1,0:T(8,128)(2,1)}) custom-call(bf16[416,768]{1,0:T(8,128)(2,1)} %bitcast.875, f32[416,768]{1,0:T(8,128)} %get-tuple-element.120.x_ref, bf16[17,2,768,384]{3,2,1,0:T(8,128)(2,1)} %bitcast.818, ...), custom_call_target="tpu_custom_call" | custom-call | flops 2453667840 | bytes 47695872 | tf_op jit(solution)/shard_map/pallas_call | solution.py:153
  344.8 9.9 %shard_map.201 = (bf16[416,768]{1,0:T(8,128)(2,1)}, f32[416,768]{1,0:T(8,128)}, f32[2,3,2,2,208]{4,3,2,1,0:T(2,128)}) custom-call(bf16[3,416,768]{2,1,0:T(8,128)(2,1)} %get-tuple-element.121.qkv_ref, f32[416,768]{1,0:T(8,128)} %get-tuple-element.122.x1_ref, bf16[17,2,768,384]{3,2,1,0:T(8,128)(2,1)} %bitcast.820), custom_call_target="tpu_custom_call" | custom-call | flops 490733568 | bytes 25185792 | tf_op jit(solution)/shard_map/pallas_call | solution.py:153
  354.7 21.8 %shard_map.203 = (f32[416,768]{1,0:T(8,128)}, bf16[2,4,2,768,384]{4,3,2,1,0:T(8,128)(2,1)}, f32[2,768]{1,0:T(2,128)}) custom-call(f32[416,768]{1,0:T(8,128)} %bitcast_convert_fusion.g_ref, f32[416,768]{1,0:T(8,128)} %get-tuple-element.123.x2_ref, bf16[17,2,768,384]{3,2,1,0:T(8,128)(2,1)} %bitcast.821, bf16[17,2,768,384]{3,2,1,0:T(8,128)(2,1)} %bitcast.822, ...), custom_call_target="tpu_custom_call" | custom-call | flops 9814671360 | bytes 53403648 | tf_op jit(solution)/shard_map/pallas_call | solution.py:153
  381.7 21.7 %shard_map.204 = (f32[416,768]{1,0:T(8,128)}, bf16[4,2,768,384]{3,2,1,0:T(8,128)(2,1)}, f32[2,768]{1,0:T(2,128)}) custom-call(f32[416,768]{1,0:T(8,128)} %get-tuple-element.126.g_ref, f32[416,768]{1,0:T(8,128)} %get-tuple-element.122.x1_ref, bf16[3,416,768]{2,1,0:T(8,128)(2,1)} %get-tuple-element.121.qkv_ref, bf16[416,768]{1,0:T(8,128)(2,1)} %get-tuple-element.127.o2_ref, ...), custom_call_target="tpu_custom_call" | custom-call | flops 3925868544 | bytes 51260928 | tf_op jit(solution)/shard_map/pallas_call | solution.py:153
  424.4 6.7 shard_map.205
  460.0 17.9 %shard_map.206 = (bf16[416,768]{1,0:T(8,128)(2,1)}, bf16[3,2,768,384]{3,2,1,0:T(8,128)(2,1)}) custom-call(bf16[416,768]{1,0:T(8,128)(2,1)} %bitcast.65.do_ref, bf16[416,768]{1,0:T(8,128)(2,1)} %bitcast.844, bf16[3,416,768]{2,1,0:T(8,128)(2,1)} %get-tuple-element.142.qkv_ref, f32[2,3,2,416]{3,2,1,0:T(2,128)} %get-tuple-element.143.log_ref, ...), custom_call_target="tpu_custom_call" | custom-call | flops 2944401408 | bytes 27446784 | tf_op jit(solution)/shard_map/pallas_call | solution.py:153
  490.7 5.2 collective-permute-done.6
  506.3 21.9 %shard_map.208 = (f32[416,768]{1,0:T(8,128)}, bf16[2,4,2,768,384]{4,3,2,1,0:T(8,128)(2,1)}, f32[2,768]{1,0:T(2,128)}) custom-call(f32[416,768]{1,0:T(8,128)} %get-tuple-element.152.g_ref, f32[416,768]{1,0:T(8,128)} %get-tuple-element.117.x2_ref, bf16[17,2,768,384]{3,2,1,0:T(8,128)(2,1)} %bitcast.811, bf16[17,2,768,384]{3,2,1,0:T(8,128)(2,1)} %bitcast.812, ...), custom_call_target="tpu_custom_call" | custom-call | flops 9814671360 | bytes 53403648 | tf_op jit(solution)/shard_map/pallas_call | solution.py:153
  531.0 5.2 copy_bitcast_fusion
  538.0 6.4 collective-permute-done.12
  551.3 12.0 %shard_map.202 = f32[416,768]{1,0:T(8,128)} custom-call(f32[416,768]{1,0:T(8,128)} %get-tuple-element.123.x2_ref, bf16[17,2,768,384]{3,2,1,0:T(8,128)(2,1)} %bitcast.827, bf16[17,2,768,384]{3,2,1,0:T(8,128)(2,1)} %bitcast.828, f32[6,768]{1,0:T(8,128)} %squeeze.265.rest_0_.gb_ref), custom_call_target="tpu_custom_call" | custom-call | flops 3925868544 | bytes 42682368 | tf_op jit(solution)/shard_map/pallas_call | solution.py:153
  579.6 21.4 %shard_map.209 = (f32[416,768]{1,0:T(8,128)}, bf16[4,2,768,384]{3,2,1,0:T(8,128)(2,1)}, f32[2,768]{1,0:T(2,128)}) custom-call(f32[416,768]{1,0:T(8,128)} %get-tuple-element.160.g_ref, f32[416,768]{1,0:T(8,128)} %get-tuple-element.116.x1_ref, bf16[3,416,768]{2,1,0:T(8,128)(2,1)} %get-tuple-element.115.qkv_ref, bf16[416,768]{1,0:T(8,128)(2,1)} %get-tuple-element.161.o2_ref, ...), custom_call_target="tpu_custom_call" | custom-call | flops 3925868544 | bytes 51260928 | tf_op jit(solution)/shard_map/pallas_call | solution.py:153
  632.2 6.2 all-to-all-done.14
  641.0 6.7 shard_map.210
  663.9 9.4 %collective-permute-done.19 = bf16[2,4,48,384]{3,2,1,0:T(8,128)(2,1)} collective-permute-done((bf16[2,4,48,384]{3,2,1,0:T(8,128)(2,1)}, bf16[2,4,48,384]{3,2,1,0:T(8,128)(2,1)}, u32[]{:S(2)}, u32[]{:S(2)}) %collective-permute-start.19) | collective-permute-done | bytes 294944 | tf_op jit(solution)/shard_map/ppermute | solution.py:724
  696.2 17.9 %shard_map.211 = (bf16[416,768]{1,0:T(8,128)(2,1)}, bf16[3,2,768,384]{3,2,1,0:T(8,128)(2,1)}) custom-call(bf16[416,768]{1,0:T(8,128)(2,1)} %bitcast.144.do_ref, bf16[416,768]{1,0:T(8,128)(2,1)} %bitcast.842, bf16[3,416,768]{2,1,0:T(8,128)(2,1)} %get-tuple-element.182.qkv_ref, f32[2,3,2,416]{3,2,1,0:T(2,128)} %get-tuple-element.183.log_ref, ...), custom_call_target="tpu_custom_call" | custom-call | flops 2944401408 | bytes 27446784 | tf_op jit(solution)/shard_map/pallas_call | solution.py:153
  730.7 9.1 %all-to-all-done.8 = bf16[4,104,768]{2,1,0:T(8,128)(2,1)} async-done(((bf16[4,104,768]{2,1,0:T(8,128)(2,1)}), bf16[4,104,768]{2,1,0:T(8,128)(2,1)}, u32[]{:S(2)}, u32[]{:S(2)}) %all-to-all-start.8) | async-done | bytes 639008 | tf_op jit(solution)/shard_map/all_to_all | solution.py:649
  760.8 5.7 all-to-all-done.17
  787.6 9.2 %collective-permute-done.33 = bf16[1,2,4,48,384]{4,3,2,1,0:T(8,128)(2,1)} collective-permute-done((bf16[1,2,4,48,384]{4,3,2,1,0:T(8,128)(2,1)}, bf16[1,2,4,48,384]{4,3,2,1,0:T(8,128)(2,1)}, u32[]{:S(2)}, u32[]{:S(2)}) %collective-permute-start.33) | collective-permute-done | bytes 294944 | tf_op jit(solution)/shard_map/ppermute | solution.py:724
  850.9 7.2 all-to-all-done.9
  (472 shorter events, 325.4 us)
Async XLA Ops:
  7.2 141.1 %all-gather.3.cloned.1.call-start = ((), (), s32[]{:S(2)}) async-start(), calls=%async_computation.18 | async-start | bytes 20680704 | tf_op jit(solution)/shard_map/all_gather | solution.py:676
  11.3 289.4 %all-gather.5.cloned.1.call-start = ((), (), s32[]{:S(2)}) async-start(), calls=%async_computation.19 | async-start | bytes 20680704 | tf_op jit(solution)/shard_map/all_gather | solution.py:676
  160.4 29.1 %all-to-all-start.2 = ((bf16[4,104,768]{2,1,0:T(8,128)(2,1)}), bf16[4,104,768]{2,1,0:T(8,128)(2,1)S(1)}, u32[]{:S(2)}, u32[]{:S(2)}) async-start(bf16[4,104,768]{2,1,0:T(8,128)(2,1)} %bitcast.897), calls=%async_computation.2 | async-start | bytes 1277952 | tf_op jit(solution)/shard_map/all_to_all | solution.py:649
  222.8 77.8 %all-to-all-start.3 = ((bf16[4,104,768]{2,1,0:T(8,128)(2,1)}), bf16[4,104,768]{2,1,0:T(8,128)(2,1)S(1)}, u32[]{:S(2)}, u32[]{:S(2)}) async-start(bf16[4,104,768]{2,1,0:T(8,128)(2,1)} %bitcast.898), calls=%async_computation.3 | async-start | bytes 1277952 | tf_op jit(solution)/shard_map/all_to_all | solution.py:649
  381.7 25.1 %collective-permute-start = (bf16[8,2,2,4,48,384]{5,4,0,3,1,2:T(8,128)(2,1)}, bf16[8,2,2,4,48,384]{5,4,0,3,1,2:T(8,128)(2,1)}, u32[]{:S(2)}, u32[]{:S(2)}) collective-permute-start(bf16[8,2,2,4,48,384]{5,4,0,3,1,2:T(8,128)(2,1)} %copy_bitcast_fusion.1), channel_id=1, source_target_pairs={{0,8},{8,0},{16,24},{24,16},{1,9},{9,1},{17,25},{25,17},{2,10},{10... | collective-permute-start | bytes 14155784 | tf_op jit(solution)/shard_map/ppermute | solution.py:724
  415.7 33.2 %collective-permute-start.3 = (bf16[4,2,2,4,48,384]{5,4,0,3,1,2:T(8,128)(2,1)}, bf16[4,2,2,4,48,384]{5,4,0,3,1,2:T(8,128)(2,1)}, u32[]{:S(2)}, u32[]{:S(2)}) collective-permute-start(bf16[4,2,2,4,48,384]{5,4,0,3,1,2:T(8,128)(2,1)} %copy_bitcast_fusion.3), channel_id=1, source_target_pairs={{0,8},{8,0},{16,24},{24,16},{1,9},{9,1},{17,25},{25,17},{2,10},{10... | collective-permute-start | bytes 7077896 | tf_op jit(solution)/shard_map/ppermute | solution.py:724
  416.2 28.2 %collective-permute-start.1 = (bf16[4,2,4,48,384]{4,3,0,2,1:T(8,128)(2,1)}, bf16[4,2,4,48,384]{4,3,0,2,1:T(8,128)(2,1)}, u32[]{:S(2)}, u32[]{:S(2)}) collective-permute-start(bf16[4,2,4,48,384]{4,3,0,2,1:T(8,128)(2,1)} %fusion.3), channel_id=1, source_target_pairs={{0,16},{8,24},{16,0},{24,8},{1,17},{9,25},{17,1},{25,9},{2,18},{10... | collective-permute-start | bytes 3538952 | tf_op jit(solution)/shard_map/ppermute | solution.py:724
  417.5 29.4 %collective-permute-start.2 = (bf16[4,2,4,48,384]{4,3,0,2,1:T(8,128)(2,1)}, bf16[4,2,4,48,384]{4,3,0,2,1:T(8,128)(2,1)}, u32[]{:S(2)}, u32[]{:S(2)}) collective-permute-start(bf16[4,2,4,48,384]{4,3,0,2,1:T(8,128)(2,1)} %fusion.2), channel_id=1, source_target_pairs={{0,1},{1,0},{2,3},{3,2},{4,5},{5,4},{6,7},{7,6},{8,9},{9,8},{10,11... | collective-permute-start | bytes 3538952 | tf_op jit(solution)/shard_map/ppermute | solution.py:724
  431.1 24.9 %all-to-all-start.5 = ((bf16[4,104,768]{2,1,0:T(8,128)(2,1)}), bf16[4,104,768]{2,1,0:T(8,128)(2,1)}, u32[]{:S(2)}, u32[]{:S(2)}) async-start(bf16[4,104,768]{2,1,0:T(8,128)(2,1)} %bitcast.895), calls=%async_computation.5 | async-start | bytes 1277952 | tf_op jit(solution)/shard_map/all_to_all | solution.py:649
  456.0 30.1 %collective-permute-start.5 = (bf16[4,4,48,384]{3,2,0,1:T(8,128)(2,1)}, bf16[4,4,48,384]{3,2,0,1:T(8,128)(2,1)}, u32[]{:S(2)}, u32[]{:S(2)}) collective-permute-start(bf16[4,4,48,384]{3,2,0,1:T(8,128)(2,1)} %fusion.24), channel_id=1, source_target_pairs={{0,16},{8,24},{16,0},{24,8},{1,17},{9,25},{17,1},{25,9},{2,18},{10... | collective-permute-start | bytes 1769480 | tf_op jit(solution)/shard_map/ppermute | solution.py:724
  458.4 29.3 %collective-permute-start.4 = (bf16[4,4,48,384]{3,2,0,1:T(8,128)(2,1)}, bf16[4,4,48,384]{3,2,0,1:T(8,128)(2,1)}, u32[]{:S(2)}, u32[]{:S(2)}) collective-permute-start(bf16[4,4,48,384]{3,2,0,1:T(8,128)(2,1)} %fusion.25), channel_id=1, source_target_pairs={{0,1},{1,0},{2,3},{3,2},{4,5},{5,4},{6,7},{7,6},{8,9},{9,8},{10,11... | collective-permute-start | bytes 1769480 | tf_op jit(solution)/shard_map/ppermute | solution.py:724
  504.9 31.2 %collective-permute-start.11 = (bf16[1,2,4,48,384]{4,3,2,1,0:T(8,128)(2,1)S(1)}, bf16[1,2,4,48,384]{4,3,2,1,0:T(8,128)(2,1)S(1)}, u32[]{:S(2)}, u32[]{:S(2)}) collective-permute-start(bf16[1,2,4,48,384]{4,3,2,1,0:T(8,128)(2,1)S(1)} %copy-done.60), channel_id=1, source_target_pairs={{0,16},{8,24},{16,0},{24,8},{1,17},{9,25},{17,1},{25,9},{2,18},{10... | collective-permute-start | bytes 884744 | tf_op jit(solution)/shard_map/ppermute | solution.py:724
  506.2 41.2 %collective-permute-start.13 = (bf16[3,2,2,4,48,384]{5,4,3,0,1,2:T(8,128)(2,1)S(1)}, bf16[3,2,2,4,48,384]{5,4,3,0,1,2:T(8,128)(2,1)S(1)}, u32[]{:S(2)}, u32[]{:S(2)}) collective-permute-start(bf16[3,2,2,4,48,384]{5,4,3,0,1,2:T(8,128)(2,1)S(1)} %copy-done.32), channel_id=1, source_target_pairs={{0,8},{8,0},{16,24},{24,16},{1,9},{9,1},{17,25},{25,17},{2,10},{10... | collective-permute-start | bytes 5308424 | tf_op jit(solution)/shard_map/ppermute | solution.py:724
  551.3 60.1 %collective-permute-start.18 = (bf16[8,2,2,4,48,384]{5,4,0,3,1,2:T(8,128)(2,1)}, bf16[8,2,2,4,48,384]{5,4,0,3,1,2:T(8,128)(2,1)}, u32[]{:S(2)}, u32[]{:S(2)}) collective-permute-start(bf16[8,2,2,4,48,384]{5,4,0,3,1,2:T(8,128)(2,1)} %copy_bitcast_fusion), channel_id=1, source_target_pairs={{0,8},{8,0},{16,24},{24,16},{1,9},{9,1},{17,25},{25,17},{2,10},{10... | collective-permute-start | bytes 14155784 | tf_op jit(solution)/shard_map/ppermute | solution.py:724
  566.1 52.2 %all-to-all-start.16 = ((bf16[4,8,48,384]{3,2,1,0:T(8,128)(2,1)}), bf16[4,8,48,384]{3,2,1,0:T(8,128)(2,1)S(1)}, u32[]{:S(2)}, u32[]{:S(2)}) async-start(bf16[4,8,48,384]{3,2,1,0:T(8,128)(2,1)} %pad_maximum_fusion), calls=%async_computation.16 | async-start | bytes 2359296 | tf_op jit(solution)/shard_map/all_to_all | solution.py:751
  575.6 29.1 %collective-permute-start.15 = (bf16[1,4,48,384]{3,2,1,0:T(8,128)(2,1)S(1)}, bf16[1,4,48,384]{3,2,1,0:T(8,128)(2,1)S(1)}, u32[]{:S(2)}, u32[]{:S(2)}) collective-permute-start(bf16[1,4,48,384]{3,2,1,0:T(8,128)(2,1)S(1)} %copy-done.75), channel_id=1, source_target_pairs={{0,16},{8,24},{16,0},{24,8},{1,17},{9,25},{17,1},{25,9},{2,18},{10... | collective-permute-start | bytes 442376 | tf_op jit(solution)/shard_map/ppermute | solution.py:724
  576.9 28.8 %collective-permute-start.14 = (bf16[1,4,48,384]{3,2,1,0:T(8,128)(2,1)S(1)}, bf16[1,4,48,384]{3,2,1,0:T(8,128)(2,1)S(1)}, u32[]{:S(2)}, u32[]{:S(2)}) collective-permute-start(bf16[1,4,48,384]{3,2,1,0:T(8,128)(2,1)S(1)} %copy-done.74), channel_id=1, source_target_pairs={{0,1},{1,0},{2,3},{3,2},{4,5},{5,4},{6,7},{7,6},{8,9},{9,8},{10,11... | collective-permute-start | bytes 442376 | tf_op jit(solution)/shard_map/ppermute | solution.py:724
  577.4 32.0 %collective-permute-start.16 = (bf16[2,2,4,48,384]{4,3,2,0,1:T(8,128)(2,1)S(1)}, bf16[2,2,4,48,384]{4,3,2,0,1:T(8,128)(2,1)S(1)}, u32[]{:S(2)}, u32[]{:S(2)}) collective-permute-start(bf16[2,2,4,48,384]{4,3,2,0,1:T(8,128)(2,1)S(1)} %fusion.17), channel_id=1, source_target_pairs={{0,16},{8,24},{16,0},{24,8},{1,17},{9,25},{17,1},{25,9},{2,18},{10... | collective-permute-start | bytes 1769480 | tf_op jit(solution)/shard_map/ppermute | solution.py:724
  578.2 29.4 %collective-permute-start.17 = (bf16[1,2,4,48,384]{4,3,2,1,0:T(8,128)(2,1)S(1)}, bf16[1,2,4,48,384]{4,3,2,1,0:T(8,128)(2,1)S(1)}, u32[]{:S(2)}, u32[]{:S(2)}) collective-permute-start(bf16[1,2,4,48,384]{4,3,2,1,0:T(8,128)(2,1)S(1)} %copy-done.70), channel_id=1, source_target_pairs={{0,1},{1,0},{2,3},{3,2},{4,5},{5,4},{6,7},{7,6},{8,9},{9,8},{10,11... | collective-permute-start | bytes 884744 | tf_op jit(solution)/shard_map/ppermute | solution.py:724
  626.0 53.8 %collective-permute-start.23 = (bf16[4,2,2,4,48,384]{5,4,0,3,1,2:T(8,128)(2,1)}, bf16[4,2,2,4,48,384]{5,4,0,3,1,2:T(8,128)(2,1)}, u32[]{:S(2)}, u32[]{:S(2)}) collective-permute-start(bf16[4,2,2,4,48,384]{5,4,0,3,1,2:T(8,128)(2,1)} %copy_bitcast_fusion.2), channel_id=1, source_target_pairs={{0,8},{8,0},{16,24},{24,16},{1,9},{9,1},{17,25},{25,17},{2,10},{10... | collective-permute-start | bytes 7077896 | tf_op jit(solution)/shard_map/ppermute | solution.py:724
  630.9 44.4 %collective-permute-start.21 = (bf16[4,2,4,48,384]{4,3,0,2,1:T(8,128)(2,1)}, bf16[4,2,4,48,384]{4,3,0,2,1:T(8,128)(2,1)}, u32[]{:S(2)}, u32[]{:S(2)}) collective-permute-start(bf16[4,2,4,48,384]{4,3,0,2,1:T(8,128)(2,1)} %fusion.1), channel_id=1, source_target_pairs={{0,16},{8,24},{16,0},{24,8},{1,17},{9,25},{17,1},{25,9},{2,18},{10... | collective-permute-start | bytes 3538952 | tf_op jit(solution)/shard_map/ppermute | solution.py:724
  639.6 38.1 %collective-permute-start.22 = (bf16[4,2,4,48,384]{4,3,0,2,1:T(8,128)(2,1)}, bf16[4,2,4,48,384]{4,3,0,2,1:T(8,128)(2,1)}, u32[]{:S(2)}, u32[]{:S(2)}) collective-permute-start(bf16[4,2,4,48,384]{4,3,0,2,1:T(8,128)(2,1)} %fusion), channel_id=1, source_target_pairs={{0,1},{1,0},{2,3},{3,2},{4,5},{5,4},{6,7},{7,6},{8,9},{9,8},{10,11... | collective-permute-start | bytes 3538952 | tf_op jit(solution)/shard_map/ppermute | solution.py:724
  647.8 39.0 %all-to-all-start.7 = ((bf16[4,104,768]{2,1,0:T(8,128)(2,1)}), bf16[4,104,768]{2,1,0:T(8,128)(2,1)}, u32[]{:S(2)}, u32[]{:S(2)}) async-start(bf16[4,104,768]{2,1,0:T(8,128)(2,1)} %bitcast.893), calls=%async_computation.7 | async-start | bytes 1277952 | tf_op jit(solution)/shard_map/all_to_all | solution.py:649
  686.8 30.2 %all-to-all-start.12 = ((bf16[4,2,48,384]{3,2,1,0:T(8,128)(2,1)}), bf16[4,2,48,384]{3,2,1,0:T(8,128)(2,1)}, u32[]{:S(2)}, u32[]{:S(2)}) async-start(bf16[4,2,48,384]{3,2,1,0:T(8,128)(2,1)} %pad_maximum_fusion.10), calls=%async_computation.12 | async-start | bytes 589824 | tf_op jit(solution)/shard_map/all_to_all | solution.py:751
  690.9 31.2 %collective-permute-start.25 = (bf16[4,4,48,384]{3,2,0,1:T(8,128)(2,1)}, bf16[4,4,48,384]{3,2,0,1:T(8,128)(2,1)}, u32[]{:S(2)}, u32[]{:S(2)}) collective-permute-start(bf16[4,4,48,384]{3,2,0,1:T(8,128)(2,1)} %fusion.15), channel_id=1, source_target_pairs={{0,16},{8,24},{16,0},{24,8},{1,17},{9,25},{17,1},{25,9},{2,18},{10... | collective-permute-start | bytes 1769480 | tf_op jit(solution)/shard_map/ppermute | solution.py:724
  693.5 30.3 %collective-permute-start.24 = (bf16[4,4,48,384]{3,2,0,1:T(8,128)(2,1)}, bf16[4,4,48,384]{3,2,0,1:T(8,128)(2,1)S(1)}, u32[]{:S(2)}, u32[]{:S(2)}) collective-permute-start(bf16[4,4,48,384]{3,2,0,1:T(8,128)(2,1)} %fusion.16), channel_id=1, source_target_pairs={{0,1},{1,0},{2,3},{3,2},{4,5},{5,4},{6,7},{7,6},{8,9},{9,8},{10,11... | collective-permute-start | bytes 1769480 | tf_op jit(solution)/shard_map/ppermute | solution.py:724
  694.0 32.7 %collective-permute-start.26 = (bf16[2,2,4,48,384]{4,3,0,2,1:T(8,128)(2,1)}, bf16[2,2,4,48,384]{4,3,0,2,1:T(8,128)(2,1)}, u32[]{:S(2)}, u32[]{:S(2)}) collective-permute-start(bf16[2,2,4,48,384]{4,3,0,2,1:T(8,128)(2,1)} %fusion.14), channel_id=1, source_target_pairs={{0,16},{8,24},{16,0},{24,8},{1,17},{9,25},{17,1},{25,9},{2,18},{10... | collective-permute-start | bytes 1769480 | tf_op jit(solution)/shard_map/ppermute | solution.py:724
  694.7 34.2 %collective-permute-start.27 = (bf16[2,2,4,48,384]{4,3,0,2,1:T(8,128)(2,1)}, bf16[2,2,4,48,384]{4,3,0,2,1:T(8,128)(2,1)}, u32[]{:S(2)}, u32[]{:S(2)}) collective-permute-start(bf16[2,2,4,48,384]{4,3,0,2,1:T(8,128)(2,1)} %fusion.13), channel_id=1, source_target_pairs={{0,1},{1,0},{2,3},{3,2},{4,5},{5,4},{6,7},{7,6},{8,9},{9,8},{10,11... | collective-permute-start | bytes 1769480 | tf_op jit(solution)/shard_map/ppermute | solution.py:724
  696.2 47.8 %collective-permute-start.28 = (bf16[2,2,2,4,48,384]{5,4,3,1,2,0:T(8,128)(2,1)}, bf16[2,2,2,4,48,384]{5,4,3,1,2,0:T(8,128)(2,1)}, u32[]{:S(2)}, u32[]{:S(2)}) collective-permute-start(bf16[2,2,2,4,48,384]{5,4,3,1,2,0:T(8,128)(2,1)} %bitcast.795), channel_id=1, source_target_pairs={{0,8},{8,0},{16,24},{24,16},{1,9},{9,1},{17,25},{25,17},{2,10},{10... | collective-permute-start | bytes 3538952 | tf_op jit(solution)/shard_map/ppermute | solution.py:724
  717.0 22.8 %all-to-all-start.8 = ((bf16[4,104,768]{2,1,0:T(8,128)(2,1)}), bf16[4,104,768]{2,1,0:T(8,128)(2,1)}, u32[]{:S(2)}, u32[]{:S(2)}) async-start(bf16[4,104,768]{2,1,0:T(8,128)(2,1)} %bitcast.894), calls=%async_computation.8 | async-start | bytes 1277952 | tf_op jit(solution)/shard_map/all_to_all | solution.py:649
  751.3 50.6 %collective-permute-start.29 = (bf16[3,2,2,4,48,384]{5,4,3,0,1,2:T(8,128)(2,1)}, bf16[3,2,2,4,48,384]{5,4,3,0,1,2:T(8,128)(2,1)}, u32[]{:S(2)}, u32[]{:S(2)}) collective-permute-start(bf16[3,2,2,4,48,384]{5,4,3,0,1,2:T(8,128)(2,1)} %copy_bitcast_fusion.4), channel_id=1, source_target_pairs={{0,8},{8,0},{16,24},{24,16},{1,9},{9,1},{17,25},{25,17},{2,10},{10... | collective-permute-start | bytes 5308424 | tf_op jit(solution)/shard_map/ppermute | solution.py:724
  767.1 45.1 %all-to-all-start.15 = ((bf16[4,8,48,384]{3,2,1,0:T(8,128)(2,1)}), bf16[4,8,48,384]{3,2,1,0:T(8,128)(2,1)S(1)}, u32[]{:S(2)}, u32[]{:S(2)}) async-start(bf16[4,8,48,384]{3,2,1,0:T(8,128)(2,1)} %pad_maximum_fusion.1), calls=%async_computation.15 | async-start | bytes 2359296 | tf_op jit(solution)/shard_map/all_to_all | solution.py:751
  (119 other events, 936.7 us)
Sparse Core Ops, SparseCore 0:
  11.4 136.9 all-gather.2
  151.4 149.1 all-gather.4

commit v3 on v1

--- a/solution.py
+++ b/solution.py
@@ -146,6 +146,31 @@
     )
 
 
+def split_rows(value, keep_ref, send_ref, at, room_ref, me_ref):
+    mine = me_ref[0]
+    room_ref[...] = value.reshape(room_ref.shape)
+    keep_ref[at] = room_ref[:, mine].astype(BF16)
+    send_ref[at] = room_ref[:, 1 - mine].astype(BF16)
+
+
+class Halves:
+    def __init__(self, clips, depth, width):
+        self.pairs = clips // 2
+        self.rows = depth // clips
+        self.width = width
+
+    def array(self, lead, block, index):
+        tail = (self.pairs, self.rows, self.width)
+        one = lambda: made(lead + tail, BF16, block + tail, lambda *g: index(*g) + (0, 0, 0))
+        return [one(), one()]
+
+    def room(self):
+        return pltpu.VMEM((self.pairs, 2, self.rows, self.width), F32)
+
+
+SCALARS = pl.BlockSpec(memory_space=pltpu.SMEM)
+
+
 def call(body, grid, ins, outs, scratch, args, flops=0):
     specs = [spec for spec in ins]
     moved = sum(math.prod(o.shape) * o.dtype.itemsize for o, _ in outs)
@@ -370,14 +395,14 @@
     )
 
 
-def mlp_backward(rows, grad, x2, w, gb):
+def mlp_backward(rows, grad, x2, w, gb, me, halves):
     t, d = x2.shape
     width = w.shape[3]
     shares = w.shape[1]
     per_share = (w.shape[0] - 9) // 2
     steps = shares * per_share
 
-    def body(g_ref, x2_ref, wi_ref, wo_ref, gb_ref, go_ref, gi_ref, gw_ref, sums_ref, a3_ref, a3t_ref, e3_ref, e3t_ref, u_ref):
+    def body(me_ref, g_ref, x2_ref, wi_ref, wo_ref, gb_ref, go_ref, keep_ref, send_ref, sums_ref, a3_ref, a3t_ref, e3_ref, e3t_ref, u_ref, room_ref):
         j = pl.program_id(0)
 
         @pl.when(j == 0)
@@ -396,8 +421,8 @@
         act = (hid * phi).astype(BF16)
         slope = phi + hid * jnp.exp(-0.5 * hid * hid) * INV_ROOT_TAU
         dhid = (nn(e3_ref[...], wo_ref[0, 0]) * slope).astype(BF16)
-        gw_ref[0, 0] = nn(e3t_ref[...], act).astype(BF16)
-        gi_ref[0, 0] = nn(a3t_ref[...], dhid).astype(BF16)
+        split_rows(nn(e3t_ref[...], act), keep_ref, send_ref, (1, 0, 0), room_ref, me_ref)
+        split_rows(nn(a3t_ref[...], dhid), keep_ref, send_ref, (0, 0, 0), room_ref, me_ref)
         u_ref[...] += nt(dhid, wi_ref[0, 0])
 
         @pl.when(j == steps - 1)
@@ -406,36 +431,37 @@
             go_ref[...] = g_ref[...] + change
             sums_ref[...] = sums
 
-    slab_out = lambda: made(
-        (per_share, shares, d, width),
-        BF16,
-        (1, 1, d, width),
-        lambda j: (j % per_share, j // per_share, 0, 0),
-    )
-    return call(
+    slab_outs = halves.array(
+        (2, per_share, shares), (2, 1, 1), lambda j: (0, j % per_share, j // per_share)
+    )
+    grad, keep, send, sums = call(
         body,
         (steps,),
         [
+            SCALARS,
             whole(grad.shape),
             whole(x2.shape),
             ff_slab(8, per_share, d, width),
             ff_slab(8 + per_share, per_share, d, width),
             whole(gb.shape),
         ],
-        [made((t, d), F32), slab_out(), slab_out(), made((2, d), F32)],
+        [made((t, d), F32), *slab_outs, made((2, d), F32)],
         [
             pltpu.VMEM((t, d), BF16),
             pltpu.VMEM((d, t), BF16),
             pltpu.VMEM((t, d), BF16),
             pltpu.VMEM((d, t), BF16),
             pltpu.VMEM((t, d), F32),
-        ],
-        (grad, x2, w, w, gb),
+            halves.room(),
+        ],
+        (me, grad, x2, w, w, gb),
         flops=10 * t * d * width * steps,
     )
-
-
-def space_backward(rows, grad, x1, qkv, o2, logs, w, gb):
+    flat = (2 * per_share,) + keep.shape[2:]
+    return grad, (keep.reshape(flat), send.reshape(flat)), sums
+
+
+def space_backward(rows, grad, x1, qkv, o2, logs, w, gb, me, halves):
     t, d = x1.shape
     width = w.shape[3]
     shares = w.shape[1]
@@ -444,7 +470,7 @@
     rate = LOG2E * scale
     n = rows.frame_rows
 
-    def body(g_ref, x1_ref, qkv_ref, o2_ref, log_ref, wo_ref, wq_ref, gb_ref, go_ref, gw_ref, gq_ref, sums_ref, e2_ref, e2t_ref, a2t_ref, do_ref, dqkv_ref, u_ref):
+    def body(me_ref, g_ref, x1_ref, qkv_ref, o2_ref, log_ref, wo_ref, wq_ref, gb_ref, go_ref, keep_ref, send_ref, sums_ref, e2_ref, e2t_ref, a2t_ref, do_ref, dqkv_ref, u_ref, room_ref):
         h = pl.program_id(0)
 
         @pl.when(h == 0)
@@ -457,7 +483,7 @@
             u_ref[...] = jnp.zeros((t, d), F32)
 
         bias = rows.space_bias()
-        gw_ref[0, 0] = nn(e2t_ref[...], o2_ref[...]).astype(BF16)
+        split_rows(nn(e2t_ref[...], o2_ref[...]), keep_ref, send_ref, (0, 0), room_ref, me_ref)
         do_ref[...] = nn(e2_ref[...], wo_ref[0, 0]).astype(BF16)
 
         @pl.loop(0, pairs)
@@ -480,7 +506,9 @@
                     dqkv_ref[part, at, lanes] = grads[part]
 
         for part in range(3):
-            gq_ref[part, 0] = nn(a2t_ref[...], dqkv_ref[part]).astype(BF16)
+            split_rows(
+                nn(a2t_ref[...], dqkv_ref[part]), keep_ref, send_ref, (part + 1, 0), room_ref, me_ref
+            )
             u_ref[...] += nt(dqkv_ref[part], wq_ref[part, 0])
 
         @pl.when(h == shares - 1)
@@ -489,10 +517,11 @@
             go_ref[...] = g_ref[...] + change
             sums_ref[...] = sums
 
-    return call(
+    grad, keep, send, sums = call(
         body,
         (shares,),
         [
+            SCALARS,
             whole(grad.shape),
             whole(x1.shape),
             pl.BlockSpec((3, t, width), lambda h: (0, 0, h)),
@@ -504,8 +533,7 @@
         ],
         [
             made((t, d), F32),
-            made((1, shares, d, width), BF16, (1, 1, d, width), lambda h: (0, h, 0, 0)),
-            made((3, shares, d, width), BF16, (3, 1, d, width), lambda h: (0, h, 0, 0)),
+            *halves.array((4, shares), (4, 1), lambda h: (0, h)),
             made((2, d), F32),
         ],
         [
@@ -515,51 +543,80 @@
             pltpu.VMEM((t, width), BF16),
             pltpu.VMEM((3, t, width), BF16),
             pltpu.VMEM((t, d), F32),
-        ],
-        (grad, x1, qkv, o2, logs, w, w, gb),
+            halves.room(),
+        ],
+        (me, grad, x1, qkv, o2, logs, w, w, gb),
         flops=2 * t * d * d * 8,
     )
-
-
-def middle_backward(rows, grad, y1, o1, w, mix):
+    return grad, (keep, send), sums
+
+
+def mix_fits(depth, shards, shares):
+    return depth // (shards * shares) % 8 == 0
+
+
+def middle_backward(rows, grad, y1, o1, w, mix, me, halves, shards):
     t, d = grad.shape
     width = w.shape[3]
     shares = w.shape[1]
-
-    def body(g_ref, y1_ref, o1_ref, to_ref, mix_ref, send_ref, gm_ref, gt_ref):
+    fits = mix_fits(d, shards, shares)
+    part = d // (shards * shares)
+
+    def body(me_ref, g_ref, y1_ref, o1_ref, to_ref, mix_ref, send_ref, gk_ref, gs_ref, *rest):
+        if fits:
+            room_ref, order_ref = rest
+        else:
+            gm_ref, room_ref = rest
         e1 = g_ref[...].astype(BF16)
-        gm_ref[...] = tn(y1_ref[...], e1).astype(BF16)
-        dy = nt(e1, mix_ref[...])
-        dy1 = dy.astype(BF16)
+        dy1 = nt(e1, mix_ref[...]).astype(BF16)
         send = rows.to_time()
         for h in range(shares):
             lanes = slice(h * width, (h + 1) * width)
-            gt_ref[0, h] = tn(dy1, o1_ref[:, lanes]).astype(BF16)
             do1 = nn(dy1, to_ref[0, h]).astype(BF16)
             send_ref[:, lanes] = nn(send, do1).astype(BF16)
-
-    return call(
+            split_rows(tn(dy1, o1_ref[:, lanes]), gk_ref, gs_ref, (0, h), room_ref, me_ref)
+        gm = tn(y1_ref[...], e1)
+        if fits:
+            gm = gm.reshape(shards, shares, part, d)
+            for h in range(shares):
+                for half in range(shares):
+                    order_ref[:, half] = gm[:, h, :, half * width : (half + 1) * width]
+                split_rows(order_ref[...], gk_ref, gs_ref, (1, h), room_ref, me_ref)
+        else:
+            gm_ref[...] = gm.astype(BF16)
+
+    outs = [made((rows.time_rows, d), BF16)]
+    outs += halves.array((1 + fits, shares), (1 + fits, shares), lambda i: (0, 0))
+    scratch = [halves.room()]
+    if fits:
+        scratch.append(pltpu.VMEM((shards, shares, part, width), F32))
+    else:
+        outs.append(made((d, d), BF16))
+    got = call(
         body,
         (1,),
         [
+            SCALARS,
             whole(grad.shape),
             whole(y1.shape),
             whole(o1.shape),
             pl.BlockSpec((1, shares, d, width), lambda i: (6, 0, 0, 0)),
             whole(mix.shape),
         ],
-        [
-            made((rows.time_rows, d), BF16),
-            made((d, d), BF16),
-            made((1, shares, d, width), BF16),
-        ],
-        [],
-        (grad, y1, o1, w, mix),
+        outs,
+        scratch,
+        (me, grad, y1, o1, w, mix),
         flops=8 * t * d * d,
     )
-
-
-def time_backward(rows, do1, a, qkv, logs, w):
+    do1, keep, send = got[:3]
+    if not fits:
+        gm = mix_slab(got[3], shards, shares).reshape((1, shares, halves.pairs, 2) + keep.shape[3:])
+        keep = jnp.concatenate((keep, lax.dynamic_index_in_dim(gm, me[0], 3, keepdims=False)), axis=0)
+        send = jnp.concatenate((send, lax.dynamic_index_in_dim(gm, 1 - me[0], 3, keepdims=False)), axis=0)
+    return do1, (keep, send)
+
+
+def time_backward(rows, do1, a, qkv, logs, w, me, halves):
     t, d = a.shape
     width = w.shape[3]
     shares = w.shape[1]
@@ -567,7 +624,7 @@
     scale = 1.0 / math.sqrt(HEAD_DIM)
     rate = LOG2E * scale
 
-    def body(do_ref, a_ref, qkv_ref, log_ref, w_ref, out_ref, gq_ref, bias_ref, dqkv_ref, at_ref, u_ref):
+    def body(me_ref, do_ref, a_ref, qkv_ref, log_ref, w_ref, out_ref, keep_ref, send_ref, bias_ref, dqkv_ref, at_ref, u_ref, room_ref):
         h = pl.program_id(0)
 
         @pl.when(h == 0)
@@ -594,17 +651,20 @@
                 dqkv_ref[part, :, lanes] = grads[part]
 
         for part in range(3):
-            gq_ref[part, 0] = nn(at_ref[...], dqkv_ref[part]).astype(BF16)
+            split_rows(
+                nn(at_ref[...], dqkv_ref[part]), keep_ref, send_ref, (part, 0), room_ref, me_ref
+            )
             u_ref[...] += nt(dqkv_ref[part], w_ref[part, 0])
 
         @pl.when(h == shares - 1)
         def _():
             out_ref[...] = u_ref[...].astype(BF16)
 
-    return call(
+    da1, keep, send = call(
         body,
         (shares,),
         [
+            SCALARS,
             pl.BlockSpec((t, width), lambda h: (0, h)),
             whole(a.shape),
             pl.BlockSpec((3, t, width), lambda h: (0, 0, h)),
@@ -613,17 +673,19 @@
         ],
         [
             made((t, d), BF16),
-            made((3, shares, d, width), BF16, (3, 1, d, width), lambda h: (0, h, 0, 0)),
+            *halves.array((3, shares), (3, 1), lambda h: (0, h)),
         ],
         [
             pltpu.VMEM((t, t), F32),
             pltpu.VMEM((3, t, width), BF16),
             pltpu.VMEM((d, t), BF16),
             pltpu.VMEM((t, d), F32),
-        ],
-        (do1, a, qkv, logs, w),
+            halves.room(),
+        ],
+        (me, do1, a, qkv, logs, w),
         flops=2 * t * d * d * 6,
     )
+    return da1, (keep, send)
 
 
 def first_norm_back(rows, back, x, grad, gb):
@@ -690,48 +752,183 @@
     return part.transpose(1, 0, 3, 2, 4).reshape(1, shares, depth, width)
 
 
-def added(a, b):
-    return (a.astype(F32) + b.astype(F32)).astype(BF16)
-
-
-def picked(a, index, axis):
-    return lax.dynamic_index_in_dim(a, index, axis, keepdims=False)
-
-
-def fold(a, axis, name, bit):
-    size = lax.axis_size(name)
-    mine = (lax.axis_index(name) >> bit) & 1
-    sent = lax.ppermute(
-        picked(a, 1 - mine, axis), name, [(i, i ^ (1 << bit)) for i in range(size)]
-    )
-    return added(picked(a, mine, axis), sent)
-
-
-def reduce_slabs(g, head_first):
-    ns, shares, depth, width = g.shape
-    clips, ways = lax.axis_size("clip"), lax.axis_size("seq")
-    r = depth // (clips * ways)
-    a = g.reshape(ns, shares, clips // 2, 2, ways, r, width)
-    a = fold(a, 3, "clip", 0)
-
-    def by_head(a):
-        return fold(a, 1, "head", 0)
-
-    def by_clip(a, axis):
-        bits = int(math.log2(clips)) - 1
-        for bit in range(bits):
-            shape = a.shape
-            a = a.reshape(shape[:axis] + (shape[axis] // 2, 2) + shape[axis + 1 :])
-            a = fold(a, axis + 1, "clip", bit + 1)
-        return a.reshape(a.shape[:axis] + a.shape[axis + 1 :])
-
-    if head_first:
-        a = by_clip(by_head(a), 1)
-    else:
-        a = by_head(by_clip(a, 2))
-    a = a.transpose(1, 0, 2, 3)
-    parts = lax.all_to_all(a, "seq", split_axis=0, concat_axis=0, tiled=True)
-    return jnp.sum(parts.astype(F32), axis=0)
+class Term:
+    def __init__(self, array, names, first, count):
+        self.array = array
+        self.names = names
+        self.first = first
+        self.count = count
+
+    def cut(self, first, count):
+        return Term(self.array, self.names, self.first + first, count)
+
+
+class Job:
+    def __init__(self, pieces, other, ways):
+        self.pieces = pieces
+        self.other = other
+        self.ways = ways
+        names = pieces[0][-1].names
+        self.lead = () if other is None else tuple(2 for n in names if n != other)
+        self.count = sum(piece[0].count for piece in pieces)
+        self.rows, self.width = pieces[0][0].array.shape[-2:]
+
+    def shape(self):
+        if self.other is None:
+            return (self.ways, self.count, self.rows // self.ways, self.width)
+        return (self.count,) + self.lead + (self.rows, self.width)
+
+
+def fold(jobs, me):
+    place = {"x": 1, "h": 2}
+    terms = [t for job in jobs for piece in job.pieces for t in piece]
+    arrays = []
+    for t in terms:
+        if not any(t.array is a for a in arrays):
+            arrays.append(t.array)
+    number = [next(i for i, a in enumerate(arrays) if a is t.array) for t in terms]
+    rooms = []
+    for job in jobs:
+        for piece in job.pieces:
+            rooms += [(t.count,) + job.lead + (job.rows, job.width) for t in piece]
+
+    def body(me_ref, *refs):
+        sources = refs[: len(arrays)]
+        outs = refs[len(arrays) : len(arrays) + len(jobs)]
+        held = refs[len(arrays) + len(jobs) : -1]
+        sems = refs[-1]
+        copies = []
+        for job in jobs:
+            for piece in job.pieces:
+                for t in piece:
+                    n = len(copies)
+                    at = [pl.ds(t.first, t.count)]
+                    for name in t.names:
+                        if name == job.other:
+                            at.append(1 - me_ref[place[name]])
+                        elif job.other is not None and name in job.pieces[0][-1].names:
+                            at.append(slice(None))
+                        else:
+                            at.append(me_ref[place[name]])
+                    copies.append(
+                        pltpu.make_async_copy(sources[number[n]].at[tuple(at)], held[n], sems.at[n])
+                    )
+        for copy in copies:
+            copy.start()
+        n = 0
+        for job, out in zip(jobs, outs):
+            base = 0
+            for piece in job.pieces:
+                these = held[n : n + len(piece)]
+                for k in range(len(piece)):
+                    copies[n + k].wait()
+                n += len(piece)
+
+                @pl.loop(0, piece[0].count)
+                def _(i, these=these, base=base, out=out, job=job):
+                    def total(at):
+                        value = these[0][at].astype(F32)
+                        for one in these[1:]:
+                            value = value + one[at].astype(F32)
+                        return value.astype(BF16)
+
+                    if job.other is None:
+                        value = total((i,))
+                        r = job.rows // job.ways
+                        for s in range(job.ways):
+                            out[s, base + i] = value[s * r : (s + 1) * r]
+                    elif job.lead:
+                        for k in range(2):
+                            out[base + i, k] = total((i, k))
+                    else:
+                        out[base + i] = total((i,))
+
+                base += piece[0].count
+
+    moved = sum(2 * math.prod(r) for r in rooms) + sum(2 * math.prod(j.shape()) for j in jobs)
+    return pl.pallas_call(
+        body,
+        out_shape=[jax.ShapeDtypeStruct(job.shape(), BF16) for job in jobs],
+        in_specs=[SCALARS] + [pl.BlockSpec(memory_space=pl.ANY)] * len(arrays),
+        out_specs=[pl.BlockSpec(memory_space=pltpu.VMEM)] * len(jobs),
+        scratch_shapes=[pltpu.VMEM(r, BF16) for r in rooms] + [pltpu.SemaphoreType.DMA((len(rooms),))],
+        compiler_params=pltpu.CompilerParams(vmem_limit_bytes=VMEM),
+        cost_estimate=pl.CostEstimate(flops=0, bytes_accessed=moved, transcendentals=0),
+    )(me, *arrays)
+
+
+def cross(a, name):
+    axis, bit = ("head", 0) if name == "h" else ("clip", 1 if name == "x" else 0)
+    size = lax.axis_size(axis)
+    return lax.ppermute(a, axis, [(i, i ^ (1 << bit)) for i in range(size)])
+
+
+class Group:
+    def __init__(self, halves_of):
+        self.pieces = []
+        for keep, send in halves_of:
+            got = cross(send, "c")
+            n = keep.shape[0]
+            self.pieces.append([Term(a, ("h", "x"), 0, n) for a in (keep, got)])
+        total = sum(p[0].count for p in self.pieces)
+        self.parts = ([], [])
+        seen = 0
+        for piece in self.pieces:
+            n = piece[0].count
+            first = min(max((total + 1) // 2 - seen, 0), n)
+            if first:
+                self.parts[0].append([t.cut(0, first) for t in piece])
+            if n > first:
+                self.parts[1].append([t.cut(first, n - first) for t in piece])
+            seen += n
+        self.step = 0
+        self.result = None
+
+    def jobs(self, ways):
+        if self.step == 2:
+            return [Job(self.parts[0] + self.parts[1], None, ways)]
+        orders = (("x", "h"), ("h", "x"))
+        return [Job(part, order[self.step], ways) for part, order in zip(self.parts, orders)]
+
+    def go(self, sums):
+        if self.step == 2:
+            got = lax.all_to_all(sums[0], "seq", split_axis=0, concat_axis=0, tiled=True)
+            self.result = jnp.sum(got.astype(F32), axis=0)
+        else:
+            orders = (("x", "h"), ("h", "x"))
+            left = (orders[0][1 - self.step], orders[1][1 - self.step])
+            for part, order, name, one in zip(self.parts, orders, left, sums):
+                got = cross(one, order[self.step])
+                base = 0
+                for piece in part:
+                    names = () if self.step else (name,)
+                    piece.append(Term(got, names, base, piece[0].count))
+                    base += piece[0].count
+        self.step += 1
+
+
+def move(x, groups, me):
+    ways = lax.axis_size("seq")
+    jobs = [g.jobs(ways) for g in groups]
+    sums = fold([j for some in jobs for j in some], me)
+    x, sums = lax.optimization_barrier((x, sums))
+    for g, some in zip(groups, jobs):
+        g.go(sums[: len(some)])
+        sums = sums[len(some) :]
+    return x
+
+
+def reduce_plain(halves_of, core):
+    def joined(keep, send):
+        low = jnp.where(core == 0, keep, send)
+        high = jnp.where(core == 0, send, keep)
+        n, shares, pairs, depth, width = keep.shape
+        return jnp.stack((low, high), axis=3).reshape(n, shares, 2 * pairs * depth, width)
+
+    g = jnp.concatenate([joined(*pair) for pair in halves_of], axis=0)
+    g = lax.psum_scatter(g, "head", scatter_dimension=1, tiled=True)
+    g = lax.psum_scatter(g.astype(F32), ("clip", "seq"), scatter_dimension=2, tiled=True)
+    return g[:, 0]
 
 
 def gather_norms(gain, bias):
@@ -816,24 +1013,51 @@
     output = from_rows(x).astype(BF16)
 
     grad = as_rows(cotangent)
-    results = [None] * layers
+    halves = Halves(lax.axis_size("clip"), d, time_qkv.shape[3])
+    clip = lax.axis_index("clip")
+    me = jnp.stack((clip & 1, (clip >> 1) & 1, lax.axis_index("head"))).astype(jnp.int32)
     norm_rows = [None] * layers
+    summed = [None] * layers
+    late = None
+    quick = lax.axis_size("clip") == 4 and shares == 2 and time_qkv.shape[1] % 16 == 0
     for l in reversed(range(layers)):
         w = weights[l]
         x, a1, qkv1, log1, o1, y1, x1, qkv2, o2, log2, x2 = kept[l]
-        grad, g_in, g_out, s3 = mlp_backward(rows, grad, x2, w, gb[l])
-        grad, g_so, g_sq, s2 = space_backward(rows, grad, x1, qkv2, o2, log2, w, gb[l])
-        do1, g_mix, g_to = middle_backward(rows, grad, y1, o1, w, mixes[l])
-        da1, g_tq = time_backward(rows, swap_places(do1), a1, qkv1, log1, w)
-        grad, s1 = first_norm_back(rows, swap_places(da1), x, grad, gb[l])
-        results[l] = (
-            reduce_slabs(g_in, True),
-            reduce_slabs(g_out, False),
-            reduce_slabs(jnp.concatenate((g_so, g_sq), axis=0), True),
-            reduce_slabs(jnp.concatenate((g_to, mix_slab(g_mix, shards, shares)), axis=0), False),
-            reduce_slabs(g_tq, True),
-        )
+        grad, g_ff, s3 = mlp_backward(rows, grad, x2, w, gb[l], me, halves)
+        ff = Group([g_ff]) if quick else None
+        grad, g_space, s2 = space_backward(rows, grad, x1, qkv2, o2, log2, w, gb[l], me, halves)
+        do1, g_out = middle_backward(rows, grad, y1, o1, w, mixes[l], me, halves, shards)
+        do1 = swap_places(do1)
+        first = l == 0
+        if quick:
+            out = Group([g_space, g_out]) if first else None
+            do1 = move(do1, [ff] + (late or []), me)
+        da1, g_time = time_backward(rows, do1, a1, qkv1, log1, w, me, halves)
+        da1 = swap_places(da1)
+        if quick and first:
+            da1 = move(da1, [ff, out] + (late[1:] if late else []), me)
+            time = Group([g_time])
+        elif quick:
+            out = Group([g_space, g_out, g_time])
+            da1 = move(da1, [ff, out], me)
+            late = [ff, out]
+        grad, s1 = first_norm_back(rows, da1, x, grad, gb[l])
         norm_rows[l] = jnp.concatenate((s1[0:1], s2[0:1], s3[0:1], s1[1:2], s2[1:2], s3[1:2]), axis=0)
+        if quick:
+            summed[l] = [ff, out] + ([time] if first else [])
+        else:
+            summed[l] = [reduce_plain([g_ff, g_space, g_out, g_time], clip & 1)]
+    if quick:
+        move((), [ff, out, time], me)
+        move((), [out, time], me)
+        move((), [time], me)
+        summed = [[g.result for g in some] for some in summed]
+    cuts = (g_ff[0].shape[0], g_space[0].shape[0], g_out[0].shape[0], g_time[0].shape[0])
+    results = []
+    for some in summed:
+        slabs_of = jnp.concatenate(some, axis=0)
+        ends = [sum(cuts[: i + 1]) for i in range(4)]
+        results.append([slabs_of[e - c : e] for c, e in zip(cuts, ends)])
     tokens_grad = from_rows(grad)
     norm_sums = reduce_norms(jnp.concatenate(norm_rows, axis=0)).reshape(layers, 2, 3, -1)
 
@@ -850,16 +1074,17 @@
         r, width = a.shape
         return a.reshape(shares, r // shares, width).transpose(1, 0, 2).reshape(r // shares, -1)
 
+    per_share = mlp_in.shape[2] // time_qkv.shape[3]
     return (
         output,
         tokens_grad,
-        stacked(lambda gi, go, s, t, q: rows_of(q)),
-        stacked(lambda gi, go, s, t, q: t[0].T),
-        stacked(lambda gi, go, s, t, q: mix_rows(t[1])),
-        stacked(lambda gi, go, s, t, q: rows_of(s[1:])),
-        stacked(lambda gi, go, s, t, q: s[0].T),
-        stacked(lambda gi, go, s, t, q: flat(gi)),
-        stacked(lambda gi, go, s, t, q: flat(go).T),
+        stacked(lambda ff, s, t, q: rows_of(q)),
+        stacked(lambda ff, s, t, q: t[0].T),
+        stacked(lambda ff, s, t, q: mix_rows(t[1])),
+        stacked(lambda ff, s, t, q: rows_of(s[1:])),
+        stacked(lambda ff, s, t, q: s[0].T),
+        stacked(lambda ff, s, t, q: flat(ff[:per_share])),
+        stacked(lambda ff, s, t, q: flat(ff[per_share:]).T),
         norm_sums[:, 0],
         norm_sums[:, 1],
     )

time: 909 us -> 832 us (0.915)
  local copies, waits for them, and re-layouts: 108 us -> 35.6 us
  other arithmetic: 78 us -> 11.8 us
  Pallas kernels: 235 us -> 278 us
  starting transfers between devices: 105 us -> 73.7 us
  waiting for transfers between devices: 334 us -> 361 us
  blocking collectives: 26.7 us -> 50.7 us
    pallas_call x0 -> x7, Pallas kernels: none -> 40 us  [fold(): pl.pallas_call(body, out_shape=[jax.ShapeDtypeStruct(job.shape(), BF16) f...]
    convert_element_type x20 -> x0, other arithmetic: 38.6 us -> none  [added(): return (a.astype(F32) + b.astype(F32)).astype(BF16)]
    all_to_all x11 -> x4, starting transfers between devices: 46.9 us -> 15.1 us  [go(): lax.all_to_all(sums[0], 'seq', split_axis=0, concat_axis=0, tiled=True)]
    dynamic_slice x16 -> x0, local copies, waits for them, and re-layouts: 28.8 us -> none  [picked(): return lax.dynamic_index_in_dim(a, index, axis, keepdims=False)]
    all_to_all x0 -> x2, blocking collectives: none -> 24 us  [the longest x1 13.9 us: go(): lax.all_to_all(sums[0], 'seq', split_axis=0, concat_axis=0, tiled=True)]
    all_to_all x11 -> x4, waiting for transfers between devices: 28.8 us -> 47.8 us  [go(): lax.all_to_all(sums[0], 'seq', split_axis=0, concat_axis=0, tiled=True)]
    squeeze x20 -> x0, local copies, waits for them, and re-layouts: 18.5 us -> none  [picked(): return lax.dynamic_index_in_dim(a, index, axis, keepdims=False)]
    transpose x10 -> x0, other arithmetic: 16.4 us -> none  [reduce_slabs(): a = a.transpose(1, 0, 2, 3)]
  transfers between devices with their start and end apart: 51 -> 42, of which waited for: 21 -> 20; matrix products, arithmetic and copies ran while one was open for 18% -> 3% of each run, Pallas kernels for 16% -> 24%
where the time goes in v3:
time: 832 us; the launch traced here: 827 us
  waiting for transfers between devices  361 us (43%)
  Pallas kernels  278 us (33%)
  starting transfers between devices  73.7 us (9%)
  blocking collectives  50.7 us (6%)
  local copies, waits for them, and re-layouts  35.6 us (4%)
  between operations  15.4 us (2%)
  other arithmetic  11.8 us (1%)
    pallas_call x19, Pallas kernels, call(): pl.pallas_call(body, out_shape=[shape for shape, _ in outs], grid=grid, i...  238 us
    all_gather x2, waiting for transfers between devices, gather_slabs(): full = lax.all_gather(pack, ('head', 'clip', 'seq'), axis=1, tiled=True)  165 us
    ppermute x28, waiting for transfers between devices, cross(): return lax.ppermute(a, axis, [(i, i ^ 1 << bit) for i in range(size)])  96.9 us
    all_to_all x4, waiting for transfers between devices, go(): lax.all_to_all(sums[0], 'seq', split_axis=0, concat_axis=0, tiled=True)  47.8 us
    all_to_all x7, waiting for transfers between devices, swap_places(): lax.all_to_all(rows_array, 'seq', split_axis=0, concat_axis=0, tiled=True)  45.4 us
    pallas_call x7, Pallas kernels, fold(): pl.pallas_call(body, out_shape=[jax.ShapeDtypeStruct(job.shape(), BF16) f...  40 us
    all_to_all x7, starting transfers between devices, swap_places(): lax.all_to_all(rows_array, 'seq', split_axis=0, concat_axis=0, tiled=True)  27.7 us
    all_to_all x1, blocking collectives, swap_places(): lax.all_to_all(rows_array, 'seq', split_axis=0, concat_axis=0, tiled=True)  26.7 us
  transfers between devices with their start and end apart: 42, of which 20 were waited for; matrix products, arithmetic and copies ran while one was open for 3% of the time, Pallas kernels for 24%

profile of v3, /device:TPU:0, one launch (start us, length us, event | category | flops | bytes accessed | tf_op | source)
XLA Modules:
  0.0 826.6 jit_solution(6841635564347286220)
XLA Ops:
  30.9 26.7 %all_to_all.135 = bf16[4,104,768]{2,1,0:T(8,128)(2,1)} all-to-all(bf16[4,104,768]{2,1,0:T(8,128)(2,1)} %bitcast.254), channel_id=1, replica_groups=mesh['clip'=4,'seq'=4,'head'=2] {'seq'}, dimensions={0} | all-to-all | bytes 1277952 | tf_op jit(solution)/shard_map/all_to_all | solution.py:711
  57.6 90.9 %all-gather.3.cloned.1.call-done = bf16[17,1536,384]{2,1,0:T(8,128)(2,1)} async-done(((bf16[17,48,384]{2,1,0:T(8,128)(2,1)}), bf16[17,1536,384]{2,1,0:T(8,128)(2,1)}) %all-gather.3.cloned.1.call-update) | async-done | bytes 20054032 | tf_op jit(solution)/shard_map/all_gather | solution.py:738
  148.6 12.0 %shard_map.195 = (bf16[3,416,768]{2,1,0:T(8,128)(2,1)}, bf16[416,768]{1,0:T(8,128)(2,1)}, f32[2,3,2,416]{3,2,1,0:T(2,128)}) custom-call(bf16[416,768]{1,0:T(8,128)(2,1)} %bitcast.243, bf16[17,2,768,384]{3,2,1,0:T(8,128)(2,1)} %bitcast.221), custom_call_target="tpu_custom_call" | custom-call | flops 1472200704 | bytes 23268864 | tf_op jit(solution)/shard_map/pallas_call | solution.py:178
  169.0 20.8 %all-to-all-done.2 = bf16[4,104,768]{2,1,0:T(8,128)(2,1)S(1)} async-done(((bf16[4,104,768]{2,1,0:T(8,128)(2,1)}), bf16[4,104,768]{2,1,0:T(8,128)(2,1)S(1)}, u32[]{:S(2)}, u32[]{:S(2)}) %all-to-all-start.2) | async-done | bytes 639008 | tf_op jit(solution)/shard_map/all_to_all | solution.py:711
  190.5 9.3 %shard_map.196 = (bf16[416,768]{1,0:T(8,128)(2,1)}, bf16[416,768]{1,0:T(8,128)(2,1)}, f32[416,768]{1,0:T(8,128)}, bf16[3,416,768]{2,1,0:T(8,128)(2,1)}) custom-call(bf16[416,768]{1,0:T(8,128)(2,1)} %bitcast.252, f32[416,768]{1,0:T(8,128)} %bitcast_convert_fusion.1.x_ref, bf16[17,2,768,384]{3,2,1,0:T(8,128)(2,1)} %bitcast.222, ...), custom_call_target="tpu_custom_call" | custom-call | flops 2453667840 | bytes 47695872 | tf_op jit(solution)/shard_map/pallas_call | solution.py:178
  199.9 9.9 %shard_map.197 = (bf16[416,768]{1,0:T(8,128)(2,1)}, f32[416,768]{1,0:T(8,128)}, f32[2,3,2,2,208]{4,3,2,1,0:T(2,128)}) custom-call(bf16[3,416,768]{2,1,0:T(8,128)(2,1)} %get-tuple-element.110.qkv_ref, f32[416,768]{1,0:T(8,128)} %get-tuple-element.111.x1_ref, bf16[17,2,768,384]{3,2,1,0:T(8,128)(2,1)} %bitcast.224), custom_call_target="tpu_custom_call" | custom-call | flops 490733568 | bytes 25185792 | tf_op jit(solution)/shard_map/pallas_call | solution.py:178
  209.7 13.2 %shard_map.198 = (f32[416,768]{1,0:T(8,128)}, bf16[416,768]{1,0:T(8,128)(2,1)}) custom-call(f32[416,768]{1,0:T(8,128)} %get-tuple-element.112.x2_ref, bf16[17,2,768,384]{3,2,1,0:T(8,128)(2,1)} %bitcast.225, bf16[17,2,768,384]{3,2,1,0:T(8,128)(2,1)} %bitcast.226, f32[6,768]{1,0:T(8,128)} %squeeze.54.gb_ref, f32[6,768]{1,0:T(8,128)} %squeeze.60.rest_0_.gb_ref), custom_call_target="tpu_custom_call" | custom-call | flops 3925868544 | bytes 43339776 | tf_op jit(solution)/shard_map/pallas_call | solution.py:178
  226.4 74.2 %all-gather.5.cloned.1.call-done = bf16[17,1536,384]{2,1,0:T(8,128)(2,1)} async-done(((bf16[17,48,384]{2,1,0:T(8,128)(2,1)}), bf16[17,1536,384]{2,1,0:T(8,128)(2,1)}) %all-gather.5.cloned.1.call-update) | async-done | bytes 20054032 | tf_op jit(solution)/shard_map/all_gather | solution.py:738
  301.5 12.0 %shard_map.199 = (bf16[3,416,768]{2,1,0:T(8,128)(2,1)}, bf16[416,768]{1,0:T(8,128)(2,1)}, f32[2,3,2,416]{3,2,1,0:T(2,128)}) custom-call(bf16[416,768]{1,0:T(8,128)(2,1)} %bitcast.245, bf16[17,2,768,384]{3,2,1,0:T(8,128)(2,1)} %bitcast.209), custom_call_target="tpu_custom_call" | custom-call | flops 1472200704 | bytes 23268864 | tf_op jit(solution)/shard_map/pallas_call | solution.py:178
  322.8 12.0 %all-to-all-done.4 = bf16[4,104,768]{2,1,0:T(8,128)(2,1)S(1)} async-done(((bf16[4,104,768]{2,1,0:T(8,128)(2,1)}), bf16[4,104,768]{2,1,0:T(8,128)(2,1)S(1)}, u32[]{:S(2)}, u32[]{:S(2)}) %all-to-all-start.4) | async-done | bytes 639008 | tf_op jit(solution)/shard_map/all_to_all | solution.py:711
  335.7 8.7 %shard_map.200 = (bf16[416,768]{1,0:T(8,128)(2,1)}, bf16[416,768]{1,0:T(8,128)(2,1)}, f32[416,768]{1,0:T(8,128)}, bf16[3,416,768]{2,1,0:T(8,128)(2,1)}) custom-call(bf16[416,768]{1,0:T(8,128)(2,1)} %bitcast.251, f32[416,768]{1,0:T(8,128)} %get-tuple-element.115.x_ref, bf16[17,2,768,384]{3,2,1,0:T(8,128)(2,1)} %bitcast.210, ...), custom_call_target="tpu_custom_call" | custom-call | flops 2453667840 | bytes 47695872 | tf_op jit(solution)/shard_map/pallas_call | solution.py:178
  344.4 9.9 %shard_map.201 = (bf16[416,768]{1,0:T(8,128)(2,1)}, f32[416,768]{1,0:T(8,128)}, f32[2,3,2,2,208]{4,3,2,1,0:T(2,128)}) custom-call(bf16[3,416,768]{2,1,0:T(8,128)(2,1)} %get-tuple-element.116.qkv_ref, f32[416,768]{1,0:T(8,128)} %get-tuple-element.117.x1_ref, bf16[17,2,768,384]{3,2,1,0:T(8,128)(2,1)} %bitcast.212), custom_call_target="tpu_custom_call" | custom-call | flops 490733568 | bytes 25185792 | tf_op jit(solution)/shard_map/pallas_call | solution.py:178
  354.3 22.3 %shard_map.203 = (f32[416,768]{1,0:T(8,128)}, bf16[2,4,2,2,192,384]{5,4,3,2,1,0:T(8,128)(2,1)}, bf16[2,4,2,2,192,384]{5,4,3,2,1,0:T(8,128)(2,1)}, f32[2,768]{1,0:T(2,128)}) custom-call(s32[3]{0:T(128)} %pad_add_fusion.me_ref, f32[416,768]{1,0:T(8,128)} %bitcast_convert_fusion.g_ref, f32[416,768]{1,0:T(8,128)} %get-tuple-element.118.x2_ref, ...), custom_call_target="tpu_custom_call" | custom-call | flops 9814671360 | bytes 53403660 | tf_op jit(solution)/shard_map/pallas_call | solution.py:178
  376.7 21.9 %shard_map.204 = (f32[416,768]{1,0:T(8,128)}, bf16[4,2,2,192,384]{4,3,2,1,0:T(8,128)(2,1)}, bf16[4,2,2,192,384]{4,3,2,1,0:T(8,128)(2,1)}, f32[2,768]{1,0:T(2,128)}) custom-call(s32[3]{0:T(128)} %pad_add_fusion.me_ref, f32[416,768]{1,0:T(8,128)} %get-tuple-element.119.g_ref, f32[416,768]{1,0:T(8,128)} %get-tuple-element.117.x1_ref, ...), custom_call_target="tpu_custom_call" | custom-call | flops 3925868544 | bytes 51260940 | tf_op jit(solution)/shard_map/pallas_call | solution.py:178
  398.5 7.6 shard_map.205
  414.9 12.6 %all-to-all-done.5 = bf16[4,104,768]{2,1,0:T(8,128)(2,1)S(1)} async-done(((bf16[4,104,768]{2,1,0:T(8,128)(2,1)}), bf16[4,104,768]{2,1,0:T(8,128)(2,1)S(1)}, u32[]{:S(2)}, u32[]{:S(2)}) %all-to-all-start.5) | async-done | bytes 639008 | tf_op jit(solution)/shard_map/all_to_all | solution.py:711
  428.3 18.2 %shard_map.207 = (bf16[416,768]{1,0:T(8,128)(2,1)}, bf16[3,2,2,192,384]{4,3,2,1,0:T(8,128)(2,1)}, bf16[3,2,2,192,384]{4,3,2,1,0:T(8,128)(2,1)}) custom-call(s32[3]{0:T(128)} %pad_add_fusion.me_ref, bf16[416,768]{1,0:T(8,128)(2,1)} %bitcast.253, bf16[416,768]{1,0:T(8,128)(2,1)} %bitcast.246, bf16[3,416,768]{2,1,0:T(8,128)(2,1)} %get-tuple-element.131.qkv_ref, ...), custom_call_target="tpu_custom_call" | custom-call | flops 2944401408 | bytes 27446796 | tf_op jit(solution)/shard_map/pallas_call | solution.py:178
  454.5 20.8 %collective-permute-done.1.refs_2_.refs_4_ = bf16[4,2,192,384]{3,2,1,0:T(8,128)(2,1)} collective-permute-done((bf16[4,2,192,384]{3,2,1,0:T(8,128)(2,1)}, bf16[4,2,192,384]{3,2,1,0:T(8,128)(2,1)}, u32[]{:S(2)}, u32[]{:S(2)}) %collective-permute-start.1) | collective-permute-done | bytes 1179680 | tf_op jit(solution)/shard_map/ppermute | solution.py:863
  486.9 22.4 %shard_map.210 = (f32[416,768]{1,0:T(8,128)}, bf16[2,4,2,2,192,384]{5,4,3,2,1,0:T(8,128)(2,1)}, bf16[2,4,2,2,192,384]{5,4,3,2,1,0:T(8,128)(2,1)}, f32[2,768]{1,0:T(2,128)}) custom-call(s32[3]{0:T(128)} %pad_add_fusion.me_ref, f32[416,768]{1,0:T(8,128)} %get-tuple-element.147.g_ref, f32[416,768]{1,0:T(8,128)} %get-tuple-element.112.x2_ref, ...), custom_call_target="tpu_custom_call" | custom-call | flops 9814671360 | bytes 53403660 | tf_op jit(solution)/shard_map/pallas_call | solution.py:178
  513.4 21.7 %shard_map.211 = (f32[416,768]{1,0:T(8,128)}, bf16[4,2,2,192,384]{4,3,2,1,0:T(8,128)(2,1)}, bf16[4,2,2,192,384]{4,3,2,1,0:T(8,128)(2,1)}, f32[2,768]{1,0:T(2,128)}) custom-call(s32[3]{0:T(128)} %pad_add_fusion.me_ref, f32[416,768]{1,0:T(8,128)} %get-tuple-element.148.g_ref, f32[416,768]{1,0:T(8,128)} %get-tuple-element.111.x1_ref, ...), custom_call_target="tpu_custom_call" | custom-call | flops 3925868544 | bytes 51260940 | tf_op jit(solution)/shard_map/pallas_call | solution.py:178
  535.3 7.7 shard_map.212
  557.9 8.0 shard_map.213
  567.2 18.1 %shard_map.214 = (bf16[416,768]{1,0:T(8,128)(2,1)}, bf16[3,2,2,192,384]{4,3,2,1,0:T(8,128)(2,1)}, bf16[3,2,2,192,384]{4,3,2,1,0:T(8,128)(2,1)}) custom-call(s32[3]{0:T(128)} %pad_add_fusion.me_ref, bf16[416,768]{1,0:T(8,128)(2,1)} %bitcast.66.do_ref, bf16[416,768]{1,0:T(8,128)(2,1)} %bitcast.244, bf16[3,416,768]{2,1,0:T(8,128)(2,1)} %get-tuple-element.167.qkv_ref, ...), custom_call_target="tpu_custom_call" | custom-call | flops 2944401408 | bytes 27446796 | tf_op jit(solution)/shard_map/pallas_call | solution.py:178
  597.4 8.6 %collective-permute-done.16.refs_15_ = bf16[4,192,384]{2,1,0:T(8,128)(2,1)S(1)} collective-permute-done((bf16[4,192,384]{2,1,0:T(8,128)(2,1)}, bf16[4,192,384]{2,1,0:T(8,128)(2,1)S(1)}, u32[]{:S(2)}, u32[]{:S(2)}) %collective-permute-start.16) | collective-permute-done | bytes 589856 | tf_op jit(solution)/shard_map/ppermute | solution.py:863
  610.4 7.7 shard_map.215
  623.5 10.0 %all_to_all.136 = f32[32,1,384]{2,1,0:T(1,128)S(1)} all-to-all(f32[32,1,384]{2,1,0:T(1,128)S(1)} %copy.127), channel_id=1, replica_groups=mesh['clip'=4,'seq'=4,'head'=2] {'clip','seq','head'}, dimensions={0} | all-to-all | bytes 98304 | tf_op jit(solution)/shard_map/all_to_all | solution.py:953
  637.2 28.9 %all-to-all-done.13 = bf16[4,8,48,384]{3,2,1,0:T(8,128)(2,1)S(1)} async-done(((bf16[4,8,48,384]{3,2,1,0:T(8,128)(2,1)}), bf16[4,8,48,384]{3,2,1,0:T(8,128)(2,1)S(1)}, u32[]{:S(2)}, u32[]{:S(2)}) %all-to-all-start.13) | async-done | bytes 1179680 | tf_op jit(solution)/shard_map/all_to_all | solution.py:895
  675.0 29.8 %collective-permute-done.18.refs_3_ = bf16[4,192,384]{2,1,0:T(8,128)(2,1)S(1)} collective-permute-done((bf16[4,192,384]{2,1,0:T(8,128)(2,1)}, bf16[4,192,384]{2,1,0:T(8,128)(2,1)S(1)}, u32[]{:S(2)}, u32[]{:S(2)}) %collective-permute-start.18) | collective-permute-done | bytes 589856 | tf_op jit(solution)/shard_map/ppermute | solution.py:863
  717.2 14.0 %collective-permute-done.25.refs_11_.refs_4_ = bf16[1,2,192,384]{3,2,1,0:T(8,128)(2,1)S(1)} collective-permute-done((bf16[1,2,192,384]{3,2,1,0:T(8,128)(2,1)}, bf16[1,2,192,384]{3,2,1,0:T(8,128)(2,1)S(1)}, u32[]{:S(2)}, u32[]{:S(2)}) %collective-permute-start.25) | collective-permute-done | bytes 294944 | tf_op jit(solution)/shard_map/ppermute | solution.py:863
  752.6 13.9 %all_to_all.137 = bf16[4,3,48,384]{3,2,1,0:T(8,128)(2,1)S(1)} all-to-all(bf16[4,3,48,384]{3,2,1,0:T(8,128)(2,1)} %shard_map.219), channel_id=1, replica_groups=mesh['clip'=4,'seq'=4,'head'=2] {'seq'}, dimensions={0} | all-to-all | bytes 884736 | tf_op jit(solution)/shard_map/all_to_all | solution.py:895
  770.8 12.1 %shard_map.202 = f32[416,768]{1,0:T(8,128)} custom-call(f32[416,768]{1,0:T(8,128)} %get-tuple-element.118.x2_ref, bf16[17,2,768,384]{3,2,1,0:T(8,128)(2,1)} %bitcast.219, bf16[17,2,768,384]{3,2,1,0:T(8,128)(2,1)} %bitcast.220, f32[6,768]{1,0:T(8,128)} %squeeze.60.rest_0_.gb_ref), custom_call_target="tpu_custom_call" | custom-call | flops 3925868544 | bytes 42682368 | tf_op jit(solution)/shard_map/pallas_call | solution.py:178
  802.0 14.4 %all-to-all-done.11 = bf16[4,6,48,384]{3,2,1,0:T(8,128)(2,1)S(1)} async-done(((bf16[4,6,48,384]{3,2,1,0:T(8,128)(2,1)}), bf16[4,6,48,384]{3,2,1,0:T(8,128)(2,1)S(1)}, u32[]{:S(2)}, u32[]{:S(2)}) %all-to-all-start.11) | async-done | bytes 884768 | tf_op jit(solution)/shard_map/all_to_all | solution.py:895
  (267 shorter events, 190.7 us)
Async XLA Ops:
  7.2 141.4 %all-gather.3.cloned.1.call-start = ((), (), s32[]{:S(2)}) async-start(), calls=%async_computation.15 | async-start | bytes 20680704 | tf_op jit(solution)/shard_map/all_gather | solution.py:738
  10.5 290.1 %all-gather.5.cloned.1.call-start = ((), (), s32[]{:S(2)}) async-start(), calls=%async_computation.16 | async-start | bytes 20680704 | tf_op jit(solution)/shard_map/all_gather | solution.py:738
  160.6 29.1 %all-to-all-start.2 = ((bf16[4,104,768]{2,1,0:T(8,128)(2,1)}), bf16[4,104,768]{2,1,0:T(8,128)(2,1)S(1)}, u32[]{:S(2)}, u32[]{:S(2)}) async-start(bf16[4,104,768]{2,1,0:T(8,128)(2,1)} %bitcast.269), calls=%async_computation.2 | async-start | bytes 1277952 | tf_op jit(solution)/shard_map/all_to_all | solution.py:711
  222.9 77.7 %all-to-all-start.3 = ((bf16[4,104,768]{2,1,0:T(8,128)(2,1)}), bf16[4,104,768]{2,1,0:T(8,128)(2,1)S(1)}, u32[]{:S(2)}, u32[]{:S(2)}) async-start(bf16[4,104,768]{2,1,0:T(8,128)(2,1)} %bitcast.270), calls=%async_computation.3 | async-start | bytes 1277952 | tf_op jit(solution)/shard_map/all_to_all | solution.py:711
  313.5 21.4 %all-to-all-start.4 = ((bf16[4,104,768]{2,1,0:T(8,128)(2,1)}), bf16[4,104,768]{2,1,0:T(8,128)(2,1)S(1)}, u32[]{:S(2)}, u32[]{:S(2)}) async-start(bf16[4,104,768]{2,1,0:T(8,128)(2,1)} %bitcast.267), calls=%async_computation.4 | async-start | bytes 1277952 | tf_op jit(solution)/shard_map/all_to_all | solution.py:711
  376.6 33.5 %collective-permute-start = (bf16[8,2,2,192,384]{4,3,2,1,0:T(8,128)(2,1)}, bf16[8,2,2,192,384]{4,3,2,1,0:T(8,128)(2,1)}, u32[]{:S(2)}, u32[]{:S(2)}) collective-permute-start(bf16[8,2,2,192,384]{4,3,2,1,0:T(8,128)(2,1)} %bitcast.285), channel_id=1, source_target_pairs={{0,8},{8,0},{16,24},{24,16},{1,9},{9,1},{17,25},{25,17},{2,10},{10... | collective-permute-start | bytes 14155784 | tf_op jit(solution)/shard_map/ppermute | solution.py:863
  409.6 44.8 %collective-permute-start.3 = (bf16[4,2,2,192,384]{4,3,2,1,0:T(8,128)(2,1)}, bf16[4,2,2,192,384]{4,3,2,1,0:T(8,128)(2,1)S(1)}, u32[]{:S(2)}, u32[]{:S(2)}) collective-permute-start(bf16[4,2,2,192,384]{4,3,2,1,0:T(8,128)(2,1)} %get-tuple-element.137), channel_id=1, source_target_pairs={{0,8},{8,0},{16,24},{24,16},{1,9},{9,1},{17,25},{25,17},{2,10},{10... | collective-permute-start | bytes 7077896 | tf_op jit(solution)/shard_map/ppermute | solution.py:863
  446.5 30.0 %collective-permute-start.5 = (bf16[3,2,2,192,384]{4,3,2,1,0:T(8,128)(2,1)}, bf16[3,2,2,192,384]{4,3,2,1,0:T(8,128)(2,1)}, u32[]{:S(2)}, u32[]{:S(2)}) collective-permute-start(bf16[3,2,2,192,384]{4,3,2,1,0:T(8,128)(2,1)} %get-tuple-element.141), channel_id=1, source_target_pairs={{0,8},{8,0},{16,24},{24,16},{1,9},{9,1},{17,25},{25,17},{2,10},{10... | collective-permute-start | bytes 5308424 | tf_op jit(solution)/shard_map/ppermute | solution.py:863
  447.0 28.3 %collective-permute-start.1 = (bf16[4,2,192,384]{3,2,1,0:T(8,128)(2,1)}, bf16[4,2,192,384]{3,2,1,0:T(8,128)(2,1)}, u32[]{:S(2)}, u32[]{:S(2)}) collective-permute-start(bf16[4,2,192,384]{3,2,1,0:T(8,128)(2,1)} %get-tuple-element.134), channel_id=1, source_target_pairs={{0,16},{8,24},{16,0},{24,8},{1,17},{9,25},{17,1},{25,9},{2,18},{10... | collective-permute-start | bytes 3538952 | tf_op jit(solution)/shard_map/ppermute | solution.py:863
  448.5 28.0 %collective-permute-start.2 = (bf16[4,2,192,384]{3,2,1,0:T(8,128)(2,1)}, bf16[4,2,192,384]{3,2,1,0:T(8,128)(2,1)}, u32[]{:S(2)}, u32[]{:S(2)}) collective-permute-start(bf16[4,2,192,384]{3,2,1,0:T(8,128)(2,1)} %get-tuple-element.135), channel_id=1, source_target_pairs={{0,1},{1,0},{2,3},{3,2},{4,5},{5,4},{6,7},{7,6},{8,9},{9,8},{10,11... | collective-permute-start | bytes 3538952 | tf_op jit(solution)/shard_map/ppermute | solution.py:863
  449.8 33.0 %all-to-all-start.6 = ((bf16[4,104,768]{2,1,0:T(8,128)(2,1)}), bf16[4,104,768]{2,1,0:T(8,128)(2,1)}, u32[]{:S(2)}, u32[]{:S(2)}) async-start(bf16[4,104,768]{2,1,0:T(8,128)(2,1)} %bitcast.265), calls=%async_computation.6 | async-start | bytes 1277952 | tf_op jit(solution)/shard_map/all_to_all | solution.py:711
  509.3 48.6 %collective-permute-start.6 = (bf16[8,2,2,192,384]{4,3,2,1,0:T(8,128)(2,1)}, bf16[8,2,2,192,384]{4,3,2,1,0:T(8,128)(2,1)}, u32[]{:S(2)}, u32[]{:S(2)}) collective-permute-start(bf16[8,2,2,192,384]{4,3,2,1,0:T(8,128)(2,1)} %bitcast.284), channel_id=1, source_target_pairs={{0,8},{8,0},{16,24},{24,16},{1,9},{9,1},{17,25},{25,17},{2,10},{10... | collective-permute-start | bytes 14155784 | tf_op jit(solution)/shard_map/ppermute | solution.py:863
  509.3 25.9 %collective-permute-start.7 = (bf16[4,192,384]{2,1,0:T(8,128)(2,1)S(1)}, bf16[4,192,384]{2,1,0:T(8,128)(2,1)S(1)}, u32[]{:S(2)}, u32[]{:S(2)}) collective-permute-start(bf16[4,192,384]{2,1,0:T(8,128)(2,1)S(1)} %copy-done.45), channel_id=1, source_target_pairs={{0,1},{1,0},{2,3},{3,2},{4,5},{5,4},{6,7},{7,6},{8,9},{9,8},{10,11... | collective-permute-start | bytes 1769480 | tf_op jit(solution)/shard_map/ppermute | solution.py:863
  510.8 36.4 %collective-permute-start.8 = (bf16[4,192,384]{2,1,0:T(8,128)(2,1)S(1)}, bf16[4,192,384]{2,1,0:T(8,128)(2,1)S(1)}, u32[]{:S(2)}, u32[]{:S(2)}) collective-permute-start(bf16[4,192,384]{2,1,0:T(8,128)(2,1)S(1)} %copy-done.44), channel_id=1, source_target_pairs={{0,16},{8,24},{16,0},{24,8},{1,17},{9,25},{17,1},{25,9},{2,18},{10... | collective-permute-start | bytes 1769480 | tf_op jit(solution)/shard_map/ppermute | solution.py:863
  511.4 39.0 %collective-permute-start.10 = (bf16[4,2,192,384]{3,2,1,0:T(8,128)(2,1)}, bf16[4,2,192,384]{3,2,1,0:T(8,128)(2,1)}, u32[]{:S(2)}, u32[]{:S(2)}) collective-permute-start(bf16[4,2,192,384]{3,2,1,0:T(8,128)(2,1)} %get-tuple-element.160), channel_id=1, source_target_pairs={{0,1},{1,0},{2,3},{3,2},{4,5},{5,4},{6,7},{7,6},{8,9},{9,8},{10,11... | collective-permute-start | bytes 3538952 | tf_op jit(solution)/shard_map/ppermute | solution.py:863
  512.0 45.9 %collective-permute-start.9 = (bf16[5,2,192,384]{3,2,1,0:T(8,128)(2,1)}, bf16[5,2,192,384]{3,2,1,0:T(8,128)(2,1)}, u32[]{:S(2)}, u32[]{:S(2)}) collective-permute-start(bf16[5,2,192,384]{3,2,1,0:T(8,128)(2,1)} %get-tuple-element.159), channel_id=1, source_target_pairs={{0,16},{8,24},{16,0},{24,8},{1,17},{9,25},{17,1},{25,9},{2,18},{10... | collective-permute-start | bytes 4423688 | tf_op jit(solution)/shard_map/ppermute | solution.py:863
  535.2 62.2 %collective-permute-start.13 = (bf16[4,2,2,192,384]{4,3,2,1,0:T(8,128)(2,1)}, bf16[4,2,2,192,384]{4,3,2,1,0:T(8,128)(2,1)S(1)}, u32[]{:S(2)}, u32[]{:S(2)}) collective-permute-start(bf16[4,2,2,192,384]{4,3,2,1,0:T(8,128)(2,1)} %get-tuple-element.173), channel_id=1, source_target_pairs={{0,8},{8,0},{16,24},{24,16},{1,9},{9,1},{17,25},{25,17},{2,10},{10... | collective-permute-start | bytes 7077896 | tf_op jit(solution)/shard_map/ppermute | solution.py:863
  543.0 22.9 %all-to-all-start.7 = ((bf16[4,104,768]{2,1,0:T(8,128)(2,1)}), bf16[4,104,768]{2,1,0:T(8,128)(2,1)}, u32[]{:S(2)}, u32[]{:S(2)}) async-start(bf16[4,104,768]{2,1,0:T(8,128)(2,1)} %bitcast.266), calls=%async_computation.7 | async-start | bytes 1277952 | tf_op jit(solution)/shard_map/all_to_all | solution.py:711
  548.0 43.8 %collective-permute-start.14 = (bf16[2,2,2,192,384]{4,3,2,1,0:T(8,128)(2,1)}, bf16[2,2,2,192,384]{4,3,2,1,0:T(8,128)(2,1)S(1)}, u32[]{:S(2)}, u32[]{:S(2)}) collective-permute-start(bf16[2,2,2,192,384]{4,3,2,1,0:T(8,128)(2,1)} %get-tuple-element.175), channel_id=1, source_target_pairs={{0,8},{8,0},{16,24},{24,16},{1,9},{9,1},{17,25},{25,17},{2,10},{10... | collective-permute-start | bytes 3538952 | tf_op jit(solution)/shard_map/ppermute | solution.py:863
  565.9 43.6 %collective-permute-start.11 = (bf16[4,2,192,384]{3,2,1,0:T(8,128)(2,1)}, bf16[4,2,192,384]{3,2,1,0:T(8,128)(2,1)}, u32[]{:S(2)}, u32[]{:S(2)}) collective-permute-start(bf16[4,2,192,384]{3,2,1,0:T(8,128)(2,1)} %get-tuple-element.170), channel_id=1, source_target_pairs={{0,16},{8,24},{16,0},{24,8},{1,17},{9,25},{17,1},{25,9},{2,18},{10... | collective-permute-start | bytes 3538952 | tf_op jit(solution)/shard_map/ppermute | solution.py:863
  566.6 42.9 %collective-permute-start.12 = (bf16[4,2,192,384]{3,2,1,0:T(8,128)(2,1)}, bf16[4,2,192,384]{3,2,1,0:T(8,128)(2,1)}, u32[]{:S(2)}, u32[]{:S(2)}) collective-permute-start(bf16[4,2,192,384]{3,2,1,0:T(8,128)(2,1)} %get-tuple-element.171), channel_id=1, source_target_pairs={{0,1},{1,0},{2,3},{3,2},{4,5},{5,4},{6,7},{7,6},{8,9},{9,8},{10,11... | collective-permute-start | bytes 3538952 | tf_op jit(solution)/shard_map/ppermute | solution.py:863
  585.3 32.8 %all-to-all-start.8 = ((bf16[4,104,768]{2,1,0:T(8,128)(2,1)}), bf16[4,104,768]{2,1,0:T(8,128)(2,1)}, u32[]{:S(2)}, u32[]{:S(2)}) async-start(bf16[4,104,768]{2,1,0:T(8,128)(2,1)} %bitcast.264), calls=%async_computation.8 | async-start | bytes 1277952 | tf_op jit(solution)/shard_map/all_to_all | solution.py:711
  633.5 32.6 %all-to-all-start.13 = ((bf16[4,8,48,384]{3,2,1,0:T(8,128)(2,1)}), bf16[4,8,48,384]{3,2,1,0:T(8,128)(2,1)S(1)}, u32[]{:S(2)}, u32[]{:S(2)}) async-start(bf16[4,8,48,384]{3,2,1,0:T(8,128)(2,1)} %get-tuple-element.200), calls=%async_computation.13 | async-start | bytes 2359296 | tf_op jit(solution)/shard_map/all_to_all | solution.py:895
  637.1 67.8 %collective-permute-start.17 = (bf16[3,2,2,192,384]{4,3,2,1,0:T(8,128)(2,1)}, bf16[3,2,2,192,384]{4,3,2,1,0:T(8,128)(2,1)S(1)}, u32[]{:S(2)}, u32[]{:S(2)}) collective-permute-start(bf16[3,2,2,192,384]{4,3,2,1,0:T(8,128)(2,1)} %get-tuple-element.186), channel_id=1, source_target_pairs={{0,8},{8,0},{16,24},{24,16},{1,9},{9,1},{17,25},{25,17},{2,10},{10... | collective-permute-start | bytes 5308424 | tf_op jit(solution)/shard_map/ppermute | solution.py:863
  667.2 85.4 %all-to-all-start.10 = ((bf16[4,9,48,384]{3,2,1,0:T(8,128)(2,1)}), bf16[4,9,48,384]{3,2,1,0:T(8,128)(2,1)S(1)}, u32[]{:S(2)}, u32[]{:S(2)}) async-start(bf16[4,9,48,384]{3,2,1,0:T(8,128)(2,1)} %get-tuple-element.197), calls=%async_computation.10 | async-start | bytes 2654208 | tf_op jit(solution)/shard_map/all_to_all | solution.py:895
  670.9 33.9 %collective-permute-start.20 = (bf16[3,2,192,384]{3,2,1,0:T(8,128)(2,1)}, bf16[3,2,192,384]{3,2,1,0:T(8,128)(2,1)S(1)}, u32[]{:S(2)}, u32[]{:S(2)}) collective-permute-start(bf16[3,2,192,384]{3,2,1,0:T(8,128)(2,1)} %get-tuple-element.189), channel_id=1, source_target_pairs={{0,16},{8,24},{16,0},{24,8},{1,17},{9,25},{17,1},{25,9},{2,18},{10... | collective-permute-start | bytes 2654216 | tf_op jit(solution)/shard_map/ppermute | solution.py:863
  671.5 33.3 %collective-permute-start.21 = (bf16[3,2,192,384]{3,2,1,0:T(8,128)(2,1)}, bf16[3,2,192,384]{3,2,1,0:T(8,128)(2,1)S(1)}, u32[]{:S(2)}, u32[]{:S(2)}) collective-permute-start(bf16[3,2,192,384]{3,2,1,0:T(8,128)(2,1)} %get-tuple-element.190), channel_id=1, source_target_pairs={{0,1},{1,0},{2,3},{3,2},{4,5},{5,4},{6,7},{7,6},{8,9},{9,8},{10,11... | collective-permute-start | bytes 2654216 | tf_op jit(solution)/shard_map/ppermute | solution.py:863
  672.3 32.6 %collective-permute-start.18 = (bf16[4,192,384]{2,1,0:T(8,128)(2,1)}, bf16[4,192,384]{2,1,0:T(8,128)(2,1)S(1)}, u32[]{:S(2)}, u32[]{:S(2)}) collective-permute-start(bf16[4,192,384]{2,1,0:T(8,128)(2,1)} %get-tuple-element.187), channel_id=1, source_target_pairs={{0,1},{1,0},{2,3},{3,2},{4,5},{5,4},{6,7},{7,6},{8,9},{9,8},{10,11... | collective-permute-start | bytes 1769480 | tf_op jit(solution)/shard_map/ppermute | solution.py:863
  673.6 31.3 %collective-permute-start.19 = (bf16[4,192,384]{2,1,0:T(8,128)(2,1)}, bf16[4,192,384]{2,1,0:T(8,128)(2,1)S(1)}, u32[]{:S(2)}, u32[]{:S(2)}) collective-permute-start(bf16[4,192,384]{2,1,0:T(8,128)(2,1)} %get-tuple-element.188), channel_id=1, source_target_pairs={{0,16},{8,24},{16,0},{24,8},{1,17},{9,25},{17,1},{25,9},{2,18},{10... | collective-permute-start | bytes 1769480 | tf_op jit(solution)/shard_map/ppermute | solution.py:863
  713.0 23.0 %collective-permute-start.22 = (bf16[2,2,192,384]{3,2,1,0:T(8,128)(2,1)}, bf16[2,2,192,384]{3,2,1,0:T(8,128)(2,1)S(1)}, u32[]{:S(2)}, u32[]{:S(2)}) collective-permute-start(bf16[2,2,192,384]{3,2,1,0:T(8,128)(2,1)} %get-tuple-element.191), channel_id=1, source_target_pairs={{0,16},{8,24},{16,0},{24,8},{1,17},{9,25},{17,1},{25,9},{2,18},{10... | collective-permute-start | bytes 1769480 | tf_op jit(solution)/shard_map/ppermute | solution.py:863
  766.5 27.6 %all-to-all-start.12 = ((bf16[4,8,48,384]{3,2,1,0:T(8,128)(2,1)}), bf16[4,8,48,384]{3,2,1,0:T(8,128)(2,1)}, u32[]{:S(2)}, u32[]{:S(2)}) async-start(bf16[4,8,48,384]{3,2,1,0:T(8,128)(2,1)} %get-tuple-element.199), calls=%async_computation.12 | async-start | bytes 2359296 | tf_op jit(solution)/shard_map/all_to_all | solution.py:895
  794.1 22.3 %all-to-all-start.11 = ((bf16[4,6,48,384]{3,2,1,0:T(8,128)(2,1)}), bf16[4,6,48,384]{3,2,1,0:T(8,128)(2,1)S(1)}, u32[]{:S(2)}, u32[]{:S(2)}) async-start(bf16[4,6,48,384]{3,2,1,0:T(8,128)(2,1)} %get-tuple-element.198), calls=%async_computation.11 | async-start | bytes 1769472 | tf_op jit(solution)/shard_map/all_to_all | solution.py:895
  (56 other events, 366.8 us)
Sparse Core Ops, SparseCore 0:
  11.1 137.4 all-gather.2
  151.6 148.9 all-gather.4

commit v4 on v3

--- a/solution.py
+++ b/solution.py
@@ -16,6 +16,7 @@
 FAR = -1e30
 LANES = 128
 VMEM = 56 * 1024 * 1024
+SHOWN = 1.0
 ALL = ("clip", "seq", "head")
 BF16 = jnp.bfloat16
 F32 = jnp.float32
@@ -183,7 +184,9 @@
         out_specs=[spec for _, spec in outs],
         scratch_shapes=scratch,
         compiler_params=pltpu.CompilerParams(vmem_limit_bytes=VMEM),
-        cost_estimate=pl.CostEstimate(flops=flops, bytes_accessed=moved, transcendentals=0),
+        cost_estimate=pl.CostEstimate(
+            flops=int(flops * SHOWN), bytes_accessed=int(moved * SHOWN), transcendentals=0
+        ),
     )(*args)
 
 
@@ -918,6 +921,19 @@
     return x
 
 
+def settle(x, groups):
+    terms = {}
+    for g in groups:
+        for part in g.parts:
+            for piece in part:
+                terms.setdefault(id(piece[-1].array), []).append(piece[-1])
+    x, arrays = lax.optimization_barrier((x, [same[0].array for same in terms.values()]))
+    for same, array in zip(terms.values(), arrays):
+        for term in same:
+            term.array = array
+    return x
+
+
 def reduce_plain(halves_of, core):
     def joined(keep, send):
         low = jnp.where(core == 0, keep, send)
@@ -1018,39 +1034,41 @@
     me = jnp.stack((clip & 1, (clip >> 1) & 1, lax.axis_index("head"))).astype(jnp.int32)
     norm_rows = [None] * layers
     summed = [None] * layers
-    late = None
+    late = []
     quick = lax.axis_size("clip") == 4 and shares == 2 and time_qkv.shape[1] % 16 == 0
     for l in reversed(range(layers)):
         w = weights[l]
         x, a1, qkv1, log1, o1, y1, x1, qkv2, o2, log2, x2 = kept[l]
         grad, g_ff, s3 = mlp_backward(rows, grad, x2, w, gb[l], me, halves)
-        ff = Group([g_ff]) if quick else None
+        if quick:
+            ff = Group([g_ff])
+            if late:
+                grad = move(grad, late, me)
         grad, g_space, s2 = space_backward(rows, grad, x1, qkv2, o2, log2, w, gb[l], me, halves)
+        if quick:
+            space = Group([g_space])
+            grad = move(grad, [ff], me)
         do1, g_out = middle_backward(rows, grad, y1, o1, w, mixes[l], me, halves, shards)
         do1 = swap_places(do1)
-        first = l == 0
         if quick:
-            out = Group([g_space, g_out]) if first else None
-            do1 = move(do1, [ff] + (late or []), me)
+            do1 = move(do1, [ff, space] + late[1:], me)
         da1, g_time = time_backward(rows, do1, a1, qkv1, log1, w, me, halves)
+        if quick:
+            da1 = settle(da1, [ff, space])
         da1 = swap_places(da1)
-        if quick and first:
-            da1 = move(da1, [ff, out] + (late[1:] if late else []), me)
-            time = Group([g_time])
-        elif quick:
-            out = Group([g_space, g_out, g_time])
-            da1 = move(da1, [ff, out], me)
-            late = [ff, out]
+        if quick:
+            rest = Group([g_out, g_time])
+            da1 = move(da1, [ff, space, rest], me)
+            late = [space, rest]
         grad, s1 = first_norm_back(rows, da1, x, grad, gb[l])
         norm_rows[l] = jnp.concatenate((s1[0:1], s2[0:1], s3[0:1], s1[1:2], s2[1:2], s3[1:2]), axis=0)
         if quick:
-            summed[l] = [ff, out] + ([time] if first else [])
+            summed[l] = [ff, space, rest]
         else:
             summed[l] = [reduce_plain([g_ff, g_space, g_out, g_time], clip & 1)]
     if quick:
-        move((), [ff, out, time], me)
-        move((), [out, time], me)
-        move((), [time], me)
+        move((), [space, rest], me)
+        move((), [rest], me)
         summed = [[g.result for g in some] for some in summed]
     cuts = (g_ff[0].shape[0], g_space[0].shape[0], g_out[0].shape[0], g_time[0].shape[0])
     results = []

time: 832 us -> 840 us (level)
  blocking collectives: 50.7 us -> 26.7 us
  starting transfers between devices: 73.7 us -> 93.7 us
    all_to_all x7, waiting for transfers between devices: 45.4 us -> 70.8 us  [swap_places(): lax.all_to_all(rows_array, 'seq', split_axis=0, concat_axis=0, tiled=True)]
    all_to_all x4 -> x6, waiting for transfers between devices: 47.8 us -> 22.7 us  [go(): lax.all_to_all(sums[0], 'seq', split_axis=0, concat_axis=0, tiled=True)]
    all_to_all x2 -> x0, blocking collectives: 24 us -> none  [the longest x1 13.9 us: go(): lax.all_to_all(sums[0], 'seq', split_axis=0, concat_axis=0, tiled=True)]
    all_to_all x4 -> x6, starting transfers between devices: 15.1 us -> 26 us  [go(): lax.all_to_all(sums[0], 'seq', split_axis=0, concat_axis=0, tiled=True)]
    pallas_call x7 -> x9, Pallas kernels: 40 us -> 45.1 us  [fold(): pl.pallas_call(body, out_shape=[jax.ShapeDtypeStruct(job.shape(), BF16) f...]
    ppermute x28 -> x32, starting transfers between devices: 23.6 us -> 26.8 us  [cross(): return lax.ppermute(a, axis, [(i, i ^ 1 << bit) for i in range(size)])]
    unnamed x109 -> x123, local copies, waits for them, and re-layouts: 19.2 us -> 22.3 us
    ppermute x28 -> x32, waiting for transfers between devices: 96.9 us -> 98.6 us  [cross(): return lax.ppermute(a, axis, [(i, i ^ 1 << bit) for i in range(size)])]
  transfers between devices with their start and end apart: 42 -> 49, of which waited for: 20 -> 23; matrix products, arithmetic and copies ran while one was open for 3% -> 4% of each run, Pallas kernels for 24% -> 24%
where the time goes in v4:
time: 840 us; the launch traced here: 834 us
  waiting for transfers between devices  363 us (43%)
  Pallas kernels  283 us (34%)
  starting transfers between devices  93.7 us (11%)
  local copies, waits for them, and re-layouts  38.8 us (5%)
  blocking collectives  26.7 us (3%)
  between operations  15.8 us (2%)
  other arithmetic  12.8 us (2%)
    pallas_call x19, Pallas kernels, call(): pl.pallas_call(body, out_shape=[shape for shape, _ in outs], grid=grid, i...  238 us
    all_gather x2, waiting for transfers between devices, gather_slabs(): full = lax.all_gather(pack, ('head', 'clip', 'seq'), axis=1, tiled=True)  165 us
    ppermute x32, waiting for transfers between devices, cross(): return lax.ppermute(a, axis, [(i, i ^ 1 << bit) for i in range(size)])  98.6 us
    all_to_all x7, waiting for transfers between devices, swap_places(): lax.all_to_all(rows_array, 'seq', split_axis=0, concat_axis=0, tiled=True)  70.8 us
    pallas_call x9, Pallas kernels, fold(): pl.pallas_call(body, out_shape=[jax.ShapeDtypeStruct(job.shape(), BF16) f...  45.1 us
    all_to_all x7, starting transfers between devices, swap_places(): lax.all_to_all(rows_array, 'seq', split_axis=0, concat_axis=0, tiled=True)  28.3 us
    ppermute x32, starting transfers between devices, cross(): return lax.ppermute(a, axis, [(i, i ^ 1 << bit) for i in range(size)])  26.8 us
    all_to_all x1, blocking collectives, swap_places(): lax.all_to_all(rows_array, 'seq', split_axis=0, concat_axis=0, tiled=True)  26.7 us
  transfers between devices with their start and end apart: 49, of which 23 were waited for; matrix products, arithmetic and copies ran while one was open for 4% of the time, Pallas kernels for 24%

profile of v4, /device:TPU:0, one launch (start us, length us, event | category | flops | bytes accessed | tf_op | source)
XLA Modules:
  0.0 834.4 jit_solution(17110709632195272255)
XLA Ops:
  12.3 7.3 all-to-all-start
  30.9 26.7 %all_to_all.140 = bf16[4,104,768]{2,1,0:T(8,128)(2,1)} all-to-all(bf16[4,104,768]{2,1,0:T(8,128)(2,1)} %bitcast.256), channel_id=1, replica_groups=mesh['clip'=4,'seq'=4,'head'=2] {'seq'}, dimensions={0} | all-to-all | bytes 1277952 | tf_op jit(solution)/shard_map/all_to_all | solution.py:714
  57.6 91.1 %all-gather.3.cloned.1.call-done = bf16[17,1536,384]{2,1,0:T(8,128)(2,1)} async-done(((bf16[17,48,384]{2,1,0:T(8,128)(2,1)}), bf16[17,1536,384]{2,1,0:T(8,128)(2,1)}) %all-gather.3.cloned.1.call-update) | async-done | bytes 20054032 | tf_op jit(solution)/shard_map/all_gather | solution.py:741
  148.6 12.0 %shard_map.195 = (bf16[3,416,768]{2,1,0:T(8,128)(2,1)}, bf16[416,768]{1,0:T(8,128)(2,1)}, f32[2,3,2,416]{3,2,1,0:T(2,128)}) custom-call(bf16[416,768]{1,0:T(8,128)(2,1)} %bitcast.246, bf16[17,2,768,384]{3,2,1,0:T(8,128)(2,1)} %bitcast.224), custom_call_target="tpu_custom_call" | custom-call | flops 1472200704 | bytes 23268864 | tf_op jit(solution)/shard_map/pallas_call | solution.py:179
  168.7 21.1 %all-to-all-done.2 = bf16[4,104,768]{2,1,0:T(8,128)(2,1)S(1)} async-done(((bf16[4,104,768]{2,1,0:T(8,128)(2,1)}), bf16[4,104,768]{2,1,0:T(8,128)(2,1)S(1)}, u32[]{:S(2)}, u32[]{:S(2)}) %all-to-all-start.2) | async-done | bytes 639008 | tf_op jit(solution)/shard_map/all_to_all | solution.py:714
  190.6 9.3 %shard_map.196 = (bf16[416,768]{1,0:T(8,128)(2,1)}, bf16[416,768]{1,0:T(8,128)(2,1)}, f32[416,768]{1,0:T(8,128)}, bf16[3,416,768]{2,1,0:T(8,128)(2,1)}) custom-call(bf16[416,768]{1,0:T(8,128)(2,1)} %bitcast.255, f32[416,768]{1,0:T(8,128)} %bitcast_convert_fusion.1.x_ref, bf16[17,2,768,384]{3,2,1,0:T(8,128)(2,1)} %bitcast.225, ...), custom_call_target="tpu_custom_call" | custom-call | flops 2453667840 | bytes 47695872 | tf_op jit(solution)/shard_map/pallas_call | solution.py:179
  199.9 9.9 %shard_map.197 = (bf16[416,768]{1,0:T(8,128)(2,1)}, f32[416,768]{1,0:T(8,128)}, f32[2,3,2,2,208]{4,3,2,1,0:T(2,128)}) custom-call(bf16[3,416,768]{2,1,0:T(8,128)(2,1)} %get-tuple-element.138.qkv_ref, f32[416,768]{1,0:T(8,128)} %get-tuple-element.139.x1_ref, bf16[17,2,768,384]{3,2,1,0:T(8,128)(2,1)} %bitcast.227), custom_call_target="tpu_custom_call" | custom-call | flops 490733568 | bytes 25185792 | tf_op jit(solution)/shard_map/pallas_call | solution.py:179
  209.8 13.2 %shard_map.198 = (f32[416,768]{1,0:T(8,128)}, bf16[416,768]{1,0:T(8,128)(2,1)}) custom-call(f32[416,768]{1,0:T(8,128)} %get-tuple-element.140.x2_ref, bf16[17,2,768,384]{3,2,1,0:T(8,128)(2,1)} %bitcast.228, bf16[17,2,768,384]{3,2,1,0:T(8,128)(2,1)} %bitcast.229, f32[6,768]{1,0:T(8,128)} %squeeze.54.gb_ref, f32[6,768]{1,0:T(8,128)} %squeeze.60.rest_0_.gb_ref), custom_call_target="tpu_custom_call" | custom-call | flops 3925868544 | bytes 43339776 | tf_op jit(solution)/shard_map/pallas_call | solution.py:179
  226.5 74.1 %all-gather.5.cloned.1.call-done = bf16[17,1536,384]{2,1,0:T(8,128)(2,1)} async-done(((bf16[17,48,384]{2,1,0:T(8,128)(2,1)}), bf16[17,1536,384]{2,1,0:T(8,128)(2,1)}) %all-gather.5.cloned.1.call-update) | async-done | bytes 20054032 | tf_op jit(solution)/shard_map/all_gather | solution.py:741
  301.5 11.9 %shard_map.199 = (bf16[3,416,768]{2,1,0:T(8,128)(2,1)}, bf16[416,768]{1,0:T(8,128)(2,1)}, f32[2,3,2,416]{3,2,1,0:T(2,128)}) custom-call(bf16[416,768]{1,0:T(8,128)(2,1)} %bitcast.248, bf16[17,2,768,384]{3,2,1,0:T(8,128)(2,1)} %bitcast.212), custom_call_target="tpu_custom_call" | custom-call | flops 1472200704 | bytes 23268864 | tf_op jit(solution)/shard_map/pallas_call | solution.py:179
  322.9 12.0 %all-to-all-done.4 = bf16[4,104,768]{2,1,0:T(8,128)(2,1)S(1)} async-done(((bf16[4,104,768]{2,1,0:T(8,128)(2,1)}), bf16[4,104,768]{2,1,0:T(8,128)(2,1)S(1)}, u32[]{:S(2)}, u32[]{:S(2)}) %all-to-all-start.4) | async-done | bytes 639008 | tf_op jit(solution)/shard_map/all_to_all | solution.py:714
  335.7 8.8 %shard_map.200 = (bf16[416,768]{1,0:T(8,128)(2,1)}, bf16[416,768]{1,0:T(8,128)(2,1)}, f32[416,768]{1,0:T(8,128)}, bf16[3,416,768]{2,1,0:T(8,128)(2,1)}) custom-call(bf16[416,768]{1,0:T(8,128)(2,1)} %bitcast.254, f32[416,768]{1,0:T(8,128)} %get-tuple-element.143.x_ref, bf16[17,2,768,384]{3,2,1,0:T(8,128)(2,1)} %bitcast.213, ...), custom_call_target="tpu_custom_call" | custom-call | flops 2453667840 | bytes 47695872 | tf_op jit(solution)/shard_map/pallas_call | solution.py:179
  344.5 9.9 %shard_map.201 = (bf16[416,768]{1,0:T(8,128)(2,1)}, f32[416,768]{1,0:T(8,128)}, f32[2,3,2,2,208]{4,3,2,1,0:T(2,128)}) custom-call(bf16[3,416,768]{2,1,0:T(8,128)(2,1)} %get-tuple-element.144.qkv_ref, f32[416,768]{1,0:T(8,128)} %get-tuple-element.145.x1_ref, bf16[17,2,768,384]{3,2,1,0:T(8,128)(2,1)} %bitcast.215), custom_call_target="tpu_custom_call" | custom-call | flops 490733568 | bytes 25185792 | tf_op jit(solution)/shard_map/pallas_call | solution.py:179
  354.4 22.4 %shard_map.203 = (f32[416,768]{1,0:T(8,128)}, bf16[2,4,2,2,192,384]{5,4,3,2,1,0:T(8,128)(2,1)}, bf16[2,4,2,2,192,384]{5,4,3,2,1,0:T(8,128)(2,1)}, f32[2,768]{1,0:T(2,128)}) custom-call(s32[3]{0:T(128)} %pad_add_fusion.me_ref, f32[416,768]{1,0:T(8,128)} %bitcast_convert_fusion.g_ref, f32[416,768]{1,0:T(8,128)} %get-tuple-element.146.x2_ref, ...), custom_call_target="tpu_custom_call" | custom-call | flops 9814671360 | bytes 53403660 | tf_op jit(solution)/shard_map/pallas_call | solution.py:179
  376.8 22.1 %shard_map.204 = (f32[416,768]{1,0:T(8,128)}, bf16[4,2,2,192,384]{4,3,2,1,0:T(8,128)(2,1)}, bf16[4,2,2,192,384]{4,3,2,1,0:T(8,128)(2,1)}, f32[2,768]{1,0:T(2,128)}) custom-call(s32[3]{0:T(128)} %pad_add_fusion.me_ref, f32[416,768]{1,0:T(8,128)} %get-tuple-element.147.g_ref, f32[416,768]{1,0:T(8,128)} %get-tuple-element.145.x1_ref, ...), custom_call_target="tpu_custom_call" | custom-call | flops 3925868544 | bytes 51260940 | tf_op jit(solution)/shard_map/pallas_call | solution.py:179
  409.4 7.6 shard_map.206
  421.4 13.1 %collective-permute-done.1.refs_2_ = bf16[4,2,192,384]{3,2,1,0:T(8,128)(2,1)S(1)} collective-permute-done((bf16[4,2,192,384]{3,2,1,0:T(8,128)(2,1)}, bf16[4,2,192,384]{3,2,1,0:T(8,128)(2,1)S(1)}, u32[]{:S(2)}, u32[]{:S(2)}) %collective-permute-start.1) | collective-permute-done | bytes 1179680 | tf_op jit(solution)/shard_map/ppermute | solution.py:866
  442.3 18.3 %shard_map.208 = (bf16[416,768]{1,0:T(8,128)(2,1)}, bf16[3,2,2,192,384]{4,3,2,1,0:T(8,128)(2,1)}, bf16[3,2,2,192,384]{4,3,2,1,0:T(8,128)(2,1)}) custom-call(s32[3]{0:T(128)} %pad_add_fusion.me_ref, bf16[416,768]{1,0:T(8,128)(2,1)} %bitcast.62.do_ref, bf16[416,768]{1,0:T(8,128)(2,1)} %bitcast.249, bf16[3,416,768]{2,1,0:T(8,128)(2,1)} %get-tuple-element.168.qkv_ref, ...), custom_call_target="tpu_custom_call" | custom-call | flops 2944401408 | bytes 27446796 | tf_op jit(solution)/shard_map/pallas_call | solution.py:179
  463.1 13.7 %collective-permute-done.5.refs_5_ = bf16[4,192,384]{2,1,0:T(8,128)(2,1)S(1)} collective-permute-done((bf16[4,192,384]{2,1,0:T(8,128)(2,1)S(1)}, bf16[4,192,384]{2,1,0:T(8,128)(2,1)S(1)}, u32[]{:S(2)}, u32[]{:S(2)}) %collective-permute-start.5) | collective-permute-done | bytes 589856 | tf_op jit(solution)/shard_map/ppermute | solution.py:866
  476.8 12.2 %collective-permute-done.6.refs_8_.refs_2_ = bf16[2,2,192,384]{3,2,1,0:T(8,128)(2,1)S(1)} collective-permute-done((bf16[2,2,192,384]{3,2,1,0:T(8,128)(2,1)S(1)}, bf16[2,2,192,384]{3,2,1,0:T(8,128)(2,1)S(1)}, u32[]{:S(2)}, u32[]{:S(2)}) %collective-permute-start.6) | collective-permute-done | bytes 589856 | tf_op jit(solution)/shard_map/ppermute | solution.py:866
  501.1 9.2 %all-to-all-done.6 = bf16[4,104,768]{2,1,0:T(8,128)(2,1)} async-done(((bf16[4,104,768]{2,1,0:T(8,128)(2,1)}), bf16[4,104,768]{2,1,0:T(8,128)(2,1)}, u32[]{:S(2)}, u32[]{:S(2)}) %all-to-all-start.6) | async-done | bytes 639008 | tf_op jit(solution)/shard_map/all_to_all | solution.py:714
  514.4 22.4 %shard_map.211 = (f32[416,768]{1,0:T(8,128)}, bf16[2,4,2,2,192,384]{5,4,3,2,1,0:T(8,128)(2,1)}, bf16[2,4,2,2,192,384]{5,4,3,2,1,0:T(8,128)(2,1)}, f32[2,768]{1,0:T(2,128)}) custom-call(s32[3]{0:T(128)} %pad_add_fusion.me_ref, f32[416,768]{1,0:T(8,128)} %get-tuple-element.190.g_ref, f32[416,768]{1,0:T(8,128)} %get-tuple-element.140.x2_ref, ...), custom_call_target="tpu_custom_call" | custom-call | flops 9814671360 | bytes 53403660 | tf_op jit(solution)/shard_map/pallas_call | solution.py:179
  544.7 15.3 %collective-permute-done.10.refs_3_ = bf16[2,192,384]{2,1,0:T(8,128)(2,1)S(1)} collective-permute-done((bf16[2,192,384]{2,1,0:T(8,128)(2,1)}, bf16[2,192,384]{2,1,0:T(8,128)(2,1)S(1)}, u32[]{:S(2)}, u32[]{:S(2)}) %collective-permute-start.10) | collective-permute-done | bytes 294944 | tf_op jit(solution)/shard_map/ppermute | solution.py:866
  571.5 21.8 %shard_map.213 = (f32[416,768]{1,0:T(8,128)}, bf16[4,2,2,192,384]{4,3,2,1,0:T(8,128)(2,1)}, bf16[4,2,2,192,384]{4,3,2,1,0:T(8,128)(2,1)}, f32[2,768]{1,0:T(2,128)}) custom-call(s32[3]{0:T(128)} %pad_add_fusion.me_ref, f32[416,768]{1,0:T(8,128)} %get-tuple-element.199.g_ref, f32[416,768]{1,0:T(8,128)} %get-tuple-element.139.x1_ref, ...), custom_call_target="tpu_custom_call" | custom-call | flops 3925868544 | bytes 51260940 | tf_op jit(solution)/shard_map/pallas_call | solution.py:179
  598.0 7.5 shard_map.215
  613.9 13.8 %all-to-all-done.7 = bf16[4,104,768]{2,1,0:T(8,128)(2,1)} async-done(((bf16[4,104,768]{2,1,0:T(8,128)(2,1)}), bf16[4,104,768]{2,1,0:T(8,128)(2,1)}, u32[]{:S(2)}, u32[]{:S(2)}) %all-to-all-start.7) | async-done | bytes 639008 | tf_op jit(solution)/shard_map/all_to_all | solution.py:714
  632.1 12.7 %collective-permute-done.19.refs_13_ = bf16[2,192,384]{2,1,0:T(8,128)(2,1)} collective-permute-done((bf16[2,192,384]{2,1,0:T(8,128)(2,1)}, bf16[2,192,384]{2,1,0:T(8,128)(2,1)}, u32[]{:S(2)}, u32[]{:S(2)}) %collective-permute-start.19) | collective-permute-done | bytes 294944 | tf_op jit(solution)/shard_map/ppermute | solution.py:866
  660.5 18.1 %shard_map.217 = (bf16[416,768]{1,0:T(8,128)(2,1)}, bf16[3,2,2,192,384]{4,3,2,1,0:T(8,128)(2,1)}, bf16[3,2,2,192,384]{4,3,2,1,0:T(8,128)(2,1)}) custom-call(s32[3]{0:T(128)} %pad_add_fusion.me_ref, bf16[416,768]{1,0:T(8,128)(2,1)} %bitcast.68.do_ref, bf16[416,768]{1,0:T(8,128)(2,1)} %bitcast.247, bf16[3,416,768]{2,1,0:T(8,128)(2,1)} %get-tuple-element.223.qkv_ref, ...), custom_call_target="tpu_custom_call" | custom-call | flops 2944401408 | bytes 27446796 | tf_op jit(solution)/shard_map/pallas_call | solution.py:179
  689.5 14.7 %all-to-all-done.8 = bf16[4,104,768]{2,1,0:T(8,128)(2,1)} async-done(((bf16[4,104,768]{2,1,0:T(8,128)(2,1)}), bf16[4,104,768]{2,1,0:T(8,128)(2,1)}, u32[]{:S(2)}, u32[]{:S(2)}) %all-to-all-start.8) | async-done | bytes 639008 | tf_op jit(solution)/shard_map/all_to_all | solution.py:714
  755.5 12.0 %shard_map.202 = f32[416,768]{1,0:T(8,128)} custom-call(f32[416,768]{1,0:T(8,128)} %get-tuple-element.146.x2_ref, bf16[17,2,768,384]{3,2,1,0:T(8,128)(2,1)} %bitcast.222, bf16[17,2,768,384]{3,2,1,0:T(8,128)(2,1)} %bitcast.223, f32[6,768]{1,0:T(8,128)} %squeeze.60.rest_0_.gb_ref), custom_call_target="tpu_custom_call" | custom-call | flops 3925868544 | bytes 42682368 | tf_op jit(solution)/shard_map/pallas_call | solution.py:179
  794.1 8.7 %all-to-all-done.13 = bf16[4,8,48,384]{3,2,1,0:T(8,128)(2,1)S(1)} async-done(((bf16[4,8,48,384]{3,2,1,0:T(8,128)(2,1)}), bf16[4,8,48,384]{3,2,1,0:T(8,128)(2,1)S(1)}, u32[]{:S(2)}, u32[]{:S(2)}) %all-to-all-start.13) | async-done | bytes 1179680 | tf_op jit(solution)/shard_map/all_to_all | solution.py:898
  810.6 14.1 %all-to-all-done.9 = bf16[4,5,48,384]{3,2,1,0:T(8,128)(2,1)S(1)} async-done(((bf16[4,5,48,384]{3,2,1,0:T(8,128)(2,1)}), bf16[4,5,48,384]{3,2,1,0:T(8,128)(2,1)S(1)}, u32[]{:S(2)}, u32[]{:S(2)}) %all-to-all-start.9) | async-done | bytes 737312 | tf_op jit(solution)/shard_map/all_to_all | solution.py:898
  (300 shorter events, 231.8 us)
Async XLA Ops:
  7.2 141.4 %all-gather.3.cloned.1.call-start = ((), (), s32[]{:S(2)}) async-start(), calls=%async_computation.16 | async-start | bytes 20680704 | tf_op jit(solution)/shard_map/all_gather | solution.py:741
  10.5 290.1 %all-gather.5.cloned.1.call-start = ((), (), s32[]{:S(2)}) async-start(), calls=%async_computation.17 | async-start | bytes 20680704 | tf_op jit(solution)/shard_map/all_gather | solution.py:741
  160.6 29.1 %all-to-all-start.2 = ((bf16[4,104,768]{2,1,0:T(8,128)(2,1)}), bf16[4,104,768]{2,1,0:T(8,128)(2,1)S(1)}, u32[]{:S(2)}, u32[]{:S(2)}) async-start(bf16[4,104,768]{2,1,0:T(8,128)(2,1)} %bitcast.270), calls=%async_computation.2 | async-start | bytes 1277952 | tf_op jit(solution)/shard_map/all_to_all | solution.py:714
  223.0 77.6 %all-to-all-start.3 = ((bf16[4,104,768]{2,1,0:T(8,128)(2,1)}), bf16[4,104,768]{2,1,0:T(8,128)(2,1)S(1)}, u32[]{:S(2)}, u32[]{:S(2)}) async-start(bf16[4,104,768]{2,1,0:T(8,128)(2,1)} %bitcast.271), calls=%async_computation.3 | async-start | bytes 1277952 | tf_op jit(solution)/shard_map/all_to_all | solution.py:714
  376.8 22.7 %collective-permute-start = (bf16[8,2,2,192,384]{4,3,2,1,0:T(8,128)(2,1)}, bf16[8,2,2,192,384]{4,3,2,1,0:T(8,128)(2,1)S(1)}, u32[]{:S(2)}, u32[]{:S(2)}) collective-permute-start(bf16[8,2,2,192,384]{4,3,2,1,0:T(8,128)(2,1)} %bitcast.288), channel_id=1, source_target_pairs={{0,8},{8,0},{16,24},{24,16},{1,9},{9,1},{17,25},{25,17},{2,10},{10... | collective-permute-start | bytes 14155784 | tf_op jit(solution)/shard_map/ppermute | solution.py:866
  398.9 22.5 %collective-permute-start.3 = (bf16[4,2,2,192,384]{4,3,2,1,0:T(8,128)(2,1)}, bf16[4,2,2,192,384]{4,3,2,1,0:T(8,128)(2,1)S(1)}, u32[]{:S(2)}, u32[]{:S(2)}) collective-permute-start(bf16[4,2,2,192,384]{4,3,2,1,0:T(8,128)(2,1)} %get-tuple-element.162), channel_id=1, source_target_pairs={{0,8},{8,0},{16,24},{24,16},{1,9},{9,1},{17,25},{25,17},{2,10},{10... | collective-permute-start | bytes 7077896 | tf_op jit(solution)/shard_map/ppermute | solution.py:866
  406.3 28.2 %collective-permute-start.1 = (bf16[4,2,192,384]{3,2,1,0:T(8,128)(2,1)}, bf16[4,2,192,384]{3,2,1,0:T(8,128)(2,1)S(1)}, u32[]{:S(2)}, u32[]{:S(2)}) collective-permute-start(bf16[4,2,192,384]{3,2,1,0:T(8,128)(2,1)} %get-tuple-element.159), channel_id=1, source_target_pairs={{0,16},{8,24},{16,0},{24,8},{1,17},{9,25},{17,1},{25,9},{2,18},{10... | collective-permute-start | bytes 3538952 | tf_op jit(solution)/shard_map/ppermute | solution.py:866
  407.8 27.9 %collective-permute-start.2 = (bf16[4,2,192,384]{3,2,1,0:T(8,128)(2,1)}, bf16[4,2,192,384]{3,2,1,0:T(8,128)(2,1)}, u32[]{:S(2)}, u32[]{:S(2)}) collective-permute-start(bf16[4,2,192,384]{3,2,1,0:T(8,128)(2,1)} %get-tuple-element.160), channel_id=1, source_target_pairs={{0,1},{1,0},{2,3},{3,2},{4,5},{5,4},{6,7},{7,6},{8,9},{9,8},{10,11... | collective-permute-start | bytes 3538952 | tf_op jit(solution)/shard_map/ppermute | solution.py:866
  417.1 23.6 %all-to-all-start.5 = ((bf16[4,104,768]{2,1,0:T(8,128)(2,1)}), bf16[4,104,768]{2,1,0:T(8,128)(2,1)}, u32[]{:S(2)}, u32[]{:S(2)}) async-start(bf16[4,104,768]{2,1,0:T(8,128)(2,1)} %bitcast.269), calls=%async_computation.5 | async-start | bytes 1277952 | tf_op jit(solution)/shard_map/all_to_all | solution.py:714
  460.6 32.6 %collective-permute-start.9 = (bf16[3,2,2,192,384]{4,3,2,1,0:T(8,128)(2,1)}, bf16[3,2,2,192,384]{4,3,2,1,0:T(8,128)(2,1)S(1)}, u32[]{:S(2)}, u32[]{:S(2)}) collective-permute-start(bf16[3,2,2,192,384]{4,3,2,1,0:T(8,128)(2,1)} %get-tuple-element.183), channel_id=1, source_target_pairs={{0,8},{8,0},{16,24},{24,16},{1,9},{9,1},{17,25},{25,17},{2,10},{10... | collective-permute-start | bytes 5308424 | tf_op jit(solution)/shard_map/ppermute | solution.py:866
  461.9 27.1 %collective-permute-start.6 = (bf16[2,2,192,384]{3,2,1,0:T(8,128)(2,1)S(1)}, bf16[2,2,192,384]{3,2,1,0:T(8,128)(2,1)S(1)}, u32[]{:S(2)}, u32[]{:S(2)}) collective-permute-start(bf16[2,2,192,384]{3,2,1,0:T(8,128)(2,1)S(1)} %copy-done.48), channel_id=1, source_target_pairs={{0,16},{8,24},{16,0},{24,8},{1,17},{9,25},{17,1},{25,9},{2,18},{10... | collective-permute-start | bytes 1769480 | tf_op jit(solution)/shard_map/ppermute | solution.py:866
  462.7 26.3 %collective-permute-start.7 = (bf16[2,2,192,384]{3,2,1,0:T(8,128)(2,1)S(1)}, bf16[2,2,192,384]{3,2,1,0:T(8,128)(2,1)}, u32[]{:S(2)}, u32[]{:S(2)}) collective-permute-start(bf16[2,2,192,384]{3,2,1,0:T(8,128)(2,1)S(1)} %copy-done.47), channel_id=1, source_target_pairs={{0,1},{1,0},{2,3},{3,2},{4,5},{5,4},{6,7},{7,6},{8,9},{9,8},{10,11... | collective-permute-start | bytes 1769480 | tf_op jit(solution)/shard_map/ppermute | solution.py:866
  463.1 30.1 %collective-permute-start.8 = (bf16[2,2,2,192,384]{4,3,2,1,0:T(8,128)(2,1)}, bf16[2,2,2,192,384]{4,3,2,1,0:T(8,128)(2,1)S(1)}, u32[]{:S(2)}, u32[]{:S(2)}) collective-permute-start(bf16[2,2,2,192,384]{4,3,2,1,0:T(8,128)(2,1)} %get-tuple-element.181), channel_id=1, source_target_pairs={{0,8},{8,0},{16,24},{24,16},{1,9},{9,1},{17,25},{25,17},{2,10},{10... | collective-permute-start | bytes 3538952 | tf_op jit(solution)/shard_map/ppermute | solution.py:866
  536.7 56.6 %collective-permute-start.14 = (bf16[8,2,2,192,384]{4,3,2,1,0:T(8,128)(2,1)}, bf16[8,2,2,192,384]{4,3,2,1,0:T(8,128)(2,1)}, u32[]{:S(2)}, u32[]{:S(2)}) collective-permute-start(bf16[8,2,2,192,384]{4,3,2,1,0:T(8,128)(2,1)} %bitcast.287), channel_id=1, source_target_pairs={{0,8},{8,0},{16,24},{24,16},{1,9},{9,1},{17,25},{25,17},{2,10},{10... | collective-permute-start | bytes 14155784 | tf_op jit(solution)/shard_map/ppermute | solution.py:866
  536.8 28.6 %collective-permute-start.12 = (bf16[3,2,192,384]{3,2,1,0:T(8,128)(2,1)}, bf16[3,2,192,384]{3,2,1,0:T(8,128)(2,1)S(1)}, u32[]{:S(2)}, u32[]{:S(2)}) collective-permute-start(bf16[3,2,192,384]{3,2,1,0:T(8,128)(2,1)} %get-tuple-element.194), channel_id=1, source_target_pairs={{0,16},{8,24},{16,0},{24,8},{1,17},{9,25},{17,1},{25,9},{2,18},{10... | collective-permute-start | bytes 2654216 | tf_op jit(solution)/shard_map/ppermute | solution.py:866
  538.1 27.3 %collective-permute-start.13 = (bf16[2,2,192,384]{3,2,1,0:T(8,128)(2,1)}, bf16[2,2,192,384]{3,2,1,0:T(8,128)(2,1)S(1)}, u32[]{:S(2)}, u32[]{:S(2)}) collective-permute-start(bf16[2,2,192,384]{3,2,1,0:T(8,128)(2,1)} %get-tuple-element.195), channel_id=1, source_target_pairs={{0,1},{1,0},{2,3},{3,2},{4,5},{5,4},{6,7},{7,6},{8,9},{9,8},{10,11... | collective-permute-start | bytes 1769480 | tf_op jit(solution)/shard_map/ppermute | solution.py:866
  540.1 25.3 %collective-permute-start.11 = (bf16[2,192,384]{2,1,0:T(8,128)(2,1)S(1)}, bf16[2,192,384]{2,1,0:T(8,128)(2,1)S(1)}, u32[]{:S(2)}, u32[]{:S(2)}) collective-permute-start(bf16[2,192,384]{2,1,0:T(8,128)(2,1)S(1)} %copy-done.52), channel_id=1, source_target_pairs={{0,16},{8,24},{16,0},{24,8},{1,17},{9,25},{17,1},{25,9},{2,18},{10... | collective-permute-start | bytes 884744 | tf_op jit(solution)/shard_map/ppermute | solution.py:866
  540.9 64.7 %all-to-all-start.14 = ((bf16[4,8,48,384]{3,2,1,0:T(8,128)(2,1)}), bf16[4,8,48,384]{3,2,1,0:T(8,128)(2,1)S(1)}, u32[]{:S(2)}, u32[]{:S(2)}) async-start(bf16[4,8,48,384]{3,2,1,0:T(8,128)(2,1)} %get-tuple-element.256), calls=%async_computation.14 | async-start | bytes 2359296 | tf_op jit(solution)/shard_map/all_to_all | solution.py:898
  593.2 55.7 %collective-permute-start.17 = (bf16[4,2,2,192,384]{4,3,2,1,0:T(8,128)(2,1)}, bf16[4,2,2,192,384]{4,3,2,1,0:T(8,128)(2,1)S(1)}, u32[]{:S(2)}, u32[]{:S(2)}) collective-permute-start(bf16[4,2,2,192,384]{4,3,2,1,0:T(8,128)(2,1)} %get-tuple-element.214), channel_id=1, source_target_pairs={{0,8},{8,0},{16,24},{24,16},{1,9},{9,1},{17,25},{25,17},{2,10},{10... | collective-permute-start | bytes 7077896 | tf_op jit(solution)/shard_map/ppermute | solution.py:866
  609.8 39.2 %collective-permute-start.15 = (bf16[4,2,192,384]{3,2,1,0:T(8,128)(2,1)}, bf16[4,2,192,384]{3,2,1,0:T(8,128)(2,1)}, u32[]{:S(2)}, u32[]{:S(2)}) collective-permute-start(bf16[4,2,192,384]{3,2,1,0:T(8,128)(2,1)} %get-tuple-element.211), channel_id=1, source_target_pairs={{0,16},{8,24},{16,0},{24,8},{1,17},{9,25},{17,1},{25,9},{2,18},{10... | collective-permute-start | bytes 3538952 | tf_op jit(solution)/shard_map/ppermute | solution.py:866
  611.0 37.9 %collective-permute-start.16 = (bf16[4,2,192,384]{3,2,1,0:T(8,128)(2,1)}, bf16[4,2,192,384]{3,2,1,0:T(8,128)(2,1)}, u32[]{:S(2)}, u32[]{:S(2)}) collective-permute-start(bf16[4,2,192,384]{3,2,1,0:T(8,128)(2,1)} %get-tuple-element.212), channel_id=1, source_target_pairs={{0,1},{1,0},{2,3},{3,2},{4,5},{5,4},{6,7},{7,6},{8,9},{9,8},{10,11... | collective-permute-start | bytes 3538952 | tf_op jit(solution)/shard_map/ppermute | solution.py:866
  611.4 37.5 %collective-permute-start.18 = (bf16[3,192,384]{2,1,0:T(8,128)(2,1)}, bf16[3,192,384]{2,1,0:T(8,128)(2,1)}, u32[]{:S(2)}, u32[]{:S(2)}) collective-permute-start(bf16[3,192,384]{2,1,0:T(8,128)(2,1)} %get-tuple-element.215), channel_id=1, source_target_pairs={{0,1},{1,0},{2,3},{3,2},{4,5},{5,4},{6,7},{7,6},{8,9},{9,8},{10,11... | collective-permute-start | bytes 1327112 | tf_op jit(solution)/shard_map/ppermute | solution.py:866
  613.1 31.8 %collective-permute-start.19 = (bf16[2,192,384]{2,1,0:T(8,128)(2,1)}, bf16[2,192,384]{2,1,0:T(8,128)(2,1)}, u32[]{:S(2)}, u32[]{:S(2)}) collective-permute-start(bf16[2,192,384]{2,1,0:T(8,128)(2,1)} %get-tuple-element.216), channel_id=1, source_target_pairs={{0,16},{8,24},{16,0},{24,8},{1,17},{9,25},{17,1},{25,9},{2,18},{10... | collective-permute-start | bytes 884744 | tf_op jit(solution)/shard_map/ppermute | solution.py:866
  627.7 56.4 %all-to-all-start.12 = ((bf16[4,4,48,384]{3,2,1,0:T(8,128)(2,1)}), bf16[4,4,48,384]{3,2,1,0:T(8,128)(2,1)}, u32[]{:S(2)}, u32[]{:S(2)}) async-start(bf16[4,4,48,384]{3,2,1,0:T(8,128)(2,1)} %get-tuple-element.254), calls=%async_computation.12 | async-start | bytes 1179648 | tf_op jit(solution)/shard_map/all_to_all | solution.py:898
  657.8 26.4 %collective-permute-start.22 = (bf16[2,2,192,384]{3,2,1,0:T(8,128)(2,1)}, bf16[2,2,192,384]{3,2,1,0:T(8,128)(2,1)S(1)}, u32[]{:S(2)}, u32[]{:S(2)}) collective-permute-start(bf16[2,2,192,384]{3,2,1,0:T(8,128)(2,1)} %get-tuple-element.228), channel_id=1, source_target_pairs={{0,16},{8,24},{16,0},{24,8},{1,17},{9,25},{17,1},{25,9},{2,18},{10... | collective-permute-start | bytes 1769480 | tf_op jit(solution)/shard_map/ppermute | solution.py:866
  659.0 25.2 %collective-permute-start.23 = (bf16[2,2,192,384]{3,2,1,0:T(8,128)(2,1)}, bf16[2,2,192,384]{3,2,1,0:T(8,128)(2,1)S(1)}, u32[]{:S(2)}, u32[]{:S(2)}) collective-permute-start(bf16[2,2,192,384]{3,2,1,0:T(8,128)(2,1)} %get-tuple-element.229), channel_id=1, source_target_pairs={{0,1},{1,0},{2,3},{3,2},{4,5},{5,4},{6,7},{7,6},{8,9},{9,8},{10,11... | collective-permute-start | bytes 1769480 | tf_op jit(solution)/shard_map/ppermute | solution.py:866
  678.7 30.6 %collective-permute-start.25 = (bf16[3,2,2,192,384]{4,3,2,1,0:T(8,128)(2,1)}, bf16[3,2,2,192,384]{4,3,2,1,0:T(8,128)(2,1)S(1)}, u32[]{:S(2)}, u32[]{:S(2)}) collective-permute-start(bf16[3,2,2,192,384]{4,3,2,1,0:T(8,128)(2,1)} %get-tuple-element.238), channel_id=1, source_target_pairs={{0,8},{8,0},{16,24},{24,16},{1,9},{9,1},{17,25},{25,17},{2,10},{10... | collective-permute-start | bytes 5308424 | tf_op jit(solution)/shard_map/ppermute | solution.py:866
  704.2 23.2 %all-to-all-start.10 = ((bf16[4,5,48,384]{3,2,1,0:T(8,128)(2,1)}), bf16[4,5,48,384]{3,2,1,0:T(8,128)(2,1)}, u32[]{:S(2)}, u32[]{:S(2)}) async-start(bf16[4,5,48,384]{3,2,1,0:T(8,128)(2,1)} %get-tuple-element.252), calls=%async_computation.10 | async-start | bytes 1474560 | tf_op jit(solution)/shard_map/all_to_all | solution.py:898
  717.3 27.4 %collective-permute-start.26 = (bf16[3,2,192,384]{3,2,1,0:T(8,128)(2,1)}, bf16[3,2,192,384]{3,2,1,0:T(8,128)(2,1)S(1)}, u32[]{:S(2)}, u32[]{:S(2)}) collective-permute-start(bf16[3,2,192,384]{3,2,1,0:T(8,128)(2,1)} %get-tuple-element.246), channel_id=1, source_target_pairs={{0,16},{8,24},{16,0},{24,8},{1,17},{9,25},{17,1},{25,9},{2,18},{10... | collective-permute-start | bytes 2654216 | tf_op jit(solution)/shard_map/ppermute | solution.py:866
  718.2 26.5 %collective-permute-start.29 = (bf16[2,2,192,384]{3,2,1,0:T(8,128)(2,1)}, bf16[2,2,192,384]{3,2,1,0:T(8,128)(2,1)S(1)}, u32[]{:S(2)}, u32[]{:S(2)}) collective-permute-start(bf16[2,2,192,384]{3,2,1,0:T(8,128)(2,1)} %get-tuple-element.249), channel_id=1, source_target_pairs={{0,1},{1,0},{2,3},{3,2},{4,5},{5,4},{6,7},{7,6},{8,9},{9,8},{10,11... | collective-permute-start | bytes 1769480 | tf_op jit(solution)/shard_map/ppermute | solution.py:866
  727.5 23.3 %all-to-all-start.15 = ((f32[32,1,384]{2,1,0:T(1,128)}), f32[32,1,384]{2,1,0:T(1,128)S(1)}, u32[]{:S(2)}, u32[]{:S(2)}) async-start(f32[32,1,384]{2,1,0:T(1,128)} %copy.127), calls=%async_computation.15 | async-start | bytes 98304 | tf_op jit(solution)/shard_map/all_to_all | solution.py:969
  771.7 31.1 %all-to-all-start.13 = ((bf16[4,8,48,384]{3,2,1,0:T(8,128)(2,1)}), bf16[4,8,48,384]{3,2,1,0:T(8,128)(2,1)S(1)}, u32[]{:S(2)}, u32[]{:S(2)}) async-start(bf16[4,8,48,384]{3,2,1,0:T(8,128)(2,1)} %get-tuple-element.255), calls=%async_computation.13 | async-start | bytes 2359296 | tf_op jit(solution)/shard_map/all_to_all | solution.py:898
  (70 other events, 676.7 us)
Sparse Core Ops, SparseCore 0:
  11.1 137.4 all-gather.2
  151.7 148.8 all-gather.4

commit v5 on v4

--- a/solution.py
+++ b/solution.py
@@ -755,109 +755,123 @@
     return part.transpose(1, 0, 3, 2, 4).reshape(1, shares, depth, width)
 
 
-class Term:
-    def __init__(self, array, names, first, count):
-        self.array = array
-        self.names = names
+class Piece:
+    def __init__(self, keep, got, first, n, order):
+        self.near = (keep, got)
         self.first = first
-        self.count = count
-
-    def cut(self, first, count):
-        return Term(self.array, self.names, self.first + first, count)
-
-
-class Job:
-    def __init__(self, pieces, other, ways):
-        self.pieces = pieces
-        self.other = other
-        self.ways = ways
-        names = pieces[0][-1].names
-        self.lead = () if other is None else tuple(2 for n in names if n != other)
-        self.count = sum(piece[0].count for piece in pieces)
-        self.rows, self.width = pieces[0][0].array.shape[-2:]
-
-    def shape(self):
-        if self.other is None:
-            return (self.ways, self.count, self.rows // self.ways, self.width)
-        return (self.count,) + self.lead + (self.rows, self.width)
-
-
-def fold(jobs, me):
-    place = {"x": 1, "h": 2}
-    terms = [t for job in jobs for piece in job.pieces for t in piece]
+        self.n = n
+        self.order = order
+        self.step = 0
+        self.held = []
+        self.result = None
+
+
+PLACE = {"x": 1, "h": 2}
+
+
+def fold(pieces, me):
+    ways = lax.axis_size("seq")
+    depth, width = pieces[0].near[0].shape[-2:]
+    r = depth // ways
+    used = {}
     arrays = []
-    for t in terms:
-        if not any(t.array is a for a in arrays):
-            arrays.append(t.array)
-    number = [next(i for i, a in enumerate(arrays) if a is t.array) for t in terms]
-    rooms = []
-    for job in jobs:
-        for piece in job.pieces:
-            rooms += [(t.count,) + job.lead + (job.rows, job.width) for t in piece]
+
+    def number(a):
+        for i, known in enumerate(arrays):
+            if known is a:
+                return i
+        arrays.append(a)
+        return len(arrays) - 1
+
+    plans = []
+    for p in pieces:
+        link = p.order[p.step] if p.step < 2 else "z"
+        blocks = p.n * (2 if p.step == 0 else 1)
+        base = used.get(link, 0)
+        used[link] = base + blocks
+        near = [number(a) for a in p.near]
+        held = [(number(a), at) for a, at in p.held]
+        plans.append((p, link, base, near, held))
+    links = sorted(used)
+    shapes = [
+        (ways, used[k], r, width) if k == "z" else (used[k], depth, width) for k in links
+    ]
+    rooms, counts = [], []
+    for p, link, base, near, held in plans:
+        each = 2 if p.step == 0 else 1
+        counts.append((each, len(near) + len(held)))
+        rooms += [(each * p.n, depth, width)] * (len(near) + len(held))
+    copies_needed = sum(each * terms for each, terms in counts)
 
     def body(me_ref, *refs):
         sources = refs[: len(arrays)]
-        outs = refs[len(arrays) : len(arrays) + len(jobs)]
-        held = refs[len(arrays) + len(jobs) : -1]
+        outs = dict(zip(links, refs[len(arrays) : len(arrays) + len(links)]))
+        held_refs = refs[len(arrays) + len(links) : -1]
         sems = refs[-1]
-        copies = []
-        for job in jobs:
-            for piece in job.pieces:
-                for t in piece:
-                    n = len(copies)
-                    at = [pl.ds(t.first, t.count)]
-                    for name in t.names:
-                        if name == job.other:
-                            at.append(1 - me_ref[place[name]])
-                        elif job.other is not None and name in job.pieces[0][-1].names:
-                            at.append(slice(None))
-                        else:
-                            at.append(me_ref[place[name]])
-                    copies.append(
-                        pltpu.make_async_copy(sources[number[n]].at[tuple(at)], held[n], sems.at[n])
-                    )
-        for copy in copies:
-            copy.start()
-        n = 0
-        for job, out in zip(jobs, outs):
-            base = 0
-            for piece in job.pieces:
-                these = held[n : n + len(piece)]
-                for k in range(len(piece)):
-                    copies[n + k].wait()
-                n += len(piece)
-
-                @pl.loop(0, piece[0].count)
-                def _(i, these=these, base=base, out=out, job=job):
-                    def total(at):
-                        value = these[0][at].astype(F32)
-                        for one in these[1:]:
-                            value = value + one[at].astype(F32)
-                        return value.astype(BF16)
-
-                    if job.other is None:
-                        value = total((i,))
-                        r = job.rows // job.ways
-                        for s in range(job.ways):
-                            out[s, base + i] = value[s * r : (s + 1) * r]
-                    elif job.lead:
-                        for k in range(2):
-                            out[base + i, k] = total((i, k))
-                    else:
-                        out[base + i] = total((i,))
-
-                base += piece[0].count
-
-    moved = sum(2 * math.prod(r) for r in rooms) + sum(2 * math.prod(j.shape()) for j in jobs)
-    return pl.pallas_call(
+        mine = {name: me_ref[PLACE[name]] for name in PLACE}
+        groups = []
+        room = 0
+        sem = 0
+        for p, link, base, near, held in plans:
+            group = []
+            if p.step == 0:
+                for term in near:
+                    for k in range(2):
+                        pick = {p.order[0]: 1 - mine[p.order[0]], p.order[1]: k}
+                        source = sources[term].at[pl.ds(p.first, p.n), pick["h"], pick["x"]]
+                        group.append((source, held_refs[room].at[pl.ds(k * p.n, p.n)]))
+                    room += 1
+            else:
+                last = p.order[1]
+                pick = {p.order[0]: mine[p.order[0]]}
+                pick[last] = 1 - mine[last] if p.step == 1 else mine[last]
+                for term in near:
+                    source = sources[term].at[pl.ds(p.first, p.n), pick["h"], pick["x"]]
+                    group.append((source, held_refs[room]))
+                    room += 1
+                for i, (term, at) in enumerate(held):
+                    start = at + pick[last] * p.n if i == 0 else at
+                    group.append((sources[term].at[pl.ds(start, p.n)], held_refs[room]))
+                    room += 1
+            made_copies = []
+            for source, target in group:
+                made_copies.append(pltpu.make_async_copy(source, target, sems.at[sem]))
+                sem += 1
+            groups.append(made_copies)
+        for group in groups:
+            for copy in group:
+                copy.start()
+        room = 0
+        for (p, link, base, near, held), (each, terms), group in zip(plans, counts, groups):
+            these = held_refs[room : room + terms]
+            room += terms
+            for copy in group:
+                copy.wait()
+
+            @pl.loop(0, each * p.n)
+            def _(i, these=these, base=base, out=outs[link], last=p.step == 2):
+                value = these[0][i].astype(F32)
+                for one in these[1:]:
+                    value = value + one[i].astype(F32)
+                value = value.astype(BF16)
+                if last:
+                    for k in range(ways):
+                        out[k, base + i] = value[k * r : (k + 1) * r]
+                else:
+                    out[base + i] = value
+
+    moved = sum(2 * math.prod(room) for room in rooms) + sum(2 * math.prod(shape) for shape in shapes)
+    sums = pl.pallas_call(
         body,
-        out_shape=[jax.ShapeDtypeStruct(job.shape(), BF16) for job in jobs],
+        out_shape=[jax.ShapeDtypeStruct(shape, BF16) for shape in shapes],
         in_specs=[SCALARS] + [pl.BlockSpec(memory_space=pl.ANY)] * len(arrays),
-        out_specs=[pl.BlockSpec(memory_space=pltpu.VMEM)] * len(jobs),
-        scratch_shapes=[pltpu.VMEM(r, BF16) for r in rooms] + [pltpu.SemaphoreType.DMA((len(rooms),))],
+        out_specs=[pl.BlockSpec(memory_space=pltpu.VMEM)] * len(links),
+        scratch_shapes=[pltpu.VMEM(room, BF16) for room in rooms]
+        + [pltpu.SemaphoreType.DMA((copies_needed,))],
         compiler_params=pltpu.CompilerParams(vmem_limit_bytes=VMEM),
         cost_estimate=pl.CostEstimate(flops=0, bytes_accessed=moved, transcendentals=0),
     )(me, *arrays)
+    return [(p, link, base) for p, link, base, _, _ in plans], dict(zip(links, sums))
 
 
 def cross(a, name):
@@ -866,71 +880,52 @@
     return lax.ppermute(a, axis, [(i, i ^ (1 << bit)) for i in range(size)])
 
 
-class Group:
-    def __init__(self, halves_of):
-        self.pieces = []
-        for keep, send in halves_of:
-            got = cross(send, "c")
-            n = keep.shape[0]
-            self.pieces.append([Term(a, ("h", "x"), 0, n) for a in (keep, got)])
-        total = sum(p[0].count for p in self.pieces)
-        self.parts = ([], [])
-        seen = 0
-        for piece in self.pieces:
-            n = piece[0].count
-            first = min(max((total + 1) // 2 - seen, 0), n)
-            if first:
-                self.parts[0].append([t.cut(0, first) for t in piece])
-            if n > first:
-                self.parts[1].append([t.cut(first, n - first) for t in piece])
-            seen += n
-        self.step = 0
-        self.result = None
-
-    def jobs(self, ways):
-        if self.step == 2:
-            return [Job(self.parts[0] + self.parts[1], None, ways)]
-        orders = (("x", "h"), ("h", "x"))
-        return [Job(part, order[self.step], ways) for part, order in zip(self.parts, orders)]
-
-    def go(self, sums):
-        if self.step == 2:
-            got = lax.all_to_all(sums[0], "seq", split_axis=0, concat_axis=0, tiled=True)
-            self.result = jnp.sum(got.astype(F32), axis=0)
+def pieces_of(halves_of):
+    total = sum(keep.shape[0] for keep, _ in halves_of)
+    found = []
+    seen = 0
+    for keep, send in halves_of:
+        got = cross(send, "c")
+        n = keep.shape[0]
+        first = min(max((total + 1) // 2 - seen, 0), n)
+        if first:
+            found.append(Piece(keep, got, 0, first, ("x", "h")))
+        if n > first:
+            found.append(Piece(keep, got, first, n - first, ("h", "x")))
+        seen += n
+    return found
+
+
+def move(x, pieces, me):
+    plans, sums = fold(pieces, me)
+    x, sums = lax.optimization_barrier((x, sums))
+    got = {}
+    for link, array in sums.items():
+        if link == "z":
+            every = lax.all_to_all(array, "seq", split_axis=0, concat_axis=0, tiled=True)
+            got[link] = jnp.sum(every.astype(F32), axis=0)
         else:
-            orders = (("x", "h"), ("h", "x"))
-            left = (orders[0][1 - self.step], orders[1][1 - self.step])
-            for part, order, name, one in zip(self.parts, orders, left, sums):
-                got = cross(one, order[self.step])
-                base = 0
-                for piece in part:
-                    names = () if self.step else (name,)
-                    piece.append(Term(got, names, base, piece[0].count))
-                    base += piece[0].count
-        self.step += 1
-
-
-def move(x, groups, me):
-    ways = lax.axis_size("seq")
-    jobs = [g.jobs(ways) for g in groups]
-    sums = fold([j for some in jobs for j in some], me)
-    x, sums = lax.optimization_barrier((x, sums))
-    for g, some in zip(groups, jobs):
-        g.go(sums[: len(some)])
-        sums = sums[len(some) :]
+            got[link] = cross(array, link)
+    for p, link, base in plans:
+        if link == "z":
+            p.result = got[link][base : base + p.n]
+        else:
+            p.held.append((got[link], base))
+        p.step += 1
     return x
 
 
-def settle(x, groups):
-    terms = {}
-    for g in groups:
-        for part in g.parts:
-            for piece in part:
-                terms.setdefault(id(piece[-1].array), []).append(piece[-1])
-    x, arrays = lax.optimization_barrier((x, [same[0].array for same in terms.values()]))
-    for same, array in zip(terms.values(), arrays):
-        for term in same:
-            term.array = array
+def settle(x, pieces):
+    arrays = []
+    for p in pieces:
+        if not any(p.held[-1][0] is a for a in arrays):
+            arrays.append(p.held[-1][0])
+    x, came = lax.optimization_barrier((x, arrays))
+    for p in pieces:
+        for old, new in zip(arrays, came):
+            if p.held[-1][0] is old:
+                p.held[-1] = (new, p.held[-1][1])
+                break
     return x
 
 
@@ -1041,35 +1036,37 @@
         x, a1, qkv1, log1, o1, y1, x1, qkv2, o2, log2, x2 = kept[l]
         grad, g_ff, s3 = mlp_backward(rows, grad, x2, w, gb[l], me, halves)
         if quick:
-            ff = Group([g_ff])
+            ff = pieces_of([g_ff])
             if late:
+                grad = settle(grad, late)
                 grad = move(grad, late, me)
+                late = [p for p in late if p.step < 3]
         grad, g_space, s2 = space_backward(rows, grad, x1, qkv2, o2, log2, w, gb[l], me, halves)
         if quick:
-            space = Group([g_space])
-            grad = move(grad, [ff], me)
+            space = pieces_of([g_space])
+            grad = move(grad, ff, me)
         do1, g_out = middle_backward(rows, grad, y1, o1, w, mixes[l], me, halves, shards)
         do1 = swap_places(do1)
         if quick:
-            do1 = move(do1, [ff, space] + late[1:], me)
+            do1 = move(do1, ff + space + late, me)
         da1, g_time = time_backward(rows, do1, a1, qkv1, log1, w, me, halves)
         if quick:
-            da1 = settle(da1, [ff, space])
+            da1 = settle(da1, ff + space)
         da1 = swap_places(da1)
         if quick:
-            rest = Group([g_out, g_time])
-            da1 = move(da1, [ff, space, rest], me)
-            late = [space, rest]
+            rest = pieces_of([g_out, g_time])
+            da1 = move(da1, ff + space + rest, me)
+            late = space + rest
         grad, s1 = first_norm_back(rows, da1, x, grad, gb[l])
         norm_rows[l] = jnp.concatenate((s1[0:1], s2[0:1], s3[0:1], s1[1:2], s2[1:2], s3[1:2]), axis=0)
         if quick:
-            summed[l] = [ff, space, rest]
+            summed[l] = ff + space + rest
         else:
             summed[l] = [reduce_plain([g_ff, g_space, g_out, g_time], clip & 1)]
     if quick:
-        move((), [space, rest], me)
-        move((), [rest], me)
-        summed = [[g.result for g in some] for some in summed]
+        move((), late, me)
+        move((), rest, me)
+        summed = [[p.result for p in some] for some in summed]
     cuts = (g_ff[0].shape[0], g_space[0].shape[0], g_out[0].shape[0], g_time[0].shape[0])
     results = []
     for some in summed:

time: 840 us -> 838 us (level)
  starting transfers between devices: 93.7 us -> 80.6 us
  blocking collectives: 26.7 us -> 38.7 us
    all_to_all x0 -> x1, blocking collectives: none -> 12 us  [reduce_norms(): every = lax.all_to_all(a, ALL, split_axis=0, concat_axis=0, tiled=True)]
    all_to_all x7 -> x6, waiting for transfers between devices: 22.8 us -> 12.7 us  [move(): lax.all_to_all(array, 'seq', split_axis=0, concat_axis=0, tiled=True)]
    ppermute x32 -> x24, starting transfers between devices: 26.8 us -> 19 us  [cross(): return lax.ppermute(a, axis, [(i, i ^ 1 << bit) for i in range(size)])]
    ppermute x32 -> x24, waiting for transfers between devices: 98.6 us -> 104 us  [cross(): return lax.ppermute(a, axis, [(i, i ^ 1 << bit) for i in range(size)])]
    all_to_all x7 -> x6, starting transfers between devices: 31.3 us -> 26.1 us  [move(): lax.all_to_all(array, 'seq', split_axis=0, concat_axis=0, tiled=True)]
    unnamed x123 -> x113, local copies, waits for them, and re-layouts: 22.3 us -> 24.8 us
  transfers between devices with their start and end apart: 49 -> 40, of which waited for: 23 -> 23; matrix products, arithmetic and copies ran while one was open for 4% -> 4% of each run, Pallas kernels for 24% -> 23%
where the time goes in v5:
time: 838 us; the launch traced here: 833 us
  waiting for transfers between devices  359 us (43%)
  Pallas kernels  283 us (34%)
  starting transfers between devices  80.6 us (10%)
  local copies, waits for them, and re-layouts  42.8 us (5%)
  blocking collectives  38.7 us (5%)
  between operations  15.3 us (2%)
  other arithmetic  13.5 us (2%)
    pallas_call x19, Pallas kernels, call(): pl.pallas_call(body, out_shape=[shape for shape, _ in outs], grid=grid, i...  238 us
    all_gather x2, waiting for transfers between devices, gather_slabs(): full = lax.all_gather(pack, ('head', 'clip', 'seq'), axis=1, tiled=True)  165 us
    ppermute x24, waiting for transfers between devices, cross(): return lax.ppermute(a, axis, [(i, i ^ 1 << bit) for i in range(size)])  104 us
    all_to_all x7, waiting for transfers between devices, swap_places(): lax.all_to_all(rows_array, 'seq', split_axis=0, concat_axis=0, tiled=True)  70.4 us
    pallas_call x9, Pallas kernels, fold(): pl.pallas_call(body, out_shape=[jax.ShapeDtypeStruct(shape, BF16) for sha...  45.6 us
    all_to_all x7, starting transfers between devices, swap_places(): lax.all_to_all(rows_array, 'seq', split_axis=0, concat_axis=0, tiled=True)  28.1 us
    all_to_all x1, blocking collectives, swap_places(): lax.all_to_all(rows_array, 'seq', split_axis=0, concat_axis=0, tiled=True)  26.7 us
    all_to_all x6, starting transfers between devices, move(): lax.all_to_all(array, 'seq', split_axis=0, concat_axis=0, tiled=True)  26.1 us
  transfers between devices with their start and end apart: 40, of which 23 were waited for; matrix products, arithmetic and copies ran while one was open for 4% of the time, Pallas kernels for 23%

profile of v5, /device:TPU:0, one launch (start us, length us, event | category | flops | bytes accessed | tf_op | source)
XLA Modules:
  0.0 832.9 jit_solution(5466718132838781845)
XLA Ops:
  12.3 7.3 all-to-all-start
  30.9 26.7 %all_to_all.140 = bf16[4,104,768]{2,1,0:T(8,128)(2,1)} all-to-all(bf16[4,104,768]{2,1,0:T(8,128)(2,1)} %bitcast.257), channel_id=1, replica_groups=mesh['clip'=4,'seq'=4,'head'=2] {'seq'}, dimensions={0} | all-to-all | bytes 1277952 | tf_op jit(solution)/shard_map/all_to_all | solution.py:714
  57.6 91.0 %all-gather.3.cloned.1.call-done = bf16[17,1536,384]{2,1,0:T(8,128)(2,1)} async-done(((bf16[17,48,384]{2,1,0:T(8,128)(2,1)}), bf16[17,1536,384]{2,1,0:T(8,128)(2,1)}) %all-gather.3.cloned.1.call-update) | async-done | bytes 20054032 | tf_op jit(solution)/shard_map/all_gather | solution.py:741
  148.6 12.0 %shard_map.195 = (bf16[3,416,768]{2,1,0:T(8,128)(2,1)}, bf16[416,768]{1,0:T(8,128)(2,1)}, f32[2,3,2,416]{3,2,1,0:T(2,128)}) custom-call(bf16[416,768]{1,0:T(8,128)(2,1)} %bitcast.246, bf16[17,2,768,384]{3,2,1,0:T(8,128)(2,1)} %bitcast.224), custom_call_target="tpu_custom_call" | custom-call | flops 1472200704 | bytes 23268864 | tf_op jit(solution)/shard_map/pallas_call | solution.py:179
  169.0 20.8 %all-to-all-done.2 = bf16[4,104,768]{2,1,0:T(8,128)(2,1)S(1)} async-done(((bf16[4,104,768]{2,1,0:T(8,128)(2,1)}), bf16[4,104,768]{2,1,0:T(8,128)(2,1)S(1)}, u32[]{:S(2)}, u32[]{:S(2)}) %all-to-all-start.2) | async-done | bytes 639008 | tf_op jit(solution)/shard_map/all_to_all | solution.py:714
  190.6 9.3 %shard_map.196 = (bf16[416,768]{1,0:T(8,128)(2,1)}, bf16[416,768]{1,0:T(8,128)(2,1)}, f32[416,768]{1,0:T(8,128)}, bf16[3,416,768]{2,1,0:T(8,128)(2,1)}) custom-call(bf16[416,768]{1,0:T(8,128)(2,1)} %bitcast.255, f32[416,768]{1,0:T(8,128)} %bitcast_convert_fusion.1.x_ref, bf16[17,2,768,384]{3,2,1,0:T(8,128)(2,1)} %bitcast.225, ...), custom_call_target="tpu_custom_call" | custom-call | flops 2453667840 | bytes 47695872 | tf_op jit(solution)/shard_map/pallas_call | solution.py:179
  199.9 9.9 %shard_map.197 = (bf16[416,768]{1,0:T(8,128)(2,1)}, f32[416,768]{1,0:T(8,128)}, f32[2,3,2,2,208]{4,3,2,1,0:T(2,128)}) custom-call(bf16[3,416,768]{2,1,0:T(8,128)(2,1)} %get-tuple-element.121.qkv_ref, f32[416,768]{1,0:T(8,128)} %get-tuple-element.122.x1_ref, bf16[17,2,768,384]{3,2,1,0:T(8,128)(2,1)} %bitcast.227), custom_call_target="tpu_custom_call" | custom-call | flops 490733568 | bytes 25185792 | tf_op jit(solution)/shard_map/pallas_call | solution.py:179
  209.8 13.2 %shard_map.198 = (f32[416,768]{1,0:T(8,128)}, bf16[416,768]{1,0:T(8,128)(2,1)}) custom-call(f32[416,768]{1,0:T(8,128)} %get-tuple-element.123.x2_ref, bf16[17,2,768,384]{3,2,1,0:T(8,128)(2,1)} %bitcast.228, bf16[17,2,768,384]{3,2,1,0:T(8,128)(2,1)} %bitcast.229, f32[6,768]{1,0:T(8,128)} %squeeze.54.gb_ref, f32[6,768]{1,0:T(8,128)} %squeeze.60.rest_0_.gb_ref), custom_call_target="tpu_custom_call" | custom-call | flops 3925868544 | bytes 43339776 | tf_op jit(solution)/shard_map/pallas_call | solution.py:179
  226.5 74.3 %all-gather.5.cloned.1.call-done = bf16[17,1536,384]{2,1,0:T(8,128)(2,1)} async-done(((bf16[17,48,384]{2,1,0:T(8,128)(2,1)}), bf16[17,1536,384]{2,1,0:T(8,128)(2,1)}) %all-gather.5.cloned.1.call-update) | async-done | bytes 20054032 | tf_op jit(solution)/shard_map/all_gather | solution.py:741
  301.5 12.0 %shard_map.199 = (bf16[3,416,768]{2,1,0:T(8,128)(2,1)}, bf16[416,768]{1,0:T(8,128)(2,1)}, f32[2,3,2,416]{3,2,1,0:T(2,128)}) custom-call(bf16[416,768]{1,0:T(8,128)(2,1)} %bitcast.248, bf16[17,2,768,384]{3,2,1,0:T(8,128)(2,1)} %bitcast.212), custom_call_target="tpu_custom_call" | custom-call | flops 1472200704 | bytes 23268864 | tf_op jit(solution)/shard_map/pallas_call | solution.py:179
  322.8 12.1 %all-to-all-done.4 = bf16[4,104,768]{2,1,0:T(8,128)(2,1)S(1)} async-done(((bf16[4,104,768]{2,1,0:T(8,128)(2,1)}), bf16[4,104,768]{2,1,0:T(8,128)(2,1)S(1)}, u32[]{:S(2)}, u32[]{:S(2)}) %all-to-all-start.4) | async-done | bytes 639008 | tf_op jit(solution)/shard_map/all_to_all | solution.py:714
  335.8 8.8 %shard_map.200 = (bf16[416,768]{1,0:T(8,128)(2,1)}, bf16[416,768]{1,0:T(8,128)(2,1)}, f32[416,768]{1,0:T(8,128)}, bf16[3,416,768]{2,1,0:T(8,128)(2,1)}) custom-call(bf16[416,768]{1,0:T(8,128)(2,1)} %bitcast.254, f32[416,768]{1,0:T(8,128)} %get-tuple-element.126.x_ref, bf16[17,2,768,384]{3,2,1,0:T(8,128)(2,1)} %bitcast.213, ...), custom_call_target="tpu_custom_call" | custom-call | flops 2453667840 | bytes 47695872 | tf_op jit(solution)/shard_map/pallas_call | solution.py:179
  344.6 9.9 %shard_map.201 = (bf16[416,768]{1,0:T(8,128)(2,1)}, f32[416,768]{1,0:T(8,128)}, f32[2,3,2,2,208]{4,3,2,1,0:T(2,128)}) custom-call(bf16[3,416,768]{2,1,0:T(8,128)(2,1)} %get-tuple-element.127.qkv_ref, f32[416,768]{1,0:T(8,128)} %get-tuple-element.128.x1_ref, bf16[17,2,768,384]{3,2,1,0:T(8,128)(2,1)} %bitcast.215), custom_call_target="tpu_custom_call" | custom-call | flops 490733568 | bytes 25185792 | tf_op jit(solution)/shard_map/pallas_call | solution.py:179
  354.5 22.4 %shard_map.203 = (f32[416,768]{1,0:T(8,128)}, bf16[2,4,2,2,192,384]{5,4,3,2,1,0:T(8,128)(2,1)}, bf16[2,4,2,2,192,384]{5,4,3,2,1,0:T(8,128)(2,1)}, f32[2,768]{1,0:T(2,128)}) custom-call(s32[3]{0:T(128)} %pad_add_fusion.me_ref, f32[416,768]{1,0:T(8,128)} %bitcast_convert_fusion.g_ref, f32[416,768]{1,0:T(8,128)} %get-tuple-element.129.x2_ref, ...), custom_call_target="tpu_custom_call" | custom-call | flops 9814671360 | bytes 53403660 | tf_op jit(solution)/shard_map/pallas_call | solution.py:179
  376.9 21.8 %shard_map.204 = (f32[416,768]{1,0:T(8,128)}, bf16[4,2,2,192,384]{4,3,2,1,0:T(8,128)(2,1)}, bf16[4,2,2,192,384]{4,3,2,1,0:T(8,128)(2,1)}, f32[2,768]{1,0:T(2,128)}) custom-call(s32[3]{0:T(128)} %pad_add_fusion.me_ref, f32[416,768]{1,0:T(8,128)} %get-tuple-element.130.g_ref, f32[416,768]{1,0:T(8,128)} %get-tuple-element.128.x1_ref, ...), custom_call_target="tpu_custom_call" | custom-call | flops 3925868544 | bytes 51260940 | tf_op jit(solution)/shard_map/pallas_call | solution.py:179
  408.9 7.6 shard_map.206
  420.7 13.5 %collective-permute-done.1.refs_2_ = bf16[8,192,384]{2,1,0:T(8,128)(2,1)S(1)} collective-permute-done((bf16[8,192,384]{2,1,0:T(8,128)(2,1)}, bf16[8,192,384]{2,1,0:T(8,128)(2,1)S(1)}, u32[]{:S(2)}, u32[]{:S(2)}) %collective-permute-start.1) | collective-permute-done | bytes 1179680 | tf_op jit(solution)/shard_map/ppermute | solution.py:880
  443.5 18.2 %shard_map.208 = (bf16[416,768]{1,0:T(8,128)(2,1)}, bf16[3,2,2,192,384]{4,3,2,1,0:T(8,128)(2,1)}, bf16[3,2,2,192,384]{4,3,2,1,0:T(8,128)(2,1)}) custom-call(s32[3]{0:T(128)} %pad_add_fusion.me_ref, bf16[416,768]{1,0:T(8,128)(2,1)} %bitcast.62.do_ref, bf16[416,768]{1,0:T(8,128)(2,1)} %bitcast.249, bf16[3,416,768]{2,1,0:T(8,128)(2,1)} %get-tuple-element.149.qkv_ref, ...), custom_call_target="tpu_custom_call" | custom-call | flops 2944401408 | bytes 27446796 | tf_op jit(solution)/shard_map/pallas_call | solution.py:179
  475.3 6.5 shard_map.209
  481.8 7.2 all-to-all-done.6
  493.0 22.4 %shard_map.211 = (f32[416,768]{1,0:T(8,128)}, bf16[2,4,2,2,192,384]{5,4,3,2,1,0:T(8,128)(2,1)}, bf16[2,4,2,2,192,384]{5,4,3,2,1,0:T(8,128)(2,1)}, f32[2,768]{1,0:T(2,128)}) custom-call(s32[3]{0:T(128)} %pad_add_fusion.me_ref, f32[416,768]{1,0:T(8,128)} %get-tuple-element.165.g_ref, f32[416,768]{1,0:T(8,128)} %get-tuple-element.123.x2_ref, ...), custom_call_target="tpu_custom_call" | custom-call | flops 9814671360 | bytes 53403660 | tf_op jit(solution)/shard_map/pallas_call | solution.py:179
  518.0 21.4 %collective-permute-done.8.refs_3_.refs_12_ = bf16[6,192,384]{2,1,0:T(8,128)(2,1)S(1)} collective-permute-done((bf16[6,192,384]{2,1,0:T(8,128)(2,1)}, bf16[6,192,384]{2,1,0:T(8,128)(2,1)S(1)}, u32[]{:S(2)}, u32[]{:S(2)}) %collective-permute-start.8) | collective-permute-done | bytes 884768 | tf_op jit(solution)/shard_map/ppermute | solution.py:880
  549.2 21.6 %shard_map.213 = (f32[416,768]{1,0:T(8,128)}, bf16[4,2,2,192,384]{4,3,2,1,0:T(8,128)(2,1)}, bf16[4,2,2,192,384]{4,3,2,1,0:T(8,128)(2,1)}, f32[2,768]{1,0:T(2,128)}) custom-call(s32[3]{0:T(128)} %pad_add_fusion.me_ref, f32[416,768]{1,0:T(8,128)} %get-tuple-element.175.g_ref, f32[416,768]{1,0:T(8,128)} %get-tuple-element.122.x1_ref, ...), custom_call_target="tpu_custom_call" | custom-call | flops 3925868544 | bytes 51260940 | tf_op jit(solution)/shard_map/pallas_call | solution.py:179
  577.7 7.6 shard_map.215
  588.9 17.0 %all-to-all-done.7 = bf16[4,104,768]{2,1,0:T(8,128)(2,1)S(1)} async-done(((bf16[4,104,768]{2,1,0:T(8,128)(2,1)}), bf16[4,104,768]{2,1,0:T(8,128)(2,1)S(1)}, u32[]{:S(2)}, u32[]{:S(2)}) %all-to-all-start.7) | async-done | bytes 639008 | tf_op jit(solution)/shard_map/all_to_all | solution.py:714
  614.5 29.4 %collective-permute-done.15.refs_13_ = bf16[2,192,384]{2,1,0:T(8,128)(2,1)S(1)} collective-permute-done((bf16[2,192,384]{2,1,0:T(8,128)(2,1)}, bf16[2,192,384]{2,1,0:T(8,128)(2,1)S(1)}, u32[]{:S(2)}, u32[]{:S(2)}) %collective-permute-start.15) | collective-permute-done | bytes 294944 | tf_op jit(solution)/shard_map/ppermute | solution.py:880
  662.8 18.2 %shard_map.217 = (bf16[416,768]{1,0:T(8,128)(2,1)}, bf16[3,2,2,192,384]{4,3,2,1,0:T(8,128)(2,1)}, bf16[3,2,2,192,384]{4,3,2,1,0:T(8,128)(2,1)}) custom-call(s32[3]{0:T(128)} %pad_add_fusion.me_ref, bf16[416,768]{1,0:T(8,128)(2,1)} %bitcast.256, bf16[416,768]{1,0:T(8,128)(2,1)} %bitcast.247, bf16[3,416,768]{2,1,0:T(8,128)(2,1)} %get-tuple-element.197.qkv_ref, ...), custom_call_target="tpu_custom_call" | custom-call | flops 2944401408 | bytes 27446796 | tf_op jit(solution)/shard_map/pallas_call | solution.py:179
  688.4 13.3 %all-to-all-done.8 = bf16[4,104,768]{2,1,0:T(8,128)(2,1)} async-done(((bf16[4,104,768]{2,1,0:T(8,128)(2,1)}), bf16[4,104,768]{2,1,0:T(8,128)(2,1)}, u32[]{:S(2)}, u32[]{:S(2)}) %all-to-all-start.8) | async-done | bytes 639008 | tf_op jit(solution)/shard_map/all_to_all | solution.py:714
  721.8 12.0 %all_to_all.141 = f32[32,1,384]{2,1,0:T(1,128)} all-to-all(f32[32,1,384]{2,1,0:T(1,128)S(1)} %copy.127), channel_id=1, replica_groups=mesh['clip'=4,'seq'=4,'head'=2] {'clip','seq','head'}, dimensions={0} | all-to-all | bytes 98304 | tf_op jit(solution)/shard_map/all_to_all | solution.py:964
  738.2 12.0 %shard_map.202 = f32[416,768]{1,0:T(8,128)} custom-call(f32[416,768]{1,0:T(8,128)} %get-tuple-element.129.x2_ref, bf16[17,2,768,384]{3,2,1,0:T(8,128)(2,1)} %bitcast.222, bf16[17,2,768,384]{3,2,1,0:T(8,128)(2,1)} %bitcast.223, f32[6,768]{1,0:T(8,128)} %squeeze.60.rest_0_.gb_ref), custom_call_target="tpu_custom_call" | custom-call | flops 3925868544 | bytes 42682368 | tf_op jit(solution)/shard_map/pallas_call | solution.py:179
  759.5 15.2 %collective-permute-done.21.refs_3_.refs_6_ = bf16[6,192,384]{2,1,0:T(8,128)(2,1)S(1)} collective-permute-done((bf16[6,192,384]{2,1,0:T(8,128)(2,1)}, bf16[6,192,384]{2,1,0:T(8,128)(2,1)S(1)}, u32[]{:S(2)}, u32[]{:S(2)}) %collective-permute-start.21) | collective-permute-done | bytes 884768 | tf_op jit(solution)/shard_map/ppermute | solution.py:880
  810.9 12.5 %all-to-all-done.9 = bf16[4,5,48,384]{3,2,1,0:T(8,128)(2,1)S(1)} async-done(((bf16[4,5,48,384]{3,2,1,0:T(8,128)(2,1)}), bf16[4,5,48,384]{3,2,1,0:T(8,128)(2,1)S(1)}, u32[]{:S(2)}, u32[]{:S(2)}) %all-to-all-start.9) | async-done | bytes 737312 | tf_op jit(solution)/shard_map/all_to_all | solution.py:905
  (273 shorter events, 210.7 us)
Async XLA Ops:
  7.2 141.4 %all-gather.3.cloned.1.call-start = ((), (), s32[]{:S(2)}) async-start(), calls=%async_computation.16 | async-start | bytes 20680704 | tf_op jit(solution)/shard_map/all_gather | solution.py:741
  10.5 290.2 %all-gather.5.cloned.1.call-start = ((), (), s32[]{:S(2)}) async-start(), calls=%async_computation.17 | async-start | bytes 20680704 | tf_op jit(solution)/shard_map/all_gather | solution.py:741
  160.6 29.2 %all-to-all-start.2 = ((bf16[4,104,768]{2,1,0:T(8,128)(2,1)}), bf16[4,104,768]{2,1,0:T(8,128)(2,1)S(1)}, u32[]{:S(2)}, u32[]{:S(2)}) async-start(bf16[4,104,768]{2,1,0:T(8,128)(2,1)} %bitcast.270), calls=%async_computation.2 | async-start | bytes 1277952 | tf_op jit(solution)/shard_map/all_to_all | solution.py:714
  223.0 77.7 %all-to-all-start.3 = ((bf16[4,104,768]{2,1,0:T(8,128)(2,1)}), bf16[4,104,768]{2,1,0:T(8,128)(2,1)S(1)}, u32[]{:S(2)}, u32[]{:S(2)}) async-start(bf16[4,104,768]{2,1,0:T(8,128)(2,1)} %bitcast.272), calls=%async_computation.3 | async-start | bytes 1277952 | tf_op jit(solution)/shard_map/all_to_all | solution.py:714
  313.5 21.4 %all-to-all-start.4 = ((bf16[4,104,768]{2,1,0:T(8,128)(2,1)}), bf16[4,104,768]{2,1,0:T(8,128)(2,1)S(1)}, u32[]{:S(2)}, u32[]{:S(2)}) async-start(bf16[4,104,768]{2,1,0:T(8,128)(2,1)} %bitcast.267), calls=%async_computation.4 | async-start | bytes 1277952 | tf_op jit(solution)/shard_map/all_to_all | solution.py:714
  376.8 22.4 %collective-permute-start = (bf16[8,2,2,192,384]{4,3,2,1,0:T(8,128)(2,1)}, bf16[8,2,2,192,384]{4,3,2,1,0:T(8,128)(2,1)S(1)}, u32[]{:S(2)}, u32[]{:S(2)}) collective-permute-start(bf16[8,2,2,192,384]{4,3,2,1,0:T(8,128)(2,1)} %bitcast.289), channel_id=1, source_target_pairs={{0,8},{8,0},{16,24},{24,16},{1,9},{9,1},{17,25},{25,17},{2,10},{10... | collective-permute-start | bytes 14155784 | tf_op jit(solution)/shard_map/ppermute | solution.py:880
  398.7 22.1 %collective-permute-start.3 = (bf16[4,2,2,192,384]{4,3,2,1,0:T(8,128)(2,1)}, bf16[4,2,2,192,384]{4,3,2,1,0:T(8,128)(2,1)S(1)}, u32[]{:S(2)}, u32[]{:S(2)}) collective-permute-start(bf16[4,2,2,192,384]{4,3,2,1,0:T(8,128)(2,1)} %get-tuple-element.145), channel_id=1, source_target_pairs={{0,8},{8,0},{16,24},{24,16},{1,9},{9,1},{17,25},{25,17},{2,10},{10... | collective-permute-start | bytes 7077896 | tf_op jit(solution)/shard_map/ppermute | solution.py:880
  406.1 28.2 %collective-permute-start.1 = (bf16[8,192,384]{2,1,0:T(8,128)(2,1)}, bf16[8,192,384]{2,1,0:T(8,128)(2,1)S(1)}, u32[]{:S(2)}, u32[]{:S(2)}) collective-permute-start(bf16[8,192,384]{2,1,0:T(8,128)(2,1)} %get-tuple-element.142), channel_id=1, source_target_pairs={{0,16},{8,24},{16,0},{24,8},{1,17},{9,25},{17,1},{25,9},{2,18},{10... | collective-permute-start | bytes 3538952 | tf_op jit(solution)/shard_map/ppermute | solution.py:880
  407.6 27.9 %collective-permute-start.2 = (bf16[8,192,384]{2,1,0:T(8,128)(2,1)}, bf16[8,192,384]{2,1,0:T(8,128)(2,1)}, u32[]{:S(2)}, u32[]{:S(2)}) collective-permute-start(bf16[8,192,384]{2,1,0:T(8,128)(2,1)} %get-tuple-element.143), channel_id=1, source_target_pairs={{0,1},{1,0},{2,3},{3,2},{4,5},{5,4},{6,7},{7,6},{8,9},{9,8},{10,11... | collective-permute-start | bytes 3538952 | tf_op jit(solution)/shard_map/ppermute | solution.py:880
  416.5 24.0 %all-to-all-start.5 = ((bf16[4,104,768]{2,1,0:T(8,128)(2,1)}), bf16[4,104,768]{2,1,0:T(8,128)(2,1)}, u32[]{:S(2)}, u32[]{:S(2)}) async-start(bf16[4,104,768]{2,1,0:T(8,128)(2,1)} %bitcast.269), calls=%async_computation.5 | async-start | bytes 1277952 | tf_op jit(solution)/shard_map/all_to_all | solution.py:714
  440.5 27.3 %collective-permute-start.4 = (bf16[8,192,384]{2,1,0:T(8,128)(2,1)}, bf16[8,192,384]{2,1,0:T(8,128)(2,1)}, u32[]{:S(2)}, u32[]{:S(2)}) collective-permute-start(bf16[8,192,384]{2,1,0:T(8,128)(2,1)} %get-tuple-element.152), channel_id=1, source_target_pairs={{0,1},{1,0},{2,3},{3,2},{4,5},{5,4},{6,7},{7,6},{8,9},{9,8},{10,11... | collective-permute-start | bytes 3538952 | tf_op jit(solution)/shard_map/ppermute | solution.py:880
  441.9 27.0 %collective-permute-start.5 = (bf16[8,192,384]{2,1,0:T(8,128)(2,1)}, bf16[8,192,384]{2,1,0:T(8,128)(2,1)}, u32[]{:S(2)}, u32[]{:S(2)}) collective-permute-start(bf16[8,192,384]{2,1,0:T(8,128)(2,1)} %get-tuple-element.153), channel_id=1, source_target_pairs={{0,16},{8,24},{16,0},{24,8},{1,17},{9,25},{17,1},{25,9},{2,18},{10... | collective-permute-start | bytes 3538952 | tf_op jit(solution)/shard_map/ppermute | solution.py:880
  515.4 55.4 %collective-permute-start.10 = (bf16[8,2,2,192,384]{4,3,2,1,0:T(8,128)(2,1)}, bf16[8,2,2,192,384]{4,3,2,1,0:T(8,128)(2,1)S(1)}, u32[]{:S(2)}, u32[]{:S(2)}) collective-permute-start(bf16[8,2,2,192,384]{4,3,2,1,0:T(8,128)(2,1)} %bitcast.288), channel_id=1, source_target_pairs={{0,8},{8,0},{16,24},{24,16},{1,9},{9,1},{17,25},{25,17},{2,10},{10... | collective-permute-start | bytes 14155784 | tf_op jit(solution)/shard_map/ppermute | solution.py:880
  515.5 28.5 %collective-permute-start.9 = (bf16[8,192,384]{2,1,0:T(8,128)(2,1)S(1)}, bf16[8,192,384]{2,1,0:T(8,128)(2,1)S(1)}, u32[]{:S(2)}, u32[]{:S(2)}) collective-permute-start(bf16[8,192,384]{2,1,0:T(8,128)(2,1)S(1)} %copy-done.47), channel_id=1, source_target_pairs={{0,16},{8,24},{16,0},{24,8},{1,17},{9,25},{17,1},{25,9},{2,18},{10... | collective-permute-start | bytes 3538952 | tf_op jit(solution)/shard_map/ppermute | solution.py:880
  517.4 21.9 %collective-permute-start.8 = (bf16[6,192,384]{2,1,0:T(8,128)(2,1)}, bf16[6,192,384]{2,1,0:T(8,128)(2,1)S(1)}, u32[]{:S(2)}, u32[]{:S(2)}) collective-permute-start(bf16[6,192,384]{2,1,0:T(8,128)(2,1)} %get-tuple-element.167), channel_id=1, source_target_pairs={{0,1},{1,0},{2,3},{3,2},{4,5},{5,4},{6,7},{7,6},{8,9},{9,8},{10,11... | collective-permute-start | bytes 2654216 | tf_op jit(solution)/shard_map/ppermute | solution.py:880
  585.3 20.6 %all-to-all-start.7 = ((bf16[4,104,768]{2,1,0:T(8,128)(2,1)}), bf16[4,104,768]{2,1,0:T(8,128)(2,1)S(1)}, u32[]{:S(2)}, u32[]{:S(2)}) async-start(bf16[4,104,768]{2,1,0:T(8,128)(2,1)} %bitcast.271), calls=%async_computation.7 | async-start | bytes 1277952 | tf_op jit(solution)/shard_map/all_to_all | solution.py:714
  588.8 59.6 %collective-permute-start.13 = (bf16[4,2,2,192,384]{4,3,2,1,0:T(8,128)(2,1)}, bf16[4,2,2,192,384]{4,3,2,1,0:T(8,128)(2,1)S(1)}, u32[]{:S(2)}, u32[]{:S(2)}) collective-permute-start(bf16[4,2,2,192,384]{4,3,2,1,0:T(8,128)(2,1)} %get-tuple-element.190), channel_id=1, source_target_pairs={{0,8},{8,0},{16,24},{24,16},{1,9},{9,1},{17,25},{25,17},{2,10},{10... | collective-permute-start | bytes 7077896 | tf_op jit(solution)/shard_map/ppermute | solution.py:880
  606.8 51.3 %all-to-all-start.14 = ((bf16[4,8,48,384]{3,2,1,0:T(8,128)(2,1)}), bf16[4,8,48,384]{3,2,1,0:T(8,128)(2,1)S(1)}, u32[]{:S(2)}, u32[]{:S(2)}) async-start(bf16[4,8,48,384]{3,2,1,0:T(8,128)(2,1)} %get-tuple-element.222), calls=%async_computation.14 | async-start | bytes 2359296 | tf_op jit(solution)/shard_map/all_to_all | solution.py:905
  610.3 38.1 %collective-permute-start.11 = (bf16[8,192,384]{2,1,0:T(8,128)(2,1)}, bf16[8,192,384]{2,1,0:T(8,128)(2,1)S(1)}, u32[]{:S(2)}, u32[]{:S(2)}) collective-permute-start(bf16[8,192,384]{2,1,0:T(8,128)(2,1)} %get-tuple-element.187), channel_id=1, source_target_pairs={{0,16},{8,24},{16,0},{24,8},{1,17},{9,25},{17,1},{25,9},{2,18},{10... | collective-permute-start | bytes 3538952 | tf_op jit(solution)/shard_map/ppermute | solution.py:880
  612.0 36.4 %collective-permute-start.12 = (bf16[8,192,384]{2,1,0:T(8,128)(2,1)}, bf16[8,192,384]{2,1,0:T(8,128)(2,1)S(1)}, u32[]{:S(2)}, u32[]{:S(2)}) collective-permute-start(bf16[8,192,384]{2,1,0:T(8,128)(2,1)} %get-tuple-element.188), channel_id=1, source_target_pairs={{0,1},{1,0},{2,3},{3,2},{4,5},{5,4},{6,7},{7,6},{8,9},{9,8},{10,11... | collective-permute-start | bytes 3538952 | tf_op jit(solution)/shard_map/ppermute | solution.py:880
  612.6 35.8 %collective-permute-start.14 = (bf16[3,192,384]{2,1,0:T(8,128)(2,1)}, bf16[3,192,384]{2,1,0:T(8,128)(2,1)S(1)}, u32[]{:S(2)}, u32[]{:S(2)}) collective-permute-start(bf16[3,192,384]{2,1,0:T(8,128)(2,1)} %get-tuple-element.191), channel_id=1, source_target_pairs={{0,1},{1,0},{2,3},{3,2},{4,5},{5,4},{6,7},{7,6},{8,9},{9,8},{10,11... | collective-permute-start | bytes 1327112 | tf_op jit(solution)/shard_map/ppermute | solution.py:880
  614.1 29.8 %collective-permute-start.15 = (bf16[2,192,384]{2,1,0:T(8,128)(2,1)}, bf16[2,192,384]{2,1,0:T(8,128)(2,1)S(1)}, u32[]{:S(2)}, u32[]{:S(2)}) collective-permute-start(bf16[2,192,384]{2,1,0:T(8,128)(2,1)} %get-tuple-element.192), channel_id=1, source_target_pairs={{0,16},{8,24},{16,0},{24,8},{1,17},{9,25},{17,1},{25,9},{2,18},{10... | collective-permute-start | bytes 884744 | tf_op jit(solution)/shard_map/ppermute | solution.py:880
  656.9 26.0 %collective-permute-start.16 = (bf16[8,192,384]{2,1,0:T(8,128)(2,1)}, bf16[8,192,384]{2,1,0:T(8,128)(2,1)S(1)}, u32[]{:S(2)}, u32[]{:S(2)}) collective-permute-start(bf16[8,192,384]{2,1,0:T(8,128)(2,1)} %get-tuple-element.200), channel_id=1, source_target_pairs={{0,1},{1,0},{2,3},{3,2},{4,5},{5,4},{6,7},{7,6},{8,9},{9,8},{10,11... | collective-permute-start | bytes 3538952 | tf_op jit(solution)/shard_map/ppermute | solution.py:880
  657.6 25.7 %collective-permute-start.17 = (bf16[8,192,384]{2,1,0:T(8,128)(2,1)}, bf16[8,192,384]{2,1,0:T(8,128)(2,1)S(1)}, u32[]{:S(2)}, u32[]{:S(2)}) collective-permute-start(bf16[8,192,384]{2,1,0:T(8,128)(2,1)} %get-tuple-element.201), channel_id=1, source_target_pairs={{0,16},{8,24},{16,0},{24,8},{1,17},{9,25},{17,1},{25,9},{2,18},{10... | collective-permute-start | bytes 3538952 | tf_op jit(solution)/shard_map/ppermute | solution.py:880
  658.1 25.2 %all-to-all-start.12 = ((bf16[4,4,48,384]{3,2,1,0:T(8,128)(2,1)}), bf16[4,4,48,384]{3,2,1,0:T(8,128)(2,1)}, u32[]{:S(2)}, u32[]{:S(2)}) async-start(bf16[4,4,48,384]{3,2,1,0:T(8,128)(2,1)} %get-tuple-element.220), calls=%async_computation.12 | async-start | bytes 1179648 | tf_op jit(solution)/shard_map/all_to_all | solution.py:905
  687.8 20.4 %collective-permute-start.19 = (bf16[3,2,2,192,384]{4,3,2,1,0:T(8,128)(2,1)}, bf16[3,2,2,192,384]{4,3,2,1,0:T(8,128)(2,1)S(1)}, u32[]{:S(2)}, u32[]{:S(2)}) collective-permute-start(bf16[3,2,2,192,384]{4,3,2,1,0:T(8,128)(2,1)} %get-tuple-element.208), channel_id=1, source_target_pairs={{0,8},{8,0},{16,24},{24,16},{1,9},{9,1},{17,25},{25,17},{2,10},{10... | collective-permute-start | bytes 5308424 | tf_op jit(solution)/shard_map/ppermute | solution.py:880
  687.9 20.4 %collective-permute-start.18 = (bf16[2,2,2,192,384]{4,3,2,1,0:T(8,128)(2,1)}, bf16[2,2,2,192,384]{4,3,2,1,0:T(8,128)(2,1)S(1)}, u32[]{:S(2)}, u32[]{:S(2)}) collective-permute-start(bf16[2,2,2,192,384]{4,3,2,1,0:T(8,128)(2,1)} %get-tuple-element.206), channel_id=1, source_target_pairs={{0,8},{8,0},{16,24},{24,16},{1,9},{9,1},{17,25},{25,17},{2,10},{10... | collective-permute-start | bytes 3538952 | tf_op jit(solution)/shard_map/ppermute | solution.py:880
  733.7 47.1 %all-to-all-start.13 = ((bf16[4,8,48,384]{3,2,1,0:T(8,128)(2,1)}), bf16[4,8,48,384]{3,2,1,0:T(8,128)(2,1)S(1)}, u32[]{:S(2)}, u32[]{:S(2)}) async-start(bf16[4,8,48,384]{3,2,1,0:T(8,128)(2,1)} %get-tuple-element.221), calls=%async_computation.13 | async-start | bytes 2359296 | tf_op jit(solution)/shard_map/all_to_all | solution.py:905
  737.5 37.2 %collective-permute-start.20 = (bf16[8,192,384]{2,1,0:T(8,128)(2,1)}, bf16[8,192,384]{2,1,0:T(8,128)(2,1)S(1)}, u32[]{:S(2)}, u32[]{:S(2)}) collective-permute-start(bf16[8,192,384]{2,1,0:T(8,128)(2,1)} %get-tuple-element.214), channel_id=1, source_target_pairs={{0,16},{8,24},{16,0},{24,8},{1,17},{9,25},{17,1},{25,9},{2,18},{10... | collective-permute-start | bytes 3538952 | tf_op jit(solution)/shard_map/ppermute | solution.py:880
  753.1 21.6 %collective-permute-start.21 = (bf16[6,192,384]{2,1,0:T(8,128)(2,1)}, bf16[6,192,384]{2,1,0:T(8,128)(2,1)S(1)}, u32[]{:S(2)}, u32[]{:S(2)}) collective-permute-start(bf16[6,192,384]{2,1,0:T(8,128)(2,1)} %get-tuple-element.215), channel_id=1, source_target_pairs={{0,1},{1,0},{2,3},{3,2},{4,5},{5,4},{6,7},{7,6},{8,9},{9,8},{10,11... | collective-permute-start | bytes 2654216 | tf_op jit(solution)/shard_map/ppermute | solution.py:880
  780.8 21.5 %all-to-all-start.11 = ((bf16[4,4,48,384]{3,2,1,0:T(8,128)(2,1)}), bf16[4,4,48,384]{3,2,1,0:T(8,128)(2,1)S(1)}, u32[]{:S(2)}, u32[]{:S(2)}) async-start(bf16[4,4,48,384]{3,2,1,0:T(8,128)(2,1)} %get-tuple-element.219), calls=%async_computation.11 | async-start | bytes 1179648 | tf_op jit(solution)/shard_map/all_to_all | solution.py:905
  802.3 21.1 %all-to-all-start.9 = ((bf16[4,5,48,384]{3,2,1,0:T(8,128)(2,1)}), bf16[4,5,48,384]{3,2,1,0:T(8,128)(2,1)S(1)}, u32[]{:S(2)}, u32[]{:S(2)}) async-start(bf16[4,5,48,384]{3,2,1,0:T(8,128)(2,1)} %shard_map.221), calls=%async_computation.9 | async-start | bytes 1474560 | tf_op jit(solution)/shard_map/all_to_all | solution.py:905
  (56 other events, 329.1 us)
Sparse Core Ops, SparseCore 0:
  11.1 137.4 all-gather.2
  151.7 148.9 all-gather.4

commit v6 on v5

--- a/solution.py
+++ b/solution.py
@@ -405,7 +405,7 @@
     per_share = (w.shape[0] - 9) // 2
     steps = shares * per_share
 
-    def body(me_ref, g_ref, x2_ref, wi_ref, wo_ref, gb_ref, go_ref, keep_ref, send_ref, sums_ref, a3_ref, a3t_ref, e3_ref, e3t_ref, u_ref, room_ref):
+    def body(me_ref, g_ref, x2_ref, wi_ref, wo_ref, gb_ref, go_ref, ki_ref, si_ref, ko_ref, so_ref, sums_ref, a3_ref, a3t_ref, e3_ref, e3t_ref, u_ref, room_ref):
         j = pl.program_id(0)
 
         @pl.when(j == 0)
@@ -424,8 +424,8 @@
         act = (hid * phi).astype(BF16)
         slope = phi + hid * jnp.exp(-0.5 * hid * hid) * INV_ROOT_TAU
         dhid = (nn(e3_ref[...], wo_ref[0, 0]) * slope).astype(BF16)
-        split_rows(nn(e3t_ref[...], act), keep_ref, send_ref, (1, 0, 0), room_ref, me_ref)
-        split_rows(nn(a3t_ref[...], dhid), keep_ref, send_ref, (0, 0, 0), room_ref, me_ref)
+        split_rows(nn(e3t_ref[...], act), ko_ref, so_ref, (0, 0), room_ref, me_ref)
+        split_rows(nn(a3t_ref[...], dhid), ki_ref, si_ref, (0, 0), room_ref, me_ref)
         u_ref[...] += nt(dhid, wi_ref[0, 0])
 
         @pl.when(j == steps - 1)
@@ -434,10 +434,14 @@
             go_ref[...] = g_ref[...] + change
             sums_ref[...] = sums
 
-    slab_outs = halves.array(
-        (2, per_share, shares), (2, 1, 1), lambda j: (0, j % per_share, j // per_share)
-    )
-    grad, keep, send, sums = call(
+    slab_outs = [
+        one
+        for _ in range(2)
+        for one in halves.array(
+            (per_share, shares), (1, 1), lambda j: (j % per_share, j // per_share)
+        )
+    ]
+    grad, ki, si, ko, so, sums = call(
         body,
         (steps,),
         [
@@ -460,8 +464,7 @@
         (me, grad, x2, w, w, gb),
         flops=10 * t * d * width * steps,
     )
-    flat = (2 * per_share,) + keep.shape[2:]
-    return grad, (keep.reshape(flat), send.reshape(flat)), sums
+    return grad, [(ki, si), (ko, so)], sums
 
 
 def space_backward(rows, grad, x1, qkv, o2, logs, w, gb, me, halves):
@@ -769,7 +772,7 @@
 PLACE = {"x": 1, "h": 2}
 
 
-def fold(pieces, me):
+def fold(pieces, me, last_by_rows):
     ways = lax.axis_size("seq")
     depth, width = pieces[0].near[0].shape[-2:]
     r = depth // ways
@@ -794,7 +797,8 @@
         plans.append((p, link, base, near, held))
     links = sorted(used)
     shapes = [
-        (ways, used[k], r, width) if k == "z" else (used[k], depth, width) for k in links
+        (ways, used[k], r, width) if k == "z" and last_by_rows else (used[k], depth, width)
+        for k in links
     ]
     rooms, counts = [], []
     for p, link, base, near, held in plans:
@@ -849,7 +853,7 @@
                 copy.wait()
 
             @pl.loop(0, each * p.n)
-            def _(i, these=these, base=base, out=outs[link], last=p.step == 2):
+            def _(i, these=these, base=base, out=outs[link], last=p.step == 2 and last_by_rows):
                 value = these[0][i].astype(F32)
                 for one in these[1:]:
                     value = value + one[i].astype(F32)
@@ -864,7 +868,7 @@
     sums = pl.pallas_call(
         body,
         out_shape=[jax.ShapeDtypeStruct(shape, BF16) for shape in shapes],
-        in_specs=[SCALARS] + [pl.BlockSpec(memory_space=pl.ANY)] * len(arrays),
+        in_specs=[SCALARS] + [pl.BlockSpec(memory_space=pltpu.HBM)] * len(arrays),
         out_specs=[pl.BlockSpec(memory_space=pltpu.VMEM)] * len(links),
         scratch_shapes=[pltpu.VMEM(room, BF16) for room in rooms]
         + [pltpu.SemaphoreType.DMA((copies_needed,))],
@@ -896,14 +900,18 @@
     return found
 
 
-def move(x, pieces, me):
-    plans, sums = fold(pieces, me)
+def move(x, pieces, me, at_end=False):
+    plans, sums = fold(pieces, me, at_end)
     x, sums = lax.optimization_barrier((x, sums))
     got = {}
     for link, array in sums.items():
         if link == "z":
-            every = lax.all_to_all(array, "seq", split_axis=0, concat_axis=0, tiled=True)
-            got[link] = jnp.sum(every.astype(F32), axis=0)
+            if at_end:
+                every = lax.all_to_all(array, "seq", split_axis=0, concat_axis=0, tiled=True)
+                got[link] = jnp.sum(every.astype(F32), axis=0)
+            else:
+                own = lax.psum_scatter(array, "seq", scatter_dimension=1, tiled=True)
+                got[link] = own.astype(F32)
         else:
             got[link] = cross(array, link)
     for p, link, base in plans:
@@ -1036,7 +1044,7 @@
         x, a1, qkv1, log1, o1, y1, x1, qkv2, o2, log2, x2 = kept[l]
         grad, g_ff, s3 = mlp_backward(rows, grad, x2, w, gb[l], me, halves)
         if quick:
-            ff = pieces_of([g_ff])
+            ff = pieces_of(g_ff)
             if late:
                 grad = settle(grad, late)
                 grad = move(grad, late, me)
@@ -1062,12 +1070,12 @@
         if quick:
             summed[l] = ff + space + rest
         else:
-            summed[l] = [reduce_plain([g_ff, g_space, g_out, g_time], clip & 1)]
+            summed[l] = [reduce_plain(g_ff + [g_space, g_out, g_time], clip & 1)]
     if quick:
-        move((), late, me)
-        move((), rest, me)
+        move((), late, me, True)
+        move((), rest, me, True)
         summed = [[p.result for p in some] for some in summed]
-    cuts = (g_ff[0].shape[0], g_space[0].shape[0], g_out[0].shape[0], g_time[0].shape[0])
+    cuts = (2 * g_ff[0][0].shape[0], g_space[0].shape[0], g_out[0].shape[0], g_time[0].shape[0])
     results = []
     for some in summed:
         slabs_of = jnp.concatenate(some, axis=0)

time: 838 us -> 745 us (0.89)
  waiting for transfers between devices: 359 us -> 293 us
  blocking collectives: 38.7 us -> 26.7 us
  starting transfers between devices: 80.6 us -> 69.9 us
    ppermute x24 -> x26, waiting for transfers between devices: 104 us -> 70.6 us  [cross(): return lax.ppermute(a, axis, [(i, i ^ 1 << bit) for i in range(size)])]
    all_to_all x7, waiting for transfers between devices: 70.4 us -> 40.7 us  [swap_places(): lax.all_to_all(rows_array, 'seq', split_axis=0, concat_axis=0, tiled=True)]
    all_to_all x6 -> x2, starting transfers between devices: 26.1 us -> 9.66 us  [move(): lax.all_to_all(array, 'seq', split_axis=0, concat_axis=0, tiled=True)]
    all_to_all x1 -> x0, blocking collectives: 12 us -> none  [reduce_norms(): every = lax.all_to_all(a, ALL, split_axis=0, concat_axis=0, tiled=True)]
    unnamed x113 -> x105, local copies, waits for them, and re-layouts: 24.8 us -> 21.5 us
    ppermute x24 -> x26, starting transfers between devices: 19 us -> 18.8 us  [cross(): return lax.ppermute(a, axis, [(i, i ^ 1 << bit) for i in range(size)])]
  transfers between devices with their start and end apart: 40 -> 43, of which waited for: 23 -> 20; matrix products, arithmetic and copies ran while one was open for 4% -> 4% of each run, Pallas kernels for 23% -> 31%
where the time goes in v6:
time: 745 us; the launch traced here: 740 us
  waiting for transfers between devices  293 us (39%)
  Pallas kernels  284 us (38%)
  starting transfers between devices  69.9 us (9%)
  local copies, waits for them, and re-layouts  37 us (5%)
  blocking collectives  26.7 us (4%)
  between operations  15.4 us (2%)
  other arithmetic  14 us (2%)
    pallas_call x19, Pallas kernels, call(): pl.pallas_call(body, out_shape=[shape for shape, _ in outs], grid=grid, i...  238 us
    all_gather x2, waiting for transfers between devices, gather_slabs(): full = lax.all_gather(pack, ('head', 'clip', 'seq'), axis=1, tiled=True)  165 us
    ppermute x26, waiting for transfers between devices, cross(): return lax.ppermute(a, axis, [(i, i ^ 1 << bit) for i in range(size)])  70.6 us
    pallas_call x9, Pallas kernels, fold(): pl.pallas_call(body, out_shape=[jax.ShapeDtypeStruct(shape, BF16) for sha...  45.7 us
    all_to_all x7, waiting for transfers between devices, swap_places(): lax.all_to_all(rows_array, 'seq', split_axis=0, concat_axis=0, tiled=True)  40.7 us
    all_to_all x7, starting transfers between devices, swap_places(): lax.all_to_all(rows_array, 'seq', split_axis=0, concat_axis=0, tiled=True)  28.1 us
    all_to_all x1, blocking collectives, swap_places(): lax.all_to_all(rows_array, 'seq', split_axis=0, concat_axis=0, tiled=True)  26.7 us
    unnamed x105, local copies, waits for them, and re-layouts  21.5 us
  transfers between devices with their start and end apart: 43, of which 20 were waited for; matrix products, arithmetic and copies ran while one was open for 4% of the time, Pallas kernels for 31%

profile of v6, /device:TPU:0, one launch (start us, length us, event | category | flops | bytes accessed | tf_op | source)
XLA Modules:
  0.0 739.5 jit_solution(4995537612393205194)
XLA Ops:
  12.3 7.3 all-to-all-start
  30.9 26.7 %all_to_all.120 = bf16[4,104,768]{2,1,0:T(8,128)(2,1)} all-to-all(bf16[4,104,768]{2,1,0:T(8,128)(2,1)} %bitcast.244), channel_id=1, replica_groups=mesh['clip'=4,'seq'=4,'head'=2] {'seq'}, dimensions={0} | all-to-all | bytes 1277952 | tf_op jit(solution)/shard_map/all_to_all | solution.py:717
  57.6 91.0 %all-gather.3.cloned.1.call-done = bf16[17,1536,384]{2,1,0:T(8,128)(2,1)} async-done(((bf16[17,48,384]{2,1,0:T(8,128)(2,1)}), bf16[17,1536,384]{2,1,0:T(8,128)(2,1)}) %all-gather.3.cloned.1.call-update) | async-done | bytes 20054032 | tf_op jit(solution)/shard_map/all_gather | solution.py:744
  148.6 12.0 %shard_map.195 = (bf16[3,416,768]{2,1,0:T(8,128)(2,1)}, bf16[416,768]{1,0:T(8,128)(2,1)}, f32[2,3,2,416]{3,2,1,0:T(2,128)}) custom-call(bf16[416,768]{1,0:T(8,128)(2,1)} %bitcast.234, bf16[17,2,768,384]{3,2,1,0:T(8,128)(2,1)} %bitcast.218), custom_call_target="tpu_custom_call" | custom-call | flops 1472200704 | bytes 23268864 | tf_op jit(solution)/shard_map/pallas_call | solution.py:179
  168.8 21.0 %all-to-all-done.2 = bf16[4,104,768]{2,1,0:T(8,128)(2,1)S(1)} async-done(((bf16[4,104,768]{2,1,0:T(8,128)(2,1)}), bf16[4,104,768]{2,1,0:T(8,128)(2,1)S(1)}, u32[]{:S(2)}, u32[]{:S(2)}) %all-to-all-start.2) | async-done | bytes 639008 | tf_op jit(solution)/shard_map/all_to_all | solution.py:717
  190.6 9.3 %shard_map.196 = (bf16[416,768]{1,0:T(8,128)(2,1)}, bf16[416,768]{1,0:T(8,128)(2,1)}, f32[416,768]{1,0:T(8,128)}, bf16[3,416,768]{2,1,0:T(8,128)(2,1)}) custom-call(bf16[416,768]{1,0:T(8,128)(2,1)} %bitcast.243, f32[416,768]{1,0:T(8,128)} %bitcast_convert_fusion.1.x_ref, bf16[17,2,768,384]{3,2,1,0:T(8,128)(2,1)} %bitcast.219, ...), custom_call_target="tpu_custom_call" | custom-call | flops 2453667840 | bytes 47695872 | tf_op jit(solution)/shard_map/pallas_call | solution.py:179
  199.9 9.9 %shard_map.197 = (bf16[416,768]{1,0:T(8,128)(2,1)}, f32[416,768]{1,0:T(8,128)}, f32[2,3,2,2,208]{4,3,2,1,0:T(2,128)}) custom-call(bf16[3,416,768]{2,1,0:T(8,128)(2,1)} %get-tuple-element.125.qkv_ref, f32[416,768]{1,0:T(8,128)} %get-tuple-element.126.x1_ref, bf16[17,2,768,384]{3,2,1,0:T(8,128)(2,1)} %bitcast.221), custom_call_target="tpu_custom_call" | custom-call | flops 490733568 | bytes 25185792 | tf_op jit(solution)/shard_map/pallas_call | solution.py:179
  209.8 13.2 %shard_map.198 = (f32[416,768]{1,0:T(8,128)}, bf16[416,768]{1,0:T(8,128)(2,1)}) custom-call(f32[416,768]{1,0:T(8,128)} %get-tuple-element.127.x2_ref, bf16[17,2,768,384]{3,2,1,0:T(8,128)(2,1)} %bitcast.222, bf16[17,2,768,384]{3,2,1,0:T(8,128)(2,1)} %bitcast.223, f32[6,768]{1,0:T(8,128)} %squeeze.54.gb_ref, f32[6,768]{1,0:T(8,128)} %squeeze.60.rest_0_.gb_ref), custom_call_target="tpu_custom_call" | custom-call | flops 3925868544 | bytes 43339776 | tf_op jit(solution)/shard_map/pallas_call | solution.py:179
  226.5 74.3 %all-gather.5.cloned.1.call-done = bf16[17,1536,384]{2,1,0:T(8,128)(2,1)} async-done(((bf16[17,48,384]{2,1,0:T(8,128)(2,1)}), bf16[17,1536,384]{2,1,0:T(8,128)(2,1)}) %all-gather.5.cloned.1.call-update) | async-done | bytes 20054032 | tf_op jit(solution)/shard_map/all_gather | solution.py:744
  301.6 12.0 %shard_map.199 = (bf16[3,416,768]{2,1,0:T(8,128)(2,1)}, bf16[416,768]{1,0:T(8,128)(2,1)}, f32[2,3,2,416]{3,2,1,0:T(2,128)}) custom-call(bf16[416,768]{1,0:T(8,128)(2,1)} %bitcast.236, bf16[17,2,768,384]{3,2,1,0:T(8,128)(2,1)} %bitcast.206), custom_call_target="tpu_custom_call" | custom-call | flops 1472200704 | bytes 23268864 | tf_op jit(solution)/shard_map/pallas_call | solution.py:179
  323.3 12.0 %all-to-all-done.4 = bf16[4,104,768]{2,1,0:T(8,128)(2,1)S(1)} async-done(((bf16[4,104,768]{2,1,0:T(8,128)(2,1)}), bf16[4,104,768]{2,1,0:T(8,128)(2,1)S(1)}, u32[]{:S(2)}, u32[]{:S(2)}) %all-to-all-start.4) | async-done | bytes 639008 | tf_op jit(solution)/shard_map/all_to_all | solution.py:717
  336.2 8.8 %shard_map.200 = (bf16[416,768]{1,0:T(8,128)(2,1)}, bf16[416,768]{1,0:T(8,128)(2,1)}, f32[416,768]{1,0:T(8,128)}, bf16[3,416,768]{2,1,0:T(8,128)(2,1)}) custom-call(bf16[416,768]{1,0:T(8,128)(2,1)} %bitcast.242, f32[416,768]{1,0:T(8,128)} %get-tuple-element.130.x_ref, bf16[17,2,768,384]{3,2,1,0:T(8,128)(2,1)} %bitcast.207, ...), custom_call_target="tpu_custom_call" | custom-call | flops 2453667840 | bytes 47695872 | tf_op jit(solution)/shard_map/pallas_call | solution.py:179
  345.0 9.9 %shard_map.201 = (bf16[416,768]{1,0:T(8,128)(2,1)}, f32[416,768]{1,0:T(8,128)}, f32[2,3,2,2,208]{4,3,2,1,0:T(2,128)}) custom-call(bf16[3,416,768]{2,1,0:T(8,128)(2,1)} %get-tuple-element.131.qkv_ref, f32[416,768]{1,0:T(8,128)} %get-tuple-element.132.x1_ref, bf16[17,2,768,384]{3,2,1,0:T(8,128)(2,1)} %bitcast.209), custom_call_target="tpu_custom_call" | custom-call | flops 490733568 | bytes 25185792 | tf_op jit(solution)/shard_map/pallas_call | solution.py:179
  354.8 22.4 %shard_map.203 = (f32[416,768]{1,0:T(8,128)}, bf16[4,2,2,192,384]{4,3,2,1,0:T(8,128)(2,1)}, bf16[4,2,2,192,384]{4,3,2,1,0:T(8,128)(2,1)}, bf16[4,2,2,192,384]{4,...) custom-call(s32[3]{0:T(128)} %pad_add_fusion.me_ref, ...), custom_call_target="tpu_custom_call" | custom-call | flops 9814671360 | bytes 53403660 | tf_op jit(solution)/shard_map/pallas_call | solution.py:179
  377.8 21.8 %shard_map.204 = (f32[416,768]{1,0:T(8,128)}, bf16[4,2,2,192,384]{4,3,2,1,0:T(8,128)(2,1)}, bf16[4,2,2,192,384]{4,3,2,1,0:T(8,128)(2,1)}, f32[2,768]{1,0:T(2,128)}) custom-call(s32[3]{0:T(128)} %pad_add_fusion.me_ref, f32[416,768]{1,0:T(8,128)} %get-tuple-element.134.g_ref, f32[416,768]{1,0:T(8,128)} %get-tuple-element.132.x1_ref, ...), custom_call_target="tpu_custom_call" | custom-call | flops 3925868544 | bytes 51260940 | tf_op jit(solution)/shard_map/pallas_call | solution.py:179
  409.5 7.5 %shard_map.206 = (bf16[416,768]{1,0:T(8,128)(2,1)}, bf16[2,2,2,192,384]{4,3,2,1,0:T(8,128)(2,1)}, bf16[2,2,2,192,384]{4,3,2,1,0:T(8,128)(2,1)}) custom-call(s32[3]{0:T(128)} %pad_add_fusion.me_ref, f32[416,768]{1,0:T(8,128)} %get-tuple-element.144.g_ref, bf16[416,768]{1,0:T(8,128)(2,1)} %get-tuple-element.145.y1_ref, ...), custom_call_target="tpu_custom_call" | custom-call | flops 1962934272 | bytes 26787852 | tf_op jit(solution)/shard_map/pallas_call | solution.py:179
  421.3 13.9 %collective-permute-done.2.refs_2_ = bf16[8,192,384]{2,1,0:T(8,128)(2,1)S(1)} collective-permute-done((bf16[8,192,384]{2,1,0:T(8,128)(2,1)}, bf16[8,192,384]{2,1,0:T(8,128)(2,1)S(1)}, u32[]{:S(2)}, u32[]{:S(2)}) %collective-permute-start.2) | collective-permute-done | bytes 1179680 | tf_op jit(solution)/shard_map/ppermute | solution.py:884
  444.2 18.2 %shard_map.208 = (bf16[416,768]{1,0:T(8,128)(2,1)}, bf16[3,2,2,192,384]{4,3,2,1,0:T(8,128)(2,1)}, bf16[3,2,2,192,384]{4,3,2,1,0:T(8,128)(2,1)}) custom-call(s32[3]{0:T(128)} %pad_add_fusion.me_ref, bf16[416,768]{1,0:T(8,128)(2,1)} %bitcast.60.do_ref, bf16[416,768]{1,0:T(8,128)(2,1)} %bitcast.237, bf16[3,416,768]{2,1,0:T(8,128)(2,1)} %get-tuple-element.155.qkv_ref, ...), custom_call_target="tpu_custom_call" | custom-call | flops 2944401408 | bytes 27446796 | tf_op jit(solution)/shard_map/pallas_call | solution.py:179
  462.9 6.4 collective-permute-done.5.refs_3_.refs_4_
  476.4 6.4 shard_map.209
  482.7 7.8 %all-to-all-done.6 = bf16[4,104,768]{2,1,0:T(8,128)(2,1)} async-done(((bf16[4,104,768]{2,1,0:T(8,128)(2,1)}), bf16[4,104,768]{2,1,0:T(8,128)(2,1)}, u32[]{:S(2)}, u32[]{:S(2)}) %all-to-all-start.6) | async-done | bytes 639008 | tf_op jit(solution)/shard_map/all_to_all | solution.py:717
  496.8 22.3 %shard_map.211 = (f32[416,768]{1,0:T(8,128)}, bf16[4,2,2,192,384]{4,3,2,1,0:T(8,128)(2,1)}, bf16[4,2,2,192,384]{4,3,2,1,0:T(8,128)(2,1)}, bf16[4,2,2,192,384]{4,...) custom-call(s32[3]{0:T(128)} %pad_add_fusion.me_ref, f32[416,768]{1,0:T(8,128)} %get-tuple-element.171.g_ref, ...), custom_call_target="tpu_custom_call" | custom-call | flops 9814671360 | bytes 53403660 | tf_op jit(solution)/shard_map/pallas_call | solution.py:179
  527.2 21.7 %shard_map.213 = (f32[416,768]{1,0:T(8,128)}, bf16[4,2,2,192,384]{4,3,2,1,0:T(8,128)(2,1)}, bf16[4,2,2,192,384]{4,3,2,1,0:T(8,128)(2,1)}, f32[2,768]{1,0:T(2,128)}) custom-call(s32[3]{0:T(128)} %pad_add_fusion.me_ref, f32[416,768]{1,0:T(8,128)} %get-tuple-element.181.g_ref, f32[416,768]{1,0:T(8,128)} %get-tuple-element.126.x1_ref, ...), custom_call_target="tpu_custom_call" | custom-call | flops 3925868544 | bytes 51260940 | tf_op jit(solution)/shard_map/pallas_call | solution.py:179
  556.9 7.7 %shard_map.215 = (bf16[416,768]{1,0:T(8,128)(2,1)}, bf16[2,2,2,192,384]{4,3,2,1,0:T(8,128)(2,1)}, bf16[2,2,2,192,384]{4,3,2,1,0:T(8,128)(2,1)}) custom-call(s32[3]{0:T(128)} %pad_add_fusion.me_ref, f32[416,768]{1,0:T(8,128)} %get-tuple-element.191.g_ref, bf16[416,768]{1,0:T(8,128)(2,1)} %get-tuple-element.192.y1_ref, ...), custom_call_target="tpu_custom_call" | custom-call | flops 1962934272 | bytes 26787852 | tf_op jit(solution)/shard_map/pallas_call | solution.py:179
  570.0 18.8 %collective-permute-done.17.refs_15_ = bf16[2,192,384]{2,1,0:T(8,128)(2,1)S(1)} collective-permute-done((bf16[2,192,384]{2,1,0:T(8,128)(2,1)}, bf16[2,192,384]{2,1,0:T(8,128)(2,1)S(1)}, u32[]{:S(2)}, u32[]{:S(2)}) %collective-permute-start.17) | collective-permute-done | bytes 294944 | tf_op jit(solution)/shard_map/ppermute | solution.py:884
  595.1 6.2 shard_map.216
  603.3 18.2 %shard_map.217 = (bf16[416,768]{1,0:T(8,128)(2,1)}, bf16[3,2,2,192,384]{4,3,2,1,0:T(8,128)(2,1)}, bf16[3,2,2,192,384]{4,3,2,1,0:T(8,128)(2,1)}) custom-call(s32[3]{0:T(128)} %pad_add_fusion.me_ref, bf16[416,768]{1,0:T(8,128)(2,1)} %bitcast.64.do_ref, bf16[416,768]{1,0:T(8,128)(2,1)} %bitcast.235, bf16[3,416,768]{2,1,0:T(8,128)(2,1)} %get-tuple-element.205.qkv_ref, ...), custom_call_target="tpu_custom_call" | custom-call | flops 2944401408 | bytes 27446796 | tf_op jit(solution)/shard_map/pallas_call | solution.py:179
  622.0 7.1 collective-permute-done.18.refs_3_.refs_4_
  634.5 12.3 %shard_map.202 = f32[416,768]{1,0:T(8,128)} custom-call(f32[416,768]{1,0:T(8,128)} %get-tuple-element.133.x2_ref, bf16[17,2,768,384]{3,2,1,0:T(8,128)(2,1)} %bitcast.216, bf16[17,2,768,384]{3,2,1,0:T(8,128)(2,1)} %bitcast.217, f32[6,768]{1,0:T(8,128)} %squeeze.60.rest_0_.gb_ref), custom_call_target="tpu_custom_call" | custom-call | flops 3925868544 | bytes 42682368 | tf_op jit(solution)/shard_map/pallas_call | solution.py:179
  651.2 6.5 shard_map.218
  678.5 6.2 collective-permute-done.22.refs_5_.refs_2_
  720.1 10.0 %all-to-all-done.9 = bf16[4,5,48,384]{3,2,1,0:T(8,128)(2,1)S(1)} async-done(((bf16[4,5,48,384]{3,2,1,0:T(8,128)(2,1)}), bf16[4,5,48,384]{3,2,1,0:T(8,128)(2,1)S(1)}, u32[]{:S(2)}, u32[]{:S(2)}) %all-to-all-start.9) | async-done | bytes 737312 | tf_op jit(solution)/shard_map/all_to_all | solution.py:910
  (275 shorter events, 175.6 us)
Async XLA Ops:
  7.2 141.4 %all-gather.3.cloned.1.call-start = ((), (), s32[]{:S(2)}) async-start(), calls=%async_computation.16 | async-start | bytes 20680704 | tf_op jit(solution)/shard_map/all_gather | solution.py:744
  10.5 290.2 %all-gather.5.cloned.1.call-start = ((), (), s32[]{:S(2)}) async-start(), calls=%async_computation.17 | async-start | bytes 20680704 | tf_op jit(solution)/shard_map/all_gather | solution.py:744
  160.6 29.1 %all-to-all-start.2 = ((bf16[4,104,768]{2,1,0:T(8,128)(2,1)}), bf16[4,104,768]{2,1,0:T(8,128)(2,1)S(1)}, u32[]{:S(2)}, u32[]{:S(2)}) async-start(bf16[4,104,768]{2,1,0:T(8,128)(2,1)} %bitcast.258), calls=%async_computation.2 | async-start | bytes 1277952 | tf_op jit(solution)/shard_map/all_to_all | solution.py:717
  223.0 77.8 %all-to-all-start.3 = ((bf16[4,104,768]{2,1,0:T(8,128)(2,1)}), bf16[4,104,768]{2,1,0:T(8,128)(2,1)S(1)}, u32[]{:S(2)}, u32[]{:S(2)}) async-start(bf16[4,104,768]{2,1,0:T(8,128)(2,1)} %bitcast.259), calls=%async_computation.3 | async-start | bytes 1277952 | tf_op jit(solution)/shard_map/all_to_all | solution.py:717
  313.6 21.8 %all-to-all-start.4 = ((bf16[4,104,768]{2,1,0:T(8,128)(2,1)}), bf16[4,104,768]{2,1,0:T(8,128)(2,1)S(1)}, u32[]{:S(2)}, u32[]{:S(2)}) async-start(bf16[4,104,768]{2,1,0:T(8,128)(2,1)} %bitcast.256), calls=%async_computation.4 | async-start | bytes 1277952 | tf_op jit(solution)/shard_map/all_to_all | solution.py:717
  377.2 22.5 %collective-permute-start = (bf16[4,2,2,192,384]{4,3,2,1,0:T(8,128)(2,1)}, bf16[4,2,2,192,384]{4,3,2,1,0:T(8,128)(2,1)S(1)}, u32[]{:S(2)}, u32[]{:S(2)}) collective-permute-start(bf16[4,2,2,192,384]{4,3,2,1,0:T(8,128)(2,1)} %get-tuple-element.139), channel_id=1, source_target_pairs={{0,8},{8,0},{16,24},{24,16},{1,9},{9,1},{17,25},{25,17},{2,10},{10... | collective-permute-start | bytes 7077896 | tf_op jit(solution)/shard_map/ppermute | solution.py:884
  377.3 22.4 %collective-permute-start.1 = (bf16[4,2,2,192,384]{4,3,2,1,0:T(8,128)(2,1)}, bf16[4,2,2,192,384]{4,3,2,1,0:T(8,128)(2,1)S(1)}, u32[]{:S(2)}, u32[]{:S(2)}) collective-permute-start(bf16[4,2,2,192,384]{4,3,2,1,0:T(8,128)(2,1)} %get-tuple-element.141), channel_id=1, source_target_pairs={{0,8},{8,0},{16,24},{24,16},{1,9},{9,1},{17,25},{25,17},{2,10},{10... | collective-permute-start | bytes 7077896 | tf_op jit(solution)/shard_map/ppermute | solution.py:884
  406.6 28.6 %collective-permute-start.2 = (bf16[8,192,384]{2,1,0:T(8,128)(2,1)}, bf16[8,192,384]{2,1,0:T(8,128)(2,1)S(1)}, u32[]{:S(2)}, u32[]{:S(2)}) collective-permute-start(bf16[8,192,384]{2,1,0:T(8,128)(2,1)} %get-tuple-element.148), channel_id=1, source_target_pairs={{0,16},{8,24},{16,0},{24,8},{1,17},{9,25},{17,1},{25,9},{2,18},{10... | collective-permute-start | bytes 3538952 | tf_op jit(solution)/shard_map/ppermute | solution.py:884
  408.0 28.3 %collective-permute-start.3 = (bf16[8,192,384]{2,1,0:T(8,128)(2,1)}, bf16[8,192,384]{2,1,0:T(8,128)(2,1)}, u32[]{:S(2)}, u32[]{:S(2)}) collective-permute-start(bf16[8,192,384]{2,1,0:T(8,128)(2,1)} %get-tuple-element.149), channel_id=1, source_target_pairs={{0,1},{1,0},{2,3},{3,2},{4,5},{5,4},{6,7},{7,6},{8,9},{9,8},{10,11... | collective-permute-start | bytes 3538952 | tf_op jit(solution)/shard_map/ppermute | solution.py:884
  417.1 24.2 %all-to-all-start.5 = ((bf16[4,104,768]{2,1,0:T(8,128)(2,1)}), bf16[4,104,768]{2,1,0:T(8,128)(2,1)}, u32[]{:S(2)}, u32[]{:S(2)}) async-start(bf16[4,104,768]{2,1,0:T(8,128)(2,1)} %bitcast.257), calls=%async_computation.5 | async-start | bytes 1277952 | tf_op jit(solution)/shard_map/all_to_all | solution.py:717
  441.3 28.0 %collective-permute-start.5 = (bf16[8,192,384]{2,1,0:T(8,128)(2,1)}, bf16[8,192,384]{2,1,0:T(8,128)(2,1)}, u32[]{:S(2)}, u32[]{:S(2)}) collective-permute-start(bf16[8,192,384]{2,1,0:T(8,128)(2,1)} %get-tuple-element.158), channel_id=1, source_target_pairs={{0,1},{1,0},{2,3},{3,2},{4,5},{5,4},{6,7},{7,6},{8,9},{9,8},{10,11... | collective-permute-start | bytes 3538952 | tf_op jit(solution)/shard_map/ppermute | solution.py:884
  443.0 27.5 %collective-permute-start.6 = (bf16[8,192,384]{2,1,0:T(8,128)(2,1)}, bf16[8,192,384]{2,1,0:T(8,128)(2,1)}, u32[]{:S(2)}, u32[]{:S(2)}) collective-permute-start(bf16[8,192,384]{2,1,0:T(8,128)(2,1)} %get-tuple-element.159), channel_id=1, source_target_pairs={{0,16},{8,24},{16,0},{24,8},{1,17},{9,25},{17,1},{25,9},{2,18},{10... | collective-permute-start | bytes 3538952 | tf_op jit(solution)/shard_map/ppermute | solution.py:884
  474.6 184.5 %reduce-scatter.7.cloned.1.call-start = ((), (), s32[]{:S(2)}) async-start(), calls=%async_computation.19 | async-start | bytes 737280 | tf_op jit(solution)/shard_map/reduce_scatter | solution.py:913
  494.7 25.0 %collective-permute-start.9 = (bf16[6,192,384]{2,1,0:T(8,128)(2,1)S(1)}, bf16[6,192,384]{2,1,0:T(8,128)(2,1)S(1)}, u32[]{:S(2)}, u32[]{:S(2)}) collective-permute-start(bf16[6,192,384]{2,1,0:T(8,128)(2,1)S(1)} %copy-done.43), channel_id=1, source_target_pairs={{0,1},{1,0},{2,3},{3,2},{4,5},{5,4},{6,7},{7,6},{8,9},{9,8},{10,11... | collective-permute-start | bytes 2654216 | tf_op jit(solution)/shard_map/ppermute | solution.py:884
  495.3 26.6 %collective-permute-start.10 = (bf16[8,192,384]{2,1,0:T(8,128)(2,1)S(1)}, bf16[8,192,384]{2,1,0:T(8,128)(2,1)S(1)}, u32[]{:S(2)}, u32[]{:S(2)}) collective-permute-start(bf16[8,192,384]{2,1,0:T(8,128)(2,1)S(1)} %copy-done.42), channel_id=1, source_target_pairs={{0,16},{8,24},{16,0},{24,8},{1,17},{9,25},{17,1},{25,9},{2,18},{10... | collective-permute-start | bytes 3538952 | tf_op jit(solution)/shard_map/ppermute | solution.py:884
  519.1 30.0 %collective-permute-start.11 = (bf16[4,2,2,192,384]{4,3,2,1,0:T(8,128)(2,1)}, bf16[4,2,2,192,384]{4,3,2,1,0:T(8,128)(2,1)}, u32[]{:S(2)}, u32[]{:S(2)}) collective-permute-start(bf16[4,2,2,192,384]{4,3,2,1,0:T(8,128)(2,1)} %get-tuple-element.186), channel_id=1, source_target_pairs={{0,8},{8,0},{16,24},{24,16},{1,9},{9,1},{17,25},{25,17},{2,10},{10... | collective-permute-start | bytes 7077896 | tf_op jit(solution)/shard_map/ppermute | solution.py:884
  519.2 29.9 %collective-permute-start.12 = (bf16[4,2,2,192,384]{4,3,2,1,0:T(8,128)(2,1)}, bf16[4,2,2,192,384]{4,3,2,1,0:T(8,128)(2,1)}, u32[]{:S(2)}, u32[]{:S(2)}) collective-permute-start(bf16[4,2,2,192,384]{4,3,2,1,0:T(8,128)(2,1)} %get-tuple-element.188), channel_id=1, source_target_pairs={{0,8},{8,0},{16,24},{24,16},{1,9},{9,1},{17,25},{25,17},{2,10},{10... | collective-permute-start | bytes 7077896 | tf_op jit(solution)/shard_map/ppermute | solution.py:884
  548.9 44.3 %collective-permute-start.15 = (bf16[4,2,2,192,384]{4,3,2,1,0:T(8,128)(2,1)}, bf16[4,2,2,192,384]{4,3,2,1,0:T(8,128)(2,1)S(1)}, u32[]{:S(2)}, u32[]{:S(2)}) collective-permute-start(bf16[4,2,2,192,384]{4,3,2,1,0:T(8,128)(2,1)} %get-tuple-element.198), channel_id=1, source_target_pairs={{0,8},{8,0},{16,24},{24,16},{1,9},{9,1},{17,25},{25,17},{2,10},{10... | collective-permute-start | bytes 7077896 | tf_op jit(solution)/shard_map/ppermute | solution.py:884
  549.1 123.4 %reduce-scatter.11.cloned.1.call-start = ((), (), s32[]{:S(2)}) async-start(), calls=%async_computation.21 | async-start | bytes 1474560 | tf_op jit(solution)/shard_map/reduce_scatter | solution.py:913
  553.9 39.3 %collective-permute-start.13 = (bf16[8,192,384]{2,1,0:T(8,128)(2,1)}, bf16[8,192,384]{2,1,0:T(8,128)(2,1)S(1)}, u32[]{:S(2)}, u32[]{:S(2)}) collective-permute-start(bf16[8,192,384]{2,1,0:T(8,128)(2,1)} %get-tuple-element.195), channel_id=1, source_target_pairs={{0,16},{8,24},{16,0},{24,8},{1,17},{9,25},{17,1},{25,9},{2,18},{10... | collective-permute-start | bytes 3538952 | tf_op jit(solution)/shard_map/ppermute | solution.py:884
  555.4 37.8 %collective-permute-start.14 = (bf16[8,192,384]{2,1,0:T(8,128)(2,1)}, bf16[8,192,384]{2,1,0:T(8,128)(2,1)}, u32[]{:S(2)}, u32[]{:S(2)}) collective-permute-start(bf16[8,192,384]{2,1,0:T(8,128)(2,1)} %get-tuple-element.196), channel_id=1, source_target_pairs={{0,1},{1,0},{2,3},{3,2},{4,5},{5,4},{6,7},{7,6},{8,9},{9,8},{10,11... | collective-permute-start | bytes 3538952 | tf_op jit(solution)/shard_map/ppermute | solution.py:884
  564.6 36.8 %all-to-all-start.7 = ((bf16[4,104,768]{2,1,0:T(8,128)(2,1)}), bf16[4,104,768]{2,1,0:T(8,128)(2,1)}, u32[]{:S(2)}, u32[]{:S(2)}) async-start(bf16[4,104,768]{2,1,0:T(8,128)(2,1)} %bitcast.254), calls=%async_computation.7 | async-start | bytes 1277952 | tf_op jit(solution)/shard_map/all_to_all | solution.py:717
  568.8 126.3 %reduce-scatter.5.cloned.1.call-start = ((), (), s32[]{:S(2)}) async-start(), calls=%async_computation.18 | async-start | bytes 921600 | tf_op jit(solution)/shard_map/reduce_scatter | solution.py:913
  568.8 24.4 %collective-permute-start.16 = (bf16[3,192,384]{2,1,0:T(8,128)(2,1)}, bf16[3,192,384]{2,1,0:T(8,128)(2,1)S(1)}, u32[]{:S(2)}, u32[]{:S(2)}) collective-permute-start(bf16[3,192,384]{2,1,0:T(8,128)(2,1)} %get-tuple-element.199), channel_id=1, source_target_pairs={{0,1},{1,0},{2,3},{3,2},{4,5},{5,4},{6,7},{7,6},{8,9},{9,8},{10,11... | collective-permute-start | bytes 1327112 | tf_op jit(solution)/shard_map/ppermute | solution.py:884
  601.3 27.7 %collective-permute-start.18 = (bf16[8,192,384]{2,1,0:T(8,128)(2,1)}, bf16[8,192,384]{2,1,0:T(8,128)(2,1)}, u32[]{:S(2)}, u32[]{:S(2)}) collective-permute-start(bf16[8,192,384]{2,1,0:T(8,128)(2,1)} %get-tuple-element.208), channel_id=1, source_target_pairs={{0,1},{1,0},{2,3},{3,2},{4,5},{5,4},{6,7},{7,6},{8,9},{9,8},{10,11... | collective-permute-start | bytes 3538952 | tf_op jit(solution)/shard_map/ppermute | solution.py:884
  602.8 27.4 %collective-permute-start.19 = (bf16[8,192,384]{2,1,0:T(8,128)(2,1)}, bf16[8,192,384]{2,1,0:T(8,128)(2,1)}, u32[]{:S(2)}, u32[]{:S(2)}) collective-permute-start(bf16[8,192,384]{2,1,0:T(8,128)(2,1)} %get-tuple-element.209), channel_id=1, source_target_pairs={{0,16},{8,24},{16,0},{24,8},{1,17},{9,25},{17,1},{25,9},{2,18},{10... | collective-permute-start | bytes 3538952 | tf_op jit(solution)/shard_map/ppermute | solution.py:884
  621.5 28.1 %collective-permute-start.21 = (bf16[3,2,2,192,384]{4,3,2,1,0:T(8,128)(2,1)}, bf16[3,2,2,192,384]{4,3,2,1,0:T(8,128)(2,1)S(1)}, u32[]{:S(2)}, u32[]{:S(2)}) collective-permute-start(bf16[3,2,2,192,384]{4,3,2,1,0:T(8,128)(2,1)} %get-tuple-element.216), channel_id=1, source_target_pairs={{0,8},{8,0},{16,24},{24,16},{1,9},{9,1},{17,25},{25,17},{2,10},{10... | collective-permute-start | bytes 5308424 | tf_op jit(solution)/shard_map/ppermute | solution.py:884
  621.5 28.1 %collective-permute-start.20 = (bf16[2,2,2,192,384]{4,3,2,1,0:T(8,128)(2,1)}, bf16[2,2,2,192,384]{4,3,2,1,0:T(8,128)(2,1)S(1)}, u32[]{:S(2)}, u32[]{:S(2)}) collective-permute-start(bf16[2,2,2,192,384]{4,3,2,1,0:T(8,128)(2,1)} %get-tuple-element.214), channel_id=1, source_target_pairs={{0,8},{8,0},{16,24},{24,16},{1,9},{9,1},{17,25},{25,17},{2,10},{10... | collective-permute-start | bytes 3538952 | tf_op jit(solution)/shard_map/ppermute | solution.py:884
  630.3 27.5 %all-to-all-start.8 = ((bf16[4,104,768]{2,1,0:T(8,128)(2,1)}), bf16[4,104,768]{2,1,0:T(8,128)(2,1)}, u32[]{:S(2)}, u32[]{:S(2)}) async-start(bf16[4,104,768]{2,1,0:T(8,128)(2,1)} %bitcast.253), calls=%async_computation.8 | async-start | bytes 1277952 | tf_op jit(solution)/shard_map/all_to_all | solution.py:717
  634.4 82.6 %reduce-scatter.9.cloned.1.call-start = ((), (), s32[]{:S(2)}) async-start(), calls=%async_computation.20 | async-start | bytes 1474560 | tf_op jit(solution)/shard_map/reduce_scatter | solution.py:913
  657.8 26.9 %collective-permute-start.22 = (bf16[8,192,384]{2,1,0:T(8,128)(2,1)}, bf16[8,192,384]{2,1,0:T(8,128)(2,1)S(1)}, u32[]{:S(2)}, u32[]{:S(2)}) collective-permute-start(bf16[8,192,384]{2,1,0:T(8,128)(2,1)} %get-tuple-element.222), channel_id=1, source_target_pairs={{0,16},{8,24},{16,0},{24,8},{1,17},{9,25},{17,1},{25,9},{2,18},{10... | collective-permute-start | bytes 3538952 | tf_op jit(solution)/shard_map/ppermute | solution.py:884
  666.0 24.0 %all-to-all-start.11 = ((f32[32,1,384]{2,1,0:T(1,128)}), f32[32,1,384]{2,1,0:T(1,128)S(1)}, u32[]{:S(2)}, u32[]{:S(2)}) async-start(f32[32,1,384]{2,1,0:T(1,128)} %copy.109), calls=%async_computation.15 | async-start | bytes 98304 | tf_op jit(solution)/shard_map/all_to_all | solution.py:972
  (55 other events, 316.7 us)
Sparse Core Ops, SparseCore 0:
  11.1 137.4 all-gather.2
  151.7 149.0 all-gather.4
  549.2 20.2 reduce-scatter.6
  571.6 33.0 reduce-scatter.10
  622.1 23.3 reduce-scatter.4
  660.2 31.1 reduce-scatter.8

commit v7 on v6

--- a/solution.py
+++ b/solution.py
@@ -84,12 +84,27 @@
         real = rest < self.frames * self.block
         return way, frame, rest - frame * self.block, real
 
-    def to_time(self):
-        r = lax.broadcasted_iota(jnp.int32, (self.time_rows, 1), 0)
-        way, frame, place, real = self.split(r)
+    def to_time(self, k, member):
+        r = lax.broadcasted_iota(jnp.int32, (self.chunk, 1), 0)
+        _, frame, place, real = self.split(r)
+        way = jnp.bitwise_xor(member, k)
         source = jnp.where(real, frame * self.frame_rows + way * self.block + place, -1)
-        c = lax.broadcasted_iota(jnp.int32, (self.time_rows, self.rows), 1)
+        c = lax.broadcasted_iota(jnp.int32, (self.chunk, self.rows), 1)
         return jnp.where(c == source, 1.0, 0.0).astype(BF16)
+
+    def gathered(self, chunk_refs, member):
+        total = tn(self.to_time(0, member), chunk_refs[0][...])
+        for k in range(1, self.ways):
+            total = total + tn(self.to_time(k, member), chunk_refs[k][...])
+        return total
+
+    def chunks(self, width, block=None, index=None):
+        return [
+            made((self.chunk, width), BF16)
+            if block is None
+            else made((self.chunk, width), BF16, (self.chunk, block), index)
+            for _ in range(self.ways)
+        ]
 
     def time_bias(self):
         def label(r):
@@ -204,27 +219,37 @@
     return pl.BlockSpec((count, 1, depth, width), lambda h, *_: (first // count, h, 0, 0))
 
 
-def send_first(rows, x, gb):
-    def body(x_ref, gb_ref, out_ref):
+def send_first(rows, x, gb, me):
+    def body(me_ref, x_ref, gb_ref, *out_refs):
         a = norm_rounded(x_ref[...], gb_ref[0:1], gb_ref[3:4])
-        out_ref[...] = nn(rows.to_time(), a).astype(BF16)
+        for k in range(rows.ways):
+            out_refs[k][...] = nn(rows.to_time(k, me_ref[3]), a).astype(BF16)
 
     d = x.shape[1]
     return call(
-        body, (1,), [whole(x.shape), whole(gb.shape)], [made((rows.time_rows, d), BF16)], [], (x, gb)
-    )[0]
-
-
-def time_forward(rows, a, w, head_shares):
-    t, d = a.shape
+        body, (1,), [SCALARS, whole(x.shape), whole(gb.shape)], rows.chunks(d), [], (me, x, gb)
+    )
+
+
+def time_forward(rows, chunks, w):
+    t, d = rows.time_rows, chunks[0].shape[1]
     width = w.shape[3]
+    shares = w.shape[1]
     pairs = width // LANES
+    ways = rows.ways
     rate = LOG2E / math.sqrt(HEAD_DIM)
 
-    def body(a_ref, w_ref, qkv_ref, out_ref, log_ref, bias_ref):
+    def body(*refs):
+        chunk_refs = refs[:ways]
+        w_ref, a_ref, qkv_ref, log_ref = refs[ways : ways + 4]
+        out_refs = refs[ways + 4 : 2 * ways + 4]
+        bias_ref, mixed_ref = refs[2 * ways + 4 :]
+
         @pl.when(pl.program_id(0) == 0)
         def _():
             bias_ref[...] = rows.time_bias()
+            for k in range(ways):
+                a_ref[k * rows.chunk : (k + 1) * rows.chunk] = chunk_refs[k][...]
 
         act = a_ref[...]
         for g in range(3):
@@ -236,31 +261,37 @@
             mixed, logs = pair_forward(
                 qkv_ref[0, :, lanes], qkv_ref[1, :, lanes], qkv_ref[2, :, lanes], bias_ref[...], rate
             )
-            out_ref[:, lanes] = mixed
+            mixed_ref[:, lanes] = mixed
             log_ref[0, i] = jnp.concatenate(logs, axis=0)
 
-    return call(
+        for k in range(ways):
+            out_refs[k][...] = mixed_ref[k * rows.chunk : (k + 1) * rows.chunk]
+
+    got = call(
         body,
-        (head_shares,),
-        [whole(a.shape), slabs(3, 0, width, d)],
+        (shares,),
+        [whole(c.shape) for c in chunks] + [slabs(3, 0, width, d)],
         [
+            made((t, d), BF16),
             made((3, t, d), BF16, (3, t, width), lambda h: (0, 0, h)),
-            made((t, d), BF16, (t, width), lambda h: (0, h)),
-            made((head_shares, pairs, 2, t), F32, (1, pairs, 2, t), lambda h: (h, 0, 0, 0)),
+            made((shares, pairs, 2, t), F32, (1, pairs, 2, t), lambda h: (h, 0, 0, 0)),
+            *rows.chunks(d, width, lambda h: (0, h)),
         ],
-        [pltpu.VMEM((t, t), F32)],
-        (a, w),
+        [pltpu.VMEM((t, t), F32), pltpu.VMEM((t, width), BF16)],
+        (*chunks, w),
         flops=2 * t * d * 3 * d,
     )
-
-
-def middle_forward(rows, back, x, w, mix, gb):
+    return got[0], got[1], got[2], got[3:]
+
+
+def middle_forward(rows, back, x, w, mix, gb, me):
     t, d = x.shape
     width = w.shape[3]
     shares = w.shape[1]
 
-    def body(back_ref, x_ref, to_ref, sq_ref, mix_ref, gb_ref, o1_ref, y1_ref, x1_ref, qkv_ref):
-        o1 = tn(rows.to_time(), back_ref[...]).astype(BF16)
+    def body(me_ref, *refs):
+        x_ref, to_ref, sq_ref, mix_ref, gb_ref, o1_ref, y1_ref, x1_ref, qkv_ref = refs[rows.ways :]
+        o1 = rows.gathered(refs[: rows.ways], me_ref[3]).astype(BF16)
         o1_ref[...] = o1
         y1 = jnp.zeros((t, d), F32)
         for h in range(shares):
@@ -278,7 +309,8 @@
         body,
         (1,),
         [
-            whole(back.shape),
+            SCALARS,
+            *(whole(c.shape) for c in back),
             whole(x.shape),
             pl.BlockSpec((1, shares, d, width), lambda i: (6, 0, 0, 0)),
             pl.BlockSpec((3, shares, d, width), lambda i: (1, 0, 0, 0)),
@@ -287,7 +319,7 @@
         ],
         [made((t, d), BF16), made((t, d), BF16), made((t, d), F32), made((3, t, d), BF16)],
         [],
-        (back, x, w, w, mix, gb),
+        (me, *back, x, w, w, mix, gb),
         flops=2 * t * d * 5 * d,
     )
 
@@ -350,7 +382,7 @@
     )
 
 
-def mlp_forward(rows, x2, w, gb, gb_next):
+def mlp_forward(rows, x2, w, gb, gb_next, me):
     t, d = x2.shape
     width = w.shape[3]
     shares = w.shape[1]
@@ -362,7 +394,8 @@
         if last:
             x3_ref, a3_ref = rest
         else:
-            gn_ref, x3_ref, send_ref, a3_ref = rest
+            me_ref, gn_ref, x3_ref = rest[:3]
+            send_refs, a3_ref = rest[3:-1], rest[-1]
         j = pl.program_id(0)
 
         @pl.when(j == 0)
@@ -379,7 +412,8 @@
             @pl.when(j == steps - 1)
             def _():
                 a = norm_rounded(x3_ref[...], gn_ref[0:1], gn_ref[3:4])
-                send_ref[...] = nn(rows.to_time(), a).astype(BF16)
+                for k in range(rows.ways):
+                    send_refs[k][...] = nn(rows.to_time(k, me_ref[3]), a).astype(BF16)
 
     ins = [
         whole(x2.shape),
@@ -390,9 +424,9 @@
     outs = [made((t, d), F32)]
     args = [x2, w, w, gb]
     if not last:
-        ins.append(whole(gb_next.shape))
-        outs.append(made((rows.time_rows, d), BF16))
-        args.append(gb_next)
+        ins += [SCALARS, whole(gb_next.shape)]
+        outs += rows.chunks(d)
+        args += [me, gb_next]
     return call(
         body, (steps,), ins, outs, [pltpu.VMEM((t, d), BF16)], tuple(args), flops=4 * t * d * width * steps
     )
@@ -568,18 +602,21 @@
     fits = mix_fits(d, shards, shares)
     part = d // (shards * shares)
 
-    def body(me_ref, g_ref, y1_ref, o1_ref, to_ref, mix_ref, send_ref, gk_ref, gs_ref, *rest):
+    def body(me_ref, g_ref, y1_ref, o1_ref, to_ref, mix_ref, *rest):
+        send_refs, rest = rest[: rows.ways], rest[rows.ways :]
+        gk_ref, gs_ref, *rest = rest
         if fits:
             room_ref, order_ref = rest
         else:
             gm_ref, room_ref = rest
         e1 = g_ref[...].astype(BF16)
         dy1 = nt(e1, mix_ref[...]).astype(BF16)
-        send = rows.to_time()
+        sends = [rows.to_time(k, me_ref[3]) for k in range(rows.ways)]
         for h in range(shares):
             lanes = slice(h * width, (h + 1) * width)
             do1 = nn(dy1, to_ref[0, h]).astype(BF16)
-            send_ref[:, lanes] = nn(send, do1).astype(BF16)
+            for k in range(rows.ways):
+                send_refs[k][:, lanes] = nn(sends[k], do1).astype(BF16)
             split_rows(tn(dy1, o1_ref[:, lanes]), gk_ref, gs_ref, (0, h), room_ref, me_ref)
         gm = tn(y1_ref[...], e1)
         if fits:
@@ -591,7 +628,7 @@
         else:
             gm_ref[...] = gm.astype(BF16)
 
-    outs = [made((rows.time_rows, d), BF16)]
+    outs = rows.chunks(d)
     outs += halves.array((1 + fits, shares), (1 + fits, shares), lambda i: (0, 0))
     scratch = [halves.room()]
     if fits:
@@ -614,9 +651,9 @@
         (me, grad, y1, o1, w, mix),
         flops=8 * t * d * d,
     )
-    do1, keep, send = got[:3]
+    do1, (keep, send) = got[: rows.ways], got[rows.ways : rows.ways + 2]
     if not fits:
-        gm = mix_slab(got[3], shards, shares).reshape((1, shares, halves.pairs, 2) + keep.shape[3:])
+        gm = mix_slab(got[-1], shards, shares).reshape((1, shares, halves.pairs, 2) + keep.shape[3:])
         keep = jnp.concatenate((keep, lax.dynamic_index_in_dim(gm, me[0], 3, keepdims=False)), axis=0)
         send = jnp.concatenate((send, lax.dynamic_index_in_dim(gm, 1 - me[0], 3, keepdims=False)), axis=0)
     return do1, (keep, send)
@@ -630,7 +667,11 @@
     scale = 1.0 / math.sqrt(HEAD_DIM)
     rate = LOG2E * scale
 
-    def body(me_ref, do_ref, a_ref, qkv_ref, log_ref, w_ref, out_ref, keep_ref, send_ref, bias_ref, dqkv_ref, at_ref, u_ref, room_ref):
+    def body(me_ref, *refs):
+        do_refs, refs = refs[: rows.ways], refs[rows.ways :]
+        a_ref, qkv_ref, log_ref, w_ref = refs[:4]
+        out_refs, refs = refs[4 : 4 + rows.ways], refs[4 + rows.ways :]
+        keep_ref, send_ref, bias_ref, dqkv_ref, at_ref, u_ref, room_ref, do_ref = refs
         h = pl.program_id(0)
 
         @pl.when(h == 0)
@@ -638,6 +679,9 @@
             bias_ref[...] = rows.time_bias()
             at_ref[...] = a_ref[...].T
             u_ref[...] = jnp.zeros((t, d), F32)
+
+        for k in range(rows.ways):
+            do_ref[k * rows.chunk : (k + 1) * rows.chunk] = do_refs[k][...]
 
         @pl.loop(0, pairs)
         def _(i):
@@ -664,21 +708,22 @@
 
         @pl.when(h == shares - 1)
         def _():
-            out_ref[...] = u_ref[...].astype(BF16)
-
-    da1, keep, send = call(
+            for k in range(rows.ways):
+                out_refs[k][...] = u_ref[k * rows.chunk : (k + 1) * rows.chunk].astype(BF16)
+
+    got = call(
         body,
         (shares,),
         [
             SCALARS,
-            pl.BlockSpec((t, width), lambda h: (0, h)),
+            *(pl.BlockSpec((rows.chunk, width), lambda h: (0, h)) for _ in do1),
             whole(a.shape),
             pl.BlockSpec((3, t, width), lambda h: (0, 0, h)),
             pl.BlockSpec((1,) + logs.shape[1:], lambda h: (h, 0, 0, 0)),
             slabs(3, 0, width, d),
         ],
         [
-            made((t, d), BF16),
+            *rows.chunks(d),
             *halves.array((3, shares), (3, 1), lambda h: (0, h)),
         ],
         [
@@ -687,18 +732,20 @@
             pltpu.VMEM((d, t), BF16),
             pltpu.VMEM((t, d), F32),
             halves.room(),
+            pltpu.VMEM((t, width), BF16),
         ],
-        (me, do1, a, qkv, logs, w),
+        (me, *do1, a, qkv, logs, w),
         flops=2 * t * d * d * 6,
     )
-    return da1, (keep, send)
-
-
-def first_norm_back(rows, back, x, grad, gb):
+    return got[: rows.ways], tuple(got[rows.ways :])
+
+
+def first_norm_back(rows, back, x, grad, gb, me):
     t, d = x.shape
 
-    def body(back_ref, x_ref, g_ref, gb_ref, go_ref, sums_ref):
-        u = tn(rows.to_time(), back_ref[...])
+    def body(me_ref, *refs):
+        x_ref, g_ref, gb_ref, go_ref, sums_ref = refs[rows.ways :]
+        u = rows.gathered(refs[: rows.ways], me_ref[3])
         change, sums = norm_back(u, x_ref[...], gb_ref[0:1])
         go_ref[...] = g_ref[...] + change
         sums_ref[...] = sums
@@ -706,15 +753,49 @@
     return call(
         body,
         (1,),
-        [whole(back.shape), whole(x.shape), whole(grad.shape), whole(gb.shape)],
+        [SCALARS, *(whole(c.shape) for c in back), whole(x.shape), whole(grad.shape), whole(gb.shape)],
         [made((t, d), F32), made((2, d), F32)],
         [],
-        (back, x, grad, gb),
-    )
-
-
-def swap_places(rows_array):
-    return lax.all_to_all(rows_array, "seq", split_axis=0, concat_axis=0, tiled=True)
+        (me, *back, x, grad, gb),
+    )
+
+
+def homes():
+    clips, ways = lax.axis_size("clip"), lax.axis_size("seq")
+    pairs = []
+    for clip in range(clips):
+        for seq in range(ways):
+            home_clip = clip - clip % 2 + seq % 2
+            home_seq = seq // 2 + (ways // 2) * (clip % 2)
+            pairs.append((clip * ways + seq, home_clip * ways + home_seq))
+    return pairs
+
+
+def go_home(a):
+    return lax.ppermute(a, ("clip", "seq"), homes())
+
+
+def go_back(a):
+    return lax.ppermute(a, ("clip", "seq"), [(home, device) for device, home in homes()])
+
+
+def member_of(clip, seq):
+    return clip % 2 + 2 * (seq % (lax.axis_size("seq") // 2))
+
+
+def swap_places(chunks):
+    clips, ways = lax.axis_size("clip"), lax.axis_size("seq")
+    got = [chunks[0]]
+    for k in range(1, ways):
+        pairs = []
+        for clip in range(clips):
+            for seq in range(ways):
+                other = member_of(clip, seq) ^ k
+                to_clip = clip - clip % 2 + other % 2
+                to_seq = seq - seq % (ways // 2) + other // 2
+                pairs.append((clip * ways + seq, to_clip * ways + to_seq))
+        got.append(lax.ppermute(chunks[k], ("clip", "seq"), pairs))
+    return got
 
 
 def pack_layer(time_qkv, time_out, time_mix, space_qkv, space_out, mlp_in, mlp_out):
@@ -1014,27 +1095,28 @@
     ]
     mixes = [mix_whole(w[-1], shards) for w in weights]
 
-    x = as_rows(tokens)
-    send = send_first(rows, x, gb[0])
+    halves = Halves(lax.axis_size("clip"), d, time_qkv.shape[3])
+    clip = lax.axis_index("clip")
+    member = member_of(clip, lax.axis_index("seq"))
+    me = jnp.stack((clip & 1, (clip >> 1) & 1, lax.axis_index("head"), member)).astype(jnp.int32)
+
+    x = as_rows(go_home(tokens))
+    send = send_first(rows, x, gb[0], me)
     kept = []
     for l in range(layers):
         w = weights[l]
-        a1 = swap_places(send)
-        qkv1, o1_time, log1 = time_forward(rows, a1, w, shares)
+        a1, qkv1, log1, o1_time = time_forward(rows, swap_places(send), w)
         back = swap_places(o1_time)
-        o1, y1, x1, qkv2 = middle_forward(rows, back, x, w, mixes[l], gb[l])
+        o1, y1, x1, qkv2 = middle_forward(rows, back, x, w, mixes[l], gb[l], me)
         o2, x2, log2 = space_forward(rows, qkv2, x1, w)
         kept.append((x, a1, qkv1, log1, o1, y1, x1, qkv2, o2, log2, x2))
         if l + 1 < layers:
-            x, send = mlp_forward(rows, x2, w, gb[l], gb[l + 1])
+            x, *send = mlp_forward(rows, x2, w, gb[l], gb[l + 1], me)
         else:
-            (x,) = mlp_forward(rows, x2, w, gb[l], None)
-    output = from_rows(x).astype(BF16)
-
-    grad = as_rows(cotangent)
-    halves = Halves(lax.axis_size("clip"), d, time_qkv.shape[3])
-    clip = lax.axis_index("clip")
-    me = jnp.stack((clip & 1, (clip >> 1) & 1, lax.axis_index("head"))).astype(jnp.int32)
+            (x,) = mlp_forward(rows, x2, w, gb[l], None, me)
+    output = go_back(from_rows(x.astype(BF16)))
+
+    grad = as_rows(go_home(cotangent))
     norm_rows = [None] * layers
     summed = [None] * layers
     late = []
@@ -1065,7 +1147,7 @@
             rest = pieces_of([g_out, g_time])
             da1 = move(da1, ff + space + rest, me)
             late = space + rest
-        grad, s1 = first_norm_back(rows, da1, x, grad, gb[l])
+        grad, s1 = first_norm_back(rows, da1, x, grad, gb[l], me)
         norm_rows[l] = jnp.concatenate((s1[0:1], s2[0:1], s3[0:1], s1[1:2], s2[1:2], s3[1:2]), axis=0)
         if quick:
             summed[l] = ff + space + rest
@@ -1081,7 +1163,7 @@
         slabs_of = jnp.concatenate(some, axis=0)
         ends = [sum(cuts[: i + 1]) for i in range(4)]
         results.append([slabs_of[e - c : e] for c, e in zip(cuts, ends)])
-    tokens_grad = from_rows(grad)
+    tokens_grad = go_back(from_rows(grad.astype(BF16))).astype(F32)
     norm_sums = reduce_norms(jnp.concatenate(norm_rows, axis=0)).reshape(layers, 2, 3, -1)
 
     def stacked(form):

time: 745 us -> 782 us (1.050)
  waiting for transfers between devices: 293 us -> 344 us
  blocking collectives: 26.7 us -> 0 us
    ppermute x0 -> x28, waiting for transfers between devices: none -> 41.4 us  [the longest x24 41.4 us: swap_places(): got.append(lax.ppermute(chunks[k], ('clip', 'seq'), pairs))]
    all_to_all x7 -> x0, waiting for transfers between devices: 40.7 us -> none  [swap_places(): lax.all_to_all(rows_array, 'seq', split_axis=0, concat_axis=0, tiled=True)]
    ppermute x26, waiting for transfers between devices: 70.6 us -> 104 us  [cross(): return lax.ppermute(a, axis, [(i, i ^ 1 << bit) for i in range(size)])]
    all_to_all x7 -> x0, starting transfers between devices: 28.1 us -> none  [swap_places(): lax.all_to_all(rows_array, 'seq', split_axis=0, concat_axis=0, tiled=True)]
    all_to_all x1 -> x0, blocking collectives: 26.7 us -> none  [swap_places(): lax.all_to_all(rows_array, 'seq', split_axis=0, concat_axis=0, tiled=True)]
    ppermute x0 -> x28, starting transfers between devices: none -> 22 us  [the longest x24 19.2 us: swap_places(): got.append(lax.ppermute(chunks[k], ('clip', 'seq'), pairs))]
    all_to_all x1, waiting for transfers between devices: 5.99 us -> 26 us  [gather_norms(): lax.all_to_all(jnp.broadcast_to(padded, (count, width)), ALL, split_axis=...]
    all_to_all x2, starting transfers between devices: 9.66 us -> 21.1 us  [move(): lax.all_to_all(array, 'seq', split_axis=0, concat_axis=0, tiled=True)]
  transfers between devices with their start and end apart: 43 -> 64, of which waited for: 20 -> 22; matrix products, arithmetic and copies ran while one was open for 4% -> 4% of each run, Pallas kernels for 31% -> 28%
where the time goes in v7:
time: 782 us; the launch traced here: 773 us
  waiting for transfers between devices  344 us (44%)
  Pallas kernels  287 us (37%)
  starting transfers between devices  76.1 us (10%)
  local copies, waits for them, and re-layouts  35.4 us (5%)
  between operations  15.9 us (2%)
  other arithmetic  15.4 us (2%)
    pallas_call x19, Pallas kernels, call(): pl.pallas_call(body, out_shape=[shape for shape, _ in outs], grid=grid, i...  241 us
    all_gather x2, waiting for transfers between devices, gather_slabs(): full = lax.all_gather(pack, ('head', 'clip', 'seq'), axis=1, tiled=True)  157 us
    ppermute x26, waiting for transfers between devices, cross(): return lax.ppermute(a, axis, [(i, i ^ 1 << bit) for i in range(size)])  104 us
    pallas_call x9, Pallas kernels, fold(): pl.pallas_call(body, out_shape=[jax.ShapeDtypeStruct(shape, BF16) for sha...  45.9 us
    ppermute x24, waiting for transfers between devices, swap_places(): got.append(lax.ppermute(chunks[k], ('clip', 'seq'), pairs))  41.4 us
    all_to_all x1, waiting for transfers between devices, gather_norms(): lax.all_to_all(jnp.broadcast_to(padded, (count, width)), ALL, split_axis=...  26 us
    unnamed x156, local copies, waits for them, and re-layouts  21.8 us
    ppermute x26, starting transfers between devices, cross(): return lax.ppermute(a, axis, [(i, i ^ 1 << bit) for i in range(size)])  21.2 us
  transfers between devices with their start and end apart: 64, of which 22 were waited for; matrix products, arithmetic and copies ran while one was open for 4% of the time, Pallas kernels for 28%

profile of v7, /device:TPU:0, one launch (start us, length us, event | category | flops | bytes accessed | tf_op | source)
XLA Modules:
  0.0 773.3 jit_solution(11207589026820994233)
XLA Ops:
  13.0 8.8 %all-to-all-start = ((f32[32,1,384]{2,1,0:T(1,128)}), f32[32,1,384]{2,1,0:T(1,128)S(1)}, u32[]{:S(2)}, u32[]{:S(2)}) async-start(f32[32,1,384]{2,1,0:T(1,128)} %broadcast_in_dim.17), calls=%async_computation | async-start | bytes 98304 | tf_op jit(solution)/shard_map/all_to_all | solution.py:1040
  22.5 26.0 %all-to-all-done = f32[32,1,384]{2,1,0:T(1,128)S(1)} async-done(((f32[32,1,384]{2,1,0:T(1,128)}), f32[32,1,384]{2,1,0:T(1,128)S(1)}, u32[]{:S(2)}, u32[]{:S(2)}) %all-to-all-start) | async-done | bytes 49184 | tf_op jit(solution)/shard_map/all_to_all | solution.py:1040
  55.5 14.2 %collective-permute-done.2.refs_2_ = bf16[104,768]{1,0:T(8,128)(2,1)S(1)} collective-permute-done((bf16[104,768]{1,0:T(8,128)(2,1)}, bf16[104,768]{1,0:T(8,128)(2,1)S(1)}, u32[]{:S(2)}, u32[]{:S(2)}) %collective-permute-start.2) | collective-permute-done | bytes 159776 | tf_op jit(solution)/shard_map/ppermute | solution.py:797
  69.8 11.5 %collective-permute-done.3.refs_3_ = bf16[104,768]{1,0:T(8,128)(2,1)S(1)} collective-permute-done((bf16[104,768]{1,0:T(8,128)(2,1)}, bf16[104,768]{1,0:T(8,128)(2,1)S(1)}, u32[]{:S(2)}, u32[]{:S(2)}) %collective-permute-start.3) | collective-permute-done | bytes 159776 | tf_op jit(solution)/shard_map/ppermute | solution.py:797
  81.3 72.9 %all-gather.3.cloned.1.call-done = bf16[17,1536,384]{2,1,0:T(8,128)(2,1)} async-done(((bf16[17,48,384]{2,1,0:T(8,128)(2,1)}), bf16[17,1536,384]{2,1,0:T(8,128)(2,1)}) %all-gather.3.cloned.1.call-update) | async-done | bytes 20054032 | tf_op jit(solution)/shard_map/all_gather | solution.py:825
  154.1 12.3 %shard_map.195 = (bf16[416,768]{1,0:T(8,128)(2,1)}, bf16[3,416,768]{2,1,0:T(8,128)(2,1)}, f32[2,3,2,416]{3,2,1,0:T(2,128)}, bf16[104,768]{1,0:T(8,128)(2,1)}, bf...) custom-call(bf16[104,768]{1,0:T(8,128)(2,1)} %get-tuple-element.169.refs_0_, ...), custom_call_target="tpu_custom_call" | custom-call | flops 1472200704 | bytes 23907840 | tf_op jit(solution)/shard_map/pallas_call | solution.py:194
  173.4 6.7 collective-permute-done.5.refs_2_
  186.9 9.4 %shard_map.196 = (bf16[416,768]{1,0:T(8,128)(2,1)}, bf16[416,768]{1,0:T(8,128)(2,1)}, f32[416,768]{1,0:T(8,128)}, bf16[3,416,768]{2,1,0:T(8,128)(2,1)}) custom-call(s32[4]{0:T(128)} %pad_add_fusion.me_ref.rest_0_, bf16[104,768]{1,0:T(8,128)(2,1)} %get-tuple-element.173.refs_0_, bf16[104,768]{1,0:T(8,128)(2,1)} %copy-done.46, bf16[104,768]{1,0:T(8,128)(2,1)} %copy-done.47, ...), custom_call_target="tpu_custom_call" | custom-call | flops 2453667840 | bytes 47695888 | tf_op jit(solution)/shard_map/pallas_call | solution.py:194
  196.3 10.0 %shard_map.197 = (bf16[416,768]{1,0:T(8,128)(2,1)}, f32[416,768]{1,0:T(8,128)}, f32[2,3,2,2,208]{4,3,2,1,0:T(2,128)}) custom-call(bf16[3,416,768]{2,1,0:T(8,128)(2,1)} %get-tuple-element.177.qkv_ref, f32[416,768]{1,0:T(8,128)} %get-tuple-element.178.x1_ref, bf16[17,2,768,384]{3,2,1,0:T(8,128)(2,1)} %bitcast.206), custom_call_target="tpu_custom_call" | custom-call | flops 490733568 | bytes 25185792 | tf_op jit(solution)/shard_map/pallas_call | solution.py:194
  206.3 13.3 %shard_map.198 = (f32[416,768]{1,0:T(8,128)}, bf16[104,768]{1,0:T(8,128)(2,1)}, bf16[104,768]{1,0:T(8,128)(2,1)}, bf16[104,768]{1,0:T(8,128)(2,1)}, bf16[104,768]{1,0:T(8,128)(2,1)}) custom-call(f32[416,768]{1,0:T(8,128)} %get-tuple-element.179.x2_ref, bf16[17,2,768,384]{3,2,1,0:T(8,128)(2,1)} %bitcast.207, bf16[17,2,768,384]{3,2,1,0:T(8,128)(2,1)} %bitcast.208, ...), custom_call_target="tpu_custom_call" | custom-call | flops 3925868544 | bytes 43339792 | tf_op jit(solution)/shard_map/pallas_call | solution.py:194
  221.6 84.1 %all-gather.5.cloned.1.call-done = bf16[17,1536,384]{2,1,0:T(8,128)(2,1)} async-done(((bf16[17,48,384]{2,1,0:T(8,128)(2,1)}), bf16[17,1536,384]{2,1,0:T(8,128)(2,1)}) %all-gather.5.cloned.1.call-update) | async-done | bytes 20054032 | tf_op jit(solution)/shard_map/all_gather | solution.py:825
  306.4 12.2 %shard_map.199 = (bf16[416,768]{1,0:T(8,128)(2,1)}, bf16[3,416,768]{2,1,0:T(8,128)(2,1)}, f32[2,3,2,416]{3,2,1,0:T(2,128)}, bf16[104,768]{1,0:T(8,128)(2,1)}, bf...) custom-call(bf16[104,768]{1,0:T(8,128)(2,1)} %get-tuple-element.180.refs_0_, ...), custom_call_target="tpu_custom_call" | custom-call | flops 1472200704 | bytes 23907840 | tf_op jit(solution)/shard_map/pallas_call | solution.py:194
  328.8 9.4 %shard_map.200 = (bf16[416,768]{1,0:T(8,128)(2,1)}, bf16[416,768]{1,0:T(8,128)(2,1)}, f32[416,768]{1,0:T(8,128)}, bf16[3,416,768]{2,1,0:T(8,128)(2,1)}) custom-call(s32[4]{0:T(128)} %pad_add_fusion.me_ref.rest_0_, bf16[104,768]{1,0:T(8,128)(2,1)} %get-tuple-element.184.refs_0_, bf16[104,768]{1,0:T(8,128)(2,1)} %copy-done.49, bf16[104,768]{1,0:T(8,128)(2,1)} %copy-done.50, ...), custom_call_target="tpu_custom_call" | custom-call | flops 2453667840 | bytes 47695888 | tf_op jit(solution)/shard_map/pallas_call | solution.py:194
  338.2 9.9 %shard_map.201 = (bf16[416,768]{1,0:T(8,128)(2,1)}, f32[416,768]{1,0:T(8,128)}, f32[2,3,2,2,208]{4,3,2,1,0:T(2,128)}) custom-call(bf16[3,416,768]{2,1,0:T(8,128)(2,1)} %get-tuple-element.189.qkv_ref, f32[416,768]{1,0:T(8,128)} %get-tuple-element.190.x1_ref, bf16[17,2,768,384]{3,2,1,0:T(8,128)(2,1)} %bitcast.194), custom_call_target="tpu_custom_call" | custom-call | flops 490733568 | bytes 25185792 | tf_op jit(solution)/shard_map/pallas_call | solution.py:194
  348.0 22.6 %shard_map.203 = (f32[416,768]{1,0:T(8,128)}, bf16[4,2,2,192,384]{4,3,2,1,0:T(8,128)(2,1)}, bf16[4,2,2,192,384]{4,3,2,1,0:T(8,128)(2,1)}, bf16[4,2,2,192,384]{4,...) custom-call(s32[4]{0:T(128)} %pad_add_fusion.me_ref.rest_0_, ...), custom_call_target="tpu_custom_call" | custom-call | flops 9814671360 | bytes 53403664 | tf_op jit(solution)/shard_map/pallas_call | solution.py:194
  371.3 21.6 %shard_map.204 = (f32[416,768]{1,0:T(8,128)}, bf16[4,2,2,192,384]{4,3,2,1,0:T(8,128)(2,1)}, bf16[4,2,2,192,384]{4,3,2,1,0:T(8,128)(2,1)}, f32[2,768]{1,0:T(2,128)}) custom-call(s32[4]{0:T(128)} %pad_add_fusion.me_ref.rest_0_, f32[416,768]{1,0:T(8,128)} %get-tuple-element.192.g_ref, f32[416,768]{1,0:T(8,128)} %get-tuple-element.190.x1_ref, ...), custom_call_target="tpu_custom_call" | custom-call | flops 3925868544 | bytes 51260944 | tf_op jit(solution)/shard_map/pallas_call | solution.py:194
  402.4 7.8 %shard_map.206 = (bf16[104,768]{1,0:T(8,128)(2,1)}, bf16[104,768]{1,0:T(8,128)(2,1)}, bf16[104,768]{1,0:T(8,128)(2,1)}, bf16[104,768]{1,0:T(8,128)(2,1)}, bf16[2...) custom-call(s32[4]{0:T(128)} %pad_add_fusion.me_ref.rest_0_, ...), custom_call_target="tpu_custom_call" | custom-call | flops 1962934272 | bytes 26787856 | tf_op jit(solution)/shard_map/pallas_call | solution.py:194
  412.1 16.5 %collective-permute-done.20.refs_2_ = bf16[8,192,384]{2,1,0:T(8,128)(2,1)S(1)} collective-permute-done((bf16[8,192,384]{2,1,0:T(8,128)(2,1)}, bf16[8,192,384]{2,1,0:T(8,128)(2,1)S(1)}, u32[]{:S(2)}, u32[]{:S(2)}) %collective-permute-start.20) | collective-permute-done | bytes 1179680 | tf_op jit(solution)/shard_map/ppermute | solution.py:965
  436.6 18.4 %shard_map.208 = (bf16[104,768]{1,0:T(8,128)(2,1)}, bf16[104,768]{1,0:T(8,128)(2,1)}, bf16[104,768]{1,0:T(8,128)(2,1)}, bf16[104,768]{1,0:T(8,128)(2,1)}, bf16[3...) custom-call(s32[4]{0:T(128)} %pad_add_fusion.me_ref.rest_0_, ...), custom_call_target="tpu_custom_call" | custom-call | flops 2944401408 | bytes 27446800 | tf_op jit(solution)/shard_map/pallas_call | solution.py:194
  457.2 26.4 %collective-permute-done.23.refs_3_.refs_4_ = bf16[8,192,384]{2,1,0:T(8,128)(2,1)S(1)} collective-permute-done((bf16[8,192,384]{2,1,0:T(8,128)(2,1)}, bf16[8,192,384]{2,1,0:T(8,128)(2,1)S(1)}, u32[]{:S(2)}, u32[]{:S(2)}) %collective-permute-start.23) | collective-permute-done | bytes 1179680 | tf_op jit(solution)/shard_map/ppermute | solution.py:965
  487.5 6.5 shard_map.209
  500.3 22.5 %shard_map.211 = (f32[416,768]{1,0:T(8,128)}, bf16[4,2,2,192,384]{4,3,2,1,0:T(8,128)(2,1)}, bf16[4,2,2,192,384]{4,3,2,1,0:T(8,128)(2,1)}, bf16[4,2,2,192,384]{4,...) custom-call(s32[4]{0:T(128)} %pad_add_fusion.me_ref.rest_0_, ...), custom_call_target="tpu_custom_call" | custom-call | flops 9814671360 | bytes 53403664 | tf_op jit(solution)/shard_map/pallas_call | solution.py:194
  529.0 21.6 %shard_map.213 = (f32[416,768]{1,0:T(8,128)}, bf16[4,2,2,192,384]{4,3,2,1,0:T(8,128)(2,1)}, bf16[4,2,2,192,384]{4,3,2,1,0:T(8,128)(2,1)}, f32[2,768]{1,0:T(2,128)}) custom-call(s32[4]{0:T(128)} %pad_add_fusion.me_ref.rest_0_, f32[416,768]{1,0:T(8,128)} %get-tuple-element.255.g_ref, f32[416,768]{1,0:T(8,128)} %get-tuple-element.178.x1_ref, ...), custom_call_target="tpu_custom_call" | custom-call | flops 3925868544 | bytes 51260944 | tf_op jit(solution)/shard_map/pallas_call | solution.py:194
  559.9 7.9 %shard_map.215 = (bf16[104,768]{1,0:T(8,128)(2,1)}, bf16[104,768]{1,0:T(8,128)(2,1)}, bf16[104,768]{1,0:T(8,128)(2,1)}, bf16[104,768]{1,0:T(8,128)(2,1)}, bf16[2...) custom-call(s32[4]{0:T(128)} %pad_add_fusion.me_ref.rest_0_, ...), custom_call_target="tpu_custom_call" | custom-call | flops 1962934272 | bytes 26787856 | tf_op jit(solution)/shard_map/pallas_call | solution.py:194
  567.7 22.9 %collective-permute-done.41.refs_15_ = bf16[2,192,384]{2,1,0:T(8,128)(2,1)S(1)} collective-permute-done((bf16[2,192,384]{2,1,0:T(8,128)(2,1)S(1)}, bf16[2,192,384]{2,1,0:T(8,128)(2,1)S(1)}, u32[]{:S(2)}, u32[]{:S(2)}) %collective-permute-start.41) | collective-permute-done | bytes 294944 | tf_op jit(solution)/shard_map/ppermute | solution.py:965
  604.5 18.3 %shard_map.217 = (bf16[104,768]{1,0:T(8,128)(2,1)}, bf16[104,768]{1,0:T(8,128)(2,1)}, bf16[104,768]{1,0:T(8,128)(2,1)}, bf16[104,768]{1,0:T(8,128)(2,1)}, bf16[3...) custom-call(s32[4]{0:T(128)} %pad_add_fusion.me_ref.rest_0_, ...), custom_call_target="tpu_custom_call" | custom-call | flops 2944401408 | bytes 27446800 | tf_op jit(solution)/shard_map/pallas_call | solution.py:194
  625.9 12.1 %shard_map.202 = f32[416,768]{1,0:T(8,128)} custom-call(f32[416,768]{1,0:T(8,128)} %get-tuple-element.191.x2_ref, bf16[17,2,768,384]{3,2,1,0:T(8,128)(2,1)} %bitcast.201, bf16[17,2,768,384]{3,2,1,0:T(8,128)(2,1)} %bitcast.202, f32[6,768]{1,0:T(8,128)} %squeeze.60.rest_1_.refs_8_.gb_ref.refs_6_), custom_call_target="tpu_custom_call" | custom-call | flops 3925868544 | bytes 42682368 | tf_op jit(solution)/shard_map/pallas_call | solution.py:194
  640.7 11.2 %collective-permute-done.42.refs_3_.refs_4_ = bf16[8,192,384]{2,1,0:T(8,128)(2,1)} collective-permute-done((bf16[8,192,384]{2,1,0:T(8,128)(2,1)}, bf16[8,192,384]{2,1,0:T(8,128)(2,1)}, u32[]{:S(2)}, u32[]{:S(2)}) %collective-permute-start.42) | collective-permute-done | bytes 1179680 | tf_op jit(solution)/shard_map/ppermute | solution.py:965
  661.4 6.5 shard_map.218
  682.0 10.1 %collective-permute-done.51.refs_3_.refs_6_ = bf16[6,192,384]{2,1,0:T(8,128)(2,1)S(1)} collective-permute-done((bf16[6,192,384]{2,1,0:T(8,128)(2,1)}, bf16[6,192,384]{2,1,0:T(8,128)(2,1)S(1)}, u32[]{:S(2)}, u32[]{:S(2)}) %collective-permute-start.51) | collective-permute-done | bytes 884768 | tf_op jit(solution)/shard_map/ppermute | solution.py:965
  725.0 17.6 %all-to-all-start.1 = ((bf16[4,5,48,384]{3,2,1,0:T(8,128)(2,1)}), bf16[4,5,48,384]{3,2,1,0:T(8,128)(2,1)S(1)}, u32[]{:S(2)}, u32[]{:S(2)}) async-start(bf16[4,5,48,384]{3,2,1,0:T(8,128)(2,1)} %shard_map.221), calls=%async_computation.1 | async-start | bytes 1474560 | tf_op jit(solution)/shard_map/all_to_all | solution.py:991
  747.3 15.4 %all-to-all-done.1 = bf16[4,5,48,384]{3,2,1,0:T(8,128)(2,1)S(1)} async-done(((bf16[4,5,48,384]{3,2,1,0:T(8,128)(2,1)}), bf16[4,5,48,384]{3,2,1,0:T(8,128)(2,1)S(1)}, u32[]{:S(2)}, u32[]{:S(2)}) %all-to-all-start.1) | async-done | bytes 737312 | tf_op jit(solution)/shard_map/all_to_all | solution.py:991
  (371 shorter events, 170.8 us)
Async XLA Ops:
  7.2 146.9 %all-gather.3.cloned.1.call-start = ((), (), s32[]{:S(2)}) async-start(), calls=%async_computation.8 | async-start | bytes 20680704 | tf_op jit(solution)/shard_map/all_gather | solution.py:825
  10.5 295.2 %all-gather.5.cloned.1.call-start = ((), (), s32[]{:S(2)}) async-start(), calls=%async_computation.9 | async-start | bytes 20680704 | tf_op jit(solution)/shard_map/all_gather | solution.py:825
  11.5 37.9 %collective-permute-start = (bf16[1,2,196,768]{3,1,2,0:T(2,128)(2,1)S(1)}, bf16[1,2,196,768]{3,1,2,0:T(2,128)(2,1)S(1)}, u32[]{:S(2)}, u32[]{:S(2)}) collective-permute-start(bf16[1,2,196,768]{3,1,2,0:T(2,128)(2,1)S(1)} %copy-done.63), channel_id=1, source_target_pairs={{0,0},{2,8},{4,2},{6,10},{8,4},{10,12},{12,6},{14,14},{16,16},{18,... | collective-permute-start | bytes 1806344 | tf_op jit(solution)/shard_map/ppermute | solution.py:775
  13.0 35.4 %all-to-all-start = ((f32[32,1,384]{2,1,0:T(1,128)}), f32[32,1,384]{2,1,0:T(1,128)S(1)}, u32[]{:S(2)}, u32[]{:S(2)}) async-start(f32[32,1,384]{2,1,0:T(1,128)} %broadcast_in_dim.17), calls=%async_computation | async-start | bytes 98304 | tf_op jit(solution)/shard_map/all_to_all | solution.py:1040
  21.8 649.2 %reduce-scatter.7.cloned.1.call-start = ((), (), s32[]{:S(2)}) async-start(), calls=%async_computation.11 | async-start | bytes 737280 | tf_op jit(solution)/shard_map/reduce_scatter | solution.py:994
  168.3 53.1 %collective-permute-start.14 = (bf16[1,2,196,768]{3,1,2,0:T(2,128)(2,1)S(1)}, bf16[1,2,196,768]{3,1,2,0:T(2,128)(2,1)S(1)}, u32[]{:S(2)}, u32[]{:S(2)}) collective-permute-start(bf16[1,2,196,768]{3,1,2,0:T(2,128)(2,1)S(1)} %copy-done.64), channel_id=1, source_target_pairs={{0,0},{2,8},{4,2},{6,10},{8,4},{10,12},{12,6},{14,14},{16,16},{18,... | collective-permute-start | bytes 1806344 | tf_op jit(solution)/shard_map/ppermute | solution.py:775
  219.6 86.1 %collective-permute-start.7 = (bf16[104,768]{1,0:T(8,128)(2,1)}, bf16[104,768]{1,0:T(8,128)(2,1)S(1)}, u32[]{:S(2)}, u32[]{:S(2)}) collective-permute-start(bf16[104,768]{1,0:T(8,128)(2,1)} %get-tuple-element.181), channel_id=1, source_target_pairs={{0,8},{2,10},{4,12},{6,14},{8,0},{10,2},{12,4},{14,6},{16,24},{18,... | collective-permute-start | bytes 479240 | tf_op jit(solution)/shard_map/ppermute | solution.py:797
  220.0 85.7 %collective-permute-start.8 = (bf16[104,768]{1,0:T(8,128)(2,1)}, bf16[104,768]{1,0:T(8,128)(2,1)S(1)}, u32[]{:S(2)}, u32[]{:S(2)}) collective-permute-start(bf16[104,768]{1,0:T(8,128)(2,1)} %get-tuple-element.182), channel_id=1, source_target_pairs={{0,2},{2,0},{4,6},{6,4},{8,10},{10,8},{12,14},{14,12},{16,18},{18,... | collective-permute-start | bytes 479240 | tf_op jit(solution)/shard_map/ppermute | solution.py:797
  220.0 85.7 %collective-permute-start.9 = (bf16[104,768]{1,0:T(8,128)(2,1)}, bf16[104,768]{1,0:T(8,128)(2,1)S(1)}, u32[]{:S(2)}, u32[]{:S(2)}) collective-permute-start(bf16[104,768]{1,0:T(8,128)(2,1)} %get-tuple-element.183), channel_id=1, source_target_pairs={{0,10},{2,8},{4,14},{6,12},{8,2},{10,0},{12,6},{14,4},{16,26},{18,... | collective-permute-start | bytes 479240 | tf_op jit(solution)/shard_map/ppermute | solution.py:797
  400.3 28.2 %collective-permute-start.20 = (bf16[8,192,384]{2,1,0:T(8,128)(2,1)}, bf16[8,192,384]{2,1,0:T(8,128)(2,1)S(1)}, u32[]{:S(2)}, u32[]{:S(2)}) collective-permute-start(bf16[8,192,384]{2,1,0:T(8,128)(2,1)} %get-tuple-element.209), channel_id=1, source_target_pairs={{0,16},{8,24},{16,0},{24,8},{1,17},{9,25},{17,1},{25,9},{2,18},{10... | collective-permute-start | bytes 3538952 | tf_op jit(solution)/shard_map/ppermute | solution.py:965
  455.0 30.8 %collective-permute-start.29 = (bf16[3,2,2,192,384]{4,3,2,1,0:T(8,128)(2,1)}, bf16[3,2,2,192,384]{4,3,2,1,0:T(8,128)(2,1)S(1)}, u32[]{:S(2)}, u32[]{:S(2)}) collective-permute-start(bf16[3,2,2,192,384]{4,3,2,1,0:T(8,128)(2,1)} %get-tuple-element.237), channel_id=1, source_target_pairs={{0,8},{8,0},{16,24},{24,16},{1,9},{9,1},{17,25},{25,17},{2,10},{10... | collective-permute-start | bytes 5308424 | tf_op jit(solution)/shard_map/ppermute | solution.py:965
  455.1 28.6 %collective-permute-start.23 = (bf16[8,192,384]{2,1,0:T(8,128)(2,1)}, bf16[8,192,384]{2,1,0:T(8,128)(2,1)S(1)}, u32[]{:S(2)}, u32[]{:S(2)}) collective-permute-start(bf16[8,192,384]{2,1,0:T(8,128)(2,1)} %get-tuple-element.226), channel_id=1, source_target_pairs={{0,1},{1,0},{2,3},{3,2},{4,5},{5,4},{6,7},{7,6},{8,9},{9,8},{10,11... | collective-permute-start | bytes 3538952 | tf_op jit(solution)/shard_map/ppermute | solution.py:965
  455.9 28.0 %collective-permute-start.24 = (bf16[8,192,384]{2,1,0:T(8,128)(2,1)S(1)}, bf16[8,192,384]{2,1,0:T(8,128)(2,1)S(1)}, u32[]{:S(2)}, u32[]{:S(2)}) collective-permute-start(bf16[8,192,384]{2,1,0:T(8,128)(2,1)S(1)} %copy-done.62), channel_id=1, source_target_pairs={{0,16},{8,24},{16,0},{24,8},{1,17},{9,25},{17,1},{25,9},{2,18},{10... | collective-permute-start | bytes 3538952 | tf_op jit(solution)/shard_map/ppermute | solution.py:965
  457.2 28.6 %collective-permute-start.28 = (bf16[2,2,2,192,384]{4,3,2,1,0:T(8,128)(2,1)S(1)}, bf16[2,2,2,192,384]{4,3,2,1,0:T(8,128)(2,1)S(1)}, u32[]{:S(2)}, u32[]{:S(2)}) collective-permute-start(bf16[2,2,2,192,384]{4,3,2,1,0:T(8,128)(2,1)S(1)} %copy-done.61), channel_id=1, source_target_pairs={{0,8},{8,0},{16,24},{24,16},{1,9},{9,1},{17,25},{25,17},{2,10},{10... | collective-permute-start | bytes 3538952 | tf_op jit(solution)/shard_map/ppermute | solution.py:965
  494.1 29.3 %collective-permute-start.30 = (bf16[6,192,384]{2,1,0:T(8,128)(2,1)}, bf16[6,192,384]{2,1,0:T(8,128)(2,1)S(1)}, u32[]{:S(2)}, u32[]{:S(2)}) collective-permute-start(bf16[6,192,384]{2,1,0:T(8,128)(2,1)} %get-tuple-element.247), channel_id=1, source_target_pairs={{0,1},{1,0},{2,3},{3,2},{4,5},{5,4},{6,7},{7,6},{8,9},{9,8},{10,11... | collective-permute-start | bytes 2654216 | tf_op jit(solution)/shard_map/ppermute | solution.py:965
  495.2 28.1 %collective-permute-start.31 = (bf16[8,192,384]{2,1,0:T(8,128)(2,1)}, bf16[8,192,384]{2,1,0:T(8,128)(2,1)S(1)}, u32[]{:S(2)}, u32[]{:S(2)}) collective-permute-start(bf16[8,192,384]{2,1,0:T(8,128)(2,1)} %get-tuple-element.248), channel_id=1, source_target_pairs={{0,16},{8,24},{16,0},{24,8},{1,17},{9,25},{17,1},{25,9},{2,18},{10... | collective-permute-start | bytes 3538952 | tf_op jit(solution)/shard_map/ppermute | solution.py:965
  522.8 28.0 %collective-permute-start.32 = (bf16[4,2,2,192,384]{4,3,2,1,0:T(8,128)(2,1)}, bf16[4,2,2,192,384]{4,3,2,1,0:T(8,128)(2,1)}, u32[]{:S(2)}, u32[]{:S(2)}) collective-permute-start(bf16[4,2,2,192,384]{4,3,2,1,0:T(8,128)(2,1)} %get-tuple-element.260), channel_id=1, source_target_pairs={{0,8},{8,0},{16,24},{24,16},{1,9},{9,1},{17,25},{25,17},{2,10},{10... | collective-permute-start | bytes 7077896 | tf_op jit(solution)/shard_map/ppermute | solution.py:965
  522.9 28.0 %collective-permute-start.33 = (bf16[4,2,2,192,384]{4,3,2,1,0:T(8,128)(2,1)}, bf16[4,2,2,192,384]{4,3,2,1,0:T(8,128)(2,1)}, u32[]{:S(2)}, u32[]{:S(2)}) collective-permute-start(bf16[4,2,2,192,384]{4,3,2,1,0:T(8,128)(2,1)} %get-tuple-element.262), channel_id=1, source_target_pairs={{0,8},{8,0},{16,24},{24,16},{1,9},{9,1},{17,25},{25,17},{2,10},{10... | collective-permute-start | bytes 7077896 | tf_op jit(solution)/shard_map/ppermute | solution.py:965
  529.0 152.1 %reduce-scatter.11.cloned.1.call-start = ((), (), s32[]{:S(2)}) async-start(), calls=%async_computation.13 | async-start | bytes 1474560 | tf_op jit(solution)/shard_map/reduce_scatter | solution.py:994
  550.6 44.7 %collective-permute-start.39 = (bf16[4,2,2,192,384]{4,3,2,1,0:T(8,128)(2,1)}, bf16[4,2,2,192,384]{4,3,2,1,0:T(8,128)(2,1)S(1)}, u32[]{:S(2)}, u32[]{:S(2)}) collective-permute-start(bf16[4,2,2,192,384]{4,3,2,1,0:T(8,128)(2,1)} %get-tuple-element.275), channel_id=1, source_target_pairs={{0,8},{8,0},{16,24},{24,16},{1,9},{9,1},{17,25},{25,17},{2,10},{10... | collective-permute-start | bytes 7077896 | tf_op jit(solution)/shard_map/ppermute | solution.py:965
  550.8 155.6 %reduce-scatter.5.cloned.1.call-start = ((), (), s32[]{:S(2)}) async-start(), calls=%async_computation.10 | async-start | bytes 921600 | tf_op jit(solution)/shard_map/reduce_scatter | solution.py:994
  555.7 39.8 %collective-permute-start.37 = (bf16[8,192,384]{2,1,0:T(8,128)(2,1)}, bf16[8,192,384]{2,1,0:T(8,128)(2,1)S(1)}, u32[]{:S(2)}, u32[]{:S(2)}) collective-permute-start(bf16[8,192,384]{2,1,0:T(8,128)(2,1)} %get-tuple-element.272), channel_id=1, source_target_pairs={{0,16},{8,24},{16,0},{24,8},{1,17},{9,25},{17,1},{25,9},{2,18},{10... | collective-permute-start | bytes 3538952 | tf_op jit(solution)/shard_map/ppermute | solution.py:965
  557.1 38.4 %collective-permute-start.38 = (bf16[8,192,384]{2,1,0:T(8,128)(2,1)}, bf16[8,192,384]{2,1,0:T(8,128)(2,1)S(1)}, u32[]{:S(2)}, u32[]{:S(2)}) collective-permute-start(bf16[8,192,384]{2,1,0:T(8,128)(2,1)} %get-tuple-element.273), channel_id=1, source_target_pairs={{0,1},{1,0},{2,3},{3,2},{4,5},{5,4},{6,7},{7,6},{8,9},{9,8},{10,11... | collective-permute-start | bytes 3538952 | tf_op jit(solution)/shard_map/ppermute | solution.py:965
  558.0 36.8 %collective-permute-start.40 = (bf16[3,192,384]{2,1,0:T(8,128)(2,1)S(1)}, bf16[3,192,384]{2,1,0:T(8,128)(2,1)S(1)}, u32[]{:S(2)}, u32[]{:S(2)}) collective-permute-start(bf16[3,192,384]{2,1,0:T(8,128)(2,1)S(1)} %copy-done.65), channel_id=1, source_target_pairs={{0,1},{1,0},{2,3},{3,2},{4,5},{5,4},{6,7},{7,6},{8,9},{9,8},{10,11... | collective-permute-start | bytes 1327112 | tf_op jit(solution)/shard_map/ppermute | solution.py:965
  559.1 31.5 %collective-permute-start.41 = (bf16[2,192,384]{2,1,0:T(8,128)(2,1)S(1)}, bf16[2,192,384]{2,1,0:T(8,128)(2,1)S(1)}, u32[]{:S(2)}, u32[]{:S(2)}) collective-permute-start(bf16[2,192,384]{2,1,0:T(8,128)(2,1)S(1)} %copy-done.66), channel_id=1, source_target_pairs={{0,16},{8,24},{16,0},{24,8},{1,17},{9,25},{17,1},{25,9},{2,18},{10... | collective-permute-start | bytes 884744 | tf_op jit(solution)/shard_map/ppermute | solution.py:965
  622.7 37.1 %collective-permute-start.48 = (bf16[3,2,2,192,384]{4,3,2,1,0:T(8,128)(2,1)}, bf16[3,2,2,192,384]{4,3,2,1,0:T(8,128)(2,1)S(1)}, u32[]{:S(2)}, u32[]{:S(2)}) collective-permute-start(bf16[3,2,2,192,384]{4,3,2,1,0:T(8,128)(2,1)} %get-tuple-element.303), channel_id=1, source_target_pairs={{0,8},{8,0},{16,24},{24,16},{1,9},{9,1},{17,25},{25,17},{2,10},{10... | collective-permute-start | bytes 5308424 | tf_op jit(solution)/shard_map/ppermute | solution.py:965
  623.7 28.3 %collective-permute-start.42 = (bf16[8,192,384]{2,1,0:T(8,128)(2,1)}, bf16[8,192,384]{2,1,0:T(8,128)(2,1)}, u32[]{:S(2)}, u32[]{:S(2)}) collective-permute-start(bf16[8,192,384]{2,1,0:T(8,128)(2,1)} %get-tuple-element.292), channel_id=1, source_target_pairs={{0,1},{1,0},{2,3},{3,2},{4,5},{5,4},{6,7},{7,6},{8,9},{9,8},{10,11... | collective-permute-start | bytes 3538952 | tf_op jit(solution)/shard_map/ppermute | solution.py:965
  624.6 28.0 %collective-permute-start.43 = (bf16[8,192,384]{2,1,0:T(8,128)(2,1)}, bf16[8,192,384]{2,1,0:T(8,128)(2,1)}, u32[]{:S(2)}, u32[]{:S(2)}) collective-permute-start(bf16[8,192,384]{2,1,0:T(8,128)(2,1)} %get-tuple-element.293), channel_id=1, source_target_pairs={{0,16},{8,24},{16,0},{24,8},{1,17},{9,25},{17,1},{25,9},{2,18},{10... | collective-permute-start | bytes 3538952 | tf_op jit(solution)/shard_map/ppermute | solution.py:965
  625.8 34.0 %collective-permute-start.47 = (bf16[2,2,2,192,384]{4,3,2,1,0:T(8,128)(2,1)}, bf16[2,2,2,192,384]{4,3,2,1,0:T(8,128)(2,1)S(1)}, u32[]{:S(2)}, u32[]{:S(2)}) collective-permute-start(bf16[2,2,2,192,384]{4,3,2,1,0:T(8,128)(2,1)} %get-tuple-element.301), channel_id=1, source_target_pairs={{0,8},{8,0},{16,24},{24,16},{1,9},{9,1},{17,25},{25,17},{2,10},{10... | collective-permute-start | bytes 3538952 | tf_op jit(solution)/shard_map/ppermute | solution.py:965
  625.9 118.4 %reduce-scatter.9.cloned.1.call-start = ((), (), s32[]{:S(2)}) async-start(), calls=%async_computation.12 | async-start | bytes 1474560 | tf_op jit(solution)/shard_map/reduce_scatter | solution.py:994
  667.9 29.3 %collective-permute-start.50 = (bf16[8,192,384]{2,1,0:T(8,128)(2,1)}, bf16[8,192,384]{2,1,0:T(8,128)(2,1)S(1)}, u32[]{:S(2)}, u32[]{:S(2)}) collective-permute-start(bf16[8,192,384]{2,1,0:T(8,128)(2,1)} %get-tuple-element.312), channel_id=1, source_target_pairs={{0,16},{8,24},{16,0},{24,8},{1,17},{9,25},{17,1},{25,9},{2,18},{10... | collective-permute-start | bytes 3538952 | tf_op jit(solution)/shard_map/ppermute | solution.py:965
  725.0 37.7 %all-to-all-start.1 = ((bf16[4,5,48,384]{3,2,1,0:T(8,128)(2,1)}), bf16[4,5,48,384]{3,2,1,0:T(8,128)(2,1)S(1)}, u32[]{:S(2)}, u32[]{:S(2)}) async-start(bf16[4,5,48,384]{3,2,1,0:T(8,128)(2,1)} %shard_map.221), calls=%async_computation.1 | async-start | bytes 1474560 | tf_op jit(solution)/shard_map/all_to_all | solution.py:991
  (102 other events, 1039.0 us)
Sparse Core Ops, SparseCore 0:
  11.7 142.3 all-gather.2
  157.2 148.4 all-gather.4
  529.1 20.2 reduce-scatter.6
  551.5 27.5 reduce-scatter.10
  626.0 21.2 reduce-scatter.4
  672.1 28.1 reduce-scatter.8

commit v8 on v7

--- a/solution.py
+++ b/solution.py
@@ -388,14 +388,9 @@
     shares = w.shape[1]
     per_share = (w.shape[0] - 9) // 2
     steps = shares * per_share
-    last = gb_next is None
-
-    def body(x2_ref, wi_ref, wo_ref, gb_ref, *rest):
-        if last:
-            x3_ref, a3_ref = rest
-        else:
-            me_ref, gn_ref, x3_ref = rest[:3]
-            send_refs, a3_ref = rest[3:-1], rest[-1]
+
+    def body(x2_ref, wi_ref, wo_ref, gb_ref, me_ref, gn_ref, x3_ref, *rest):
+        send_refs, a3_ref = rest[:-1], rest[-1]
         j = pl.program_id(0)
 
         @pl.when(j == 0)
@@ -407,13 +402,11 @@
         act = (0.5 * hid * (1.0 + lax.erf(hid * HALF_ROOT))).astype(BF16)
         x3_ref[...] += nt(act, wo_ref[0, 0])
 
-        if not last:
-
-            @pl.when(j == steps - 1)
-            def _():
-                a = norm_rounded(x3_ref[...], gn_ref[0:1], gn_ref[3:4])
-                for k in range(rows.ways):
-                    send_refs[k][...] = nn(rows.to_time(k, me_ref[3]), a).astype(BF16)
+        @pl.when(j == steps - 1)
+        def _():
+            a = norm_rounded(x3_ref[...], gn_ref[0:1], gn_ref[3:4])
+            for k in range(rows.ways):
+                send_refs[k][...] = nn(rows.to_time(k, me_ref[3]), a).astype(BF16)
 
     ins = [
         whole(x2.shape),
@@ -421,25 +414,25 @@
         ff_slab(8 + per_share, per_share, d, width),
         whole(gb.shape),
     ]
-    outs = [made((t, d), F32)]
-    args = [x2, w, w, gb]
-    if not last:
-        ins += [SCALARS, whole(gb_next.shape)]
-        outs += rows.chunks(d)
-        args += [me, gb_next]
+    ins += [SCALARS, whole(gb_next.shape)]
+    outs = [made((t, d), F32)] + rows.chunks(d)
+    args = (x2, w, w, gb, me, gb_next)
     return call(
-        body, (steps,), ins, outs, [pltpu.VMEM((t, d), BF16)], tuple(args), flops=4 * t * d * width * steps
-    )
-
-
-def mlp_backward(rows, grad, x2, w, gb, me, halves):
+        body, (steps,), ins, outs, [pltpu.VMEM((t, d), BF16)], args, flops=4 * t * d * width * steps
+    )
+
+
+def mlp_backward(rows, grad, x2, w, gb, me, halves, with_output):
     t, d = x2.shape
     width = w.shape[3]
     shares = w.shape[1]
     per_share = (w.shape[0] - 9) // 2
     steps = shares * per_share
 
-    def body(me_ref, g_ref, x2_ref, wi_ref, wo_ref, gb_ref, go_ref, ki_ref, si_ref, ko_ref, so_ref, sums_ref, a3_ref, a3t_ref, e3_ref, e3t_ref, u_ref, room_ref):
+    def body(me_ref, g_ref, x2_ref, wi_ref, wo_ref, gb_ref, go_ref, ki_ref, si_ref, ko_ref, so_ref, sums_ref, *rest):
+        if with_output:
+            x3_ref, *rest = rest
+        a3_ref, a3t_ref, e3_ref, e3t_ref, u_ref, room_ref = rest
         j = pl.program_id(0)
 
         @pl.when(j == 0)
@@ -452,6 +445,8 @@
             e3_ref[...] = g.astype(BF16)
             e3t_ref[...] = g.T.astype(BF16)
             u_ref[...] = jnp.zeros((t, d), F32)
+            if with_output:
+                x3_ref[...] = x2_ref[...]
 
         hid = nn(a3_ref[...], wi_ref[0, 0])
         phi = 0.5 * (1.0 + lax.erf(hid * HALF_ROOT))
@@ -461,6 +456,8 @@
         split_rows(nn(e3t_ref[...], act), ko_ref, so_ref, (0, 0), room_ref, me_ref)
         split_rows(nn(a3t_ref[...], dhid), ki_ref, si_ref, (0, 0), room_ref, me_ref)
         u_ref[...] += nt(dhid, wi_ref[0, 0])
+        if with_output:
+            x3_ref[...] += nt(act, wo_ref[0, 0])
 
         @pl.when(j == steps - 1)
         def _():
@@ -475,7 +472,7 @@
             (per_share, shares), (1, 1), lambda j: (j % per_share, j // per_share)
         )
     ]
-    grad, ki, si, ko, so, sums = call(
+    grad, ki, si, ko, so, sums, *x3 = call(
         body,
         (steps,),
         [
@@ -486,7 +483,7 @@
             ff_slab(8 + per_share, per_share, d, width),
             whole(gb.shape),
         ],
-        [made((t, d), F32), *slab_outs, made((2, d), F32)],
+        [made((t, d), F32), *slab_outs, made((2, d), F32)] + [made((t, d), F32)] * with_output,
         [
             pltpu.VMEM((t, d), BF16),
             pltpu.VMEM((d, t), BF16),
@@ -498,7 +495,7 @@
         (me, grad, x2, w, w, gb),
         flops=10 * t * d * width * steps,
     )
-    return grad, [(ki, si), (ko, so)], sums
+    return grad, [(ki, si), (ko, so)], sums, x3
 
 
 def space_backward(rows, grad, x1, qkv, o2, logs, w, gb, me, halves):
@@ -671,7 +668,8 @@
         do_refs, refs = refs[: rows.ways], refs[rows.ways :]
         a_ref, qkv_ref, log_ref, w_ref = refs[:4]
         out_refs, refs = refs[4 : 4 + rows.ways], refs[4 + rows.ways :]
-        keep_ref, send_ref, bias_ref, dqkv_ref, at_ref, u_ref, room_ref, do_ref = refs
+        half_refs, refs = refs[:6], refs[6:]
+        bias_ref, dqkv_ref, at_ref, u_ref, room_ref, do_ref = refs
         h = pl.program_id(0)
 
         @pl.when(h == 0)
@@ -701,9 +699,8 @@
                 dqkv_ref[part, :, lanes] = grads[part]
 
         for part in range(3):
-            split_rows(
-                nn(at_ref[...], dqkv_ref[part]), keep_ref, send_ref, (part, 0), room_ref, me_ref
-            )
+            value = nn(at_ref[...], dqkv_ref[part])
+            split_rows(value, half_refs[2 * part], half_refs[2 * part + 1], (0, 0), room_ref, me_ref)
             u_ref[...] += nt(dqkv_ref[part], w_ref[part, 0])
 
         @pl.when(h == shares - 1)
@@ -724,7 +721,7 @@
         ],
         [
             *rows.chunks(d),
-            *halves.array((3, shares), (3, 1), lambda h: (0, h)),
+            *(one for _ in range(3) for one in halves.array((1, shares), (1, 1), lambda h: (0, h))),
         ],
         [
             pltpu.VMEM((t, t), F32),
@@ -737,7 +734,8 @@
         (me, *do1, a, qkv, logs, w),
         flops=2 * t * d * d * 6,
     )
-    return got[: rows.ways], tuple(got[rows.ways :])
+    parts = got[rows.ways :]
+    return got[: rows.ways], [tuple(parts[i : i + 2]) for i in (0, 2, 4)]
 
 
 def first_norm_back(rows, back, x, grad, gb, me):
@@ -1112,9 +1110,6 @@
         kept.append((x, a1, qkv1, log1, o1, y1, x1, qkv2, o2, log2, x2))
         if l + 1 < layers:
             x, *send = mlp_forward(rows, x2, w, gb[l], gb[l + 1], me)
-        else:
-            (x,) = mlp_forward(rows, x2, w, gb[l], None, me)
-    output = go_back(from_rows(x.astype(BF16)))
 
     grad = as_rows(go_home(cotangent))
     norm_rows = [None] * layers
@@ -1124,7 +1119,9 @@
     for l in reversed(range(layers)):
         w = weights[l]
         x, a1, qkv1, log1, o1, y1, x1, qkv2, o2, log2, x2 = kept[l]
-        grad, g_ff, s3 = mlp_backward(rows, grad, x2, w, gb[l], me, halves)
+        grad, g_ff, s3, x3 = mlp_backward(rows, grad, x2, w, gb[l], me, halves, l + 1 == layers)
+        if x3:
+            output = go_back(from_rows(x3[0].astype(BF16)))
         if quick:
             ff = pieces_of(g_ff)
             if late:
@@ -1134,7 +1131,7 @@
         grad, g_space, s2 = space_backward(rows, grad, x1, qkv2, o2, log2, w, gb[l], me, halves)
         if quick:
             space = pieces_of([g_space])
-            grad = move(grad, ff, me)
+            grad, output = move((grad, output), ff, me)
         do1, g_out = middle_backward(rows, grad, y1, o1, w, mixes[l], me, halves, shards)
         do1 = swap_places(do1)
         if quick:
@@ -1144,7 +1141,7 @@
             da1 = settle(da1, ff + space)
         da1 = swap_places(da1)
         if quick:
-            rest = pieces_of([g_out, g_time])
+            rest = pieces_of([g_out] + g_time)
             da1 = move(da1, ff + space + rest, me)
             late = space + rest
         grad, s1 = first_norm_back(rows, da1, x, grad, gb[l], me)
@@ -1152,12 +1149,12 @@
         if quick:
             summed[l] = ff + space + rest
         else:
-            summed[l] = [reduce_plain(g_ff + [g_space, g_out, g_time], clip & 1)]
+            summed[l] = [reduce_plain(g_ff + [g_space, g_out] + g_time, clip & 1)]
     if quick:
         move((), late, me, True)
         move((), rest, me, True)
         summed = [[p.result for p in some] for some in summed]
-    cuts = (2 * g_ff[0][0].shape[0], g_space[0].shape[0], g_out[0].shape[0], g_time[0].shape[0])
+    cuts = (2 * g_ff[0][0].shape[0], g_space[0].shape[0], g_out[0].shape[0], len(g_time))
     results = []
     for some in summed:
         slabs_of = jnp.concatenate(some, axis=0)

time: 782 us -> 750 us (0.959)
  waiting for transfers between devices: 344 us -> 300 us
  starting transfers between devices: 76.1 us -> 95.7 us
  Pallas kernels: 287 us -> 278 us
    ppermute x26 -> x30, waiting for transfers between devices: 104 us -> 59.1 us  [cross(): return lax.ppermute(a, axis, [(i, i ^ 1 << bit) for i in range(size)])]
    ppermute x24, starting transfers between devices: 19.2 us -> 36.4 us  [swap_places(): got.append(lax.ppermute(chunks[k], ('clip', 'seq'), pairs))]
    pallas_call x19 -> x18, Pallas kernels: 241 us -> 232 us  [call(): pl.pallas_call(body, out_shape=[shape for shape, _ in outs], grid=grid, i...]
    ppermute x26 -> x30, starting transfers between devices: 21.2 us -> 27.5 us  [cross(): return lax.ppermute(a, axis, [(i, i ^ 1 << bit) for i in range(size)])]
    unnamed x156 -> x166, local copies, waits for them, and re-layouts: 21.8 us -> 23.1 us
  transfers between devices with their start and end apart: 64 -> 68, of which waited for: 22 -> 20; matrix products, arithmetic and copies ran while one was open for 4% -> 4% of each run, Pallas kernels for 28% -> 30%
where the time goes in v8:
time: 750 us; the launch traced here: 741 us
  waiting for transfers between devices  300 us (40%)
  Pallas kernels  278 us (37%)
  starting transfers between devices  95.7 us (13%)
  local copies, waits for them, and re-layouts  37.4 us (5%)
  between operations  15.7 us (2%)
  other arithmetic  15.4 us (2%)
    pallas_call x18, Pallas kernels, call(): pl.pallas_call(body, out_shape=[shape for shape, _ in outs], grid=grid, i...  232 us
    all_gather x2, waiting for transfers between devices, gather_slabs(): full = lax.all_gather(pack, ('head', 'clip', 'seq'), axis=1, tiled=True)  157 us
    ppermute x30, waiting for transfers between devices, cross(): return lax.ppermute(a, axis, [(i, i ^ 1 << bit) for i in range(size)])  59.1 us
    pallas_call x9, Pallas kernels, fold(): pl.pallas_call(body, out_shape=[jax.ShapeDtypeStruct(shape, BF16) for sha...  45.6 us
    ppermute x24, waiting for transfers between devices, swap_places(): got.append(lax.ppermute(chunks[k], ('clip', 'seq'), pairs))  41.9 us
    ppermute x24, starting transfers between devices, swap_places(): got.append(lax.ppermute(chunks[k], ('clip', 'seq'), pairs))  36.4 us
    ppermute x30, starting transfers between devices, cross(): return lax.ppermute(a, axis, [(i, i ^ 1 << bit) for i in range(size)])  27.5 us
    all_to_all x1, waiting for transfers between devices, gather_norms(): lax.all_to_all(jnp.broadcast_to(padded, (count, width)), ALL, split_axis=...  25.9 us
  transfers between devices with their start and end apart: 68, of which 20 were waited for; matrix products, arithmetic and copies ran while one was open for 4% of the time, Pallas kernels for 30%

profile of v8, /device:TPU:0, one launch (start us, length us, event | category | flops | bytes accessed | tf_op | source)
XLA Modules:
  0.0 741.4 jit_solution(16154229267402344800)
XLA Ops:
  13.0 8.8 %all-to-all-start = ((f32[32,1,384]{2,1,0:T(1,128)}), f32[32,1,384]{2,1,0:T(1,128)S(1)}, u32[]{:S(2)}, u32[]{:S(2)}) async-start(f32[32,1,384]{2,1,0:T(1,128)} %broadcast_in_dim.17), calls=%async_computation | async-start | bytes 98304 | tf_op jit(solution)/shard_map/all_to_all | solution.py:1038
  22.5 25.9 %all-to-all-done = f32[32,1,384]{2,1,0:T(1,128)S(1)} async-done(((f32[32,1,384]{2,1,0:T(1,128)}), f32[32,1,384]{2,1,0:T(1,128)S(1)}, u32[]{:S(2)}, u32[]{:S(2)}) %all-to-all-start) | async-done | bytes 49184 | tf_op jit(solution)/shard_map/all_to_all | solution.py:1038
  55.5 14.3 %collective-permute-done.3.refs_2_ = bf16[104,768]{1,0:T(8,128)(2,1)S(1)} collective-permute-done((bf16[104,768]{1,0:T(8,128)(2,1)}, bf16[104,768]{1,0:T(8,128)(2,1)S(1)}, u32[]{:S(2)}, u32[]{:S(2)}) %collective-permute-start.3) | collective-permute-done | bytes 159776 | tf_op jit(solution)/shard_map/ppermute | solution.py:795
  69.8 11.5 %collective-permute-done.4.refs_3_ = bf16[104,768]{1,0:T(8,128)(2,1)S(1)} collective-permute-done((bf16[104,768]{1,0:T(8,128)(2,1)}, bf16[104,768]{1,0:T(8,128)(2,1)S(1)}, u32[]{:S(2)}, u32[]{:S(2)}) %collective-permute-start.4) | collective-permute-done | bytes 159776 | tf_op jit(solution)/shard_map/ppermute | solution.py:795
  81.2 72.9 %all-gather.3.cloned.1.call-done = bf16[17,1536,384]{2,1,0:T(8,128)(2,1)} async-done(((bf16[17,48,384]{2,1,0:T(8,128)(2,1)}), bf16[17,1536,384]{2,1,0:T(8,128)(2,1)}) %all-gather.3.cloned.1.call-update) | async-done | bytes 20054032 | tf_op jit(solution)/shard_map/all_gather | solution.py:823
  154.1 12.3 %shard_map.195 = (bf16[416,768]{1,0:T(8,128)(2,1)}, bf16[3,416,768]{2,1,0:T(8,128)(2,1)}, f32[2,3,2,416]{3,2,1,0:T(2,128)}, bf16[104,768]{1,0:T(8,128)(2,1)}, bf...) custom-call(bf16[104,768]{1,0:T(8,128)(2,1)} %get-tuple-element.180.refs_0_, ...), custom_call_target="tpu_custom_call" | custom-call | flops 1472200704 | bytes 23907840 | tf_op jit(solution)/shard_map/pallas_call | solution.py:194
  173.4 6.7 collective-permute-done.6.refs_2_
  186.9 9.4 %shard_map.196 = (bf16[416,768]{1,0:T(8,128)(2,1)}, bf16[416,768]{1,0:T(8,128)(2,1)}, f32[416,768]{1,0:T(8,128)}, bf16[3,416,768]{2,1,0:T(8,128)(2,1)}) custom-call(s32[4]{0:T(128)} %pad_add_fusion.me_ref, bf16[104,768]{1,0:T(8,128)(2,1)} %get-tuple-element.184.refs_0_, bf16[104,768]{1,0:T(8,128)(2,1)} %copy-done.55, bf16[104,768]{1,0:T(8,128)(2,1)} %copy-done.56, ...), custom_call_target="tpu_custom_call" | custom-call | flops 2453667840 | bytes 47695888 | tf_op jit(solution)/shard_map/pallas_call | solution.py:194
  196.3 10.1 %shard_map.197 = (bf16[416,768]{1,0:T(8,128)(2,1)}, f32[416,768]{1,0:T(8,128)}, f32[2,3,2,2,208]{4,3,2,1,0:T(2,128)}) custom-call(bf16[3,416,768]{2,1,0:T(8,128)(2,1)} %get-tuple-element.188.qkv_ref, f32[416,768]{1,0:T(8,128)} %get-tuple-element.189.x1_ref, bf16[17,2,768,384]{3,2,1,0:T(8,128)(2,1)} %bitcast.194), custom_call_target="tpu_custom_call" | custom-call | flops 490733568 | bytes 25185792 | tf_op jit(solution)/shard_map/pallas_call | solution.py:194
  206.4 13.3 %shard_map.198 = (f32[416,768]{1,0:T(8,128)}, bf16[104,768]{1,0:T(8,128)(2,1)}, bf16[104,768]{1,0:T(8,128)(2,1)}, bf16[104,768]{1,0:T(8,128)(2,1)}, bf16[104,768]{1,0:T(8,128)(2,1)}) custom-call(f32[416,768]{1,0:T(8,128)} %get-tuple-element.190.x2_ref, bf16[17,2,768,384]{3,2,1,0:T(8,128)(2,1)} %bitcast.195, bf16[17,2,768,384]{3,2,1,0:T(8,128)(2,1)} %bitcast.196, ...), custom_call_target="tpu_custom_call" | custom-call | flops 3925868544 | bytes 43339792 | tf_op jit(solution)/shard_map/pallas_call | solution.py:194
  221.7 84.1 %all-gather.5.cloned.1.call-done = bf16[17,1536,384]{2,1,0:T(8,128)(2,1)} async-done(((bf16[17,48,384]{2,1,0:T(8,128)(2,1)}), bf16[17,1536,384]{2,1,0:T(8,128)(2,1)}) %all-gather.5.cloned.1.call-update) | async-done | bytes 20054032 | tf_op jit(solution)/shard_map/all_gather | solution.py:823
  306.6 12.2 %shard_map.199 = (bf16[416,768]{1,0:T(8,128)(2,1)}, bf16[3,416,768]{2,1,0:T(8,128)(2,1)}, f32[2,3,2,416]{3,2,1,0:T(2,128)}, bf16[104,768]{1,0:T(8,128)(2,1)}, bf...) custom-call(bf16[104,768]{1,0:T(8,128)(2,1)} %get-tuple-element.191.refs_0_, ...), custom_call_target="tpu_custom_call" | custom-call | flops 1472200704 | bytes 23907840 | tf_op jit(solution)/shard_map/pallas_call | solution.py:194
  329.0 9.4 %shard_map.200 = (bf16[416,768]{1,0:T(8,128)(2,1)}, bf16[416,768]{1,0:T(8,128)(2,1)}, f32[416,768]{1,0:T(8,128)}, bf16[3,416,768]{2,1,0:T(8,128)(2,1)}) custom-call(s32[4]{0:T(128)} %pad_add_fusion.me_ref, bf16[104,768]{1,0:T(8,128)(2,1)} %get-tuple-element.195.refs_0_, bf16[104,768]{1,0:T(8,128)(2,1)} %copy-done.58, bf16[104,768]{1,0:T(8,128)(2,1)} %copy-done.59, ...), custom_call_target="tpu_custom_call" | custom-call | flops 2453667840 | bytes 47695888 | tf_op jit(solution)/shard_map/pallas_call | solution.py:194
  338.3 9.9 %shard_map.201 = (bf16[416,768]{1,0:T(8,128)(2,1)}, f32[416,768]{1,0:T(8,128)}, f32[2,3,2,2,208]{4,3,2,1,0:T(2,128)}) custom-call(bf16[3,416,768]{2,1,0:T(8,128)(2,1)} %get-tuple-element.200.qkv_ref, f32[416,768]{1,0:T(8,128)} %get-tuple-element.201.x1_ref, bf16[17,2,768,384]{3,2,1,0:T(8,128)(2,1)} %bitcast.206), custom_call_target="tpu_custom_call" | custom-call | flops 490733568 | bytes 25185792 | tf_op jit(solution)/shard_map/pallas_call | solution.py:194
  348.3 25.7 %shard_map.202 = (f32[416,768]{1,0:T(8,128)}, bf16[4,2,2,192,384]{4,3,2,1,0:T(8,128)(2,1)}, bf16[4,2,2,192,384]{4,3,2,1,0:T(8,128)(2,1)}, bf16[4,2,2,192,384]{4,...) custom-call(s32[4]{0:T(128)} %pad_add_fusion.me_ref, ...), custom_call_target="tpu_custom_call" | custom-call | flops 9814671360 | bytes 54681616 | tf_op jit(solution)/shard_map/pallas_call | solution.py:194
  374.7 21.6 %shard_map.203 = (f32[416,768]{1,0:T(8,128)}, bf16[4,2,2,192,384]{4,3,2,1,0:T(8,128)(2,1)}, bf16[4,2,2,192,384]{4,3,2,1,0:T(8,128)(2,1)}, f32[2,768]{1,0:T(2,128)}) custom-call(s32[4]{0:T(128)} %pad_add_fusion.me_ref, f32[416,768]{1,0:T(8,128)} %get-tuple-element.203.g_ref, f32[416,768]{1,0:T(8,128)} %get-tuple-element.201.x1_ref, ...), custom_call_target="tpu_custom_call" | custom-call | flops 3925868544 | bytes 51260944 | tf_op jit(solution)/shard_map/pallas_call | solution.py:194
  408.3 7.8 %shard_map.205 = (bf16[104,768]{1,0:T(8,128)(2,1)}, bf16[104,768]{1,0:T(8,128)(2,1)}, bf16[104,768]{1,0:T(8,128)(2,1)}, bf16[104,768]{1,0:T(8,128)(2,1)}, bf16[2...) custom-call(s32[4]{0:T(128)} %pad_add_fusion.me_ref, f32[416,768]{1,0:T(8,128)} %get-tuple-element.214.g_ref.refs_5_, ...), custom_call_target="tpu_custom_call" | custom-call | flops 1962934272 | bytes 26787856 | tf_op jit(solution)/shard_map/pallas_call | solution.py:194
  416.1 9.0 %collective-permute-start.17 = (bf16[104,768]{1,0:T(8,128)(2,1)}, bf16[104,768]{1,0:T(8,128)(2,1)S(1)}, u32[]{:S(2)}, u32[]{:S(2)}) collective-permute-start(bf16[104,768]{1,0:T(8,128)(2,1)} %get-tuple-element.218), channel_id=1, source_target_pairs={{0,8},{2,10},{4,12},{6,14},{8,0},{10,2},{12,4},{14,6},{16,24},{18,... | collective-permute-start | bytes 479240 | tf_op jit(solution)/shard_map/ppermute | solution.py:795
  436.8 7.7 %collective-permute-start.28 = (bf16[2,2,2,192,384]{4,3,2,1,0:T(8,128)(2,1)S(1)}, bf16[2,2,2,192,384]{4,3,2,1,0:T(8,128)(2,1)S(1)}, u32[]{:S(2)}, u32[]{:S(2)}) collective-permute-start(bf16[2,2,2,192,384]{4,3,2,1,0:T(8,128)(2,1)S(1)} %copy-done.70), channel_id=1, source_target_pairs={{0,8},{8,0},{16,24},{24,16},{1,9},{9,1},{17,25},{25,17},{2,10},{10... | collective-permute-start | bytes 3538952 | tf_op jit(solution)/shard_map/ppermute | solution.py:963
  444.4 18.3 %shard_map.207 = (bf16[104,768]{1,0:T(8,128)(2,1)}, bf16[104,768]{1,0:T(8,128)(2,1)}, bf16[104,768]{1,0:T(8,128)(2,1)}, bf16[104,768]{1,0:T(8,128)(2,1)}, bf16[1...) custom-call(s32[4]{0:T(128)} %pad_add_fusion.me_ref, ...), custom_call_target="tpu_custom_call" | custom-call | flops 2944401408 | bytes 27446800 | tf_op jit(solution)/shard_map/pallas_call | solution.py:194
  464.3 13.9 %collective-permute-start.26 = (bf16[104,768]{1,0:T(8,128)(2,1)}, bf16[104,768]{1,0:T(8,128)(2,1)S(1)}, u32[]{:S(2)}, u32[]{:S(2)}) collective-permute-start(bf16[104,768]{1,0:T(8,128)(2,1)} %get-tuple-element.242), channel_id=1, source_target_pairs={{0,2},{2,0},{4,6},{6,4},{8,10},{10,8},{12,14},{14,12},{16,18},{18,... | collective-permute-start | bytes 479240 | tf_op jit(solution)/shard_map/ppermute | solution.py:795
  479.4 6.3 shard_map.208
  492.6 22.7 %shard_map.210 = (f32[416,768]{1,0:T(8,128)}, bf16[4,2,2,192,384]{4,3,2,1,0:T(8,128)(2,1)}, bf16[4,2,2,192,384]{4,3,2,1,0:T(8,128)(2,1)}, bf16[4,2,2,192,384]{4,...) custom-call(s32[4]{0:T(128)} %pad_add_fusion.me_ref, f32[416,768]{1,0:T(8,128)} %get-tuple-element.261.g_ref, ...), custom_call_target="tpu_custom_call" | custom-call | flops 9814671360 | bytes 53403664 | tf_op jit(solution)/shard_map/pallas_call | solution.py:194
  521.5 21.6 %shard_map.212 = (f32[416,768]{1,0:T(8,128)}, bf16[4,2,2,192,384]{4,3,2,1,0:T(8,128)(2,1)}, bf16[4,2,2,192,384]{4,3,2,1,0:T(8,128)(2,1)}, f32[2,768]{1,0:T(2,128)}) custom-call(s32[4]{0:T(128)} %pad_add_fusion.me_ref, f32[416,768]{1,0:T(8,128)} %get-tuple-element.271.g_ref, f32[416,768]{1,0:T(8,128)} %get-tuple-element.189.x1_ref, ...), custom_call_target="tpu_custom_call" | custom-call | flops 3925868544 | bytes 51260944 | tf_op jit(solution)/shard_map/pallas_call | solution.py:194
  552.4 7.8 %shard_map.214 = (bf16[104,768]{1,0:T(8,128)(2,1)}, bf16[104,768]{1,0:T(8,128)(2,1)}, bf16[104,768]{1,0:T(8,128)(2,1)}, bf16[104,768]{1,0:T(8,128)(2,1)}, bf16[2...) custom-call(s32[4]{0:T(128)} %pad_add_fusion.me_ref, f32[416,768]{1,0:T(8,128)} %get-tuple-element.283.g_ref.refs_5_, ...), custom_call_target="tpu_custom_call" | custom-call | flops 1962934272 | bytes 26787856 | tf_op jit(solution)/shard_map/pallas_call | solution.py:194
  560.2 23.0 %collective-permute-done.43.refs_17_ = bf16[2,192,384]{2,1,0:T(8,128)(2,1)S(1)} collective-permute-done((bf16[2,192,384]{2,1,0:T(8,128)(2,1)S(1)}, bf16[2,192,384]{2,1,0:T(8,128)(2,1)S(1)}, u32[]{:S(2)}, u32[]{:S(2)}) %collective-permute-start.43) | collective-permute-done | bytes 294944 | tf_op jit(solution)/shard_map/ppermute | solution.py:963
  599.2 18.5 %shard_map.216 = (bf16[104,768]{1,0:T(8,128)(2,1)}, bf16[104,768]{1,0:T(8,128)(2,1)}, bf16[104,768]{1,0:T(8,128)(2,1)}, bf16[104,768]{1,0:T(8,128)(2,1)}, bf16[1...) custom-call(s32[4]{0:T(128)} %pad_add_fusion.me_ref, ...), custom_call_target="tpu_custom_call" | custom-call | flops 2944401408 | bytes 27446800 | tf_op jit(solution)/shard_map/pallas_call | solution.py:194
  618.3 6.7 collective-permute-done.44.refs_3_.refs_4_
  629.5 6.5 shard_map.217
  649.2 10.5 %collective-permute-done.55.refs_3_.refs_8_ = bf16[6,192,384]{2,1,0:T(8,128)(2,1)S(1)} collective-permute-done((bf16[6,192,384]{2,1,0:T(8,128)(2,1)}, bf16[6,192,384]{2,1,0:T(8,128)(2,1)S(1)}, u32[]{:S(2)}, u32[]{:S(2)}) %collective-permute-start.55) | collective-permute-done | bytes 884768 | tf_op jit(solution)/shard_map/ppermute | solution.py:963
  698.3 12.8 %all-to-all-start.1 = ((bf16[4,5,48,384]{3,2,1,0:T(8,128)(2,1)}), bf16[4,5,48,384]{3,2,1,0:T(8,128)(2,1)S(1)}, u32[]{:S(2)}, u32[]{:S(2)}) async-start(bf16[4,5,48,384]{3,2,1,0:T(8,128)(2,1)} %shard_map.220), calls=%async_computation.1 | async-start | bytes 1474560 | tf_op jit(solution)/shard_map/all_to_all | solution.py:989
  715.7 15.4 %all-to-all-done.1 = bf16[4,5,48,384]{3,2,1,0:T(8,128)(2,1)S(1)} async-done(((bf16[4,5,48,384]{3,2,1,0:T(8,128)(2,1)}), bf16[4,5,48,384]{3,2,1,0:T(8,128)(2,1)S(1)}, u32[]{:S(2)}, u32[]{:S(2)}) %all-to-all-start.1) | async-done | bytes 737312 | tf_op jit(solution)/shard_map/all_to_all | solution.py:989
  (388 shorter events, 169.3 us)
Async XLA Ops:
  7.2 146.9 %all-gather.3.cloned.1.call-start = ((), (), s32[]{:S(2)}) async-start(), calls=%async_computation.8 | async-start | bytes 20680704 | tf_op jit(solution)/shard_map/all_gather | solution.py:823
  10.5 295.3 %all-gather.5.cloned.1.call-start = ((), (), s32[]{:S(2)}) async-start(), calls=%async_computation.9 | async-start | bytes 20680704 | tf_op jit(solution)/shard_map/all_gather | solution.py:823
  11.5 37.9 %collective-permute-start.1 = (bf16[1,2,196,768]{3,1,2,0:T(2,128)(2,1)S(1)}, bf16[1,2,196,768]{3,1,2,0:T(2,128)(2,1)S(1)}, u32[]{:S(2)}, u32[]{:S(2)}) collective-permute-start(bf16[1,2,196,768]{3,1,2,0:T(2,128)(2,1)S(1)} %copy-done.71), channel_id=1, source_target_pairs={{0,0},{2,8},{4,2},{6,10},{8,4},{10,12},{12,6},{14,14},{16,16},{18,... | collective-permute-start | bytes 1806344 | tf_op jit(solution)/shard_map/ppermute | solution.py:773
  13.0 35.4 %all-to-all-start = ((f32[32,1,384]{2,1,0:T(1,128)}), f32[32,1,384]{2,1,0:T(1,128)S(1)}, u32[]{:S(2)}, u32[]{:S(2)}) async-start(f32[32,1,384]{2,1,0:T(1,128)} %broadcast_in_dim.17), calls=%async_computation | async-start | bytes 98304 | tf_op jit(solution)/shard_map/all_to_all | solution.py:1038
  21.8 616.4 %reduce-scatter.7.cloned.1.call-start = ((), (), s32[]{:S(2)}) async-start(), calls=%async_computation.11 | async-start | bytes 737280 | tf_op jit(solution)/shard_map/reduce_scatter | solution.py:992
  54.8 26.5 %collective-permute-start.4 = (bf16[104,768]{1,0:T(8,128)(2,1)}, bf16[104,768]{1,0:T(8,128)(2,1)S(1)}, u32[]{:S(2)}, u32[]{:S(2)}) collective-permute-start(bf16[104,768]{1,0:T(8,128)(2,1)} %get-tuple-element.183), channel_id=1, source_target_pairs={{0,10},{2,8},{4,14},{6,12},{8,2},{10,0},{12,6},{14,4},{16,26},{18,... | collective-permute-start | bytes 479240 | tf_op jit(solution)/shard_map/ppermute | solution.py:795
  168.3 53.2 %collective-permute-start = (bf16[1,2,196,768]{3,1,2,0:T(2,128)(2,1)S(1)}, bf16[1,2,196,768]{3,1,2,0:T(2,128)(2,1)S(1)}, u32[]{:S(2)}, u32[]{:S(2)}) collective-permute-start(bf16[1,2,196,768]{3,1,2,0:T(2,128)(2,1)S(1)} %copy-done.72), channel_id=1, source_target_pairs={{0,0},{2,8},{4,2},{6,10},{8,4},{10,12},{12,6},{14,14},{16,16},{18,... | collective-permute-start | bytes 1806344 | tf_op jit(solution)/shard_map/ppermute | solution.py:773
  219.7 86.1 %collective-permute-start.8 = (bf16[104,768]{1,0:T(8,128)(2,1)}, bf16[104,768]{1,0:T(8,128)(2,1)S(1)}, u32[]{:S(2)}, u32[]{:S(2)}) collective-permute-start(bf16[104,768]{1,0:T(8,128)(2,1)} %get-tuple-element.192), channel_id=1, source_target_pairs={{0,8},{2,10},{4,12},{6,14},{8,0},{10,2},{12,4},{14,6},{16,24},{18,... | collective-permute-start | bytes 479240 | tf_op jit(solution)/shard_map/ppermute | solution.py:795
  220.1 85.7 %collective-permute-start.9 = (bf16[104,768]{1,0:T(8,128)(2,1)}, bf16[104,768]{1,0:T(8,128)(2,1)S(1)}, u32[]{:S(2)}, u32[]{:S(2)}) collective-permute-start(bf16[104,768]{1,0:T(8,128)(2,1)} %get-tuple-element.193), channel_id=1, source_target_pairs={{0,2},{2,0},{4,6},{6,4},{8,10},{10,8},{12,14},{14,12},{16,18},{18,... | collective-permute-start | bytes 479240 | tf_op jit(solution)/shard_map/ppermute | solution.py:795
  220.1 85.7 %collective-permute-start.10 = (bf16[104,768]{1,0:T(8,128)(2,1)}, bf16[104,768]{1,0:T(8,128)(2,1)S(1)}, u32[]{:S(2)}, u32[]{:S(2)}) collective-permute-start(bf16[104,768]{1,0:T(8,128)(2,1)} %get-tuple-element.194), channel_id=1, source_target_pairs={{0,10},{2,8},{4,14},{6,12},{8,2},{10,0},{12,6},{14,4},{16,26},{18,... | collective-permute-start | bytes 479240 | tf_op jit(solution)/shard_map/ppermute | solution.py:795
  396.2 29.6 %collective-permute-start.22 = (bf16[4,2,2,192,384]{4,3,2,1,0:T(8,128)(2,1)}, bf16[4,2,2,192,384]{4,3,2,1,0:T(8,128)(2,1)S(1)}, u32[]{:S(2)}, u32[]{:S(2)}) collective-permute-start(bf16[4,2,2,192,384]{4,3,2,1,0:T(8,128)(2,1)} %get-tuple-element.224), channel_id=1, source_target_pairs={{0,8},{8,0},{16,24},{24,16},{1,9},{9,1},{17,25},{25,17},{2,10},{10... | collective-permute-start | bytes 7077896 | tf_op jit(solution)/shard_map/ppermute | solution.py:963
  434.6 28.7 %collective-permute-start.23 = (bf16[8,192,384]{2,1,0:T(8,128)(2,1)}, bf16[8,192,384]{2,1,0:T(8,128)(2,1)S(1)}, u32[]{:S(2)}, u32[]{:S(2)}) collective-permute-start(bf16[8,192,384]{2,1,0:T(8,128)(2,1)} %get-tuple-element.238), channel_id=1, source_target_pairs={{0,1},{1,0},{2,3},{3,2},{4,5},{5,4},{6,7},{7,6},{8,9},{9,8},{10,11... | collective-permute-start | bytes 3538952 | tf_op jit(solution)/shard_map/ppermute | solution.py:963
  435.4 28.2 %collective-permute-start.24 = (bf16[8,192,384]{2,1,0:T(8,128)(2,1)}, bf16[8,192,384]{2,1,0:T(8,128)(2,1)S(1)}, u32[]{:S(2)}, u32[]{:S(2)}) collective-permute-start(bf16[8,192,384]{2,1,0:T(8,128)(2,1)} %get-tuple-element.239), channel_id=1, source_target_pairs={{0,16},{8,24},{16,0},{24,8},{1,17},{9,25},{17,1},{25,9},{2,18},{10... | collective-permute-start | bytes 3538952 | tf_op jit(solution)/shard_map/ppermute | solution.py:963
  436.8 27.5 %collective-permute-start.28 = (bf16[2,2,2,192,384]{4,3,2,1,0:T(8,128)(2,1)S(1)}, bf16[2,2,2,192,384]{4,3,2,1,0:T(8,128)(2,1)S(1)}, u32[]{:S(2)}, u32[]{:S(2)}) collective-permute-start(bf16[2,2,2,192,384]{4,3,2,1,0:T(8,128)(2,1)S(1)} %copy-done.70), channel_id=1, source_target_pairs={{0,8},{8,0},{16,24},{24,16},{1,9},{9,1},{17,25},{25,17},{2,10},{10... | collective-permute-start | bytes 3538952 | tf_op jit(solution)/shard_map/ppermute | solution.py:963
  486.2 29.7 %collective-permute-start.32 = (bf16[6,192,384]{2,1,0:T(8,128)(2,1)}, bf16[6,192,384]{2,1,0:T(8,128)(2,1)S(1)}, u32[]{:S(2)}, u32[]{:S(2)}) collective-permute-start(bf16[6,192,384]{2,1,0:T(8,128)(2,1)} %get-tuple-element.263), channel_id=1, source_target_pairs={{0,1},{1,0},{2,3},{3,2},{4,5},{5,4},{6,7},{7,6},{8,9},{9,8},{10,11... | collective-permute-start | bytes 2654216 | tf_op jit(solution)/shard_map/ppermute | solution.py:963
  487.3 28.6 %collective-permute-start.33 = (bf16[8,192,384]{2,1,0:T(8,128)(2,1)}, bf16[8,192,384]{2,1,0:T(8,128)(2,1)S(1)}, u32[]{:S(2)}, u32[]{:S(2)}) collective-permute-start(bf16[8,192,384]{2,1,0:T(8,128)(2,1)} %get-tuple-element.264), channel_id=1, source_target_pairs={{0,16},{8,24},{16,0},{24,8},{1,17},{9,25},{17,1},{25,9},{2,18},{10... | collective-permute-start | bytes 3538952 | tf_op jit(solution)/shard_map/ppermute | solution.py:963
  515.4 27.9 %collective-permute-start.34 = (bf16[4,2,2,192,384]{4,3,2,1,0:T(8,128)(2,1)}, bf16[4,2,2,192,384]{4,3,2,1,0:T(8,128)(2,1)}, u32[]{:S(2)}, u32[]{:S(2)}) collective-permute-start(bf16[4,2,2,192,384]{4,3,2,1,0:T(8,128)(2,1)} %get-tuple-element.277), channel_id=1, source_target_pairs={{0,8},{8,0},{16,24},{24,16},{1,9},{9,1},{17,25},{25,17},{2,10},{10... | collective-permute-start | bytes 7077896 | tf_op jit(solution)/shard_map/ppermute | solution.py:963
  515.5 27.9 %collective-permute-start.35 = (bf16[4,2,2,192,384]{4,3,2,1,0:T(8,128)(2,1)}, bf16[4,2,2,192,384]{4,3,2,1,0:T(8,128)(2,1)}, u32[]{:S(2)}, u32[]{:S(2)}) collective-permute-start(bf16[4,2,2,192,384]{4,3,2,1,0:T(8,128)(2,1)} %get-tuple-element.279), channel_id=1, source_target_pairs={{0,8},{8,0},{16,24},{24,16},{1,9},{9,1},{17,25},{25,17},{2,10},{10... | collective-permute-start | bytes 7077896 | tf_op jit(solution)/shard_map/ppermute | solution.py:963
  521.4 126.7 %reduce-scatter.11.cloned.1.call-start = ((), (), s32[]{:S(2)}) async-start(), calls=%async_computation.13 | async-start | bytes 1474560 | tf_op jit(solution)/shard_map/reduce_scatter | solution.py:992
  543.1 45.5 %collective-permute-start.41 = (bf16[4,2,2,192,384]{4,3,2,1,0:T(8,128)(2,1)}, bf16[4,2,2,192,384]{4,3,2,1,0:T(8,128)(2,1)S(1)}, u32[]{:S(2)}, u32[]{:S(2)}) collective-permute-start(bf16[4,2,2,192,384]{4,3,2,1,0:T(8,128)(2,1)} %get-tuple-element.293), channel_id=1, source_target_pairs={{0,8},{8,0},{16,24},{24,16},{1,9},{9,1},{17,25},{25,17},{2,10},{10... | collective-permute-start | bytes 7077896 | tf_op jit(solution)/shard_map/ppermute | solution.py:963
  543.3 136.4 %reduce-scatter.5.cloned.1.call-start = ((), (), s32[]{:S(2)}) async-start(), calls=%async_computation.10 | async-start | bytes 921600 | tf_op jit(solution)/shard_map/reduce_scatter | solution.py:992
  548.2 40.4 %collective-permute-start.39 = (bf16[8,192,384]{2,1,0:T(8,128)(2,1)}, bf16[8,192,384]{2,1,0:T(8,128)(2,1)S(1)}, u32[]{:S(2)}, u32[]{:S(2)}) collective-permute-start(bf16[8,192,384]{2,1,0:T(8,128)(2,1)} %get-tuple-element.290), channel_id=1, source_target_pairs={{0,16},{8,24},{16,0},{24,8},{1,17},{9,25},{17,1},{25,9},{2,18},{10... | collective-permute-start | bytes 3538952 | tf_op jit(solution)/shard_map/ppermute | solution.py:963
  549.4 39.3 %collective-permute-start.40 = (bf16[8,192,384]{2,1,0:T(8,128)(2,1)}, bf16[8,192,384]{2,1,0:T(8,128)(2,1)S(1)}, u32[]{:S(2)}, u32[]{:S(2)}) collective-permute-start(bf16[8,192,384]{2,1,0:T(8,128)(2,1)} %get-tuple-element.291), channel_id=1, source_target_pairs={{0,1},{1,0},{2,3},{3,2},{4,5},{5,4},{6,7},{7,6},{8,9},{9,8},{10,11... | collective-permute-start | bytes 3538952 | tf_op jit(solution)/shard_map/ppermute | solution.py:963
  550.3 36.8 %collective-permute-start.42 = (bf16[3,192,384]{2,1,0:T(8,128)(2,1)S(1)}, bf16[3,192,384]{2,1,0:T(8,128)(2,1)S(1)}, u32[]{:S(2)}, u32[]{:S(2)}) collective-permute-start(bf16[3,192,384]{2,1,0:T(8,128)(2,1)S(1)} %copy-done.73), channel_id=1, source_target_pairs={{0,1},{1,0},{2,3},{3,2},{4,5},{5,4},{6,7},{7,6},{8,9},{9,8},{10,11... | collective-permute-start | bytes 1327112 | tf_op jit(solution)/shard_map/ppermute | solution.py:963
  551.4 31.8 %collective-permute-start.43 = (bf16[2,192,384]{2,1,0:T(8,128)(2,1)S(1)}, bf16[2,192,384]{2,1,0:T(8,128)(2,1)S(1)}, u32[]{:S(2)}, u32[]{:S(2)}) collective-permute-start(bf16[2,192,384]{2,1,0:T(8,128)(2,1)S(1)} %copy-done.74), channel_id=1, source_target_pairs={{0,16},{8,24},{16,0},{24,8},{1,17},{9,25},{17,1},{25,9},{2,18},{10... | collective-permute-start | bytes 884744 | tf_op jit(solution)/shard_map/ppermute | solution.py:963
  597.1 28.0 %collective-permute-start.44 = (bf16[8,192,384]{2,1,0:T(8,128)(2,1)}, bf16[8,192,384]{2,1,0:T(8,128)(2,1)S(1)}, u32[]{:S(2)}, u32[]{:S(2)}) collective-permute-start(bf16[8,192,384]{2,1,0:T(8,128)(2,1)} %get-tuple-element.310), channel_id=1, source_target_pairs={{0,1},{1,0},{2,3},{3,2},{4,5},{5,4},{6,7},{7,6},{8,9},{9,8},{10,11... | collective-permute-start | bytes 3538952 | tf_op jit(solution)/shard_map/ppermute | solution.py:963
  598.0 28.1 %collective-permute-start.45 = (bf16[8,192,384]{2,1,0:T(8,128)(2,1)}, bf16[8,192,384]{2,1,0:T(8,128)(2,1)}, u32[]{:S(2)}, u32[]{:S(2)}) collective-permute-start(bf16[8,192,384]{2,1,0:T(8,128)(2,1)} %get-tuple-element.311), channel_id=1, source_target_pairs={{0,16},{8,24},{16,0},{24,8},{1,17},{9,25},{17,1},{25,9},{2,18},{10... | collective-permute-start | bytes 3538952 | tf_op jit(solution)/shard_map/ppermute | solution.py:963
  599.1 27.6 %collective-permute-start.49 = (bf16[2,2,2,192,384]{4,3,2,1,0:T(8,128)(2,1)}, bf16[2,2,2,192,384]{4,3,2,1,0:T(8,128)(2,1)S(1)}, u32[]{:S(2)}, u32[]{:S(2)}) collective-permute-start(bf16[2,2,2,192,384]{4,3,2,1,0:T(8,128)(2,1)} %get-tuple-element.319), channel_id=1, source_target_pairs={{0,8},{8,0},{16,24},{24,16},{1,9},{9,1},{17,25},{25,17},{2,10},{10... | collective-permute-start | bytes 3538952 | tf_op jit(solution)/shard_map/ppermute | solution.py:963
  599.1 113.6 %reduce-scatter.9.cloned.1.call-start = ((), (), s32[]{:S(2)}) async-start(), calls=%async_computation.12 | async-start | bytes 1474560 | tf_op jit(solution)/shard_map/reduce_scatter | solution.py:992
  636.1 29.0 %collective-permute-start.54 = (bf16[8,192,384]{2,1,0:T(8,128)(2,1)}, bf16[8,192,384]{2,1,0:T(8,128)(2,1)S(1)}, u32[]{:S(2)}, u32[]{:S(2)}) collective-permute-start(bf16[8,192,384]{2,1,0:T(8,128)(2,1)} %get-tuple-element.334), channel_id=1, source_target_pairs={{0,16},{8,24},{16,0},{24,8},{1,17},{9,25},{17,1},{25,9},{2,18},{10... | collective-permute-start | bytes 3538952 | tf_op jit(solution)/shard_map/ppermute | solution.py:963
  670.4 27.9 %all-to-all-start.2 = ((bf16[4,4,48,384]{3,2,1,0:T(8,128)(2,1)}), bf16[4,4,48,384]{3,2,1,0:T(8,128)(2,1)S(1)}, u32[]{:S(2)}, u32[]{:S(2)}) async-start(bf16[4,4,48,384]{3,2,1,0:T(8,128)(2,1)} %get-tuple-element.339), calls=%async_computation.3 | async-start | bytes 1179648 | tf_op jit(solution)/shard_map/all_to_all | solution.py:989
  698.3 32.8 %all-to-all-start.1 = ((bf16[4,5,48,384]{3,2,1,0:T(8,128)(2,1)}), bf16[4,5,48,384]{3,2,1,0:T(8,128)(2,1)S(1)}, u32[]{:S(2)}, u32[]{:S(2)}) async-start(bf16[4,5,48,384]{3,2,1,0:T(8,128)(2,1)} %shard_map.220), calls=%async_computation.1 | async-start | bytes 1474560 | tf_op jit(solution)/shard_map/all_to_all | solution.py:989
  (111 other events, 1082.0 us)
Sparse Core Ops, SparseCore 0:
  11.7 142.3 all-gather.2
  157.2 148.5 all-gather.4
  521.6 20.0 reduce-scatter.6
  543.8 27.5 reduce-scatter.10
  599.2 20.4 reduce-scatter.4
  639.3 28.0 reduce-scatter.8

commit v9 on v8

--- a/solution.py
+++ b/solution.py
@@ -386,7 +386,7 @@
     t, d = x2.shape
     width = w.shape[3]
     shares = w.shape[1]
-    per_share = (w.shape[0] - 9) // 2
+    per_share = w.shape[0] // 2
     steps = shares * per_share
 
     def body(x2_ref, wi_ref, wo_ref, gb_ref, me_ref, gn_ref, x3_ref, *rest):
@@ -410,8 +410,8 @@
 
     ins = [
         whole(x2.shape),
-        ff_slab(8, per_share, d, width),
-        ff_slab(8 + per_share, per_share, d, width),
+        ff_slab(0, per_share, d, width),
+        ff_slab(per_share, per_share, d, width),
         whole(gb.shape),
     ]
     ins += [SCALARS, whole(gb_next.shape)]
@@ -426,7 +426,7 @@
     t, d = x2.shape
     width = w.shape[3]
     shares = w.shape[1]
-    per_share = (w.shape[0] - 9) // 2
+    per_share = w.shape[0] // 2
     steps = shares * per_share
 
     def body(me_ref, g_ref, x2_ref, wi_ref, wo_ref, gb_ref, go_ref, ki_ref, si_ref, ko_ref, so_ref, sums_ref, *rest):
@@ -479,8 +479,8 @@
             SCALARS,
             whole(grad.shape),
             whole(x2.shape),
-            ff_slab(8, per_share, d, width),
-            ff_slab(8 + per_share, per_share, d, width),
+            ff_slab(0, per_share, d, width),
+            ff_slab(per_share, per_share, d, width),
             whole(gb.shape),
         ],
         [made((t, d), F32), *slab_outs, made((2, d), F32)] + [made((t, d), F32)] * with_output,
@@ -796,32 +796,82 @@
     return got
 
 
-def pack_layer(time_qkv, time_out, time_mix, space_qkv, space_out, mlp_in, mlp_out):
-    width = time_qkv.shape[2]
-    r = time_qkv.shape[0]
-    halves = time_mix.shape[1] // width
-
-    def columns(a):
-        return a.reshape(r, -1, width).transpose(1, 0, 2)
-
-    mix = time_mix.reshape(-1, halves, width).transpose(1, 0, 2).reshape(1, r, width)
+def columns(a, r, width):
+    return a.reshape(r, -1, width).transpose(1, 0, 2)
+
+
+def pack_attention(time_qkv, time_out, time_mix, space_qkv, space_out):
+    r, _, width = time_qkv.shape
+    mix = time_mix.reshape(-1, time_mix.shape[1] // width, width).transpose(1, 0, 2).reshape(1, r, width)
     return jnp.concatenate(
         (
-            columns(time_qkv),
-            columns(space_qkv),
+            columns(time_qkv, r, width),
+            columns(space_qkv, r, width),
             time_out.T[None],
             space_out.T[None],
-            columns(mlp_in),
-            columns(mlp_out.T),
             mix,
         ),
         axis=0,
     )
 
 
+def pack_feed_forward(mlp_in, mlp_out, width):
+    r = mlp_in.shape[0]
+    return jnp.concatenate((columns(mlp_in, r, width), columns(mlp_out.T, r, width)), axis=0)
+
+
 def gather_slabs(pack):
     full = lax.all_gather(pack, ("head", "clip", "seq"), axis=1, tiled=True)
     return full.reshape(pack.shape[0], lax.axis_size("head"), -1, pack.shape[2])
+
+
+def spread_slabs(pack, me):
+    ways, clips = lax.axis_size("seq"), lax.axis_size("clip")
+    shares = lax.axis_size("head")
+    n, r, width = pack.shape
+    turned = [pack] + [
+        lax.ppermute(pack, "seq", [(i, (i + k) % ways) for i in range(ways)]) for k in range(1, ways)
+    ]
+    runs = []
+    for steps, first, second in (((0, 1), "x", "h"), ((3, 2), "h", "x")):
+        some = jnp.stack([turned[k] for k in steps])
+        some = jnp.concatenate((some, cross(some, first)), axis=0)
+        where = [(k, {first: f}) for f in (0, 1) for k in steps]
+        for g, blocks in enumerate((some, cross(some, second))):
+            runs.append((blocks, [(k, {**at, second: g}) for k, at in where], 0))
+    runs += [(cross(blocks, "c"), where, 1) for blocks, where, _ in runs]
+    count = sum(len(where) for _, where, _ in runs)
+
+    def body(me_ref, *refs):
+        sources, out_ref, sems = refs[: len(runs)], refs[-2], refs[-1]
+        copies = []
+        for source, (_, where, core) in zip(sources, runs):
+            for i, (k, at) in enumerate(where):
+                share = jnp.bitwise_xor(me_ref[2], at["h"])
+                clip = 2 * jnp.bitwise_xor(me_ref[1], at["x"]) + jnp.bitwise_xor(me_ref[0], core)
+                seq = lax.rem(me_ref[4] + (ways - k), ways)
+                copies.append(
+                    pltpu.make_async_copy(
+                        source.at[i], out_ref.at[:, share, clip * ways + seq], sems.at[len(copies)]
+                    )
+                )
+        for copy in copies:
+            copy.start()
+        for copy in copies:
+            copy.wait()
+
+    full = pl.pallas_call(
+        body,
+        out_shape=jax.ShapeDtypeStruct((n, shares, clips * ways, r, width), BF16),
+        in_specs=[SCALARS] + [pl.BlockSpec(memory_space=pltpu.HBM)] * len(runs),
+        out_specs=pl.BlockSpec(memory_space=pltpu.HBM),
+        scratch_shapes=[pltpu.SemaphoreType.DMA((count,))],
+        compiler_params=pltpu.CompilerParams(vmem_limit_bytes=VMEM),
+        cost_estimate=pl.CostEstimate(
+            flops=0, bytes_accessed=4 * n * shares * clips * ways * r * width, transcendentals=0
+        ),
+    )(me, *(blocks for blocks, _, _ in runs))
+    return full.reshape(n, shares, clips * ways * r, width)
 
 
 def mix_whole(slab, shards):
@@ -1083,43 +1133,54 @@
 
     gbs = gather_norms(norm_gain, norm_bias)
     gb = [gbs[l] for l in range(layers)]
-    weights = [
-        gather_slabs(
-            pack_layer(
-                time_qkv[l], time_out[l], time_mix[l], space_qkv[l], space_out[l], mlp_in[l], mlp_out[l]
-            )
-        )
+    packs = [
+        pack_attention(time_qkv[l], time_out[l], time_mix[l], space_qkv[l], space_out[l])
         for l in range(layers)
     ]
+    packs_ff = [pack_feed_forward(mlp_in[l], mlp_out[l], time_qkv.shape[3]) for l in range(layers)]
+    weights = [gather_slabs(pack) for pack in packs]
     mixes = [mix_whole(w[-1], shards) for w in weights]
+    quick = lax.axis_size("clip") == 4 and shares == 2 and ways == 4 and time_qkv.shape[1] % 16 == 0
 
     halves = Halves(lax.axis_size("clip"), d, time_qkv.shape[3])
     clip = lax.axis_index("clip")
     member = member_of(clip, lax.axis_index("seq"))
-    me = jnp.stack((clip & 1, (clip >> 1) & 1, lax.axis_index("head"), member)).astype(jnp.int32)
+    me = jnp.stack((clip & 1, (clip >> 1) & 1, lax.axis_index("head"), member, lax.axis_index("seq"))).astype(
+        jnp.int32
+    )
+    if quick:
+        weights_ff = [spread_slabs(pack, me) for pack in packs_ff]
+    else:
+        weights_ff = [gather_slabs(pack) for pack in packs_ff]
 
     x = as_rows(go_home(tokens))
     send = send_first(rows, x, gb[0], me)
     kept = []
     for l in range(layers):
         w = weights[l]
-        a1, qkv1, log1, o1_time = time_forward(rows, swap_places(send), w)
+        send = swap_places(send)
+        if quick and l == 0:
+            send, weights_ff[l] = lax.optimization_barrier((send, weights_ff[l]))
+        a1, qkv1, log1, o1_time = time_forward(rows, send, w)
         back = swap_places(o1_time)
         o1, y1, x1, qkv2 = middle_forward(rows, back, x, w, mixes[l], gb[l], me)
+        if quick and l == 0:
+            x1, weights_ff[1:] = lax.optimization_barrier((x1, weights_ff[1:]))
         o2, x2, log2 = space_forward(rows, qkv2, x1, w)
         kept.append((x, a1, qkv1, log1, o1, y1, x1, qkv2, o2, log2, x2))
         if l + 1 < layers:
-            x, *send = mlp_forward(rows, x2, w, gb[l], gb[l + 1], me)
+            x, *send = mlp_forward(rows, x2, weights_ff[l], gb[l], gb[l + 1], me)
 
     grad = as_rows(go_home(cotangent))
     norm_rows = [None] * layers
     summed = [None] * layers
     late = []
-    quick = lax.axis_size("clip") == 4 and shares == 2 and time_qkv.shape[1] % 16 == 0
     for l in reversed(range(layers)):
         w = weights[l]
         x, a1, qkv1, log1, o1, y1, x1, qkv2, o2, log2, x2 = kept[l]
-        grad, g_ff, s3, x3 = mlp_backward(rows, grad, x2, w, gb[l], me, halves, l + 1 == layers)
+        grad, g_ff, s3, x3 = mlp_backward(
+            rows, grad, x2, weights_ff[l], gb[l], me, halves, l + 1 == layers
+        )
         if x3:
             output = go_back(from_rows(x3[0].astype(BF16)))
         if quick:
@@ -1131,6 +1192,8 @@
         grad, g_space, s2 = space_backward(rows, grad, x1, qkv2, o2, log2, w, gb[l], me, halves)
         if quick:
             space = pieces_of([g_space])
+            if late:
+                grad = settle(grad, late)
             grad, output = move((grad, output), ff, me)
         do1, g_out = middle_backward(rows, grad, y1, o1, w, mixes[l], me, halves, shards)
         do1 = swap_places(do1)
@@ -1151,7 +1214,7 @@
         else:
             summed[l] = [reduce_plain(g_ff + [g_space, g_out] + g_time, clip & 1)]
     if quick:
-        move((), late, me, True)
+        tokens_grad = move(go_back(from_rows(grad.astype(BF16))), late, me, True)
         move((), rest, me, True)
         summed = [[p.result for p in some] for some in summed]
     cuts = (2 * g_ff[0][0].shape[0], g_space[0].shape[0], g_out[0].shape[0], len(g_time))
@@ -1160,7 +1223,9 @@
         slabs_of = jnp.concatenate(some, axis=0)
         ends = [sum(cuts[: i + 1]) for i in range(4)]
         results.append([slabs_of[e - c : e] for c, e in zip(cuts, ends)])
-    tokens_grad = go_back(from_rows(grad.astype(BF16))).astype(F32)
+    if not quick:
+        tokens_grad = go_back(from_rows(grad.astype(BF16)))
+    tokens_grad = tokens_grad.astype(F32)
     norm_sums = reduce_norms(jnp.concatenate(norm_rows, axis=0)).reshape(layers, 2, 3, -1)
 
     def stacked(form):

time: 750 us -> 1290 us (1.72)
  Pallas kernels: 278 us -> 853 us
  waiting for transfers between devices: 300 us -> 215 us
  starting transfers between devices: 95.7 us -> 134 us
    pallas_call x0 -> x2, Pallas kernels: none -> 576 us  [spread_slabs(): pl.pallas_call(body, out_shape=jax.ShapeDtypeStruct((n, shares, clips * w...]
    all_gather x2, waiting for transfers between devices: 157 us -> 0.04 us  [gather_slabs(): full = lax.all_gather(pack, ('head', 'clip', 'seq'), axis=1, tiled=True)]
    ppermute x30 -> x46, waiting for transfers between devices: 59.1 us -> 114 us  [cross(): return lax.ppermute(a, axis, [(i, i ^ 1 << bit) for i in range(size)])]
    ppermute x0 -> x6, waiting for transfers between devices: none -> 40.8 us  [spread_slabs(): lax.ppermute(pack, 'seq', [(i, (i + k) % ways) for i in range(ways)])]
    ppermute x24, waiting for transfers between devices: 41.9 us -> 23.4 us  [swap_places(): got.append(lax.ppermute(chunks[k], ('clip', 'seq'), pairs))]
    ppermute x2, starting transfers between devices: 1.39 us -> 18.9 us  [go_home(): return lax.ppermute(a, ('clip', 'seq'), homes())]
    ppermute x0 -> x6, starting transfers between devices: none -> 17.3 us  [spread_slabs(): lax.ppermute(pack, 'seq', [(i, (i + k) % ways) for i in range(ways)])]
    all_to_all x1, waiting for transfers between devices: 25.9 us -> 9.46 us  [gather_norms(): lax.all_to_all(jnp.broadcast_to(padded, (count, width)), ALL, split_axis=...]
  transfers between devices with their start and end apart: 68 -> 90, of which waited for: 20 -> 28; matrix products, arithmetic and copies ran while one was open for 4% -> 3% of each run, Pallas kernels for 30% -> 62%
where the time goes in v9:
time: 1290 us; the launch traced here: 1280 us
  Pallas kernels  853 us (66%)
  waiting for transfers between devices  215 us (17%)
  starting transfers between devices  134 us (10%)
  local copies, waits for them, and re-layouts  41 us (3%)
  other arithmetic  21.4 us (2%)
  between operations  15.9 us (1%)
    pallas_call x2, Pallas kernels, spread_slabs(): pl.pallas_call(body, out_shape=jax.ShapeDtypeStruct((n, shares, clips * w...  576 us
    pallas_call x18, Pallas kernels, call(): pl.pallas_call(body, out_shape=[shape for shape, _ in outs], grid=grid, i...  232 us
    ppermute x46, waiting for transfers between devices, cross(): return lax.ppermute(a, axis, [(i, i ^ 1 << bit) for i in range(size)])  114 us
    pallas_call x9, Pallas kernels, fold(): pl.pallas_call(body, out_shape=[jax.ShapeDtypeStruct(shape, BF16) for sha...  45.5 us
    ppermute x24, starting transfers between devices, swap_places(): got.append(lax.ppermute(chunks[k], ('clip', 'seq'), pairs))  41.2 us
    ppermute x6, waiting for transfers between devices, spread_slabs(): lax.ppermute(pack, 'seq', [(i, (i + k) % ways) for i in range(ways)])  40.8 us
    ppermute x46, starting transfers between devices, cross(): return lax.ppermute(a, axis, [(i, i ^ 1 << bit) for i in range(size)])  38 us
  transfers between devices with their start and end apart: 90, of which 28 were waited for; matrix products, arithmetic and copies ran while one was open for 3% of the time, Pallas kernels for 62%

profile of v9, /device:TPU:0, one launch (start us, length us, event | category | flops | bytes accessed | tf_op | source)
XLA Modules:
  0.0 1280.0 jit_solution(17344332045894880363)
XLA Ops:
  25.4 30.4 %collective-permute-done.9 = bf16[8,48,384]{2,1,0:T(8,128)(2,1)S(1)} collective-permute-done((bf16[8,48,384]{2,1,0:T(8,128)(2,1)S(1)}, bf16[8,48,384]{2,1,0:T(8,128)(2,1)S(1)}, u32[]{:S(2)}, u32[]{:S(2)}) %collective-permute-start.9) | collective-permute-done | bytes 294944 | tf_op jit(solution)/shard_map/ppermute | solution.py:833
  66.1 9.5 all-to-all-done
  77.1 7.5 collective-permute-start.23
  94.2 9.6 collective-permute-done.23
  108.6 13.1 %collective-permute-done.3.refs_2_ = bf16[104,768]{1,0:T(8,128)(2,1)S(1)} collective-permute-done((bf16[104,768]{1,0:T(8,128)(2,1)S(1)}, bf16[104,768]{1,0:T(8,128)(2,1)S(1)}, u32[]{:S(2)}, u32[]{:S(2)}) %collective-permute-start.3) | collective-permute-done | bytes 159776 | tf_op jit(solution)/shard_map/ppermute | solution.py:795
  123.1 9.6 collective-permute-done.24
  132.9 25.1 %collective-permute-done.20 = bf16[2,8,48,384]{3,2,1,0:T(8,128)(2,1)S(1)} collective-permute-done((bf16[2,8,48,384]{3,2,1,0:T(8,128)(2,1)S(1)}, bf16[2,8,48,384]{3,2,1,0:T(8,128)(2,1)S(1)}, u32[]{:S(2)}, u32[]{:S(2)}) %collective-permute-start.20) | collective-permute-done | bytes 589856 | tf_op jit(solution)/shard_map/ppermute | solution.py:1013
  162.1 25.6 %collective-permute-done.25.refs_3_ = bf16[4,8,48,384]{3,2,1,0:T(8,128)(2,1)} collective-permute-done((bf16[4,8,48,384]{3,2,1,0:T(8,128)(2,1)S(1)}, bf16[4,8,48,384]{3,2,1,0:T(8,128)(2,1)}, u32[]{:S(2)}, u32[]{:S(2)}) %collective-permute-start.25) | collective-permute-done | bytes 1179680 | tf_op jit(solution)/shard_map/ppermute | solution.py:1013
  192.4 287.9 %shard_map.195 = bf16[8,2,16,48,384]{4,3,2,1,0:T(8,128)(2,1)} custom-call(s32[5]{0:T(128)} %stack.110.me_ref, bf16[4,8,48,384]{3,2,1,0:T(8,128)(2,1)} %copy-done.24, bf16[4,8,48,384]{3,2,1,0:T(8,128)(2,1)} %copy-done.29, bf16[4,8,48,384]{3,2,1,0:T(8,128)(2,1)} %copy-done.21, bf16[4,8,48,384]{3,2,1,0:T(8,128)(2,1)} %copy-done.28, ...), custom_call_target="tpu_custom_call" | custom-call | bytes 18874368 | tf_op jit(solution)/shard_map/pallas_call | solution.py:863
  481.1 12.3 shard_map.196
  496.1 12.5 collective-permute-start
  508.6 287.9 %shard_map.198 = bf16[8,2,16,48,384]{4,3,2,1,0:T(8,128)(2,1)} custom-call(s32[5]{0:T(128)} %stack.110.me_ref, bf16[4,8,48,384]{3,2,1,0:T(8,128)(2,1)} %copy-done.23, bf16[4,8,48,384]{3,2,1,0:T(8,128)(2,1)} %collective-permute-done.21.refs_1_, bf16[4,8,48,384]{3,2,1,0:T(8,128)(2,1)} %copy-done.22, bf16[4,8,48,384]{3,2,1,0:T(8,128)(2,1)} %collective-permute-done.25.refs_3_, ...), custom_call_target="tpu_custom_call" | custom-call | bytes 18874368 | tf_op jit(solution)/shard_map/pallas_call | solution.py:863
  800.9 9.3 shard_map.197
  810.2 9.9 shard_map.199
  820.1 13.2 %shard_map.200 = (f32[416,768]{1,0:T(8,128)}, bf16[104,768]{1,0:T(8,128)(2,1)}, bf16[104,768]{1,0:T(8,128)(2,1)}, bf16[104,768]{1,0:T(8,128)(2,1)}, bf16[104,768]{1,0:T(8,128)(2,1)}) custom-call(f32[416,768]{1,0:T(8,128)} %get-tuple-element.209.x2_ref, bf16[8,2,768,384]{3,2,1,0:T(8,128)(2,1)} %bitcast.216, bf16[8,2,768,384]{3,2,1,0:T(8,128)(2,1)} %bitcast.217, ...), custom_call_target="tpu_custom_call" | custom-call | flops 3925868544 | bytes 22106132 | tf_op jit(solution)/shard_map/pallas_call | solution.py:194
  846.1 12.2 shard_map.201
  868.7 9.3 shard_map.202
  878.0 9.9 shard_map.203
  887.9 25.7 %shard_map.204 = (f32[416,768]{1,0:T(8,128)}, bf16[4,2,2,192,384]{4,3,2,1,0:T(8,128)(2,1)}, bf16[4,2,2,192,384]{4,3,2,1,0:T(8,128)(2,1)}, bf16[4,2,2,192,384]{4,...) custom-call(s32[5]{0:T(128)} %stack.110.me_ref, ...), custom_call_target="tpu_custom_call" | custom-call | flops 9814671360 | bytes 33447956 | tf_op jit(solution)/shard_map/pallas_call | solution.py:194
  914.4 21.6 %shard_map.205 = (f32[416,768]{1,0:T(8,128)}, bf16[4,2,2,192,384]{4,3,2,1,0:T(8,128)(2,1)}, bf16[4,2,2,192,384]{4,3,2,1,0:T(8,128)(2,1)}, f32[2,768]{1,0:T(2,128)}) custom-call(s32[5]{0:T(128)} %stack.110.me_ref, f32[416,768]{1,0:T(8,128)} %get-tuple-element.224.g_ref, f32[416,768]{1,0:T(8,128)} %get-tuple-element.221.x1_ref, ...), custom_call_target="tpu_custom_call" | custom-call | flops 3925868544 | bytes 32386580 | tf_op jit(solution)/shard_map/pallas_call | solution.py:194
  948.2 7.8 shard_map.207
  955.9 9.3 collective-permute-start.39
  983.3 18.3 %shard_map.209 = (bf16[104,768]{1,0:T(8,128)(2,1)}, bf16[104,768]{1,0:T(8,128)(2,1)}, bf16[104,768]{1,0:T(8,128)(2,1)}, bf16[104,768]{1,0:T(8,128)(2,1)}, bf16[1...) custom-call(s32[5]{0:T(128)} %stack.110.me_ref, ...), custom_call_target="tpu_custom_call" | custom-call | flops 2944401408 | bytes 18009620 | tf_op jit(solution)/shard_map/pallas_call | solution.py:194
  1004.4 14.5 %collective-permute-start.48 = (bf16[104,768]{1,0:T(8,128)(2,1)}, bf16[104,768]{1,0:T(8,128)(2,1)S(1)}, u32[]{:S(2)}, u32[]{:S(2)}) collective-permute-start(bf16[104,768]{1,0:T(8,128)(2,1)} %get-tuple-element.263), channel_id=1, source_target_pairs={{0,2},{2,0},{4,6},{6,4},{8,10},{10,8},{12,14},{14,12},{16,18},{18,... | collective-permute-start | bytes 479240 | tf_op jit(solution)/shard_map/ppermute | solution.py:795
  1033.6 22.7 %shard_map.212 = (f32[416,768]{1,0:T(8,128)}, bf16[4,2,2,192,384]{4,3,2,1,0:T(8,128)(2,1)}, bf16[4,2,2,192,384]{4,3,2,1,0:T(8,128)(2,1)}, bf16[4,2,2,192,384]{4,...) custom-call(s32[5]{0:T(128)} %stack.110.me_ref, f32[416,768]{1,0:T(8,128)} %get-tuple-element.282.g_ref, ...), custom_call_target="tpu_custom_call" | custom-call | flops 9814671360 | bytes 32170004 | tf_op jit(solution)/shard_map/pallas_call | solution.py:194
  1062.5 21.6 %shard_map.214 = (f32[416,768]{1,0:T(8,128)}, bf16[4,2,2,192,384]{4,3,2,1,0:T(8,128)(2,1)}, bf16[4,2,2,192,384]{4,3,2,1,0:T(8,128)(2,1)}, f32[2,768]{1,0:T(2,128)}) custom-call(s32[5]{0:T(128)} %stack.110.me_ref, f32[416,768]{1,0:T(8,128)} %get-tuple-element.292.g_ref, f32[416,768]{1,0:T(8,128)} %get-tuple-element.208.x1_ref, ...), custom_call_target="tpu_custom_call" | custom-call | flops 3925868544 | bytes 32386580 | tf_op jit(solution)/shard_map/pallas_call | solution.py:194
  1086.7 7.7 collective-permute-done.57.refs_17_
  1103.8 7.8 shard_map.216
  1113.5 16.2 %collective-permute-done.63.refs_2_ = bf16[8,192,384]{2,1,0:T(8,128)(2,1)S(1)} collective-permute-done((bf16[8,192,384]{2,1,0:T(8,128)(2,1)}, bf16[8,192,384]{2,1,0:T(8,128)(2,1)S(1)}, u32[]{:S(2)}, u32[]{:S(2)}) %collective-permute-start.63) | collective-permute-done | bytes 1179680 | tf_op jit(solution)/shard_map/ppermute | solution.py:1013
  1139.4 18.4 %shard_map.218 = (bf16[104,768]{1,0:T(8,128)(2,1)}, bf16[104,768]{1,0:T(8,128)(2,1)}, bf16[104,768]{1,0:T(8,128)(2,1)}, bf16[104,768]{1,0:T(8,128)(2,1)}, bf16[1...) custom-call(s32[5]{0:T(128)} %stack.110.me_ref, ...), custom_call_target="tpu_custom_call" | custom-call | flops 2944401408 | bytes 18009620 | tf_op jit(solution)/shard_map/pallas_call | solution.py:194
  1209.2 13.8 %all-to-all-done.3 = f32[32,1,384]{2,1,0:T(1,128)} async-done(((f32[32,1,384]{2,1,0:T(1,128)}), f32[32,1,384]{2,1,0:T(1,128)}, u32[]{:S(2)}, u32[]{:S(2)}) %all-to-all-start.3) | async-done | bytes 49184 | tf_op jit(solution)/shard_map/all_to_all | solution.py:1101
  1256.4 13.2 %all-to-all-done.1 = bf16[4,5,48,384]{3,2,1,0:T(8,128)(2,1)S(1)} async-done(((bf16[4,5,48,384]{3,2,1,0:T(8,128)(2,1)}), bf16[4,5,48,384]{3,2,1,0:T(8,128)(2,1)S(1)}, u32[]{:S(2)}, u32[]{:S(2)}) %all-to-all-start.1) | async-done | bytes 737312 | tf_op jit(solution)/shard_map/all_to_all | solution.py:1039
  (464 shorter events, 250.6 us)
Async XLA Ops:
  7.2 473.2 %all-gather.3.cloned.1.call-start = ((), (), s32[]{:S(2)}) async-start(), calls=%async_computation.8 | async-start | bytes 10948608 | tf_op jit(solution)/shard_map/all_gather | solution.py:824
  11.0 827.2 %all-gather.5.cloned.1.call-start = ((), (), s32[]{:S(2)}) async-start(), calls=%async_computation.9 | async-start | bytes 10948608 | tf_op jit(solution)/shard_map/all_gather | solution.py:824
  17.2 38.7 %collective-permute-start.9 = (bf16[8,48,384]{2,1,0:T(8,128)(2,1)S(1)}, bf16[8,48,384]{2,1,0:T(8,128)(2,1)S(1)}, u32[]{:S(2)}, u32[]{:S(2)}) collective-permute-start(bf16[8,48,384]{2,1,0:T(8,128)(2,1)S(1)} %get-tuple-element.434), channel_id=1, source_target_pairs={{0,4},{2,6},{4,0},{6,2},{1,5},{3,7},{5,1},{7,3},{8,12},{10,14},{12... | collective-permute-start | bytes 884744 | tf_op jit(solution)/shard_map/ppermute | solution.py:833
  17.2 60.0 %collective-permute-start.5 = (bf16[8,48,384]{2,1,0:T(8,128)(2,1)S(1)}, bf16[8,48,384]{2,1,0:T(8,128)(2,1)S(1)}, u32[]{:S(2)}, u32[]{:S(2)}) collective-permute-start(bf16[8,48,384]{2,1,0:T(8,128)(2,1)S(1)} %get-tuple-element.434), channel_id=1, source_target_pairs={{0,2},{2,4},{4,6},{6,0},{1,3},{3,5},{5,7},{7,1},{8,10},{10,12},{12... | collective-permute-start | bytes 884744 | tf_op jit(solution)/shard_map/ppermute | solution.py:833
  18.2 67.4 %collective-permute-start.1 = (bf16[1,2,196,768]{3,1,2,0:T(2,128)(2,1)}, bf16[1,2,196,768]{3,1,2,0:T(2,128)(2,1)}, u32[]{:S(2)}, u32[]{:S(2)}) collective-permute-start(bf16[1,2,196,768]{3,1,2,0:T(2,128)(2,1)} %param.11), channel_id=1, source_target_pairs={{0,0},{2,8},{4,2},{6,10},{8,4},{10,12},{12,6},{14,14},{16,16},{18,... | collective-permute-start | bytes 1806344 | tf_op jit(solution)/shard_map/ppermute | solution.py:773
  55.9 32.3 %collective-permute-start.10 = (bf16[2,8,48,384]{3,2,1,0:T(8,128)(2,1)S(1)}, bf16[2,8,48,384]{3,2,1,0:T(8,128)(2,1)}, u32[]{:S(2)}, u32[]{:S(2)}) collective-permute-start(bf16[2,8,48,384]{3,2,1,0:T(8,128)(2,1)S(1)} %pad_maximum_fusion.5), channel_id=1, source_target_pairs={{0,1},{1,0},{2,3},{3,2},{4,5},{5,4},{6,7},{7,6},{8,9},{9,8},{10,11... | collective-permute-start | bytes 1769480 | tf_op jit(solution)/shard_map/ppermute | solution.py:1013
  60.9 1115.7 %reduce-scatter.7.cloned.1.call-start = ((), (), s32[]{:S(2)}) async-start(), calls=%async_computation.11 | async-start | bytes 737280 | tf_op jit(solution)/shard_map/reduce_scatter | solution.py:1042
  65.4 38.4 %collective-permute-start.19 = (bf16[8,48,384]{2,1,0:T(8,128)(2,1)}, bf16[8,48,384]{2,1,0:T(8,128)(2,1)S(1)}, u32[]{:S(2)}, u32[]{:S(2)}) collective-permute-start(bf16[8,48,384]{2,1,0:T(8,128)(2,1)} %get-tuple-element.428), channel_id=1, source_target_pairs={{0,2},{2,4},{4,6},{6,0},{1,3},{3,5},{5,7},{7,1},{8,10},{10,12},{12... | collective-permute-start | bytes 884744 | tf_op jit(solution)/shard_map/ppermute | solution.py:833
  89.4 69.6 %collective-permute-start.14 = (bf16[4,8,48,384]{3,2,1,0:T(8,128)(2,1)S(1)}, bf16[4,8,48,384]{3,2,1,0:T(8,128)(2,1)S(1)}, u32[]{:S(2)}, u32[]{:S(2)}) collective-permute-start(bf16[4,8,48,384]{3,2,1,0:T(8,128)(2,1)S(1)} %pad_maximum_fusion.1.refs_2_), channel_id=1, source_target_pairs={{0,8},{8,0},{16,24},{24,16},{1,9},{9,1},{17,25},{25,17},{2,10},{10... | collective-permute-start | bytes 3538952 | tf_op jit(solution)/shard_map/ppermute | solution.py:1013
  89.5 71.0 %collective-permute-start.11 = (bf16[4,8,48,384]{3,2,1,0:T(8,128)(2,1)S(1)}, bf16[4,8,48,384]{3,2,1,0:T(8,128)(2,1)S(1)}, u32[]{:S(2)}, u32[]{:S(2)}) collective-permute-start(bf16[4,8,48,384]{3,2,1,0:T(8,128)(2,1)S(1)} %pad_maximum_fusion.1.refs_2_), channel_id=1, source_target_pairs={{0,16},{8,24},{16,0},{24,8},{1,17},{9,25},{17,1},{25,9},{2,18},{10... | collective-permute-start | bytes 3538952 | tf_op jit(solution)/shard_map/ppermute | solution.py:1013
  105.6 52.4 %collective-permute-start.20 = (bf16[2,8,48,384]{3,2,1,0:T(8,128)(2,1)S(1)}, bf16[2,8,48,384]{3,2,1,0:T(8,128)(2,1)S(1)}, u32[]{:S(2)}, u32[]{:S(2)}) collective-permute-start(bf16[2,8,48,384]{3,2,1,0:T(8,128)(2,1)S(1)} %pad_maximum_fusion.6), channel_id=1, source_target_pairs={{0,16},{8,24},{16,0},{24,8},{1,17},{9,25},{17,1},{25,9},{2,18},{10... | collective-permute-start | bytes 1769480 | tf_op jit(solution)/shard_map/ppermute | solution.py:1013
  121.6 39.9 %collective-permute-start.7 = (bf16[4,8,48,384]{3,2,1,0:T(8,128)(2,1)S(1)}, bf16[4,8,48,384]{3,2,1,0:T(8,128)(2,1)S(1)}, u32[]{:S(2)}, u32[]{:S(2)}) collective-permute-start(bf16[4,8,48,384]{3,2,1,0:T(8,128)(2,1)S(1)} %pad_maximum_fusion.refs_0_), channel_id=1, source_target_pairs={{0,1},{1,0},{2,3},{3,2},{4,5},{5,4},{6,7},{7,6},{8,9},{9,8},{10,11... | collective-permute-start | bytes 3538952 | tf_op jit(solution)/shard_map/ppermute | solution.py:1013
  158.0 29.7 %collective-permute-start.25 = (bf16[4,8,48,384]{3,2,1,0:T(8,128)(2,1)S(1)}, bf16[4,8,48,384]{3,2,1,0:T(8,128)(2,1)}, u32[]{:S(2)}, u32[]{:S(2)}) collective-permute-start(bf16[4,8,48,384]{3,2,1,0:T(8,128)(2,1)S(1)} %pad_maximum_fusion.3.refs_2_), channel_id=1, source_target_pairs={{0,16},{8,24},{16,0},{24,8},{1,17},{9,25},{17,1},{25,9},{2,18},{10... | collective-permute-start | bytes 3538952 | tf_op jit(solution)/shard_map/ppermute | solution.py:1013
  159.0 30.1 %collective-permute-start.21 = (bf16[4,8,48,384]{3,2,1,0:T(8,128)(2,1)S(1)}, bf16[4,8,48,384]{3,2,1,0:T(8,128)(2,1)}, u32[]{:S(2)}, u32[]{:S(2)}) collective-permute-start(bf16[4,8,48,384]{3,2,1,0:T(8,128)(2,1)S(1)} %pad_maximum_fusion.2.refs_0_), channel_id=1, source_target_pairs={{0,1},{1,0},{2,3},{3,2},{4,5},{5,4},{6,7},{7,6},{8,9},{9,8},{10,11... | collective-permute-start | bytes 3538952 | tf_op jit(solution)/shard_map/ppermute | solution.py:1013
  161.6 332.2 %collective-permute-start.28 = (bf16[4,8,48,384]{3,2,1,0:T(8,128)(2,1)S(1)}, bf16[4,8,48,384]{3,2,1,0:T(8,128)(2,1)}, u32[]{:S(2)}, u32[]{:S(2)}) collective-permute-start(bf16[4,8,48,384]{3,2,1,0:T(8,128)(2,1)S(1)} %pad_maximum_fusion.3.refs_2_), channel_id=1, source_target_pairs={{0,8},{8,0},{16,24},{24,16},{1,9},{9,1},{17,25},{25,17},{2,10},{10... | collective-permute-start | bytes 3538952 | tf_op jit(solution)/shard_map/ppermute | solution.py:1013
  187.7 306.3 %collective-permute-start.26 = (bf16[4,8,48,384]{3,2,1,0:T(8,128)(2,1)S(1)}, bf16[4,8,48,384]{3,2,1,0:T(8,128)(2,1)}, u32[]{:S(2)}, u32[]{:S(2)}) collective-permute-start(bf16[4,8,48,384]{3,2,1,0:T(8,128)(2,1)S(1)} %pad_maximum_fusion.2.refs_0_), channel_id=1, source_target_pairs={{0,8},{8,0},{16,24},{24,16},{1,9},{9,1},{17,25},{25,17},{2,10},{10... | collective-permute-start | bytes 3538952 | tf_op jit(solution)/shard_map/ppermute | solution.py:1013
  189.2 306.9 %collective-permute-start.29 = (bf16[4,8,48,384]{3,2,1,0:T(8,128)(2,1)}, bf16[4,8,48,384]{3,2,1,0:T(8,128)(2,1)}, u32[]{:S(2)}, u32[]{:S(2)}) collective-permute-start(bf16[4,8,48,384]{3,2,1,0:T(8,128)(2,1)} %collective-permute-done.25.refs_3_), channel_id=1, source_target_pairs={{0,8},{8,0},{16,24},{24,16},{1,9},{9,1},{17,25},{25,17},{2,10},{10... | collective-permute-start | bytes 3538952 | tf_op jit(solution)/shard_map/ppermute | solution.py:1013
  189.2 319.4 %collective-permute-start.27 = (bf16[4,8,48,384]{3,2,1,0:T(8,128)(2,1)}, bf16[4,8,48,384]{3,2,1,0:T(8,128)(2,1)}, u32[]{:S(2)}, u32[]{:S(2)}) collective-permute-start(bf16[4,8,48,384]{3,2,1,0:T(8,128)(2,1)} %collective-permute-done.21.refs_1_), channel_id=1, source_target_pairs={{0,8},{8,0},{16,24},{24,16},{1,9},{9,1},{17,25},{25,17},{2,10},{10... | collective-permute-start | bytes 3538952 | tf_op jit(solution)/shard_map/ppermute | solution.py:1013
  190.7 289.6 %collective-permute-start.4 = (bf16[104,768]{1,0:T(8,128)(2,1)S(1)}, bf16[104,768]{1,0:T(8,128)(2,1)S(1)}, u32[]{:S(2)}, u32[]{:S(2)}) collective-permute-start(bf16[104,768]{1,0:T(8,128)(2,1)S(1)} %copy-done.83), channel_id=1, source_target_pairs={{0,10},{2,8},{4,14},{6,12},{8,2},{10,0},{12,6},{14,4},{16,26},{18,... | collective-permute-start | bytes 479240 | tf_op jit(solution)/shard_map/ppermute | solution.py:795
  493.3 306.8 %collective-permute-start.16 = (bf16[104,768]{1,0:T(8,128)(2,1)}, bf16[104,768]{1,0:T(8,128)(2,1)S(1)}, u32[]{:S(2)}, u32[]{:S(2)}) collective-permute-start(bf16[104,768]{1,0:T(8,128)(2,1)} %get-tuple-element.203), channel_id=1, source_target_pairs={{0,8},{2,10},{4,12},{6,14},{8,0},{10,2},{12,4},{14,6},{16,24},{18,... | collective-permute-start | bytes 479240 | tf_op jit(solution)/shard_map/ppermute | solution.py:795
  493.8 306.4 %collective-permute-start.17 = (bf16[104,768]{1,0:T(8,128)(2,1)}, bf16[104,768]{1,0:T(8,128)(2,1)S(1)}, u32[]{:S(2)}, u32[]{:S(2)}) collective-permute-start(bf16[104,768]{1,0:T(8,128)(2,1)} %get-tuple-element.204), channel_id=1, source_target_pairs={{0,2},{2,0},{4,6},{6,4},{8,10},{10,8},{12,14},{14,12},{16,18},{18,... | collective-permute-start | bytes 479240 | tf_op jit(solution)/shard_map/ppermute | solution.py:795
  494.0 306.2 %collective-permute-start.18 = (bf16[104,768]{1,0:T(8,128)(2,1)}, bf16[104,768]{1,0:T(8,128)(2,1)S(1)}, u32[]{:S(2)}, u32[]{:S(2)}) collective-permute-start(bf16[104,768]{1,0:T(8,128)(2,1)} %get-tuple-element.205), channel_id=1, source_target_pairs={{0,10},{2,8},{4,14},{6,12},{8,2},{10,0},{12,6},{14,4},{16,26},{18,... | collective-permute-start | bytes 479240 | tf_op jit(solution)/shard_map/ppermute | solution.py:795
  496.1 342.0 %collective-permute-start = (bf16[1,2,196,768]{3,1,2,0:T(2,128)(2,1)S(1)}, bf16[1,2,196,768]{3,1,2,0:T(2,128)(2,1)S(1)}, u32[]{:S(2)}, u32[]{:S(2)}) collective-permute-start(bf16[1,2,196,768]{3,1,2,0:T(2,128)(2,1)S(1)} %copy-done.80), channel_id=1, source_target_pairs={{0,0},{2,8},{4,2},{6,10},{8,4},{10,12},{12,6},{14,14},{16,16},{18,... | collective-permute-start | bytes 1806344 | tf_op jit(solution)/shard_map/ppermute | solution.py:773
  936.0 29.2 %collective-permute-start.44 = (bf16[4,2,2,192,384]{4,3,2,1,0:T(8,128)(2,1)}, bf16[4,2,2,192,384]{4,3,2,1,0:T(8,128)(2,1)S(1)}, u32[]{:S(2)}, u32[]{:S(2)}) collective-permute-start(bf16[4,2,2,192,384]{4,3,2,1,0:T(8,128)(2,1)} %get-tuple-element.245), channel_id=1, source_target_pairs={{0,8},{8,0},{16,24},{24,16},{1,9},{9,1},{17,25},{25,17},{2,10},{10... | collective-permute-start | bytes 7077896 | tf_op jit(solution)/shard_map/ppermute | solution.py:1013
  1026.8 30.1 %collective-permute-start.54 = (bf16[6,192,384]{2,1,0:T(8,128)(2,1)}, bf16[6,192,384]{2,1,0:T(8,128)(2,1)S(1)}, u32[]{:S(2)}, u32[]{:S(2)}) collective-permute-start(bf16[6,192,384]{2,1,0:T(8,128)(2,1)} %get-tuple-element.284), channel_id=1, source_target_pairs={{0,1},{1,0},{2,3},{3,2},{4,5},{5,4},{6,7},{7,6},{8,9},{9,8},{10,11... | collective-permute-start | bytes 2654216 | tf_op jit(solution)/shard_map/ppermute | solution.py:1013
  1056.3 41.0 %collective-permute-start.58 = (bf16[4,2,2,192,384]{4,3,2,1,0:T(8,128)(2,1)}, bf16[4,2,2,192,384]{4,3,2,1,0:T(8,128)(2,1)}, u32[]{:S(2)}, u32[]{:S(2)}) collective-permute-start(bf16[4,2,2,192,384]{4,3,2,1,0:T(8,128)(2,1)} %get-tuple-element.301), channel_id=1, source_target_pairs={{0,8},{8,0},{16,24},{24,16},{1,9},{9,1},{17,25},{25,17},{2,10},{10... | collective-permute-start | bytes 7077896 | tf_op jit(solution)/shard_map/ppermute | solution.py:1013
  1056.4 40.9 %collective-permute-start.59 = (bf16[4,2,2,192,384]{4,3,2,1,0:T(8,128)(2,1)}, bf16[4,2,2,192,384]{4,3,2,1,0:T(8,128)(2,1)}, u32[]{:S(2)}, u32[]{:S(2)}) collective-permute-start(bf16[4,2,2,192,384]{4,3,2,1,0:T(8,128)(2,1)} %get-tuple-element.303), channel_id=1, source_target_pairs={{0,8},{8,0},{16,24},{24,16},{1,9},{9,1},{17,25},{25,17},{2,10},{10... | collective-permute-start | bytes 7077896 | tf_op jit(solution)/shard_map/ppermute | solution.py:1013
  1062.4 131.4 %reduce-scatter.11.cloned.1.call-start = ((), (), s32[]{:S(2)}) async-start(), calls=%async_computation.13 | async-start | bytes 1474560 | tf_op jit(solution)/shard_map/reduce_scatter | solution.py:1042
  1084.3 144.6 %reduce-scatter.5.cloned.1.call-start = ((), (), s32[]{:S(2)}) async-start(), calls=%async_computation.10 | async-start | bytes 921600 | tf_op jit(solution)/shard_map/reduce_scatter | solution.py:1042
  1139.3 114.1 %reduce-scatter.9.cloned.1.call-start = ((), (), s32[]{:S(2)}) async-start(), calls=%async_computation.12 | async-start | bytes 1474560 | tf_op jit(solution)/shard_map/reduce_scatter | solution.py:1042
  1175.0 29.0 %collective-permute-start.77 = (bf16[8,192,384]{2,1,0:T(8,128)(2,1)}, bf16[8,192,384]{2,1,0:T(8,128)(2,1)S(1)}, u32[]{:S(2)}, u32[]{:S(2)}) collective-permute-start(bf16[8,192,384]{2,1,0:T(8,128)(2,1)} %get-tuple-element.359), channel_id=1, source_target_pairs={{0,16},{8,24},{16,0},{24,8},{1,17},{9,25},{17,1},{25,9},{2,18},{10... | collective-permute-start | bytes 3538952 | tf_op jit(solution)/shard_map/ppermute | solution.py:1013
  1189.1 33.9 %all-to-all-start.3 = ((f32[32,1,384]{2,1,0:T(1,128)}), f32[32,1,384]{2,1,0:T(1,128)}, u32[]{:S(2)}, u32[]{:S(2)}) async-start(f32[32,1,384]{2,1,0:T(1,128)} %copy.131), calls=%async_computation.7 | async-start | bytes 98304 | tf_op jit(solution)/shard_map/all_to_all | solution.py:1101
  (143 other events, 2047.3 us)
Sparse Core Ops, SparseCore 0:
  11.7 146.3 all-gather.2
  161.7 89.0 all-gather.4
  1062.6 19.7 reduce-scatter.6
  1084.5 27.6 reduce-scatter.10
  1139.4 21.8 reduce-scatter.4
  1186.5 35.4 reduce-scatter.8

commit v10 on v9

--- a/solution.py
+++ b/solution.py
@@ -825,21 +825,27 @@
     return full.reshape(pack.shape[0], lax.axis_size("head"), -1, pack.shape[2])
 
 
-def spread_slabs(pack, me):
+def spread_steps(pack, me):
     ways, clips = lax.axis_size("seq"), lax.axis_size("clip")
     shares = lax.axis_size("head")
     n, r, width = pack.shape
+    pack = yield pack
     turned = [pack] + [
         lax.ppermute(pack, "seq", [(i, (i + k) % ways) for i in range(ways)]) for k in range(1, ways)
     ]
+    turned = yield turned
+    orders = (((0, 1), "x", "h"), ((3, 2), "h", "x"))
+    some = [jnp.stack([turned[k] for k in steps]) for steps, _, _ in orders]
+    come = yield [cross(a, first) for a, (_, first, _) in zip(some, orders)]
+    some = [jnp.concatenate(pair, axis=0) for pair in zip(some, come)]
+    come = yield [cross(a, second) for a, (_, _, second) in zip(some, orders)]
     runs = []
-    for steps, first, second in (((0, 1), "x", "h"), ((3, 2), "h", "x")):
-        some = jnp.stack([turned[k] for k in steps])
-        some = jnp.concatenate((some, cross(some, first)), axis=0)
+    for mine, other, (steps, first, second) in zip(some, come, orders):
         where = [(k, {first: f}) for f in (0, 1) for k in steps]
-        for g, blocks in enumerate((some, cross(some, second))):
+        for g, blocks in enumerate((mine, other)):
             runs.append((blocks, [(k, {**at, second: g}) for k, at in where], 0))
-    runs += [(cross(blocks, "c"), where, 1) for blocks, where, _ in runs]
+    come = yield [cross(blocks, "c") for blocks, _, _ in runs]
+    runs += [(far, where, 1) for far, (_, where, _) in zip(come, runs)]
     count = sum(len(where) for _, where, _ in runs)
 
     def body(me_ref, *refs):
@@ -864,14 +870,33 @@
         body,
         out_shape=jax.ShapeDtypeStruct((n, shares, clips * ways, r, width), BF16),
         in_specs=[SCALARS] + [pl.BlockSpec(memory_space=pltpu.HBM)] * len(runs),
-        out_specs=pl.BlockSpec(memory_space=pltpu.HBM),
+        out_specs=pl.BlockSpec(memory_space=pltpu.VMEM),
         scratch_shapes=[pltpu.SemaphoreType.DMA((count,))],
         compiler_params=pltpu.CompilerParams(vmem_limit_bytes=VMEM),
         cost_estimate=pl.CostEstimate(
             flops=0, bytes_accessed=4 * n * shares * clips * ways * r * width, transcendentals=0
         ),
     )(me, *(blocks for blocks, _, _ in runs))
-    return full.reshape(n, shares, clips * ways * r, width)
+    yield full.reshape(n, shares, clips * ways * r, width)
+
+
+def spread_slabs(pack, me):
+    way = spread_steps(pack, me)
+    come = next(way)
+    for _ in range(5):
+        come = way.send(come)
+    return come
+
+
+class Spread:
+    def __init__(self, pack, me):
+        self.way = spread_steps(pack, me)
+        self.come = next(self.way)
+
+    def step(self, x):
+        x, come = lax.optimization_barrier((x, self.come))
+        self.come = self.way.send(come)
+        return x
 
 
 def mix_whole(slab, shards):
@@ -1149,7 +1174,7 @@
         jnp.int32
     )
     if quick:
-        weights_ff = [spread_slabs(pack, me) for pack in packs_ff]
+        weights_ff = [spread_slabs(packs_ff[0], me)]
     else:
         weights_ff = [gather_slabs(pack) for pack in packs_ff]
 
@@ -1159,14 +1184,25 @@
     for l in range(layers):
         w = weights[l]
         send = swap_places(send)
-        if quick and l == 0:
-            send, weights_ff[l] = lax.optimization_barrier((send, weights_ff[l]))
+        if quick:
+            if l + 1 < layers:
+                send, weights_ff[l] = lax.optimization_barrier((send, weights_ff[l]))
+                spread = Spread(packs_ff[l + 1], me)
+                send, w = spread.step((send, w))
+            else:
+                send = spread.step(send)
         a1, qkv1, log1, o1_time = time_forward(rows, send, w)
         back = swap_places(o1_time)
+        if quick:
+            back = spread.step(back)
         o1, y1, x1, qkv2 = middle_forward(rows, back, x, w, mixes[l], gb[l], me)
-        if quick and l == 0:
-            x1, weights_ff[1:] = lax.optimization_barrier((x1, weights_ff[1:]))
         o2, x2, log2 = space_forward(rows, qkv2, x1, w)
+        if quick:
+            if l + 1 == layers:
+                weights_ff.append(spread.come)
+                x2, weights_ff[l] = lax.optimization_barrier((x2, weights_ff[l]))
+            else:
+                x2 = spread.step(x2)
         kept.append((x, a1, qkv1, log1, o1, y1, x1, qkv2, o2, log2, x2))
         if l + 1 < layers:
             x, *send = mlp_forward(rows, x2, weights_ff[l], gb[l], gb[l + 1], me)

time: 1290 us -> 750 us (0.58)
  Pallas kernels: 853 us -> 294 us
  waiting for transfers between devices: 215 us -> 236 us
    pallas_call x2, Pallas kernels: 576 us -> 16.5 us  [spread_steps(): pl.pallas_call(body, out_shape=jax.ShapeDtypeStruct((n, shares, clips * w...]
    ppermute x24, waiting for transfers between devices: 23.4 us -> 50.3 us  [swap_places(): got.append(lax.ppermute(chunks[k], ('clip', 'seq'), pairs))]
    ppermute x24, starting transfers between devices: 41.2 us -> 58.7 us  [swap_places(): got.append(lax.ppermute(chunks[k], ('clip', 'seq'), pairs))]
  transfers between devices with their start and end apart: 90 -> 90, of which waited for: 28 -> 29; matrix products, arithmetic and copies ran while one was open for 3% -> 6% of each run, Pallas kernels for 62% -> 32%
where the time goes in v10:
time: 750 us; the launch traced here: 744 us
  Pallas kernels  294 us (39%)
  waiting for transfers between devices  236 us (31%)
  starting transfers between devices  133 us (18%)
  local copies, waits for them, and re-layouts  46.7 us (6%)
  other arithmetic  17.8 us (2%)
  between operations  15.8 us (2%)
    pallas_call x18, Pallas kernels, call(): pl.pallas_call(body, out_shape=[shape for shape, _ in outs], grid=grid, i...  232 us
    ppermute x46, waiting for transfers between devices, cross(): return lax.ppermute(a, axis, [(i, i ^ 1 << bit) for i in range(size)])  109 us
    ppermute x24, starting transfers between devices, swap_places(): got.append(lax.ppermute(chunks[k], ('clip', 'seq'), pairs))  58.7 us
    ppermute x24, waiting for transfers between devices, swap_places(): got.append(lax.ppermute(chunks[k], ('clip', 'seq'), pairs))  50.3 us
    pallas_call x9, Pallas kernels, fold(): pl.pallas_call(body, out_shape=[jax.ShapeDtypeStruct(shape, BF16) for sha...  45.4 us
    ppermute x46, starting transfers between devices, cross(): return lax.ppermute(a, axis, [(i, i ^ 1 << bit) for i in range(size)])  38.6 us
    ppermute x6, waiting for transfers between devices, spread_steps(): lax.ppermute(pack, 'seq', [(i, (i + k) % ways) for i in range(ways)])  31.6 us
    unnamed x167, local copies, waits for them, and re-layouts  22.2 us
  transfers between devices with their start and end apart: 90, of which 29 were waited for; matrix products, arithmetic and copies ran while one was open for 6% of the time, Pallas kernels for 32%

profile of v10, /device:TPU:0, one launch (start us, length us, event | category | flops | bytes accessed | tf_op | source)
XLA Modules:
  0.0 743.6 jit_solution(16404253036049575209)
XLA Ops:
  19.5 8.5 %collective-permute-done.8 = bf16[8,48,384]{2,1,0:T(8,128)(2,1)S(1)} collective-permute-done((bf16[8,48,384]{2,1,0:T(8,128)(2,1)S(1)}, bf16[8,48,384]{2,1,0:T(8,128)(2,1)S(1)}, u32[]{:S(2)}, u32[]{:S(2)}) %collective-permute-start.8) | collective-permute-done | bytes 294944 | tf_op jit(solution)/shard_map/ppermute | solution.py:834
  28.0 22.8 %collective-permute-done.9 = bf16[8,48,384]{2,1,0:T(8,128)(2,1)S(1)} collective-permute-done((bf16[8,48,384]{2,1,0:T(8,128)(2,1)S(1)}, bf16[8,48,384]{2,1,0:T(8,128)(2,1)S(1)}, u32[]{:S(2)}, u32[]{:S(2)}) %collective-permute-start.9) | collective-permute-done | bytes 294944 | tf_op jit(solution)/shard_map/ppermute | solution.py:834
  54.0 15.7 %collective-permute-done.10 = bf16[2,8,48,384]{3,2,1,0:T(8,128)(2,1)S(1)} collective-permute-done((bf16[2,8,48,384]{3,2,1,0:T(8,128)(2,1)S(1)}, bf16[2,8,48,384]{3,2,1,0:T(8,128)(2,1)S(1)}, u32[]{:S(2)}, u32[]{:S(2)}) %collective-permute-start.10) | collective-permute-done | bytes 589856 | tf_op jit(solution)/shard_map/ppermute | solution.py:1038
  79.1 34.6 %collective-permute-done.11.refs_3_ = bf16[4,8,48,384]{3,2,1,0:T(8,128)(2,1)S(1)} collective-permute-done((bf16[4,8,48,384]{3,2,1,0:T(8,128)(2,1)S(1)}, bf16[4,8,48,384]{3,2,1,0:T(8,128)(2,1)S(1)}, u32[]{:S(2)}, u32[]{:S(2)}) %collective-permute-start.11) | collective-permute-done | bytes 1179680 | tf_op jit(solution)/shard_map/ppermute | solution.py:1038
  126.7 17.5 %all-to-all-done = f32[32,1,384]{2,1,0:T(1,128)} async-done(((f32[32,1,384]{2,1,0:T(1,128)}), f32[32,1,384]{2,1,0:T(1,128)}, u32[]{:S(2)}, u32[]{:S(2)}) %all-to-all-start) | async-done | bytes 49184 | tf_op jit(solution)/shard_map/all_to_all | solution.py:1113
  159.8 8.2 %shard_map.195 = bf16[8,2,16,48,384]{4,3,2,1,0:T(8,128)(2,1)} custom-call(s32[5]{0:T(128)} %stack.110.me_ref, bf16[4,8,48,384]{3,2,1,0:T(8,128)(2,1)} %copy-done.22, bf16[4,8,48,384]{3,2,1,0:T(8,128)(2,1)} %collective-permute-done.7.refs_1_, bf16[4,8,48,384]{3,2,1,0:T(8,128)(2,1)} %copy-done.21, bf16[4,8,48,384]{3,2,1,0:T(8,128)(2,1)} %copy-done.27, ...), custom_call_target="tpu_custom_call" | custom-call | bytes 18874368 | tf_op jit(solution)/shard_map/pallas_call | solution.py:869
  172.6 12.2 %shard_map.196 = (bf16[416,768]{1,0:T(8,128)(2,1)}, bf16[3,416,768]{2,1,0:T(8,128)(2,1)}, f32[2,3,2,416]{3,2,1,0:T(2,128)}, bf16[104,768]{1,0:T(8,128)(2,1)}, bf...) custom-call(bf16[104,768]{1,0:T(8,128)(2,1)} %get-tuple-element.233.refs_0_, ...), custom_call_target="tpu_custom_call" | custom-call | flops 1472200704 | bytes 14470656 | tf_op jit(solution)/shard_map/pallas_call | solution.py:194
  191.7 24.9 %collective-permute-done.17.refs_2_ = bf16[104,768]{1,0:T(8,128)(2,1)S(1)} collective-permute-done((bf16[104,768]{1,0:T(8,128)(2,1)}, bf16[104,768]{1,0:T(8,128)(2,1)S(1)}, u32[]{:S(2)}, u32[]{:S(2)}) %collective-permute-start.17) | collective-permute-done | bytes 159776 | tf_op jit(solution)/shard_map/ppermute | solution.py:795
  228.9 9.4 %shard_map.197 = (bf16[416,768]{1,0:T(8,128)(2,1)}, bf16[416,768]{1,0:T(8,128)(2,1)}, f32[416,768]{1,0:T(8,128)}, bf16[3,416,768]{2,1,0:T(8,128)(2,1)}) custom-call(s32[5]{0:T(128)} %stack.110.me_ref, bf16[104,768]{1,0:T(8,128)(2,1)} %get-tuple-element.243.refs_0_, bf16[104,768]{1,0:T(8,128)(2,1)} %copy-done.44, bf16[104,768]{1,0:T(8,128)(2,1)} %copy-done.47, ...), custom_call_target="tpu_custom_call" | custom-call | flops 2453667840 | bytes 28821524 | tf_op jit(solution)/shard_map/pallas_call | solution.py:194
  238.3 9.9 %shard_map.198 = (bf16[416,768]{1,0:T(8,128)(2,1)}, f32[416,768]{1,0:T(8,128)}, f32[2,3,2,2,208]{4,3,2,1,0:T(2,128)}) custom-call(bf16[3,416,768]{2,1,0:T(8,128)(2,1)} %get-tuple-element.247.qkv_ref, f32[416,768]{1,0:T(8,128)} %get-tuple-element.248.x1_ref, bf16[9,2,768,384]{3,2,1,0:T(8,128)(2,1)} %bitcast.202), custom_call_target="tpu_custom_call" | custom-call | flops 490733568 | bytes 15748608 | tf_op jit(solution)/shard_map/pallas_call | solution.py:194
  253.1 13.5 %shard_map.199 = (f32[416,768]{1,0:T(8,128)}, bf16[104,768]{1,0:T(8,128)(2,1)}, bf16[104,768]{1,0:T(8,128)(2,1)}, bf16[104,768]{1,0:T(8,128)(2,1)}, bf16[104,768]{1,0:T(8,128)(2,1)}) custom-call(f32[416,768]{1,0:T(8,128)} %get-tuple-element.254.x2_ref, bf16[8,2,768,384]{3,2,1,0:T(8,128)(2,1)} %bitcast.215, bf16[8,2,768,384]{3,2,1,0:T(8,128)(2,1)} %bitcast.216, ...), custom_call_target="tpu_custom_call" | custom-call | flops 3925868544 | bytes 22106132 | tf_op jit(solution)/shard_map/pallas_call | solution.py:194
  281.5 12.7 %shard_map.200 = (bf16[416,768]{1,0:T(8,128)(2,1)}, bf16[3,416,768]{2,1,0:T(8,128)(2,1)}, f32[2,3,2,416]{3,2,1,0:T(2,128)}, bf16[104,768]{1,0:T(8,128)(2,1)}, bf...) custom-call(bf16[104,768]{1,0:T(8,128)(2,1)} %get-tuple-element.262.refs_0_, ...), custom_call_target="tpu_custom_call" | custom-call | flops 1472200704 | bytes 14470656 | tf_op jit(solution)/shard_map/pallas_call | solution.py:194
  294.2 11.2 %collective-permute-start.29 = (bf16[104,768]{1,0:T(8,128)(2,1)}, bf16[104,768]{1,0:T(8,128)(2,1)S(1)}, u32[]{:S(2)}, u32[]{:S(2)}) collective-permute-start(bf16[104,768]{1,0:T(8,128)(2,1)} %get-tuple-element.267), channel_id=1, source_target_pairs={{0,8},{2,10},{4,12},{6,14},{8,0},{10,2},{12,4},{14,6},{16,24},{18,... | collective-permute-start | bytes 479240 | tf_op jit(solution)/shard_map/ppermute | solution.py:795
  305.4 8.0 %collective-permute-start.30 = (bf16[104,768]{1,0:T(8,128)(2,1)}, bf16[104,768]{1,0:T(8,128)(2,1)S(1)}, u32[]{:S(2)}, u32[]{:S(2)}) collective-permute-start(bf16[104,768]{1,0:T(8,128)(2,1)} %get-tuple-element.268), channel_id=1, source_target_pairs={{0,2},{2,0},{4,6},{6,4},{8,10},{10,8},{12,14},{14,12},{16,18},{18,... | collective-permute-start | bytes 479240 | tf_op jit(solution)/shard_map/ppermute | solution.py:795
  322.1 9.3 %shard_map.201 = (bf16[416,768]{1,0:T(8,128)(2,1)}, bf16[416,768]{1,0:T(8,128)(2,1)}, f32[416,768]{1,0:T(8,128)}, bf16[3,416,768]{2,1,0:T(8,128)(2,1)}) custom-call(s32[5]{0:T(128)} %stack.110.me_ref, bf16[104,768]{1,0:T(8,128)(2,1)} %get-tuple-element.272.refs_0_, bf16[104,768]{1,0:T(8,128)(2,1)} %copy-done.48, bf16[104,768]{1,0:T(8,128)(2,1)} %copy-done.50, ...), custom_call_target="tpu_custom_call" | custom-call | flops 2453667840 | bytes 28821524 | tf_op jit(solution)/shard_map/pallas_call | solution.py:194
  331.5 9.9 %shard_map.202 = (bf16[416,768]{1,0:T(8,128)(2,1)}, f32[416,768]{1,0:T(8,128)}, f32[2,3,2,2,208]{4,3,2,1,0:T(2,128)}) custom-call(bf16[3,416,768]{2,1,0:T(8,128)(2,1)} %get-tuple-element.277.qkv_ref, f32[416,768]{1,0:T(8,128)} %get-tuple-element.278.x1_ref, bf16[9,2,768,384]{3,2,1,0:T(8,128)(2,1)} %bitcast.210), custom_call_target="tpu_custom_call" | custom-call | flops 490733568 | bytes 15748608 | tf_op jit(solution)/shard_map/pallas_call | solution.py:194
  341.4 8.3 %shard_map.203 = bf16[8,2,16,48,384]{4,3,2,1,0:T(8,128)(2,1)} custom-call(s32[5]{0:T(128)} %stack.110.me_ref, bf16[4,8,48,384]{3,2,1,0:T(8,128)(2,1)} %copy-done.23, bf16[4,8,48,384]{3,2,1,0:T(8,128)(2,1)} %collective-permute-done.27.refs_1_, bf16[4,8,48,384]{3,2,1,0:T(8,128)(2,1)} %copy-done.24, bf16[4,8,48,384]{3,2,1,0:T(8,128)(2,1)} %collective-permute-done.28.refs_3_, ...), custom_call_target="tpu_custom_call" | custom-call | bytes 18874368 | tf_op jit(solution)/shard_map/pallas_call | solution.py:869
  349.6 25.4 %shard_map.204 = (f32[416,768]{1,0:T(8,128)}, bf16[4,2,2,192,384]{4,3,2,1,0:T(8,128)(2,1)}, bf16[4,2,2,192,384]{4,3,2,1,0:T(8,128)(2,1)}, bf16[4,2,2,192,384]{4,...) custom-call(s32[5]{0:T(128)} %stack.110.me_ref, ...), custom_call_target="tpu_custom_call" | custom-call | flops 9814671360 | bytes 33447956 | tf_op jit(solution)/shard_map/pallas_call | solution.py:194
  375.6 21.7 %shard_map.205 = (f32[416,768]{1,0:T(8,128)}, bf16[4,2,2,192,384]{4,3,2,1,0:T(8,128)(2,1)}, bf16[4,2,2,192,384]{4,3,2,1,0:T(8,128)(2,1)}, f32[2,768]{1,0:T(2,128)}) custom-call(s32[5]{0:T(128)} %stack.110.me_ref, f32[416,768]{1,0:T(8,128)} %get-tuple-element.286.g_ref, f32[416,768]{1,0:T(8,128)} %get-tuple-element.278.x1_ref, ...), custom_call_target="tpu_custom_call" | custom-call | flops 3925868544 | bytes 32386580 | tf_op jit(solution)/shard_map/pallas_call | solution.py:194
  409.1 7.8 %shard_map.207 = (bf16[104,768]{1,0:T(8,128)(2,1)}, bf16[104,768]{1,0:T(8,128)(2,1)}, bf16[104,768]{1,0:T(8,128)(2,1)}, bf16[104,768]{1,0:T(8,128)(2,1)}, bf16[2...) custom-call(s32[5]{0:T(128)} %stack.110.me_ref, f32[416,768]{1,0:T(8,128)} %get-tuple-element.297.g_ref.refs_5_, ...), custom_call_target="tpu_custom_call" | custom-call | flops 1962934272 | bytes 17350676 | tf_op jit(solution)/shard_map/pallas_call | solution.py:194
  416.8 10.4 %collective-permute-start.39 = (bf16[104,768]{1,0:T(8,128)(2,1)}, bf16[104,768]{1,0:T(8,128)(2,1)S(1)}, u32[]{:S(2)}, u32[]{:S(2)}) collective-permute-start(bf16[104,768]{1,0:T(8,128)(2,1)} %get-tuple-element.301), channel_id=1, source_target_pairs={{0,8},{2,10},{4,12},{6,14},{8,0},{10,2},{12,4},{14,6},{16,24},{18,... | collective-permute-start | bytes 479240 | tf_op jit(solution)/shard_map/ppermute | solution.py:795
  438.1 6.8 collective-permute-start.50
  444.9 18.3 %shard_map.209 = (bf16[104,768]{1,0:T(8,128)(2,1)}, bf16[104,768]{1,0:T(8,128)(2,1)}, bf16[104,768]{1,0:T(8,128)(2,1)}, bf16[104,768]{1,0:T(8,128)(2,1)}, bf16[1...) custom-call(s32[5]{0:T(128)} %stack.110.me_ref, ...), custom_call_target="tpu_custom_call" | custom-call | flops 2944401408 | bytes 18009620 | tf_op jit(solution)/shard_map/pallas_call | solution.py:194
  466.3 15.3 %collective-permute-start.48 = (bf16[104,768]{1,0:T(8,128)(2,1)}, bf16[104,768]{1,0:T(8,128)(2,1)S(1)}, u32[]{:S(2)}, u32[]{:S(2)}) collective-permute-start(bf16[104,768]{1,0:T(8,128)(2,1)} %get-tuple-element.325), channel_id=1, source_target_pairs={{0,2},{2,0},{4,6},{6,4},{8,10},{10,8},{12,14},{14,12},{16,18},{18,... | collective-permute-start | bytes 479240 | tf_op jit(solution)/shard_map/ppermute | solution.py:795
  496.2 22.8 %shard_map.212 = (f32[416,768]{1,0:T(8,128)}, bf16[4,2,2,192,384]{4,3,2,1,0:T(8,128)(2,1)}, bf16[4,2,2,192,384]{4,3,2,1,0:T(8,128)(2,1)}, bf16[4,2,2,192,384]{4,...) custom-call(s32[5]{0:T(128)} %stack.110.me_ref, f32[416,768]{1,0:T(8,128)} %get-tuple-element.344.g_ref, ...), custom_call_target="tpu_custom_call" | custom-call | flops 9814671360 | bytes 32170004 | tf_op jit(solution)/shard_map/pallas_call | solution.py:194
  525.0 21.7 %shard_map.214 = (f32[416,768]{1,0:T(8,128)}, bf16[4,2,2,192,384]{4,3,2,1,0:T(8,128)(2,1)}, bf16[4,2,2,192,384]{4,3,2,1,0:T(8,128)(2,1)}, f32[2,768]{1,0:T(2,128)}) custom-call(s32[5]{0:T(128)} %stack.110.me_ref, f32[416,768]{1,0:T(8,128)} %get-tuple-element.354.g_ref, f32[416,768]{1,0:T(8,128)} %get-tuple-element.248.x1_ref, ...), custom_call_target="tpu_custom_call" | custom-call | flops 3925868544 | bytes 32386580 | tf_op jit(solution)/shard_map/pallas_call | solution.py:194
  549.6 8.2 %collective-permute-done.57.refs_17_ = bf16[2,192,384]{2,1,0:T(8,128)(2,1)S(1)} collective-permute-done((bf16[2,192,384]{2,1,0:T(8,128)(2,1)S(1)}, bf16[2,192,384]{2,1,0:T(8,128)(2,1)S(1)}, u32[]{:S(2)}, u32[]{:S(2)}) %collective-permute-start.57) | collective-permute-done | bytes 294944 | tf_op jit(solution)/shard_map/ppermute | solution.py:1038
  566.7 7.8 %shard_map.216 = (bf16[104,768]{1,0:T(8,128)(2,1)}, bf16[104,768]{1,0:T(8,128)(2,1)}, bf16[104,768]{1,0:T(8,128)(2,1)}, bf16[104,768]{1,0:T(8,128)(2,1)}, bf16[2...) custom-call(s32[5]{0:T(128)} %stack.110.me_ref, f32[416,768]{1,0:T(8,128)} %get-tuple-element.369.g_ref.refs_5_, ...), custom_call_target="tpu_custom_call" | custom-call | flops 1962934272 | bytes 17350676 | tf_op jit(solution)/shard_map/pallas_call | solution.py:194
  576.3 15.8 %collective-permute-done.63.refs_2_ = bf16[8,192,384]{2,1,0:T(8,128)(2,1)S(1)} collective-permute-done((bf16[8,192,384]{2,1,0:T(8,128)(2,1)}, bf16[8,192,384]{2,1,0:T(8,128)(2,1)S(1)}, u32[]{:S(2)}, u32[]{:S(2)}) %collective-permute-start.63) | collective-permute-done | bytes 1179680 | tf_op jit(solution)/shard_map/ppermute | solution.py:1038
  602.8 18.5 %shard_map.218 = (bf16[104,768]{1,0:T(8,128)(2,1)}, bf16[104,768]{1,0:T(8,128)(2,1)}, bf16[104,768]{1,0:T(8,128)(2,1)}, bf16[104,768]{1,0:T(8,128)(2,1)}, bf16[1...) custom-call(s32[5]{0:T(128)} %stack.110.me_ref, ...), custom_call_target="tpu_custom_call" | custom-call | flops 2944401408 | bytes 18009620 | tf_op jit(solution)/shard_map/pallas_call | solution.py:194
  671.7 14.7 %all-to-all-done.3 = f32[32,1,384]{2,1,0:T(1,128)} async-done(((f32[32,1,384]{2,1,0:T(1,128)}), f32[32,1,384]{2,1,0:T(1,128)}, u32[]{:S(2)}, u32[]{:S(2)}) %all-to-all-start.3) | async-done | bytes 49184 | tf_op jit(solution)/shard_map/all_to_all | solution.py:1126
  719.9 13.3 %all-to-all-done.1 = bf16[4,5,48,384]{3,2,1,0:T(8,128)(2,1)S(1)} async-done(((bf16[4,5,48,384]{3,2,1,0:T(8,128)(2,1)}), bf16[4,5,48,384]{3,2,1,0:T(8,128)(2,1)S(1)}, u32[]{:S(2)}, u32[]{:S(2)}) %all-to-all-start.1) | async-done | bytes 737312 | tf_op jit(solution)/shard_map/all_to_all | solution.py:1064
  (448 shorter events, 262.8 us)
Async XLA Ops:
  7.2 164.7 %all-gather.3.cloned.1.call-start = ((), (), s32[]{:S(2)}) async-start(), calls=%async_computation.8 | async-start | bytes 10948608 | tf_op jit(solution)/shard_map/all_gather | solution.py:824
  11.0 270.5 %all-gather.5.cloned.1.call-start = ((), (), s32[]{:S(2)}) async-start(), calls=%async_computation.9 | async-start | bytes 10948608 | tf_op jit(solution)/shard_map/all_gather | solution.py:824
  18.5 32.3 %collective-permute-start.9 = (bf16[8,48,384]{2,1,0:T(8,128)(2,1)S(1)}, bf16[8,48,384]{2,1,0:T(8,128)(2,1)S(1)}, u32[]{:S(2)}, u32[]{:S(2)}) collective-permute-start(bf16[8,48,384]{2,1,0:T(8,128)(2,1)S(1)} %get-tuple-element.494), channel_id=1, source_target_pairs={{0,4},{2,6},{4,0},{6,2},{1,5},{3,7},{5,1},{7,3},{8,12},{10,14},{12... | collective-permute-start | bytes 884744 | tf_op jit(solution)/shard_map/ppermute | solution.py:834
  18.5 33.9 %collective-permute-start.5 = (bf16[8,48,384]{2,1,0:T(8,128)(2,1)S(1)}, bf16[8,48,384]{2,1,0:T(8,128)(2,1)S(1)}, u32[]{:S(2)}, u32[]{:S(2)}) collective-permute-start(bf16[8,48,384]{2,1,0:T(8,128)(2,1)S(1)} %get-tuple-element.494), channel_id=1, source_target_pairs={{0,2},{2,4},{4,6},{6,0},{1,3},{3,5},{5,7},{7,1},{8,10},{10,12},{12... | collective-permute-start | bytes 884744 | tf_op jit(solution)/shard_map/ppermute | solution.py:834
  69.9 43.8 %collective-permute-start.11 = (bf16[4,8,48,384]{3,2,1,0:T(8,128)(2,1)S(1)}, bf16[4,8,48,384]{3,2,1,0:T(8,128)(2,1)S(1)}, u32[]{:S(2)}, u32[]{:S(2)}) collective-permute-start(bf16[4,8,48,384]{3,2,1,0:T(8,128)(2,1)S(1)} %pad_maximum_fusion.1.refs_2_), channel_id=1, source_target_pairs={{0,16},{8,24},{16,0},{24,8},{1,17},{9,25},{17,1},{25,9},{2,18},{10... | collective-permute-start | bytes 3538952 | tf_op jit(solution)/shard_map/ppermute | solution.py:1038
  78.4 37.1 %collective-permute-start.7 = (bf16[4,8,48,384]{3,2,1,0:T(8,128)(2,1)S(1)}, bf16[4,8,48,384]{3,2,1,0:T(8,128)(2,1)}, u32[]{:S(2)}, u32[]{:S(2)}) collective-permute-start(bf16[4,8,48,384]{3,2,1,0:T(8,128)(2,1)S(1)} %pad_maximum_fusion.refs_0_), channel_id=1, source_target_pairs={{0,1},{1,0},{2,3},{3,2},{4,5},{5,4},{6,7},{7,6},{8,9},{9,8},{10,11... | collective-permute-start | bytes 3538952 | tf_op jit(solution)/shard_map/ppermute | solution.py:1038
  78.5 77.5 %collective-permute-start.14 = (bf16[4,8,48,384]{3,2,1,0:T(8,128)(2,1)S(1)}, bf16[4,8,48,384]{3,2,1,0:T(8,128)(2,1)}, u32[]{:S(2)}, u32[]{:S(2)}) collective-permute-start(bf16[4,8,48,384]{3,2,1,0:T(8,128)(2,1)S(1)} %pad_maximum_fusion.1.refs_2_), channel_id=1, source_target_pairs={{0,8},{8,0},{16,24},{24,16},{1,9},{9,1},{17,25},{25,17},{2,10},{10... | collective-permute-start | bytes 3538952 | tf_op jit(solution)/shard_map/ppermute | solution.py:1038
  78.6 78.2 %collective-permute-start.12 = (bf16[4,8,48,384]{3,2,1,0:T(8,128)(2,1)S(1)}, bf16[4,8,48,384]{3,2,1,0:T(8,128)(2,1)}, u32[]{:S(2)}, u32[]{:S(2)}) collective-permute-start(bf16[4,8,48,384]{3,2,1,0:T(8,128)(2,1)S(1)} %pad_maximum_fusion.refs_0_), channel_id=1, source_target_pairs={{0,8},{8,0},{16,24},{24,16},{1,9},{9,1},{17,25},{25,17},{2,10},{10... | collective-permute-start | bytes 3538952 | tf_op jit(solution)/shard_map/ppermute | solution.py:1038
  113.7 46.0 %collective-permute-start.15 = (bf16[4,8,48,384]{3,2,1,0:T(8,128)(2,1)S(1)}, bf16[4,8,48,384]{3,2,1,0:T(8,128)(2,1)}, u32[]{:S(2)}, u32[]{:S(2)}) collective-permute-start(bf16[4,8,48,384]{3,2,1,0:T(8,128)(2,1)S(1)} %collective-permute-done.11.refs_3_), channel_id=1, source_target_pairs={{0,8},{8,0},{16,24},{24,16},{1,9},{9,1},{17,25},{25,17},{2,10},{10... | collective-permute-start | bytes 3538952 | tf_op jit(solution)/shard_map/ppermute | solution.py:1038
  115.6 44.2 %collective-permute-start.13 = (bf16[4,8,48,384]{3,2,1,0:T(8,128)(2,1)}, bf16[4,8,48,384]{3,2,1,0:T(8,128)(2,1)}, u32[]{:S(2)}, u32[]{:S(2)}) collective-permute-start(bf16[4,8,48,384]{3,2,1,0:T(8,128)(2,1)} %collective-permute-done.7.refs_1_), channel_id=1, source_target_pairs={{0,8},{8,0},{16,24},{24,16},{1,9},{9,1},{17,25},{25,17},{2,10},{10... | collective-permute-start | bytes 3538952 | tf_op jit(solution)/shard_map/ppermute | solution.py:1038
  115.6 35.1 %collective-permute-start.1 = (bf16[1,2,196,768]{3,1,2,0:T(2,128)(2,1)}, bf16[1,2,196,768]{3,1,2,0:T(2,128)(2,1)}, u32[]{:S(2)}, u32[]{:S(2)}) collective-permute-start(bf16[1,2,196,768]{3,1,2,0:T(2,128)(2,1)} %param.11), channel_id=1, source_target_pairs={{0,0},{2,8},{4,2},{6,10},{8,4},{10,12},{12,6},{14,14},{16,16},{18,... | collective-permute-start | bytes 1806344 | tf_op jit(solution)/shard_map/ppermute | solution.py:773
  126.0 514.1 %reduce-scatter.7.cloned.1.call-start = ((), (), s32[]{:S(2)}) async-start(), calls=%async_computation.11 | async-start | bytes 737280 | tf_op jit(solution)/shard_map/reduce_scatter | solution.py:1067
  185.0 38.2 %collective-permute-start.21 = (bf16[8,48,384]{2,1,0:T(8,128)(2,1)S(1)}, bf16[8,48,384]{2,1,0:T(8,128)(2,1)S(1)}, u32[]{:S(2)}, u32[]{:S(2)}) collective-permute-start(bf16[8,48,384]{2,1,0:T(8,128)(2,1)S(1)} %pad_maximum_fusion.13), channel_id=1, source_target_pairs={{0,6},{2,0},{4,2},{6,4},{1,7},{3,1},{5,3},{7,5},{8,14},{10,8},{12,... | collective-permute-start | bytes 884744 | tf_op jit(solution)/shard_map/ppermute | solution.py:834
  188.0 35.5 %collective-permute-start.20 = (bf16[8,48,384]{2,1,0:T(8,128)(2,1)S(1)}, bf16[8,48,384]{2,1,0:T(8,128)(2,1)S(1)}, u32[]{:S(2)}, u32[]{:S(2)}) collective-permute-start(bf16[8,48,384]{2,1,0:T(8,128)(2,1)S(1)} %pad_maximum_fusion.13), channel_id=1, source_target_pairs={{0,4},{2,6},{4,0},{6,2},{1,5},{3,7},{5,1},{7,3},{8,12},{10,14},{12... | collective-permute-start | bytes 884744 | tf_op jit(solution)/shard_map/ppermute | solution.py:834
  188.0 35.5 %collective-permute-start.19 = (bf16[8,48,384]{2,1,0:T(8,128)(2,1)S(1)}, bf16[8,48,384]{2,1,0:T(8,128)(2,1)S(1)}, u32[]{:S(2)}, u32[]{:S(2)}) collective-permute-start(bf16[8,48,384]{2,1,0:T(8,128)(2,1)S(1)} %pad_maximum_fusion.13), channel_id=1, source_target_pairs={{0,2},{2,4},{4,6},{6,0},{1,3},{3,5},{5,7},{7,1},{8,10},{10,12},{12... | collective-permute-start | bytes 884744 | tf_op jit(solution)/shard_map/ppermute | solution.py:834
  191.7 31.5 %collective-permute-start.18 = (bf16[104,768]{1,0:T(8,128)(2,1)}, bf16[104,768]{1,0:T(8,128)(2,1)S(1)}, u32[]{:S(2)}, u32[]{:S(2)}) collective-permute-start(bf16[104,768]{1,0:T(8,128)(2,1)} %get-tuple-element.241), channel_id=1, source_target_pairs={{0,10},{2,8},{4,14},{6,12},{8,2},{10,0},{12,6},{14,4},{16,26},{18,... | collective-permute-start | bytes 479240 | tf_op jit(solution)/shard_map/ppermute | solution.py:795
  250.2 29.8 %collective-permute-start.28 = (bf16[4,8,48,384]{3,2,1,0:T(8,128)(2,1)S(1)}, bf16[4,8,48,384]{3,2,1,0:T(8,128)(2,1)}, u32[]{:S(2)}, u32[]{:S(2)}) collective-permute-start(bf16[4,8,48,384]{3,2,1,0:T(8,128)(2,1)S(1)} %pad_maximum_fusion.3.refs_2_), channel_id=1, source_target_pairs={{0,16},{8,24},{16,0},{24,8},{1,17},{9,25},{17,1},{25,9},{2,18},{10... | collective-permute-start | bytes 3538952 | tf_op jit(solution)/shard_map/ppermute | solution.py:1038
  268.2 37.2 %collective-permute-start.34 = (bf16[4,8,48,384]{3,2,1,0:T(8,128)(2,1)S(1)}, bf16[4,8,48,384]{3,2,1,0:T(8,128)(2,1)}, u32[]{:S(2)}, u32[]{:S(2)}) collective-permute-start(bf16[4,8,48,384]{3,2,1,0:T(8,128)(2,1)S(1)} %pad_maximum_fusion.3.refs_2_), channel_id=1, source_target_pairs={{0,8},{8,0},{16,24},{24,16},{1,9},{9,1},{17,25},{25,17},{2,10},{10... | collective-permute-start | bytes 3538952 | tf_op jit(solution)/shard_map/ppermute | solution.py:1038
  268.4 45.0 %collective-permute-start.32 = (bf16[4,8,48,384]{3,2,1,0:T(8,128)(2,1)S(1)}, bf16[4,8,48,384]{3,2,1,0:T(8,128)(2,1)}, u32[]{:S(2)}, u32[]{:S(2)}) collective-permute-start(bf16[4,8,48,384]{3,2,1,0:T(8,128)(2,1)S(1)} %pad_maximum_fusion.2.refs_0_), channel_id=1, source_target_pairs={{0,8},{8,0},{16,24},{24,16},{1,9},{9,1},{17,25},{25,17},{2,10},{10... | collective-permute-start | bytes 3538952 | tf_op jit(solution)/shard_map/ppermute | solution.py:1038
  280.0 41.5 %collective-permute-start.33 = (bf16[4,8,48,384]{3,2,1,0:T(8,128)(2,1)}, bf16[4,8,48,384]{3,2,1,0:T(8,128)(2,1)}, u32[]{:S(2)}, u32[]{:S(2)}) collective-permute-start(bf16[4,8,48,384]{3,2,1,0:T(8,128)(2,1)} %collective-permute-done.27.refs_1_), channel_id=1, source_target_pairs={{0,8},{8,0},{16,24},{24,16},{1,9},{9,1},{17,25},{25,17},{2,10},{10... | collective-permute-start | bytes 3538952 | tf_op jit(solution)/shard_map/ppermute | solution.py:1038
  280.2 41.3 %collective-permute-start.35 = (bf16[4,8,48,384]{3,2,1,0:T(8,128)(2,1)}, bf16[4,8,48,384]{3,2,1,0:T(8,128)(2,1)}, u32[]{:S(2)}, u32[]{:S(2)}) collective-permute-start(bf16[4,8,48,384]{3,2,1,0:T(8,128)(2,1)} %collective-permute-done.28.refs_3_), channel_id=1, source_target_pairs={{0,8},{8,0},{16,24},{24,16},{1,9},{9,1},{17,25},{25,17},{2,10},{10... | collective-permute-start | bytes 3538952 | tf_op jit(solution)/shard_map/ppermute | solution.py:1038
  397.3 30.0 %collective-permute-start.44 = (bf16[4,2,2,192,384]{4,3,2,1,0:T(8,128)(2,1)}, bf16[4,2,2,192,384]{4,3,2,1,0:T(8,128)(2,1)S(1)}, u32[]{:S(2)}, u32[]{:S(2)}) collective-permute-start(bf16[4,2,2,192,384]{4,3,2,1,0:T(8,128)(2,1)} %get-tuple-element.307), channel_id=1, source_target_pairs={{0,8},{8,0},{16,24},{24,16},{1,9},{9,1},{17,25},{25,17},{2,10},{10... | collective-permute-start | bytes 7077896 | tf_op jit(solution)/shard_map/ppermute | solution.py:1038
  489.7 29.8 %collective-permute-start.54 = (bf16[6,192,384]{2,1,0:T(8,128)(2,1)}, bf16[6,192,384]{2,1,0:T(8,128)(2,1)S(1)}, u32[]{:S(2)}, u32[]{:S(2)}) collective-permute-start(bf16[6,192,384]{2,1,0:T(8,128)(2,1)} %get-tuple-element.346), channel_id=1, source_target_pairs={{0,1},{1,0},{2,3},{3,2},{4,5},{5,4},{6,7},{7,6},{8,9},{9,8},{10,11... | collective-permute-start | bytes 2654216 | tf_op jit(solution)/shard_map/ppermute | solution.py:1038
  491.0 28.4 %collective-permute-start.55 = (bf16[8,192,384]{2,1,0:T(8,128)(2,1)}, bf16[8,192,384]{2,1,0:T(8,128)(2,1)S(1)}, u32[]{:S(2)}, u32[]{:S(2)}) collective-permute-start(bf16[8,192,384]{2,1,0:T(8,128)(2,1)} %get-tuple-element.347), channel_id=1, source_target_pairs={{0,16},{8,24},{16,0},{24,8},{1,17},{9,25},{17,1},{25,9},{2,18},{10... | collective-permute-start | bytes 3538952 | tf_op jit(solution)/shard_map/ppermute | solution.py:1038
  518.9 40.9 %collective-permute-start.58 = (bf16[4,2,2,192,384]{4,3,2,1,0:T(8,128)(2,1)}, bf16[4,2,2,192,384]{4,3,2,1,0:T(8,128)(2,1)}, u32[]{:S(2)}, u32[]{:S(2)}) collective-permute-start(bf16[4,2,2,192,384]{4,3,2,1,0:T(8,128)(2,1)} %get-tuple-element.363), channel_id=1, source_target_pairs={{0,8},{8,0},{16,24},{24,16},{1,9},{9,1},{17,25},{25,17},{2,10},{10... | collective-permute-start | bytes 7077896 | tf_op jit(solution)/shard_map/ppermute | solution.py:1038
  519.0 40.8 %collective-permute-start.59 = (bf16[4,2,2,192,384]{4,3,2,1,0:T(8,128)(2,1)}, bf16[4,2,2,192,384]{4,3,2,1,0:T(8,128)(2,1)}, u32[]{:S(2)}, u32[]{:S(2)}) collective-permute-start(bf16[4,2,2,192,384]{4,3,2,1,0:T(8,128)(2,1)} %get-tuple-element.365), channel_id=1, source_target_pairs={{0,8},{8,0},{16,24},{24,16},{1,9},{9,1},{17,25},{25,17},{2,10},{10... | collective-permute-start | bytes 7077896 | tf_op jit(solution)/shard_map/ppermute | solution.py:1038
  524.9 131.5 %reduce-scatter.11.cloned.1.call-start = ((), (), s32[]{:S(2)}) async-start(), calls=%async_computation.13 | async-start | bytes 1474560 | tf_op jit(solution)/shard_map/reduce_scatter | solution.py:1067
  546.7 29.4 %collective-permute-start.65 = (bf16[4,2,2,192,384]{4,3,2,1,0:T(8,128)(2,1)}, bf16[4,2,2,192,384]{4,3,2,1,0:T(8,128)(2,1)S(1)}, u32[]{:S(2)}, u32[]{:S(2)}) collective-permute-start(bf16[4,2,2,192,384]{4,3,2,1,0:T(8,128)(2,1)} %get-tuple-element.379), channel_id=1, source_target_pairs={{0,8},{8,0},{16,24},{24,16},{1,9},{9,1},{17,25},{25,17},{2,10},{10... | collective-permute-start | bytes 7077896 | tf_op jit(solution)/shard_map/ppermute | solution.py:1038
  546.8 145.5 %reduce-scatter.5.cloned.1.call-start = ((), (), s32[]{:S(2)}) async-start(), calls=%async_computation.10 | async-start | bytes 921600 | tf_op jit(solution)/shard_map/reduce_scatter | solution.py:1067
  602.7 114.2 %reduce-scatter.9.cloned.1.call-start = ((), (), s32[]{:S(2)}) async-start(), calls=%async_computation.12 | async-start | bytes 1474560 | tf_op jit(solution)/shard_map/reduce_scatter | solution.py:1067
  637.7 28.8 %collective-permute-start.77 = (bf16[8,192,384]{2,1,0:T(8,128)(2,1)}, bf16[8,192,384]{2,1,0:T(8,128)(2,1)S(1)}, u32[]{:S(2)}, u32[]{:S(2)}) collective-permute-start(bf16[8,192,384]{2,1,0:T(8,128)(2,1)} %get-tuple-element.421), channel_id=1, source_target_pairs={{0,16},{8,24},{16,0},{24,8},{1,17},{9,25},{17,1},{25,9},{2,18},{10... | collective-permute-start | bytes 3538952 | tf_op jit(solution)/shard_map/ppermute | solution.py:1038
  652.7 33.7 %all-to-all-start.3 = ((f32[32,1,384]{2,1,0:T(1,128)}), f32[32,1,384]{2,1,0:T(1,128)}, u32[]{:S(2)}, u32[]{:S(2)}) async-start(f32[32,1,384]{2,1,0:T(1,128)} %copy.131), calls=%async_computation.7 | async-start | bytes 98304 | tf_op jit(solution)/shard_map/all_to_all | solution.py:1126
  (135 other events, 1705.7 us)
Sparse Core Ops, SparseCore 0:
  11.7 128.6 all-gather.2
  144.0 117.6 all-gather.4
  525.1 20.1 reduce-scatter.6
  547.4 27.5 reduce-scatter.10
  602.8 21.1 reduce-scatter.4
  650.1 34.4 reduce-scatter.8

commit v11 on v10

--- a/solution.py
+++ b/solution.py
@@ -878,14 +878,6 @@
         ),
     )(me, *(blocks for blocks, _, _ in runs))
     yield full.reshape(n, shares, clips * ways * r, width)
-
-
-def spread_slabs(pack, me):
-    way = spread_steps(pack, me)
-    come = next(way)
-    for _ in range(5):
-        come = way.send(come)
-    return come
 
 
 class Spread:
@@ -1174,34 +1166,44 @@
         jnp.int32
     )
     if quick:
-        weights_ff = [spread_slabs(packs_ff[0], me)]
+        spreads = [Spread(pack, me) for pack in packs_ff]
+        spreads[0].step(())
+        weights_ff = []
     else:
         weights_ff = [gather_slabs(pack) for pack in packs_ff]
 
-    x = as_rows(go_home(tokens))
+    home = go_home(tokens)
+    if quick:
+        (home, gb, later), first = (home, gb, packs_ff[1:]), spreads[0]
+        home, gb, later = first.step((home, gb, later))
+        for spread, pack in zip(spreads[1:], later):
+            spread.come = pack
+            spread.step(())
+    x = as_rows(home)
     send = send_first(rows, x, gb[0], me)
     kept = []
     for l in range(layers):
         w = weights[l]
         send = swap_places(send)
-        if quick:
-            if l + 1 < layers:
-                send, weights_ff[l] = lax.optimization_barrier((send, weights_ff[l]))
-                spread = Spread(packs_ff[l + 1], me)
-                send, w = spread.step((send, w))
-            else:
+        if quick and l == 0:
+            for _ in range(3):
+                send = first.step(send)
+            weights_ff.append(first.come)
+            send, weights_ff[0] = lax.optimization_barrier((send, weights_ff[0]))
+            for spread in spreads[1:]:
                 send = spread.step(send)
+        elif quick:
+            send = spreads[l].step(send)
+            weights_ff.append(spreads[l].come)
         a1, qkv1, log1, o1_time = time_forward(rows, send, w)
         back = swap_places(o1_time)
-        if quick:
-            back = spread.step(back)
+        if quick and l == 0:
+            for spread in spreads[1:]:
+                back = spread.step(back)
         o1, y1, x1, qkv2 = middle_forward(rows, back, x, w, mixes[l], gb[l], me)
         o2, x2, log2 = space_forward(rows, qkv2, x1, w)
-        if quick:
-            if l + 1 == layers:
-                weights_ff.append(spread.come)
-                x2, weights_ff[l] = lax.optimization_barrier((x2, weights_ff[l]))
-            else:
+        if quick and l == 0:
+            for spread in spreads[1:]:
                 x2 = spread.step(x2)
         kept.append((x, a1, qkv1, log1, o1, y1, x1, qkv2, o2, log2, x2))
         if l + 1 < layers:
@@ -1250,7 +1252,7 @@
         else:
             summed[l] = [reduce_plain(g_ff + [g_space, g_out] + g_time, clip & 1)]
     if quick:
-        tokens_grad = move(go_back(from_rows(grad.astype(BF16))), late, me, True)
+        tokens_grad = move(go_back(from_rows(grad.astype(BF16))), late, me)
         move((), rest, me, True)
         summed = [[p.result for p in some] for some in summed]
     cuts = (2 * g_ff[0][0].shape[0], g_space[0].shape[0], g_out[0].shape[0], len(g_time))

time: 750 us -> 749 us (level)
  waiting for transfers between devices: 236 us -> 262 us
  starting transfers between devices: 133 us -> 117 us
  local copies, waits for them, and re-layouts: 46.7 us -> 34.6 us
    all_to_all x1, waiting for transfers between devices: 17.5 us -> 55.8 us  [gather_norms(): lax.all_to_all(jnp.broadcast_to(padded, (count, width)), ALL, split_axis=...]
    reduce_scatter x4 -> x5, waiting for transfers between devices: 0.04 us -> 21.5 us  [move(): own = lax.psum_scatter(array, 'seq', scatter_dimension=1, tiled=True)]
    ppermute x24, waiting for transfers between devices: 50.3 us -> 36.5 us  [swap_places(): got.append(lax.ppermute(chunks[k], ('clip', 'seq'), pairs))]
    all_to_all x2 -> x1, waiting for transfers between devices: 13.3 us -> 2.01 us  [move(): lax.all_to_all(array, 'seq', split_axis=0, concat_axis=0, tiled=True)]
    ppermute x24, starting transfers between devices: 58.7 us -> 48.2 us  [swap_places(): got.append(lax.ppermute(chunks[k], ('clip', 'seq'), pairs))]
    ppermute x6, waiting for transfers between devices: 31.6 us -> 21.5 us  [spread_steps(): lax.ppermute(pack, 'seq', [(i, (i + k) % ways) for i in range(ways)])]
    ppermute x46, waiting for transfers between devices: 109 us -> 118 us  [cross(): return lax.ppermute(a, axis, [(i, i ^ 1 << bit) for i in range(size)])]
    unnamed x167 -> x171, local copies, waits for them, and re-layouts: 22.2 us -> 22.6 us
  transfers between devices with their start and end apart: 90 -> 90, of which waited for: 29 -> 34; matrix products, arithmetic and copies ran while one was open for 6% -> 5% of each run, Pallas kernels for 32% -> 32%
where the time goes in v11:
time: 749 us; the launch traced here: 744 us
  Pallas kernels  294 us (39%)
  waiting for transfers between devices  262 us (35%)
  starting transfers between devices  117 us (16%)
  local copies, waits for them, and re-layouts  34.6 us (5%)
  other arithmetic  20.4 us (3%)
  between operations  16 us (2%)
    pallas_call x18, Pallas kernels, call(): pl.pallas_call(body, out_shape=[shape for shape, _ in outs], grid=grid, i...  232 us
    ppermute x46, waiting for transfers between devices, cross(): return lax.ppermute(a, axis, [(i, i ^ 1 << bit) for i in range(size)])  118 us
    all_to_all x1, waiting for transfers between devices, gather_norms(): lax.all_to_all(jnp.broadcast_to(padded, (count, width)), ALL, split_axis=...  55.8 us
    ppermute x24, starting transfers between devices, swap_places(): got.append(lax.ppermute(chunks[k], ('clip', 'seq'), pairs))  48.2 us
    pallas_call x9, Pallas kernels, fold(): pl.pallas_call(body, out_shape=[jax.ShapeDtypeStruct(shape, BF16) for sha...  45.2 us
    ppermute x46, starting transfers between devices, cross(): return lax.ppermute(a, axis, [(i, i ^ 1 << bit) for i in range(size)])  40 us
    ppermute x24, waiting for transfers between devices, swap_places(): got.append(lax.ppermute(chunks[k], ('clip', 'seq'), pairs))  36.5 us
    unnamed x171, local copies, waits for them, and re-layouts  22.6 us
  transfers between devices with their start and end apart: 90, of which 34 were waited for; matrix products, arithmetic and copies ran while one was open for 5% of the time, Pallas kernels for 32%

profile of v11, /device:TPU:0, one launch (start us, length us, event | category | flops | bytes accessed | tf_op | source)
XLA Modules:
  0.0 743.9 jit_solution(9842302654595496480)
XLA Ops:
  26.2 55.8 %all-to-all-done = f32[32,1,384]{2,1,0:T(1,128)S(1)} async-done(((f32[32,1,384]{2,1,0:T(1,128)}), f32[32,1,384]{2,1,0:T(1,128)S(1)}, u32[]{:S(2)}, u32[]{:S(2)}) %all-to-all-start) | async-done | bytes 49184 | tf_op jit(solution)/shard_map/all_to_all | solution.py:1105
  92.1 10.7 %collective-permute-done.6.refs_2_ = bf16[104,768]{1,0:T(8,128)(2,1)S(1)} collective-permute-done((bf16[104,768]{1,0:T(8,128)(2,1)}, bf16[104,768]{1,0:T(8,128)(2,1)S(1)}, u32[]{:S(2)}, u32[]{:S(2)}) %collective-permute-start.6) | collective-permute-done | bytes 159776 | tf_op jit(solution)/shard_map/ppermute | solution.py:795
  118.8 24.4 %collective-permute-done.11.refs_3_ = bf16[4,8,48,384]{3,2,1,0:T(8,128)(2,1)S(1)} collective-permute-done((bf16[4,8,48,384]{3,2,1,0:T(8,128)(2,1)S(1)}, bf16[4,8,48,384]{3,2,1,0:T(8,128)(2,1)S(1)}, u32[]{:S(2)}, u32[]{:S(2)}) %collective-permute-start.11) | collective-permute-done | bytes 1179680 | tf_op jit(solution)/shard_map/ppermute | solution.py:1030
  149.0 8.2 %shard_map.195 = bf16[8,2,16,48,384]{4,3,2,1,0:T(8,128)(2,1)} custom-call(s32[5]{0:T(128)} %stack.110.me_ref, bf16[4,8,48,384]{3,2,1,0:T(8,128)(2,1)} %copy-done.22, bf16[4,8,48,384]{3,2,1,0:T(8,128)(2,1)} %copy-done.31, bf16[4,8,48,384]{3,2,1,0:T(8,128)(2,1)} %copy-done.23, bf16[4,8,48,384]{3,2,1,0:T(8,128)(2,1)} %copy-done.30, ...), custom_call_target="tpu_custom_call" | custom-call | bytes 18874368 | tf_op jit(solution)/shard_map/pallas_call | solution.py:869
  159.9 18.8 %collective-permute-done.17 = bf16[8,48,384]{2,1,0:T(8,128)(2,1)S(1)} collective-permute-done((bf16[8,48,384]{2,1,0:T(8,128)(2,1)S(1)}, bf16[8,48,384]{2,1,0:T(8,128)(2,1)S(1)}, u32[]{:S(2)}, u32[]{:S(2)}) %collective-permute-start.17) | collective-permute-done | bytes 294944 | tf_op jit(solution)/shard_map/ppermute | solution.py:834
  182.0 12.2 %shard_map.196 = (bf16[416,768]{1,0:T(8,128)(2,1)}, bf16[3,416,768]{2,1,0:T(8,128)(2,1)}, f32[2,3,2,416]{3,2,1,0:T(2,128)}, bf16[104,768]{1,0:T(8,128)(2,1)}, bf...) custom-call(bf16[104,768]{1,0:T(8,128)(2,1)} %get-tuple-element.280.refs_0_, ...), custom_call_target="tpu_custom_call" | custom-call | flops 1472200704 | bytes 14470656 | tf_op jit(solution)/shard_map/pallas_call | solution.py:194
  213.6 10.0 %shard_map.197 = (bf16[416,768]{1,0:T(8,128)(2,1)}, bf16[416,768]{1,0:T(8,128)(2,1)}, f32[416,768]{1,0:T(8,128)}, bf16[3,416,768]{2,1,0:T(8,128)(2,1)}) custom-call(s32[5]{0:T(128)} %stack.110.me_ref, bf16[104,768]{1,0:T(8,128)(2,1)} %get-tuple-element.292.refs_0_, bf16[104,768]{1,0:T(8,128)(2,1)} %copy-done.44, bf16[104,768]{1,0:T(8,128)(2,1)} %copy-done.46, ...), custom_call_target="tpu_custom_call" | custom-call | flops 2453667840 | bytes 28821524 | tf_op jit(solution)/shard_map/pallas_call | solution.py:194
  223.6 9.9 %shard_map.198 = (bf16[416,768]{1,0:T(8,128)(2,1)}, f32[416,768]{1,0:T(8,128)}, f32[2,3,2,2,208]{4,3,2,1,0:T(2,128)}) custom-call(bf16[3,416,768]{2,1,0:T(8,128)(2,1)} %get-tuple-element.296.qkv_ref, f32[416,768]{1,0:T(8,128)} %get-tuple-element.297.x1_ref, bf16[9,2,768,384]{3,2,1,0:T(8,128)(2,1)} %bitcast.201), custom_call_target="tpu_custom_call" | custom-call | flops 490733568 | bytes 15748608 | tf_op jit(solution)/shard_map/pallas_call | solution.py:194
  233.5 20.3 %collective-permute-done.25.refs_3_ = bf16[4,8,48,384]{3,2,1,0:T(8,128)(2,1)S(1)} collective-permute-done((bf16[4,8,48,384]{3,2,1,0:T(8,128)(2,1)S(1)}, bf16[4,8,48,384]{3,2,1,0:T(8,128)(2,1)S(1)}, u32[]{:S(2)}, u32[]{:S(2)}) %collective-permute-start.25) | collective-permute-done | bytes 1179680 | tf_op jit(solution)/shard_map/ppermute | solution.py:1030
  257.1 13.3 %shard_map.199 = (f32[416,768]{1,0:T(8,128)}, bf16[104,768]{1,0:T(8,128)(2,1)}, bf16[104,768]{1,0:T(8,128)(2,1)}, bf16[104,768]{1,0:T(8,128)(2,1)}, bf16[104,768]{1,0:T(8,128)(2,1)}) custom-call(f32[416,768]{1,0:T(8,128)} %get-tuple-element.301.x2_ref, bf16[8,2,768,384]{3,2,1,0:T(8,128)(2,1)} %bitcast.214, bf16[8,2,768,384]{3,2,1,0:T(8,128)(2,1)} %bitcast.215, ...), custom_call_target="tpu_custom_call" | custom-call | flops 3925868544 | bytes 22106132 | tf_op jit(solution)/shard_map/pallas_call | solution.py:194
  270.5 6.7 collective-permute-start.26
  289.4 12.2 %shard_map.200 = (bf16[416,768]{1,0:T(8,128)(2,1)}, bf16[3,416,768]{2,1,0:T(8,128)(2,1)}, f32[2,3,2,416]{3,2,1,0:T(2,128)}, bf16[104,768]{1,0:T(8,128)(2,1)}, bf...) custom-call(bf16[104,768]{1,0:T(8,128)(2,1)} %get-tuple-element.310.refs_0_, ...), custom_call_target="tpu_custom_call" | custom-call | flops 1472200704 | bytes 14470656 | tf_op jit(solution)/shard_map/pallas_call | solution.py:194
  308.4 8.2 %shard_map.203 = bf16[8,2,16,48,384]{4,3,2,1,0:T(8,128)(2,1)} custom-call(s32[5]{0:T(128)} %stack.110.me_ref, bf16[4,8,48,384]{3,2,1,0:T(8,128)(2,1)} %copy-done.20, bf16[4,8,48,384]{3,2,1,0:T(8,128)(2,1)} %copy-done.27, bf16[4,8,48,384]{3,2,1,0:T(8,128)(2,1)} %copy-done.21, bf16[4,8,48,384]{3,2,1,0:T(8,128)(2,1)} %copy-done.26, ...), custom_call_target="tpu_custom_call" | custom-call | bytes 18874368 | tf_op jit(solution)/shard_map/pallas_call | solution.py:869
  317.4 9.4 %shard_map.201 = (bf16[416,768]{1,0:T(8,128)(2,1)}, bf16[416,768]{1,0:T(8,128)(2,1)}, f32[416,768]{1,0:T(8,128)}, bf16[3,416,768]{2,1,0:T(8,128)(2,1)}) custom-call(s32[5]{0:T(128)} %stack.110.me_ref, bf16[104,768]{1,0:T(8,128)(2,1)} %get-tuple-element.314.refs_0_, bf16[104,768]{1,0:T(8,128)(2,1)} %copy-done.49, bf16[104,768]{1,0:T(8,128)(2,1)} %copy-done.50, ...), custom_call_target="tpu_custom_call" | custom-call | flops 2453667840 | bytes 28821524 | tf_op jit(solution)/shard_map/pallas_call | solution.py:194
  326.7 9.9 %shard_map.202 = (bf16[416,768]{1,0:T(8,128)(2,1)}, f32[416,768]{1,0:T(8,128)}, f32[2,3,2,2,208]{4,3,2,1,0:T(2,128)}) custom-call(bf16[3,416,768]{2,1,0:T(8,128)(2,1)} %get-tuple-element.319.qkv_ref, f32[416,768]{1,0:T(8,128)} %get-tuple-element.320.x1_ref, bf16[9,2,768,384]{3,2,1,0:T(8,128)(2,1)} %bitcast.209), custom_call_target="tpu_custom_call" | custom-call | flops 490733568 | bytes 15748608 | tf_op jit(solution)/shard_map/pallas_call | solution.py:194
  336.6 25.5 %shard_map.204 = (f32[416,768]{1,0:T(8,128)}, bf16[4,2,2,192,384]{4,3,2,1,0:T(8,128)(2,1)}, bf16[4,2,2,192,384]{4,3,2,1,0:T(8,128)(2,1)}, bf16[4,2,2,192,384]{4,...) custom-call(s32[5]{0:T(128)} %stack.110.me_ref, ...), custom_call_target="tpu_custom_call" | custom-call | flops 9814671360 | bytes 33447956 | tf_op jit(solution)/shard_map/pallas_call | solution.py:194
  362.7 21.7 %shard_map.205 = (f32[416,768]{1,0:T(8,128)}, bf16[4,2,2,192,384]{4,3,2,1,0:T(8,128)(2,1)}, bf16[4,2,2,192,384]{4,3,2,1,0:T(8,128)(2,1)}, f32[2,768]{1,0:T(2,128)}) custom-call(s32[5]{0:T(128)} %stack.110.me_ref, f32[416,768]{1,0:T(8,128)} %get-tuple-element.326.g_ref, f32[416,768]{1,0:T(8,128)} %get-tuple-element.320.x1_ref, ...), custom_call_target="tpu_custom_call" | custom-call | flops 3925868544 | bytes 32386580 | tf_op jit(solution)/shard_map/pallas_call | solution.py:194
  396.6 7.8 %shard_map.207 = (bf16[104,768]{1,0:T(8,128)(2,1)}, bf16[104,768]{1,0:T(8,128)(2,1)}, bf16[104,768]{1,0:T(8,128)(2,1)}, bf16[104,768]{1,0:T(8,128)(2,1)}, bf16[2...) custom-call(s32[5]{0:T(128)} %stack.110.me_ref, f32[416,768]{1,0:T(8,128)} %get-tuple-element.337.g_ref.refs_5_, ...), custom_call_target="tpu_custom_call" | custom-call | flops 1962934272 | bytes 17350676 | tf_op jit(solution)/shard_map/pallas_call | solution.py:194
  404.3 10.2 %collective-permute-start.39 = (bf16[104,768]{1,0:T(8,128)(2,1)}, bf16[104,768]{1,0:T(8,128)(2,1)S(1)}, u32[]{:S(2)}, u32[]{:S(2)}) collective-permute-start(bf16[104,768]{1,0:T(8,128)(2,1)} %get-tuple-element.341), channel_id=1, source_target_pairs={{0,8},{2,10},{4,12},{6,14},{8,0},{10,2},{12,4},{14,6},{16,24},{18,... | collective-permute-start | bytes 479240 | tf_op jit(solution)/shard_map/ppermute | solution.py:795
  425.2 7.3 collective-permute-start.50
  432.6 18.3 %shard_map.209 = (bf16[104,768]{1,0:T(8,128)(2,1)}, bf16[104,768]{1,0:T(8,128)(2,1)}, bf16[104,768]{1,0:T(8,128)(2,1)}, bf16[104,768]{1,0:T(8,128)(2,1)}, bf16[1...) custom-call(s32[5]{0:T(128)} %stack.110.me_ref, ...), custom_call_target="tpu_custom_call" | custom-call | flops 2944401408 | bytes 18009620 | tf_op jit(solution)/shard_map/pallas_call | solution.py:194
  453.6 15.4 %collective-permute-start.48 = (bf16[104,768]{1,0:T(8,128)(2,1)}, bf16[104,768]{1,0:T(8,128)(2,1)S(1)}, u32[]{:S(2)}, u32[]{:S(2)}) collective-permute-start(bf16[104,768]{1,0:T(8,128)(2,1)} %get-tuple-element.365), channel_id=1, source_target_pairs={{0,2},{2,0},{4,6},{6,4},{8,10},{10,8},{12,14},{14,12},{16,18},{18,... | collective-permute-start | bytes 479240 | tf_op jit(solution)/shard_map/ppermute | solution.py:795
  483.1 22.5 %shard_map.212 = (f32[416,768]{1,0:T(8,128)}, bf16[4,2,2,192,384]{4,3,2,1,0:T(8,128)(2,1)}, bf16[4,2,2,192,384]{4,3,2,1,0:T(8,128)(2,1)}, bf16[4,2,2,192,384]{4,...) custom-call(s32[5]{0:T(128)} %stack.110.me_ref, f32[416,768]{1,0:T(8,128)} %get-tuple-element.384.g_ref, ...), custom_call_target="tpu_custom_call" | custom-call | flops 9814671360 | bytes 32170004 | tf_op jit(solution)/shard_map/pallas_call | solution.py:194
  511.7 21.8 %shard_map.214 = (f32[416,768]{1,0:T(8,128)}, bf16[4,2,2,192,384]{4,3,2,1,0:T(8,128)(2,1)}, bf16[4,2,2,192,384]{4,3,2,1,0:T(8,128)(2,1)}, f32[2,768]{1,0:T(2,128)}) custom-call(s32[5]{0:T(128)} %stack.110.me_ref, f32[416,768]{1,0:T(8,128)} %get-tuple-element.394.g_ref, f32[416,768]{1,0:T(8,128)} %get-tuple-element.297.x1_ref, ...), custom_call_target="tpu_custom_call" | custom-call | flops 3925868544 | bytes 32386580 | tf_op jit(solution)/shard_map/pallas_call | solution.py:194
  536.0 8.5 %collective-permute-done.57.refs_17_ = bf16[2,192,384]{2,1,0:T(8,128)(2,1)} collective-permute-done((bf16[2,192,384]{2,1,0:T(8,128)(2,1)S(1)}, bf16[2,192,384]{2,1,0:T(8,128)(2,1)}, u32[]{:S(2)}, u32[]{:S(2)}) %collective-permute-start.57) | collective-permute-done | bytes 294944 | tf_op jit(solution)/shard_map/ppermute | solution.py:1030
  553.8 7.8 %shard_map.216 = (bf16[104,768]{1,0:T(8,128)(2,1)}, bf16[104,768]{1,0:T(8,128)(2,1)}, bf16[104,768]{1,0:T(8,128)(2,1)}, bf16[104,768]{1,0:T(8,128)(2,1)}, bf16[2...) custom-call(s32[5]{0:T(128)} %stack.110.me_ref, f32[416,768]{1,0:T(8,128)} %get-tuple-element.409.g_ref.refs_5_, ...), custom_call_target="tpu_custom_call" | custom-call | flops 1962934272 | bytes 17350676 | tf_op jit(solution)/shard_map/pallas_call | solution.py:194
  563.5 15.5 %collective-permute-done.63.refs_2_ = bf16[8,192,384]{2,1,0:T(8,128)(2,1)S(1)} collective-permute-done((bf16[8,192,384]{2,1,0:T(8,128)(2,1)}, bf16[8,192,384]{2,1,0:T(8,128)(2,1)S(1)}, u32[]{:S(2)}, u32[]{:S(2)}) %collective-permute-start.63) | collective-permute-done | bytes 1179680 | tf_op jit(solution)/shard_map/ppermute | solution.py:1030
  588.7 18.3 %shard_map.218 = (bf16[104,768]{1,0:T(8,128)(2,1)}, bf16[104,768]{1,0:T(8,128)(2,1)}, bf16[104,768]{1,0:T(8,128)(2,1)}, bf16[104,768]{1,0:T(8,128)(2,1)}, bf16[1...) custom-call(s32[5]{0:T(128)} %stack.110.me_ref, ...), custom_call_target="tpu_custom_call" | custom-call | flops 2944401408 | bytes 18009620 | tf_op jit(solution)/shard_map/pallas_call | solution.py:194
  607.6 7.6 %collective-permute-done.66.refs_3_.refs_4_ = bf16[8,192,384]{2,1,0:T(8,128)(2,1)S(1)} collective-permute-done((bf16[8,192,384]{2,1,0:T(8,128)(2,1)}, bf16[8,192,384]{2,1,0:T(8,128)(2,1)S(1)}, u32[]{:S(2)}, u32[]{:S(2)}) %collective-permute-start.66) | collective-permute-done | bytes 1179680 | tf_op jit(solution)/shard_map/ppermute | solution.py:1030
  644.0 13.5 %collective-permute-done.76.refs_3_.refs_8_ = bf16[6,192,384]{2,1,0:T(8,128)(2,1)S(1)} collective-permute-done((bf16[6,192,384]{2,1,0:T(8,128)(2,1)}, bf16[6,192,384]{2,1,0:T(8,128)(2,1)S(1)}, u32[]{:S(2)}, u32[]{:S(2)}) %collective-permute-start.76) | collective-permute-done | bytes 884768 | tf_op jit(solution)/shard_map/ppermute | solution.py:1030
  674.6 7.3 all-to-all-done.2
  707.1 21.4 %reduce-scatter.12.cloned.1.call-done = bf16[8,48,384]{2,1,0:T(8,128)(2,1)} async-done(((bf16[8,192,384]{2,1,0:T(8,128)(2,1)}), bf16[8,48,384]{2,1,0:T(8,128)(2,1)}) %reduce-scatter.12.cloned.1.call-update) | async-done | bytes 294928 | tf_op jit(solution)/shard_map/reduce_scatter | solution.py:1059
  (453 shorter events, 247.6 us)
Async XLA Ops:
  7.2 174.8 %all-gather.3.cloned.1.call-start = ((), (), s32[]{:S(2)}) async-start(), calls=%async_computation.8 | async-start | bytes 10948608 | tf_op jit(solution)/shard_map/all_gather | solution.py:824
  11.0 277.7 %all-gather.5.cloned.1.call-start = ((), (), s32[]{:S(2)}) async-start(), calls=%async_computation.9 | async-start | bytes 10948608 | tf_op jit(solution)/shard_map/all_gather | solution.py:824
  11.9 71.9 %collective-permute-start.1 = (bf16[1,2,196,768]{3,1,2,0:T(2,128)(2,1)S(1)}, bf16[1,2,196,768]{3,1,2,0:T(2,128)(2,1)S(1)}, u32[]{:S(2)}, u32[]{:S(2)}) collective-permute-start(bf16[1,2,196,768]{3,1,2,0:T(2,128)(2,1)S(1)} %copy-done.75), channel_id=1, source_target_pairs={{0,0},{2,8},{4,2},{6,10},{8,4},{10,12},{12,6},{14,14},{16,16},{18,... | collective-permute-start | bytes 1806344 | tf_op jit(solution)/shard_map/ppermute | solution.py:773
  12.9 71.0 %collective-permute-start.4 = (bf16[8,48,384]{2,1,0:T(8,128)(2,1)S(1)}, bf16[8,48,384]{2,1,0:T(8,128)(2,1)S(1)}, u32[]{:S(2)}, u32[]{:S(2)}) collective-permute-start(bf16[8,48,384]{2,1,0:T(8,128)(2,1)S(1)} %pad_maximum_fusion.13), channel_id=1, source_target_pairs={{0,6},{2,0},{4,2},{6,4},{1,7},{3,1},{5,3},{7,5},{8,14},{10,8},{12,... | collective-permute-start | bytes 884744 | tf_op jit(solution)/shard_map/ppermute | solution.py:834
  19.2 64.7 %collective-permute-start.3 = (bf16[8,48,384]{2,1,0:T(8,128)(2,1)S(1)}, bf16[8,48,384]{2,1,0:T(8,128)(2,1)S(1)}, u32[]{:S(2)}, u32[]{:S(2)}) collective-permute-start(bf16[8,48,384]{2,1,0:T(8,128)(2,1)S(1)} %pad_maximum_fusion.13), channel_id=1, source_target_pairs={{0,4},{2,6},{4,0},{6,2},{1,5},{3,7},{5,1},{7,3},{8,12},{10,14},{12... | collective-permute-start | bytes 884744 | tf_op jit(solution)/shard_map/ppermute | solution.py:834
  19.2 64.7 %collective-permute-start.2 = (bf16[8,48,384]{2,1,0:T(8,128)(2,1)S(1)}, bf16[8,48,384]{2,1,0:T(8,128)(2,1)S(1)}, u32[]{:S(2)}, u32[]{:S(2)}) collective-permute-start(bf16[8,48,384]{2,1,0:T(8,128)(2,1)S(1)} %pad_maximum_fusion.13), channel_id=1, source_target_pairs={{0,2},{2,4},{4,6},{6,0},{1,3},{3,5},{5,7},{7,1},{8,10},{10,12},{12... | collective-permute-start | bytes 884744 | tf_op jit(solution)/shard_map/ppermute | solution.py:834
  21.4 60.6 %all-to-all-start = ((f32[32,1,384]{2,1,0:T(1,128)}), f32[32,1,384]{2,1,0:T(1,128)S(1)}, u32[]{:S(2)}, u32[]{:S(2)}) async-start(f32[32,1,384]{2,1,0:T(1,128)} %broadcast_in_dim.17), calls=%async_computation | async-start | bytes 98304 | tf_op jit(solution)/shard_map/all_to_all | solution.py:1105
  26.1 640.6 %reduce-scatter.10.cloned.1.call-start = ((), (), s32[]{:S(2)}) async-start(), calls=%async_computation.12 | async-start | bytes 737280 | tf_op jit(solution)/shard_map/reduce_scatter | solution.py:1059
  83.9 28.6 %collective-permute-start.9 = (bf16[2,8,48,384]{3,2,1,0:T(8,128)(2,1)S(1)}, bf16[2,8,48,384]{3,2,1,0:T(8,128)(2,1)}, u32[]{:S(2)}, u32[]{:S(2)}) collective-permute-start(bf16[2,8,48,384]{3,2,1,0:T(8,128)(2,1)S(1)} %pad_maximum_fusion.5), channel_id=1, source_target_pairs={{0,1},{1,0},{2,3},{3,2},{4,5},{5,4},{6,7},{7,6},{8,9},{9,8},{10,11... | collective-permute-start | bytes 1769480 | tf_op jit(solution)/shard_map/ppermute | solution.py:1030
  84.8 28.6 %collective-permute-start.8 = (bf16[2,8,48,384]{3,2,1,0:T(8,128)(2,1)S(1)}, bf16[2,8,48,384]{3,2,1,0:T(8,128)(2,1)}, u32[]{:S(2)}, u32[]{:S(2)}) collective-permute-start(bf16[2,8,48,384]{3,2,1,0:T(8,128)(2,1)S(1)} %pad_maximum_fusion.4), channel_id=1, source_target_pairs={{0,16},{8,24},{16,0},{24,8},{1,17},{9,25},{17,1},{25,9},{2,18},{10... | collective-permute-start | bytes 1769480 | tf_op jit(solution)/shard_map/ppermute | solution.py:1030
  146.0 32.7 %collective-permute-start.17 = (bf16[8,48,384]{2,1,0:T(8,128)(2,1)S(1)}, bf16[8,48,384]{2,1,0:T(8,128)(2,1)S(1)}, u32[]{:S(2)}, u32[]{:S(2)}) collective-permute-start(bf16[8,48,384]{2,1,0:T(8,128)(2,1)S(1)} %pad_maximum_fusion.12), channel_id=1, source_target_pairs={{0,4},{2,6},{4,0},{6,2},{1,5},{3,7},{5,1},{7,3},{8,12},{10,14},{12... | collective-permute-start | bytes 884744 | tf_op jit(solution)/shard_map/ppermute | solution.py:834
  146.0 32.7 %collective-permute-start.16 = (bf16[8,48,384]{2,1,0:T(8,128)(2,1)S(1)}, bf16[8,48,384]{2,1,0:T(8,128)(2,1)S(1)}, u32[]{:S(2)}, u32[]{:S(2)}) collective-permute-start(bf16[8,48,384]{2,1,0:T(8,128)(2,1)S(1)} %pad_maximum_fusion.12), channel_id=1, source_target_pairs={{0,2},{2,4},{4,6},{6,0},{1,3},{3,5},{5,7},{7,1},{8,10},{10,12},{12... | collective-permute-start | bytes 884744 | tf_op jit(solution)/shard_map/ppermute | solution.py:834
  206.8 47.0 %collective-permute-start.25 = (bf16[4,8,48,384]{3,2,1,0:T(8,128)(2,1)S(1)}, bf16[4,8,48,384]{3,2,1,0:T(8,128)(2,1)S(1)}, u32[]{:S(2)}, u32[]{:S(2)}) collective-permute-start(bf16[4,8,48,384]{3,2,1,0:T(8,128)(2,1)S(1)} %pad_maximum_fusion.3.refs_2_), channel_id=1, source_target_pairs={{0,16},{8,24},{16,0},{24,8},{1,17},{9,25},{17,1},{25,9},{2,18},{10... | collective-permute-start | bytes 3538952 | tf_op jit(solution)/shard_map/ppermute | solution.py:1030
  206.9 47.8 %collective-permute-start.24 = (bf16[4,8,48,384]{3,2,1,0:T(8,128)(2,1)S(1)}, bf16[4,8,48,384]{3,2,1,0:T(8,128)(2,1)S(1)}, u32[]{:S(2)}, u32[]{:S(2)}) collective-permute-start(bf16[4,8,48,384]{3,2,1,0:T(8,128)(2,1)S(1)} %pad_maximum_fusion.2.refs_0_), channel_id=1, source_target_pairs={{0,1},{1,0},{2,3},{3,2},{4,5},{5,4},{6,7},{7,6},{8,9},{9,8},{10,11... | collective-permute-start | bytes 3538952 | tf_op jit(solution)/shard_map/ppermute | solution.py:1030
  213.1 64.1 %collective-permute-start.31 = (bf16[4,8,48,384]{3,2,1,0:T(8,128)(2,1)S(1)}, bf16[4,8,48,384]{3,2,1,0:T(8,128)(2,1)S(1)}, u32[]{:S(2)}, u32[]{:S(2)}) collective-permute-start(bf16[4,8,48,384]{3,2,1,0:T(8,128)(2,1)S(1)} %pad_maximum_fusion.3.refs_2_), channel_id=1, source_target_pairs={{0,8},{8,0},{16,24},{24,16},{1,9},{9,1},{17,25},{25,17},{2,10},{10... | collective-permute-start | bytes 3538952 | tf_op jit(solution)/shard_map/ppermute | solution.py:1030
  213.1 67.5 %collective-permute-start.29 = (bf16[4,8,48,384]{3,2,1,0:T(8,128)(2,1)S(1)}, bf16[4,8,48,384]{3,2,1,0:T(8,128)(2,1)S(1)}, u32[]{:S(2)}, u32[]{:S(2)}) collective-permute-start(bf16[4,8,48,384]{3,2,1,0:T(8,128)(2,1)S(1)} %pad_maximum_fusion.2.refs_0_), channel_id=1, source_target_pairs={{0,8},{8,0},{16,24},{24,16},{1,9},{9,1},{17,25},{25,17},{2,10},{10... | collective-permute-start | bytes 3538952 | tf_op jit(solution)/shard_map/ppermute | solution.py:1030
  254.8 34.0 %collective-permute-start.30 = (bf16[4,8,48,384]{3,2,1,0:T(8,128)(2,1)S(1)}, bf16[4,8,48,384]{3,2,1,0:T(8,128)(2,1)}, u32[]{:S(2)}, u32[]{:S(2)}) collective-permute-start(bf16[4,8,48,384]{3,2,1,0:T(8,128)(2,1)S(1)} %collective-permute-done.24.refs_1_), channel_id=1, source_target_pairs={{0,8},{8,0},{16,24},{24,16},{1,9},{9,1},{17,25},{25,17},{2,10},{10... | collective-permute-start | bytes 3538952 | tf_op jit(solution)/shard_map/ppermute | solution.py:1030
  254.8 34.0 %collective-permute-start.32 = (bf16[4,8,48,384]{3,2,1,0:T(8,128)(2,1)S(1)}, bf16[4,8,48,384]{3,2,1,0:T(8,128)(2,1)}, u32[]{:S(2)}, u32[]{:S(2)}) collective-permute-start(bf16[4,8,48,384]{3,2,1,0:T(8,128)(2,1)S(1)} %collective-permute-done.25.refs_3_), channel_id=1, source_target_pairs={{0,8},{8,0},{16,24},{24,16},{1,9},{9,1},{17,25},{25,17},{2,10},{10... | collective-permute-start | bytes 3538952 | tf_op jit(solution)/shard_map/ppermute | solution.py:1030
  384.4 30.4 %collective-permute-start.44 = (bf16[4,2,2,192,384]{4,3,2,1,0:T(8,128)(2,1)}, bf16[4,2,2,192,384]{4,3,2,1,0:T(8,128)(2,1)S(1)}, u32[]{:S(2)}, u32[]{:S(2)}) collective-permute-start(bf16[4,2,2,192,384]{4,3,2,1,0:T(8,128)(2,1)} %get-tuple-element.347), channel_id=1, source_target_pairs={{0,8},{8,0},{16,24},{24,16},{1,9},{9,1},{17,25},{25,17},{2,10},{10... | collective-permute-start | bytes 7077896 | tf_op jit(solution)/shard_map/ppermute | solution.py:1030
  425.2 28.3 %collective-permute-start.50 = (bf16[2,2,2,192,384]{4,3,2,1,0:T(8,128)(2,1)S(1)}, bf16[2,2,2,192,384]{4,3,2,1,0:T(8,128)(2,1)S(1)}, u32[]{:S(2)}, u32[]{:S(2)}) collective-permute-start(bf16[2,2,2,192,384]{4,3,2,1,0:T(8,128)(2,1)S(1)} %copy-done.74), channel_id=1, source_target_pairs={{0,8},{8,0},{16,24},{24,16},{1,9},{9,1},{17,25},{25,17},{2,10},{10... | collective-permute-start | bytes 3538952 | tf_op jit(solution)/shard_map/ppermute | solution.py:1030
  477.0 29.2 %collective-permute-start.54 = (bf16[6,192,384]{2,1,0:T(8,128)(2,1)}, bf16[6,192,384]{2,1,0:T(8,128)(2,1)S(1)}, u32[]{:S(2)}, u32[]{:S(2)}) collective-permute-start(bf16[6,192,384]{2,1,0:T(8,128)(2,1)} %get-tuple-element.386), channel_id=1, source_target_pairs={{0,1},{1,0},{2,3},{3,2},{4,5},{5,4},{6,7},{7,6},{8,9},{9,8},{10,11... | collective-permute-start | bytes 2654216 | tf_op jit(solution)/shard_map/ppermute | solution.py:1030
  505.6 40.7 %collective-permute-start.58 = (bf16[4,2,2,192,384]{4,3,2,1,0:T(8,128)(2,1)}, bf16[4,2,2,192,384]{4,3,2,1,0:T(8,128)(2,1)}, u32[]{:S(2)}, u32[]{:S(2)}) collective-permute-start(bf16[4,2,2,192,384]{4,3,2,1,0:T(8,128)(2,1)} %get-tuple-element.403), channel_id=1, source_target_pairs={{0,8},{8,0},{16,24},{24,16},{1,9},{9,1},{17,25},{25,17},{2,10},{10... | collective-permute-start | bytes 7077896 | tf_op jit(solution)/shard_map/ppermute | solution.py:1030
  505.7 40.7 %collective-permute-start.59 = (bf16[4,2,2,192,384]{4,3,2,1,0:T(8,128)(2,1)}, bf16[4,2,2,192,384]{4,3,2,1,0:T(8,128)(2,1)}, u32[]{:S(2)}, u32[]{:S(2)}) collective-permute-start(bf16[4,2,2,192,384]{4,3,2,1,0:T(8,128)(2,1)} %get-tuple-element.405), channel_id=1, source_target_pairs={{0,8},{8,0},{16,24},{24,16},{1,9},{9,1},{17,25},{25,17},{2,10},{10... | collective-permute-start | bytes 7077896 | tf_op jit(solution)/shard_map/ppermute | solution.py:1030
  533.5 29.8 %collective-permute-start.65 = (bf16[4,2,2,192,384]{4,3,2,1,0:T(8,128)(2,1)}, bf16[4,2,2,192,384]{4,3,2,1,0:T(8,128)(2,1)S(1)}, u32[]{:S(2)}, u32[]{:S(2)}) collective-permute-start(bf16[4,2,2,192,384]{4,3,2,1,0:T(8,128)(2,1)} %get-tuple-element.419), channel_id=1, source_target_pairs={{0,8},{8,0},{16,24},{24,16},{1,9},{9,1},{17,25},{25,17},{2,10},{10... | collective-permute-start | bytes 7077896 | tf_op jit(solution)/shard_map/ppermute | solution.py:1030
  533.6 134.1 %reduce-scatter.14.cloned.1.call-start = ((), (), s32[]{:S(2)}) async-start(), calls=%async_computation.14 | async-start | bytes 1474560 | tf_op jit(solution)/shard_map/reduce_scatter | solution.py:1059
  553.6 129.6 %reduce-scatter.6.cloned.1.call-start = ((), (), s32[]{:S(2)}) async-start(), calls=%async_computation.10 | async-start | bytes 921600 | tf_op jit(solution)/shard_map/reduce_scatter | solution.py:1059
  586.5 28.7 %collective-permute-start.66 = (bf16[8,192,384]{2,1,0:T(8,128)(2,1)}, bf16[8,192,384]{2,1,0:T(8,128)(2,1)S(1)}, u32[]{:S(2)}, u32[]{:S(2)}) collective-permute-start(bf16[8,192,384]{2,1,0:T(8,128)(2,1)} %get-tuple-element.436), channel_id=1, source_target_pairs={{0,1},{1,0},{2,3},{3,2},{4,5},{5,4},{6,7},{7,6},{8,9},{9,8},{10,11... | collective-permute-start | bytes 3538952 | tf_op jit(solution)/shard_map/ppermute | solution.py:1030
  587.9 28.9 %collective-permute-start.67 = (bf16[8,192,384]{2,1,0:T(8,128)(2,1)}, bf16[8,192,384]{2,1,0:T(8,128)(2,1)}, u32[]{:S(2)}, u32[]{:S(2)}) collective-permute-start(bf16[8,192,384]{2,1,0:T(8,128)(2,1)} %get-tuple-element.437), channel_id=1, source_target_pairs={{0,16},{8,24},{16,0},{24,8},{1,17},{9,25},{17,1},{25,9},{2,18},{10... | collective-permute-start | bytes 3538952 | tf_op jit(solution)/shard_map/ppermute | solution.py:1030
  588.7 28.5 %collective-permute-start.71 = (bf16[2,2,2,192,384]{4,3,2,1,0:T(8,128)(2,1)}, bf16[2,2,2,192,384]{4,3,2,1,0:T(8,128)(2,1)S(1)}, u32[]{:S(2)}, u32[]{:S(2)}) collective-permute-start(bf16[2,2,2,192,384]{4,3,2,1,0:T(8,128)(2,1)} %get-tuple-element.445), channel_id=1, source_target_pairs={{0,8},{8,0},{16,24},{24,16},{1,9},{9,1},{17,25},{25,17},{2,10},{10... | collective-permute-start | bytes 3538952 | tf_op jit(solution)/shard_map/ppermute | solution.py:1030
  616.3 88.4 %reduce-scatter.8.cloned.1.call-start = ((), (), s32[]{:S(2)}) async-start(), calls=%async_computation.11 | async-start | bytes 737280 | tf_op jit(solution)/shard_map/reduce_scatter | solution.py:1059
  666.4 62.1 %reduce-scatter.12.cloned.1.call-start = ((), (), s32[]{:S(2)}) async-start(), calls=%async_computation.13 | async-start | bytes 1474560 | tf_op jit(solution)/shard_map/reduce_scatter | solution.py:1059
  701.1 32.5 %all-to-all-start.1 = ((bf16[4,5,48,384]{3,2,1,0:T(8,128)(2,1)}), bf16[4,5,48,384]{3,2,1,0:T(8,128)(2,1)S(1)}, u32[]{:S(2)}, u32[]{:S(2)}) async-start(bf16[4,5,48,384]{3,2,1,0:T(8,128)(2,1)} %shard_map.222), calls=%async_computation.1 | async-start | bytes 1474560 | tf_op jit(solution)/shard_map/all_to_all | solution.py:1056
  (137 other events, 1506.4 us)
Sparse Core Ops, SparseCore 0:
  11.7 121.0 all-gather.2
  136.4 135.5 all-gather.4
  533.7 20.4 reduce-scatter.9
  556.4 33.5 reduce-scatter.13
  616.4 24.5 reduce-scatter.5
  666.6 22.0 reduce-scatter.7
  691.0 37.4 reduce-scatter.11

commit v12 on v11

--- a/solution.py
+++ b/solution.py
@@ -284,7 +284,7 @@
     return got[0], got[1], got[2], got[3:]
 
 
-def middle_forward(rows, back, x, w, mix, gb, me):
+def middle_forward(rows, back, x, w, ws, mix, gb, me):
     t, d = x.shape
     width = w.shape[3]
     shares = w.shape[1]
@@ -312,14 +312,14 @@
             SCALARS,
             *(whole(c.shape) for c in back),
             whole(x.shape),
-            pl.BlockSpec((1, shares, d, width), lambda i: (6, 0, 0, 0)),
-            pl.BlockSpec((3, shares, d, width), lambda i: (1, 0, 0, 0)),
+            pl.BlockSpec((1, shares, d, width), lambda i: (3, 0, 0, 0)),
+            pl.BlockSpec((3, shares, d, width), lambda i: (0, 0, 0, 0)),
             whole(mix.shape),
             whole(gb.shape),
         ],
         [made((t, d), BF16), made((t, d), BF16), made((t, d), F32), made((3, t, d), BF16)],
         [],
-        (me, *back, x, w, w, mix, gb),
+        (me, *back, x, w, ws, mix, gb),
         flops=2 * t * d * 5 * d,
     )
 
@@ -358,7 +358,7 @@
         [
             pl.BlockSpec((3, t, width), lambda h: (0, 0, h)),
             whole(x1.shape),
-            slabs(1, 7, width, d),
+            slabs(1, 3, width, d),
         ],
         [
             made((t, d), BF16, (t, width), lambda h: (0, h)),
@@ -386,7 +386,7 @@
     t, d = x2.shape
     width = w.shape[3]
     shares = w.shape[1]
-    per_share = w.shape[0] // 2
+    per_share = (w.shape[0] - 4) // 2
     steps = shares * per_share
 
     def body(x2_ref, wi_ref, wo_ref, gb_ref, me_ref, gn_ref, x3_ref, *rest):
@@ -410,8 +410,8 @@
 
     ins = [
         whole(x2.shape),
-        ff_slab(0, per_share, d, width),
-        ff_slab(per_share, per_share, d, width),
+        ff_slab(4, per_share, d, width),
+        ff_slab(4 + per_share, per_share, d, width),
         whole(gb.shape),
     ]
     ins += [SCALARS, whole(gb_next.shape)]
@@ -426,7 +426,7 @@
     t, d = x2.shape
     width = w.shape[3]
     shares = w.shape[1]
-    per_share = w.shape[0] // 2
+    per_share = (w.shape[0] - 4) // 2
     steps = shares * per_share
 
     def body(me_ref, g_ref, x2_ref, wi_ref, wo_ref, gb_ref, go_ref, ki_ref, si_ref, ko_ref, so_ref, sums_ref, *rest):
@@ -479,8 +479,8 @@
             SCALARS,
             whole(grad.shape),
             whole(x2.shape),
-            ff_slab(0, per_share, d, width),
-            ff_slab(per_share, per_share, d, width),
+            ff_slab(4, per_share, d, width),
+            ff_slab(4 + per_share, per_share, d, width),
             whole(gb.shape),
         ],
         [made((t, d), F32), *slab_outs, made((2, d), F32)] + [made((t, d), F32)] * with_output,
@@ -564,8 +564,8 @@
             pl.BlockSpec((3, t, width), lambda h: (0, 0, h)),
             pl.BlockSpec((t, width), lambda h: (0, h)),
             pl.BlockSpec((1,) + logs.shape[1:], lambda h: (h, 0, 0, 0, 0)),
-            slabs(1, 7, width, d),
-            slabs(3, 3, width, d),
+            slabs(1, 3, width, d),
+            slabs(3, 0, width, d),
             whole(gb.shape),
         ],
         [
@@ -640,7 +640,7 @@
             whole(grad.shape),
             whole(y1.shape),
             whole(o1.shape),
-            pl.BlockSpec((1, shares, d, width), lambda i: (6, 0, 0, 0)),
+            pl.BlockSpec((1, shares, d, width), lambda i: (3, 0, 0, 0)),
             whole(mix.shape),
         ],
         outs,
@@ -800,24 +800,23 @@
     return a.reshape(r, -1, width).transpose(1, 0, 2)
 
 
-def pack_attention(time_qkv, time_out, time_mix, space_qkv, space_out):
+def pack_time(time_qkv, time_out, time_mix):
     r, _, width = time_qkv.shape
     mix = time_mix.reshape(-1, time_mix.shape[1] // width, width).transpose(1, 0, 2).reshape(1, r, width)
+    return jnp.concatenate((columns(time_qkv, r, width), time_out.T[None], mix), axis=0)
+
+
+def pack_rest(space_qkv, space_out, mlp_in, mlp_out):
+    r, _, width = space_qkv.shape
     return jnp.concatenate(
         (
-            columns(time_qkv, r, width),
             columns(space_qkv, r, width),
-            time_out.T[None],
             space_out.T[None],
-            mix,
+            columns(mlp_in, r, width),
+            columns(mlp_out.T, r, width),
         ),
         axis=0,
     )
-
-
-def pack_feed_forward(mlp_in, mlp_out, width):
-    r = mlp_in.shape[0]
-    return jnp.concatenate((columns(mlp_in, r, width), columns(mlp_out.T, r, width)), axis=0)
 
 
 def gather_slabs(pack):
@@ -838,14 +837,17 @@
     some = [jnp.stack([turned[k] for k in steps]) for steps, _, _ in orders]
     come = yield [cross(a, first) for a, (_, first, _) in zip(some, orders)]
     some = [jnp.concatenate(pair, axis=0) for pair in zip(some, come)]
-    come = yield [cross(a, second) for a, (_, _, second) in zip(some, orders)]
+    come = yield [cross(a, second) for a, (_, _, second) in zip(some, orders)] + [
+        cross(a, "c") for a in some
+    ]
+    far = yield come + [cross(a, "c") for a in come[:2]]
+    come, far = far[:2], far[2:]
     runs = []
-    for mine, other, (steps, first, second) in zip(some, come, orders):
+    for i, (steps, first, second) in enumerate(orders):
         where = [(k, {first: f}) for f in (0, 1) for k in steps]
-        for g, blocks in enumerate((mine, other)):
-            runs.append((blocks, [(k, {**at, second: g}) for k, at in where], 0))
-    come = yield [cross(blocks, "c") for blocks, _, _ in runs]
-    runs += [(far, where, 1) for far, (_, where, _) in zip(come, runs)]
+        near = [(k, {**at, second: 0}) for k, at in where]
+        past = [(k, {**at, second: 1}) for k, at in where]
+        runs += [(some[i], near, 0), (come[i], past, 0), (far[i], near, 1), (far[2 + i], past, 1)]
     count = sum(len(where) for _, where, _ in runs)
 
     def body(me_ref, *refs):
@@ -885,9 +887,13 @@
         self.way = spread_steps(pack, me)
         self.come = next(self.way)
 
+    def hold(self, x):
+        x, self.come = lax.optimization_barrier((x, self.come))
+        return x
+
     def step(self, x):
-        x, come = lax.optimization_barrier((x, self.come))
-        self.come = self.way.send(come)
+        x = self.hold(x)
+        self.come = self.way.send(self.come)
         return x
 
 
@@ -1151,10 +1157,10 @@
     gbs = gather_norms(norm_gain, norm_bias)
     gb = [gbs[l] for l in range(layers)]
     packs = [
-        pack_attention(time_qkv[l], time_out[l], time_mix[l], space_qkv[l], space_out[l])
+        pack_time(time_qkv[l], time_out[l], time_mix[l])
         for l in range(layers)
     ]
-    packs_ff = [pack_feed_forward(mlp_in[l], mlp_out[l], time_qkv.shape[3]) for l in range(layers)]
+    packs_ff = [pack_rest(space_qkv[l], space_out[l], mlp_in[l], mlp_out[l]) for l in range(layers)]
     weights = [gather_slabs(pack) for pack in packs]
     mixes = [mix_whole(w[-1], shards) for w in weights]
     quick = lax.axis_size("clip") == 4 and shares == 2 and ways == 4 and time_qkv.shape[1] % 16 == 0
@@ -1167,18 +1173,14 @@
     )
     if quick:
         spreads = [Spread(pack, me) for pack in packs_ff]
-        spreads[0].step(())
         weights_ff = []
     else:
         weights_ff = [gather_slabs(pack) for pack in packs_ff]
 
     home = go_home(tokens)
     if quick:
-        (home, gb, later), first = (home, gb, packs_ff[1:]), spreads[0]
-        home, gb, later = first.step((home, gb, later))
-        for spread, pack in zip(spreads[1:], later):
-            spread.come = pack
-            spread.step(())
+        first = spreads[0]
+        home, gb = first.step((home, gb))
     x = as_rows(home)
     send = send_first(rows, x, gb[0], me)
     kept = []
@@ -1186,22 +1188,23 @@
         w = weights[l]
         send = swap_places(send)
         if quick and l == 0:
-            for _ in range(3):
-                send = first.step(send)
-            weights_ff.append(first.come)
-            send, weights_ff[0] = lax.optimization_barrier((send, weights_ff[0]))
+            send = first.step(send)
             for spread in spreads[1:]:
                 send = spread.step(send)
-        elif quick:
-            send = spreads[l].step(send)
-            weights_ff.append(spreads[l].come)
+            send = first.step(send)
+            for spread in spreads[1:]:
+                send = spread.hold(send)
         a1, qkv1, log1, o1_time = time_forward(rows, send, w)
         back = swap_places(o1_time)
-        if quick and l == 0:
-            for spread in spreads[1:]:
-                back = spread.step(back)
-        o1, y1, x1, qkv2 = middle_forward(rows, back, x, w, mixes[l], gb[l], me)
-        o2, x2, log2 = space_forward(rows, qkv2, x1, w)
+        if quick:
+            for _ in range(2):
+                back = spreads[l].step(back)
+            if l == 0:
+                for spread in spreads[1:]:
+                    back = spread.step(back)
+            weights_ff.append(spreads[l].come)
+        o1, y1, x1, qkv2 = middle_forward(rows, back, x, w, weights_ff[l], mixes[l], gb[l], me)
+        o2, x2, log2 = space_forward(rows, qkv2, x1, weights_ff[l])
         if quick and l == 0:
             for spread in spreads[1:]:
                 x2 = spread.step(x2)
@@ -1227,7 +1230,9 @@
                 grad = settle(grad, late)
                 grad = move(grad, late, me)
                 late = [p for p in late if p.step < 3]
-        grad, g_space, s2 = space_backward(rows, grad, x1, qkv2, o2, log2, w, gb[l], me, halves)
+        grad, g_space, s2 = space_backward(
+            rows, grad, x1, qkv2, o2, log2, weights_ff[l], gb[l], me, halves
+        )
         if quick:
             space = pieces_of([g_space])
             if late:

time: 749 us -> 793 us (1.059)
  starting transfers between devices: 117 us -> 145 us
    all_to_all x1, waiting for transfers between devices: 55.8 us -> 3.04 us  [gather_norms(): lax.all_to_all(jnp.broadcast_to(padded, (count, width)), ALL, split_axis=...]
    ppermute x6, waiting for transfers between devices: 21.5 us -> 64.6 us  [spread_steps(): lax.ppermute(pack, 'seq', [(i, (i + k) % ways) for i in range(ways)])]
    ppermute x24, waiting for transfers between devices: 36.5 us -> 75.9 us  [swap_places(): got.append(lax.ppermute(chunks[k], ('clip', 'seq'), pairs))]
    ppermute x46, waiting for transfers between devices: 118 us -> 84.8 us  [cross(): return lax.ppermute(a, axis, [(i, i ^ 1 << bit) for i in range(size)])]
    ppermute x24, starting transfers between devices: 48.2 us -> 66.8 us  [swap_places(): got.append(lax.ppermute(chunks[k], ('clip', 'seq'), pairs))]
    unnamed x171 -> x179, local copies, waits for them, and re-layouts: 22.6 us -> 21.8 us
  transfers between devices with their start and end apart: 90 -> 90, of which waited for: 34 -> 38; matrix products, arithmetic and copies ran while one was open for 5% -> 6% of each run, Pallas kernels for 32% -> 31%
where the time goes in v12:
time: 793 us; the launch traced here: 787 us
  Pallas kernels  299 us (38%)
  waiting for transfers between devices  259 us (33%)
  starting transfers between devices  145 us (18%)
  local copies, waits for them, and re-layouts  41.6 us (5%)
  other arithmetic  26.2 us (3%)
  between operations  15.9 us (2%)
    pallas_call x18, Pallas kernels, call(): pl.pallas_call(body, out_shape=[shape for shape, _ in outs], grid=grid, i...  232 us
    ppermute x46, waiting for transfers between devices, cross(): return lax.ppermute(a, axis, [(i, i ^ 1 << bit) for i in range(size)])  84.8 us
    ppermute x24, waiting for transfers between devices, swap_places(): got.append(lax.ppermute(chunks[k], ('clip', 'seq'), pairs))  75.9 us
    ppermute x24, starting transfers between devices, swap_places(): got.append(lax.ppermute(chunks[k], ('clip', 'seq'), pairs))  66.8 us
    ppermute x6, waiting for transfers between devices, spread_steps(): lax.ppermute(pack, 'seq', [(i, (i + k) % ways) for i in range(ways)])  64.6 us
    pallas_call x9, Pallas kernels, fold(): pl.pallas_call(body, out_shape=[jax.ShapeDtypeStruct(shape, BF16) for sha...  45.6 us
    ppermute x46, starting transfers between devices, cross(): return lax.ppermute(a, axis, [(i, i ^ 1 << bit) for i in range(size)])  43.2 us
    pallas_call x2, Pallas kernels, spread_steps(): pl.pallas_call(body, out_shape=jax.ShapeDtypeStruct((n, shares, clips * w...  22 us
  transfers between devices with their start and end apart: 90, of which 38 were waited for; matrix products, arithmetic and copies ran while one was open for 6% of the time, Pallas kernels for 31%

profile of v12, /device:TPU:0, one launch (start us, length us, event | category | flops | bytes accessed | tf_op | source)
XLA Modules:
  0.0 787.2 jit_solution(4366205956163959357)
XLA Ops:
  28.7 8.3 %collective-permute-start.7 = (bf16[12,48,384]{2,1,0:T(8,128)(2,1)S(1)}, bf16[12,48,384]{2,1,0:T(8,128)(2,1)S(1)}, u32[]{:S(2)}, u32[]{:S(2)}) collective-permute-start(bf16[12,48,384]{2,1,0:T(8,128)(2,1)S(1)} %pad_maximum_fusion.10), channel_id=1, source_target_pairs={{0,6},{2,0},{4,2},{6,4},{1,7},{3,1},{5,3},{7,5},{8,14},{10,8},{12,... | collective-permute-start | bytes 1327112 | tf_op jit(solution)/shard_map/ppermute | solution.py:833
  37.1 8.2 %collective-permute-start.6 = (bf16[12,48,384]{2,1,0:T(8,128)(2,1)S(1)}, bf16[12,48,384]{2,1,0:T(8,128)(2,1)S(1)}, u32[]{:S(2)}, u32[]{:S(2)}) collective-permute-start(bf16[12,48,384]{2,1,0:T(8,128)(2,1)S(1)} %pad_maximum_fusion.10), channel_id=1, source_target_pairs={{0,4},{2,6},{4,0},{6,2},{1,5},{3,7},{5,1},{7,3},{8,12},{10,14},{12... | collective-permute-start | bytes 1327112 | tf_op jit(solution)/shard_map/ppermute | solution.py:833
  49.4 27.1 %collective-permute-start.2 = (bf16[104,768]{1,0:T(8,128)(2,1)}, bf16[104,768]{1,0:T(8,128)(2,1)S(1)}, u32[]{:S(2)}, u32[]{:S(2)}) collective-permute-start(bf16[104,768]{1,0:T(8,128)(2,1)} %get-tuple-element.268), channel_id=1, source_target_pairs={{0,8},{2,10},{4,12},{6,14},{8,0},{10,2},{12,4},{14,6},{16,24},{18,... | collective-permute-start | bytes 479240 | tf_op jit(solution)/shard_map/ppermute | solution.py:795
  77.9 12.9 %collective-permute-done.3.refs_2_ = bf16[104,768]{1,0:T(8,128)(2,1)S(1)} collective-permute-done((bf16[104,768]{1,0:T(8,128)(2,1)}, bf16[104,768]{1,0:T(8,128)(2,1)S(1)}, u32[]{:S(2)}, u32[]{:S(2)}) %collective-permute-start.3) | collective-permute-done | bytes 159776 | tf_op jit(solution)/shard_map/ppermute | solution.py:795
  90.8 19.7 %collective-permute-done.4.refs_3_ = bf16[104,768]{1,0:T(8,128)(2,1)S(1)} collective-permute-done((bf16[104,768]{1,0:T(8,128)(2,1)}, bf16[104,768]{1,0:T(8,128)(2,1)S(1)}, u32[]{:S(2)}, u32[]{:S(2)}) %collective-permute-start.4) | collective-permute-done | bytes 159776 | tf_op jit(solution)/shard_map/ppermute | solution.py:795
  119.3 12.4 %collective-permute-done.9 = bf16[2,12,48,384]{3,2,1,0:T(8,128)(2,1)S(1)} collective-permute-done((bf16[2,12,48,384]{3,2,1,0:T(8,128)(2,1)S(1)}, bf16[2,12,48,384]{3,2,1,0:T(8,128)(2,1)S(1)}, u32[]{:S(2)}, u32[]{:S(2)}) %collective-permute-start.9) | collective-permute-done | bytes 884768 | tf_op jit(solution)/shard_map/ppermute | solution.py:1036
  139.8 16.8 %collective-permute-done.12 = bf16[12,48,384]{2,1,0:T(8,128)(2,1)S(1)} collective-permute-done((bf16[12,48,384]{2,1,0:T(8,128)(2,1)S(1)}, bf16[12,48,384]{2,1,0:T(8,128)(2,1)S(1)}, u32[]{:S(2)}, u32[]{:S(2)}) %collective-permute-start.12) | collective-permute-done | bytes 442400 | tf_op jit(solution)/shard_map/ppermute | solution.py:833
  156.6 31.9 %collective-permute-done.11 = bf16[12,48,384]{2,1,0:T(8,128)(2,1)S(1)} collective-permute-done((bf16[12,48,384]{2,1,0:T(8,128)(2,1)S(1)}, bf16[12,48,384]{2,1,0:T(8,128)(2,1)S(1)}, u32[]{:S(2)}, u32[]{:S(2)}) %collective-permute-start.11) | collective-permute-done | bytes 442400 | tf_op jit(solution)/shard_map/ppermute | solution.py:833
  189.3 15.9 %collective-permute-done.10 = bf16[12,48,384]{2,1,0:T(8,128)(2,1)} collective-permute-done((bf16[12,48,384]{2,1,0:T(8,128)(2,1)S(1)}, bf16[12,48,384]{2,1,0:T(8,128)(2,1)}, u32[]{:S(2)}, u32[]{:S(2)}) %collective-permute-start.10) | collective-permute-done | bytes 442400 | tf_op jit(solution)/shard_map/ppermute | solution.py:833
  205.1 12.4 %shard_map.195 = (bf16[416,768]{1,0:T(8,128)(2,1)}, bf16[3,416,768]{2,1,0:T(8,128)(2,1)}, f32[2,3,2,416]{3,2,1,0:T(2,128)}, bf16[104,768]{1,0:T(8,128)(2,1)}, bf...) custom-call(bf16[104,768]{1,0:T(8,128)(2,1)} %get-tuple-element.289.refs_0_, ...), custom_call_target="tpu_custom_call" | custom-call | flops 1472200704 | bytes 9752064 | tf_op jit(solution)/shard_map/pallas_call | solution.py:194
  240.8 11.0 %shard_map.196 = bf16[12,2,16,48,384]{4,3,2,1,0:T(8,128)(2,1)} custom-call(s32[5]{0:T(128)} %stack.110.me_ref, bf16[4,12,48,384]{3,2,1,0:T(8,128)(2,1)} %copy-done.9, bf16[4,12,48,384]{3,2,1,0:T(8,128)(2,1)} %collective-permute-done.16.refs_1_, bf16[4,12,48,384]{3,2,1,0:T(8,128)(2,1)} %collective-permute-done.18.refs_2_, ...), custom_call_target="tpu_custom_call" | custom-call | bytes 28311552 | tf_op jit(solution)/shard_map/pallas_call | solution.py:871
  251.8 9.4 %shard_map.197 = (bf16[416,768]{1,0:T(8,128)(2,1)}, bf16[416,768]{1,0:T(8,128)(2,1)}, f32[416,768]{1,0:T(8,128)}, bf16[3,416,768]{2,1,0:T(8,128)(2,1)}) custom-call(s32[5]{0:T(128)} %stack.110.me_ref, bf16[104,768]{1,0:T(8,128)(2,1)} %get-tuple-element.315.refs_0_, bf16[104,768]{1,0:T(8,128)(2,1)} %copy-done.62, bf16[104,768]{1,0:T(8,128)(2,1)} %copy-done.64, ...), custom_call_target="tpu_custom_call" | custom-call | flops 2453667840 | bytes 27641876 | tf_op jit(solution)/shard_map/pallas_call | solution.py:194
  261.2 9.9 %shard_map.198 = (bf16[416,768]{1,0:T(8,128)(2,1)}, f32[416,768]{1,0:T(8,128)}, f32[2,3,2,2,208]{4,3,2,1,0:T(2,128)}) custom-call(bf16[3,416,768]{2,1,0:T(8,128)(2,1)} %get-tuple-element.325.qkv_ref, f32[416,768]{1,0:T(8,128)} %get-tuple-element.326.x1_ref, bf16[12,2,768,384]{3,2,1,0:T(8,128)(2,1)} %bitcast.197), custom_call_target="tpu_custom_call" | custom-call | flops 490733568 | bytes 19287552 | tf_op jit(solution)/shard_map/pallas_call | solution.py:194
  274.9 13.2 %shard_map.199 = (f32[416,768]{1,0:T(8,128)}, bf16[104,768]{1,0:T(8,128)(2,1)}, bf16[104,768]{1,0:T(8,128)(2,1)}, bf16[104,768]{1,0:T(8,128)(2,1)}, bf16[104,768]{1,0:T(8,128)(2,1)}) custom-call(f32[416,768]{1,0:T(8,128)} %get-tuple-element.332.x2_ref, bf16[12,2,768,384]{3,2,1,0:T(8,128)(2,1)} %bitcast.198, bf16[12,2,768,384]{3,2,1,0:T(8,128)(2,1)} %bitcast.199, ...), custom_call_target="tpu_custom_call" | custom-call | flops 3925868544 | bytes 31543316 | tf_op jit(solution)/shard_map/pallas_call | solution.py:194
  302.6 12.4 %shard_map.200 = (bf16[416,768]{1,0:T(8,128)(2,1)}, bf16[3,416,768]{2,1,0:T(8,128)(2,1)}, f32[2,3,2,416]{3,2,1,0:T(2,128)}, bf16[104,768]{1,0:T(8,128)(2,1)}, bf...) custom-call(bf16[104,768]{1,0:T(8,128)(2,1)} %get-tuple-element.334.refs_0_, ...), custom_call_target="tpu_custom_call" | custom-call | flops 1472200704 | bytes 9752064 | tf_op jit(solution)/shard_map/pallas_call | solution.py:194
  337.9 11.0 %shard_map.201 = bf16[12,2,16,48,384]{4,3,2,1,0:T(8,128)(2,1)} custom-call(s32[5]{0:T(128)} %stack.110.me_ref, bf16[4,12,48,384]{3,2,1,0:T(8,128)(2,1)} %copy-done.7, bf16[4,12,48,384]{3,2,1,0:T(8,128)(2,1)} %collective-permute-done.30.refs_1_, bf16[4,12,48,384]{3,2,1,0:T(8,128)(2,1)} %collective-permute-done.32.refs_2_, ...), custom_call_target="tpu_custom_call" | custom-call | bytes 28311552 | tf_op jit(solution)/shard_map/pallas_call | solution.py:871
  348.9 9.3 %shard_map.202 = (bf16[416,768]{1,0:T(8,128)(2,1)}, bf16[416,768]{1,0:T(8,128)(2,1)}, f32[416,768]{1,0:T(8,128)}, bf16[3,416,768]{2,1,0:T(8,128)(2,1)}) custom-call(s32[5]{0:T(128)} %stack.110.me_ref, bf16[104,768]{1,0:T(8,128)(2,1)} %get-tuple-element.352.refs_0_, bf16[104,768]{1,0:T(8,128)(2,1)} %copy-done.61, bf16[104,768]{1,0:T(8,128)(2,1)} %copy-done.63, ...), custom_call_target="tpu_custom_call" | custom-call | flops 2453667840 | bytes 27641876 | tf_op jit(solution)/shard_map/pallas_call | solution.py:194
  358.3 10.3 %shard_map.203 = (bf16[416,768]{1,0:T(8,128)(2,1)}, f32[416,768]{1,0:T(8,128)}, f32[2,3,2,2,208]{4,3,2,1,0:T(2,128)}) custom-call(bf16[3,416,768]{2,1,0:T(8,128)(2,1)} %get-tuple-element.363.qkv_ref, f32[416,768]{1,0:T(8,128)} %get-tuple-element.364.x1_ref, bf16[12,2,768,384]{3,2,1,0:T(8,128)(2,1)} %bitcast.205), custom_call_target="tpu_custom_call" | custom-call | flops 490733568 | bytes 19287552 | tf_op jit(solution)/shard_map/pallas_call | solution.py:194
  368.6 25.2 %shard_map.204 = (f32[416,768]{1,0:T(8,128)}, bf16[4,2,2,192,384]{4,3,2,1,0:T(8,128)(2,1)}, bf16[4,2,2,192,384]{4,3,2,1,0:T(8,128)(2,1)}, bf16[4,2,2,192,384]{4,...) custom-call(s32[5]{0:T(128)} %stack.110.me_ref, ...), custom_call_target="tpu_custom_call" | custom-call | flops 9814671360 | bytes 42885140 | tf_op jit(solution)/shard_map/pallas_call | solution.py:194
  393.8 10.8 %collective-permute-start.37 = (bf16[4,2,2,192,384]{4,3,2,1,0:T(8,128)(2,1)}, bf16[4,2,2,192,384]{4,3,2,1,0:T(8,128)(2,1)S(1)}, u32[]{:S(2)}, u32[]{:S(2)}) collective-permute-start(bf16[4,2,2,192,384]{4,3,2,1,0:T(8,128)(2,1)} %get-tuple-element.372), channel_id=1, source_target_pairs={{0,8},{8,0},{16,24},{24,16},{1,9},{9,1},{17,25},{25,17},{2,10},{10... | collective-permute-start | bytes 7077896 | tf_op jit(solution)/shard_map/ppermute | solution.py:1036
  404.7 21.7 %shard_map.205 = (f32[416,768]{1,0:T(8,128)}, bf16[4,2,2,192,384]{4,3,2,1,0:T(8,128)(2,1)}, bf16[4,2,2,192,384]{4,3,2,1,0:T(8,128)(2,1)}, f32[2,768]{1,0:T(2,128)}) custom-call(s32[5]{0:T(128)} %stack.110.me_ref, f32[416,768]{1,0:T(8,128)} %get-tuple-element.366.g_ref, f32[416,768]{1,0:T(8,128)} %get-tuple-element.364.x1_ref, ...), custom_call_target="tpu_custom_call" | custom-call | flops 3925868544 | bytes 39464468 | tf_op jit(solution)/shard_map/pallas_call | solution.py:194
  446.3 12.9 %collective-permute-start.39 = (bf16[104,768]{1,0:T(8,128)(2,1)}, bf16[104,768]{1,0:T(8,128)(2,1)S(1)}, u32[]{:S(2)}, u32[]{:S(2)}) collective-permute-start(bf16[104,768]{1,0:T(8,128)(2,1)} %get-tuple-element.381), channel_id=1, source_target_pairs={{0,8},{2,10},{4,12},{6,14},{8,0},{10,2},{12,4},{14,6},{16,24},{18,... | collective-permute-start | bytes 479240 | tf_op jit(solution)/shard_map/ppermute | solution.py:795
  474.8 18.3 %shard_map.209 = (bf16[104,768]{1,0:T(8,128)(2,1)}, bf16[104,768]{1,0:T(8,128)(2,1)}, bf16[104,768]{1,0:T(8,128)(2,1)}, bf16[104,768]{1,0:T(8,128)(2,1)}, bf16[1...) custom-call(s32[5]{0:T(128)} %stack.110.me_ref, ...), custom_call_target="tpu_custom_call" | custom-call | flops 2944401408 | bytes 13291028 | tf_op jit(solution)/shard_map/pallas_call | solution.py:194
  500.7 15.2 %collective-permute-start.48 = (bf16[104,768]{1,0:T(8,128)(2,1)}, bf16[104,768]{1,0:T(8,128)(2,1)S(1)}, u32[]{:S(2)}, u32[]{:S(2)}) collective-permute-start(bf16[104,768]{1,0:T(8,128)(2,1)} %get-tuple-element.405), channel_id=1, source_target_pairs={{0,2},{2,0},{4,6},{6,4},{8,10},{10,8},{12,14},{14,12},{16,18},{18,... | collective-permute-start | bytes 479240 | tf_op jit(solution)/shard_map/ppermute | solution.py:795
  530.5 22.5 %shard_map.212 = (f32[416,768]{1,0:T(8,128)}, bf16[4,2,2,192,384]{4,3,2,1,0:T(8,128)(2,1)}, bf16[4,2,2,192,384]{4,3,2,1,0:T(8,128)(2,1)}, bf16[4,2,2,192,384]{4,...) custom-call(s32[5]{0:T(128)} %stack.110.me_ref, f32[416,768]{1,0:T(8,128)} %get-tuple-element.424.g_ref, ...), custom_call_target="tpu_custom_call" | custom-call | flops 9814671360 | bytes 41607188 | tf_op jit(solution)/shard_map/pallas_call | solution.py:194
  559.1 21.7 %shard_map.214 = (f32[416,768]{1,0:T(8,128)}, bf16[4,2,2,192,384]{4,3,2,1,0:T(8,128)(2,1)}, bf16[4,2,2,192,384]{4,3,2,1,0:T(8,128)(2,1)}, f32[2,768]{1,0:T(2,128)}) custom-call(s32[5]{0:T(128)} %stack.110.me_ref, f32[416,768]{1,0:T(8,128)} %get-tuple-element.434.g_ref, f32[416,768]{1,0:T(8,128)} %get-tuple-element.326.x1_ref, ...), custom_call_target="tpu_custom_call" | custom-call | flops 3925868544 | bytes 39464468 | tf_op jit(solution)/shard_map/pallas_call | solution.py:194
  583.1 8.0 %collective-permute-done.57.refs_17_ = bf16[2,192,384]{2,1,0:T(8,128)(2,1)S(1)} collective-permute-done((bf16[2,192,384]{2,1,0:T(8,128)(2,1)S(1)}, bf16[2,192,384]{2,1,0:T(8,128)(2,1)S(1)}, u32[]{:S(2)}, u32[]{:S(2)}) %collective-permute-start.57) | collective-permute-done | bytes 294944 | tf_op jit(solution)/shard_map/ppermute | solution.py:1036
  600.4 7.8 shard_map.216
  610.1 16.2 %collective-permute-done.63.refs_2_ = bf16[8,192,384]{2,1,0:T(8,128)(2,1)S(1)} collective-permute-done((bf16[8,192,384]{2,1,0:T(8,128)(2,1)}, bf16[8,192,384]{2,1,0:T(8,128)(2,1)S(1)}, u32[]{:S(2)}, u32[]{:S(2)}) %collective-permute-start.63) | collective-permute-done | bytes 1179680 | tf_op jit(solution)/shard_map/ppermute | solution.py:1036
  636.4 18.3 %shard_map.218 = (bf16[104,768]{1,0:T(8,128)(2,1)}, bf16[104,768]{1,0:T(8,128)(2,1)}, bf16[104,768]{1,0:T(8,128)(2,1)}, bf16[104,768]{1,0:T(8,128)(2,1)}, bf16[1...) custom-call(s32[5]{0:T(128)} %stack.110.me_ref, ...), custom_call_target="tpu_custom_call" | custom-call | flops 2944401408 | bytes 13291028 | tf_op jit(solution)/shard_map/pallas_call | solution.py:194
  686.0 12.3 %collective-permute-done.76.refs_3_.refs_8_ = bf16[6,192,384]{2,1,0:T(8,128)(2,1)S(1)} collective-permute-done((bf16[6,192,384]{2,1,0:T(8,128)(2,1)}, bf16[6,192,384]{2,1,0:T(8,128)(2,1)S(1)}, u32[]{:S(2)}, u32[]{:S(2)}) %collective-permute-start.76) | collective-permute-done | bytes 884768 | tf_op jit(solution)/shard_map/ppermute | solution.py:1036
  750.8 20.5 %reduce-scatter.12.cloned.1.call-done = bf16[8,48,384]{2,1,0:T(8,128)(2,1)} async-done(((bf16[8,192,384]{2,1,0:T(8,128)(2,1)}), bf16[8,48,384]{2,1,0:T(8,128)(2,1)}) %reduce-scatter.12.cloned.1.call-update) | async-done | bytes 294928 | tf_op jit(solution)/shard_map/reduce_scatter | solution.py:1065
  (465 shorter events, 287.6 us)
Async XLA Ops:
  7.2 197.9 %all-gather.3.cloned.1.call-start = ((), (), s32[]{:S(2)}) async-start(), calls=%async_computation.8 | async-start | bytes 6082560 | tf_op jit(solution)/shard_map/all_gather | solution.py:823
  10.7 285.7 %all-gather.5.cloned.1.call-start = ((), (), s32[]{:S(2)}) async-start(), calls=%async_computation.9 | async-start | bytes 6082560 | tf_op jit(solution)/shard_map/all_gather | solution.py:823
  19.6 690.4 %reduce-scatter.14.cloned.1.call-start = ((), (), s32[]{:S(2)}) async-start(), calls=%async_computation.14 | async-start | bytes 1474560 | tf_op jit(solution)/shard_map/reduce_scatter | solution.py:1065
  28.7 81.8 %collective-permute-start.7 = (bf16[12,48,384]{2,1,0:T(8,128)(2,1)S(1)}, bf16[12,48,384]{2,1,0:T(8,128)(2,1)S(1)}, u32[]{:S(2)}, u32[]{:S(2)}) collective-permute-start(bf16[12,48,384]{2,1,0:T(8,128)(2,1)S(1)} %pad_maximum_fusion.10), channel_id=1, source_target_pairs={{0,6},{2,0},{4,2},{6,4},{1,7},{3,1},{5,3},{7,5},{8,14},{10,8},{12,... | collective-permute-start | bytes 1327112 | tf_op jit(solution)/shard_map/ppermute | solution.py:833
  37.1 73.4 %collective-permute-start.6 = (bf16[12,48,384]{2,1,0:T(8,128)(2,1)S(1)}, bf16[12,48,384]{2,1,0:T(8,128)(2,1)S(1)}, u32[]{:S(2)}, u32[]{:S(2)}) collective-permute-start(bf16[12,48,384]{2,1,0:T(8,128)(2,1)S(1)} %pad_maximum_fusion.10), channel_id=1, source_target_pairs={{0,4},{2,6},{4,0},{6,2},{1,5},{3,7},{5,1},{7,3},{8,12},{10,14},{12... | collective-permute-start | bytes 1327112 | tf_op jit(solution)/shard_map/ppermute | solution.py:833
  45.2 65.3 %collective-permute-start.5 = (bf16[12,48,384]{2,1,0:T(8,128)(2,1)S(1)}, bf16[12,48,384]{2,1,0:T(8,128)(2,1)S(1)}, u32[]{:S(2)}, u32[]{:S(2)}) collective-permute-start(bf16[12,48,384]{2,1,0:T(8,128)(2,1)S(1)} %pad_maximum_fusion.10), channel_id=1, source_target_pairs={{0,2},{2,4},{4,6},{6,0},{1,3},{3,5},{5,7},{7,1},{8,10},{10,12},{12... | collective-permute-start | bytes 1327112 | tf_op jit(solution)/shard_map/ppermute | solution.py:833
  49.4 28.4 %collective-permute-start.2 = (bf16[104,768]{1,0:T(8,128)(2,1)}, bf16[104,768]{1,0:T(8,128)(2,1)S(1)}, u32[]{:S(2)}, u32[]{:S(2)}) collective-permute-start(bf16[104,768]{1,0:T(8,128)(2,1)} %get-tuple-element.268), channel_id=1, source_target_pairs={{0,8},{2,10},{4,12},{6,14},{8,0},{10,2},{12,4},{14,6},{16,24},{18,... | collective-permute-start | bytes 479240 | tf_op jit(solution)/shard_map/ppermute | solution.py:795
  77.7 32.8 %collective-permute-start.4 = (bf16[104,768]{1,0:T(8,128)(2,1)}, bf16[104,768]{1,0:T(8,128)(2,1)S(1)}, u32[]{:S(2)}, u32[]{:S(2)}) collective-permute-start(bf16[104,768]{1,0:T(8,128)(2,1)} %get-tuple-element.270), channel_id=1, source_target_pairs={{0,10},{2,8},{4,14},{6,12},{8,2},{10,0},{12,6},{14,4},{16,26},{18,... | collective-permute-start | bytes 479240 | tf_op jit(solution)/shard_map/ppermute | solution.py:795
  135.9 81.7 %collective-permute-start.19 = (bf16[4,12,48,384]{3,2,1,0:T(8,128)(2,1)S(1)}, bf16[4,12,48,384]{3,2,1,0:T(8,128)(2,1)}, u32[]{:S(2)}, u32[]{:S(2)}) collective-permute-start(bf16[4,12,48,384]{3,2,1,0:T(8,128)(2,1)S(1)} %pad_maximum_fusion.1.refs_4_), channel_id=1, source_target_pairs={{0,8},{8,0},{16,24},{24,16},{1,9},{9,1},{17,25},{25,17},{2,10},{10... | collective-permute-start | bytes 5308424 | tf_op jit(solution)/shard_map/ppermute | solution.py:1036
  136.0 81.8 %collective-permute-start.17 = (bf16[4,12,48,384]{3,2,1,0:T(8,128)(2,1)S(1)}, bf16[4,12,48,384]{3,2,1,0:T(8,128)(2,1)}, u32[]{:S(2)}, u32[]{:S(2)}) collective-permute-start(bf16[4,12,48,384]{3,2,1,0:T(8,128)(2,1)S(1)} %pad_maximum_fusion.1.refs_4_), channel_id=1, source_target_pairs={{0,16},{8,24},{16,0},{24,8},{1,17},{9,25},{17,1},{25,9},{2,18},{10... | collective-permute-start | bytes 5308424 | tf_op jit(solution)/shard_map/ppermute | solution.py:1036
  139.0 80.5 %collective-permute-start.18 = (bf16[4,12,48,384]{3,2,1,0:T(8,128)(2,1)S(1)}, bf16[4,12,48,384]{3,2,1,0:T(8,128)(2,1)}, u32[]{:S(2)}, u32[]{:S(2)}) collective-permute-start(bf16[4,12,48,384]{3,2,1,0:T(8,128)(2,1)S(1)} %pad_maximum_fusion.refs_0_), channel_id=1, source_target_pairs={{0,8},{8,0},{16,24},{24,16},{1,9},{9,1},{17,25},{25,17},{2,10},{10... | collective-permute-start | bytes 5308424 | tf_op jit(solution)/shard_map/ppermute | solution.py:1036
  139.2 80.3 %collective-permute-start.16 = (bf16[4,12,48,384]{3,2,1,0:T(8,128)(2,1)S(1)}, bf16[4,12,48,384]{3,2,1,0:T(8,128)(2,1)}, u32[]{:S(2)}, u32[]{:S(2)}) collective-permute-start(bf16[4,12,48,384]{3,2,1,0:T(8,128)(2,1)S(1)} %pad_maximum_fusion.refs_0_), channel_id=1, source_target_pairs={{0,1},{1,0},{2,3},{3,2},{4,5},{5,4},{6,7},{7,6},{8,9},{9,8},{10,11... | collective-permute-start | bytes 5308424 | tf_op jit(solution)/shard_map/ppermute | solution.py:1036
  156.6 31.9 %collective-permute-start.11 = (bf16[12,48,384]{2,1,0:T(8,128)(2,1)S(1)}, bf16[12,48,384]{2,1,0:T(8,128)(2,1)S(1)}, u32[]{:S(2)}, u32[]{:S(2)}) collective-permute-start(bf16[12,48,384]{2,1,0:T(8,128)(2,1)S(1)} %pad_maximum_fusion.11), channel_id=1, source_target_pairs={{0,4},{2,6},{4,0},{6,2},{1,5},{3,7},{5,1},{7,3},{8,12},{10,14},{12... | collective-permute-start | bytes 1327112 | tf_op jit(solution)/shard_map/ppermute | solution.py:833
  233.9 37.1 %collective-permute-start.23 = (bf16[2,12,48,384]{3,2,1,0:T(8,128)(2,1)S(1)}, bf16[2,12,48,384]{3,2,1,0:T(8,128)(2,1)S(1)}, u32[]{:S(2)}, u32[]{:S(2)}) collective-permute-start(bf16[2,12,48,384]{3,2,1,0:T(8,128)(2,1)S(1)} %pad_maximum_fusion.7), channel_id=1, source_target_pairs={{0,1},{1,0},{2,3},{3,2},{4,5},{5,4},{6,7},{7,6},{8,9},{9,8},{10,11... | collective-permute-start | bytes 2654216 | tf_op jit(solution)/shard_map/ppermute | solution.py:1036
  236.6 34.4 %collective-permute-start.22 = (bf16[2,12,48,384]{3,2,1,0:T(8,128)(2,1)S(1)}, bf16[2,12,48,384]{3,2,1,0:T(8,128)(2,1)S(1)}, u32[]{:S(2)}, u32[]{:S(2)}) collective-permute-start(bf16[2,12,48,384]{3,2,1,0:T(8,128)(2,1)S(1)} %pad_maximum_fusion.6), channel_id=1, source_target_pairs={{0,16},{8,24},{16,0},{24,8},{1,17},{9,25},{17,1},{25,9},{2,18},{10... | collective-permute-start | bytes 2654216 | tf_op jit(solution)/shard_map/ppermute | solution.py:1036
  271.3 57.9 %collective-permute-start.33 = (bf16[4,12,48,384]{3,2,1,0:T(8,128)(2,1)S(1)}, bf16[4,12,48,384]{3,2,1,0:T(8,128)(2,1)}, u32[]{:S(2)}, u32[]{:S(2)}) collective-permute-start(bf16[4,12,48,384]{3,2,1,0:T(8,128)(2,1)S(1)} %pad_maximum_fusion.3.refs_4_), channel_id=1, source_target_pairs={{0,8},{8,0},{16,24},{24,16},{1,9},{9,1},{17,25},{25,17},{2,10},{10... | collective-permute-start | bytes 5308424 | tf_op jit(solution)/shard_map/ppermute | solution.py:1036
  271.4 57.8 %collective-permute-start.31 = (bf16[4,12,48,384]{3,2,1,0:T(8,128)(2,1)S(1)}, bf16[4,12,48,384]{3,2,1,0:T(8,128)(2,1)}, u32[]{:S(2)}, u32[]{:S(2)}) collective-permute-start(bf16[4,12,48,384]{3,2,1,0:T(8,128)(2,1)S(1)} %pad_maximum_fusion.3.refs_4_), channel_id=1, source_target_pairs={{0,16},{8,24},{16,0},{24,8},{1,17},{9,25},{17,1},{25,9},{2,18},{10... | collective-permute-start | bytes 5308424 | tf_op jit(solution)/shard_map/ppermute | solution.py:1036
  274.2 55.1 %collective-permute-start.32 = (bf16[4,12,48,384]{3,2,1,0:T(8,128)(2,1)S(1)}, bf16[4,12,48,384]{3,2,1,0:T(8,128)(2,1)}, u32[]{:S(2)}, u32[]{:S(2)}) collective-permute-start(bf16[4,12,48,384]{3,2,1,0:T(8,128)(2,1)S(1)} %pad_maximum_fusion.2.refs_0_), channel_id=1, source_target_pairs={{0,8},{8,0},{16,24},{24,16},{1,9},{9,1},{17,25},{25,17},{2,10},{10... | collective-permute-start | bytes 5308424 | tf_op jit(solution)/shard_map/ppermute | solution.py:1036
  274.4 54.8 %collective-permute-start.30 = (bf16[4,12,48,384]{3,2,1,0:T(8,128)(2,1)S(1)}, bf16[4,12,48,384]{3,2,1,0:T(8,128)(2,1)}, u32[]{:S(2)}, u32[]{:S(2)}) collective-permute-start(bf16[4,12,48,384]{3,2,1,0:T(8,128)(2,1)S(1)} %pad_maximum_fusion.2.refs_0_), channel_id=1, source_target_pairs={{0,1},{1,0},{2,3},{3,2},{4,5},{5,4},{6,7},{7,6},{8,9},{9,8},{10,11... | collective-permute-start | bytes 5308424 | tf_op jit(solution)/shard_map/ppermute | solution.py:1036
  393.8 35.6 %collective-permute-start.37 = (bf16[4,2,2,192,384]{4,3,2,1,0:T(8,128)(2,1)}, bf16[4,2,2,192,384]{4,3,2,1,0:T(8,128)(2,1)S(1)}, u32[]{:S(2)}, u32[]{:S(2)}) collective-permute-start(bf16[4,2,2,192,384]{4,3,2,1,0:T(8,128)(2,1)} %get-tuple-element.372), channel_id=1, source_target_pairs={{0,8},{8,0},{16,24},{24,16},{1,9},{9,1},{17,25},{25,17},{2,10},{10... | collective-permute-start | bytes 7077896 | tf_op jit(solution)/shard_map/ppermute | solution.py:1036
  426.3 36.0 %collective-permute-start.44 = (bf16[4,2,2,192,384]{4,3,2,1,0:T(8,128)(2,1)}, bf16[4,2,2,192,384]{4,3,2,1,0:T(8,128)(2,1)S(1)}, u32[]{:S(2)}, u32[]{:S(2)}) collective-permute-start(bf16[4,2,2,192,384]{4,3,2,1,0:T(8,128)(2,1)} %get-tuple-element.387), channel_id=1, source_target_pairs={{0,8},{8,0},{16,24},{24,16},{1,9},{9,1},{17,25},{25,17},{2,10},{10... | collective-permute-start | bytes 7077896 | tf_op jit(solution)/shard_map/ppermute | solution.py:1036
  471.9 28.3 %collective-permute-start.46 = (bf16[8,192,384]{2,1,0:T(8,128)(2,1)}, bf16[8,192,384]{2,1,0:T(8,128)(2,1)S(1)}, u32[]{:S(2)}, u32[]{:S(2)}) collective-permute-start(bf16[8,192,384]{2,1,0:T(8,128)(2,1)} %get-tuple-element.402), channel_id=1, source_target_pairs={{0,16},{8,24},{16,0},{24,8},{1,17},{9,25},{17,1},{25,9},{2,18},{10... | collective-permute-start | bytes 3538952 | tf_op jit(solution)/shard_map/ppermute | solution.py:1036
  524.0 29.6 %collective-permute-start.54 = (bf16[6,192,384]{2,1,0:T(8,128)(2,1)}, bf16[6,192,384]{2,1,0:T(8,128)(2,1)S(1)}, u32[]{:S(2)}, u32[]{:S(2)}) collective-permute-start(bf16[6,192,384]{2,1,0:T(8,128)(2,1)} %get-tuple-element.426), channel_id=1, source_target_pairs={{0,1},{1,0},{2,3},{3,2},{4,5},{5,4},{6,7},{7,6},{8,9},{9,8},{10,11... | collective-permute-start | bytes 2654216 | tf_op jit(solution)/shard_map/ppermute | solution.py:1036
  524.9 28.7 %collective-permute-start.55 = (bf16[8,192,384]{2,1,0:T(8,128)(2,1)}, bf16[8,192,384]{2,1,0:T(8,128)(2,1)S(1)}, u32[]{:S(2)}, u32[]{:S(2)}) collective-permute-start(bf16[8,192,384]{2,1,0:T(8,128)(2,1)} %get-tuple-element.427), channel_id=1, source_target_pairs={{0,16},{8,24},{16,0},{24,8},{1,17},{9,25},{17,1},{25,9},{2,18},{10... | collective-permute-start | bytes 3538952 | tf_op jit(solution)/shard_map/ppermute | solution.py:1036
  553.0 40.6 %collective-permute-start.58 = (bf16[4,2,2,192,384]{4,3,2,1,0:T(8,128)(2,1)}, bf16[4,2,2,192,384]{4,3,2,1,0:T(8,128)(2,1)}, u32[]{:S(2)}, u32[]{:S(2)}) collective-permute-start(bf16[4,2,2,192,384]{4,3,2,1,0:T(8,128)(2,1)} %get-tuple-element.443), channel_id=1, source_target_pairs={{0,8},{8,0},{16,24},{24,16},{1,9},{9,1},{17,25},{25,17},{2,10},{10... | collective-permute-start | bytes 7077896 | tf_op jit(solution)/shard_map/ppermute | solution.py:1036
  553.1 40.6 %collective-permute-start.59 = (bf16[4,2,2,192,384]{4,3,2,1,0:T(8,128)(2,1)}, bf16[4,2,2,192,384]{4,3,2,1,0:T(8,128)(2,1)}, u32[]{:S(2)}, u32[]{:S(2)}) collective-permute-start(bf16[4,2,2,192,384]{4,3,2,1,0:T(8,128)(2,1)} %get-tuple-element.445), channel_id=1, source_target_pairs={{0,8},{8,0},{16,24},{24,16},{1,9},{9,1},{17,25},{25,17},{2,10},{10... | collective-permute-start | bytes 7077896 | tf_op jit(solution)/shard_map/ppermute | solution.py:1036
  580.8 29.0 %collective-permute-start.65 = (bf16[4,2,2,192,384]{4,3,2,1,0:T(8,128)(2,1)}, bf16[4,2,2,192,384]{4,3,2,1,0:T(8,128)(2,1)S(1)}, u32[]{:S(2)}, u32[]{:S(2)}) collective-permute-start(bf16[4,2,2,192,384]{4,3,2,1,0:T(8,128)(2,1)} %get-tuple-element.459), channel_id=1, source_target_pairs={{0,8},{8,0},{16,24},{24,16},{1,9},{9,1},{17,25},{25,17},{2,10},{10... | collective-permute-start | bytes 7077896 | tf_op jit(solution)/shard_map/ppermute | solution.py:1036
  581.0 130.4 %reduce-scatter.10.cloned.1.call-start = ((), (), s32[]{:S(2)}) async-start(), calls=%async_computation.12 | async-start | bytes 737280 | tf_op jit(solution)/shard_map/reduce_scatter | solution.py:1065
  635.3 91.6 %reduce-scatter.6.cloned.1.call-start = ((), (), s32[]{:S(2)}) async-start(), calls=%async_computation.10 | async-start | bytes 921600 | tf_op jit(solution)/shard_map/reduce_scatter | solution.py:1065
  662.2 86.1 %reduce-scatter.8.cloned.1.call-start = ((), (), s32[]{:S(2)}) async-start(), calls=%async_computation.11 | async-start | bytes 737280 | tf_op jit(solution)/shard_map/reduce_scatter | solution.py:1065
  709.8 61.6 %reduce-scatter.12.cloned.1.call-start = ((), (), s32[]{:S(2)}) async-start(), calls=%async_computation.13 | async-start | bytes 1474560 | tf_op jit(solution)/shard_map/reduce_scatter | solution.py:1065
  744.8 32.1 %all-to-all-start.1 = ((bf16[4,5,48,384]{3,2,1,0:T(8,128)(2,1)}), bf16[4,5,48,384]{3,2,1,0:T(8,128)(2,1)S(1)}, u32[]{:S(2)}, u32[]{:S(2)}) async-start(bf16[4,5,48,384]{3,2,1,0:T(8,128)(2,1)} %shard_map.222), calls=%async_computation.1 | async-start | bytes 1474560 | tf_op jit(solution)/shard_map/all_to_all | solution.py:1062
  (143 other events, 1889.4 us)
Sparse Core Ops, SparseCore 0:
  11.7 93.2 all-gather.2
  108.7 88.3 all-gather.4
  581.1 27.3 reduce-scatter.13
  635.4 20.3 reduce-scatter.9
  662.4 25.6 reduce-scatter.5
  709.9 21.4 reduce-scatter.7
  733.8 37.5 reduce-scatter.11

commit v13 on v12

--- a/solution.py
+++ b/solution.py
@@ -819,9 +819,13 @@
     )
 
 
-def gather_slabs(pack):
-    full = lax.all_gather(pack, ("head", "clip", "seq"), axis=1, tiled=True)
-    return full.reshape(pack.shape[0], lax.axis_size("head"), -1, pack.shape[2])
+def along_seq(pack):
+    return lax.all_gather(pack, "seq", axis=1, tiled=True)
+
+
+def gather_slabs(part):
+    full = lax.all_gather(part, ("head", "clip"), axis=1, tiled=True)
+    return full.reshape(part.shape[0], lax.axis_size("head"), -1, part.shape[2])
 
 
 def spread_steps(pack, me):
@@ -1161,8 +1165,6 @@
         for l in range(layers)
     ]
     packs_ff = [pack_rest(space_qkv[l], space_out[l], mlp_in[l], mlp_out[l]) for l in range(layers)]
-    weights = [gather_slabs(pack) for pack in packs]
-    mixes = [mix_whole(w[-1], shards) for w in weights]
     quick = lax.axis_size("clip") == 4 and shares == 2 and ways == 4 and time_qkv.shape[1] % 16 == 0
 
     halves = Halves(lax.axis_size("clip"), d, time_qkv.shape[3])
@@ -1175,18 +1177,27 @@
         spreads = [Spread(pack, me) for pack in packs_ff]
         weights_ff = []
     else:
-        weights_ff = [gather_slabs(pack) for pack in packs_ff]
+        weights_ff = [gather_slabs(along_seq(pack)) for pack in packs_ff]
 
     home = go_home(tokens)
     if quick:
         first = spreads[0]
-        home, gb = first.step((home, gb))
+        gb, home, packs[0] = lax.optimization_barrier((gb, home, packs[0]))
+    part = along_seq(packs[0])
+    if quick:
+        part = first.step(part)
+    weights = [gather_slabs(part)]
     x = as_rows(home)
-    send = send_first(rows, x, gb[0], me)
+    send = swap_places(send_first(rows, x, gb[0], me))
+    if quick:
+        send, packs[1:] = lax.optimization_barrier((send, packs[1:]))
+    weights += [gather_slabs(along_seq(pack)) for pack in packs[1:]]
+    mixes = [mix_whole(w[-1], shards) for w in weights]
     kept = []
     for l in range(layers):
         w = weights[l]
-        send = swap_places(send)
+        if l:
+            send = swap_places(send)
         if quick and l == 0:
             send = first.step(send)
             for spread in spreads[1:]:

time: 793 us -> 798 us (level)
  blocking collectives: 0 us -> 44.8 us
  starting transfers between devices: 145 us -> 110 us
    all_gather x0 -> x2, blocking collectives: none -> 44.8 us  [along_seq(): return lax.all_gather(pack, 'seq', axis=1, tiled=True)]
    ppermute x24, waiting for transfers between devices: 75.9 us -> 49.9 us  [swap_places(): got.append(lax.ppermute(chunks[k], ('clip', 'seq'), pairs))]
    ppermute x24, starting transfers between devices: 66.8 us -> 42 us  [swap_places(): got.append(lax.ppermute(chunks[k], ('clip', 'seq'), pairs))]
    ppermute x46, waiting for transfers between devices: 84.8 us -> 101 us  [cross(): return lax.ppermute(a, axis, [(i, i ^ 1 << bit) for i in range(size)])]
    ppermute x6, waiting for transfers between devices: 64.6 us -> 79.1 us  [spread_steps(): lax.ppermute(pack, 'seq', [(i, (i + k) % ways) for i in range(ways)])]
    ppermute x6, starting transfers between devices: 16.5 us -> 5.3 us  [spread_steps(): lax.ppermute(pack, 'seq', [(i, (i + k) % ways) for i in range(ways)])]
    unnamed x179 -> x167, local copies, waits for them, and re-layouts: 21.8 us -> 21.2 us
  transfers between devices with their start and end apart: 90 -> 90, of which waited for: 38 -> 36; matrix products, arithmetic and copies ran while one was open for 6% -> 5% of each run, Pallas kernels for 31% -> 31%
where the time goes in v13:
time: 798 us; the launch traced here: 792 us
  Pallas kernels  299 us (37%)
  waiting for transfers between devices  262 us (33%)
  starting transfers between devices  110 us (14%)
  blocking collectives  44.8 us (6%)
  local copies, waits for them, and re-layouts  36.7 us (5%)
  other arithmetic  24.4 us (3%)
  between operations  15.9 us (2%)
    pallas_call x18, Pallas kernels, call(): pl.pallas_call(body, out_shape=[shape for shape, _ in outs], grid=grid, i...  232 us
    ppermute x46, waiting for transfers between devices, cross(): return lax.ppermute(a, axis, [(i, i ^ 1 << bit) for i in range(size)])  101 us
    ppermute x6, waiting for transfers between devices, spread_steps(): lax.ppermute(pack, 'seq', [(i, (i + k) % ways) for i in range(ways)])  79.1 us
    ppermute x24, waiting for transfers between devices, swap_places(): got.append(lax.ppermute(chunks[k], ('clip', 'seq'), pairs))  49.9 us
    pallas_call x9, Pallas kernels, fold(): pl.pallas_call(body, out_shape=[jax.ShapeDtypeStruct(shape, BF16) for sha...  45.2 us
    all_gather x2, blocking collectives, along_seq(): return lax.all_gather(pack, 'seq', axis=1, tiled=True)  44.8 us
    ppermute x46, starting transfers between devices, cross(): return lax.ppermute(a, axis, [(i, i ^ 1 << bit) for i in range(size)])  42.8 us
    ppermute x24, starting transfers between devices, swap_places(): got.append(lax.ppermute(chunks[k], ('clip', 'seq'), pairs))  42 us
  transfers between devices with their start and end apart: 90, of which 36 were waited for; matrix products, arithmetic and copies ran while one was open for 5% of the time, Pallas kernels for 31%

profile of v13, /device:TPU:0, one launch (start us, length us, event | category | flops | bytes accessed | tf_op | source)
XLA Modules:
  0.0 792.0 jit_solution(1408555670894852384)
XLA Ops:
  25.0 26.4 %all_gather.12 = bf16[5,192,384]{2,1,0:T(8,128)(2,1)} all-gather(bf16[5,48,384]{2,1,0:T(8,128)(2,1)S(1)} %pad_maximum_fusion.14), channel_id=1, replica_groups=mesh['clip'=4,'seq'=4,'head'=2] {'seq'}, dimensions={1}, use_global_device_ids=true | all-gather | bytes 921600 | tf_op jit(solution)/shard_map/all_gather | solution.py:823
  66.2 18.3 %all_gather.14 = bf16[5,192,384]{2,1,0:T(8,128)(2,1)} all-gather(bf16[5,48,384]{2,1,0:T(8,128)(2,1)S(1)} %pad_maximum_fusion.15), channel_id=1, replica_groups=mesh['clip'=4,'seq'=4,'head'=2] {'seq'}, dimensions={1}, use_global_device_ids=true | all-gather | bytes 921600 | tf_op jit(solution)/shard_map/all_gather | solution.py:823
  87.5 9.7 %collective-permute-done.7 = bf16[12,48,384]{2,1,0:T(8,128)(2,1)S(1)} collective-permute-done((bf16[12,48,384]{2,1,0:T(8,128)(2,1)S(1)}, bf16[12,48,384]{2,1,0:T(8,128)(2,1)S(1)}, u32[]{:S(2)}, u32[]{:S(2)}) %collective-permute-start.7) | collective-permute-done | bytes 442400 | tf_op jit(solution)/shard_map/ppermute | solution.py:837
  97.3 25.6 %collective-permute-done.6 = bf16[12,48,384]{2,1,0:T(8,128)(2,1)S(1)} collective-permute-done((bf16[12,48,384]{2,1,0:T(8,128)(2,1)S(1)}, bf16[12,48,384]{2,1,0:T(8,128)(2,1)S(1)}, u32[]{:S(2)}, u32[]{:S(2)}) %collective-permute-start.6) | collective-permute-done | bytes 442400 | tf_op jit(solution)/shard_map/ppermute | solution.py:837
  127.2 30.7 %collective-permute-done.9 = bf16[2,12,48,384]{3,2,1,0:T(8,128)(2,1)S(1)} collective-permute-done((bf16[2,12,48,384]{3,2,1,0:T(8,128)(2,1)S(1)}, bf16[2,12,48,384]{3,2,1,0:T(8,128)(2,1)S(1)}, u32[]{:S(2)}, u32[]{:S(2)}) %collective-permute-start.9) | collective-permute-done | bytes 884768 | tf_op jit(solution)/shard_map/ppermute | solution.py:1040
  164.1 12.1 %collective-permute-done.12 = bf16[12,48,384]{2,1,0:T(8,128)(2,1)S(1)} collective-permute-done((bf16[12,48,384]{2,1,0:T(8,128)(2,1)S(1)}, bf16[12,48,384]{2,1,0:T(8,128)(2,1)S(1)}, u32[]{:S(2)}, u32[]{:S(2)}) %collective-permute-start.12) | collective-permute-done | bytes 442400 | tf_op jit(solution)/shard_map/ppermute | solution.py:837
  178.7 19.4 %collective-permute-done.11 = bf16[12,48,384]{2,1,0:T(8,128)(2,1)S(1)} collective-permute-done((bf16[12,48,384]{2,1,0:T(8,128)(2,1)S(1)}, bf16[12,48,384]{2,1,0:T(8,128)(2,1)S(1)}, u32[]{:S(2)}, u32[]{:S(2)}) %collective-permute-start.11) | collective-permute-done | bytes 442400 | tf_op jit(solution)/shard_map/ppermute | solution.py:837
  198.8 12.2 %collective-permute-done.10 = bf16[12,48,384]{2,1,0:T(8,128)(2,1)} collective-permute-done((bf16[12,48,384]{2,1,0:T(8,128)(2,1)S(1)}, bf16[12,48,384]{2,1,0:T(8,128)(2,1)}, u32[]{:S(2)}, u32[]{:S(2)}) %collective-permute-start.10) | collective-permute-done | bytes 442400 | tf_op jit(solution)/shard_map/ppermute | solution.py:837
  211.0 12.4 %shard_map.195 = (bf16[416,768]{1,0:T(8,128)(2,1)}, bf16[3,416,768]{2,1,0:T(8,128)(2,1)}, f32[2,3,2,416]{3,2,1,0:T(2,128)}, bf16[104,768]{1,0:T(8,128)(2,1)}, bf...) custom-call(bf16[104,768]{1,0:T(8,128)(2,1)} %get-tuple-element.301.refs_0_, ...), custom_call_target="tpu_custom_call" | custom-call | flops 1472200704 | bytes 9752064 | tf_op jit(solution)/shard_map/pallas_call | solution.py:194
  246.5 10.9 %shard_map.196 = bf16[12,2,16,48,384]{4,3,2,1,0:T(8,128)(2,1)} custom-call(s32[5]{0:T(128)} %stack.110.me_ref, bf16[4,12,48,384]{3,2,1,0:T(8,128)(2,1)} %copy-done.9, bf16[4,12,48,384]{3,2,1,0:T(8,128)(2,1)} %collective-permute-done.16.refs_1_, bf16[4,12,48,384]{3,2,1,0:T(8,128)(2,1)} %collective-permute-done.18.refs_2_, ...), custom_call_target="tpu_custom_call" | custom-call | bytes 28311552 | tf_op jit(solution)/shard_map/pallas_call | solution.py:875
  257.4 9.4 %shard_map.197 = (bf16[416,768]{1,0:T(8,128)(2,1)}, bf16[416,768]{1,0:T(8,128)(2,1)}, f32[416,768]{1,0:T(8,128)}, bf16[3,416,768]{2,1,0:T(8,128)(2,1)}) custom-call(s32[5]{0:T(128)} %stack.110.me_ref, bf16[104,768]{1,0:T(8,128)(2,1)} %get-tuple-element.328.refs_0_, bf16[104,768]{1,0:T(8,128)(2,1)} %copy-done.60, bf16[104,768]{1,0:T(8,128)(2,1)} %copy-done.62, ...), custom_call_target="tpu_custom_call" | custom-call | flops 2453667840 | bytes 27641876 | tf_op jit(solution)/shard_map/pallas_call | solution.py:194
  266.8 9.9 %shard_map.198 = (bf16[416,768]{1,0:T(8,128)(2,1)}, f32[416,768]{1,0:T(8,128)}, f32[2,3,2,2,208]{4,3,2,1,0:T(2,128)}) custom-call(bf16[3,416,768]{2,1,0:T(8,128)(2,1)} %get-tuple-element.338.qkv_ref, f32[416,768]{1,0:T(8,128)} %get-tuple-element.339.x1_ref, bf16[12,2,768,384]{3,2,1,0:T(8,128)(2,1)} %bitcast.197), custom_call_target="tpu_custom_call" | custom-call | flops 490733568 | bytes 19287552 | tf_op jit(solution)/shard_map/pallas_call | solution.py:194
  280.9 13.2 %shard_map.199 = (f32[416,768]{1,0:T(8,128)}, bf16[104,768]{1,0:T(8,128)(2,1)}, bf16[104,768]{1,0:T(8,128)(2,1)}, bf16[104,768]{1,0:T(8,128)(2,1)}, bf16[104,768]{1,0:T(8,128)(2,1)}) custom-call(f32[416,768]{1,0:T(8,128)} %get-tuple-element.345.x2_ref, bf16[12,2,768,384]{3,2,1,0:T(8,128)(2,1)} %bitcast.198, bf16[12,2,768,384]{3,2,1,0:T(8,128)(2,1)} %bitcast.199, ...), custom_call_target="tpu_custom_call" | custom-call | flops 3925868544 | bytes 31543316 | tf_op jit(solution)/shard_map/pallas_call | solution.py:194
  308.6 12.4 %shard_map.200 = (bf16[416,768]{1,0:T(8,128)(2,1)}, bf16[3,416,768]{2,1,0:T(8,128)(2,1)}, f32[2,3,2,416]{3,2,1,0:T(2,128)}, bf16[104,768]{1,0:T(8,128)(2,1)}, bf...) custom-call(bf16[104,768]{1,0:T(8,128)(2,1)} %get-tuple-element.347.refs_0_, ...), custom_call_target="tpu_custom_call" | custom-call | flops 1472200704 | bytes 9752064 | tf_op jit(solution)/shard_map/pallas_call | solution.py:194
  343.8 11.0 %shard_map.201 = bf16[12,2,16,48,384]{4,3,2,1,0:T(8,128)(2,1)} custom-call(s32[5]{0:T(128)} %stack.110.me_ref, bf16[4,12,48,384]{3,2,1,0:T(8,128)(2,1)} %copy-done.7, bf16[4,12,48,384]{3,2,1,0:T(8,128)(2,1)} %collective-permute-done.30.refs_1_, bf16[4,12,48,384]{3,2,1,0:T(8,128)(2,1)} %collective-permute-done.32.refs_2_, ...), custom_call_target="tpu_custom_call" | custom-call | bytes 28311552 | tf_op jit(solution)/shard_map/pallas_call | solution.py:875
  354.8 9.4 %shard_map.202 = (bf16[416,768]{1,0:T(8,128)(2,1)}, bf16[416,768]{1,0:T(8,128)(2,1)}, f32[416,768]{1,0:T(8,128)}, bf16[3,416,768]{2,1,0:T(8,128)(2,1)}) custom-call(s32[5]{0:T(128)} %stack.110.me_ref, bf16[104,768]{1,0:T(8,128)(2,1)} %get-tuple-element.366.refs_0_, bf16[104,768]{1,0:T(8,128)(2,1)} %copy-done.59, bf16[104,768]{1,0:T(8,128)(2,1)} %copy-done.61, ...), custom_call_target="tpu_custom_call" | custom-call | flops 2453667840 | bytes 27641876 | tf_op jit(solution)/shard_map/pallas_call | solution.py:194
  364.2 10.3 %shard_map.203 = (bf16[416,768]{1,0:T(8,128)(2,1)}, f32[416,768]{1,0:T(8,128)}, f32[2,3,2,2,208]{4,3,2,1,0:T(2,128)}) custom-call(bf16[3,416,768]{2,1,0:T(8,128)(2,1)} %get-tuple-element.377.qkv_ref, f32[416,768]{1,0:T(8,128)} %get-tuple-element.378.x1_ref, bf16[12,2,768,384]{3,2,1,0:T(8,128)(2,1)} %bitcast.205), custom_call_target="tpu_custom_call" | custom-call | flops 490733568 | bytes 19287552 | tf_op jit(solution)/shard_map/pallas_call | solution.py:194
  374.5 25.2 %shard_map.204 = (f32[416,768]{1,0:T(8,128)}, bf16[4,2,2,192,384]{4,3,2,1,0:T(8,128)(2,1)}, bf16[4,2,2,192,384]{4,3,2,1,0:T(8,128)(2,1)}, bf16[4,2,2,192,384]{4,...) custom-call(s32[5]{0:T(128)} %stack.110.me_ref, ...), custom_call_target="tpu_custom_call" | custom-call | flops 9814671360 | bytes 42885140 | tf_op jit(solution)/shard_map/pallas_call | solution.py:194
  399.7 10.8 %collective-permute-start.37 = (bf16[4,2,2,192,384]{4,3,2,1,0:T(8,128)(2,1)}, bf16[4,2,2,192,384]{4,3,2,1,0:T(8,128)(2,1)S(1)}, u32[]{:S(2)}, u32[]{:S(2)}) collective-permute-start(bf16[4,2,2,192,384]{4,3,2,1,0:T(8,128)(2,1)} %get-tuple-element.386), channel_id=1, source_target_pairs={{0,8},{8,0},{16,24},{24,16},{1,9},{9,1},{17,25},{25,17},{2,10},{10... | collective-permute-start | bytes 7077896 | tf_op jit(solution)/shard_map/ppermute | solution.py:1040
  410.6 21.6 %shard_map.205 = (f32[416,768]{1,0:T(8,128)}, bf16[4,2,2,192,384]{4,3,2,1,0:T(8,128)(2,1)}, bf16[4,2,2,192,384]{4,3,2,1,0:T(8,128)(2,1)}, f32[2,768]{1,0:T(2,128)}) custom-call(s32[5]{0:T(128)} %stack.110.me_ref, f32[416,768]{1,0:T(8,128)} %get-tuple-element.380.g_ref, f32[416,768]{1,0:T(8,128)} %get-tuple-element.378.x1_ref, ...), custom_call_target="tpu_custom_call" | custom-call | flops 3925868544 | bytes 39464468 | tf_op jit(solution)/shard_map/pallas_call | solution.py:194
  444.0 7.8 shard_map.207
  451.8 13.0 %collective-permute-start.39 = (bf16[104,768]{1,0:T(8,128)(2,1)}, bf16[104,768]{1,0:T(8,128)(2,1)S(1)}, u32[]{:S(2)}, u32[]{:S(2)}) collective-permute-start(bf16[104,768]{1,0:T(8,128)(2,1)} %get-tuple-element.395), channel_id=1, source_target_pairs={{0,8},{2,10},{4,12},{6,14},{8,0},{10,2},{12,4},{14,6},{16,24},{18,... | collective-permute-start | bytes 479240 | tf_op jit(solution)/shard_map/ppermute | solution.py:795
  480.2 18.3 %shard_map.209 = (bf16[104,768]{1,0:T(8,128)(2,1)}, bf16[104,768]{1,0:T(8,128)(2,1)}, bf16[104,768]{1,0:T(8,128)(2,1)}, bf16[104,768]{1,0:T(8,128)(2,1)}, bf16[1...) custom-call(s32[5]{0:T(128)} %stack.110.me_ref, ...), custom_call_target="tpu_custom_call" | custom-call | flops 2944401408 | bytes 13291028 | tf_op jit(solution)/shard_map/pallas_call | solution.py:194
  505.8 15.4 %collective-permute-start.48 = (bf16[104,768]{1,0:T(8,128)(2,1)}, bf16[104,768]{1,0:T(8,128)(2,1)S(1)}, u32[]{:S(2)}, u32[]{:S(2)}) collective-permute-start(bf16[104,768]{1,0:T(8,128)(2,1)} %get-tuple-element.419), channel_id=1, source_target_pairs={{0,2},{2,0},{4,6},{6,4},{8,10},{10,8},{12,14},{14,12},{16,18},{18,... | collective-permute-start | bytes 479240 | tf_op jit(solution)/shard_map/ppermute | solution.py:795
  535.8 22.5 %shard_map.212 = (f32[416,768]{1,0:T(8,128)}, bf16[4,2,2,192,384]{4,3,2,1,0:T(8,128)(2,1)}, bf16[4,2,2,192,384]{4,3,2,1,0:T(8,128)(2,1)}, bf16[4,2,2,192,384]{4,...) custom-call(s32[5]{0:T(128)} %stack.110.me_ref, f32[416,768]{1,0:T(8,128)} %get-tuple-element.438.g_ref, ...), custom_call_target="tpu_custom_call" | custom-call | flops 9814671360 | bytes 41607188 | tf_op jit(solution)/shard_map/pallas_call | solution.py:194
  564.4 21.7 %shard_map.214 = (f32[416,768]{1,0:T(8,128)}, bf16[4,2,2,192,384]{4,3,2,1,0:T(8,128)(2,1)}, bf16[4,2,2,192,384]{4,3,2,1,0:T(8,128)(2,1)}, f32[2,768]{1,0:T(2,128)}) custom-call(s32[5]{0:T(128)} %stack.110.me_ref, f32[416,768]{1,0:T(8,128)} %get-tuple-element.448.g_ref, f32[416,768]{1,0:T(8,128)} %get-tuple-element.339.x1_ref, ...), custom_call_target="tpu_custom_call" | custom-call | flops 3925868544 | bytes 39464468 | tf_op jit(solution)/shard_map/pallas_call | solution.py:194
  588.3 8.1 %collective-permute-done.57.refs_17_ = bf16[2,192,384]{2,1,0:T(8,128)(2,1)S(1)} collective-permute-done((bf16[2,192,384]{2,1,0:T(8,128)(2,1)S(1)}, bf16[2,192,384]{2,1,0:T(8,128)(2,1)S(1)}, u32[]{:S(2)}, u32[]{:S(2)}) %collective-permute-start.57) | collective-permute-done | bytes 294944 | tf_op jit(solution)/shard_map/ppermute | solution.py:1040
  605.7 7.8 shard_map.216
  615.4 16.2 %collective-permute-done.63.refs_2_ = bf16[8,192,384]{2,1,0:T(8,128)(2,1)S(1)} collective-permute-done((bf16[8,192,384]{2,1,0:T(8,128)(2,1)}, bf16[8,192,384]{2,1,0:T(8,128)(2,1)S(1)}, u32[]{:S(2)}, u32[]{:S(2)}) %collective-permute-start.63) | collective-permute-done | bytes 1179680 | tf_op jit(solution)/shard_map/ppermute | solution.py:1040
  641.7 18.3 %shard_map.218 = (bf16[104,768]{1,0:T(8,128)(2,1)}, bf16[104,768]{1,0:T(8,128)(2,1)}, bf16[104,768]{1,0:T(8,128)(2,1)}, bf16[104,768]{1,0:T(8,128)(2,1)}, bf16[1...) custom-call(s32[5]{0:T(128)} %stack.110.me_ref, ...), custom_call_target="tpu_custom_call" | custom-call | flops 2944401408 | bytes 13291028 | tf_op jit(solution)/shard_map/pallas_call | solution.py:194
  690.8 12.4 %collective-permute-done.76.refs_3_.refs_8_ = bf16[6,192,384]{2,1,0:T(8,128)(2,1)S(1)} collective-permute-done((bf16[6,192,384]{2,1,0:T(8,128)(2,1)}, bf16[6,192,384]{2,1,0:T(8,128)(2,1)S(1)}, u32[]{:S(2)}, u32[]{:S(2)}) %collective-permute-start.76) | collective-permute-done | bytes 884768 | tf_op jit(solution)/shard_map/ppermute | solution.py:1040
  755.7 20.5 %reduce-scatter.12.cloned.1.call-done = bf16[8,48,384]{2,1,0:T(8,128)(2,1)} async-done(((bf16[8,192,384]{2,1,0:T(8,128)(2,1)}), bf16[8,48,384]{2,1,0:T(8,128)(2,1)}) %reduce-scatter.12.cloned.1.call-update) | async-done | bytes 294928 | tf_op jit(solution)/shard_map/reduce_scatter | solution.py:1069
  (455 shorter events, 283.1 us)
Async XLA Ops:
  16.0 195.0 %all-gather.3.cloned.1.call-start = ((), (), s32[]{:S(2)}) async-start(), calls=%async_computation.8 | async-start | bytes 6635520 | tf_op jit(solution)/shard_map/all_gather | solution.py:827
  51.5 250.9 %all-gather.5.cloned.1.call-start = ((), (), s32[]{:S(2)}) async-start(), calls=%async_computation.9 | async-start | bytes 6635520 | tf_op jit(solution)/shard_map/all_gather | solution.py:827
  84.6 630.1 %reduce-scatter.14.cloned.1.call-start = ((), (), s32[]{:S(2)}) async-start(), calls=%async_computation.14 | async-start | bytes 1474560 | tf_op jit(solution)/shard_map/reduce_scatter | solution.py:1069
  86.6 36.3 %collective-permute-start.6 = (bf16[12,48,384]{2,1,0:T(8,128)(2,1)S(1)}, bf16[12,48,384]{2,1,0:T(8,128)(2,1)S(1)}, u32[]{:S(2)}, u32[]{:S(2)}) collective-permute-start(bf16[12,48,384]{2,1,0:T(8,128)(2,1)S(1)} %pad_maximum_fusion.10), channel_id=1, source_target_pairs={{0,4},{2,6},{4,0},{6,2},{1,5},{3,7},{5,1},{7,3},{8,12},{10,14},{12... | collective-permute-start | bytes 1327112 | tf_op jit(solution)/shard_map/ppermute | solution.py:837
  86.6 36.3 %collective-permute-start.5 = (bf16[12,48,384]{2,1,0:T(8,128)(2,1)S(1)}, bf16[12,48,384]{2,1,0:T(8,128)(2,1)S(1)}, u32[]{:S(2)}, u32[]{:S(2)}) collective-permute-start(bf16[12,48,384]{2,1,0:T(8,128)(2,1)S(1)} %pad_maximum_fusion.10), channel_id=1, source_target_pairs={{0,2},{2,4},{4,6},{6,0},{1,3},{3,5},{5,7},{7,1},{8,10},{10,12},{12... | collective-permute-start | bytes 1327112 | tf_op jit(solution)/shard_map/ppermute | solution.py:837
  123.0 34.9 %collective-permute-start.9 = (bf16[2,12,48,384]{3,2,1,0:T(8,128)(2,1)S(1)}, bf16[2,12,48,384]{3,2,1,0:T(8,128)(2,1)S(1)}, u32[]{:S(2)}, u32[]{:S(2)}) collective-permute-start(bf16[2,12,48,384]{3,2,1,0:T(8,128)(2,1)S(1)} %pad_maximum_fusion.5), channel_id=1, source_target_pairs={{0,1},{1,0},{2,3},{3,2},{4,5},{5,4},{6,7},{7,6},{8,9},{9,8},{10,11... | collective-permute-start | bytes 2654216 | tf_op jit(solution)/shard_map/ppermute | solution.py:1040
  125.5 33.3 %collective-permute-start.8 = (bf16[2,12,48,384]{3,2,1,0:T(8,128)(2,1)}, bf16[2,12,48,384]{3,2,1,0:T(8,128)(2,1)}, u32[]{:S(2)}, u32[]{:S(2)}) collective-permute-start(bf16[2,12,48,384]{3,2,1,0:T(8,128)(2,1)} %pad_maximum_fusion.4), channel_id=1, source_target_pairs={{0,16},{8,24},{16,0},{24,8},{1,17},{9,25},{17,1},{25,9},{2,18},{10... | collective-permute-start | bytes 2654216 | tf_op jit(solution)/shard_map/ppermute | solution.py:1040
  160.2 63.4 %collective-permute-start.19 = (bf16[4,12,48,384]{3,2,1,0:T(8,128)(2,1)S(1)}, bf16[4,12,48,384]{3,2,1,0:T(8,128)(2,1)}, u32[]{:S(2)}, u32[]{:S(2)}) collective-permute-start(bf16[4,12,48,384]{3,2,1,0:T(8,128)(2,1)S(1)} %pad_maximum_fusion.1.refs_4_), channel_id=1, source_target_pairs={{0,8},{8,0},{16,24},{24,16},{1,9},{9,1},{17,25},{25,17},{2,10},{10... | collective-permute-start | bytes 5308424 | tf_op jit(solution)/shard_map/ppermute | solution.py:1040
  160.2 63.4 %collective-permute-start.17 = (bf16[4,12,48,384]{3,2,1,0:T(8,128)(2,1)S(1)}, bf16[4,12,48,384]{3,2,1,0:T(8,128)(2,1)}, u32[]{:S(2)}, u32[]{:S(2)}) collective-permute-start(bf16[4,12,48,384]{3,2,1,0:T(8,128)(2,1)S(1)} %pad_maximum_fusion.1.refs_4_), channel_id=1, source_target_pairs={{0,16},{8,24},{16,0},{24,8},{1,17},{9,25},{17,1},{25,9},{2,18},{10... | collective-permute-start | bytes 5308424 | tf_op jit(solution)/shard_map/ppermute | solution.py:1040
  163.1 62.3 %collective-permute-start.18 = (bf16[4,12,48,384]{3,2,1,0:T(8,128)(2,1)S(1)}, bf16[4,12,48,384]{3,2,1,0:T(8,128)(2,1)}, u32[]{:S(2)}, u32[]{:S(2)}) collective-permute-start(bf16[4,12,48,384]{3,2,1,0:T(8,128)(2,1)S(1)} %pad_maximum_fusion.refs_0_), channel_id=1, source_target_pairs={{0,8},{8,0},{16,24},{24,16},{1,9},{9,1},{17,25},{25,17},{2,10},{10... | collective-permute-start | bytes 5308424 | tf_op jit(solution)/shard_map/ppermute | solution.py:1040
  163.3 62.1 %collective-permute-start.16 = (bf16[4,12,48,384]{3,2,1,0:T(8,128)(2,1)S(1)}, bf16[4,12,48,384]{3,2,1,0:T(8,128)(2,1)}, u32[]{:S(2)}, u32[]{:S(2)}) collective-permute-start(bf16[4,12,48,384]{3,2,1,0:T(8,128)(2,1)S(1)} %pad_maximum_fusion.refs_0_), channel_id=1, source_target_pairs={{0,1},{1,0},{2,3},{3,2},{4,5},{5,4},{6,7},{7,6},{8,9},{9,8},{10,11... | collective-permute-start | bytes 5308424 | tf_op jit(solution)/shard_map/ppermute | solution.py:1040
  239.9 36.8 %collective-permute-start.23 = (bf16[2,12,48,384]{3,2,1,0:T(8,128)(2,1)S(1)}, bf16[2,12,48,384]{3,2,1,0:T(8,128)(2,1)S(1)}, u32[]{:S(2)}, u32[]{:S(2)}) collective-permute-start(bf16[2,12,48,384]{3,2,1,0:T(8,128)(2,1)S(1)} %pad_maximum_fusion.7), channel_id=1, source_target_pairs={{0,1},{1,0},{2,3},{3,2},{4,5},{5,4},{6,7},{7,6},{8,9},{9,8},{10,11... | collective-permute-start | bytes 2654216 | tf_op jit(solution)/shard_map/ppermute | solution.py:1040
  242.1 34.6 %collective-permute-start.22 = (bf16[2,12,48,384]{3,2,1,0:T(8,128)(2,1)S(1)}, bf16[2,12,48,384]{3,2,1,0:T(8,128)(2,1)S(1)}, u32[]{:S(2)}, u32[]{:S(2)}) collective-permute-start(bf16[2,12,48,384]{3,2,1,0:T(8,128)(2,1)S(1)} %pad_maximum_fusion.6), channel_id=1, source_target_pairs={{0,16},{8,24},{16,0},{24,8},{1,17},{9,25},{17,1},{25,9},{2,18},{10... | collective-permute-start | bytes 2654216 | tf_op jit(solution)/shard_map/ppermute | solution.py:1040
  276.9 58.2 %collective-permute-start.33 = (bf16[4,12,48,384]{3,2,1,0:T(8,128)(2,1)S(1)}, bf16[4,12,48,384]{3,2,1,0:T(8,128)(2,1)}, u32[]{:S(2)}, u32[]{:S(2)}) collective-permute-start(bf16[4,12,48,384]{3,2,1,0:T(8,128)(2,1)S(1)} %pad_maximum_fusion.3.refs_4_), channel_id=1, source_target_pairs={{0,8},{8,0},{16,24},{24,16},{1,9},{9,1},{17,25},{25,17},{2,10},{10... | collective-permute-start | bytes 5308424 | tf_op jit(solution)/shard_map/ppermute | solution.py:1040
  277.0 58.1 %collective-permute-start.31 = (bf16[4,12,48,384]{3,2,1,0:T(8,128)(2,1)S(1)}, bf16[4,12,48,384]{3,2,1,0:T(8,128)(2,1)}, u32[]{:S(2)}, u32[]{:S(2)}) collective-permute-start(bf16[4,12,48,384]{3,2,1,0:T(8,128)(2,1)S(1)} %pad_maximum_fusion.3.refs_4_), channel_id=1, source_target_pairs={{0,16},{8,24},{16,0},{24,8},{1,17},{9,25},{17,1},{25,9},{2,18},{10... | collective-permute-start | bytes 5308424 | tf_op jit(solution)/shard_map/ppermute | solution.py:1040
  279.6 55.5 %collective-permute-start.32 = (bf16[4,12,48,384]{3,2,1,0:T(8,128)(2,1)S(1)}, bf16[4,12,48,384]{3,2,1,0:T(8,128)(2,1)}, u32[]{:S(2)}, u32[]{:S(2)}) collective-permute-start(bf16[4,12,48,384]{3,2,1,0:T(8,128)(2,1)S(1)} %pad_maximum_fusion.2.refs_0_), channel_id=1, source_target_pairs={{0,8},{8,0},{16,24},{24,16},{1,9},{9,1},{17,25},{25,17},{2,10},{10... | collective-permute-start | bytes 5308424 | tf_op jit(solution)/shard_map/ppermute | solution.py:1040
  279.9 55.3 %collective-permute-start.30 = (bf16[4,12,48,384]{3,2,1,0:T(8,128)(2,1)S(1)}, bf16[4,12,48,384]{3,2,1,0:T(8,128)(2,1)}, u32[]{:S(2)}, u32[]{:S(2)}) collective-permute-start(bf16[4,12,48,384]{3,2,1,0:T(8,128)(2,1)S(1)} %pad_maximum_fusion.2.refs_0_), channel_id=1, source_target_pairs={{0,1},{1,0},{2,3},{3,2},{4,5},{5,4},{6,7},{7,6},{8,9},{9,8},{10,11... | collective-permute-start | bytes 5308424 | tf_op jit(solution)/shard_map/ppermute | solution.py:1040
  399.7 35.5 %collective-permute-start.37 = (bf16[4,2,2,192,384]{4,3,2,1,0:T(8,128)(2,1)}, bf16[4,2,2,192,384]{4,3,2,1,0:T(8,128)(2,1)S(1)}, u32[]{:S(2)}, u32[]{:S(2)}) collective-permute-start(bf16[4,2,2,192,384]{4,3,2,1,0:T(8,128)(2,1)} %get-tuple-element.386), channel_id=1, source_target_pairs={{0,8},{8,0},{16,24},{24,16},{1,9},{9,1},{17,25},{25,17},{2,10},{10... | collective-permute-start | bytes 7077896 | tf_op jit(solution)/shard_map/ppermute | solution.py:1040
  432.2 35.7 %collective-permute-start.44 = (bf16[4,2,2,192,384]{4,3,2,1,0:T(8,128)(2,1)}, bf16[4,2,2,192,384]{4,3,2,1,0:T(8,128)(2,1)S(1)}, u32[]{:S(2)}, u32[]{:S(2)}) collective-permute-start(bf16[4,2,2,192,384]{4,3,2,1,0:T(8,128)(2,1)} %get-tuple-element.401), channel_id=1, source_target_pairs={{0,8},{8,0},{16,24},{24,16},{1,9},{9,1},{17,25},{25,17},{2,10},{10... | collective-permute-start | bytes 7077896 | tf_op jit(solution)/shard_map/ppermute | solution.py:1040
  476.0 27.6 %collective-permute-start.45 = (bf16[8,192,384]{2,1,0:T(8,128)(2,1)}, bf16[8,192,384]{2,1,0:T(8,128)(2,1)S(1)}, u32[]{:S(2)}, u32[]{:S(2)}) collective-permute-start(bf16[8,192,384]{2,1,0:T(8,128)(2,1)} %get-tuple-element.415), channel_id=1, source_target_pairs={{0,1},{1,0},{2,3},{3,2},{4,5},{5,4},{6,7},{7,6},{8,9},{9,8},{10,11... | collective-permute-start | bytes 3538952 | tf_op jit(solution)/shard_map/ppermute | solution.py:1040
  476.9 27.9 %collective-permute-start.46 = (bf16[8,192,384]{2,1,0:T(8,128)(2,1)}, bf16[8,192,384]{2,1,0:T(8,128)(2,1)S(1)}, u32[]{:S(2)}, u32[]{:S(2)}) collective-permute-start(bf16[8,192,384]{2,1,0:T(8,128)(2,1)} %get-tuple-element.416), channel_id=1, source_target_pairs={{0,16},{8,24},{16,0},{24,8},{1,17},{9,25},{17,1},{25,9},{2,18},{10... | collective-permute-start | bytes 3538952 | tf_op jit(solution)/shard_map/ppermute | solution.py:1040
  529.3 29.5 %collective-permute-start.54 = (bf16[6,192,384]{2,1,0:T(8,128)(2,1)}, bf16[6,192,384]{2,1,0:T(8,128)(2,1)S(1)}, u32[]{:S(2)}, u32[]{:S(2)}) collective-permute-start(bf16[6,192,384]{2,1,0:T(8,128)(2,1)} %get-tuple-element.440), channel_id=1, source_target_pairs={{0,1},{1,0},{2,3},{3,2},{4,5},{5,4},{6,7},{7,6},{8,9},{9,8},{10,11... | collective-permute-start | bytes 2654216 | tf_op jit(solution)/shard_map/ppermute | solution.py:1040
  530.3 28.5 %collective-permute-start.55 = (bf16[8,192,384]{2,1,0:T(8,128)(2,1)}, bf16[8,192,384]{2,1,0:T(8,128)(2,1)S(1)}, u32[]{:S(2)}, u32[]{:S(2)}) collective-permute-start(bf16[8,192,384]{2,1,0:T(8,128)(2,1)} %get-tuple-element.441), channel_id=1, source_target_pairs={{0,16},{8,24},{16,0},{24,8},{1,17},{9,25},{17,1},{25,9},{2,18},{10... | collective-permute-start | bytes 3538952 | tf_op jit(solution)/shard_map/ppermute | solution.py:1040
  558.3 40.5 %collective-permute-start.58 = (bf16[4,2,2,192,384]{4,3,2,1,0:T(8,128)(2,1)}, bf16[4,2,2,192,384]{4,3,2,1,0:T(8,128)(2,1)}, u32[]{:S(2)}, u32[]{:S(2)}) collective-permute-start(bf16[4,2,2,192,384]{4,3,2,1,0:T(8,128)(2,1)} %get-tuple-element.457), channel_id=1, source_target_pairs={{0,8},{8,0},{16,24},{24,16},{1,9},{9,1},{17,25},{25,17},{2,10},{10... | collective-permute-start | bytes 7077896 | tf_op jit(solution)/shard_map/ppermute | solution.py:1040
  558.4 40.5 %collective-permute-start.59 = (bf16[4,2,2,192,384]{4,3,2,1,0:T(8,128)(2,1)}, bf16[4,2,2,192,384]{4,3,2,1,0:T(8,128)(2,1)}, u32[]{:S(2)}, u32[]{:S(2)}) collective-permute-start(bf16[4,2,2,192,384]{4,3,2,1,0:T(8,128)(2,1)} %get-tuple-element.459), channel_id=1, source_target_pairs={{0,8},{8,0},{16,24},{24,16},{1,9},{9,1},{17,25},{25,17},{2,10},{10... | collective-permute-start | bytes 7077896 | tf_op jit(solution)/shard_map/ppermute | solution.py:1040
  586.1 29.1 %collective-permute-start.65 = (bf16[4,2,2,192,384]{4,3,2,1,0:T(8,128)(2,1)}, bf16[4,2,2,192,384]{4,3,2,1,0:T(8,128)(2,1)S(1)}, u32[]{:S(2)}, u32[]{:S(2)}) collective-permute-start(bf16[4,2,2,192,384]{4,3,2,1,0:T(8,128)(2,1)} %get-tuple-element.473), channel_id=1, source_target_pairs={{0,8},{8,0},{16,24},{24,16},{1,9},{9,1},{17,25},{25,17},{2,10},{10... | collective-permute-start | bytes 7077896 | tf_op jit(solution)/shard_map/ppermute | solution.py:1040
  586.2 129.9 %reduce-scatter.10.cloned.1.call-start = ((), (), s32[]{:S(2)}) async-start(), calls=%async_computation.12 | async-start | bytes 737280 | tf_op jit(solution)/shard_map/reduce_scatter | solution.py:1069
  603.7 27.9 %collective-permute-start.63 = (bf16[8,192,384]{2,1,0:T(8,128)(2,1)}, bf16[8,192,384]{2,1,0:T(8,128)(2,1)S(1)}, u32[]{:S(2)}, u32[]{:S(2)}) collective-permute-start(bf16[8,192,384]{2,1,0:T(8,128)(2,1)} %get-tuple-element.470), channel_id=1, source_target_pairs={{0,16},{8,24},{16,0},{24,8},{1,17},{9,25},{17,1},{25,9},{2,18},{10... | collective-permute-start | bytes 3538952 | tf_op jit(solution)/shard_map/ppermute | solution.py:1040
  640.5 91.2 %reduce-scatter.6.cloned.1.call-start = ((), (), s32[]{:S(2)}) async-start(), calls=%async_computation.10 | async-start | bytes 921600 | tf_op jit(solution)/shard_map/reduce_scatter | solution.py:1069
  667.2 86.0 %reduce-scatter.8.cloned.1.call-start = ((), (), s32[]{:S(2)}) async-start(), calls=%async_computation.11 | async-start | bytes 737280 | tf_op jit(solution)/shard_map/reduce_scatter | solution.py:1069
  714.5 61.7 %reduce-scatter.12.cloned.1.call-start = ((), (), s32[]{:S(2)}) async-start(), calls=%async_computation.13 | async-start | bytes 1474560 | tf_op jit(solution)/shard_map/reduce_scatter | solution.py:1069
  749.7 32.1 %all-to-all-start.1 = ((bf16[4,5,48,384]{3,2,1,0:T(8,128)(2,1)}), bf16[4,5,48,384]{3,2,1,0:T(8,128)(2,1)S(1)}, u32[]{:S(2)}, u32[]{:S(2)}) async-start(bf16[4,5,48,384]{3,2,1,0:T(8,128)(2,1)} %shard_map.222), calls=%async_computation.1 | async-start | bytes 1474560 | tf_op jit(solution)/shard_map/all_to_all | solution.py:1066
  (137 other events, 1784.3 us)
Sparse Core Ops, SparseCore 0:
  51.6 43.4 all-gather.2
  97.0 58.5 all-gather.4
  586.3 27.4 reduce-scatter.13
  640.6 20.2 reduce-scatter.9
  667.3 25.8 reduce-scatter.5
  714.6 21.6 reduce-scatter.7
  738.6 37.5 reduce-scatter.11

commit v14 on v13

--- a/solution.py
+++ b/solution.py
@@ -1182,16 +1182,13 @@
     home = go_home(tokens)
     if quick:
         first = spreads[0]
-        gb, home, packs[0] = lax.optimization_barrier((gb, home, packs[0]))
-    part = along_seq(packs[0])
+        gb, home, packs = lax.optimization_barrier((gb, home, packs))
+    part = along_seq(jnp.concatenate(packs, axis=0))
     if quick:
         part = first.step(part)
-    weights = [gather_slabs(part)]
+    weights = [gather_slabs(a) for a in jnp.split(part, layers, axis=0)]
     x = as_rows(home)
     send = swap_places(send_first(rows, x, gb[0], me))
-    if quick:
-        send, packs[1:] = lax.optimization_barrier((send, packs[1:]))
-    weights += [gather_slabs(along_seq(pack)) for pack in packs[1:]]
     mixes = [mix_whole(w[-1], shards) for w in weights]
     kept = []
     for l in range(layers):
@@ -1199,7 +1196,8 @@
         if l:
             send = swap_places(send)
         if quick and l == 0:
-            send = first.step(send)
+            for _ in range(2):
+                send = first.step(send)
             for spread in spreads[1:]:
                 send = spread.step(send)
             send = first.step(send)
@@ -1208,7 +1206,7 @@
         a1, qkv1, log1, o1_time = time_forward(rows, send, w)
         back = swap_places(o1_time)
         if quick:
-            for _ in range(2):
+            for _ in range(2 if l else 1):
                 back = spreads[l].step(back)
             if l == 0:
                 for spread in spreads[1:]:

time: 798 us -> 825 us (1.034)
  waiting for transfers between devices: 262 us -> 328 us
  blocking collectives: 44.8 us -> 0 us
    all_gather x2 -> x0, blocking collectives: 44.8 us -> none  [along_seq(): return lax.all_gather(pack, 'seq', axis=1, tiled=True)]
    ppermute x46, waiting for transfers between devices: 101 us -> 144 us  [cross(): return lax.ppermute(a, axis, [(i, i ^ 1 << bit) for i in range(size)])]
    all_gather x0 -> x1, waiting for transfers between devices: none -> 41.7 us  [along_seq(): return lax.all_gather(pack, 'seq', axis=1, tiled=True)]
    ppermute x6, waiting for transfers between devices: 79.1 us -> 40.1 us  [spread_steps(): lax.ppermute(pack, 'seq', [(i, (i + k) % ways) for i in range(ways)])]
    ppermute x24, waiting for transfers between devices: 49.9 us -> 68.7 us  [swap_places(): got.append(lax.ppermute(chunks[k], ('clip', 'seq'), pairs))]
    unnamed x167 -> x157, local copies, waits for them, and re-layouts: 21.2 us -> 19.9 us
  transfers between devices with their start and end apart: 90 -> 91, of which waited for: 36 -> 39; matrix products, arithmetic and copies ran while one was open for 5% -> 5% of each run, Pallas kernels for 31% -> 30%
where the time goes in v14:
time: 825 us; the launch traced here: 820 us
  waiting for transfers between devices  328 us (40%)
  Pallas kernels  299 us (36%)
  starting transfers between devices  113 us (14%)
  local copies, waits for them, and re-layouts  42.2 us (5%)
  other arithmetic  20.7 us (3%)
  between operations  15.8 us (2%)
    pallas_call x18, Pallas kernels, call(): pl.pallas_call(body, out_shape=[shape for shape, _ in outs], grid=grid, i...  232 us
    ppermute x46, waiting for transfers between devices, cross(): return lax.ppermute(a, axis, [(i, i ^ 1 << bit) for i in range(size)])  144 us
    ppermute x24, waiting for transfers between devices, swap_places(): got.append(lax.ppermute(chunks[k], ('clip', 'seq'), pairs))  68.7 us
    pallas_call x9, Pallas kernels, fold(): pl.pallas_call(body, out_shape=[jax.ShapeDtypeStruct(shape, BF16) for sha...  45.4 us
    ppermute x24, starting transfers between devices, swap_places(): got.append(lax.ppermute(chunks[k], ('clip', 'seq'), pairs))  42.1 us
    ppermute x46, starting transfers between devices, cross(): return lax.ppermute(a, axis, [(i, i ^ 1 << bit) for i in range(size)])  42.1 us
    all_gather x1, waiting for transfers between devices, along_seq(): return lax.all_gather(pack, 'seq', axis=1, tiled=True)  41.7 us
    ppermute x6, waiting for transfers between devices, spread_steps(): lax.ppermute(pack, 'seq', [(i, (i + k) % ways) for i in range(ways)])  40.1 us
  transfers between devices with their start and end apart: 91, of which 39 were waited for; matrix products, arithmetic and copies ran while one was open for 5% of the time, Pallas kernels for 30%

profile of v14, /device:TPU:0, one launch (start us, length us, event | category | flops | bytes accessed | tf_op | source)
XLA Modules:
  0.0 819.6 jit_solution(9098486385009551661)
XLA Ops:
  8.7 7.3 all-to-all-start
  28.7 41.7 %all-gather.4.cloned.1.call-done = bf16[10,192,384]{2,1,0:T(8,128)(2,1)} async-done(((bf16[10,48,384]{2,1,0:T(8,128)(2,1)}), bf16[10,192,384]{2,1,0:T(8,128)(2,1)}) %all-gather.4.cloned.1.call-update) | async-done | bytes 1474576 | tf_op jit(solution)/shard_map/all_gather | solution.py:823
  84.9 24.2 %collective-permute-done.3.refs_2_ = bf16[104,768]{1,0:T(8,128)(2,1)S(1)} collective-permute-done((bf16[104,768]{1,0:T(8,128)(2,1)}, bf16[104,768]{1,0:T(8,128)(2,1)S(1)}, u32[]{:S(2)}, u32[]{:S(2)}) %collective-permute-start.3) | collective-permute-done | bytes 159776 | tf_op jit(solution)/shard_map/ppermute | solution.py:795
  118.0 25.0 %collective-permute-done.9 = bf16[2,12,48,384]{3,2,1,0:T(8,128)(2,1)S(1)} collective-permute-done((bf16[2,12,48,384]{3,2,1,0:T(8,128)(2,1)S(1)}, bf16[2,12,48,384]{3,2,1,0:T(8,128)(2,1)S(1)}, u32[]{:S(2)}, u32[]{:S(2)}) %collective-permute-start.9) | collective-permute-done | bytes 884768 | tf_op jit(solution)/shard_map/ppermute | solution.py:1040
  151.9 49.8 %collective-permute-done.11.refs_5_ = bf16[4,12,48,384]{3,2,1,0:T(8,128)(2,1)} collective-permute-done((bf16[4,12,48,384]{3,2,1,0:T(8,128)(2,1)S(1)}, bf16[4,12,48,384]{3,2,1,0:T(8,128)(2,1)}, u32[]{:S(2)}, u32[]{:S(2)}) %collective-permute-start.11) | collective-permute-done | bytes 1769504 | tf_op jit(solution)/shard_map/ppermute | solution.py:1040
  210.1 7.0 collective-permute-done.16
  217.1 29.7 %collective-permute-done.15 = bf16[12,48,384]{2,1,0:T(8,128)(2,1)S(1)} collective-permute-done((bf16[12,48,384]{2,1,0:T(8,128)(2,1)S(1)}, bf16[12,48,384]{2,1,0:T(8,128)(2,1)S(1)}, u32[]{:S(2)}, u32[]{:S(2)}) %collective-permute-start.15) | collective-permute-done | bytes 442400 | tf_op jit(solution)/shard_map/ppermute | solution.py:837
  246.7 12.4 %shard_map.195 = (bf16[416,768]{1,0:T(8,128)(2,1)}, bf16[3,416,768]{2,1,0:T(8,128)(2,1)}, f32[2,3,2,416]{3,2,1,0:T(2,128)}, bf16[104,768]{1,0:T(8,128)(2,1)}, bf...) custom-call(bf16[104,768]{1,0:T(8,128)(2,1)} %get-tuple-element.300.refs_0_, ...), custom_call_target="tpu_custom_call" | custom-call | flops 1472200704 | bytes 9752064 | tf_op jit(solution)/shard_map/pallas_call | solution.py:194
  274.2 10.9 %shard_map.196 = bf16[12,2,16,48,384]{4,3,2,1,0:T(8,128)(2,1)} custom-call(s32[5]{0:T(128)} %stack.110.me_ref, bf16[4,12,48,384]{3,2,1,0:T(8,128)(2,1)} %copy-done.8, bf16[4,12,48,384]{3,2,1,0:T(8,128)(2,1)} %collective-permute-done.10.refs_1_, bf16[4,12,48,384]{3,2,1,0:T(8,128)(2,1)} %collective-permute-done.12.refs_2_, ...), custom_call_target="tpu_custom_call" | custom-call | bytes 28311552 | tf_op jit(solution)/shard_map/pallas_call | solution.py:875
  285.2 9.4 %shard_map.197 = (bf16[416,768]{1,0:T(8,128)(2,1)}, bf16[416,768]{1,0:T(8,128)(2,1)}, f32[416,768]{1,0:T(8,128)}, bf16[3,416,768]{2,1,0:T(8,128)(2,1)}) custom-call(s32[5]{0:T(128)} %stack.110.me_ref, bf16[104,768]{1,0:T(8,128)(2,1)} %get-tuple-element.321.refs_0_, bf16[104,768]{1,0:T(8,128)(2,1)} %copy-done.56, bf16[104,768]{1,0:T(8,128)(2,1)} %copy-done.57, ...), custom_call_target="tpu_custom_call" | custom-call | flops 2453667840 | bytes 27641876 | tf_op jit(solution)/shard_map/pallas_call | solution.py:194
  294.6 9.9 %shard_map.198 = (bf16[416,768]{1,0:T(8,128)(2,1)}, f32[416,768]{1,0:T(8,128)}, f32[2,3,2,2,208]{4,3,2,1,0:T(2,128)}) custom-call(bf16[3,416,768]{2,1,0:T(8,128)(2,1)} %get-tuple-element.331.qkv_ref, f32[416,768]{1,0:T(8,128)} %get-tuple-element.332.x1_ref, bf16[12,2,768,384]{3,2,1,0:T(8,128)(2,1)} %bitcast.197), custom_call_target="tpu_custom_call" | custom-call | flops 490733568 | bytes 19287552 | tf_op jit(solution)/shard_map/pallas_call | solution.py:194
  308.0 13.2 %shard_map.199 = (f32[416,768]{1,0:T(8,128)}, bf16[104,768]{1,0:T(8,128)(2,1)}, bf16[104,768]{1,0:T(8,128)(2,1)}, bf16[104,768]{1,0:T(8,128)(2,1)}, bf16[104,768]{1,0:T(8,128)(2,1)}) custom-call(f32[416,768]{1,0:T(8,128)} %get-tuple-element.338.x2_ref, bf16[12,2,768,384]{3,2,1,0:T(8,128)(2,1)} %bitcast.198, bf16[12,2,768,384]{3,2,1,0:T(8,128)(2,1)} %bitcast.199, ...), custom_call_target="tpu_custom_call" | custom-call | flops 3925868544 | bytes 31543316 | tf_op jit(solution)/shard_map/pallas_call | solution.py:194
  335.7 12.4 %shard_map.200 = (bf16[416,768]{1,0:T(8,128)(2,1)}, bf16[3,416,768]{2,1,0:T(8,128)(2,1)}, f32[2,3,2,416]{3,2,1,0:T(2,128)}, bf16[104,768]{1,0:T(8,128)(2,1)}, bf...) custom-call(bf16[104,768]{1,0:T(8,128)(2,1)} %get-tuple-element.340.refs_0_, ...), custom_call_target="tpu_custom_call" | custom-call | flops 1472200704 | bytes 9752064 | tf_op jit(solution)/shard_map/pallas_call | solution.py:194
  371.0 11.0 %shard_map.201 = bf16[12,2,16,48,384]{4,3,2,1,0:T(8,128)(2,1)} custom-call(s32[5]{0:T(128)} %stack.110.me_ref, bf16[4,12,48,384]{3,2,1,0:T(8,128)(2,1)} %copy-done.9, bf16[4,12,48,384]{3,2,1,0:T(8,128)(2,1)} %collective-permute-done.30.refs_1_, bf16[4,12,48,384]{3,2,1,0:T(8,128)(2,1)} %collective-permute-done.32.refs_2_, ...), custom_call_target="tpu_custom_call" | custom-call | bytes 28311552 | tf_op jit(solution)/shard_map/pallas_call | solution.py:875
  382.0 9.4 %shard_map.202 = (bf16[416,768]{1,0:T(8,128)(2,1)}, bf16[416,768]{1,0:T(8,128)(2,1)}, f32[416,768]{1,0:T(8,128)}, bf16[3,416,768]{2,1,0:T(8,128)(2,1)}) custom-call(s32[5]{0:T(128)} %stack.110.me_ref, bf16[104,768]{1,0:T(8,128)(2,1)} %get-tuple-element.358.refs_0_, bf16[104,768]{1,0:T(8,128)(2,1)} %copy-done.53, bf16[104,768]{1,0:T(8,128)(2,1)} %copy-done.54, ...), custom_call_target="tpu_custom_call" | custom-call | flops 2453667840 | bytes 27641876 | tf_op jit(solution)/shard_map/pallas_call | solution.py:194
  391.4 10.3 %shard_map.203 = (bf16[416,768]{1,0:T(8,128)(2,1)}, f32[416,768]{1,0:T(8,128)}, f32[2,3,2,2,208]{4,3,2,1,0:T(2,128)}) custom-call(bf16[3,416,768]{2,1,0:T(8,128)(2,1)} %get-tuple-element.369.qkv_ref, f32[416,768]{1,0:T(8,128)} %get-tuple-element.370.x1_ref, bf16[12,2,768,384]{3,2,1,0:T(8,128)(2,1)} %bitcast.205), custom_call_target="tpu_custom_call" | custom-call | flops 490733568 | bytes 19287552 | tf_op jit(solution)/shard_map/pallas_call | solution.py:194
  401.7 25.3 %shard_map.204 = (f32[416,768]{1,0:T(8,128)}, bf16[4,2,2,192,384]{4,3,2,1,0:T(8,128)(2,1)}, bf16[4,2,2,192,384]{4,3,2,1,0:T(8,128)(2,1)}, bf16[4,2,2,192,384]{4,...) custom-call(s32[5]{0:T(128)} %stack.110.me_ref, ...), custom_call_target="tpu_custom_call" | custom-call | flops 9814671360 | bytes 42885140 | tf_op jit(solution)/shard_map/pallas_call | solution.py:194
  426.9 10.8 %collective-permute-start.37 = (bf16[4,2,2,192,384]{4,3,2,1,0:T(8,128)(2,1)}, bf16[4,2,2,192,384]{4,3,2,1,0:T(8,128)(2,1)S(1)}, u32[]{:S(2)}, u32[]{:S(2)}) collective-permute-start(bf16[4,2,2,192,384]{4,3,2,1,0:T(8,128)(2,1)} %get-tuple-element.378), channel_id=1, source_target_pairs={{0,8},{8,0},{16,24},{24,16},{1,9},{9,1},{17,25},{25,17},{2,10},{10... | collective-permute-start | bytes 7077896 | tf_op jit(solution)/shard_map/ppermute | solution.py:1040
  437.8 21.6 %shard_map.205 = (f32[416,768]{1,0:T(8,128)}, bf16[4,2,2,192,384]{4,3,2,1,0:T(8,128)(2,1)}, bf16[4,2,2,192,384]{4,3,2,1,0:T(8,128)(2,1)}, f32[2,768]{1,0:T(2,128)}) custom-call(s32[5]{0:T(128)} %stack.110.me_ref, f32[416,768]{1,0:T(8,128)} %get-tuple-element.372.g_ref, f32[416,768]{1,0:T(8,128)} %get-tuple-element.370.x1_ref, ...), custom_call_target="tpu_custom_call" | custom-call | flops 3925868544 | bytes 39464468 | tf_op jit(solution)/shard_map/pallas_call | solution.py:194
  470.9 7.8 shard_map.207
  478.7 13.0 %collective-permute-start.39 = (bf16[104,768]{1,0:T(8,128)(2,1)}, bf16[104,768]{1,0:T(8,128)(2,1)S(1)}, u32[]{:S(2)}, u32[]{:S(2)}) collective-permute-start(bf16[104,768]{1,0:T(8,128)(2,1)} %get-tuple-element.387), channel_id=1, source_target_pairs={{0,8},{2,10},{4,12},{6,14},{8,0},{10,2},{12,4},{14,6},{16,24},{18,... | collective-permute-start | bytes 479240 | tf_op jit(solution)/shard_map/ppermute | solution.py:795
  506.9 18.3 %shard_map.209 = (bf16[104,768]{1,0:T(8,128)(2,1)}, bf16[104,768]{1,0:T(8,128)(2,1)}, bf16[104,768]{1,0:T(8,128)(2,1)}, bf16[104,768]{1,0:T(8,128)(2,1)}, bf16[1...) custom-call(s32[5]{0:T(128)} %stack.110.me_ref, ...), custom_call_target="tpu_custom_call" | custom-call | flops 2944401408 | bytes 13291028 | tf_op jit(solution)/shard_map/pallas_call | solution.py:194
  533.2 15.0 %collective-permute-start.48 = (bf16[104,768]{1,0:T(8,128)(2,1)}, bf16[104,768]{1,0:T(8,128)(2,1)S(1)}, u32[]{:S(2)}, u32[]{:S(2)}) collective-permute-start(bf16[104,768]{1,0:T(8,128)(2,1)} %get-tuple-element.411), channel_id=1, source_target_pairs={{0,2},{2,0},{4,6},{6,4},{8,10},{10,8},{12,14},{14,12},{16,18},{18,... | collective-permute-start | bytes 479240 | tf_op jit(solution)/shard_map/ppermute | solution.py:795
  563.0 22.6 %shard_map.212 = (f32[416,768]{1,0:T(8,128)}, bf16[4,2,2,192,384]{4,3,2,1,0:T(8,128)(2,1)}, bf16[4,2,2,192,384]{4,3,2,1,0:T(8,128)(2,1)}, bf16[4,2,2,192,384]{4,...) custom-call(s32[5]{0:T(128)} %stack.110.me_ref, f32[416,768]{1,0:T(8,128)} %get-tuple-element.430.g_ref, ...), custom_call_target="tpu_custom_call" | custom-call | flops 9814671360 | bytes 41607188 | tf_op jit(solution)/shard_map/pallas_call | solution.py:194
  591.7 21.7 %shard_map.214 = (f32[416,768]{1,0:T(8,128)}, bf16[4,2,2,192,384]{4,3,2,1,0:T(8,128)(2,1)}, bf16[4,2,2,192,384]{4,3,2,1,0:T(8,128)(2,1)}, f32[2,768]{1,0:T(2,128)}) custom-call(s32[5]{0:T(128)} %stack.110.me_ref, f32[416,768]{1,0:T(8,128)} %get-tuple-element.440.g_ref, f32[416,768]{1,0:T(8,128)} %get-tuple-element.332.x1_ref, ...), custom_call_target="tpu_custom_call" | custom-call | flops 3925868544 | bytes 39464468 | tf_op jit(solution)/shard_map/pallas_call | solution.py:194
  615.3 8.1 collective-permute-done.57.refs_17_
  632.7 7.8 shard_map.216
  642.4 16.5 %collective-permute-done.63.refs_2_ = bf16[8,192,384]{2,1,0:T(8,128)(2,1)S(1)} collective-permute-done((bf16[8,192,384]{2,1,0:T(8,128)(2,1)}, bf16[8,192,384]{2,1,0:T(8,128)(2,1)S(1)}, u32[]{:S(2)}, u32[]{:S(2)}) %collective-permute-start.63) | collective-permute-done | bytes 1179680 | tf_op jit(solution)/shard_map/ppermute | solution.py:1040
  668.7 18.3 %shard_map.218 = (bf16[104,768]{1,0:T(8,128)(2,1)}, bf16[104,768]{1,0:T(8,128)(2,1)}, bf16[104,768]{1,0:T(8,128)(2,1)}, bf16[104,768]{1,0:T(8,128)(2,1)}, bf16[1...) custom-call(s32[5]{0:T(128)} %stack.110.me_ref, ...), custom_call_target="tpu_custom_call" | custom-call | flops 2944401408 | bytes 13291028 | tf_op jit(solution)/shard_map/pallas_call | solution.py:194
  718.4 12.7 %collective-permute-done.76.refs_3_.refs_8_ = bf16[6,192,384]{2,1,0:T(8,128)(2,1)S(1)} collective-permute-done((bf16[6,192,384]{2,1,0:T(8,128)(2,1)}, bf16[6,192,384]{2,1,0:T(8,128)(2,1)S(1)}, u32[]{:S(2)}, u32[]{:S(2)}) %collective-permute-start.76) | collective-permute-done | bytes 884768 | tf_op jit(solution)/shard_map/ppermute | solution.py:1040
  750.4 7.6 all-to-all-done.2
  783.5 20.1 %reduce-scatter.12.cloned.1.call-done = bf16[8,48,384]{2,1,0:T(8,128)(2,1)} async-done(((bf16[8,192,384]{2,1,0:T(8,128)(2,1)}), bf16[8,48,384]{2,1,0:T(8,128)(2,1)}) %reduce-scatter.12.cloned.1.call-update) | async-done | bytes 294928 | tf_op jit(solution)/shard_map/reduce_scatter | solution.py:1069
  (448 shorter events, 273.2 us)
Async XLA Ops:
  16.0 54.4 %all-gather.4.cloned.1.call-start = ((), (), s32[]{:S(2)}) async-start(), calls=%async_computation.8 | async-start | bytes 1843200 | tf_op jit(solution)/shard_map/all_gather | solution.py:823
  25.8 220.9 %all-gather.6.cloned.1.call-start = ((), (), s32[]{:S(2)}) async-start(), calls=%async_computation.9 | async-start | bytes 6635520 | tf_op jit(solution)/shard_map/all_gather | solution.py:827
  73.0 256.5 %all-gather.8.cloned.1.call-start = ((), (), s32[]{:S(2)}) async-start(), calls=%async_computation.10 | async-start | bytes 6635520 | tf_op jit(solution)/shard_map/all_gather | solution.py:827
  73.7 668.4 %reduce-scatter.14.cloned.1.call-start = ((), (), s32[]{:S(2)}) async-start(), calls=%async_computation.15 | async-start | bytes 1474560 | tf_op jit(solution)/shard_map/reduce_scatter | solution.py:1069
  74.6 36.7 %collective-permute-start.7 = (bf16[12,48,384]{2,1,0:T(8,128)(2,1)S(1)}, bf16[12,48,384]{2,1,0:T(8,128)(2,1)S(1)}, u32[]{:S(2)}, u32[]{:S(2)}) collective-permute-start(bf16[12,48,384]{2,1,0:T(8,128)(2,1)S(1)} %pad_maximum_fusion.10), channel_id=1, source_target_pairs={{0,6},{2,0},{4,2},{6,4},{1,7},{3,1},{5,3},{7,5},{8,14},{10,8},{12,... | collective-permute-start | bytes 1327112 | tf_op jit(solution)/shard_map/ppermute | solution.py:837
  75.9 38.8 %collective-permute-start.6 = (bf16[12,48,384]{2,1,0:T(8,128)(2,1)S(1)}, bf16[12,48,384]{2,1,0:T(8,128)(2,1)S(1)}, u32[]{:S(2)}, u32[]{:S(2)}) collective-permute-start(bf16[12,48,384]{2,1,0:T(8,128)(2,1)S(1)} %pad_maximum_fusion.10), channel_id=1, source_target_pairs={{0,4},{2,6},{4,0},{6,2},{1,5},{3,7},{5,1},{7,3},{8,12},{10,14},{12... | collective-permute-start | bytes 1327112 | tf_op jit(solution)/shard_map/ppermute | solution.py:837
  76.6 38.1 %collective-permute-start.5 = (bf16[12,48,384]{2,1,0:T(8,128)(2,1)S(1)}, bf16[12,48,384]{2,1,0:T(8,128)(2,1)S(1)}, u32[]{:S(2)}, u32[]{:S(2)}) collective-permute-start(bf16[12,48,384]{2,1,0:T(8,128)(2,1)S(1)} %pad_maximum_fusion.10), channel_id=1, source_target_pairs={{0,2},{2,4},{4,6},{6,0},{1,3},{3,5},{5,7},{7,1},{8,10},{10,12},{12... | collective-permute-start | bytes 1327112 | tf_op jit(solution)/shard_map/ppermute | solution.py:837
  144.8 56.9 %collective-permute-start.11 = (bf16[4,12,48,384]{3,2,1,0:T(8,128)(2,1)S(1)}, bf16[4,12,48,384]{3,2,1,0:T(8,128)(2,1)}, u32[]{:S(2)}, u32[]{:S(2)}) collective-permute-start(bf16[4,12,48,384]{3,2,1,0:T(8,128)(2,1)S(1)} %pad_maximum_fusion.1.refs_4_), channel_id=1, source_target_pairs={{0,16},{8,24},{16,0},{24,8},{1,17},{9,25},{17,1},{25,9},{2,18},{10... | collective-permute-start | bytes 5308424 | tf_op jit(solution)/shard_map/ppermute | solution.py:1040
  146.5 55.2 %collective-permute-start.12 = (bf16[4,12,48,384]{3,2,1,0:T(8,128)(2,1)S(1)}, bf16[4,12,48,384]{3,2,1,0:T(8,128)(2,1)}, u32[]{:S(2)}, u32[]{:S(2)}) collective-permute-start(bf16[4,12,48,384]{3,2,1,0:T(8,128)(2,1)S(1)} %pad_maximum_fusion.refs_0_), channel_id=1, source_target_pairs={{0,8},{8,0},{16,24},{24,16},{1,9},{9,1},{17,25},{25,17},{2,10},{10... | collective-permute-start | bytes 5308424 | tf_op jit(solution)/shard_map/ppermute | solution.py:1040
  146.8 56.8 %collective-permute-start.10 = (bf16[4,12,48,384]{3,2,1,0:T(8,128)(2,1)S(1)}, bf16[4,12,48,384]{3,2,1,0:T(8,128)(2,1)}, u32[]{:S(2)}, u32[]{:S(2)}) collective-permute-start(bf16[4,12,48,384]{3,2,1,0:T(8,128)(2,1)S(1)} %pad_maximum_fusion.refs_0_), channel_id=1, source_target_pairs={{0,1},{1,0},{2,3},{3,2},{4,5},{5,4},{6,7},{7,6},{8,9},{9,8},{10,11... | collective-permute-start | bytes 5308424 | tf_op jit(solution)/shard_map/ppermute | solution.py:1040
  203.5 57.5 %collective-permute-start.20 = (bf16[4,12,48,384]{3,2,1,0:T(8,128)(2,1)}, bf16[4,12,48,384]{3,2,1,0:T(8,128)(2,1)}, u32[]{:S(2)}, u32[]{:S(2)}) collective-permute-start(bf16[4,12,48,384]{3,2,1,0:T(8,128)(2,1)} %collective-permute-done.10.refs_1_), channel_id=1, source_target_pairs={{0,8},{8,0},{16,24},{24,16},{1,9},{9,1},{17,25},{25,17},{2,10},{10... | collective-permute-start | bytes 5308424 | tf_op jit(solution)/shard_map/ppermute | solution.py:1040
  203.5 57.5 %collective-permute-start.21 = (bf16[4,12,48,384]{3,2,1,0:T(8,128)(2,1)}, bf16[4,12,48,384]{3,2,1,0:T(8,128)(2,1)}, u32[]{:S(2)}, u32[]{:S(2)}) collective-permute-start(bf16[4,12,48,384]{3,2,1,0:T(8,128)(2,1)} %collective-permute-done.11.refs_5_), channel_id=1, source_target_pairs={{0,8},{8,0},{16,24},{24,16},{1,9},{9,1},{17,25},{25,17},{2,10},{10... | collective-permute-start | bytes 5308424 | tf_op jit(solution)/shard_map/ppermute | solution.py:1040
  206.4 40.3 %collective-permute-start.15 = (bf16[12,48,384]{2,1,0:T(8,128)(2,1)S(1)}, bf16[12,48,384]{2,1,0:T(8,128)(2,1)S(1)}, u32[]{:S(2)}, u32[]{:S(2)}) collective-permute-start(bf16[12,48,384]{2,1,0:T(8,128)(2,1)S(1)} %pad_maximum_fusion.11), channel_id=1, source_target_pairs={{0,4},{2,6},{4,0},{6,2},{1,5},{3,7},{5,1},{7,3},{8,12},{10,14},{12... | collective-permute-start | bytes 1327112 | tf_op jit(solution)/shard_map/ppermute | solution.py:837
  207.9 38.8 %collective-permute-start.14 = (bf16[12,48,384]{2,1,0:T(8,128)(2,1)S(1)}, bf16[12,48,384]{2,1,0:T(8,128)(2,1)S(1)}, u32[]{:S(2)}, u32[]{:S(2)}) collective-permute-start(bf16[12,48,384]{2,1,0:T(8,128)(2,1)S(1)} %pad_maximum_fusion.11), channel_id=1, source_target_pairs={{0,2},{2,4},{4,6},{6,0},{1,3},{3,5},{5,7},{7,1},{8,10},{10,12},{12... | collective-permute-start | bytes 1327112 | tf_op jit(solution)/shard_map/ppermute | solution.py:837
  269.0 35.5 %collective-permute-start.23 = (bf16[2,12,48,384]{3,2,1,0:T(8,128)(2,1)S(1)}, bf16[2,12,48,384]{3,2,1,0:T(8,128)(2,1)S(1)}, u32[]{:S(2)}, u32[]{:S(2)}) collective-permute-start(bf16[2,12,48,384]{3,2,1,0:T(8,128)(2,1)S(1)} %pad_maximum_fusion.7), channel_id=1, source_target_pairs={{0,1},{1,0},{2,3},{3,2},{4,5},{5,4},{6,7},{7,6},{8,9},{9,8},{10,11... | collective-permute-start | bytes 2654216 | tf_op jit(solution)/shard_map/ppermute | solution.py:1040
  269.8 34.7 %collective-permute-start.22 = (bf16[2,12,48,384]{3,2,1,0:T(8,128)(2,1)S(1)}, bf16[2,12,48,384]{3,2,1,0:T(8,128)(2,1)S(1)}, u32[]{:S(2)}, u32[]{:S(2)}) collective-permute-start(bf16[2,12,48,384]{3,2,1,0:T(8,128)(2,1)S(1)} %pad_maximum_fusion.6), channel_id=1, source_target_pairs={{0,16},{8,24},{16,0},{24,8},{1,17},{9,25},{17,1},{25,9},{2,18},{10... | collective-permute-start | bytes 2654216 | tf_op jit(solution)/shard_map/ppermute | solution.py:1040
  304.7 57.5 %collective-permute-start.33 = (bf16[4,12,48,384]{3,2,1,0:T(8,128)(2,1)S(1)}, bf16[4,12,48,384]{3,2,1,0:T(8,128)(2,1)}, u32[]{:S(2)}, u32[]{:S(2)}) collective-permute-start(bf16[4,12,48,384]{3,2,1,0:T(8,128)(2,1)S(1)} %pad_maximum_fusion.3.refs_4_), channel_id=1, source_target_pairs={{0,8},{8,0},{16,24},{24,16},{1,9},{9,1},{17,25},{25,17},{2,10},{10... | collective-permute-start | bytes 5308424 | tf_op jit(solution)/shard_map/ppermute | solution.py:1040
  304.8 57.5 %collective-permute-start.31 = (bf16[4,12,48,384]{3,2,1,0:T(8,128)(2,1)S(1)}, bf16[4,12,48,384]{3,2,1,0:T(8,128)(2,1)}, u32[]{:S(2)}, u32[]{:S(2)}) collective-permute-start(bf16[4,12,48,384]{3,2,1,0:T(8,128)(2,1)S(1)} %pad_maximum_fusion.3.refs_4_), channel_id=1, source_target_pairs={{0,16},{8,24},{16,0},{24,8},{1,17},{9,25},{17,1},{25,9},{2,18},{10... | collective-permute-start | bytes 5308424 | tf_op jit(solution)/shard_map/ppermute | solution.py:1040
  306.3 56.0 %collective-permute-start.32 = (bf16[4,12,48,384]{3,2,1,0:T(8,128)(2,1)S(1)}, bf16[4,12,48,384]{3,2,1,0:T(8,128)(2,1)}, u32[]{:S(2)}, u32[]{:S(2)}) collective-permute-start(bf16[4,12,48,384]{3,2,1,0:T(8,128)(2,1)S(1)} %pad_maximum_fusion.2.refs_0_), channel_id=1, source_target_pairs={{0,8},{8,0},{16,24},{24,16},{1,9},{9,1},{17,25},{25,17},{2,10},{10... | collective-permute-start | bytes 5308424 | tf_op jit(solution)/shard_map/ppermute | solution.py:1040
  306.6 55.7 %collective-permute-start.30 = (bf16[4,12,48,384]{3,2,1,0:T(8,128)(2,1)S(1)}, bf16[4,12,48,384]{3,2,1,0:T(8,128)(2,1)}, u32[]{:S(2)}, u32[]{:S(2)}) collective-permute-start(bf16[4,12,48,384]{3,2,1,0:T(8,128)(2,1)S(1)} %pad_maximum_fusion.2.refs_0_), channel_id=1, source_target_pairs={{0,1},{1,0},{2,3},{3,2},{4,5},{5,4},{6,7},{7,6},{8,9},{9,8},{10,11... | collective-permute-start | bytes 5308424 | tf_op jit(solution)/shard_map/ppermute | solution.py:1040
  426.9 35.5 %collective-permute-start.37 = (bf16[4,2,2,192,384]{4,3,2,1,0:T(8,128)(2,1)}, bf16[4,2,2,192,384]{4,3,2,1,0:T(8,128)(2,1)S(1)}, u32[]{:S(2)}, u32[]{:S(2)}) collective-permute-start(bf16[4,2,2,192,384]{4,3,2,1,0:T(8,128)(2,1)} %get-tuple-element.378), channel_id=1, source_target_pairs={{0,8},{8,0},{16,24},{24,16},{1,9},{9,1},{17,25},{25,17},{2,10},{10... | collective-permute-start | bytes 7077896 | tf_op jit(solution)/shard_map/ppermute | solution.py:1040
  459.4 35.4 %collective-permute-start.44 = (bf16[4,2,2,192,384]{4,3,2,1,0:T(8,128)(2,1)}, bf16[4,2,2,192,384]{4,3,2,1,0:T(8,128)(2,1)S(1)}, u32[]{:S(2)}, u32[]{:S(2)}) collective-permute-start(bf16[4,2,2,192,384]{4,3,2,1,0:T(8,128)(2,1)} %get-tuple-element.393), channel_id=1, source_target_pairs={{0,8},{8,0},{16,24},{24,16},{1,9},{9,1},{17,25},{25,17},{2,10},{10... | collective-permute-start | bytes 7077896 | tf_op jit(solution)/shard_map/ppermute | solution.py:1040
  556.3 29.9 %collective-permute-start.54 = (bf16[6,192,384]{2,1,0:T(8,128)(2,1)}, bf16[6,192,384]{2,1,0:T(8,128)(2,1)S(1)}, u32[]{:S(2)}, u32[]{:S(2)}) collective-permute-start(bf16[6,192,384]{2,1,0:T(8,128)(2,1)} %get-tuple-element.432), channel_id=1, source_target_pairs={{0,1},{1,0},{2,3},{3,2},{4,5},{5,4},{6,7},{7,6},{8,9},{9,8},{10,11... | collective-permute-start | bytes 2654216 | tf_op jit(solution)/shard_map/ppermute | solution.py:1040
  557.5 28.6 %collective-permute-start.55 = (bf16[8,192,384]{2,1,0:T(8,128)(2,1)}, bf16[8,192,384]{2,1,0:T(8,128)(2,1)S(1)}, u32[]{:S(2)}, u32[]{:S(2)}) collective-permute-start(bf16[8,192,384]{2,1,0:T(8,128)(2,1)} %get-tuple-element.433), channel_id=1, source_target_pairs={{0,16},{8,24},{16,0},{24,8},{1,17},{9,25},{17,1},{25,9},{2,18},{10... | collective-permute-start | bytes 3538952 | tf_op jit(solution)/shard_map/ppermute | solution.py:1040
  585.6 40.6 %collective-permute-start.58 = (bf16[4,2,2,192,384]{4,3,2,1,0:T(8,128)(2,1)}, bf16[4,2,2,192,384]{4,3,2,1,0:T(8,128)(2,1)}, u32[]{:S(2)}, u32[]{:S(2)}) collective-permute-start(bf16[4,2,2,192,384]{4,3,2,1,0:T(8,128)(2,1)} %get-tuple-element.449), channel_id=1, source_target_pairs={{0,8},{8,0},{16,24},{24,16},{1,9},{9,1},{17,25},{25,17},{2,10},{10... | collective-permute-start | bytes 7077896 | tf_op jit(solution)/shard_map/ppermute | solution.py:1040
  585.6 40.5 %collective-permute-start.59 = (bf16[4,2,2,192,384]{4,3,2,1,0:T(8,128)(2,1)}, bf16[4,2,2,192,384]{4,3,2,1,0:T(8,128)(2,1)}, u32[]{:S(2)}, u32[]{:S(2)}) collective-permute-start(bf16[4,2,2,192,384]{4,3,2,1,0:T(8,128)(2,1)} %get-tuple-element.451), channel_id=1, source_target_pairs={{0,8},{8,0},{16,24},{24,16},{1,9},{9,1},{17,25},{25,17},{2,10},{10... | collective-permute-start | bytes 7077896 | tf_op jit(solution)/shard_map/ppermute | solution.py:1040
  613.4 28.7 %collective-permute-start.65 = (bf16[4,2,2,192,384]{4,3,2,1,0:T(8,128)(2,1)}, bf16[4,2,2,192,384]{4,3,2,1,0:T(8,128)(2,1)S(1)}, u32[]{:S(2)}, u32[]{:S(2)}) collective-permute-start(bf16[4,2,2,192,384]{4,3,2,1,0:T(8,128)(2,1)} %get-tuple-element.465), channel_id=1, source_target_pairs={{0,8},{8,0},{16,24},{24,16},{1,9},{9,1},{17,25},{25,17},{2,10},{10... | collective-permute-start | bytes 7077896 | tf_op jit(solution)/shard_map/ppermute | solution.py:1040
  613.5 130.0 %reduce-scatter.10.cloned.1.call-start = ((), (), s32[]{:S(2)}) async-start(), calls=%async_computation.13 | async-start | bytes 737280 | tf_op jit(solution)/shard_map/reduce_scatter | solution.py:1069
  667.6 91.8 %reduce-scatter.6.cloned.1.call-start = ((), (), s32[]{:S(2)}) async-start(), calls=%async_computation.11 | async-start | bytes 921600 | tf_op jit(solution)/shard_map/reduce_scatter | solution.py:1069
  694.6 86.5 %reduce-scatter.8.cloned.1.call-start = ((), (), s32[]{:S(2)}) async-start(), calls=%async_computation.12 | async-start | bytes 737280 | tf_op jit(solution)/shard_map/reduce_scatter | solution.py:1069
  741.9 61.6 %reduce-scatter.12.cloned.1.call-start = ((), (), s32[]{:S(2)}) async-start(), calls=%async_computation.14 | async-start | bytes 1474560 | tf_op jit(solution)/shard_map/reduce_scatter | solution.py:1069
  777.5 31.9 %all-to-all-start.1 = ((bf16[4,5,48,384]{3,2,1,0:T(8,128)(2,1)}), bf16[4,5,48,384]{3,2,1,0:T(8,128)(2,1)S(1)}, u32[]{:S(2)}, u32[]{:S(2)}) async-start(bf16[4,5,48,384]{3,2,1,0:T(8,128)(2,1)} %shard_map.222), calls=%async_computation.1 | async-start | bytes 1474560 | tf_op jit(solution)/shard_map/all_to_all | solution.py:1066
  (133 other events, 1776.1 us)
Sparse Core Ops, SparseCore 0:
  25.9 44.3 all-gather.3
  73.1 42.7 all-gather.5
  117.8 66.7 all-gather.7
  613.6 27.1 reduce-scatter.13
  667.7 20.5 reduce-scatter.9
  694.7 25.5 reduce-scatter.5
  742.1 21.8 reduce-scatter.7
  766.2 37.2 reduce-scatter.11

commit v15 on v11

--- a/solution.py
+++ b/solution.py
@@ -885,9 +885,13 @@
         self.way = spread_steps(pack, me)
         self.come = next(self.way)
 
+    def hold(self, x):
+        x, self.come = lax.optimization_barrier((x, self.come))
+        return x
+
     def step(self, x):
-        x, come = lax.optimization_barrier((x, self.come))
-        self.come = self.way.send(come)
+        x = self.hold(x)
+        self.come = self.way.send(self.come)
         return x
 
 
@@ -1167,18 +1171,14 @@
     )
     if quick:
         spreads = [Spread(pack, me) for pack in packs_ff]
-        spreads[0].step(())
         weights_ff = []
     else:
         weights_ff = [gather_slabs(pack) for pack in packs_ff]
 
     home = go_home(tokens)
     if quick:
-        (home, gb, later), first = (home, gb, packs_ff[1:]), spreads[0]
-        home, gb, later = first.step((home, gb, later))
-        for spread, pack in zip(spreads[1:], later):
-            spread.come = pack
-            spread.step(())
+        first = spreads[0]
+        home, gb = first.step((home, gb))
     x = as_rows(home)
     send = send_first(rows, x, gb[0], me)
     kept = []
@@ -1186,20 +1186,22 @@
         w = weights[l]
         send = swap_places(send)
         if quick and l == 0:
-            for _ in range(3):
+            for _ in range(2):
                 send = first.step(send)
-            weights_ff.append(first.come)
-            send, weights_ff[0] = lax.optimization_barrier((send, weights_ff[0]))
             for spread in spreads[1:]:
                 send = spread.step(send)
+                send = spread.hold(send)
+            send = first.step(send)
         elif quick:
             send = spreads[l].step(send)
-            weights_ff.append(spreads[l].come)
         a1, qkv1, log1, o1_time = time_forward(rows, send, w)
         back = swap_places(o1_time)
-        if quick and l == 0:
-            for spread in spreads[1:]:
-                back = spread.step(back)
+        if quick:
+            back = spreads[l].step(back)
+            weights_ff.append(spreads[l].come)
+            if l == 0:
+                for spread in spreads[1:]:
+                    back = spread.step(back)
         o1, y1, x1, qkv2 = middle_forward(rows, back, x, w, mixes[l], gb[l], me)
         o2, x2, log2 = space_forward(rows, qkv2, x1, w)
         if quick and l == 0:
@@ -1251,8 +1253,10 @@
             summed[l] = ff + space + rest
         else:
             summed[l] = [reduce_plain(g_ff + [g_space, g_out] + g_time, clip & 1)]
+    norm_sums = reduce_norms(jnp.concatenate(norm_rows, axis=0)).reshape(layers, 2, 3, -1)
     if quick:
-        tokens_grad = move(go_back(from_rows(grad.astype(BF16))), late, me)
+        tokens_grad = go_back(from_rows(grad.astype(BF16)))
+        tokens_grad, norm_sums = move((tokens_grad, norm_sums), late, me, True)
         move((), rest, me, True)
         summed = [[p.result for p in some] for some in summed]
     cuts = (2 * g_ff[0][0].shape[0], g_space[0].shape[0], g_out[0].shape[0], len(g_time))
@@ -1264,7 +1268,6 @@
     if not quick:
         tokens_grad = go_back(from_rows(grad.astype(BF16)))
     tokens_grad = tokens_grad.astype(F32)
-    norm_sums = reduce_norms(jnp.concatenate(norm_rows, axis=0)).reshape(layers, 2, 3, -1)
 
     def stacked(form):
         return jnp.stack([form(*results[l]) for l in range(layers)])

time: 749 us -> 738 us (0.985)
  waiting for transfers between devices: 262 us -> 240 us
  starting transfers between devices: 117 us -> 126 us
    all_to_all x1, waiting for transfers between devices: 55.8 us -> 5.65 us  [gather_norms(): lax.all_to_all(jnp.broadcast_to(padded, (count, width)), ALL, split_axis=...]
    ppermute x46, waiting for transfers between devices: 118 us -> 72.6 us  [cross(): return lax.ppermute(a, axis, [(i, i ^ 1 << bit) for i in range(size)])]
    ppermute x24, waiting for transfers between devices: 36.5 us -> 60 us  [swap_places(): got.append(lax.ppermute(chunks[k], ('clip', 'seq'), pairs))]
    all_gather x2, waiting for transfers between devices: 0.02 us -> 22.6 us  [gather_slabs(): full = lax.all_gather(pack, ('head', 'clip', 'seq'), axis=1, tiled=True)]
    reduce_scatter x5 -> x4, waiting for transfers between devices: 21.5 us -> 0.06 us  [move(): own = lax.psum_scatter(array, 'seq', scatter_dimension=1, tiled=True)]
    all_to_all x1, waiting for transfers between devices: 7.25 us -> 28.2 us  [reduce_norms(): every = lax.all_to_all(a, ALL, split_axis=0, concat_axis=0, tiled=True)]
    ppermute x6, waiting for transfers between devices: 21.5 us -> 37.2 us  [spread_steps(): lax.ppermute(pack, 'seq', [(i, (i + k) % ways) for i in range(ways)])]
    all_to_all x1 -> x2, waiting for transfers between devices: 2.01 us -> 13.2 us  [move(): lax.all_to_all(array, 'seq', split_axis=0, concat_axis=0, tiled=True)]
  transfers between devices with their start and end apart: 90 -> 90, of which waited for: 34 -> 30; matrix products, arithmetic and copies ran while one was open for 5% -> 5% of each run, Pallas kernels for 32% -> 33%
where the time goes in v15:
time: 738 us; the launch traced here: 733 us
  Pallas kernels  295 us (40%)
  waiting for transfers between devices  240 us (33%)
  starting transfers between devices  126 us (17%)
  local copies, waits for them, and re-layouts  38.9 us (5%)
  other arithmetic  17.8 us (2%)
  between operations  16 us (2%)
    pallas_call x18, Pallas kernels, call(): pl.pallas_call(body, out_shape=[shape for shape, _ in outs], grid=grid, i...  232 us
    ppermute x46, waiting for transfers between devices, cross(): return lax.ppermute(a, axis, [(i, i ^ 1 << bit) for i in range(size)])  72.6 us
    ppermute x24, waiting for transfers between devices, swap_places(): got.append(lax.ppermute(chunks[k], ('clip', 'seq'), pairs))  60 us
    ppermute x24, starting transfers between devices, swap_places(): got.append(lax.ppermute(chunks[k], ('clip', 'seq'), pairs))  47.2 us
    pallas_call x9, Pallas kernels, fold(): pl.pallas_call(body, out_shape=[jax.ShapeDtypeStruct(shape, BF16) for sha...  45.4 us
    ppermute x46, starting transfers between devices, cross(): return lax.ppermute(a, axis, [(i, i ^ 1 << bit) for i in range(size)])  38.9 us
    ppermute x6, waiting for transfers between devices, spread_steps(): lax.ppermute(pack, 'seq', [(i, (i + k) % ways) for i in range(ways)])  37.2 us
    all_to_all x1, waiting for transfers between devices, reduce_norms(): every = lax.all_to_all(a, ALL, split_axis=0, concat_axis=0, tiled=True)  28.2 us
  transfers between devices with their start and end apart: 90, of which 30 were waited for; matrix products, arithmetic and copies ran while one was open for 5% of the time, Pallas kernels for 33%

profile of v15, /device:TPU:0, one launch (start us, length us, event | category | flops | bytes accessed | tf_op | source)
XLA Modules:
  0.0 732.7 jit_solution(7497735219475231082)
XLA Ops:
  33.3 8.0 %collective-permute-start.2 = (bf16[104,768]{1,0:T(8,128)(2,1)}, bf16[104,768]{1,0:T(8,128)(2,1)S(1)}, u32[]{:S(2)}, u32[]{:S(2)}) collective-permute-start(bf16[104,768]{1,0:T(8,128)(2,1)} %get-tuple-element.261), channel_id=1, source_target_pairs={{0,8},{2,10},{4,12},{6,14},{8,0},{10,2},{12,4},{14,6},{16,24},{18,... | collective-permute-start | bytes 479240 | tf_op jit(solution)/shard_map/ppermute | solution.py:795
  44.4 8.8 %collective-permute-start.6 = (bf16[8,48,384]{2,1,0:T(8,128)(2,1)S(1)}, bf16[8,48,384]{2,1,0:T(8,128)(2,1)S(1)}, u32[]{:S(2)}, u32[]{:S(2)}) collective-permute-start(bf16[8,48,384]{2,1,0:T(8,128)(2,1)S(1)} %pad_maximum_fusion.12), channel_id=1, source_target_pairs={{0,4},{2,6},{4,0},{6,2},{1,5},{3,7},{5,1},{7,3},{8,12},{10,14},{12... | collective-permute-start | bytes 884744 | tf_op jit(solution)/shard_map/ppermute | solution.py:834
  54.5 27.6 %collective-permute-done.3.refs_2_ = bf16[104,768]{1,0:T(8,128)(2,1)S(1)} collective-permute-done((bf16[104,768]{1,0:T(8,128)(2,1)}, bf16[104,768]{1,0:T(8,128)(2,1)S(1)}, u32[]{:S(2)}, u32[]{:S(2)}) %collective-permute-start.3) | collective-permute-done | bytes 159776 | tf_op jit(solution)/shard_map/ppermute | solution.py:795
  93.3 25.4 %collective-permute-done.9 = bf16[2,8,48,384]{3,2,1,0:T(8,128)(2,1)S(1)} collective-permute-done((bf16[2,8,48,384]{3,2,1,0:T(8,128)(2,1)S(1)}, bf16[2,8,48,384]{3,2,1,0:T(8,128)(2,1)S(1)}, u32[]{:S(2)}, u32[]{:S(2)}) %collective-permute-start.9) | collective-permute-done | bytes 589856 | tf_op jit(solution)/shard_map/ppermute | solution.py:1034
  126.6 13.1 %collective-permute-done.12 = bf16[8,48,384]{2,1,0:T(8,128)(2,1)S(1)} collective-permute-done((bf16[8,48,384]{2,1,0:T(8,128)(2,1)S(1)}, bf16[8,48,384]{2,1,0:T(8,128)(2,1)S(1)}, u32[]{:S(2)}, u32[]{:S(2)}) %collective-permute-start.12) | collective-permute-done | bytes 294944 | tf_op jit(solution)/shard_map/ppermute | solution.py:834
  139.6 19.2 %collective-permute-done.11 = bf16[8,48,384]{2,1,0:T(8,128)(2,1)S(1)} collective-permute-done((bf16[8,48,384]{2,1,0:T(8,128)(2,1)S(1)}, bf16[8,48,384]{2,1,0:T(8,128)(2,1)S(1)}, u32[]{:S(2)}, u32[]{:S(2)}) %collective-permute-start.11) | collective-permute-done | bytes 294944 | tf_op jit(solution)/shard_map/ppermute | solution.py:834
  159.5 12.4 %shard_map.195 = (bf16[416,768]{1,0:T(8,128)(2,1)}, bf16[3,416,768]{2,1,0:T(8,128)(2,1)}, f32[2,3,2,416]{3,2,1,0:T(2,128)}, bf16[104,768]{1,0:T(8,128)(2,1)}, bf...) custom-call(bf16[104,768]{1,0:T(8,128)(2,1)} %get-tuple-element.288.refs_0_, ...), custom_call_target="tpu_custom_call" | custom-call | flops 1472200704 | bytes 14470656 | tf_op jit(solution)/shard_map/pallas_call | solution.py:194
  173.9 7.6 %collective-permute-done.16.refs_2_ = bf16[104,768]{1,0:T(8,128)(2,1)S(1)} collective-permute-done((bf16[104,768]{1,0:T(8,128)(2,1)}, bf16[104,768]{1,0:T(8,128)(2,1)S(1)}, u32[]{:S(2)}, u32[]{:S(2)}) %collective-permute-start.16) | collective-permute-done | bytes 159776 | tf_op jit(solution)/shard_map/ppermute | solution.py:795
  191.6 9.3 %shard_map.196 = (bf16[416,768]{1,0:T(8,128)(2,1)}, bf16[416,768]{1,0:T(8,128)(2,1)}, f32[416,768]{1,0:T(8,128)}, bf16[3,416,768]{2,1,0:T(8,128)(2,1)}) custom-call(s32[5]{0:T(128)} %stack.110.me_ref, bf16[104,768]{1,0:T(8,128)(2,1)} %get-tuple-element.306.refs_0_, bf16[104,768]{1,0:T(8,128)(2,1)} %copy-done.45, bf16[104,768]{1,0:T(8,128)(2,1)} %copy-done.46, ...), custom_call_target="tpu_custom_call" | custom-call | flops 2453667840 | bytes 28821524 | tf_op jit(solution)/shard_map/pallas_call | solution.py:194
  200.9 9.9 %shard_map.197 = (bf16[416,768]{1,0:T(8,128)(2,1)}, f32[416,768]{1,0:T(8,128)}, f32[2,3,2,2,208]{4,3,2,1,0:T(2,128)}) custom-call(bf16[3,416,768]{2,1,0:T(8,128)(2,1)} %get-tuple-element.310.qkv_ref, f32[416,768]{1,0:T(8,128)} %get-tuple-element.311.x1_ref, bf16[9,2,768,384]{3,2,1,0:T(8,128)(2,1)} %bitcast.201), custom_call_target="tpu_custom_call" | custom-call | flops 490733568 | bytes 15748608 | tf_op jit(solution)/shard_map/pallas_call | solution.py:194
  213.6 8.9 %shard_map.198 = bf16[8,2,16,48,384]{4,3,2,1,0:T(8,128)(2,1)} custom-call(s32[5]{0:T(128)} %stack.110.me_ref, bf16[4,8,48,384]{3,2,1,0:T(8,128)(2,1)} %copy-done.21, bf16[4,8,48,384]{3,2,1,0:T(8,128)(2,1)} %collective-permute-done.13.refs_1_, bf16[4,8,48,384]{3,2,1,0:T(8,128)(2,1)} %copy-done.22, bf16[4,8,48,384]{3,2,1,0:T(8,128)(2,1)} %collective-permute-done.14.refs_3_, ...), custom_call_target="tpu_custom_call" | custom-call | bytes 18874368 | tf_op jit(solution)/shard_map/pallas_call | solution.py:869
  222.5 13.3 %shard_map.199 = (f32[416,768]{1,0:T(8,128)}, bf16[104,768]{1,0:T(8,128)(2,1)}, bf16[104,768]{1,0:T(8,128)(2,1)}, bf16[104,768]{1,0:T(8,128)(2,1)}, bf16[104,768]{1,0:T(8,128)(2,1)}) custom-call(f32[416,768]{1,0:T(8,128)} %get-tuple-element.317.x2_ref, bf16[8,2,768,384]{3,2,1,0:T(8,128)(2,1)} %bitcast.214, bf16[8,2,768,384]{3,2,1,0:T(8,128)(2,1)} %bitcast.215, ...), custom_call_target="tpu_custom_call" | custom-call | flops 3925868544 | bytes 22106132 | tf_op jit(solution)/shard_map/pallas_call | solution.py:194
  242.6 8.1 %collective-permute-done.26.refs_3_ = bf16[104,768]{1,0:T(8,128)(2,1)S(1)} collective-permute-done((bf16[104,768]{1,0:T(8,128)(2,1)}, bf16[104,768]{1,0:T(8,128)(2,1)S(1)}, u32[]{:S(2)}, u32[]{:S(2)}) %collective-permute-start.26) | collective-permute-done | bytes 159776 | tf_op jit(solution)/shard_map/ppermute | solution.py:795
  259.0 22.6 %all-gather.5.cloned.1.call-done = bf16[9,1536,384]{2,1,0:T(8,128)(2,1)} async-done(((bf16[9,48,384]{2,1,0:T(8,128)(2,1)}), bf16[9,1536,384]{2,1,0:T(8,128)(2,1)}) %all-gather.5.cloned.1.call-update) | async-done | bytes 10616848 | tf_op jit(solution)/shard_map/all_gather | solution.py:824
  281.6 12.6 %shard_map.200 = (bf16[416,768]{1,0:T(8,128)(2,1)}, bf16[3,416,768]{2,1,0:T(8,128)(2,1)}, f32[2,3,2,416]{3,2,1,0:T(2,128)}, bf16[104,768]{1,0:T(8,128)(2,1)}, bf...) custom-call(bf16[104,768]{1,0:T(8,128)(2,1)} %get-tuple-element.329.refs_0_, ...), custom_call_target="tpu_custom_call" | custom-call | flops 1472200704 | bytes 14470656 | tf_op jit(solution)/shard_map/pallas_call | solution.py:194
  306.1 9.4 %shard_map.201 = (bf16[416,768]{1,0:T(8,128)(2,1)}, bf16[416,768]{1,0:T(8,128)(2,1)}, f32[416,768]{1,0:T(8,128)}, bf16[3,416,768]{2,1,0:T(8,128)(2,1)}) custom-call(s32[5]{0:T(128)} %stack.110.me_ref, bf16[104,768]{1,0:T(8,128)(2,1)} %get-tuple-element.339.refs_0_, bf16[104,768]{1,0:T(8,128)(2,1)} %copy-done.47, bf16[104,768]{1,0:T(8,128)(2,1)} %copy-done.49, ...), custom_call_target="tpu_custom_call" | custom-call | flops 2453667840 | bytes 28821524 | tf_op jit(solution)/shard_map/pallas_call | solution.py:194
  315.4 9.9 %shard_map.202 = (bf16[416,768]{1,0:T(8,128)(2,1)}, f32[416,768]{1,0:T(8,128)}, f32[2,3,2,2,208]{4,3,2,1,0:T(2,128)}) custom-call(bf16[3,416,768]{2,1,0:T(8,128)(2,1)} %get-tuple-element.344.qkv_ref, f32[416,768]{1,0:T(8,128)} %get-tuple-element.345.x1_ref, bf16[9,2,768,384]{3,2,1,0:T(8,128)(2,1)} %bitcast.209), custom_call_target="tpu_custom_call" | custom-call | flops 490733568 | bytes 15748608 | tf_op jit(solution)/shard_map/pallas_call | solution.py:194
  325.4 8.2 %shard_map.203 = bf16[8,2,16,48,384]{4,3,2,1,0:T(8,128)(2,1)} custom-call(s32[5]{0:T(128)} %stack.110.me_ref, bf16[4,8,48,384]{3,2,1,0:T(8,128)(2,1)} %copy-done.23, bf16[4,8,48,384]{3,2,1,0:T(8,128)(2,1)} %collective-permute-done.27.refs_1_, bf16[4,8,48,384]{3,2,1,0:T(8,128)(2,1)} %copy-done.24, bf16[4,8,48,384]{3,2,1,0:T(8,128)(2,1)} %collective-permute-done.28.refs_3_, ...), custom_call_target="tpu_custom_call" | custom-call | bytes 18874368 | tf_op jit(solution)/shard_map/pallas_call | solution.py:869
  333.6 25.4 %shard_map.204 = (f32[416,768]{1,0:T(8,128)}, bf16[4,2,2,192,384]{4,3,2,1,0:T(8,128)(2,1)}, bf16[4,2,2,192,384]{4,3,2,1,0:T(8,128)(2,1)}, bf16[4,2,2,192,384]{4,...) custom-call(s32[5]{0:T(128)} %stack.110.me_ref, ...), custom_call_target="tpu_custom_call" | custom-call | flops 9814671360 | bytes 33447956 | tf_op jit(solution)/shard_map/pallas_call | solution.py:194
  359.6 21.7 %shard_map.205 = (f32[416,768]{1,0:T(8,128)}, bf16[4,2,2,192,384]{4,3,2,1,0:T(8,128)(2,1)}, bf16[4,2,2,192,384]{4,3,2,1,0:T(8,128)(2,1)}, f32[2,768]{1,0:T(2,128)}) custom-call(s32[5]{0:T(128)} %stack.110.me_ref, f32[416,768]{1,0:T(8,128)} %get-tuple-element.351.g_ref, f32[416,768]{1,0:T(8,128)} %get-tuple-element.345.x1_ref, ...), custom_call_target="tpu_custom_call" | custom-call | flops 3925868544 | bytes 32386580 | tf_op jit(solution)/shard_map/pallas_call | solution.py:194
  392.7 7.8 %shard_map.207 = (bf16[104,768]{1,0:T(8,128)(2,1)}, bf16[104,768]{1,0:T(8,128)(2,1)}, bf16[104,768]{1,0:T(8,128)(2,1)}, bf16[104,768]{1,0:T(8,128)(2,1)}, bf16[2...) custom-call(s32[5]{0:T(128)} %stack.110.me_ref, f32[416,768]{1,0:T(8,128)} %get-tuple-element.362.g_ref.refs_5_, ...), custom_call_target="tpu_custom_call" | custom-call | flops 1962934272 | bytes 17350676 | tf_op jit(solution)/shard_map/pallas_call | solution.py:194
  400.5 10.3 %collective-permute-start.39 = (bf16[104,768]{1,0:T(8,128)(2,1)}, bf16[104,768]{1,0:T(8,128)(2,1)S(1)}, u32[]{:S(2)}, u32[]{:S(2)}) collective-permute-start(bf16[104,768]{1,0:T(8,128)(2,1)} %get-tuple-element.366), channel_id=1, source_target_pairs={{0,8},{2,10},{4,12},{6,14},{8,0},{10,2},{12,4},{14,6},{16,24},{18,... | collective-permute-start | bytes 479240 | tf_op jit(solution)/shard_map/ppermute | solution.py:795
  428.5 18.3 %shard_map.209 = (bf16[104,768]{1,0:T(8,128)(2,1)}, bf16[104,768]{1,0:T(8,128)(2,1)}, bf16[104,768]{1,0:T(8,128)(2,1)}, bf16[104,768]{1,0:T(8,128)(2,1)}, bf16[1...) custom-call(s32[5]{0:T(128)} %stack.110.me_ref, ...), custom_call_target="tpu_custom_call" | custom-call | flops 2944401408 | bytes 18009620 | tf_op jit(solution)/shard_map/pallas_call | solution.py:194
  450.0 15.3 %collective-permute-start.48 = (bf16[104,768]{1,0:T(8,128)(2,1)}, bf16[104,768]{1,0:T(8,128)(2,1)S(1)}, u32[]{:S(2)}, u32[]{:S(2)}) collective-permute-start(bf16[104,768]{1,0:T(8,128)(2,1)} %get-tuple-element.390), channel_id=1, source_target_pairs={{0,2},{2,0},{4,6},{6,4},{8,10},{10,8},{12,14},{14,12},{16,18},{18,... | collective-permute-start | bytes 479240 | tf_op jit(solution)/shard_map/ppermute | solution.py:795
  480.0 22.7 %shard_map.212 = (f32[416,768]{1,0:T(8,128)}, bf16[4,2,2,192,384]{4,3,2,1,0:T(8,128)(2,1)}, bf16[4,2,2,192,384]{4,3,2,1,0:T(8,128)(2,1)}, bf16[4,2,2,192,384]{4,...) custom-call(s32[5]{0:T(128)} %stack.110.me_ref, f32[416,768]{1,0:T(8,128)} %get-tuple-element.409.g_ref, ...), custom_call_target="tpu_custom_call" | custom-call | flops 9814671360 | bytes 32170004 | tf_op jit(solution)/shard_map/pallas_call | solution.py:194
  508.8 21.7 %shard_map.214 = (f32[416,768]{1,0:T(8,128)}, bf16[4,2,2,192,384]{4,3,2,1,0:T(8,128)(2,1)}, bf16[4,2,2,192,384]{4,3,2,1,0:T(8,128)(2,1)}, f32[2,768]{1,0:T(2,128)}) custom-call(s32[5]{0:T(128)} %stack.110.me_ref, f32[416,768]{1,0:T(8,128)} %get-tuple-element.419.g_ref, f32[416,768]{1,0:T(8,128)} %get-tuple-element.311.x1_ref, ...), custom_call_target="tpu_custom_call" | custom-call | flops 3925868544 | bytes 32386580 | tf_op jit(solution)/shard_map/pallas_call | solution.py:194
  533.1 8.0 %collective-permute-done.57.refs_17_ = bf16[2,192,384]{2,1,0:T(8,128)(2,1)S(1)} collective-permute-done((bf16[2,192,384]{2,1,0:T(8,128)(2,1)S(1)}, bf16[2,192,384]{2,1,0:T(8,128)(2,1)S(1)}, u32[]{:S(2)}, u32[]{:S(2)}) %collective-permute-start.57) | collective-permute-done | bytes 294944 | tf_op jit(solution)/shard_map/ppermute | solution.py:1034
  550.2 7.8 %shard_map.216 = (bf16[104,768]{1,0:T(8,128)(2,1)}, bf16[104,768]{1,0:T(8,128)(2,1)}, bf16[104,768]{1,0:T(8,128)(2,1)}, bf16[104,768]{1,0:T(8,128)(2,1)}, bf16[2...) custom-call(s32[5]{0:T(128)} %stack.110.me_ref, f32[416,768]{1,0:T(8,128)} %get-tuple-element.434.g_ref.refs_5_, ...), custom_call_target="tpu_custom_call" | custom-call | flops 1962934272 | bytes 17350676 | tf_op jit(solution)/shard_map/pallas_call | solution.py:194
  559.9 16.1 %collective-permute-done.63.refs_2_ = bf16[8,192,384]{2,1,0:T(8,128)(2,1)S(1)} collective-permute-done((bf16[8,192,384]{2,1,0:T(8,128)(2,1)}, bf16[8,192,384]{2,1,0:T(8,128)(2,1)S(1)}, u32[]{:S(2)}, u32[]{:S(2)}) %collective-permute-start.63) | collective-permute-done | bytes 1179680 | tf_op jit(solution)/shard_map/ppermute | solution.py:1034
  586.1 18.5 %shard_map.218 = (bf16[104,768]{1,0:T(8,128)(2,1)}, bf16[104,768]{1,0:T(8,128)(2,1)}, bf16[104,768]{1,0:T(8,128)(2,1)}, bf16[104,768]{1,0:T(8,128)(2,1)}, bf16[1...) custom-call(s32[5]{0:T(128)} %stack.110.me_ref, ...), custom_call_target="tpu_custom_call" | custom-call | flops 2944401408 | bytes 18009620 | tf_op jit(solution)/shard_map/pallas_call | solution.py:194
  641.2 28.2 %all-to-all-done.1 = f32[32,1,384]{2,1,0:T(1,128)} async-done(((f32[32,1,384]{2,1,0:T(1,128)}), f32[32,1,384]{2,1,0:T(1,128)}, u32[]{:S(2)}, u32[]{:S(2)}) %all-to-all-start.1) | async-done | bytes 49184 | tf_op jit(solution)/shard_map/all_to_all | solution.py:1122
  709.2 13.2 %all-to-all-done.2 = bf16[4,5,48,384]{3,2,1,0:T(8,128)(2,1)S(1)} async-done(((bf16[4,5,48,384]{3,2,1,0:T(8,128)(2,1)}), bf16[4,5,48,384]{3,2,1,0:T(8,128)(2,1)S(1)}, u32[]{:S(2)}, u32[]{:S(2)}) %all-to-all-start.2) | async-done | bytes 737312 | tf_op jit(solution)/shard_map/all_to_all | solution.py:1060
  (454 shorter events, 247.5 us)
Async XLA Ops:
  7.2 152.3 %all-gather.3.cloned.1.call-start = ((), (), s32[]{:S(2)}) async-start(), calls=%async_computation.8 | async-start | bytes 10948608 | tf_op jit(solution)/shard_map/all_gather | solution.py:824
  11.0 270.6 %all-gather.5.cloned.1.call-start = ((), (), s32[]{:S(2)}) async-start(), calls=%async_computation.9 | async-start | bytes 10948608 | tf_op jit(solution)/shard_map/all_gather | solution.py:824
  20.0 603.4 %reduce-scatter.7.cloned.1.call-start = ((), (), s32[]{:S(2)}) async-start(), calls=%async_computation.11 | async-start | bytes 737280 | tf_op jit(solution)/shard_map/reduce_scatter | solution.py:1063
  41.3 43.9 %collective-permute-start.7 = (bf16[8,48,384]{2,1,0:T(8,128)(2,1)S(1)}, bf16[8,48,384]{2,1,0:T(8,128)(2,1)S(1)}, u32[]{:S(2)}, u32[]{:S(2)}) collective-permute-start(bf16[8,48,384]{2,1,0:T(8,128)(2,1)S(1)} %pad_maximum_fusion.12), channel_id=1, source_target_pairs={{0,6},{2,0},{4,2},{6,4},{1,7},{3,1},{5,3},{7,5},{8,14},{10,8},{12,... | collective-permute-start | bytes 884744 | tf_op jit(solution)/shard_map/ppermute | solution.py:834
  44.4 45.7 %collective-permute-start.6 = (bf16[8,48,384]{2,1,0:T(8,128)(2,1)S(1)}, bf16[8,48,384]{2,1,0:T(8,128)(2,1)S(1)}, u32[]{:S(2)}, u32[]{:S(2)}) collective-permute-start(bf16[8,48,384]{2,1,0:T(8,128)(2,1)S(1)} %pad_maximum_fusion.12), channel_id=1, source_target_pairs={{0,4},{2,6},{4,0},{6,2},{1,5},{3,7},{5,1},{7,3},{8,12},{10,14},{12... | collective-permute-start | bytes 884744 | tf_op jit(solution)/shard_map/ppermute | solution.py:834
  53.2 36.9 %collective-permute-start.5 = (bf16[8,48,384]{2,1,0:T(8,128)(2,1)S(1)}, bf16[8,48,384]{2,1,0:T(8,128)(2,1)S(1)}, u32[]{:S(2)}, u32[]{:S(2)}) collective-permute-start(bf16[8,48,384]{2,1,0:T(8,128)(2,1)S(1)} %pad_maximum_fusion.12), channel_id=1, source_target_pairs={{0,2},{2,4},{4,6},{6,0},{1,3},{3,5},{5,7},{7,1},{8,10},{10,12},{12... | collective-permute-start | bytes 884744 | tf_op jit(solution)/shard_map/ppermute | solution.py:834
  53.2 28.8 %collective-permute-start.3 = (bf16[104,768]{1,0:T(8,128)(2,1)}, bf16[104,768]{1,0:T(8,128)(2,1)S(1)}, u32[]{:S(2)}, u32[]{:S(2)}) collective-permute-start(bf16[104,768]{1,0:T(8,128)(2,1)} %get-tuple-element.262), channel_id=1, source_target_pairs={{0,2},{2,0},{4,6},{6,4},{8,10},{10,8},{12,14},{14,12},{16,18},{18,... | collective-permute-start | bytes 479240 | tf_op jit(solution)/shard_map/ppermute | solution.py:795
  53.8 31.3 %collective-permute-start.4 = (bf16[104,768]{1,0:T(8,128)(2,1)}, bf16[104,768]{1,0:T(8,128)(2,1)S(1)}, u32[]{:S(2)}, u32[]{:S(2)}) collective-permute-start(bf16[104,768]{1,0:T(8,128)(2,1)} %get-tuple-element.263), channel_id=1, source_target_pairs={{0,10},{2,8},{4,14},{6,12},{8,2},{10,0},{12,6},{14,4},{16,26},{18,... | collective-permute-start | bytes 479240 | tf_op jit(solution)/shard_map/ppermute | solution.py:795
  90.1 28.6 %collective-permute-start.9 = (bf16[2,8,48,384]{3,2,1,0:T(8,128)(2,1)S(1)}, bf16[2,8,48,384]{3,2,1,0:T(8,128)(2,1)S(1)}, u32[]{:S(2)}, u32[]{:S(2)}) collective-permute-start(bf16[2,8,48,384]{3,2,1,0:T(8,128)(2,1)S(1)} %pad_maximum_fusion.5), channel_id=1, source_target_pairs={{0,1},{1,0},{2,3},{3,2},{4,5},{5,4},{6,7},{7,6},{8,9},{9,8},{10,11... | collective-permute-start | bytes 1769480 | tf_op jit(solution)/shard_map/ppermute | solution.py:1034
  120.5 38.3 %collective-permute-start.14 = (bf16[4,8,48,384]{3,2,1,0:T(8,128)(2,1)S(1)}, bf16[4,8,48,384]{3,2,1,0:T(8,128)(2,1)}, u32[]{:S(2)}, u32[]{:S(2)}) collective-permute-start(bf16[4,8,48,384]{3,2,1,0:T(8,128)(2,1)S(1)} %pad_maximum_fusion.1.refs_2_), channel_id=1, source_target_pairs={{0,16},{8,24},{16,0},{24,8},{1,17},{9,25},{17,1},{25,9},{2,18},{10... | collective-permute-start | bytes 3538952 | tf_op jit(solution)/shard_map/ppermute | solution.py:1034
  122.1 36.8 %collective-permute-start.13 = (bf16[4,8,48,384]{3,2,1,0:T(8,128)(2,1)S(1)}, bf16[4,8,48,384]{3,2,1,0:T(8,128)(2,1)}, u32[]{:S(2)}, u32[]{:S(2)}) collective-permute-start(bf16[4,8,48,384]{3,2,1,0:T(8,128)(2,1)S(1)} %pad_maximum_fusion.refs_0_), channel_id=1, source_target_pairs={{0,1},{1,0},{2,3},{3,2},{4,5},{5,4},{6,7},{7,6},{8,9},{9,8},{10,11... | collective-permute-start | bytes 3538952 | tf_op jit(solution)/shard_map/ppermute | solution.py:1034
  123.7 35.1 %collective-permute-start.11 = (bf16[8,48,384]{2,1,0:T(8,128)(2,1)S(1)}, bf16[8,48,384]{2,1,0:T(8,128)(2,1)S(1)}, u32[]{:S(2)}, u32[]{:S(2)}) collective-permute-start(bf16[8,48,384]{2,1,0:T(8,128)(2,1)S(1)} %pad_maximum_fusion.13), channel_id=1, source_target_pairs={{0,4},{2,6},{4,0},{6,2},{1,5},{3,7},{5,1},{7,3},{8,12},{10,14},{12... | collective-permute-start | bytes 884744 | tf_op jit(solution)/shard_map/ppermute | solution.py:834
  124.6 34.2 %collective-permute-start.10 = (bf16[8,48,384]{2,1,0:T(8,128)(2,1)S(1)}, bf16[8,48,384]{2,1,0:T(8,128)(2,1)S(1)}, u32[]{:S(2)}, u32[]{:S(2)}) collective-permute-start(bf16[8,48,384]{2,1,0:T(8,128)(2,1)S(1)} %pad_maximum_fusion.13), channel_id=1, source_target_pairs={{0,2},{2,4},{4,6},{6,0},{1,3},{3,5},{5,7},{7,1},{8,10},{10,12},{12... | collective-permute-start | bytes 884744 | tf_op jit(solution)/shard_map/ppermute | solution.py:834
  139.6 32.8 %collective-permute-start.20 = (bf16[4,8,48,384]{3,2,1,0:T(8,128)(2,1)S(1)}, bf16[4,8,48,384]{3,2,1,0:T(8,128)(2,1)}, u32[]{:S(2)}, u32[]{:S(2)}) collective-permute-start(bf16[4,8,48,384]{3,2,1,0:T(8,128)(2,1)S(1)} %pad_maximum_fusion.1.refs_2_), channel_id=1, source_target_pairs={{0,8},{8,0},{16,24},{24,16},{1,9},{9,1},{17,25},{25,17},{2,10},{10... | collective-permute-start | bytes 3538952 | tf_op jit(solution)/shard_map/ppermute | solution.py:1034
  211.4 45.2 %collective-permute-start.28 = (bf16[4,8,48,384]{3,2,1,0:T(8,128)(2,1)S(1)}, bf16[4,8,48,384]{3,2,1,0:T(8,128)(2,1)}, u32[]{:S(2)}, u32[]{:S(2)}) collective-permute-start(bf16[4,8,48,384]{3,2,1,0:T(8,128)(2,1)S(1)} %pad_maximum_fusion.3.refs_2_), channel_id=1, source_target_pairs={{0,16},{8,24},{16,0},{24,8},{1,17},{9,25},{17,1},{25,9},{2,18},{10... | collective-permute-start | bytes 3538952 | tf_op jit(solution)/shard_map/ppermute | solution.py:1034
  211.9 45.7 %collective-permute-start.27 = (bf16[4,8,48,384]{3,2,1,0:T(8,128)(2,1)S(1)}, bf16[4,8,48,384]{3,2,1,0:T(8,128)(2,1)}, u32[]{:S(2)}, u32[]{:S(2)}) collective-permute-start(bf16[4,8,48,384]{3,2,1,0:T(8,128)(2,1)S(1)} %pad_maximum_fusion.2.refs_0_), channel_id=1, source_target_pairs={{0,1},{1,0},{2,3},{3,2},{4,5},{5,4},{6,7},{7,6},{8,9},{9,8},{10,11... | collective-permute-start | bytes 3538952 | tf_op jit(solution)/shard_map/ppermute | solution.py:1034
  236.1 58.5 %collective-permute-start.34 = (bf16[4,8,48,384]{3,2,1,0:T(8,128)(2,1)S(1)}, bf16[4,8,48,384]{3,2,1,0:T(8,128)(2,1)}, u32[]{:S(2)}, u32[]{:S(2)}) collective-permute-start(bf16[4,8,48,384]{3,2,1,0:T(8,128)(2,1)S(1)} %pad_maximum_fusion.3.refs_2_), channel_id=1, source_target_pairs={{0,8},{8,0},{16,24},{24,16},{1,9},{9,1},{17,25},{25,17},{2,10},{10... | collective-permute-start | bytes 3538952 | tf_op jit(solution)/shard_map/ppermute | solution.py:1034
  237.4 59.9 %collective-permute-start.32 = (bf16[4,8,48,384]{3,2,1,0:T(8,128)(2,1)S(1)}, bf16[4,8,48,384]{3,2,1,0:T(8,128)(2,1)}, u32[]{:S(2)}, u32[]{:S(2)}) collective-permute-start(bf16[4,8,48,384]{3,2,1,0:T(8,128)(2,1)S(1)} %pad_maximum_fusion.2.refs_0_), channel_id=1, source_target_pairs={{0,8},{8,0},{16,24},{24,16},{1,9},{9,1},{17,25},{25,17},{2,10},{10... | collective-permute-start | bytes 3538952 | tf_op jit(solution)/shard_map/ppermute | solution.py:1034
  257.6 47.8 %collective-permute-start.33 = (bf16[4,8,48,384]{3,2,1,0:T(8,128)(2,1)}, bf16[4,8,48,384]{3,2,1,0:T(8,128)(2,1)}, u32[]{:S(2)}, u32[]{:S(2)}) collective-permute-start(bf16[4,8,48,384]{3,2,1,0:T(8,128)(2,1)} %collective-permute-done.27.refs_1_), channel_id=1, source_target_pairs={{0,8},{8,0},{16,24},{24,16},{1,9},{9,1},{17,25},{25,17},{2,10},{10... | collective-permute-start | bytes 3538952 | tf_op jit(solution)/shard_map/ppermute | solution.py:1034
  257.6 47.8 %collective-permute-start.35 = (bf16[4,8,48,384]{3,2,1,0:T(8,128)(2,1)}, bf16[4,8,48,384]{3,2,1,0:T(8,128)(2,1)}, u32[]{:S(2)}, u32[]{:S(2)}) collective-permute-start(bf16[4,8,48,384]{3,2,1,0:T(8,128)(2,1)} %collective-permute-done.28.refs_3_), channel_id=1, source_target_pairs={{0,8},{8,0},{16,24},{24,16},{1,9},{9,1},{17,25},{25,17},{2,10},{10... | collective-permute-start | bytes 3538952 | tf_op jit(solution)/shard_map/ppermute | solution.py:1034
  381.3 29.8 %collective-permute-start.44 = (bf16[4,2,2,192,384]{4,3,2,1,0:T(8,128)(2,1)}, bf16[4,2,2,192,384]{4,3,2,1,0:T(8,128)(2,1)S(1)}, u32[]{:S(2)}, u32[]{:S(2)}) collective-permute-start(bf16[4,2,2,192,384]{4,3,2,1,0:T(8,128)(2,1)} %get-tuple-element.372), channel_id=1, source_target_pairs={{0,8},{8,0},{16,24},{24,16},{1,9},{9,1},{17,25},{25,17},{2,10},{10... | collective-permute-start | bytes 7077896 | tf_op jit(solution)/shard_map/ppermute | solution.py:1034
  473.2 30.1 %collective-permute-start.54 = (bf16[6,192,384]{2,1,0:T(8,128)(2,1)}, bf16[6,192,384]{2,1,0:T(8,128)(2,1)S(1)}, u32[]{:S(2)}, u32[]{:S(2)}) collective-permute-start(bf16[6,192,384]{2,1,0:T(8,128)(2,1)} %get-tuple-element.411), channel_id=1, source_target_pairs={{0,1},{1,0},{2,3},{3,2},{4,5},{5,4},{6,7},{7,6},{8,9},{9,8},{10,11... | collective-permute-start | bytes 2654216 | tf_op jit(solution)/shard_map/ppermute | solution.py:1034
  502.7 40.9 %collective-permute-start.58 = (bf16[4,2,2,192,384]{4,3,2,1,0:T(8,128)(2,1)}, bf16[4,2,2,192,384]{4,3,2,1,0:T(8,128)(2,1)}, u32[]{:S(2)}, u32[]{:S(2)}) collective-permute-start(bf16[4,2,2,192,384]{4,3,2,1,0:T(8,128)(2,1)} %get-tuple-element.428), channel_id=1, source_target_pairs={{0,8},{8,0},{16,24},{24,16},{1,9},{9,1},{17,25},{25,17},{2,10},{10... | collective-permute-start | bytes 7077896 | tf_op jit(solution)/shard_map/ppermute | solution.py:1034
  502.8 40.8 %collective-permute-start.59 = (bf16[4,2,2,192,384]{4,3,2,1,0:T(8,128)(2,1)}, bf16[4,2,2,192,384]{4,3,2,1,0:T(8,128)(2,1)}, u32[]{:S(2)}, u32[]{:S(2)}) collective-permute-start(bf16[4,2,2,192,384]{4,3,2,1,0:T(8,128)(2,1)} %get-tuple-element.430), channel_id=1, source_target_pairs={{0,8},{8,0},{16,24},{24,16},{1,9},{9,1},{17,25},{25,17},{2,10},{10... | collective-permute-start | bytes 7077896 | tf_op jit(solution)/shard_map/ppermute | solution.py:1034
  508.7 131.5 %reduce-scatter.11.cloned.1.call-start = ((), (), s32[]{:S(2)}) async-start(), calls=%async_computation.13 | async-start | bytes 1474560 | tf_op jit(solution)/shard_map/reduce_scatter | solution.py:1063
  530.5 28.9 %collective-permute-start.65 = (bf16[4,2,2,192,384]{4,3,2,1,0:T(8,128)(2,1)}, bf16[4,2,2,192,384]{4,3,2,1,0:T(8,128)(2,1)S(1)}, u32[]{:S(2)}, u32[]{:S(2)}) collective-permute-start(bf16[4,2,2,192,384]{4,3,2,1,0:T(8,128)(2,1)} %get-tuple-element.444), channel_id=1, source_target_pairs={{0,8},{8,0},{16,24},{24,16},{1,9},{9,1},{17,25},{25,17},{2,10},{10... | collective-permute-start | bytes 7077896 | tf_op jit(solution)/shard_map/ppermute | solution.py:1034
  530.6 150.4 %reduce-scatter.5.cloned.1.call-start = ((), (), s32[]{:S(2)}) async-start(), calls=%async_computation.10 | async-start | bytes 921600 | tf_op jit(solution)/shard_map/reduce_scatter | solution.py:1063
  586.0 120.2 %reduce-scatter.9.cloned.1.call-start = ((), (), s32[]{:S(2)}) async-start(), calls=%async_computation.12 | async-start | bytes 1474560 | tf_op jit(solution)/shard_map/reduce_scatter | solution.py:1063
  621.4 49.6 %collective-permute-start.77 = (bf16[8,192,384]{2,1,0:T(8,128)(2,1)}, bf16[8,192,384]{2,1,0:T(8,128)(2,1)S(1)}, u32[]{:S(2)}, u32[]{:S(2)}) collective-permute-start(bf16[8,192,384]{2,1,0:T(8,128)(2,1)} %get-tuple-element.492), channel_id=1, source_target_pairs={{0,16},{8,24},{16,0},{24,8},{1,17},{9,25},{17,1},{25,9},{2,18},{10... | collective-permute-start | bytes 3538952 | tf_op jit(solution)/shard_map/ppermute | solution.py:1034
  622.5 48.5 %collective-permute-start.76 = (bf16[6,192,384]{2,1,0:T(8,128)(2,1)}, bf16[6,192,384]{2,1,0:T(8,128)(2,1)S(1)}, u32[]{:S(2)}, u32[]{:S(2)}) collective-permute-start(bf16[6,192,384]{2,1,0:T(8,128)(2,1)} %get-tuple-element.491), channel_id=1, source_target_pairs={{0,1},{1,0},{2,3},{3,2},{4,5},{5,4},{6,7},{7,6},{8,9},{9,8},{10,11... | collective-permute-start | bytes 2654216 | tf_op jit(solution)/shard_map/ppermute | solution.py:1034
  631.5 45.7 %collective-permute-start.75 = (bf16[1,2,196,768]{3,1,2,0:T(2,128)(2,1)}, bf16[1,2,196,768]{3,1,2,0:T(2,128)(2,1)S(1)}, u32[]{:S(2)}, u32[]{:S(2)}) collective-permute-start(bf16[1,2,196,768]{3,1,2,0:T(2,128)(2,1)} %bitcast.189), channel_id=1, source_target_pairs={{0,0},{8,2},{2,4},{10,6},{4,8},{12,10},{6,12},{14,14},{16,16},{24,... | collective-permute-start | bytes 1806344 | tf_op jit(solution)/shard_map/ppermute | solution.py:777
  636.0 33.5 %all-to-all-start.1 = ((f32[32,1,384]{2,1,0:T(1,128)}), f32[32,1,384]{2,1,0:T(1,128)}, u32[]{:S(2)}, u32[]{:S(2)}) async-start(f32[32,1,384]{2,1,0:T(1,128)} %copy.125), calls=%async_computation.1 | async-start | bytes 98304 | tf_op jit(solution)/shard_map/all_to_all | solution.py:1122
  (138 other events, 1572.8 us)
Sparse Core Ops, SparseCore 0:
  11.7 144.2 all-gather.2
  159.6 122.0 all-gather.4
  508.9 19.8 reduce-scatter.6
  530.9 27.5 reduce-scatter.10
  586.1 21.4 reduce-scatter.4
  633.4 34.9 reduce-scatter.8

commit v16 on v15

--- a/solution.py
+++ b/solution.py
@@ -169,6 +169,21 @@
     send_ref[at] = room_ref[:, 1 - mine].astype(BF16)
 
 
+def store_by_core(ref, value, halves):
+    n = halves.rows
+    for core in range(2):
+        for pair in range(halves.pairs):
+            first = (2 * pair + core) * n
+            ref[core, pair * n : (pair + 1) * n] = value[first : first + n]
+
+
+def split_product(left_ref, right, keep_ref, send_ref, at, me_ref):
+    mine = me_ref[0]
+    shape = keep_ref.shape[len(at) :]
+    keep_ref[at] = nn(left_ref[mine], right).reshape(shape).astype(BF16)
+    send_ref[at] = nn(left_ref[1 - mine], right).reshape(shape).astype(BF16)
+
+
 class Halves:
     def __init__(self, clips, depth, width):
         self.pairs = clips // 2
@@ -179,6 +194,9 @@
         tail = (self.pairs, self.rows, self.width)
         one = lambda: made(lead + tail, BF16, block + tail, lambda *g: index(*g) + (0, 0, 0))
         return [one(), one()]
+
+    def turned(self, columns):
+        return pltpu.VMEM((2, self.pairs * self.rows, columns), BF16)
 
     def room(self):
         return pltpu.VMEM((self.pairs, 2, self.rows, self.width), F32)
@@ -432,7 +450,7 @@
     def body(me_ref, g_ref, x2_ref, wi_ref, wo_ref, gb_ref, go_ref, ki_ref, si_ref, ko_ref, so_ref, sums_ref, *rest):
         if with_output:
             x3_ref, *rest = rest
-        a3_ref, a3t_ref, e3_ref, e3t_ref, u_ref, room_ref = rest
+        a3_ref, a3t_ref, e3_ref, e3t_ref, u_ref = rest
         j = pl.program_id(0)
 
         @pl.when(j == 0)
@@ -440,10 +458,10 @@
             hat, _ = norm_parts(x2_ref[...])
             a3 = hat * gb_ref[2:3] + gb_ref[5:6]
             a3_ref[...] = a3.astype(BF16)
-            a3t_ref[...] = a3.T.astype(BF16)
+            store_by_core(a3t_ref, a3.T.astype(BF16), halves)
             g = g_ref[...]
             e3_ref[...] = g.astype(BF16)
-            e3t_ref[...] = g.T.astype(BF16)
+            store_by_core(e3t_ref, g.T.astype(BF16), halves)
             u_ref[...] = jnp.zeros((t, d), F32)
             if with_output:
                 x3_ref[...] = x2_ref[...]
@@ -453,8 +471,8 @@
         act = (hid * phi).astype(BF16)
         slope = phi + hid * jnp.exp(-0.5 * hid * hid) * INV_ROOT_TAU
         dhid = (nn(e3_ref[...], wo_ref[0, 0]) * slope).astype(BF16)
-        split_rows(nn(e3t_ref[...], act), ko_ref, so_ref, (0, 0), room_ref, me_ref)
-        split_rows(nn(a3t_ref[...], dhid), ki_ref, si_ref, (0, 0), room_ref, me_ref)
+        split_product(e3t_ref, act, ko_ref, so_ref, (0, 0), me_ref)
+        split_product(a3t_ref, dhid, ki_ref, si_ref, (0, 0), me_ref)
         u_ref[...] += nt(dhid, wi_ref[0, 0])
         if with_output:
             x3_ref[...] += nt(act, wo_ref[0, 0])
@@ -486,11 +504,10 @@
         [made((t, d), F32), *slab_outs, made((2, d), F32)] + [made((t, d), F32)] * with_output,
         [
             pltpu.VMEM((t, d), BF16),
-            pltpu.VMEM((d, t), BF16),
+            halves.turned(t),
             pltpu.VMEM((t, d), BF16),
-            pltpu.VMEM((d, t), BF16),
+            halves.turned(t),
             pltpu.VMEM((t, d), F32),
-            halves.room(),
         ],
         (me, grad, x2, w, w, gb),
         flops=10 * t * d * width * steps,
@@ -507,20 +524,20 @@
     rate = LOG2E * scale
     n = rows.frame_rows
 
-    def body(me_ref, g_ref, x1_ref, qkv_ref, o2_ref, log_ref, wo_ref, wq_ref, gb_ref, go_ref, keep_ref, send_ref, sums_ref, e2_ref, e2t_ref, a2t_ref, do_ref, dqkv_ref, u_ref, room_ref):
+    def body(me_ref, g_ref, x1_ref, qkv_ref, o2_ref, log_ref, wo_ref, wq_ref, gb_ref, go_ref, keep_ref, send_ref, sums_ref, e2_ref, e2t_ref, a2t_ref, do_ref, dqkv_ref, u_ref):
         h = pl.program_id(0)
 
         @pl.when(h == 0)
         def _():
             g = g_ref[...]
             e2_ref[...] = g.astype(BF16)
-            e2t_ref[...] = g.T.astype(BF16)
+            store_by_core(e2t_ref, g.T.astype(BF16), halves)
             hat, _ = norm_parts(x1_ref[...])
-            a2t_ref[...] = (hat * gb_ref[1:2] + gb_ref[4:5]).T.astype(BF16)
+            store_by_core(a2t_ref, (hat * gb_ref[1:2] + gb_ref[4:5]).T.astype(BF16), halves)
             u_ref[...] = jnp.zeros((t, d), F32)
 
         bias = rows.space_bias()
-        split_rows(nn(e2t_ref[...], o2_ref[...]), keep_ref, send_ref, (0, 0), room_ref, me_ref)
+        split_product(e2t_ref, o2_ref[...], keep_ref, send_ref, (0, 0), me_ref)
         do_ref[...] = nn(e2_ref[...], wo_ref[0, 0]).astype(BF16)
 
         @pl.loop(0, pairs)
@@ -543,9 +560,7 @@
                     dqkv_ref[part, at, lanes] = grads[part]
 
         for part in range(3):
-            split_rows(
-                nn(a2t_ref[...], dqkv_ref[part]), keep_ref, send_ref, (part + 1, 0), room_ref, me_ref
-            )
+            split_product(a2t_ref, dqkv_ref[part], keep_ref, send_ref, (part + 1, 0), me_ref)
             u_ref[...] += nt(dqkv_ref[part], wq_ref[part, 0])
 
         @pl.when(h == shares - 1)
@@ -575,12 +590,11 @@
         ],
         [
             pltpu.VMEM((t, d), BF16),
-            pltpu.VMEM((d, t), BF16),
-            pltpu.VMEM((d, t), BF16),
+            halves.turned(t),
+            halves.turned(t),
             pltpu.VMEM((t, width), BF16),
             pltpu.VMEM((3, t, width), BF16),
             pltpu.VMEM((t, d), F32),
-            halves.room(),
         ],
         (me, grad, x1, qkv, o2, logs, w, w, gb),
         flops=2 * t * d * d * 8,
@@ -669,13 +683,13 @@
         a_ref, qkv_ref, log_ref, w_ref = refs[:4]
         out_refs, refs = refs[4 : 4 + rows.ways], refs[4 + rows.ways :]
         half_refs, refs = refs[:6], refs[6:]
-        bias_ref, dqkv_ref, at_ref, u_ref, room_ref, do_ref = refs
+        bias_ref, dqkv_ref, at_ref, u_ref, do_ref = refs
         h = pl.program_id(0)
 
         @pl.when(h == 0)
         def _():
             bias_ref[...] = rows.time_bias()
-            at_ref[...] = a_ref[...].T
+            store_by_core(at_ref, a_ref[...].T, halves)
             u_ref[...] = jnp.zeros((t, d), F32)
 
         for k in range(rows.ways):
@@ -699,8 +713,9 @@
                 dqkv_ref[part, :, lanes] = grads[part]
 
         for part in range(3):
-            value = nn(at_ref[...], dqkv_ref[part])
-            split_rows(value, half_refs[2 * part], half_refs[2 * part + 1], (0, 0), room_ref, me_ref)
+            split_product(
+                at_ref, dqkv_ref[part], half_refs[2 * part], half_refs[2 * part + 1], (0, 0), me_ref
+            )
             u_ref[...] += nt(dqkv_ref[part], w_ref[part, 0])
 
         @pl.when(h == shares - 1)
@@ -726,9 +741,8 @@
         [
             pltpu.VMEM((t, t), F32),
             pltpu.VMEM((3, t, width), BF16),
-            pltpu.VMEM((d, t), BF16),
+            halves.turned(t),
             pltpu.VMEM((t, d), F32),
-            halves.room(),
             pltpu.VMEM((t, width), BF16),
         ],
         (me, *do1, a, qkv, logs, w),

time: 738 us -> 737 us (level)
  no operation moved by 1% of the time
where the time goes in v16:
time: 737 us; the launch traced here: 732 us
  Pallas kernels  293 us (40%)
  waiting for transfers between devices  240 us (33%)
  starting transfers between devices  126 us (17%)
  local copies, waits for them, and re-layouts  38.9 us (5%)
  other arithmetic  17.8 us (2%)
  between operations  16 us (2%)
    pallas_call x18, Pallas kernels, call(): pl.pallas_call(body, out_shape=[shape for shape, _ in outs], grid=grid, i...  231 us
    ppermute x46, waiting for transfers between devices, cross(): return lax.ppermute(a, axis, [(i, i ^ 1 << bit) for i in range(size)])  72.7 us
    ppermute x24, waiting for transfers between devices, swap_places(): got.append(lax.ppermute(chunks[k], ('clip', 'seq'), pairs))  60 us
    ppermute x24, starting transfers between devices, swap_places(): got.append(lax.ppermute(chunks[k], ('clip', 'seq'), pairs))  47.3 us
    pallas_call x9, Pallas kernels, fold(): pl.pallas_call(body, out_shape=[jax.ShapeDtypeStruct(shape, BF16) for sha...  45.4 us
    ppermute x46, starting transfers between devices, cross(): return lax.ppermute(a, axis, [(i, i ^ 1 << bit) for i in range(size)])  39.2 us
    ppermute x6, waiting for transfers between devices, spread_steps(): lax.ppermute(pack, 'seq', [(i, (i + k) % ways) for i in range(ways)])  37.2 us
    all_to_all x1, waiting for transfers between devices, reduce_norms(): every = lax.all_to_all(a, ALL, split_axis=0, concat_axis=0, tiled=True)  28.3 us
  transfers between devices with their start and end apart: 90, of which 30 were waited for; matrix products, arithmetic and copies ran while one was open for 5% of the time, Pallas kernels for 33%

profile of v16, /device:TPU:0, one launch (start us, length us, event | category | flops | bytes accessed | tf_op | source)
XLA Modules:
  0.0 732.0 jit_solution(3444341968378106067)
XLA Ops:
  33.3 8.0 %collective-permute-start.2 = (bf16[104,768]{1,0:T(8,128)(2,1)}, bf16[104,768]{1,0:T(8,128)(2,1)S(1)}, u32[]{:S(2)}, u32[]{:S(2)}) collective-permute-start(bf16[104,768]{1,0:T(8,128)(2,1)} %get-tuple-element.261), channel_id=1, source_target_pairs={{0,8},{2,10},{4,12},{6,14},{8,0},{10,2},{12,4},{14,6},{16,24},{18,... | collective-permute-start | bytes 479240 | tf_op jit(solution)/shard_map/ppermute | solution.py:809
  44.4 8.8 %collective-permute-start.6 = (bf16[8,48,384]{2,1,0:T(8,128)(2,1)S(1)}, bf16[8,48,384]{2,1,0:T(8,128)(2,1)S(1)}, u32[]{:S(2)}, u32[]{:S(2)}) collective-permute-start(bf16[8,48,384]{2,1,0:T(8,128)(2,1)S(1)} %pad_maximum_fusion.12), channel_id=1, source_target_pairs={{0,4},{2,6},{4,0},{6,2},{1,5},{3,7},{5,1},{7,3},{8,12},{10,14},{12... | collective-permute-start | bytes 884744 | tf_op jit(solution)/shard_map/ppermute | solution.py:848
  54.5 27.6 %collective-permute-done.3.refs_2_ = bf16[104,768]{1,0:T(8,128)(2,1)S(1)} collective-permute-done((bf16[104,768]{1,0:T(8,128)(2,1)}, bf16[104,768]{1,0:T(8,128)(2,1)S(1)}, u32[]{:S(2)}, u32[]{:S(2)}) %collective-permute-start.3) | collective-permute-done | bytes 159776 | tf_op jit(solution)/shard_map/ppermute | solution.py:809
  93.3 25.4 %collective-permute-done.9 = bf16[2,8,48,384]{3,2,1,0:T(8,128)(2,1)S(1)} collective-permute-done((bf16[2,8,48,384]{3,2,1,0:T(8,128)(2,1)S(1)}, bf16[2,8,48,384]{3,2,1,0:T(8,128)(2,1)S(1)}, u32[]{:S(2)}, u32[]{:S(2)}) %collective-permute-start.9) | collective-permute-done | bytes 589856 | tf_op jit(solution)/shard_map/ppermute | solution.py:1048
  126.6 13.1 %collective-permute-done.12 = bf16[8,48,384]{2,1,0:T(8,128)(2,1)S(1)} collective-permute-done((bf16[8,48,384]{2,1,0:T(8,128)(2,1)S(1)}, bf16[8,48,384]{2,1,0:T(8,128)(2,1)S(1)}, u32[]{:S(2)}, u32[]{:S(2)}) %collective-permute-start.12) | collective-permute-done | bytes 294944 | tf_op jit(solution)/shard_map/ppermute | solution.py:848
  139.6 19.2 %collective-permute-done.11 = bf16[8,48,384]{2,1,0:T(8,128)(2,1)S(1)} collective-permute-done((bf16[8,48,384]{2,1,0:T(8,128)(2,1)S(1)}, bf16[8,48,384]{2,1,0:T(8,128)(2,1)S(1)}, u32[]{:S(2)}, u32[]{:S(2)}) %collective-permute-start.11) | collective-permute-done | bytes 294944 | tf_op jit(solution)/shard_map/ppermute | solution.py:848
  159.5 12.4 %shard_map.195 = (bf16[416,768]{1,0:T(8,128)(2,1)}, bf16[3,416,768]{2,1,0:T(8,128)(2,1)}, f32[2,3,2,416]{3,2,1,0:T(2,128)}, bf16[104,768]{1,0:T(8,128)(2,1)}, bf...) custom-call(bf16[104,768]{1,0:T(8,128)(2,1)} %get-tuple-element.288.refs_0_, ...), custom_call_target="tpu_custom_call" | custom-call | flops 1472200704 | bytes 14470656 | tf_op jit(solution)/shard_map/pallas_call | solution.py:212
  173.9 7.6 %collective-permute-done.16.refs_2_ = bf16[104,768]{1,0:T(8,128)(2,1)S(1)} collective-permute-done((bf16[104,768]{1,0:T(8,128)(2,1)}, bf16[104,768]{1,0:T(8,128)(2,1)S(1)}, u32[]{:S(2)}, u32[]{:S(2)}) %collective-permute-start.16) | collective-permute-done | bytes 159776 | tf_op jit(solution)/shard_map/ppermute | solution.py:809
  191.6 9.3 %shard_map.196 = (bf16[416,768]{1,0:T(8,128)(2,1)}, bf16[416,768]{1,0:T(8,128)(2,1)}, f32[416,768]{1,0:T(8,128)}, bf16[3,416,768]{2,1,0:T(8,128)(2,1)}) custom-call(s32[5]{0:T(128)} %stack.110.me_ref, bf16[104,768]{1,0:T(8,128)(2,1)} %get-tuple-element.306.refs_0_, bf16[104,768]{1,0:T(8,128)(2,1)} %copy-done.45, bf16[104,768]{1,0:T(8,128)(2,1)} %copy-done.46, ...), custom_call_target="tpu_custom_call" | custom-call | flops 2453667840 | bytes 28821524 | tf_op jit(solution)/shard_map/pallas_call | solution.py:212
  200.9 9.9 %shard_map.197 = (bf16[416,768]{1,0:T(8,128)(2,1)}, f32[416,768]{1,0:T(8,128)}, f32[2,3,2,2,208]{4,3,2,1,0:T(2,128)}) custom-call(bf16[3,416,768]{2,1,0:T(8,128)(2,1)} %get-tuple-element.310.qkv_ref, f32[416,768]{1,0:T(8,128)} %get-tuple-element.311.x1_ref, bf16[9,2,768,384]{3,2,1,0:T(8,128)(2,1)} %bitcast.201), custom_call_target="tpu_custom_call" | custom-call | flops 490733568 | bytes 15748608 | tf_op jit(solution)/shard_map/pallas_call | solution.py:212
  213.6 8.9 %shard_map.198 = bf16[8,2,16,48,384]{4,3,2,1,0:T(8,128)(2,1)} custom-call(s32[5]{0:T(128)} %stack.110.me_ref, bf16[4,8,48,384]{3,2,1,0:T(8,128)(2,1)} %copy-done.21, bf16[4,8,48,384]{3,2,1,0:T(8,128)(2,1)} %collective-permute-done.13.refs_1_, bf16[4,8,48,384]{3,2,1,0:T(8,128)(2,1)} %copy-done.22, bf16[4,8,48,384]{3,2,1,0:T(8,128)(2,1)} %collective-permute-done.14.refs_3_, ...), custom_call_target="tpu_custom_call" | custom-call | bytes 18874368 | tf_op jit(solution)/shard_map/pallas_call | solution.py:883
  222.5 13.3 %shard_map.199 = (f32[416,768]{1,0:T(8,128)}, bf16[104,768]{1,0:T(8,128)(2,1)}, bf16[104,768]{1,0:T(8,128)(2,1)}, bf16[104,768]{1,0:T(8,128)(2,1)}, bf16[104,768]{1,0:T(8,128)(2,1)}) custom-call(f32[416,768]{1,0:T(8,128)} %get-tuple-element.317.x2_ref, bf16[8,2,768,384]{3,2,1,0:T(8,128)(2,1)} %bitcast.214, bf16[8,2,768,384]{3,2,1,0:T(8,128)(2,1)} %bitcast.215, ...), custom_call_target="tpu_custom_call" | custom-call | flops 3925868544 | bytes 22106132 | tf_op jit(solution)/shard_map/pallas_call | solution.py:212
  242.6 8.0 %collective-permute-done.26.refs_3_ = bf16[104,768]{1,0:T(8,128)(2,1)S(1)} collective-permute-done((bf16[104,768]{1,0:T(8,128)(2,1)}, bf16[104,768]{1,0:T(8,128)(2,1)S(1)}, u32[]{:S(2)}, u32[]{:S(2)}) %collective-permute-start.26) | collective-permute-done | bytes 159776 | tf_op jit(solution)/shard_map/ppermute | solution.py:809
  259.0 22.6 %all-gather.5.cloned.1.call-done = bf16[9,1536,384]{2,1,0:T(8,128)(2,1)} async-done(((bf16[9,48,384]{2,1,0:T(8,128)(2,1)}), bf16[9,1536,384]{2,1,0:T(8,128)(2,1)}) %all-gather.5.cloned.1.call-update) | async-done | bytes 10616848 | tf_op jit(solution)/shard_map/all_gather | solution.py:838
  281.6 12.4 %shard_map.200 = (bf16[416,768]{1,0:T(8,128)(2,1)}, bf16[3,416,768]{2,1,0:T(8,128)(2,1)}, f32[2,3,2,416]{3,2,1,0:T(2,128)}, bf16[104,768]{1,0:T(8,128)(2,1)}, bf...) custom-call(bf16[104,768]{1,0:T(8,128)(2,1)} %get-tuple-element.329.refs_0_, ...), custom_call_target="tpu_custom_call" | custom-call | flops 1472200704 | bytes 14470656 | tf_op jit(solution)/shard_map/pallas_call | solution.py:212
  305.9 9.4 %shard_map.201 = (bf16[416,768]{1,0:T(8,128)(2,1)}, bf16[416,768]{1,0:T(8,128)(2,1)}, f32[416,768]{1,0:T(8,128)}, bf16[3,416,768]{2,1,0:T(8,128)(2,1)}) custom-call(s32[5]{0:T(128)} %stack.110.me_ref, bf16[104,768]{1,0:T(8,128)(2,1)} %get-tuple-element.339.refs_0_, bf16[104,768]{1,0:T(8,128)(2,1)} %copy-done.47, bf16[104,768]{1,0:T(8,128)(2,1)} %copy-done.49, ...), custom_call_target="tpu_custom_call" | custom-call | flops 2453667840 | bytes 28821524 | tf_op jit(solution)/shard_map/pallas_call | solution.py:212
  315.3 9.9 %shard_map.202 = (bf16[416,768]{1,0:T(8,128)(2,1)}, f32[416,768]{1,0:T(8,128)}, f32[2,3,2,2,208]{4,3,2,1,0:T(2,128)}) custom-call(bf16[3,416,768]{2,1,0:T(8,128)(2,1)} %get-tuple-element.344.qkv_ref, f32[416,768]{1,0:T(8,128)} %get-tuple-element.345.x1_ref, bf16[9,2,768,384]{3,2,1,0:T(8,128)(2,1)} %bitcast.209), custom_call_target="tpu_custom_call" | custom-call | flops 490733568 | bytes 15748608 | tf_op jit(solution)/shard_map/pallas_call | solution.py:212
  325.2 8.2 %shard_map.203 = bf16[8,2,16,48,384]{4,3,2,1,0:T(8,128)(2,1)} custom-call(s32[5]{0:T(128)} %stack.110.me_ref, bf16[4,8,48,384]{3,2,1,0:T(8,128)(2,1)} %copy-done.23, bf16[4,8,48,384]{3,2,1,0:T(8,128)(2,1)} %collective-permute-done.27.refs_1_, bf16[4,8,48,384]{3,2,1,0:T(8,128)(2,1)} %copy-done.24, bf16[4,8,48,384]{3,2,1,0:T(8,128)(2,1)} %collective-permute-done.28.refs_3_, ...), custom_call_target="tpu_custom_call" | custom-call | bytes 18874368 | tf_op jit(solution)/shard_map/pallas_call | solution.py:883
  333.4 25.3 %shard_map.204 = (f32[416,768]{1,0:T(8,128)}, bf16[4,2,2,192,384]{4,3,2,1,0:T(8,128)(2,1)}, bf16[4,2,2,192,384]{4,3,2,1,0:T(8,128)(2,1)}, bf16[4,2,2,192,384]{4,...) custom-call(s32[5]{0:T(128)} %stack.110.me_ref, ...), custom_call_target="tpu_custom_call" | custom-call | flops 9814671360 | bytes 33447956 | tf_op jit(solution)/shard_map/pallas_call | solution.py:212
  359.3 21.5 %shard_map.205 = (f32[416,768]{1,0:T(8,128)}, bf16[4,2,2,192,384]{4,3,2,1,0:T(8,128)(2,1)}, bf16[4,2,2,192,384]{4,3,2,1,0:T(8,128)(2,1)}, f32[2,768]{1,0:T(2,128)}) custom-call(s32[5]{0:T(128)} %stack.110.me_ref, f32[416,768]{1,0:T(8,128)} %get-tuple-element.351.g_ref, f32[416,768]{1,0:T(8,128)} %get-tuple-element.345.x1_ref, ...), custom_call_target="tpu_custom_call" | custom-call | flops 3925868544 | bytes 32386580 | tf_op jit(solution)/shard_map/pallas_call | solution.py:212
  392.4 7.8 %shard_map.207 = (bf16[104,768]{1,0:T(8,128)(2,1)}, bf16[104,768]{1,0:T(8,128)(2,1)}, bf16[104,768]{1,0:T(8,128)(2,1)}, bf16[104,768]{1,0:T(8,128)(2,1)}, bf16[2...) custom-call(s32[5]{0:T(128)} %stack.110.me_ref, f32[416,768]{1,0:T(8,128)} %get-tuple-element.362.g_ref.refs_5_, ...), custom_call_target="tpu_custom_call" | custom-call | flops 1962934272 | bytes 17350676 | tf_op jit(solution)/shard_map/pallas_call | solution.py:212
  400.1 10.3 %collective-permute-start.39 = (bf16[104,768]{1,0:T(8,128)(2,1)}, bf16[104,768]{1,0:T(8,128)(2,1)S(1)}, u32[]{:S(2)}, u32[]{:S(2)}) collective-permute-start(bf16[104,768]{1,0:T(8,128)(2,1)} %get-tuple-element.366), channel_id=1, source_target_pairs={{0,8},{2,10},{4,12},{6,14},{8,0},{10,2},{12,4},{14,6},{16,24},{18,... | collective-permute-start | bytes 479240 | tf_op jit(solution)/shard_map/ppermute | solution.py:809
  428.1 18.1 %shard_map.209 = (bf16[104,768]{1,0:T(8,128)(2,1)}, bf16[104,768]{1,0:T(8,128)(2,1)}, bf16[104,768]{1,0:T(8,128)(2,1)}, bf16[104,768]{1,0:T(8,128)(2,1)}, bf16[1...) custom-call(s32[5]{0:T(128)} %stack.110.me_ref, ...), custom_call_target="tpu_custom_call" | custom-call | flops 2944401408 | bytes 18009620 | tf_op jit(solution)/shard_map/pallas_call | solution.py:212
  449.7 15.3 %collective-permute-start.48 = (bf16[104,768]{1,0:T(8,128)(2,1)}, bf16[104,768]{1,0:T(8,128)(2,1)S(1)}, u32[]{:S(2)}, u32[]{:S(2)}) collective-permute-start(bf16[104,768]{1,0:T(8,128)(2,1)} %get-tuple-element.390), channel_id=1, source_target_pairs={{0,2},{2,0},{4,6},{6,4},{8,10},{10,8},{12,14},{14,12},{16,18},{18,... | collective-permute-start | bytes 479240 | tf_op jit(solution)/shard_map/ppermute | solution.py:809
  479.6 22.3 %shard_map.212 = (f32[416,768]{1,0:T(8,128)}, bf16[4,2,2,192,384]{4,3,2,1,0:T(8,128)(2,1)}, bf16[4,2,2,192,384]{4,3,2,1,0:T(8,128)(2,1)}, bf16[4,2,2,192,384]{4,...) custom-call(s32[5]{0:T(128)} %stack.110.me_ref, f32[416,768]{1,0:T(8,128)} %get-tuple-element.409.g_ref, ...), custom_call_target="tpu_custom_call" | custom-call | flops 9814671360 | bytes 32170004 | tf_op jit(solution)/shard_map/pallas_call | solution.py:212
  508.0 21.5 %shard_map.214 = (f32[416,768]{1,0:T(8,128)}, bf16[4,2,2,192,384]{4,3,2,1,0:T(8,128)(2,1)}, bf16[4,2,2,192,384]{4,3,2,1,0:T(8,128)(2,1)}, f32[2,768]{1,0:T(2,128)}) custom-call(s32[5]{0:T(128)} %stack.110.me_ref, f32[416,768]{1,0:T(8,128)} %get-tuple-element.419.g_ref, f32[416,768]{1,0:T(8,128)} %get-tuple-element.311.x1_ref, ...), custom_call_target="tpu_custom_call" | custom-call | flops 3925868544 | bytes 32386580 | tf_op jit(solution)/shard_map/pallas_call | solution.py:212
  532.2 7.9 %collective-permute-done.57.refs_17_ = bf16[2,192,384]{2,1,0:T(8,128)(2,1)S(1)} collective-permute-done((bf16[2,192,384]{2,1,0:T(8,128)(2,1)S(1)}, bf16[2,192,384]{2,1,0:T(8,128)(2,1)S(1)}, u32[]{:S(2)}, u32[]{:S(2)}) %collective-permute-start.57) | collective-permute-done | bytes 294944 | tf_op jit(solution)/shard_map/ppermute | solution.py:1048
  549.3 7.8 %shard_map.216 = (bf16[104,768]{1,0:T(8,128)(2,1)}, bf16[104,768]{1,0:T(8,128)(2,1)}, bf16[104,768]{1,0:T(8,128)(2,1)}, bf16[104,768]{1,0:T(8,128)(2,1)}, bf16[2...) custom-call(s32[5]{0:T(128)} %stack.110.me_ref, f32[416,768]{1,0:T(8,128)} %get-tuple-element.434.g_ref.refs_5_, ...), custom_call_target="tpu_custom_call" | custom-call | flops 1962934272 | bytes 17350676 | tf_op jit(solution)/shard_map/pallas_call | solution.py:212
  559.0 16.1 %collective-permute-done.63.refs_2_ = bf16[8,192,384]{2,1,0:T(8,128)(2,1)S(1)} collective-permute-done((bf16[8,192,384]{2,1,0:T(8,128)(2,1)}, bf16[8,192,384]{2,1,0:T(8,128)(2,1)S(1)}, u32[]{:S(2)}, u32[]{:S(2)}) %collective-permute-start.63) | collective-permute-done | bytes 1179680 | tf_op jit(solution)/shard_map/ppermute | solution.py:1048
  585.1 18.3 %shard_map.218 = (bf16[104,768]{1,0:T(8,128)(2,1)}, bf16[104,768]{1,0:T(8,128)(2,1)}, bf16[104,768]{1,0:T(8,128)(2,1)}, bf16[104,768]{1,0:T(8,128)(2,1)}, bf16[1...) custom-call(s32[5]{0:T(128)} %stack.110.me_ref, ...), custom_call_target="tpu_custom_call" | custom-call | flops 2944401408 | bytes 18009620 | tf_op jit(solution)/shard_map/pallas_call | solution.py:212
  640.3 28.3 %all-to-all-done.1 = f32[32,1,384]{2,1,0:T(1,128)} async-done(((f32[32,1,384]{2,1,0:T(1,128)}), f32[32,1,384]{2,1,0:T(1,128)}, u32[]{:S(2)}, u32[]{:S(2)}) %all-to-all-start.1) | async-done | bytes 49184 | tf_op jit(solution)/shard_map/all_to_all | solution.py:1136
  708.4 13.3 %all-to-all-done.2 = bf16[4,5,48,384]{3,2,1,0:T(8,128)(2,1)S(1)} async-done(((bf16[4,5,48,384]{3,2,1,0:T(8,128)(2,1)}), bf16[4,5,48,384]{3,2,1,0:T(8,128)(2,1)S(1)}, u32[]{:S(2)}, u32[]{:S(2)}) %all-to-all-start.2) | async-done | bytes 737312 | tf_op jit(solution)/shard_map/all_to_all | solution.py:1074
  (454 shorter events, 248.0 us)
Async XLA Ops:
  7.2 152.3 %all-gather.3.cloned.1.call-start = ((), (), s32[]{:S(2)}) async-start(), calls=%async_computation.8 | async-start | bytes 10948608 | tf_op jit(solution)/shard_map/all_gather | solution.py:838
  11.0 270.6 %all-gather.5.cloned.1.call-start = ((), (), s32[]{:S(2)}) async-start(), calls=%async_computation.9 | async-start | bytes 10948608 | tf_op jit(solution)/shard_map/all_gather | solution.py:838
  20.0 602.5 %reduce-scatter.7.cloned.1.call-start = ((), (), s32[]{:S(2)}) async-start(), calls=%async_computation.11 | async-start | bytes 737280 | tf_op jit(solution)/shard_map/reduce_scatter | solution.py:1077
  41.3 43.9 %collective-permute-start.7 = (bf16[8,48,384]{2,1,0:T(8,128)(2,1)S(1)}, bf16[8,48,384]{2,1,0:T(8,128)(2,1)S(1)}, u32[]{:S(2)}, u32[]{:S(2)}) collective-permute-start(bf16[8,48,384]{2,1,0:T(8,128)(2,1)S(1)} %pad_maximum_fusion.12), channel_id=1, source_target_pairs={{0,6},{2,0},{4,2},{6,4},{1,7},{3,1},{5,3},{7,5},{8,14},{10,8},{12,... | collective-permute-start | bytes 884744 | tf_op jit(solution)/shard_map/ppermute | solution.py:848
  44.4 45.7 %collective-permute-start.6 = (bf16[8,48,384]{2,1,0:T(8,128)(2,1)S(1)}, bf16[8,48,384]{2,1,0:T(8,128)(2,1)S(1)}, u32[]{:S(2)}, u32[]{:S(2)}) collective-permute-start(bf16[8,48,384]{2,1,0:T(8,128)(2,1)S(1)} %pad_maximum_fusion.12), channel_id=1, source_target_pairs={{0,4},{2,6},{4,0},{6,2},{1,5},{3,7},{5,1},{7,3},{8,12},{10,14},{12... | collective-permute-start | bytes 884744 | tf_op jit(solution)/shard_map/ppermute | solution.py:848
  53.2 36.9 %collective-permute-start.5 = (bf16[8,48,384]{2,1,0:T(8,128)(2,1)S(1)}, bf16[8,48,384]{2,1,0:T(8,128)(2,1)S(1)}, u32[]{:S(2)}, u32[]{:S(2)}) collective-permute-start(bf16[8,48,384]{2,1,0:T(8,128)(2,1)S(1)} %pad_maximum_fusion.12), channel_id=1, source_target_pairs={{0,2},{2,4},{4,6},{6,0},{1,3},{3,5},{5,7},{7,1},{8,10},{10,12},{12... | collective-permute-start | bytes 884744 | tf_op jit(solution)/shard_map/ppermute | solution.py:848
  53.2 28.8 %collective-permute-start.3 = (bf16[104,768]{1,0:T(8,128)(2,1)}, bf16[104,768]{1,0:T(8,128)(2,1)S(1)}, u32[]{:S(2)}, u32[]{:S(2)}) collective-permute-start(bf16[104,768]{1,0:T(8,128)(2,1)} %get-tuple-element.262), channel_id=1, source_target_pairs={{0,2},{2,0},{4,6},{6,4},{8,10},{10,8},{12,14},{14,12},{16,18},{18,... | collective-permute-start | bytes 479240 | tf_op jit(solution)/shard_map/ppermute | solution.py:809
  53.8 31.3 %collective-permute-start.4 = (bf16[104,768]{1,0:T(8,128)(2,1)}, bf16[104,768]{1,0:T(8,128)(2,1)S(1)}, u32[]{:S(2)}, u32[]{:S(2)}) collective-permute-start(bf16[104,768]{1,0:T(8,128)(2,1)} %get-tuple-element.263), channel_id=1, source_target_pairs={{0,10},{2,8},{4,14},{6,12},{8,2},{10,0},{12,6},{14,4},{16,26},{18,... | collective-permute-start | bytes 479240 | tf_op jit(solution)/shard_map/ppermute | solution.py:809
  90.1 28.6 %collective-permute-start.9 = (bf16[2,8,48,384]{3,2,1,0:T(8,128)(2,1)S(1)}, bf16[2,8,48,384]{3,2,1,0:T(8,128)(2,1)S(1)}, u32[]{:S(2)}, u32[]{:S(2)}) collective-permute-start(bf16[2,8,48,384]{3,2,1,0:T(8,128)(2,1)S(1)} %pad_maximum_fusion.5), channel_id=1, source_target_pairs={{0,1},{1,0},{2,3},{3,2},{4,5},{5,4},{6,7},{7,6},{8,9},{9,8},{10,11... | collective-permute-start | bytes 1769480 | tf_op jit(solution)/shard_map/ppermute | solution.py:1048
  120.5 38.3 %collective-permute-start.14 = (bf16[4,8,48,384]{3,2,1,0:T(8,128)(2,1)S(1)}, bf16[4,8,48,384]{3,2,1,0:T(8,128)(2,1)}, u32[]{:S(2)}, u32[]{:S(2)}) collective-permute-start(bf16[4,8,48,384]{3,2,1,0:T(8,128)(2,1)S(1)} %pad_maximum_fusion.1.refs_2_), channel_id=1, source_target_pairs={{0,16},{8,24},{16,0},{24,8},{1,17},{9,25},{17,1},{25,9},{2,18},{10... | collective-permute-start | bytes 3538952 | tf_op jit(solution)/shard_map/ppermute | solution.py:1048
  122.1 36.8 %collective-permute-start.13 = (bf16[4,8,48,384]{3,2,1,0:T(8,128)(2,1)S(1)}, bf16[4,8,48,384]{3,2,1,0:T(8,128)(2,1)}, u32[]{:S(2)}, u32[]{:S(2)}) collective-permute-start(bf16[4,8,48,384]{3,2,1,0:T(8,128)(2,1)S(1)} %pad_maximum_fusion.refs_0_), channel_id=1, source_target_pairs={{0,1},{1,0},{2,3},{3,2},{4,5},{5,4},{6,7},{7,6},{8,9},{9,8},{10,11... | collective-permute-start | bytes 3538952 | tf_op jit(solution)/shard_map/ppermute | solution.py:1048
  123.7 35.1 %collective-permute-start.11 = (bf16[8,48,384]{2,1,0:T(8,128)(2,1)S(1)}, bf16[8,48,384]{2,1,0:T(8,128)(2,1)S(1)}, u32[]{:S(2)}, u32[]{:S(2)}) collective-permute-start(bf16[8,48,384]{2,1,0:T(8,128)(2,1)S(1)} %pad_maximum_fusion.13), channel_id=1, source_target_pairs={{0,4},{2,6},{4,0},{6,2},{1,5},{3,7},{5,1},{7,3},{8,12},{10,14},{12... | collective-permute-start | bytes 884744 | tf_op jit(solution)/shard_map/ppermute | solution.py:848
  124.6 34.2 %collective-permute-start.10 = (bf16[8,48,384]{2,1,0:T(8,128)(2,1)S(1)}, bf16[8,48,384]{2,1,0:T(8,128)(2,1)S(1)}, u32[]{:S(2)}, u32[]{:S(2)}) collective-permute-start(bf16[8,48,384]{2,1,0:T(8,128)(2,1)S(1)} %pad_maximum_fusion.13), channel_id=1, source_target_pairs={{0,2},{2,4},{4,6},{6,0},{1,3},{3,5},{5,7},{7,1},{8,10},{10,12},{12... | collective-permute-start | bytes 884744 | tf_op jit(solution)/shard_map/ppermute | solution.py:848
  139.6 32.8 %collective-permute-start.20 = (bf16[4,8,48,384]{3,2,1,0:T(8,128)(2,1)S(1)}, bf16[4,8,48,384]{3,2,1,0:T(8,128)(2,1)}, u32[]{:S(2)}, u32[]{:S(2)}) collective-permute-start(bf16[4,8,48,384]{3,2,1,0:T(8,128)(2,1)S(1)} %pad_maximum_fusion.1.refs_2_), channel_id=1, source_target_pairs={{0,8},{8,0},{16,24},{24,16},{1,9},{9,1},{17,25},{25,17},{2,10},{10... | collective-permute-start | bytes 3538952 | tf_op jit(solution)/shard_map/ppermute | solution.py:1048
  211.4 45.2 %collective-permute-start.28 = (bf16[4,8,48,384]{3,2,1,0:T(8,128)(2,1)S(1)}, bf16[4,8,48,384]{3,2,1,0:T(8,128)(2,1)}, u32[]{:S(2)}, u32[]{:S(2)}) collective-permute-start(bf16[4,8,48,384]{3,2,1,0:T(8,128)(2,1)S(1)} %pad_maximum_fusion.3.refs_2_), channel_id=1, source_target_pairs={{0,16},{8,24},{16,0},{24,8},{1,17},{9,25},{17,1},{25,9},{2,18},{10... | collective-permute-start | bytes 3538952 | tf_op jit(solution)/shard_map/ppermute | solution.py:1048
  211.9 45.7 %collective-permute-start.27 = (bf16[4,8,48,384]{3,2,1,0:T(8,128)(2,1)S(1)}, bf16[4,8,48,384]{3,2,1,0:T(8,128)(2,1)}, u32[]{:S(2)}, u32[]{:S(2)}) collective-permute-start(bf16[4,8,48,384]{3,2,1,0:T(8,128)(2,1)S(1)} %pad_maximum_fusion.2.refs_0_), channel_id=1, source_target_pairs={{0,1},{1,0},{2,3},{3,2},{4,5},{5,4},{6,7},{7,6},{8,9},{9,8},{10,11... | collective-permute-start | bytes 3538952 | tf_op jit(solution)/shard_map/ppermute | solution.py:1048
  236.1 58.3 %collective-permute-start.34 = (bf16[4,8,48,384]{3,2,1,0:T(8,128)(2,1)S(1)}, bf16[4,8,48,384]{3,2,1,0:T(8,128)(2,1)}, u32[]{:S(2)}, u32[]{:S(2)}) collective-permute-start(bf16[4,8,48,384]{3,2,1,0:T(8,128)(2,1)S(1)} %pad_maximum_fusion.3.refs_2_), channel_id=1, source_target_pairs={{0,8},{8,0},{16,24},{24,16},{1,9},{9,1},{17,25},{25,17},{2,10},{10... | collective-permute-start | bytes 3538952 | tf_op jit(solution)/shard_map/ppermute | solution.py:1048
  237.5 59.7 %collective-permute-start.32 = (bf16[4,8,48,384]{3,2,1,0:T(8,128)(2,1)S(1)}, bf16[4,8,48,384]{3,2,1,0:T(8,128)(2,1)}, u32[]{:S(2)}, u32[]{:S(2)}) collective-permute-start(bf16[4,8,48,384]{3,2,1,0:T(8,128)(2,1)S(1)} %pad_maximum_fusion.2.refs_0_), channel_id=1, source_target_pairs={{0,8},{8,0},{16,24},{24,16},{1,9},{9,1},{17,25},{25,17},{2,10},{10... | collective-permute-start | bytes 3538952 | tf_op jit(solution)/shard_map/ppermute | solution.py:1048
  257.6 47.6 %collective-permute-start.33 = (bf16[4,8,48,384]{3,2,1,0:T(8,128)(2,1)}, bf16[4,8,48,384]{3,2,1,0:T(8,128)(2,1)}, u32[]{:S(2)}, u32[]{:S(2)}) collective-permute-start(bf16[4,8,48,384]{3,2,1,0:T(8,128)(2,1)} %collective-permute-done.27.refs_1_), channel_id=1, source_target_pairs={{0,8},{8,0},{16,24},{24,16},{1,9},{9,1},{17,25},{25,17},{2,10},{10... | collective-permute-start | bytes 3538952 | tf_op jit(solution)/shard_map/ppermute | solution.py:1048
  257.6 47.6 %collective-permute-start.35 = (bf16[4,8,48,384]{3,2,1,0:T(8,128)(2,1)}, bf16[4,8,48,384]{3,2,1,0:T(8,128)(2,1)}, u32[]{:S(2)}, u32[]{:S(2)}) collective-permute-start(bf16[4,8,48,384]{3,2,1,0:T(8,128)(2,1)} %collective-permute-done.28.refs_3_), channel_id=1, source_target_pairs={{0,8},{8,0},{16,24},{24,16},{1,9},{9,1},{17,25},{25,17},{2,10},{10... | collective-permute-start | bytes 3538952 | tf_op jit(solution)/shard_map/ppermute | solution.py:1048
  380.9 29.8 %collective-permute-start.44 = (bf16[4,2,2,192,384]{4,3,2,1,0:T(8,128)(2,1)}, bf16[4,2,2,192,384]{4,3,2,1,0:T(8,128)(2,1)S(1)}, u32[]{:S(2)}, u32[]{:S(2)}) collective-permute-start(bf16[4,2,2,192,384]{4,3,2,1,0:T(8,128)(2,1)} %get-tuple-element.372), channel_id=1, source_target_pairs={{0,8},{8,0},{16,24},{24,16},{1,9},{9,1},{17,25},{25,17},{2,10},{10... | collective-permute-start | bytes 7077896 | tf_op jit(solution)/shard_map/ppermute | solution.py:1048
  472.8 29.7 %collective-permute-start.54 = (bf16[6,192,384]{2,1,0:T(8,128)(2,1)}, bf16[6,192,384]{2,1,0:T(8,128)(2,1)S(1)}, u32[]{:S(2)}, u32[]{:S(2)}) collective-permute-start(bf16[6,192,384]{2,1,0:T(8,128)(2,1)} %get-tuple-element.411), channel_id=1, source_target_pairs={{0,1},{1,0},{2,3},{3,2},{4,5},{5,4},{6,7},{7,6},{8,9},{9,8},{10,11... | collective-permute-start | bytes 2654216 | tf_op jit(solution)/shard_map/ppermute | solution.py:1048
  502.0 40.7 %collective-permute-start.58 = (bf16[4,2,2,192,384]{4,3,2,1,0:T(8,128)(2,1)}, bf16[4,2,2,192,384]{4,3,2,1,0:T(8,128)(2,1)}, u32[]{:S(2)}, u32[]{:S(2)}) collective-permute-start(bf16[4,2,2,192,384]{4,3,2,1,0:T(8,128)(2,1)} %get-tuple-element.428), channel_id=1, source_target_pairs={{0,8},{8,0},{16,24},{24,16},{1,9},{9,1},{17,25},{25,17},{2,10},{10... | collective-permute-start | bytes 7077896 | tf_op jit(solution)/shard_map/ppermute | solution.py:1048
  502.0 40.7 %collective-permute-start.59 = (bf16[4,2,2,192,384]{4,3,2,1,0:T(8,128)(2,1)}, bf16[4,2,2,192,384]{4,3,2,1,0:T(8,128)(2,1)}, u32[]{:S(2)}, u32[]{:S(2)}) collective-permute-start(bf16[4,2,2,192,384]{4,3,2,1,0:T(8,128)(2,1)} %get-tuple-element.430), channel_id=1, source_target_pairs={{0,8},{8,0},{16,24},{24,16},{1,9},{9,1},{17,25},{25,17},{2,10},{10... | collective-permute-start | bytes 7077896 | tf_op jit(solution)/shard_map/ppermute | solution.py:1048
  508.0 131.3 %reduce-scatter.11.cloned.1.call-start = ((), (), s32[]{:S(2)}) async-start(), calls=%async_computation.13 | async-start | bytes 1474560 | tf_op jit(solution)/shard_map/reduce_scatter | solution.py:1077
  529.6 28.9 %collective-permute-start.65 = (bf16[4,2,2,192,384]{4,3,2,1,0:T(8,128)(2,1)}, bf16[4,2,2,192,384]{4,3,2,1,0:T(8,128)(2,1)S(1)}, u32[]{:S(2)}, u32[]{:S(2)}) collective-permute-start(bf16[4,2,2,192,384]{4,3,2,1,0:T(8,128)(2,1)} %get-tuple-element.444), channel_id=1, source_target_pairs={{0,8},{8,0},{16,24},{24,16},{1,9},{9,1},{17,25},{25,17},{2,10},{10... | collective-permute-start | bytes 7077896 | tf_op jit(solution)/shard_map/ppermute | solution.py:1048
  529.7 150.4 %reduce-scatter.5.cloned.1.call-start = ((), (), s32[]{:S(2)}) async-start(), calls=%async_computation.10 | async-start | bytes 921600 | tf_op jit(solution)/shard_map/reduce_scatter | solution.py:1077
  585.0 120.3 %reduce-scatter.9.cloned.1.call-start = ((), (), s32[]{:S(2)}) async-start(), calls=%async_computation.12 | async-start | bytes 1474560 | tf_op jit(solution)/shard_map/reduce_scatter | solution.py:1077
  620.6 49.5 %collective-permute-start.77 = (bf16[8,192,384]{2,1,0:T(8,128)(2,1)}, bf16[8,192,384]{2,1,0:T(8,128)(2,1)S(1)}, u32[]{:S(2)}, u32[]{:S(2)}) collective-permute-start(bf16[8,192,384]{2,1,0:T(8,128)(2,1)} %get-tuple-element.492), channel_id=1, source_target_pairs={{0,16},{8,24},{16,0},{24,8},{1,17},{9,25},{17,1},{25,9},{2,18},{10... | collective-permute-start | bytes 3538952 | tf_op jit(solution)/shard_map/ppermute | solution.py:1048
  621.6 48.5 %collective-permute-start.76 = (bf16[6,192,384]{2,1,0:T(8,128)(2,1)}, bf16[6,192,384]{2,1,0:T(8,128)(2,1)S(1)}, u32[]{:S(2)}, u32[]{:S(2)}) collective-permute-start(bf16[6,192,384]{2,1,0:T(8,128)(2,1)} %get-tuple-element.491), channel_id=1, source_target_pairs={{0,1},{1,0},{2,3},{3,2},{4,5},{5,4},{6,7},{7,6},{8,9},{9,8},{10,11... | collective-permute-start | bytes 2654216 | tf_op jit(solution)/shard_map/ppermute | solution.py:1048
  630.6 45.6 %collective-permute-start.75 = (bf16[1,2,196,768]{3,1,2,0:T(2,128)(2,1)}, bf16[1,2,196,768]{3,1,2,0:T(2,128)(2,1)S(1)}, u32[]{:S(2)}, u32[]{:S(2)}) collective-permute-start(bf16[1,2,196,768]{3,1,2,0:T(2,128)(2,1)} %bitcast.189), channel_id=1, source_target_pairs={{0,0},{8,2},{2,4},{10,6},{4,8},{12,10},{6,12},{14,14},{16,16},{24,... | collective-permute-start | bytes 1806344 | tf_op jit(solution)/shard_map/ppermute | solution.py:791
  635.1 33.4 %all-to-all-start.1 = ((f32[32,1,384]{2,1,0:T(1,128)}), f32[32,1,384]{2,1,0:T(1,128)}, u32[]{:S(2)}, u32[]{:S(2)}) async-start(f32[32,1,384]{2,1,0:T(1,128)} %copy.125), calls=%async_computation.1 | async-start | bytes 98304 | tf_op jit(solution)/shard_map/all_to_all | solution.py:1136
  (138 other events, 1573.5 us)
Sparse Core Ops, SparseCore 0:
  11.7 144.2 all-gather.2
  159.6 122.0 all-gather.4
  508.1 19.8 reduce-scatter.6
  530.2 27.4 reduce-scatter.10
  585.1 21.5 reduce-scatter.4
  632.5 34.8 reduce-scatter.8

commit v17 on v16

--- a/solution.py
+++ b/solution.py
@@ -400,11 +400,11 @@
     )
 
 
-def mlp_forward(rows, x2, w, gb, gb_next, me):
+def mlp_forward(rows, x2, w, per_share, gb, gb_next, me):
     t, d = x2.shape
     width = w.shape[3]
     shares = w.shape[1]
-    per_share = w.shape[0] // 2
+    base = w.shape[0] - 2 * per_share
     steps = shares * per_share
 
     def body(x2_ref, wi_ref, wo_ref, gb_ref, me_ref, gn_ref, x3_ref, *rest):
@@ -428,8 +428,8 @@
 
     ins = [
         whole(x2.shape),
-        ff_slab(0, per_share, d, width),
-        ff_slab(per_share, per_share, d, width),
+        ff_slab(base, per_share, d, width),
+        ff_slab(base + per_share, per_share, d, width),
         whole(gb.shape),
     ]
     ins += [SCALARS, whole(gb_next.shape)]
@@ -440,11 +440,11 @@
     )
 
 
-def mlp_backward(rows, grad, x2, w, gb, me, halves, with_output):
+def mlp_backward(rows, grad, x2, w, per_share, gb, me, halves, with_output):
     t, d = x2.shape
     width = w.shape[3]
     shares = w.shape[1]
-    per_share = w.shape[0] // 2
+    base = w.shape[0] - 2 * per_share
     steps = shares * per_share
 
     def body(me_ref, g_ref, x2_ref, wi_ref, wo_ref, gb_ref, go_ref, ki_ref, si_ref, ko_ref, so_ref, sums_ref, *rest):
@@ -497,8 +497,8 @@
             SCALARS,
             whole(grad.shape),
             whole(x2.shape),
-            ff_slab(0, per_share, d, width),
-            ff_slab(per_share, per_share, d, width),
+            ff_slab(base, per_share, d, width),
+            ff_slab(base + per_share, per_share, d, width),
             whole(gb.shape),
         ],
         [made((t, d), F32), *slab_outs, made((2, d), F32)] + [made((t, d), F32)] * with_output,
@@ -1151,6 +1151,7 @@
     norm_bias,
 ):
     layers = time_qkv.shape[0]
+    per_share = mlp_in.shape[2] // time_qkv.shape[3]
     clips, frames, places, d = tokens.shape
     ways = lax.axis_size("seq")
     shards = lax.axis_size("clip") * ways
@@ -1173,8 +1174,9 @@
         for l in range(layers)
     ]
     packs_ff = [pack_feed_forward(mlp_in[l], mlp_out[l], time_qkv.shape[3]) for l in range(layers)]
+    packs[0] = jnp.concatenate((packs[0], packs_ff[0]), axis=0)
     weights = [gather_slabs(pack) for pack in packs]
-    mixes = [mix_whole(w[-1], shards) for w in weights]
+    mixes = [mix_whole(w[8], shards) for w in weights]
     quick = lax.axis_size("clip") == 4 and shares == 2 and ways == 4 and time_qkv.shape[1] % 16 == 0
 
     halves = Halves(lax.axis_size("clip"), d, time_qkv.shape[3])
@@ -1183,16 +1185,13 @@
     me = jnp.stack((clip & 1, (clip >> 1) & 1, lax.axis_index("head"), member, lax.axis_index("seq"))).astype(
         jnp.int32
     )
+    weights_ff = [weights[0]]
     if quick:
-        spreads = [Spread(pack, me) for pack in packs_ff]
-        weights_ff = []
+        spreads = [None] + [Spread(pack, me) for pack in packs_ff[1:]]
     else:
-        weights_ff = [gather_slabs(pack) for pack in packs_ff]
+        weights_ff += [gather_slabs(pack) for pack in packs_ff[1:]]
 
     home = go_home(tokens)
-    if quick:
-        first = spreads[0]
-        home, gb = first.step((home, gb))
     x = as_rows(home)
     send = send_first(rows, x, gb[0], me)
     kept = []
@@ -1200,22 +1199,18 @@
         w = weights[l]
         send = swap_places(send)
         if quick and l == 0:
-            for _ in range(2):
-                send = first.step(send)
             for spread in spreads[1:]:
-                send = spread.step(send)
-                send = spread.hold(send)
-            send = first.step(send)
+                send = spread.hold(spread.step(send))
         elif quick:
             send = spreads[l].step(send)
         a1, qkv1, log1, o1_time = time_forward(rows, send, w)
         back = swap_places(o1_time)
-        if quick:
+        if quick and l == 0:
+            for spread in spreads[1:]:
+                back = spread.step(back)
+        elif quick:
             back = spreads[l].step(back)
             weights_ff.append(spreads[l].come)
-            if l == 0:
-                for spread in spreads[1:]:
-                    back = spread.step(back)
         o1, y1, x1, qkv2 = middle_forward(rows, back, x, w, mixes[l], gb[l], me)
         o2, x2, log2 = space_forward(rows, qkv2, x1, w)
         if quick and l == 0:
@@ -1223,7 +1218,7 @@
                 x2 = spread.step(x2)
         kept.append((x, a1, qkv1, log1, o1, y1, x1, qkv2, o2, log2, x2))
         if l + 1 < layers:
-            x, *send = mlp_forward(rows, x2, weights_ff[l], gb[l], gb[l + 1], me)
+            x, *send = mlp_forward(rows, x2, weights_ff[l], per_share, gb[l], gb[l + 1], me)
 
     grad = as_rows(go_home(cotangent))
     norm_rows = [None] * layers
@@ -1233,7 +1228,7 @@
         w = weights[l]
         x, a1, qkv1, log1, o1, y1, x1, qkv2, o2, log2, x2 = kept[l]
         grad, g_ff, s3, x3 = mlp_backward(
-            rows, grad, x2, weights_ff[l], gb[l], me, halves, l + 1 == layers
+            rows, grad, x2, weights_ff[l], per_share, gb[l], me, halves, l + 1 == layers
         )
         if x3:
             output = go_back(from_rows(x3[0].astype(BF16)))
@@ -1296,7 +1291,6 @@
         r, width = a.shape
         return a.reshape(shares, r // shares, width).transpose(1, 0, 2).reshape(r // shares, -1)
 
-    per_share = mlp_in.shape[2] // time_qkv.shape[3]
     return (
         output,
         tokens_grad,

time: 737 us -> 746 us (1.012)
  waiting for transfers between devices: 240 us -> 287 us
  starting transfers between devices: 126 us -> 99.7 us
  Pallas kernels: 293 us -> 284 us
    all_gather x2, waiting for transfers between devices: 22.6 us -> 67 us  [gather_slabs(): full = lax.all_gather(pack, ('head', 'clip', 'seq'), axis=1, tiled=True)]
    ppermute x46 -> x38, waiting for transfers between devices: 72.7 us -> 45.7 us  [cross(): return lax.ppermute(a, axis, [(i, i ^ 1 << bit) for i in range(size)])]
    all_to_all x1, waiting for transfers between devices: 5.65 us -> 26 us  [gather_norms(): lax.all_to_all(jnp.broadcast_to(padded, (count, width)), ALL, split_axis=...]
    ppermute x6 -> x3, starting transfers between devices: 15.8 us -> 2.18 us  [spread_steps(): lax.ppermute(pack, 'seq', [(i, (i + k) % ways) for i in range(ways)])]
    pallas_call x2 -> x1, Pallas kernels: 17.2 us -> 8.23 us  [spread_steps(): pl.pallas_call(body, out_shape=jax.ShapeDtypeStruct((n, shares, clips * w...]
    ppermute x46 -> x38, starting transfers between devices: 39.2 us -> 31.9 us  [cross(): return lax.ppermute(a, axis, [(i, i ^ 1 << bit) for i in range(size)])]
    ppermute x6 -> x3, waiting for transfers between devices: 37.2 us -> 40 us  [spread_steps(): lax.ppermute(pack, 'seq', [(i, (i + k) % ways) for i in range(ways)])]
  transfers between devices with their start and end apart: 90 -> 79, of which waited for: 30 -> 28; matrix products, arithmetic and copies ran while one was open for 5% -> 5% of each run, Pallas kernels for 33% -> 31%
where the time goes in v17:
time: 746 us; the launch traced here: 742 us
  waiting for transfers between devices  287 us (38%)
  Pallas kernels  284 us (38%)
  starting transfers between devices  99.7 us (13%)
  local copies, waits for them, and re-layouts  37.8 us (5%)
  other arithmetic  17.3 us (2%)
  between operations  15.8 us (2%)
    pallas_call x18, Pallas kernels, call(): pl.pallas_call(body, out_shape=[shape for shape, _ in outs], grid=grid, i...  231 us
    all_gather x2, waiting for transfers between devices, gather_slabs(): full = lax.all_gather(pack, ('head', 'clip', 'seq'), axis=1, tiled=True)  67 us
    ppermute x24, waiting for transfers between devices, swap_places(): got.append(lax.ppermute(chunks[k], ('clip', 'seq'), pairs))  66.3 us
    ppermute x38, waiting for transfers between devices, cross(): return lax.ppermute(a, axis, [(i, i ^ 1 << bit) for i in range(size)])  45.7 us
    pallas_call x9, Pallas kernels, fold(): pl.pallas_call(body, out_shape=[jax.ShapeDtypeStruct(shape, BF16) for sha...  45.4 us
    ppermute x3, waiting for transfers between devices, spread_steps(): lax.ppermute(pack, 'seq', [(i, (i + k) % ways) for i in range(ways)])  40 us
    ppermute x24, starting transfers between devices, swap_places(): got.append(lax.ppermute(chunks[k], ('clip', 'seq'), pairs))  40 us
    ppermute x38, starting transfers between devices, cross(): return lax.ppermute(a, axis, [(i, i ^ 1 << bit) for i in range(size)])  31.9 us
  transfers between devices with their start and end apart: 79, of which 28 were waited for; matrix products, arithmetic and copies ran while one was open for 5% of the time, Pallas kernels for 31%

profile of v17, /device:TPU:0, one launch (start us, length us, event | category | flops | bytes accessed | tf_op | source)
XLA Modules:
  0.0 741.9 jit_solution(16247973159763698940)
XLA Ops:
  12.8 8.8 %all-to-all-start = ((f32[32,1,384]{2,1,0:T(1,128)}), f32[32,1,384]{2,1,0:T(1,128)S(1)}, u32[]{:S(2)}, u32[]{:S(2)}) async-start(f32[32,1,384]{2,1,0:T(1,128)} %broadcast_in_dim.17), calls=%async_computation | async-start | bytes 98304 | tf_op jit(solution)/shard_map/all_to_all | solution.py:1123
  22.3 26.0 %all-to-all-done = f32[32,1,384]{2,1,0:T(1,128)S(1)} async-done(((f32[32,1,384]{2,1,0:T(1,128)}), f32[32,1,384]{2,1,0:T(1,128)S(1)}, u32[]{:S(2)}, u32[]{:S(2)}) %all-to-all-start) | async-done | bytes 49184 | tf_op jit(solution)/shard_map/all_to_all | solution.py:1123
  55.4 14.1 %collective-permute-done.3.refs_2_ = bf16[104,768]{1,0:T(8,128)(2,1)S(1)} collective-permute-done((bf16[104,768]{1,0:T(8,128)(2,1)}, bf16[104,768]{1,0:T(8,128)(2,1)S(1)}, u32[]{:S(2)}, u32[]{:S(2)}) %collective-permute-start.3) | collective-permute-done | bytes 159776 | tf_op jit(solution)/shard_map/ppermute | solution.py:809
  69.6 11.5 %collective-permute-done.4.refs_3_ = bf16[104,768]{1,0:T(8,128)(2,1)S(1)} collective-permute-done((bf16[104,768]{1,0:T(8,128)(2,1)}, bf16[104,768]{1,0:T(8,128)(2,1)S(1)}, u32[]{:S(2)}, u32[]{:S(2)}) %collective-permute-start.4) | collective-permute-done | bytes 159776 | tf_op jit(solution)/shard_map/ppermute | solution.py:809
  83.2 11.5 %collective-permute-done.7 = bf16[8,48,384]{2,1,0:T(8,128)(2,1)S(1)} collective-permute-done((bf16[8,48,384]{2,1,0:T(8,128)(2,1)S(1)}, bf16[8,48,384]{2,1,0:T(8,128)(2,1)S(1)}, u32[]{:S(2)}, u32[]{:S(2)}) %collective-permute-start.7) | collective-permute-done | bytes 294944 | tf_op jit(solution)/shard_map/ppermute | solution.py:848
  94.7 28.5 %collective-permute-done.6 = bf16[8,48,384]{2,1,0:T(8,128)(2,1)S(1)} collective-permute-done((bf16[8,48,384]{2,1,0:T(8,128)(2,1)S(1)}, bf16[8,48,384]{2,1,0:T(8,128)(2,1)S(1)}, u32[]{:S(2)}, u32[]{:S(2)}) %collective-permute-start.6) | collective-permute-done | bytes 294944 | tf_op jit(solution)/shard_map/ppermute | solution.py:848
  123.2 43.8 %all-gather.3.cloned.1.call-done = bf16[17,1536,384]{2,1,0:T(8,128)(2,1)} async-done(((bf16[17,48,384]{2,1,0:T(8,128)(2,1)}), bf16[17,1536,384]{2,1,0:T(8,128)(2,1)}) %all-gather.3.cloned.1.call-update) | async-done | bytes 20054032 | tf_op jit(solution)/shard_map/all_gather | solution.py:838
  167.0 12.2 %shard_map.195 = (bf16[416,768]{1,0:T(8,128)(2,1)}, bf16[3,416,768]{2,1,0:T(8,128)(2,1)}, f32[2,3,2,416]{3,2,1,0:T(2,128)}, bf16[104,768]{1,0:T(8,128)(2,1)}, bf...) custom-call(bf16[104,768]{1,0:T(8,128)(2,1)} %get-tuple-element.235.refs_0_, ...), custom_call_target="tpu_custom_call" | custom-call | flops 1472200704 | bytes 23907840 | tf_op jit(solution)/shard_map/pallas_call | solution.py:212
  202.1 9.3 %shard_map.196 = (bf16[416,768]{1,0:T(8,128)(2,1)}, bf16[416,768]{1,0:T(8,128)(2,1)}, f32[416,768]{1,0:T(8,128)}, bf16[3,416,768]{2,1,0:T(8,128)(2,1)}) custom-call(s32[5]{0:T(128)} %stack.92.me_ref, bf16[104,768]{1,0:T(8,128)(2,1)} %get-tuple-element.247.refs_0_, bf16[104,768]{1,0:T(8,128)(2,1)} %copy-done.59, bf16[104,768]{1,0:T(8,128)(2,1)} %copy-done.60, ...), custom_call_target="tpu_custom_call" | custom-call | flops 2453667840 | bytes 47695892 | tf_op jit(solution)/shard_map/pallas_call | solution.py:212
  211.4 9.9 %shard_map.197 = (bf16[416,768]{1,0:T(8,128)(2,1)}, f32[416,768]{1,0:T(8,128)}, f32[2,3,2,2,208]{4,3,2,1,0:T(2,128)}) custom-call(bf16[3,416,768]{2,1,0:T(8,128)(2,1)} %get-tuple-element.251.qkv_ref, f32[416,768]{1,0:T(8,128)} %get-tuple-element.252.x1_ref, bf16[17,2,768,384]{3,2,1,0:T(8,128)(2,1)} %bitcast.198), custom_call_target="tpu_custom_call" | custom-call | flops 490733568 | bytes 25185792 | tf_op jit(solution)/shard_map/pallas_call | solution.py:212
  225.1 13.6 %shard_map.198 = (f32[416,768]{1,0:T(8,128)}, bf16[104,768]{1,0:T(8,128)(2,1)}, bf16[104,768]{1,0:T(8,128)(2,1)}, bf16[104,768]{1,0:T(8,128)(2,1)}, bf16[104,768]{1,0:T(8,128)(2,1)}) custom-call(f32[416,768]{1,0:T(8,128)} %get-tuple-element.258.x2_ref, bf16[17,2,768,384]{3,2,1,0:T(8,128)(2,1)} %bitcast.199, bf16[17,2,768,384]{3,2,1,0:T(8,128)(2,1)} %bitcast.200, ...), custom_call_target="tpu_custom_call" | custom-call | flops 3925868544 | bytes 43339796 | tf_op jit(solution)/shard_map/pallas_call | solution.py:212
  240.5 12.4 %collective-permute-done.14.refs_2_ = bf16[104,768]{1,0:T(8,128)(2,1)S(1)} collective-permute-done((bf16[104,768]{1,0:T(8,128)(2,1)}, bf16[104,768]{1,0:T(8,128)(2,1)S(1)}, u32[]{:S(2)}, u32[]{:S(2)}) %collective-permute-start.14) | collective-permute-done | bytes 159776 | tf_op jit(solution)/shard_map/ppermute | solution.py:809
  252.9 8.8 %collective-permute-done.15.refs_3_ = bf16[104,768]{1,0:T(8,128)(2,1)S(1)} collective-permute-done((bf16[104,768]{1,0:T(8,128)(2,1)}, bf16[104,768]{1,0:T(8,128)(2,1)S(1)}, u32[]{:S(2)}, u32[]{:S(2)}) %collective-permute-start.15) | collective-permute-done | bytes 159776 | tf_op jit(solution)/shard_map/ppermute | solution.py:809
  269.2 23.2 %all-gather.5.cloned.1.call-done = bf16[9,1536,384]{2,1,0:T(8,128)(2,1)} async-done(((bf16[9,48,384]{2,1,0:T(8,128)(2,1)}), bf16[9,1536,384]{2,1,0:T(8,128)(2,1)}) %all-gather.5.cloned.1.call-update) | async-done | bytes 10616848 | tf_op jit(solution)/shard_map/all_gather | solution.py:838
  292.4 12.2 %shard_map.199 = (bf16[416,768]{1,0:T(8,128)(2,1)}, bf16[3,416,768]{2,1,0:T(8,128)(2,1)}, f32[2,3,2,416]{3,2,1,0:T(2,128)}, bf16[104,768]{1,0:T(8,128)(2,1)}, bf...) custom-call(bf16[104,768]{1,0:T(8,128)(2,1)} %get-tuple-element.265.refs_0_, ...), custom_call_target="tpu_custom_call" | custom-call | flops 1472200704 | bytes 14470656 | tf_op jit(solution)/shard_map/pallas_call | solution.py:212
  316.0 9.4 %shard_map.200 = (bf16[416,768]{1,0:T(8,128)(2,1)}, bf16[416,768]{1,0:T(8,128)(2,1)}, f32[416,768]{1,0:T(8,128)}, bf16[3,416,768]{2,1,0:T(8,128)(2,1)}) custom-call(s32[5]{0:T(128)} %stack.92.me_ref, bf16[104,768]{1,0:T(8,128)(2,1)} %get-tuple-element.275.refs_0_, bf16[104,768]{1,0:T(8,128)(2,1)} %copy-done.41, bf16[104,768]{1,0:T(8,128)(2,1)} %copy-done.42, ...), custom_call_target="tpu_custom_call" | custom-call | flops 2453667840 | bytes 28821524 | tf_op jit(solution)/shard_map/pallas_call | solution.py:212
  325.4 9.9 %shard_map.201 = (bf16[416,768]{1,0:T(8,128)(2,1)}, f32[416,768]{1,0:T(8,128)}, f32[2,3,2,2,208]{4,3,2,1,0:T(2,128)}) custom-call(bf16[3,416,768]{2,1,0:T(8,128)(2,1)} %get-tuple-element.280.qkv_ref, f32[416,768]{1,0:T(8,128)} %get-tuple-element.281.x1_ref, bf16[9,2,768,384]{3,2,1,0:T(8,128)(2,1)} %bitcast.210), custom_call_target="tpu_custom_call" | custom-call | flops 490733568 | bytes 15748608 | tf_op jit(solution)/shard_map/pallas_call | solution.py:212
  335.3 8.2 %shard_map.202 = bf16[8,2,16,48,384]{4,3,2,1,0:T(8,128)(2,1)} custom-call(s32[5]{0:T(128)} %stack.92.me_ref, bf16[4,8,48,384]{3,2,1,0:T(8,128)(2,1)} %copy-done.21, bf16[4,8,48,384]{3,2,1,0:T(8,128)(2,1)} %collective-permute-done.16.refs_1_, bf16[4,8,48,384]{3,2,1,0:T(8,128)(2,1)} %copy-done.22, bf16[4,8,48,384]{3,2,1,0:T(8,128)(2,1)} %collective-permute-done.17.refs_3_, ...), custom_call_target="tpu_custom_call" | custom-call | bytes 18874368 | tf_op jit(solution)/shard_map/pallas_call | solution.py:883
  343.5 25.4 %shard_map.203 = (f32[416,768]{1,0:T(8,128)}, bf16[4,2,2,192,384]{4,3,2,1,0:T(8,128)(2,1)}, bf16[4,2,2,192,384]{4,3,2,1,0:T(8,128)(2,1)}, bf16[4,2,2,192,384]{4,...) custom-call(s32[5]{0:T(128)} %stack.92.me_ref, ...), custom_call_target="tpu_custom_call" | custom-call | flops 9814671360 | bytes 33447956 | tf_op jit(solution)/shard_map/pallas_call | solution.py:212
  369.5 21.4 %shard_map.204 = (f32[416,768]{1,0:T(8,128)}, bf16[4,2,2,192,384]{4,3,2,1,0:T(8,128)(2,1)}, bf16[4,2,2,192,384]{4,3,2,1,0:T(8,128)(2,1)}, f32[2,768]{1,0:T(2,128)}) custom-call(s32[5]{0:T(128)} %stack.92.me_ref, f32[416,768]{1,0:T(8,128)} %get-tuple-element.287.g_ref, f32[416,768]{1,0:T(8,128)} %get-tuple-element.281.x1_ref, ...), custom_call_target="tpu_custom_call" | custom-call | flops 3925868544 | bytes 32386580 | tf_op jit(solution)/shard_map/pallas_call | solution.py:212
  401.7 7.7 %shard_map.206 = (bf16[104,768]{1,0:T(8,128)(2,1)}, bf16[104,768]{1,0:T(8,128)(2,1)}, bf16[104,768]{1,0:T(8,128)(2,1)}, bf16[104,768]{1,0:T(8,128)(2,1)}, bf16[2...) custom-call(s32[5]{0:T(128)} %stack.92.me_ref, f32[416,768]{1,0:T(8,128)} %get-tuple-element.298.g_ref.refs_5_, ...), custom_call_target="tpu_custom_call" | custom-call | flops 1962934272 | bytes 17350676 | tf_op jit(solution)/shard_map/pallas_call | solution.py:212
  409.5 10.3 %collective-permute-start.28 = (bf16[104,768]{1,0:T(8,128)(2,1)}, bf16[104,768]{1,0:T(8,128)(2,1)S(1)}, u32[]{:S(2)}, u32[]{:S(2)}) collective-permute-start(bf16[104,768]{1,0:T(8,128)(2,1)} %get-tuple-element.302), channel_id=1, source_target_pairs={{0,8},{2,10},{4,12},{6,14},{8,0},{10,2},{12,4},{14,6},{16,24},{18,... | collective-permute-start | bytes 479240 | tf_op jit(solution)/shard_map/ppermute | solution.py:809
  437.8 18.1 %shard_map.208 = (bf16[104,768]{1,0:T(8,128)(2,1)}, bf16[104,768]{1,0:T(8,128)(2,1)}, bf16[104,768]{1,0:T(8,128)(2,1)}, bf16[104,768]{1,0:T(8,128)(2,1)}, bf16[1...) custom-call(s32[5]{0:T(128)} %stack.92.me_ref, ...), custom_call_target="tpu_custom_call" | custom-call | flops 2944401408 | bytes 18009620 | tf_op jit(solution)/shard_map/pallas_call | solution.py:212
  458.9 15.7 %collective-permute-start.37 = (bf16[104,768]{1,0:T(8,128)(2,1)}, bf16[104,768]{1,0:T(8,128)(2,1)S(1)}, u32[]{:S(2)}, u32[]{:S(2)}) collective-permute-start(bf16[104,768]{1,0:T(8,128)(2,1)} %get-tuple-element.326), channel_id=1, source_target_pairs={{0,2},{2,0},{4,6},{6,4},{8,10},{10,8},{12,14},{14,12},{16,18},{18,... | collective-permute-start | bytes 479240 | tf_op jit(solution)/shard_map/ppermute | solution.py:809
  489.7 22.4 %shard_map.211 = (f32[416,768]{1,0:T(8,128)}, bf16[4,2,2,192,384]{4,3,2,1,0:T(8,128)(2,1)}, bf16[4,2,2,192,384]{4,3,2,1,0:T(8,128)(2,1)}, bf16[4,2,2,192,384]{4,...) custom-call(s32[5]{0:T(128)} %stack.92.me_ref, f32[416,768]{1,0:T(8,128)} %get-tuple-element.345.g_ref, ...), custom_call_target="tpu_custom_call" | custom-call | flops 9814671360 | bytes 53403668 | tf_op jit(solution)/shard_map/pallas_call | solution.py:212
  518.3 21.5 %shard_map.213 = (f32[416,768]{1,0:T(8,128)}, bf16[4,2,2,192,384]{4,3,2,1,0:T(8,128)(2,1)}, bf16[4,2,2,192,384]{4,3,2,1,0:T(8,128)(2,1)}, f32[2,768]{1,0:T(2,128)}) custom-call(s32[5]{0:T(128)} %stack.92.me_ref, f32[416,768]{1,0:T(8,128)} %get-tuple-element.355.g_ref, f32[416,768]{1,0:T(8,128)} %get-tuple-element.252.x1_ref, ...), custom_call_target="tpu_custom_call" | custom-call | flops 3925868544 | bytes 51260948 | tf_op jit(solution)/shard_map/pallas_call | solution.py:212
  542.2 7.7 %collective-permute-done.46.refs_17_ = bf16[2,192,384]{2,1,0:T(8,128)(2,1)S(1)} collective-permute-done((bf16[2,192,384]{2,1,0:T(8,128)(2,1)S(1)}, bf16[2,192,384]{2,1,0:T(8,128)(2,1)S(1)}, u32[]{:S(2)}, u32[]{:S(2)}) %collective-permute-start.46) | collective-permute-done | bytes 294944 | tf_op jit(solution)/shard_map/ppermute | solution.py:1048
  559.3 7.8 %shard_map.215 = (bf16[104,768]{1,0:T(8,128)(2,1)}, bf16[104,768]{1,0:T(8,128)(2,1)}, bf16[104,768]{1,0:T(8,128)(2,1)}, bf16[104,768]{1,0:T(8,128)(2,1)}, bf16[2...) custom-call(s32[5]{0:T(128)} %stack.92.me_ref, f32[416,768]{1,0:T(8,128)} %get-tuple-element.370.g_ref.refs_5_, ...), custom_call_target="tpu_custom_call" | custom-call | flops 1962934272 | bytes 26787860 | tf_op jit(solution)/shard_map/pallas_call | solution.py:212
  569.0 16.3 %collective-permute-done.52.refs_2_ = bf16[8,192,384]{2,1,0:T(8,128)(2,1)S(1)} collective-permute-done((bf16[8,192,384]{2,1,0:T(8,128)(2,1)}, bf16[8,192,384]{2,1,0:T(8,128)(2,1)S(1)}, u32[]{:S(2)}, u32[]{:S(2)}) %collective-permute-start.52) | collective-permute-done | bytes 1179680 | tf_op jit(solution)/shard_map/ppermute | solution.py:1048
  594.8 18.3 %shard_map.217 = (bf16[104,768]{1,0:T(8,128)(2,1)}, bf16[104,768]{1,0:T(8,128)(2,1)}, bf16[104,768]{1,0:T(8,128)(2,1)}, bf16[104,768]{1,0:T(8,128)(2,1)}, bf16[1...) custom-call(s32[5]{0:T(128)} %stack.92.me_ref, ...), custom_call_target="tpu_custom_call" | custom-call | flops 2944401408 | bytes 27446804 | tf_op jit(solution)/shard_map/pallas_call | solution.py:212
  650.3 28.3 %all-to-all-done.1 = f32[32,1,384]{2,1,0:T(1,128)} async-done(((f32[32,1,384]{2,1,0:T(1,128)}), f32[32,1,384]{2,1,0:T(1,128)}, u32[]{:S(2)}, u32[]{:S(2)}) %all-to-all-start.1) | async-done | bytes 49184 | tf_op jit(solution)/shard_map/all_to_all | solution.py:1136
  718.3 13.3 %all-to-all-done.2 = bf16[4,5,48,384]{3,2,1,0:T(8,128)(2,1)S(1)} async-done(((bf16[4,5,48,384]{3,2,1,0:T(8,128)(2,1)}), bf16[4,5,48,384]{3,2,1,0:T(8,128)(2,1)S(1)}, u32[]{:S(2)}, u32[]{:S(2)}) %all-to-all-start.2) | async-done | bytes 737312 | tf_op jit(solution)/shard_map/all_to_all | solution.py:1074
  (424 shorter events, 218.4 us)
Async XLA Ops:
  7.2 159.8 %all-gather.3.cloned.1.call-start = ((), (), s32[]{:S(2)}) async-start(), calls=%async_computation.8 | async-start | bytes 20680704 | tf_op jit(solution)/shard_map/all_gather | solution.py:838
  10.4 282.0 %all-gather.5.cloned.1.call-start = ((), (), s32[]{:S(2)}) async-start(), calls=%async_computation.9 | async-start | bytes 10948608 | tf_op jit(solution)/shard_map/all_gather | solution.py:838
  11.3 37.9 %collective-permute-start.1 = (bf16[1,2,196,768]{3,1,2,0:T(2,128)(2,1)S(1)}, bf16[1,2,196,768]{3,1,2,0:T(2,128)(2,1)S(1)}, u32[]{:S(2)}, u32[]{:S(2)}) collective-permute-start(bf16[1,2,196,768]{3,1,2,0:T(2,128)(2,1)S(1)} %copy-done.74), channel_id=1, source_target_pairs={{0,0},{2,8},{4,2},{6,10},{8,4},{10,12},{12,6},{14,14},{16,16},{18,... | collective-permute-start | bytes 1806344 | tf_op jit(solution)/shard_map/ppermute | solution.py:787
  12.8 35.4 %all-to-all-start = ((f32[32,1,384]{2,1,0:T(1,128)}), f32[32,1,384]{2,1,0:T(1,128)S(1)}, u32[]{:S(2)}, u32[]{:S(2)}) async-start(f32[32,1,384]{2,1,0:T(1,128)} %broadcast_in_dim.17), calls=%async_computation | async-start | bytes 98304 | tf_op jit(solution)/shard_map/all_to_all | solution.py:1123
  21.6 610.7 %reduce-scatter.7.cloned.1.call-start = ((), (), s32[]{:S(2)}) async-start(), calls=%async_computation.11 | async-start | bytes 737280 | tf_op jit(solution)/shard_map/reduce_scatter | solution.py:1077
  82.2 41.0 %collective-permute-start.6 = (bf16[8,48,384]{2,1,0:T(8,128)(2,1)S(1)}, bf16[8,48,384]{2,1,0:T(8,128)(2,1)S(1)}, u32[]{:S(2)}, u32[]{:S(2)}) collective-permute-start(bf16[8,48,384]{2,1,0:T(8,128)(2,1)S(1)} %pad_maximum_fusion.8), channel_id=1, source_target_pairs={{0,4},{2,6},{4,0},{6,2},{1,5},{3,7},{5,1},{7,3},{8,12},{10,14},{12... | collective-permute-start | bytes 884744 | tf_op jit(solution)/shard_map/ppermute | solution.py:848
  82.2 41.0 %collective-permute-start.5 = (bf16[8,48,384]{2,1,0:T(8,128)(2,1)S(1)}, bf16[8,48,384]{2,1,0:T(8,128)(2,1)S(1)}, u32[]{:S(2)}, u32[]{:S(2)}) collective-permute-start(bf16[8,48,384]{2,1,0:T(8,128)(2,1)S(1)} %pad_maximum_fusion.8), channel_id=1, source_target_pairs={{0,2},{2,4},{4,6},{6,0},{1,3},{3,5},{5,7},{7,1},{8,10},{10,12},{12... | collective-permute-start | bytes 884744 | tf_op jit(solution)/shard_map/ppermute | solution.py:848
  222.1 42.9 %collective-permute-start.17 = (bf16[4,8,48,384]{3,2,1,0:T(8,128)(2,1)S(1)}, bf16[4,8,48,384]{3,2,1,0:T(8,128)(2,1)}, u32[]{:S(2)}, u32[]{:S(2)}) collective-permute-start(bf16[4,8,48,384]{3,2,1,0:T(8,128)(2,1)S(1)} %pad_maximum_fusion.1.refs_2_), channel_id=1, source_target_pairs={{0,16},{8,24},{16,0},{24,8},{1,17},{9,25},{17,1},{25,9},{2,18},{10... | collective-permute-start | bytes 3538952 | tf_op jit(solution)/shard_map/ppermute | solution.py:1048
  223.7 43.9 %collective-permute-start.16 = (bf16[4,8,48,384]{3,2,1,0:T(8,128)(2,1)S(1)}, bf16[4,8,48,384]{3,2,1,0:T(8,128)(2,1)}, u32[]{:S(2)}, u32[]{:S(2)}) collective-permute-start(bf16[4,8,48,384]{3,2,1,0:T(8,128)(2,1)S(1)} %pad_maximum_fusion.refs_0_), channel_id=1, source_target_pairs={{0,1},{1,0},{2,3},{3,2},{4,5},{5,4},{6,7},{7,6},{8,9},{9,8},{10,11... | collective-permute-start | bytes 3538952 | tf_op jit(solution)/shard_map/ppermute | solution.py:1048
  239.2 65.7 %collective-permute-start.23 = (bf16[4,8,48,384]{3,2,1,0:T(8,128)(2,1)S(1)}, bf16[4,8,48,384]{3,2,1,0:T(8,128)(2,1)}, u32[]{:S(2)}, u32[]{:S(2)}) collective-permute-start(bf16[4,8,48,384]{3,2,1,0:T(8,128)(2,1)S(1)} %pad_maximum_fusion.1.refs_2_), channel_id=1, source_target_pairs={{0,8},{8,0},{16,24},{24,16},{1,9},{9,1},{17,25},{25,17},{2,10},{10... | collective-permute-start | bytes 3538952 | tf_op jit(solution)/shard_map/ppermute | solution.py:1048
  240.3 66.9 %collective-permute-start.21 = (bf16[4,8,48,384]{3,2,1,0:T(8,128)(2,1)S(1)}, bf16[4,8,48,384]{3,2,1,0:T(8,128)(2,1)}, u32[]{:S(2)}, u32[]{:S(2)}) collective-permute-start(bf16[4,8,48,384]{3,2,1,0:T(8,128)(2,1)S(1)} %pad_maximum_fusion.refs_0_), channel_id=1, source_target_pairs={{0,8},{8,0},{16,24},{24,16},{1,9},{9,1},{17,25},{25,17},{2,10},{10... | collective-permute-start | bytes 3538952 | tf_op jit(solution)/shard_map/ppermute | solution.py:1048
  267.6 47.7 %collective-permute-start.22 = (bf16[4,8,48,384]{3,2,1,0:T(8,128)(2,1)}, bf16[4,8,48,384]{3,2,1,0:T(8,128)(2,1)}, u32[]{:S(2)}, u32[]{:S(2)}) collective-permute-start(bf16[4,8,48,384]{3,2,1,0:T(8,128)(2,1)} %collective-permute-done.16.refs_1_), channel_id=1, source_target_pairs={{0,8},{8,0},{16,24},{24,16},{1,9},{9,1},{17,25},{25,17},{2,10},{10... | collective-permute-start | bytes 3538952 | tf_op jit(solution)/shard_map/ppermute | solution.py:1048
  267.6 47.7 %collective-permute-start.24 = (bf16[4,8,48,384]{3,2,1,0:T(8,128)(2,1)}, bf16[4,8,48,384]{3,2,1,0:T(8,128)(2,1)}, u32[]{:S(2)}, u32[]{:S(2)}) collective-permute-start(bf16[4,8,48,384]{3,2,1,0:T(8,128)(2,1)} %collective-permute-done.17.refs_3_), channel_id=1, source_target_pairs={{0,8},{8,0},{16,24},{24,16},{1,9},{9,1},{17,25},{25,17},{2,10},{10... | collective-permute-start | bytes 3538952 | tf_op jit(solution)/shard_map/ppermute | solution.py:1048
  390.9 29.1 %collective-permute-start.33 = (bf16[4,2,2,192,384]{4,3,2,1,0:T(8,128)(2,1)}, bf16[4,2,2,192,384]{4,3,2,1,0:T(8,128)(2,1)S(1)}, u32[]{:S(2)}, u32[]{:S(2)}) collective-permute-start(bf16[4,2,2,192,384]{4,3,2,1,0:T(8,128)(2,1)} %get-tuple-element.308), channel_id=1, source_target_pairs={{0,8},{8,0},{16,24},{24,16},{1,9},{9,1},{17,25},{25,17},{2,10},{10... | collective-permute-start | bytes 7077896 | tf_op jit(solution)/shard_map/ppermute | solution.py:1048
  428.6 27.9 %collective-permute-start.34 = (bf16[8,192,384]{2,1,0:T(8,128)(2,1)}, bf16[8,192,384]{2,1,0:T(8,128)(2,1)S(1)}, u32[]{:S(2)}, u32[]{:S(2)}) collective-permute-start(bf16[8,192,384]{2,1,0:T(8,128)(2,1)} %get-tuple-element.322), channel_id=1, source_target_pairs={{0,1},{1,0},{2,3},{3,2},{4,5},{5,4},{6,7},{7,6},{8,9},{9,8},{10,11... | collective-permute-start | bytes 3538952 | tf_op jit(solution)/shard_map/ppermute | solution.py:1048
  430.0 27.5 %collective-permute-start.35 = (bf16[8,192,384]{2,1,0:T(8,128)(2,1)}, bf16[8,192,384]{2,1,0:T(8,128)(2,1)S(1)}, u32[]{:S(2)}, u32[]{:S(2)}) collective-permute-start(bf16[8,192,384]{2,1,0:T(8,128)(2,1)} %get-tuple-element.323), channel_id=1, source_target_pairs={{0,16},{8,24},{16,0},{24,8},{1,17},{9,25},{17,1},{25,9},{2,18},{10... | collective-permute-start | bytes 3538952 | tf_op jit(solution)/shard_map/ppermute | solution.py:1048
  431.7 27.2 %collective-permute-start.39 = (bf16[2,2,2,192,384]{4,3,2,1,0:T(8,128)(2,1)S(1)}, bf16[2,2,2,192,384]{4,3,2,1,0:T(8,128)(2,1)S(1)}, u32[]{:S(2)}, u32[]{:S(2)}) collective-permute-start(bf16[2,2,2,192,384]{4,3,2,1,0:T(8,128)(2,1)S(1)} %copy-done.73), channel_id=1, source_target_pairs={{0,8},{8,0},{16,24},{24,16},{1,9},{9,1},{17,25},{25,17},{2,10},{10... | collective-permute-start | bytes 3538952 | tf_op jit(solution)/shard_map/ppermute | solution.py:1048
  482.7 30.0 %collective-permute-start.43 = (bf16[6,192,384]{2,1,0:T(8,128)(2,1)}, bf16[6,192,384]{2,1,0:T(8,128)(2,1)S(1)}, u32[]{:S(2)}, u32[]{:S(2)}) collective-permute-start(bf16[6,192,384]{2,1,0:T(8,128)(2,1)} %get-tuple-element.347), channel_id=1, source_target_pairs={{0,1},{1,0},{2,3},{3,2},{4,5},{5,4},{6,7},{7,6},{8,9},{9,8},{10,11... | collective-permute-start | bytes 2654216 | tf_op jit(solution)/shard_map/ppermute | solution.py:1048
  483.9 28.8 %collective-permute-start.44 = (bf16[8,192,384]{2,1,0:T(8,128)(2,1)}, bf16[8,192,384]{2,1,0:T(8,128)(2,1)S(1)}, u32[]{:S(2)}, u32[]{:S(2)}) collective-permute-start(bf16[8,192,384]{2,1,0:T(8,128)(2,1)} %get-tuple-element.348), channel_id=1, source_target_pairs={{0,16},{8,24},{16,0},{24,8},{1,17},{9,25},{17,1},{25,9},{2,18},{10... | collective-permute-start | bytes 3538952 | tf_op jit(solution)/shard_map/ppermute | solution.py:1048
  512.1 40.8 %collective-permute-start.47 = (bf16[4,2,2,192,384]{4,3,2,1,0:T(8,128)(2,1)}, bf16[4,2,2,192,384]{4,3,2,1,0:T(8,128)(2,1)}, u32[]{:S(2)}, u32[]{:S(2)}) collective-permute-start(bf16[4,2,2,192,384]{4,3,2,1,0:T(8,128)(2,1)} %get-tuple-element.364), channel_id=1, source_target_pairs={{0,8},{8,0},{16,24},{24,16},{1,9},{9,1},{17,25},{25,17},{2,10},{10... | collective-permute-start | bytes 7077896 | tf_op jit(solution)/shard_map/ppermute | solution.py:1048
  512.2 40.7 %collective-permute-start.48 = (bf16[4,2,2,192,384]{4,3,2,1,0:T(8,128)(2,1)}, bf16[4,2,2,192,384]{4,3,2,1,0:T(8,128)(2,1)}, u32[]{:S(2)}, u32[]{:S(2)}) collective-permute-start(bf16[4,2,2,192,384]{4,3,2,1,0:T(8,128)(2,1)} %get-tuple-element.366), channel_id=1, source_target_pairs={{0,8},{8,0},{16,24},{24,16},{1,9},{9,1},{17,25},{25,17},{2,10},{10... | collective-permute-start | bytes 7077896 | tf_op jit(solution)/shard_map/ppermute | solution.py:1048
  518.2 131.0 %reduce-scatter.11.cloned.1.call-start = ((), (), s32[]{:S(2)}) async-start(), calls=%async_computation.13 | async-start | bytes 1474560 | tf_op jit(solution)/shard_map/reduce_scatter | solution.py:1077
  539.8 28.8 %collective-permute-start.54 = (bf16[4,2,2,192,384]{4,3,2,1,0:T(8,128)(2,1)}, bf16[4,2,2,192,384]{4,3,2,1,0:T(8,128)(2,1)S(1)}, u32[]{:S(2)}, u32[]{:S(2)}) collective-permute-start(bf16[4,2,2,192,384]{4,3,2,1,0:T(8,128)(2,1)} %get-tuple-element.380), channel_id=1, source_target_pairs={{0,8},{8,0},{16,24},{24,16},{1,9},{9,1},{17,25},{25,17},{2,10},{10... | collective-permute-start | bytes 7077896 | tf_op jit(solution)/shard_map/ppermute | solution.py:1048
  540.0 150.1 %reduce-scatter.5.cloned.1.call-start = ((), (), s32[]{:S(2)}) async-start(), calls=%async_computation.10 | async-start | bytes 921600 | tf_op jit(solution)/shard_map/reduce_scatter | solution.py:1077
  557.8 27.5 %collective-permute-start.52 = (bf16[8,192,384]{2,1,0:T(8,128)(2,1)}, bf16[8,192,384]{2,1,0:T(8,128)(2,1)S(1)}, u32[]{:S(2)}, u32[]{:S(2)}) collective-permute-start(bf16[8,192,384]{2,1,0:T(8,128)(2,1)} %get-tuple-element.377), channel_id=1, source_target_pairs={{0,16},{8,24},{16,0},{24,8},{1,17},{9,25},{17,1},{25,9},{2,18},{10... | collective-permute-start | bytes 3538952 | tf_op jit(solution)/shard_map/ppermute | solution.py:1048
  558.5 27.1 %collective-permute-start.53 = (bf16[8,192,384]{2,1,0:T(8,128)(2,1)}, bf16[8,192,384]{2,1,0:T(8,128)(2,1)S(1)}, u32[]{:S(2)}, u32[]{:S(2)}) collective-permute-start(bf16[8,192,384]{2,1,0:T(8,128)(2,1)} %get-tuple-element.378), channel_id=1, source_target_pairs={{0,1},{1,0},{2,3},{3,2},{4,5},{5,4},{6,7},{7,6},{8,9},{9,8},{10,11... | collective-permute-start | bytes 3538952 | tf_op jit(solution)/shard_map/ppermute | solution.py:1048
  593.7 26.8 %collective-permute-start.56 = (bf16[8,192,384]{2,1,0:T(8,128)(2,1)}, bf16[8,192,384]{2,1,0:T(8,128)(2,1)}, u32[]{:S(2)}, u32[]{:S(2)}) collective-permute-start(bf16[8,192,384]{2,1,0:T(8,128)(2,1)} %get-tuple-element.398), channel_id=1, source_target_pairs={{0,16},{8,24},{16,0},{24,8},{1,17},{9,25},{17,1},{25,9},{2,18},{10... | collective-permute-start | bytes 3538952 | tf_op jit(solution)/shard_map/ppermute | solution.py:1048
  594.7 120.5 %reduce-scatter.9.cloned.1.call-start = ((), (), s32[]{:S(2)}) async-start(), calls=%async_computation.12 | async-start | bytes 1474560 | tf_op jit(solution)/shard_map/reduce_scatter | solution.py:1077
  630.4 49.7 %collective-permute-start.66 = (bf16[8,192,384]{2,1,0:T(8,128)(2,1)}, bf16[8,192,384]{2,1,0:T(8,128)(2,1)S(1)}, u32[]{:S(2)}, u32[]{:S(2)}) collective-permute-start(bf16[8,192,384]{2,1,0:T(8,128)(2,1)} %get-tuple-element.428), channel_id=1, source_target_pairs={{0,16},{8,24},{16,0},{24,8},{1,17},{9,25},{17,1},{25,9},{2,18},{10... | collective-permute-start | bytes 3538952 | tf_op jit(solution)/shard_map/ppermute | solution.py:1048
  631.6 48.5 %collective-permute-start.65 = (bf16[6,192,384]{2,1,0:T(8,128)(2,1)}, bf16[6,192,384]{2,1,0:T(8,128)(2,1)S(1)}, u32[]{:S(2)}, u32[]{:S(2)}) collective-permute-start(bf16[6,192,384]{2,1,0:T(8,128)(2,1)} %get-tuple-element.427), channel_id=1, source_target_pairs={{0,1},{1,0},{2,3},{3,2},{4,5},{5,4},{6,7},{7,6},{8,9},{9,8},{10,11... | collective-permute-start | bytes 2654216 | tf_op jit(solution)/shard_map/ppermute | solution.py:1048
  640.4 45.8 %collective-permute-start.64 = (bf16[1,2,196,768]{3,1,2,0:T(2,128)(2,1)}, bf16[1,2,196,768]{3,1,2,0:T(2,128)(2,1)S(1)}, u32[]{:S(2)}, u32[]{:S(2)}) collective-permute-start(bf16[1,2,196,768]{3,1,2,0:T(2,128)(2,1)} %bitcast.188), channel_id=1, source_target_pairs={{0,0},{8,2},{2,4},{10,6},{4,8},{12,10},{6,12},{14,14},{16,16},{24,... | collective-permute-start | bytes 1806344 | tf_op jit(solution)/shard_map/ppermute | solution.py:791
  644.9 33.7 %all-to-all-start.1 = ((f32[32,1,384]{2,1,0:T(1,128)}), f32[32,1,384]{2,1,0:T(1,128)}, u32[]{:S(2)}, u32[]{:S(2)}) async-start(f32[32,1,384]{2,1,0:T(1,128)} %copy.127), calls=%async_computation.1 | async-start | bytes 98304 | tf_op jit(solution)/shard_map/all_to_all | solution.py:1136
  (126 other events, 1443.0 us)
Sparse Core Ops, SparseCore 0:
  11.7 155.2 all-gather.2
  170.6 121.7 all-gather.4
  518.3 19.5 reduce-scatter.6
  540.1 27.5 reduce-scatter.10
  594.8 21.5 reduce-scatter.4
  642.3 35.0 reduce-scatter.8

commit v18 on v16

--- a/solution.py
+++ b/solution.py
@@ -836,6 +836,12 @@
 
 def gather_slabs(pack):
     full = lax.all_gather(pack, ("head", "clip", "seq"), axis=1, tiled=True)
+    return full.reshape(pack.shape[0], lax.axis_size("head"), -1, pack.shape[2])
+
+
+def gather_slabs_later(pack):
+    parts = [lax.all_gather(a, "seq", axis=1, tiled=True) for a in jnp.split(pack, [5], axis=0)]
+    full = lax.all_gather(jnp.concatenate(parts, axis=0), ("head", "clip"), axis=1, tiled=True)
     return full.reshape(pack.shape[0], lax.axis_size("head"), -1, pack.shape[2])
 
 
@@ -1173,7 +1179,9 @@
         for l in range(layers)
     ]
     packs_ff = [pack_feed_forward(mlp_in[l], mlp_out[l], time_qkv.shape[3]) for l in range(layers)]
-    weights = [gather_slabs(pack) for pack in packs]
+    home = go_home(tokens)
+    gb, home, packs[1:] = lax.optimization_barrier((gb, home, packs[1:]))
+    weights = [gather_slabs(packs[0])] + [gather_slabs_later(pack) for pack in packs[1:]]
     mixes = [mix_whole(w[-1], shards) for w in weights]
     quick = lax.axis_size("clip") == 4 and shares == 2 and ways == 4 and time_qkv.shape[1] % 16 == 0
 
@@ -1189,7 +1197,6 @@
     else:
         weights_ff = [gather_slabs(pack) for pack in packs_ff]
 
-    home = go_home(tokens)
     if quick:
         first = spreads[0]
         home, gb = first.step((home, gb))

time: 737 us -> 771 us (1.046)
  blocking collectives: 0 us -> 45.9 us
  waiting for transfers between devices: 240 us -> 221 us
    all_gather x0 -> x2, blocking collectives: none -> 45.9 us  [gather_slabs_later(): lax.all_gather(a, 'seq', axis=1, tiled=True)]
    all_gather x2 -> x1, waiting for transfers between devices: 22.6 us -> 0.01 us  [gather_slabs(): full = lax.all_gather(pack, ('head', 'clip', 'seq'), axis=1, tiled=True)]
    ppermute x6, waiting for transfers between devices: 37.2 us -> 22.2 us  [spread_steps(): lax.ppermute(pack, 'seq', [(i, (i + k) % ways) for i in range(ways)])]
    all_to_all x1, waiting for transfers between devices: 5.65 us -> 20.2 us  [gather_norms(): lax.all_to_all(jnp.broadcast_to(padded, (count, width)), ALL, split_axis=...]
    ppermute x24, starting transfers between devices: 47.3 us -> 59.1 us  [swap_places(): got.append(lax.ppermute(chunks[k], ('clip', 'seq'), pairs))]
    ppermute x46, waiting for transfers between devices: 72.7 us -> 81.6 us  [cross(): return lax.ppermute(a, axis, [(i, i ^ 1 << bit) for i in range(size)])]
    unnamed x173 -> x171, local copies, waits for them, and re-layouts: 23.5 us -> 23.4 us
  transfers between devices with their start and end apart: 90 -> 90, of which waited for: 30 -> 27; matrix products, arithmetic and copies ran while one was open for 5% -> 5% of each run, Pallas kernels for 33% -> 31%
where the time goes in v18:
time: 771 us; the launch traced here: 765 us
  Pallas kernels  293 us (38%)
  waiting for transfers between devices  221 us (29%)
  starting transfers between devices  132 us (17%)
  blocking collectives  45.9 us (6%)
  local copies, waits for them, and re-layouts  38.9 us (5%)
  other arithmetic  19 us (2%)
  between operations  15.9 us (2%)
    pallas_call x18, Pallas kernels, call(): pl.pallas_call(body, out_shape=[shape for shape, _ in outs], grid=grid, i...  231 us
    ppermute x46, waiting for transfers between devices, cross(): return lax.ppermute(a, axis, [(i, i ^ 1 << bit) for i in range(size)])  81.6 us
    ppermute x24, starting transfers between devices, swap_places(): got.append(lax.ppermute(chunks[k], ('clip', 'seq'), pairs))  59.1 us
    ppermute x24, waiting for transfers between devices, swap_places(): got.append(lax.ppermute(chunks[k], ('clip', 'seq'), pairs))  54.4 us
    all_gather x2, blocking collectives, gather_slabs_later(): lax.all_gather(a, 'seq', axis=1, tiled=True)  45.9 us
    pallas_call x9, Pallas kernels, fold(): pl.pallas_call(body, out_shape=[jax.ShapeDtypeStruct(shape, BF16) for sha...  45.5 us
    ppermute x46, starting transfers between devices, cross(): return lax.ppermute(a, axis, [(i, i ^ 1 << bit) for i in range(size)])  38.9 us
    all_to_all x1, waiting for transfers between devices, reduce_norms(): every = lax.all_to_all(a, ALL, split_axis=0, concat_axis=0, tiled=True)  28.9 us
  transfers between devices with their start and end apart: 90, of which 27 were waited for; matrix products, arithmetic and copies ran while one was open for 5% of the time, Pallas kernels for 31%

profile of v18, /device:TPU:0, one launch (start us, length us, event | category | flops | bytes accessed | tf_op | source)
XLA Modules:
  0.0 765.2 jit_solution(16748106553037437310)
XLA Ops:
  12.5 8.8 %all-to-all-start = ((f32[32,1,384]{2,1,0:T(1,128)}), f32[32,1,384]{2,1,0:T(1,128)S(1)}, u32[]{:S(2)}, u32[]{:S(2)}) async-start(f32[32,1,384]{2,1,0:T(1,128)} %broadcast_in_dim.17), calls=%async_computation | async-start | bytes 98304 | tf_op jit(solution)/shard_map/all_to_all | solution.py:1129
  21.4 20.2 %all-to-all-done = f32[32,1,384]{2,1,0:T(1,128)S(1)} async-done(((f32[32,1,384]{2,1,0:T(1,128)}), f32[32,1,384]{2,1,0:T(1,128)S(1)}, u32[]{:S(2)}, u32[]{:S(2)}) %all-to-all-start) | async-done | bytes 49184 | tf_op jit(solution)/shard_map/all_to_all | solution.py:1129
  43.5 24.0 %all_gather.14 = bf16[4,192,384]{2,1,0:T(8,128)(2,1)S(1)} all-gather(bf16[4,48,384]{2,1,0:T(8,128)(2,1)S(1)} %split.7), channel_id=1, replica_groups=mesh['clip'=4,'seq'=4,'head'=2] {'seq'}, dimensions={1}, use_global_device_ids=true | all-gather | bytes 737280 | tf_op jit(solution)/shard_map/all_gather | solution.py:843
  67.5 21.8 %all_gather.13 = bf16[5,192,384]{2,1,0:T(8,128)(2,1)S(1)} all-gather(bf16[5,48,384]{2,1,0:T(8,128)(2,1)S(1)} %split.6), channel_id=1, replica_groups=mesh['clip'=4,'seq'=4,'head'=2] {'seq'}, dimensions={1}, use_global_device_ids=true | all-gather | bytes 921600 | tf_op jit(solution)/shard_map/all_gather | solution.py:843
  103.9 28.4 %collective-permute-done.3.refs_2_ = bf16[104,768]{1,0:T(8,128)(2,1)S(1)} collective-permute-done((bf16[104,768]{1,0:T(8,128)(2,1)}, bf16[104,768]{1,0:T(8,128)(2,1)S(1)}, u32[]{:S(2)}, u32[]{:S(2)}) %collective-permute-start.3) | collective-permute-done | bytes 159776 | tf_op jit(solution)/shard_map/ppermute | solution.py:809
  138.7 23.7 %collective-permute-done.9 = bf16[2,8,48,384]{3,2,1,0:T(8,128)(2,1)S(1)} collective-permute-done((bf16[2,8,48,384]{3,2,1,0:T(8,128)(2,1)S(1)}, bf16[2,8,48,384]{3,2,1,0:T(8,128)(2,1)S(1)}, u32[]{:S(2)}, u32[]{:S(2)}) %collective-permute-start.9) | collective-permute-done | bytes 589856 | tf_op jit(solution)/shard_map/ppermute | solution.py:1054
  176.7 15.9 %collective-permute-done.11 = bf16[8,48,384]{2,1,0:T(8,128)(2,1)S(1)} collective-permute-done((bf16[8,48,384]{2,1,0:T(8,128)(2,1)S(1)}, bf16[8,48,384]{2,1,0:T(8,128)(2,1)S(1)}, u32[]{:S(2)}, u32[]{:S(2)}) %collective-permute-start.11) | collective-permute-done | bytes 294944 | tf_op jit(solution)/shard_map/ppermute | solution.py:854
  192.6 17.6 %collective-permute-done.14.refs_3_ = bf16[4,8,48,384]{3,2,1,0:T(8,128)(2,1)} collective-permute-done((bf16[4,8,48,384]{3,2,1,0:T(8,128)(2,1)S(1)}, bf16[4,8,48,384]{3,2,1,0:T(8,128)(2,1)}, u32[]{:S(2)}, u32[]{:S(2)}) %collective-permute-start.14) | collective-permute-done | bytes 1179680 | tf_op jit(solution)/shard_map/ppermute | solution.py:1054
  212.0 12.4 %shard_map.195 = (bf16[416,768]{1,0:T(8,128)(2,1)}, bf16[3,416,768]{2,1,0:T(8,128)(2,1)}, f32[2,3,2,416]{3,2,1,0:T(2,128)}, bf16[104,768]{1,0:T(8,128)(2,1)}, bf...) custom-call(bf16[104,768]{1,0:T(8,128)(2,1)} %get-tuple-element.295.refs_0_, ...), custom_call_target="tpu_custom_call" | custom-call | flops 1472200704 | bytes 14470656 | tf_op jit(solution)/shard_map/pallas_call | solution.py:212
  239.8 9.3 %shard_map.196 = (bf16[416,768]{1,0:T(8,128)(2,1)}, bf16[416,768]{1,0:T(8,128)(2,1)}, f32[416,768]{1,0:T(8,128)}, bf16[3,416,768]{2,1,0:T(8,128)(2,1)}) custom-call(s32[5]{0:T(128)} %stack.110.me_ref, bf16[104,768]{1,0:T(8,128)(2,1)} %get-tuple-element.313.refs_0_, bf16[104,768]{1,0:T(8,128)(2,1)} %copy-done.44, bf16[104,768]{1,0:T(8,128)(2,1)} %copy-done.45, ...), custom_call_target="tpu_custom_call" | custom-call | flops 2453667840 | bytes 28821524 | tf_op jit(solution)/shard_map/pallas_call | solution.py:212
  249.2 9.9 %shard_map.197 = (bf16[416,768]{1,0:T(8,128)(2,1)}, f32[416,768]{1,0:T(8,128)}, f32[2,3,2,2,208]{4,3,2,1,0:T(2,128)}) custom-call(bf16[3,416,768]{2,1,0:T(8,128)(2,1)} %get-tuple-element.317.qkv_ref, f32[416,768]{1,0:T(8,128)} %get-tuple-element.318.x1_ref, bf16[9,2,768,384]{3,2,1,0:T(8,128)(2,1)} %bitcast.201), custom_call_target="tpu_custom_call" | custom-call | flops 490733568 | bytes 15748608 | tf_op jit(solution)/shard_map/pallas_call | solution.py:212
  261.7 8.2 %shard_map.198 = bf16[8,2,16,48,384]{4,3,2,1,0:T(8,128)(2,1)} custom-call(s32[5]{0:T(128)} %stack.110.me_ref, bf16[4,8,48,384]{3,2,1,0:T(8,128)(2,1)} %copy-done.21, bf16[4,8,48,384]{3,2,1,0:T(8,128)(2,1)} %collective-permute-done.13.refs_1_, bf16[4,8,48,384]{3,2,1,0:T(8,128)(2,1)} %copy-done.22, bf16[4,8,48,384]{3,2,1,0:T(8,128)(2,1)} %collective-permute-done.14.refs_3_, ...), custom_call_target="tpu_custom_call" | custom-call | bytes 18874368 | tf_op jit(solution)/shard_map/pallas_call | solution.py:889
  269.9 13.3 %shard_map.199 = (f32[416,768]{1,0:T(8,128)}, bf16[104,768]{1,0:T(8,128)(2,1)}, bf16[104,768]{1,0:T(8,128)(2,1)}, bf16[104,768]{1,0:T(8,128)(2,1)}, bf16[104,768]{1,0:T(8,128)(2,1)}) custom-call(f32[416,768]{1,0:T(8,128)} %get-tuple-element.324.x2_ref, bf16[8,2,768,384]{3,2,1,0:T(8,128)(2,1)} %bitcast.214, bf16[8,2,768,384]{3,2,1,0:T(8,128)(2,1)} %bitcast.215, ...), custom_call_target="tpu_custom_call" | custom-call | flops 3925868544 | bytes 22106132 | tf_op jit(solution)/shard_map/pallas_call | solution.py:212
  297.9 12.4 %shard_map.200 = (bf16[416,768]{1,0:T(8,128)(2,1)}, bf16[3,416,768]{2,1,0:T(8,128)(2,1)}, f32[2,3,2,416]{3,2,1,0:T(2,128)}, bf16[104,768]{1,0:T(8,128)(2,1)}, bf...) custom-call(bf16[104,768]{1,0:T(8,128)(2,1)} %get-tuple-element.336.refs_0_, ...), custom_call_target="tpu_custom_call" | custom-call | flops 1472200704 | bytes 14470656 | tf_op jit(solution)/shard_map/pallas_call | solution.py:212
  310.3 10.8 %collective-permute-start.29 = (bf16[104,768]{1,0:T(8,128)(2,1)}, bf16[104,768]{1,0:T(8,128)(2,1)S(1)}, u32[]{:S(2)}, u32[]{:S(2)}) collective-permute-start(bf16[104,768]{1,0:T(8,128)(2,1)} %get-tuple-element.342), channel_id=1, source_target_pairs={{0,8},{2,10},{4,12},{6,14},{8,0},{10,2},{12,4},{14,6},{16,24},{18,... | collective-permute-start | bytes 479240 | tf_op jit(solution)/shard_map/ppermute | solution.py:809
  321.1 8.4 %collective-permute-start.30 = (bf16[104,768]{1,0:T(8,128)(2,1)}, bf16[104,768]{1,0:T(8,128)(2,1)S(1)}, u32[]{:S(2)}, u32[]{:S(2)}) collective-permute-start(bf16[104,768]{1,0:T(8,128)(2,1)} %get-tuple-element.343), channel_id=1, source_target_pairs={{0,2},{2,0},{4,6},{6,4},{8,10},{10,8},{12,14},{14,12},{16,18},{18,... | collective-permute-start | bytes 479240 | tf_op jit(solution)/shard_map/ppermute | solution.py:809
  338.3 9.3 %shard_map.201 = (bf16[416,768]{1,0:T(8,128)(2,1)}, bf16[416,768]{1,0:T(8,128)(2,1)}, f32[416,768]{1,0:T(8,128)}, bf16[3,416,768]{2,1,0:T(8,128)(2,1)}) custom-call(s32[5]{0:T(128)} %stack.110.me_ref, bf16[104,768]{1,0:T(8,128)(2,1)} %get-tuple-element.347.refs_0_, bf16[104,768]{1,0:T(8,128)(2,1)} %copy-done.46, bf16[104,768]{1,0:T(8,128)(2,1)} %copy-done.48, ...), custom_call_target="tpu_custom_call" | custom-call | flops 2453667840 | bytes 28821524 | tf_op jit(solution)/shard_map/pallas_call | solution.py:212
  347.6 9.9 %shard_map.202 = (bf16[416,768]{1,0:T(8,128)(2,1)}, f32[416,768]{1,0:T(8,128)}, f32[2,3,2,2,208]{4,3,2,1,0:T(2,128)}) custom-call(bf16[3,416,768]{2,1,0:T(8,128)(2,1)} %get-tuple-element.352.qkv_ref, f32[416,768]{1,0:T(8,128)} %get-tuple-element.353.x1_ref, bf16[9,2,768,384]{3,2,1,0:T(8,128)(2,1)} %bitcast.209), custom_call_target="tpu_custom_call" | custom-call | flops 490733568 | bytes 15748608 | tf_op jit(solution)/shard_map/pallas_call | solution.py:212
  357.5 8.3 %shard_map.203 = bf16[8,2,16,48,384]{4,3,2,1,0:T(8,128)(2,1)} custom-call(s32[5]{0:T(128)} %stack.110.me_ref, bf16[4,8,48,384]{3,2,1,0:T(8,128)(2,1)} %copy-done.23, bf16[4,8,48,384]{3,2,1,0:T(8,128)(2,1)} %collective-permute-done.27.refs_1_, bf16[4,8,48,384]{3,2,1,0:T(8,128)(2,1)} %copy-done.24, bf16[4,8,48,384]{3,2,1,0:T(8,128)(2,1)} %collective-permute-done.28.refs_3_, ...), custom_call_target="tpu_custom_call" | custom-call | bytes 18874368 | tf_op jit(solution)/shard_map/pallas_call | solution.py:889
  365.8 25.3 %shard_map.204 = (f32[416,768]{1,0:T(8,128)}, bf16[4,2,2,192,384]{4,3,2,1,0:T(8,128)(2,1)}, bf16[4,2,2,192,384]{4,3,2,1,0:T(8,128)(2,1)}, bf16[4,2,2,192,384]{4,...) custom-call(s32[5]{0:T(128)} %stack.110.me_ref, ...), custom_call_target="tpu_custom_call" | custom-call | flops 9814671360 | bytes 33447956 | tf_op jit(solution)/shard_map/pallas_call | solution.py:212
  391.7 21.6 %shard_map.205 = (f32[416,768]{1,0:T(8,128)}, bf16[4,2,2,192,384]{4,3,2,1,0:T(8,128)(2,1)}, bf16[4,2,2,192,384]{4,3,2,1,0:T(8,128)(2,1)}, f32[2,768]{1,0:T(2,128)}) custom-call(s32[5]{0:T(128)} %stack.110.me_ref, f32[416,768]{1,0:T(8,128)} %get-tuple-element.359.g_ref, f32[416,768]{1,0:T(8,128)} %get-tuple-element.353.x1_ref, ...), custom_call_target="tpu_custom_call" | custom-call | flops 3925868544 | bytes 32386580 | tf_op jit(solution)/shard_map/pallas_call | solution.py:212
  432.7 10.3 %collective-permute-start.39 = (bf16[104,768]{1,0:T(8,128)(2,1)}, bf16[104,768]{1,0:T(8,128)(2,1)S(1)}, u32[]{:S(2)}, u32[]{:S(2)}) collective-permute-start(bf16[104,768]{1,0:T(8,128)(2,1)} %get-tuple-element.374), channel_id=1, source_target_pairs={{0,8},{2,10},{4,12},{6,14},{8,0},{10,2},{12,4},{14,6},{16,24},{18,... | collective-permute-start | bytes 479240 | tf_op jit(solution)/shard_map/ppermute | solution.py:809
  460.8 18.1 %shard_map.209 = (bf16[104,768]{1,0:T(8,128)(2,1)}, bf16[104,768]{1,0:T(8,128)(2,1)}, bf16[104,768]{1,0:T(8,128)(2,1)}, bf16[104,768]{1,0:T(8,128)(2,1)}, bf16[1...) custom-call(s32[5]{0:T(128)} %stack.110.me_ref, ...), custom_call_target="tpu_custom_call" | custom-call | flops 2944401408 | bytes 18009620 | tf_op jit(solution)/shard_map/pallas_call | solution.py:212
  481.5 15.9 %collective-permute-start.48 = (bf16[104,768]{1,0:T(8,128)(2,1)}, bf16[104,768]{1,0:T(8,128)(2,1)S(1)}, u32[]{:S(2)}, u32[]{:S(2)}) collective-permute-start(bf16[104,768]{1,0:T(8,128)(2,1)} %get-tuple-element.398), channel_id=1, source_target_pairs={{0,2},{2,0},{4,6},{6,4},{8,10},{10,8},{12,14},{14,12},{16,18},{18,... | collective-permute-start | bytes 479240 | tf_op jit(solution)/shard_map/ppermute | solution.py:809
  512.0 22.4 %shard_map.212 = (f32[416,768]{1,0:T(8,128)}, bf16[4,2,2,192,384]{4,3,2,1,0:T(8,128)(2,1)}, bf16[4,2,2,192,384]{4,3,2,1,0:T(8,128)(2,1)}, bf16[4,2,2,192,384]{4,...) custom-call(s32[5]{0:T(128)} %stack.110.me_ref, f32[416,768]{1,0:T(8,128)} %get-tuple-element.417.g_ref, ...), custom_call_target="tpu_custom_call" | custom-call | flops 9814671360 | bytes 32170004 | tf_op jit(solution)/shard_map/pallas_call | solution.py:212
  540.5 21.5 %shard_map.214 = (f32[416,768]{1,0:T(8,128)}, bf16[4,2,2,192,384]{4,3,2,1,0:T(8,128)(2,1)}, bf16[4,2,2,192,384]{4,3,2,1,0:T(8,128)(2,1)}, f32[2,768]{1,0:T(2,128)}) custom-call(s32[5]{0:T(128)} %stack.110.me_ref, f32[416,768]{1,0:T(8,128)} %get-tuple-element.427.g_ref, f32[416,768]{1,0:T(8,128)} %get-tuple-element.318.x1_ref, ...), custom_call_target="tpu_custom_call" | custom-call | flops 3925868544 | bytes 32386580 | tf_op jit(solution)/shard_map/pallas_call | solution.py:212
  564.9 8.0 %collective-permute-done.57.refs_17_ = bf16[2,192,384]{2,1,0:T(8,128)(2,1)S(1)} collective-permute-done((bf16[2,192,384]{2,1,0:T(8,128)(2,1)S(1)}, bf16[2,192,384]{2,1,0:T(8,128)(2,1)S(1)}, u32[]{:S(2)}, u32[]{:S(2)}) %collective-permute-start.57) | collective-permute-done | bytes 294944 | tf_op jit(solution)/shard_map/ppermute | solution.py:1054
  582.0 7.8 %shard_map.216 = (bf16[104,768]{1,0:T(8,128)(2,1)}, bf16[104,768]{1,0:T(8,128)(2,1)}, bf16[104,768]{1,0:T(8,128)(2,1)}, bf16[104,768]{1,0:T(8,128)(2,1)}, bf16[2...) custom-call(s32[5]{0:T(128)} %stack.110.me_ref, f32[416,768]{1,0:T(8,128)} %get-tuple-element.442.g_ref.refs_5_, ...), custom_call_target="tpu_custom_call" | custom-call | flops 1962934272 | bytes 17350676 | tf_op jit(solution)/shard_map/pallas_call | solution.py:212
  591.7 15.9 %collective-permute-done.63.refs_2_ = bf16[8,192,384]{2,1,0:T(8,128)(2,1)S(1)} collective-permute-done((bf16[8,192,384]{2,1,0:T(8,128)(2,1)}, bf16[8,192,384]{2,1,0:T(8,128)(2,1)S(1)}, u32[]{:S(2)}, u32[]{:S(2)}) %collective-permute-start.63) | collective-permute-done | bytes 1179680 | tf_op jit(solution)/shard_map/ppermute | solution.py:1054
  617.9 18.3 %shard_map.218 = (bf16[104,768]{1,0:T(8,128)(2,1)}, bf16[104,768]{1,0:T(8,128)(2,1)}, bf16[104,768]{1,0:T(8,128)(2,1)}, bf16[104,768]{1,0:T(8,128)(2,1)}, bf16[1...) custom-call(s32[5]{0:T(128)} %stack.110.me_ref, ...), custom_call_target="tpu_custom_call" | custom-call | flops 2944401408 | bytes 18009620 | tf_op jit(solution)/shard_map/pallas_call | solution.py:212
  672.7 28.9 %all-to-all-done.1 = f32[32,1,384]{2,1,0:T(1,128)} async-done(((f32[32,1,384]{2,1,0:T(1,128)}), f32[32,1,384]{2,1,0:T(1,128)}, u32[]{:S(2)}, u32[]{:S(2)}) %all-to-all-start.1) | async-done | bytes 49184 | tf_op jit(solution)/shard_map/all_to_all | solution.py:1142
  741.6 13.3 %all-to-all-done.2 = bf16[4,5,48,384]{3,2,1,0:T(8,128)(2,1)S(1)} async-done(((bf16[4,5,48,384]{3,2,1,0:T(8,128)(2,1)}), bf16[4,5,48,384]{3,2,1,0:T(8,128)(2,1)S(1)}, u32[]{:S(2)}, u32[]{:S(2)}) %all-to-all-start.2) | async-done | bytes 737312 | tf_op jit(solution)/shard_map/all_to_all | solution.py:1080
  (457 shorter events, 249.3 us)
Async XLA Ops:
  7.2 204.8 %all-gather.3.cloned.1.call-start = ((), (), s32[]{:S(2)}) async-start(), calls=%async_computation.8 | async-start | bytes 10948608 | tf_op jit(solution)/shard_map/all_gather | solution.py:838
  11.0 32.4 %collective-permute-start.1 = (bf16[1,2,196,768]{3,1,2,0:T(2,128)(2,1)S(1)}, bf16[1,2,196,768]{3,1,2,0:T(2,128)(2,1)S(1)}, u32[]{:S(2)}, u32[]{:S(2)}) collective-permute-start(bf16[1,2,196,768]{3,1,2,0:T(2,128)(2,1)S(1)} %copy-done.74), channel_id=1, source_target_pairs={{0,0},{2,8},{4,2},{6,10},{8,4},{10,12},{12,6},{14,14},{16,16},{18,... | collective-permute-start | bytes 1806344 | tf_op jit(solution)/shard_map/ppermute | solution.py:787
  12.5 29.1 %all-to-all-start = ((f32[32,1,384]{2,1,0:T(1,128)}), f32[32,1,384]{2,1,0:T(1,128)S(1)}, u32[]{:S(2)}, u32[]{:S(2)}) async-start(f32[32,1,384]{2,1,0:T(1,128)} %broadcast_in_dim.17), calls=%async_computation | async-start | bytes 98304 | tf_op jit(solution)/shard_map/all_to_all | solution.py:1129
  21.3 276.6 %all-gather.5.cloned.1.call-start = ((), (), s32[]{:S(2)}) async-start(), calls=%async_computation.9 | async-start | bytes 11943936 | tf_op jit(solution)/shard_map/all_gather | solution.py:844
  90.6 564.7 %reduce-scatter.7.cloned.1.call-start = ((), (), s32[]{:S(2)}) async-start(), calls=%async_computation.11 | async-start | bytes 737280 | tf_op jit(solution)/shard_map/reduce_scatter | solution.py:1083
  96.5 39.1 %collective-permute-start.7 = (bf16[8,48,384]{2,1,0:T(8,128)(2,1)S(1)}, bf16[8,48,384]{2,1,0:T(8,128)(2,1)S(1)}, u32[]{:S(2)}, u32[]{:S(2)}) collective-permute-start(bf16[8,48,384]{2,1,0:T(8,128)(2,1)S(1)} %pad_maximum_fusion.13), channel_id=1, source_target_pairs={{0,6},{2,0},{4,2},{6,4},{1,7},{3,1},{5,3},{7,5},{8,14},{10,8},{12,... | collective-permute-start | bytes 884744 | tf_op jit(solution)/shard_map/ppermute | solution.py:854
  100.4 36.2 %collective-permute-start.6 = (bf16[8,48,384]{2,1,0:T(8,128)(2,1)S(1)}, bf16[8,48,384]{2,1,0:T(8,128)(2,1)S(1)}, u32[]{:S(2)}, u32[]{:S(2)}) collective-permute-start(bf16[8,48,384]{2,1,0:T(8,128)(2,1)S(1)} %pad_maximum_fusion.13), channel_id=1, source_target_pairs={{0,4},{2,6},{4,0},{6,2},{1,5},{3,7},{5,1},{7,3},{8,12},{10,14},{12... | collective-permute-start | bytes 884744 | tf_op jit(solution)/shard_map/ppermute | solution.py:854
  100.4 36.2 %collective-permute-start.5 = (bf16[8,48,384]{2,1,0:T(8,128)(2,1)S(1)}, bf16[8,48,384]{2,1,0:T(8,128)(2,1)S(1)}, u32[]{:S(2)}, u32[]{:S(2)}) collective-permute-start(bf16[8,48,384]{2,1,0:T(8,128)(2,1)S(1)} %pad_maximum_fusion.13), channel_id=1, source_target_pairs={{0,2},{2,4},{4,6},{6,0},{1,3},{3,5},{5,7},{7,1},{8,10},{10,12},{12... | collective-permute-start | bytes 884744 | tf_op jit(solution)/shard_map/ppermute | solution.py:854
  101.1 31.3 %collective-permute-start.3 = (bf16[104,768]{1,0:T(8,128)(2,1)}, bf16[104,768]{1,0:T(8,128)(2,1)S(1)}, u32[]{:S(2)}, u32[]{:S(2)}) collective-permute-start(bf16[104,768]{1,0:T(8,128)(2,1)} %get-tuple-element.269), channel_id=1, source_target_pairs={{0,2},{2,0},{4,6},{6,4},{8,10},{10,8},{12,14},{14,12},{16,18},{18,... | collective-permute-start | bytes 479240 | tf_op jit(solution)/shard_map/ppermute | solution.py:809
  103.9 31.7 %collective-permute-start.4 = (bf16[104,768]{1,0:T(8,128)(2,1)}, bf16[104,768]{1,0:T(8,128)(2,1)S(1)}, u32[]{:S(2)}, u32[]{:S(2)}) collective-permute-start(bf16[104,768]{1,0:T(8,128)(2,1)} %get-tuple-element.270), channel_id=1, source_target_pairs={{0,10},{2,8},{4,14},{6,12},{8,2},{10,0},{12,6},{14,4},{16,26},{18,... | collective-permute-start | bytes 479240 | tf_op jit(solution)/shard_map/ppermute | solution.py:809
  164.5 45.7 %collective-permute-start.14 = (bf16[4,8,48,384]{3,2,1,0:T(8,128)(2,1)S(1)}, bf16[4,8,48,384]{3,2,1,0:T(8,128)(2,1)}, u32[]{:S(2)}, u32[]{:S(2)}) collective-permute-start(bf16[4,8,48,384]{3,2,1,0:T(8,128)(2,1)S(1)} %pad_maximum_fusion.2.refs_2_), channel_id=1, source_target_pairs={{0,16},{8,24},{16,0},{24,8},{1,17},{9,25},{17,1},{25,9},{2,18},{10... | collective-permute-start | bytes 3538952 | tf_op jit(solution)/shard_map/ppermute | solution.py:1054
  166.8 44.6 %collective-permute-start.13 = (bf16[4,8,48,384]{3,2,1,0:T(8,128)(2,1)S(1)}, bf16[4,8,48,384]{3,2,1,0:T(8,128)(2,1)}, u32[]{:S(2)}, u32[]{:S(2)}) collective-permute-start(bf16[4,8,48,384]{3,2,1,0:T(8,128)(2,1)S(1)} %pad_maximum_fusion.1.refs_0_), channel_id=1, source_target_pairs={{0,1},{1,0},{2,3},{3,2},{4,5},{5,4},{6,7},{7,6},{8,9},{9,8},{10,11... | collective-permute-start | bytes 3538952 | tf_op jit(solution)/shard_map/ppermute | solution.py:1054
  176.7 47.7 %collective-permute-start.20 = (bf16[4,8,48,384]{3,2,1,0:T(8,128)(2,1)S(1)}, bf16[4,8,48,384]{3,2,1,0:T(8,128)(2,1)}, u32[]{:S(2)}, u32[]{:S(2)}) collective-permute-start(bf16[4,8,48,384]{3,2,1,0:T(8,128)(2,1)S(1)} %pad_maximum_fusion.2.refs_2_), channel_id=1, source_target_pairs={{0,8},{8,0},{16,24},{24,16},{1,9},{9,1},{17,25},{25,17},{2,10},{10... | collective-permute-start | bytes 3538952 | tf_op jit(solution)/shard_map/ppermute | solution.py:1054
  192.6 33.4 %collective-permute-start.18 = (bf16[4,8,48,384]{3,2,1,0:T(8,128)(2,1)S(1)}, bf16[4,8,48,384]{3,2,1,0:T(8,128)(2,1)}, u32[]{:S(2)}, u32[]{:S(2)}) collective-permute-start(bf16[4,8,48,384]{3,2,1,0:T(8,128)(2,1)S(1)} %pad_maximum_fusion.1.refs_0_), channel_id=1, source_target_pairs={{0,8},{8,0},{16,24},{24,16},{1,9},{9,1},{17,25},{25,17},{2,10},{10... | collective-permute-start | bytes 3538952 | tf_op jit(solution)/shard_map/ppermute | solution.py:1054
  259.4 37.0 %collective-permute-start.28 = (bf16[4,8,48,384]{3,2,1,0:T(8,128)(2,1)S(1)}, bf16[4,8,48,384]{3,2,1,0:T(8,128)(2,1)}, u32[]{:S(2)}, u32[]{:S(2)}) collective-permute-start(bf16[4,8,48,384]{3,2,1,0:T(8,128)(2,1)S(1)} %pad_maximum_fusion.4.refs_2_), channel_id=1, source_target_pairs={{0,16},{8,24},{16,0},{24,8},{1,17},{9,25},{17,1},{25,9},{2,18},{10... | collective-permute-start | bytes 3538952 | tf_op jit(solution)/shard_map/ppermute | solution.py:1054
  260.8 35.7 %collective-permute-start.27 = (bf16[4,8,48,384]{3,2,1,0:T(8,128)(2,1)S(1)}, bf16[4,8,48,384]{3,2,1,0:T(8,128)(2,1)}, u32[]{:S(2)}, u32[]{:S(2)}) collective-permute-start(bf16[4,8,48,384]{3,2,1,0:T(8,128)(2,1)S(1)} %pad_maximum_fusion.3.refs_0_), channel_id=1, source_target_pairs={{0,1},{1,0},{2,3},{3,2},{4,5},{5,4},{6,7},{7,6},{8,9},{9,8},{10,11... | collective-permute-start | bytes 3538952 | tf_op jit(solution)/shard_map/ppermute | solution.py:1054
  284.8 36.3 %collective-permute-start.34 = (bf16[4,8,48,384]{3,2,1,0:T(8,128)(2,1)S(1)}, bf16[4,8,48,384]{3,2,1,0:T(8,128)(2,1)}, u32[]{:S(2)}, u32[]{:S(2)}) collective-permute-start(bf16[4,8,48,384]{3,2,1,0:T(8,128)(2,1)S(1)} %pad_maximum_fusion.4.refs_2_), channel_id=1, source_target_pairs={{0,8},{8,0},{16,24},{24,16},{1,9},{9,1},{17,25},{25,17},{2,10},{10... | collective-permute-start | bytes 3538952 | tf_op jit(solution)/shard_map/ppermute | solution.py:1054
  284.9 44.6 %collective-permute-start.32 = (bf16[4,8,48,384]{3,2,1,0:T(8,128)(2,1)S(1)}, bf16[4,8,48,384]{3,2,1,0:T(8,128)(2,1)}, u32[]{:S(2)}, u32[]{:S(2)}) collective-permute-start(bf16[4,8,48,384]{3,2,1,0:T(8,128)(2,1)S(1)} %pad_maximum_fusion.3.refs_0_), channel_id=1, source_target_pairs={{0,8},{8,0},{16,24},{24,16},{1,9},{9,1},{17,25},{25,17},{2,10},{10... | collective-permute-start | bytes 3538952 | tf_op jit(solution)/shard_map/ppermute | solution.py:1054
  296.4 41.2 %collective-permute-start.33 = (bf16[4,8,48,384]{3,2,1,0:T(8,128)(2,1)}, bf16[4,8,48,384]{3,2,1,0:T(8,128)(2,1)}, u32[]{:S(2)}, u32[]{:S(2)}) collective-permute-start(bf16[4,8,48,384]{3,2,1,0:T(8,128)(2,1)} %collective-permute-done.27.refs_1_), channel_id=1, source_target_pairs={{0,8},{8,0},{16,24},{24,16},{1,9},{9,1},{17,25},{25,17},{2,10},{10... | collective-permute-start | bytes 3538952 | tf_op jit(solution)/shard_map/ppermute | solution.py:1054
  296.6 41.0 %collective-permute-start.35 = (bf16[4,8,48,384]{3,2,1,0:T(8,128)(2,1)}, bf16[4,8,48,384]{3,2,1,0:T(8,128)(2,1)}, u32[]{:S(2)}, u32[]{:S(2)}) collective-permute-start(bf16[4,8,48,384]{3,2,1,0:T(8,128)(2,1)} %collective-permute-done.28.refs_3_), channel_id=1, source_target_pairs={{0,8},{8,0},{16,24},{24,16},{1,9},{9,1},{17,25},{25,17},{2,10},{10... | collective-permute-start | bytes 3538952 | tf_op jit(solution)/shard_map/ppermute | solution.py:1054
  413.3 29.9 %collective-permute-start.44 = (bf16[4,2,2,192,384]{4,3,2,1,0:T(8,128)(2,1)}, bf16[4,2,2,192,384]{4,3,2,1,0:T(8,128)(2,1)S(1)}, u32[]{:S(2)}, u32[]{:S(2)}) collective-permute-start(bf16[4,2,2,192,384]{4,3,2,1,0:T(8,128)(2,1)} %get-tuple-element.380), channel_id=1, source_target_pairs={{0,8},{8,0},{16,24},{24,16},{1,9},{9,1},{17,25},{25,17},{2,10},{10... | collective-permute-start | bytes 7077896 | tf_op jit(solution)/shard_map/ppermute | solution.py:1054
  505.5 29.5 %collective-permute-start.54 = (bf16[6,192,384]{2,1,0:T(8,128)(2,1)}, bf16[6,192,384]{2,1,0:T(8,128)(2,1)S(1)}, u32[]{:S(2)}, u32[]{:S(2)}) collective-permute-start(bf16[6,192,384]{2,1,0:T(8,128)(2,1)} %get-tuple-element.419), channel_id=1, source_target_pairs={{0,1},{1,0},{2,3},{3,2},{4,5},{5,4},{6,7},{7,6},{8,9},{9,8},{10,11... | collective-permute-start | bytes 2654216 | tf_op jit(solution)/shard_map/ppermute | solution.py:1054
  534.4 40.8 %collective-permute-start.58 = (bf16[4,2,2,192,384]{4,3,2,1,0:T(8,128)(2,1)}, bf16[4,2,2,192,384]{4,3,2,1,0:T(8,128)(2,1)}, u32[]{:S(2)}, u32[]{:S(2)}) collective-permute-start(bf16[4,2,2,192,384]{4,3,2,1,0:T(8,128)(2,1)} %get-tuple-element.436), channel_id=1, source_target_pairs={{0,8},{8,0},{16,24},{24,16},{1,9},{9,1},{17,25},{25,17},{2,10},{10... | collective-permute-start | bytes 7077896 | tf_op jit(solution)/shard_map/ppermute | solution.py:1054
  534.5 40.7 %collective-permute-start.59 = (bf16[4,2,2,192,384]{4,3,2,1,0:T(8,128)(2,1)}, bf16[4,2,2,192,384]{4,3,2,1,0:T(8,128)(2,1)}, u32[]{:S(2)}, u32[]{:S(2)}) collective-permute-start(bf16[4,2,2,192,384]{4,3,2,1,0:T(8,128)(2,1)} %get-tuple-element.438), channel_id=1, source_target_pairs={{0,8},{8,0},{16,24},{24,16},{1,9},{9,1},{17,25},{25,17},{2,10},{10... | collective-permute-start | bytes 7077896 | tf_op jit(solution)/shard_map/ppermute | solution.py:1054
  540.5 131.3 %reduce-scatter.11.cloned.1.call-start = ((), (), s32[]{:S(2)}) async-start(), calls=%async_computation.13 | async-start | bytes 1474560 | tf_op jit(solution)/shard_map/reduce_scatter | solution.py:1083
  562.0 29.3 %collective-permute-start.65 = (bf16[4,2,2,192,384]{4,3,2,1,0:T(8,128)(2,1)}, bf16[4,2,2,192,384]{4,3,2,1,0:T(8,128)(2,1)S(1)}, u32[]{:S(2)}, u32[]{:S(2)}) collective-permute-start(bf16[4,2,2,192,384]{4,3,2,1,0:T(8,128)(2,1)} %get-tuple-element.452), channel_id=1, source_target_pairs={{0,8},{8,0},{16,24},{24,16},{1,9},{9,1},{17,25},{25,17},{2,10},{10... | collective-permute-start | bytes 7077896 | tf_op jit(solution)/shard_map/ppermute | solution.py:1054
  562.2 151.1 %reduce-scatter.5.cloned.1.call-start = ((), (), s32[]{:S(2)}) async-start(), calls=%async_computation.10 | async-start | bytes 921600 | tf_op jit(solution)/shard_map/reduce_scatter | solution.py:1083
  617.8 120.7 %reduce-scatter.9.cloned.1.call-start = ((), (), s32[]{:S(2)}) async-start(), calls=%async_computation.12 | async-start | bytes 1474560 | tf_op jit(solution)/shard_map/reduce_scatter | solution.py:1083
  652.9 50.3 %collective-permute-start.77 = (bf16[8,192,384]{2,1,0:T(8,128)(2,1)}, bf16[8,192,384]{2,1,0:T(8,128)(2,1)S(1)}, u32[]{:S(2)}, u32[]{:S(2)}) collective-permute-start(bf16[8,192,384]{2,1,0:T(8,128)(2,1)} %get-tuple-element.500), channel_id=1, source_target_pairs={{0,16},{8,24},{16,0},{24,8},{1,17},{9,25},{17,1},{25,9},{2,18},{10... | collective-permute-start | bytes 3538952 | tf_op jit(solution)/shard_map/ppermute | solution.py:1054
  654.1 49.1 %collective-permute-start.76 = (bf16[6,192,384]{2,1,0:T(8,128)(2,1)}, bf16[6,192,384]{2,1,0:T(8,128)(2,1)S(1)}, u32[]{:S(2)}, u32[]{:S(2)}) collective-permute-start(bf16[6,192,384]{2,1,0:T(8,128)(2,1)} %get-tuple-element.499), channel_id=1, source_target_pairs={{0,1},{1,0},{2,3},{3,2},{4,5},{5,4},{6,7},{7,6},{8,9},{9,8},{10,11... | collective-permute-start | bytes 2654216 | tf_op jit(solution)/shard_map/ppermute | solution.py:1054
  663.4 46.0 %collective-permute-start.75 = (bf16[1,2,196,768]{3,1,2,0:T(2,128)(2,1)}, bf16[1,2,196,768]{3,1,2,0:T(2,128)(2,1)S(1)}, u32[]{:S(2)}, u32[]{:S(2)}) collective-permute-start(bf16[1,2,196,768]{3,1,2,0:T(2,128)(2,1)} %bitcast.189), channel_id=1, source_target_pairs={{0,0},{8,2},{2,4},{10,6},{4,8},{12,10},{6,12},{14,14},{16,16},{24,... | collective-permute-start | bytes 1806344 | tf_op jit(solution)/shard_map/ppermute | solution.py:791
  667.9 33.8 %all-to-all-start.1 = ((f32[32,1,384]{2,1,0:T(1,128)}), f32[32,1,384]{2,1,0:T(1,128)}, u32[]{:S(2)}, u32[]{:S(2)}) async-start(f32[32,1,384]{2,1,0:T(1,128)} %copy.125), calls=%async_computation.1 | async-start | bytes 98304 | tf_op jit(solution)/shard_map/all_to_all | solution.py:1142
  (137 other events, 1515.3 us)
Sparse Core Ops, SparseCore 0:
  11.7 106.6 all-gather.2
  120.3 101.8 all-gather.4
  540.6 20.0 reduce-scatter.6
  562.9 27.4 reduce-scatter.10
  617.9 20.8 reduce-scatter.4
  665.3 34.4 reduce-scatter.8

commit v19 on v18

--- a/solution.py
+++ b/solution.py
@@ -1179,10 +1179,8 @@
         for l in range(layers)
     ]
     packs_ff = [pack_feed_forward(mlp_in[l], mlp_out[l], time_qkv.shape[3]) for l in range(layers)]
+    weights = [gather_slabs(packs[0])]
     home = go_home(tokens)
-    gb, home, packs[1:] = lax.optimization_barrier((gb, home, packs[1:]))
-    weights = [gather_slabs(packs[0])] + [gather_slabs_later(pack) for pack in packs[1:]]
-    mixes = [mix_whole(w[-1], shards) for w in weights]
     quick = lax.axis_size("clip") == 4 and shares == 2 and ways == 4 and time_qkv.shape[1] % 16 == 0
 
     halves = Halves(lax.axis_size("clip"), d, time_qkv.shape[3])
@@ -1201,33 +1199,36 @@
         first = spreads[0]
         home, gb = first.step((home, gb))
     x = as_rows(home)
-    send = send_first(rows, x, gb[0], me)
+    send = swap_places(send_first(rows, x, gb[0], me))
+    if quick:
+        send, packs[1:] = first.step((send, packs[1:]))
+    weights += [gather_slabs_later(pack) for pack in packs[1:]]
+    mixes = [mix_whole(w[-1], shards) for w in weights]
     kept = []
     for l in range(layers):
         w = weights[l]
-        send = swap_places(send)
+        if l:
+            send = swap_places(send)
         if quick and l == 0:
-            for _ in range(2):
-                send = first.step(send)
             for spread in spreads[1:]:
                 send = spread.step(send)
+            send = first.step(send)
+            for spread in spreads[1:]:
                 send = spread.hold(send)
-            send = first.step(send)
-        elif quick:
-            send = spreads[l].step(send)
         a1, qkv1, log1, o1_time = time_forward(rows, send, w)
         back = swap_places(o1_time)
         if quick:
-            back = spreads[l].step(back)
+            for spread in spreads[1:]:
+                back = spread.step(back)
+        o1, y1, x1, qkv2 = middle_forward(rows, back, x, w, mixes[l], gb[l], me)
+        o2, x2, log2 = space_forward(rows, qkv2, x1, w)
+        if quick:
+            for _ in range(1 if l else 2):
+                x2 = spreads[l].step(x2)
             weights_ff.append(spreads[l].come)
             if l == 0:
                 for spread in spreads[1:]:
-                    back = spread.step(back)
-        o1, y1, x1, qkv2 = middle_forward(rows, back, x, w, mixes[l], gb[l], me)
-        o2, x2, log2 = space_forward(rows, qkv2, x1, w)
-        if quick and l == 0:
-            for spread in spreads[1:]:
-                x2 = spread.step(x2)
+                    x2 = spread.step(x2)
         kept.append((x, a1, qkv1, log1, o1, y1, x1, qkv2, o2, log2, x2))
         if l + 1 < layers:
             x, *send = mlp_forward(rows, x2, weights_ff[l], gb[l], gb[l + 1], me)

time: 771 us -> 765 us (level)
  waiting for transfers between devices: 221 us -> 194 us
  starting transfers between devices: 132 us -> 142 us
    all_to_all x1, waiting for transfers between devices: 20.2 us -> 5.55 us  [gather_norms(): lax.all_to_all(jnp.broadcast_to(padded, (count, width)), ALL, split_axis=...]
    ppermute x46, waiting for transfers between devices: 81.6 us -> 68.9 us  [cross(): return lax.ppermute(a, axis, [(i, i ^ 1 << bit) for i in range(size)])]
    ppermute x46, starting transfers between devices: 38.9 us -> 51.1 us  [cross(): return lax.ppermute(a, axis, [(i, i ^ 1 << bit) for i in range(size)])]
    ppermute x24, starting transfers between devices: 59.1 us -> 51 us  [swap_places(): got.append(lax.ppermute(chunks[k], ('clip', 'seq'), pairs))]
    unnamed x171 -> x185, local copies, waits for them, and re-layouts: 23.4 us -> 25.5 us
  transfers between devices with their start and end apart: 90 -> 90, of which waited for: 27 -> 32; matrix products, arithmetic and copies ran while one was open for 5% -> 5% of each run, Pallas kernels for 31% -> 34%
where the time goes in v19:
time: 765 us; the launch traced here: 759 us
  Pallas kernels  293 us (38%)
  waiting for transfers between devices  194 us (25%)
  starting transfers between devices  142 us (19%)
  blocking collectives  52.4 us (7%)
  local copies, waits for them, and re-layouts  41 us (5%)
  other arithmetic  21.5 us (3%)
  between operations  15.9 us (2%)
    pallas_call x18, Pallas kernels, call(): pl.pallas_call(body, out_shape=[shape for shape, _ in outs], grid=grid, i...  231 us
    ppermute x46, waiting for transfers between devices, cross(): return lax.ppermute(a, axis, [(i, i ^ 1 << bit) for i in range(size)])  68.9 us
    all_gather x2, blocking collectives, gather_slabs_later(): lax.all_gather(a, 'seq', axis=1, tiled=True)  52.4 us
    ppermute x46, starting transfers between devices, cross(): return lax.ppermute(a, axis, [(i, i ^ 1 << bit) for i in range(size)])  51.1 us
    ppermute x24, starting transfers between devices, swap_places(): got.append(lax.ppermute(chunks[k], ('clip', 'seq'), pairs))  51 us
    ppermute x24, waiting for transfers between devices, swap_places(): got.append(lax.ppermute(chunks[k], ('clip', 'seq'), pairs))  50.3 us
    pallas_call x9, Pallas kernels, fold(): pl.pallas_call(body, out_shape=[jax.ShapeDtypeStruct(shape, BF16) for sha...  45.6 us
    all_to_all x1, waiting for transfers between devices, reduce_norms(): every = lax.all_to_all(a, ALL, split_axis=0, concat_axis=0, tiled=True)  29.3 us
  transfers between devices with their start and end apart: 90, of which 32 were waited for; matrix products, arithmetic and copies ran while one was open for 5% of the time, Pallas kernels for 34%

profile of v19, /device:TPU:0, one launch (start us, length us, event | category | flops | bytes accessed | tf_op | source)
XLA Modules:
  0.0 759.4 jit_solution(2127969105038216218)
XLA Ops:
  42.4 9.6 %collective-permute-start.6 = (bf16[8,48,384]{2,1,0:T(8,128)(2,1)S(1)}, bf16[8,48,384]{2,1,0:T(8,128)(2,1)S(1)}, u32[]{:S(2)}, u32[]{:S(2)}) collective-permute-start(bf16[8,48,384]{2,1,0:T(8,128)(2,1)S(1)} %pad_maximum_fusion.13), channel_id=1, source_target_pairs={{0,4},{2,6},{4,0},{6,2},{1,5},{3,7},{5,1},{7,3},{8,12},{10,14},{12... | collective-permute-start | bytes 884744 | tf_op jit(solution)/shard_map/ppermute | solution.py:854
  53.4 26.6 %collective-permute-done.3.refs_2_ = bf16[104,768]{1,0:T(8,128)(2,1)S(1)} collective-permute-done((bf16[104,768]{1,0:T(8,128)(2,1)}, bf16[104,768]{1,0:T(8,128)(2,1)S(1)}, u32[]{:S(2)}, u32[]{:S(2)}) %collective-permute-start.3) | collective-permute-done | bytes 159776 | tf_op jit(solution)/shard_map/ppermute | solution.py:809
  83.2 8.0 %collective-permute-done.6 = bf16[8,48,384]{2,1,0:T(8,128)(2,1)S(1)} collective-permute-done((bf16[8,48,384]{2,1,0:T(8,128)(2,1)S(1)}, bf16[8,48,384]{2,1,0:T(8,128)(2,1)S(1)}, u32[]{:S(2)}, u32[]{:S(2)}) %collective-permute-start.6) | collective-permute-done | bytes 294944 | tf_op jit(solution)/shard_map/ppermute | solution.py:854
  91.3 24.1 %all_gather.14 = bf16[4,192,384]{2,1,0:T(8,128)(2,1)S(1)} all-gather(bf16[4,48,384]{2,1,0:T(8,128)(2,1)S(1)} %split.7), channel_id=1, replica_groups=mesh['clip'=4,'seq'=4,'head'=2] {'seq'}, dimensions={1}, use_global_device_ids=true | all-gather | bytes 737280 | tf_op jit(solution)/shard_map/all_gather | solution.py:843
  115.3 28.3 %all_gather.13 = bf16[5,192,384]{2,1,0:T(8,128)(2,1)S(1)} all-gather(bf16[5,48,384]{2,1,0:T(8,128)(2,1)S(1)} %split.6), channel_id=1, replica_groups=mesh['clip'=4,'seq'=4,'head'=2] {'seq'}, dimensions={1}, use_global_device_ids=true | all-gather | bytes 921600 | tf_op jit(solution)/shard_map/all_gather | solution.py:843
  148.1 10.5 %collective-permute-done.9 = bf16[2,8,48,384]{3,2,1,0:T(8,128)(2,1)} collective-permute-done((bf16[2,8,48,384]{3,2,1,0:T(8,128)(2,1)S(1)}, bf16[2,8,48,384]{3,2,1,0:T(8,128)(2,1)}, u32[]{:S(2)}, u32[]{:S(2)}) %collective-permute-start.9) | collective-permute-done | bytes 589856 | tf_op jit(solution)/shard_map/ppermute | solution.py:1054
  172.0 8.3 %collective-permute-done.12 = bf16[8,48,384]{2,1,0:T(8,128)(2,1)S(1)} collective-permute-done((bf16[8,48,384]{2,1,0:T(8,128)(2,1)S(1)}, bf16[8,48,384]{2,1,0:T(8,128)(2,1)S(1)}, u32[]{:S(2)}, u32[]{:S(2)}) %collective-permute-start.12) | collective-permute-done | bytes 294944 | tf_op jit(solution)/shard_map/ppermute | solution.py:854
  180.3 10.0 %collective-permute-done.11 = bf16[8,48,384]{2,1,0:T(8,128)(2,1)S(1)} collective-permute-done((bf16[8,48,384]{2,1,0:T(8,128)(2,1)S(1)}, bf16[8,48,384]{2,1,0:T(8,128)(2,1)S(1)}, u32[]{:S(2)}, u32[]{:S(2)}) %collective-permute-start.11) | collective-permute-done | bytes 294944 | tf_op jit(solution)/shard_map/ppermute | solution.py:854
  190.3 12.2 %shard_map.195 = (bf16[416,768]{1,0:T(8,128)(2,1)}, bf16[3,416,768]{2,1,0:T(8,128)(2,1)}, f32[2,3,2,416]{3,2,1,0:T(2,128)}, bf16[104,768]{1,0:T(8,128)(2,1)}, bf...) custom-call(bf16[104,768]{1,0:T(8,128)(2,1)} %get-tuple-element.274.refs_0_, ...), custom_call_target="tpu_custom_call" | custom-call | flops 1472200704 | bytes 14470656 | tf_op jit(solution)/shard_map/pallas_call | solution.py:212
  212.7 9.5 %shard_map.196 = (bf16[416,768]{1,0:T(8,128)(2,1)}, bf16[416,768]{1,0:T(8,128)(2,1)}, f32[416,768]{1,0:T(8,128)}, bf16[3,416,768]{2,1,0:T(8,128)(2,1)}) custom-call(s32[5]{0:T(128)} %stack.110.me_ref, bf16[104,768]{1,0:T(8,128)(2,1)} %get-tuple-element.286.refs_0_, bf16[104,768]{1,0:T(8,128)(2,1)} %copy-done.55, bf16[104,768]{1,0:T(8,128)(2,1)} %copy-done.56, ...), custom_call_target="tpu_custom_call" | custom-call | flops 2453667840 | bytes 28821524 | tf_op jit(solution)/shard_map/pallas_call | solution.py:212
  222.1 9.9 %shard_map.197 = (bf16[416,768]{1,0:T(8,128)(2,1)}, f32[416,768]{1,0:T(8,128)}, f32[2,3,2,2,208]{4,3,2,1,0:T(2,128)}) custom-call(bf16[3,416,768]{2,1,0:T(8,128)(2,1)} %get-tuple-element.290.qkv_ref, f32[416,768]{1,0:T(8,128)} %get-tuple-element.291.x1_ref, bf16[9,2,768,384]{3,2,1,0:T(8,128)(2,1)} %bitcast.201), custom_call_target="tpu_custom_call" | custom-call | flops 490733568 | bytes 15748608 | tf_op jit(solution)/shard_map/pallas_call | solution.py:212
  237.5 11.5 %collective-permute-done.23 = bf16[2,8,48,384]{3,2,1,0:T(8,128)(2,1)S(1)} collective-permute-done((bf16[2,8,48,384]{3,2,1,0:T(8,128)(2,1)S(1)}, bf16[2,8,48,384]{3,2,1,0:T(8,128)(2,1)S(1)}, u32[]{:S(2)}, u32[]{:S(2)}) %collective-permute-start.23) | collective-permute-done | bytes 589856 | tf_op jit(solution)/shard_map/ppermute | solution.py:1054
  253.0 8.2 %shard_map.198 = bf16[8,2,16,48,384]{4,3,2,1,0:T(8,128)(2,1)} custom-call(s32[5]{0:T(128)} %stack.110.me_ref, bf16[4,8,48,384]{3,2,1,0:T(8,128)(2,1)} %copy-done.21, bf16[4,8,48,384]{3,2,1,0:T(8,128)(2,1)} %collective-permute-done.16.refs_1_, bf16[4,8,48,384]{3,2,1,0:T(8,128)(2,1)} %copy-done.23, bf16[4,8,48,384]{3,2,1,0:T(8,128)(2,1)} %collective-permute-done.17.refs_3_, ...), custom_call_target="tpu_custom_call" | custom-call | bytes 18874368 | tf_op jit(solution)/shard_map/pallas_call | solution.py:889
  261.1 13.2 %shard_map.199 = (f32[416,768]{1,0:T(8,128)}, bf16[104,768]{1,0:T(8,128)(2,1)}, bf16[104,768]{1,0:T(8,128)(2,1)}, bf16[104,768]{1,0:T(8,128)(2,1)}, bf16[104,768]{1,0:T(8,128)(2,1)}) custom-call(f32[416,768]{1,0:T(8,128)} %get-tuple-element.303.x2_ref, bf16[8,2,768,384]{3,2,1,0:T(8,128)(2,1)} %bitcast.214, bf16[8,2,768,384]{3,2,1,0:T(8,128)(2,1)} %bitcast.215, ...), custom_call_target="tpu_custom_call" | custom-call | flops 3925868544 | bytes 22106132 | tf_op jit(solution)/shard_map/pallas_call | solution.py:212
  284.8 12.5 %shard_map.200 = (bf16[416,768]{1,0:T(8,128)(2,1)}, bf16[3,416,768]{2,1,0:T(8,128)(2,1)}, f32[2,3,2,416]{3,2,1,0:T(2,128)}, bf16[104,768]{1,0:T(8,128)(2,1)}, bf...) custom-call(bf16[104,768]{1,0:T(8,128)(2,1)} %get-tuple-element.309.refs_0_, ...), custom_call_target="tpu_custom_call" | custom-call | flops 1472200704 | bytes 14470656 | tf_op jit(solution)/shard_map/pallas_call | solution.py:212
  314.1 9.4 %shard_map.201 = (bf16[416,768]{1,0:T(8,128)(2,1)}, bf16[416,768]{1,0:T(8,128)(2,1)}, f32[416,768]{1,0:T(8,128)}, bf16[3,416,768]{2,1,0:T(8,128)(2,1)}) custom-call(s32[5]{0:T(128)} %stack.110.me_ref, bf16[104,768]{1,0:T(8,128)(2,1)} %get-tuple-element.320.refs_0_, bf16[104,768]{1,0:T(8,128)(2,1)} %copy-done.49, bf16[104,768]{1,0:T(8,128)(2,1)} %copy-done.50, ...), custom_call_target="tpu_custom_call" | custom-call | flops 2453667840 | bytes 28821524 | tf_op jit(solution)/shard_map/pallas_call | solution.py:212
  323.5 10.3 %shard_map.202 = (bf16[416,768]{1,0:T(8,128)(2,1)}, f32[416,768]{1,0:T(8,128)}, f32[2,3,2,2,208]{4,3,2,1,0:T(2,128)}) custom-call(bf16[3,416,768]{2,1,0:T(8,128)(2,1)} %get-tuple-element.325.qkv_ref, f32[416,768]{1,0:T(8,128)} %get-tuple-element.326.x1_ref, bf16[9,2,768,384]{3,2,1,0:T(8,128)(2,1)} %bitcast.209), custom_call_target="tpu_custom_call" | custom-call | flops 490733568 | bytes 15748608 | tf_op jit(solution)/shard_map/pallas_call | solution.py:212
  335.9 8.2 %shard_map.203 = bf16[8,2,16,48,384]{4,3,2,1,0:T(8,128)(2,1)} custom-call(s32[5]{0:T(128)} %stack.110.me_ref, bf16[4,8,48,384]{3,2,1,0:T(8,128)(2,1)} %copy-done.22, bf16[4,8,48,384]{3,2,1,0:T(8,128)(2,1)} %collective-permute-done.30.refs_1_, bf16[4,8,48,384]{3,2,1,0:T(8,128)(2,1)} %copy-done.24, bf16[4,8,48,384]{3,2,1,0:T(8,128)(2,1)} %collective-permute-done.31.refs_3_, ...), custom_call_target="tpu_custom_call" | custom-call | bytes 18874368 | tf_op jit(solution)/shard_map/pallas_call | solution.py:889
  344.2 25.0 %shard_map.204 = (f32[416,768]{1,0:T(8,128)}, bf16[4,2,2,192,384]{4,3,2,1,0:T(8,128)(2,1)}, bf16[4,2,2,192,384]{4,3,2,1,0:T(8,128)(2,1)}, bf16[4,2,2,192,384]{4,...) custom-call(s32[5]{0:T(128)} %stack.110.me_ref, ...), custom_call_target="tpu_custom_call" | custom-call | flops 9814671360 | bytes 33447956 | tf_op jit(solution)/shard_map/pallas_call | solution.py:212
  369.2 10.3 %collective-permute-start.37 = (bf16[4,2,2,192,384]{4,3,2,1,0:T(8,128)(2,1)}, bf16[4,2,2,192,384]{4,3,2,1,0:T(8,128)(2,1)S(1)}, u32[]{:S(2)}, u32[]{:S(2)}) collective-permute-start(bf16[4,2,2,192,384]{4,3,2,1,0:T(8,128)(2,1)} %get-tuple-element.341), channel_id=1, source_target_pairs={{0,8},{8,0},{16,24},{24,16},{1,9},{9,1},{17,25},{25,17},{2,10},{10... | collective-permute-start | bytes 7077896 | tf_op jit(solution)/shard_map/ppermute | solution.py:1054
  379.5 21.5 %shard_map.205 = (f32[416,768]{1,0:T(8,128)}, bf16[4,2,2,192,384]{4,3,2,1,0:T(8,128)(2,1)}, bf16[4,2,2,192,384]{4,3,2,1,0:T(8,128)(2,1)}, f32[2,768]{1,0:T(2,128)}) custom-call(s32[5]{0:T(128)} %stack.110.me_ref, f32[416,768]{1,0:T(8,128)} %get-tuple-element.335.g_ref, f32[416,768]{1,0:T(8,128)} %get-tuple-element.326.x1_ref, ...), custom_call_target="tpu_custom_call" | custom-call | flops 3925868544 | bytes 32386580 | tf_op jit(solution)/shard_map/pallas_call | solution.py:212
  413.0 7.8 %shard_map.207 = (bf16[104,768]{1,0:T(8,128)(2,1)}, bf16[104,768]{1,0:T(8,128)(2,1)}, bf16[104,768]{1,0:T(8,128)(2,1)}, bf16[104,768]{1,0:T(8,128)(2,1)}, bf16[2...) custom-call(s32[5]{0:T(128)} %stack.110.me_ref, f32[416,768]{1,0:T(8,128)} %get-tuple-element.346.g_ref.refs_5_, ...), custom_call_target="tpu_custom_call" | custom-call | flops 1962934272 | bytes 17350676 | tf_op jit(solution)/shard_map/pallas_call | solution.py:212
  420.8 16.1 %collective-permute-start.39 = (bf16[104,768]{1,0:T(8,128)(2,1)}, bf16[104,768]{1,0:T(8,128)(2,1)S(1)}, u32[]{:S(2)}, u32[]{:S(2)}) collective-permute-start(bf16[104,768]{1,0:T(8,128)(2,1)} %get-tuple-element.350), channel_id=1, source_target_pairs={{0,8},{2,10},{4,12},{6,14},{8,0},{10,2},{12,4},{14,6},{16,24},{18,... | collective-permute-start | bytes 479240 | tf_op jit(solution)/shard_map/ppermute | solution.py:809
  451.4 18.1 %shard_map.209 = (bf16[104,768]{1,0:T(8,128)(2,1)}, bf16[104,768]{1,0:T(8,128)(2,1)}, bf16[104,768]{1,0:T(8,128)(2,1)}, bf16[104,768]{1,0:T(8,128)(2,1)}, bf16[1...) custom-call(s32[5]{0:T(128)} %stack.110.me_ref, ...), custom_call_target="tpu_custom_call" | custom-call | flops 2944401408 | bytes 18009620 | tf_op jit(solution)/shard_map/pallas_call | solution.py:212
  475.2 16.6 %collective-permute-start.48 = (bf16[104,768]{1,0:T(8,128)(2,1)}, bf16[104,768]{1,0:T(8,128)(2,1)S(1)}, u32[]{:S(2)}, u32[]{:S(2)}) collective-permute-start(bf16[104,768]{1,0:T(8,128)(2,1)} %get-tuple-element.374), channel_id=1, source_target_pairs={{0,2},{2,0},{4,6},{6,4},{8,10},{10,8},{12,14},{14,12},{16,18},{18,... | collective-permute-start | bytes 479240 | tf_op jit(solution)/shard_map/ppermute | solution.py:809
  505.7 22.3 %shard_map.212 = (f32[416,768]{1,0:T(8,128)}, bf16[4,2,2,192,384]{4,3,2,1,0:T(8,128)(2,1)}, bf16[4,2,2,192,384]{4,3,2,1,0:T(8,128)(2,1)}, bf16[4,2,2,192,384]{4,...) custom-call(s32[5]{0:T(128)} %stack.110.me_ref, f32[416,768]{1,0:T(8,128)} %get-tuple-element.393.g_ref, ...), custom_call_target="tpu_custom_call" | custom-call | flops 9814671360 | bytes 32170004 | tf_op jit(solution)/shard_map/pallas_call | solution.py:212
  534.2 21.5 %shard_map.214 = (f32[416,768]{1,0:T(8,128)}, bf16[4,2,2,192,384]{4,3,2,1,0:T(8,128)(2,1)}, bf16[4,2,2,192,384]{4,3,2,1,0:T(8,128)(2,1)}, f32[2,768]{1,0:T(2,128)}) custom-call(s32[5]{0:T(128)} %stack.110.me_ref, f32[416,768]{1,0:T(8,128)} %get-tuple-element.403.g_ref, f32[416,768]{1,0:T(8,128)} %get-tuple-element.291.x1_ref, ...), custom_call_target="tpu_custom_call" | custom-call | flops 3925868544 | bytes 32386580 | tf_op jit(solution)/shard_map/pallas_call | solution.py:212
  576.4 7.8 %shard_map.216 = (bf16[104,768]{1,0:T(8,128)(2,1)}, bf16[104,768]{1,0:T(8,128)(2,1)}, bf16[104,768]{1,0:T(8,128)(2,1)}, bf16[104,768]{1,0:T(8,128)(2,1)}, bf16[2...) custom-call(s32[5]{0:T(128)} %stack.110.me_ref, f32[416,768]{1,0:T(8,128)} %get-tuple-element.418.g_ref.refs_5_, ...), custom_call_target="tpu_custom_call" | custom-call | flops 1962934272 | bytes 17350676 | tf_op jit(solution)/shard_map/pallas_call | solution.py:212
  586.1 15.1 %collective-permute-done.63.refs_2_ = bf16[8,192,384]{2,1,0:T(8,128)(2,1)S(1)} collective-permute-done((bf16[8,192,384]{2,1,0:T(8,128)(2,1)}, bf16[8,192,384]{2,1,0:T(8,128)(2,1)S(1)}, u32[]{:S(2)}, u32[]{:S(2)}) %collective-permute-start.63) | collective-permute-done | bytes 1179680 | tf_op jit(solution)/shard_map/ppermute | solution.py:1054
  611.7 18.3 %shard_map.218 = (bf16[104,768]{1,0:T(8,128)(2,1)}, bf16[104,768]{1,0:T(8,128)(2,1)}, bf16[104,768]{1,0:T(8,128)(2,1)}, bf16[104,768]{1,0:T(8,128)(2,1)}, bf16[1...) custom-call(s32[5]{0:T(128)} %stack.110.me_ref, ...), custom_call_target="tpu_custom_call" | custom-call | flops 2944401408 | bytes 18009620 | tf_op jit(solution)/shard_map/pallas_call | solution.py:212
  666.6 29.3 %all-to-all-done.1 = f32[32,1,384]{2,1,0:T(1,128)} async-done(((f32[32,1,384]{2,1,0:T(1,128)}), f32[32,1,384]{2,1,0:T(1,128)}, u32[]{:S(2)}, u32[]{:S(2)}) %all-to-all-start.1) | async-done | bytes 49184 | tf_op jit(solution)/shard_map/all_to_all | solution.py:1142
  735.7 13.4 %all-to-all-done.2 = bf16[4,5,48,384]{3,2,1,0:T(8,128)(2,1)S(1)} async-done(((bf16[4,5,48,384]{3,2,1,0:T(8,128)(2,1)}), bf16[4,5,48,384]{3,2,1,0:T(8,128)(2,1)S(1)}, u32[]{:S(2)}, u32[]{:S(2)}) %all-to-all-start.2) | async-done | bytes 737312 | tf_op jit(solution)/shard_map/all_to_all | solution.py:1080
  (471 shorter events, 270.0 us)
Async XLA Ops:
  7.2 183.1 %all-gather.3.cloned.1.call-start = ((), (), s32[]{:S(2)}) async-start(), calls=%async_computation.8 | async-start | bytes 10948608 | tf_op jit(solution)/shard_map/all_gather | solution.py:838
  19.1 257.1 %all-gather.5.cloned.1.call-start = ((), (), s32[]{:S(2)}) async-start(), calls=%async_computation.9 | async-start | bytes 11943936 | tf_op jit(solution)/shard_map/all_gather | solution.py:844
  39.4 43.8 %collective-permute-start.7 = (bf16[8,48,384]{2,1,0:T(8,128)(2,1)S(1)}, bf16[8,48,384]{2,1,0:T(8,128)(2,1)S(1)}, u32[]{:S(2)}, u32[]{:S(2)}) collective-permute-start(bf16[8,48,384]{2,1,0:T(8,128)(2,1)S(1)} %pad_maximum_fusion.13), channel_id=1, source_target_pairs={{0,6},{2,0},{4,2},{6,4},{1,7},{3,1},{5,3},{7,5},{8,14},{10,8},{12,... | collective-permute-start | bytes 884744 | tf_op jit(solution)/shard_map/ppermute | solution.py:854
  42.4 48.8 %collective-permute-start.6 = (bf16[8,48,384]{2,1,0:T(8,128)(2,1)S(1)}, bf16[8,48,384]{2,1,0:T(8,128)(2,1)S(1)}, u32[]{:S(2)}, u32[]{:S(2)}) collective-permute-start(bf16[8,48,384]{2,1,0:T(8,128)(2,1)S(1)} %pad_maximum_fusion.13), channel_id=1, source_target_pairs={{0,4},{2,6},{4,0},{6,2},{1,5},{3,7},{5,1},{7,3},{8,12},{10,14},{12... | collective-permute-start | bytes 884744 | tf_op jit(solution)/shard_map/ppermute | solution.py:854
  52.1 39.2 %collective-permute-start.5 = (bf16[8,48,384]{2,1,0:T(8,128)(2,1)S(1)}, bf16[8,48,384]{2,1,0:T(8,128)(2,1)S(1)}, u32[]{:S(2)}, u32[]{:S(2)}) collective-permute-start(bf16[8,48,384]{2,1,0:T(8,128)(2,1)S(1)} %pad_maximum_fusion.13), channel_id=1, source_target_pairs={{0,2},{2,4},{4,6},{6,0},{1,3},{3,5},{5,7},{7,1},{8,10},{10,12},{12... | collective-permute-start | bytes 884744 | tf_op jit(solution)/shard_map/ppermute | solution.py:854
  52.5 27.5 %collective-permute-start.3 = (bf16[104,768]{1,0:T(8,128)(2,1)}, bf16[104,768]{1,0:T(8,128)(2,1)S(1)}, u32[]{:S(2)}, u32[]{:S(2)}) collective-permute-start(bf16[104,768]{1,0:T(8,128)(2,1)} %get-tuple-element.254), channel_id=1, source_target_pairs={{0,2},{2,0},{4,6},{6,4},{8,10},{10,8},{12,14},{14,12},{16,18},{18,... | collective-permute-start | bytes 479240 | tf_op jit(solution)/shard_map/ppermute | solution.py:809
  52.6 30.6 %collective-permute-start.4 = (bf16[104,768]{1,0:T(8,128)(2,1)}, bf16[104,768]{1,0:T(8,128)(2,1)S(1)}, u32[]{:S(2)}, u32[]{:S(2)}) collective-permute-start(bf16[104,768]{1,0:T(8,128)(2,1)} %get-tuple-element.255), channel_id=1, source_target_pairs={{0,10},{2,8},{4,14},{6,12},{8,2},{10,0},{12,6},{14,4},{16,26},{18,... | collective-permute-start | bytes 479240 | tf_op jit(solution)/shard_map/ppermute | solution.py:809
  144.9 504.4 %reduce-scatter.7.cloned.1.call-start = ((), (), s32[]{:S(2)}) async-start(), calls=%async_computation.11 | async-start | bytes 737280 | tf_op jit(solution)/shard_map/reduce_scatter | solution.py:1083
  167.1 64.9 %collective-permute-start.17 = (bf16[4,8,48,384]{3,2,1,0:T(8,128)(2,1)S(1)}, bf16[4,8,48,384]{3,2,1,0:T(8,128)(2,1)}, u32[]{:S(2)}, u32[]{:S(2)}) collective-permute-start(bf16[4,8,48,384]{3,2,1,0:T(8,128)(2,1)S(1)} %pad_maximum_fusion.2.refs_2_), channel_id=1, source_target_pairs={{0,16},{8,24},{16,0},{24,8},{1,17},{9,25},{17,1},{25,9},{2,18},{10... | collective-permute-start | bytes 3538952 | tf_op jit(solution)/shard_map/ppermute | solution.py:1054
  169.8 62.3 %collective-permute-start.16 = (bf16[4,8,48,384]{3,2,1,0:T(8,128)(2,1)S(1)}, bf16[4,8,48,384]{3,2,1,0:T(8,128)(2,1)}, u32[]{:S(2)}, u32[]{:S(2)}) collective-permute-start(bf16[4,8,48,384]{3,2,1,0:T(8,128)(2,1)S(1)} %pad_maximum_fusion.1.refs_0_), channel_id=1, source_target_pairs={{0,1},{1,0},{2,3},{3,2},{4,5},{5,4},{6,7},{7,6},{8,9},{9,8},{10,11... | collective-permute-start | bytes 3538952 | tf_op jit(solution)/shard_map/ppermute | solution.py:1054
  202.7 32.2 %collective-permute-start.20 = (bf16[4,8,48,384]{3,2,1,0:T(8,128)(2,1)S(1)}, bf16[4,8,48,384]{3,2,1,0:T(8,128)(2,1)S(1)}, u32[]{:S(2)}, u32[]{:S(2)}) collective-permute-start(bf16[4,8,48,384]{3,2,1,0:T(8,128)(2,1)S(1)} %pad_maximum_fusion.2.refs_2_), channel_id=1, source_target_pairs={{0,8},{8,0},{16,24},{24,16},{1,9},{9,1},{17,25},{25,17},{2,10},{10... | collective-permute-start | bytes 3538952 | tf_op jit(solution)/shard_map/ppermute | solution.py:1054
  250.7 56.0 %collective-permute-start.31 = (bf16[4,8,48,384]{3,2,1,0:T(8,128)(2,1)S(1)}, bf16[4,8,48,384]{3,2,1,0:T(8,128)(2,1)}, u32[]{:S(2)}, u32[]{:S(2)}) collective-permute-start(bf16[4,8,48,384]{3,2,1,0:T(8,128)(2,1)S(1)} %pad_maximum_fusion.4.refs_2_), channel_id=1, source_target_pairs={{0,16},{8,24},{16,0},{24,8},{1,17},{9,25},{17,1},{25,9},{2,18},{10... | collective-permute-start | bytes 3538952 | tf_op jit(solution)/shard_map/ppermute | solution.py:1054
  251.4 55.3 %collective-permute-start.30 = (bf16[4,8,48,384]{3,2,1,0:T(8,128)(2,1)S(1)}, bf16[4,8,48,384]{3,2,1,0:T(8,128)(2,1)}, u32[]{:S(2)}, u32[]{:S(2)}) collective-permute-start(bf16[4,8,48,384]{3,2,1,0:T(8,128)(2,1)S(1)} %pad_maximum_fusion.3.refs_0_), channel_id=1, source_target_pairs={{0,1},{1,0},{2,3},{3,2},{4,5},{5,4},{6,7},{7,6},{8,9},{9,8},{10,11... | collective-permute-start | bytes 3538952 | tf_op jit(solution)/shard_map/ppermute | solution.py:1054
  299.2 34.6 %collective-permute-start.34 = (bf16[4,8,48,384]{3,2,1,0:T(8,128)(2,1)S(1)}, bf16[4,8,48,384]{3,2,1,0:T(8,128)(2,1)S(1)}, u32[]{:S(2)}, u32[]{:S(2)}) collective-permute-start(bf16[4,8,48,384]{3,2,1,0:T(8,128)(2,1)S(1)} %pad_maximum_fusion.4.refs_2_), channel_id=1, source_target_pairs={{0,8},{8,0},{16,24},{24,16},{1,9},{9,1},{17,25},{25,17},{2,10},{10... | collective-permute-start | bytes 3538952 | tf_op jit(solution)/shard_map/ppermute | solution.py:1054
  304.7 29.1 %collective-permute-start.32 = (bf16[4,8,48,384]{3,2,1,0:T(8,128)(2,1)S(1)}, bf16[4,8,48,384]{3,2,1,0:T(8,128)(2,1)S(1)}, u32[]{:S(2)}, u32[]{:S(2)}) collective-permute-start(bf16[4,8,48,384]{3,2,1,0:T(8,128)(2,1)S(1)} %pad_maximum_fusion.3.refs_0_), channel_id=1, source_target_pairs={{0,8},{8,0},{16,24},{24,16},{1,9},{9,1},{17,25},{25,17},{2,10},{10... | collective-permute-start | bytes 3538952 | tf_op jit(solution)/shard_map/ppermute | solution.py:1054
  369.2 35.0 %collective-permute-start.37 = (bf16[4,2,2,192,384]{4,3,2,1,0:T(8,128)(2,1)}, bf16[4,2,2,192,384]{4,3,2,1,0:T(8,128)(2,1)S(1)}, u32[]{:S(2)}, u32[]{:S(2)}) collective-permute-start(bf16[4,2,2,192,384]{4,3,2,1,0:T(8,128)(2,1)} %get-tuple-element.341), channel_id=1, source_target_pairs={{0,8},{8,0},{16,24},{24,16},{1,9},{9,1},{17,25},{25,17},{2,10},{10... | collective-permute-start | bytes 7077896 | tf_op jit(solution)/shard_map/ppermute | solution.py:1054
  401.0 36.7 %collective-permute-start.44 = (bf16[4,2,2,192,384]{4,3,2,1,0:T(8,128)(2,1)}, bf16[4,2,2,192,384]{4,3,2,1,0:T(8,128)(2,1)S(1)}, u32[]{:S(2)}, u32[]{:S(2)}) collective-permute-start(bf16[4,2,2,192,384]{4,3,2,1,0:T(8,128)(2,1)} %get-tuple-element.356), channel_id=1, source_target_pairs={{0,8},{8,0},{16,24},{24,16},{1,9},{9,1},{17,25},{25,17},{2,10},{10... | collective-permute-start | bytes 7077896 | tf_op jit(solution)/shard_map/ppermute | solution.py:1054
  446.3 28.3 %collective-permute-start.46 = (bf16[8,192,384]{2,1,0:T(8,128)(2,1)}, bf16[8,192,384]{2,1,0:T(8,128)(2,1)S(1)}, u32[]{:S(2)}, u32[]{:S(2)}) collective-permute-start(bf16[8,192,384]{2,1,0:T(8,128)(2,1)} %get-tuple-element.371), channel_id=1, source_target_pairs={{0,16},{8,24},{16,0},{24,8},{1,17},{9,25},{17,1},{25,9},{2,18},{10... | collective-permute-start | bytes 3538952 | tf_op jit(solution)/shard_map/ppermute | solution.py:1054
  446.6 28.6 %collective-permute-start.50 = (bf16[2,2,2,192,384]{4,3,2,1,0:T(8,128)(2,1)S(1)}, bf16[2,2,2,192,384]{4,3,2,1,0:T(8,128)(2,1)S(1)}, u32[]{:S(2)}, u32[]{:S(2)}) collective-permute-start(bf16[2,2,2,192,384]{4,3,2,1,0:T(8,128)(2,1)S(1)} %copy-done.81), channel_id=1, source_target_pairs={{0,8},{8,0},{16,24},{24,16},{1,9},{9,1},{17,25},{25,17},{2,10},{10... | collective-permute-start | bytes 3538952 | tf_op jit(solution)/shard_map/ppermute | solution.py:1054
  499.9 28.7 %collective-permute-start.54 = (bf16[6,192,384]{2,1,0:T(8,128)(2,1)}, bf16[6,192,384]{2,1,0:T(8,128)(2,1)S(1)}, u32[]{:S(2)}, u32[]{:S(2)}) collective-permute-start(bf16[6,192,384]{2,1,0:T(8,128)(2,1)} %get-tuple-element.395), channel_id=1, source_target_pairs={{0,1},{1,0},{2,3},{3,2},{4,5},{5,4},{6,7},{7,6},{8,9},{9,8},{10,11... | collective-permute-start | bytes 2654216 | tf_op jit(solution)/shard_map/ppermute | solution.py:1054
  500.3 28.3 %collective-permute-start.55 = (bf16[8,192,384]{2,1,0:T(8,128)(2,1)}, bf16[8,192,384]{2,1,0:T(8,128)(2,1)S(1)}, u32[]{:S(2)}, u32[]{:S(2)}) collective-permute-start(bf16[8,192,384]{2,1,0:T(8,128)(2,1)} %get-tuple-element.396), channel_id=1, source_target_pairs={{0,16},{8,24},{16,0},{24,8},{1,17},{9,25},{17,1},{25,9},{2,18},{10... | collective-permute-start | bytes 3538952 | tf_op jit(solution)/shard_map/ppermute | solution.py:1054
  528.0 40.8 %collective-permute-start.58 = (bf16[4,2,2,192,384]{4,3,2,1,0:T(8,128)(2,1)}, bf16[4,2,2,192,384]{4,3,2,1,0:T(8,128)(2,1)}, u32[]{:S(2)}, u32[]{:S(2)}) collective-permute-start(bf16[4,2,2,192,384]{4,3,2,1,0:T(8,128)(2,1)} %get-tuple-element.412), channel_id=1, source_target_pairs={{0,8},{8,0},{16,24},{24,16},{1,9},{9,1},{17,25},{25,17},{2,10},{10... | collective-permute-start | bytes 7077896 | tf_op jit(solution)/shard_map/ppermute | solution.py:1054
  528.1 40.8 %collective-permute-start.59 = (bf16[4,2,2,192,384]{4,3,2,1,0:T(8,128)(2,1)}, bf16[4,2,2,192,384]{4,3,2,1,0:T(8,128)(2,1)}, u32[]{:S(2)}, u32[]{:S(2)}) collective-permute-start(bf16[4,2,2,192,384]{4,3,2,1,0:T(8,128)(2,1)} %get-tuple-element.414), channel_id=1, source_target_pairs={{0,8},{8,0},{16,24},{24,16},{1,9},{9,1},{17,25},{25,17},{2,10},{10... | collective-permute-start | bytes 7077896 | tf_op jit(solution)/shard_map/ppermute | solution.py:1054
  534.1 131.5 %reduce-scatter.11.cloned.1.call-start = ((), (), s32[]{:S(2)}) async-start(), calls=%async_computation.13 | async-start | bytes 1474560 | tf_op jit(solution)/shard_map/reduce_scatter | solution.py:1083
  555.7 30.0 %collective-permute-start.65 = (bf16[4,2,2,192,384]{4,3,2,1,0:T(8,128)(2,1)}, bf16[4,2,2,192,384]{4,3,2,1,0:T(8,128)(2,1)S(1)}, u32[]{:S(2)}, u32[]{:S(2)}) collective-permute-start(bf16[4,2,2,192,384]{4,3,2,1,0:T(8,128)(2,1)} %get-tuple-element.428), channel_id=1, source_target_pairs={{0,8},{8,0},{16,24},{24,16},{1,9},{9,1},{17,25},{25,17},{2,10},{10... | collective-permute-start | bytes 7077896 | tf_op jit(solution)/shard_map/ppermute | solution.py:1054
  555.9 151.7 %reduce-scatter.5.cloned.1.call-start = ((), (), s32[]{:S(2)}) async-start(), calls=%async_computation.10 | async-start | bytes 921600 | tf_op jit(solution)/shard_map/reduce_scatter | solution.py:1083
  573.8 27.5 %collective-permute-start.63 = (bf16[8,192,384]{2,1,0:T(8,128)(2,1)}, bf16[8,192,384]{2,1,0:T(8,128)(2,1)S(1)}, u32[]{:S(2)}, u32[]{:S(2)}) collective-permute-start(bf16[8,192,384]{2,1,0:T(8,128)(2,1)} %get-tuple-element.425), channel_id=1, source_target_pairs={{0,16},{8,24},{16,0},{24,8},{1,17},{9,25},{17,1},{25,9},{2,18},{10... | collective-permute-start | bytes 3538952 | tf_op jit(solution)/shard_map/ppermute | solution.py:1054
  611.6 121.0 %reduce-scatter.9.cloned.1.call-start = ((), (), s32[]{:S(2)}) async-start(), calls=%async_computation.12 | async-start | bytes 1474560 | tf_op jit(solution)/shard_map/reduce_scatter | solution.py:1083
  646.5 50.9 %collective-permute-start.77 = (bf16[8,192,384]{2,1,0:T(8,128)(2,1)}, bf16[8,192,384]{2,1,0:T(8,128)(2,1)S(1)}, u32[]{:S(2)}, u32[]{:S(2)}) collective-permute-start(bf16[8,192,384]{2,1,0:T(8,128)(2,1)} %get-tuple-element.476), channel_id=1, source_target_pairs={{0,16},{8,24},{16,0},{24,8},{1,17},{9,25},{17,1},{25,9},{2,18},{10... | collective-permute-start | bytes 3538952 | tf_op jit(solution)/shard_map/ppermute | solution.py:1054
  647.7 49.7 %collective-permute-start.76 = (bf16[6,192,384]{2,1,0:T(8,128)(2,1)}, bf16[6,192,384]{2,1,0:T(8,128)(2,1)S(1)}, u32[]{:S(2)}, u32[]{:S(2)}) collective-permute-start(bf16[6,192,384]{2,1,0:T(8,128)(2,1)} %get-tuple-element.475), channel_id=1, source_target_pairs={{0,1},{1,0},{2,3},{3,2},{4,5},{5,4},{6,7},{7,6},{8,9},{9,8},{10,11... | collective-permute-start | bytes 2654216 | tf_op jit(solution)/shard_map/ppermute | solution.py:1054
  657.5 46.2 %collective-permute-start.75 = (bf16[1,2,196,768]{3,1,2,0:T(2,128)(2,1)}, bf16[1,2,196,768]{3,1,2,0:T(2,128)(2,1)S(1)}, u32[]{:S(2)}, u32[]{:S(2)}) collective-permute-start(bf16[1,2,196,768]{3,1,2,0:T(2,128)(2,1)} %bitcast.189), channel_id=1, source_target_pairs={{0,0},{8,2},{2,4},{10,6},{4,8},{12,10},{6,12},{14,14},{16,16},{24,... | collective-permute-start | bytes 1806344 | tf_op jit(solution)/shard_map/ppermute | solution.py:791
  661.9 34.0 %all-to-all-start.1 = ((f32[32,1,384]{2,1,0:T(1,128)}), f32[32,1,384]{2,1,0:T(1,128)}, u32[]{:S(2)}, u32[]{:S(2)}) async-start(f32[32,1,384]{2,1,0:T(1,128)} %copy.125), calls=%async_computation.1 | async-start | bytes 98304 | tf_op jit(solution)/shard_map/all_to_all | solution.py:1142
  (144 other events, 1592.9 us)
Sparse Core Ops, SparseCore 0:
  11.7 134.0 all-gather.2
  147.7 81.0 all-gather.4
  534.3 20.7 reduce-scatter.6
  557.2 27.5 reduce-scatter.10
  611.7 21.1 reduce-scatter.4
  659.3 34.3 reduce-scatter.8

commit v20 on v19

--- a/solution.py
+++ b/solution.py
@@ -1209,20 +1209,21 @@
         w = weights[l]
         if l:
             send = swap_places(send)
-        if quick and l == 0:
-            for spread in spreads[1:]:
-                send = spread.step(send)
-            send = first.step(send)
-            for spread in spreads[1:]:
-                send = spread.hold(send)
+        if quick and l:
+            send = spreads[l].step(send)
         a1, qkv1, log1, o1_time = time_forward(rows, send, w)
         back = swap_places(o1_time)
         if quick:
-            for spread in spreads[1:]:
-                back = spread.step(back)
+            back = spreads[l].step(back)
+            if l == 0:
+                for spread in spreads[1:]:
+                    back = spread.step(back)
         o1, y1, x1, qkv2 = middle_forward(rows, back, x, w, mixes[l], gb[l], me)
         o2, x2, log2 = space_forward(rows, qkv2, x1, w)
         if quick:
+            if l == 0:
+                for spread in spreads[1:]:
+                    x2 = spread.hold(x2)
             for _ in range(1 if l else 2):
                 x2 = spreads[l].step(x2)
             weights_ff.append(spreads[l].come)

time: 765 us -> 750 us (0.980)
  waiting for transfers between devices: 194 us -> 180 us
    ppermute x6, waiting for transfers between devices: 26.4 us -> 7.4 us  [spread_steps(): lax.ppermute(pack, 'seq', [(i, (i + k) % ways) for i in range(ways)])]
    unnamed x185 -> x187, local copies, waits for them, and re-layouts: 25.5 us -> 26 us
  transfers between devices with their start and end apart: 90 -> 90, of which waited for: 32 -> 31; matrix products, arithmetic and copies ran while one was open for 5% -> 5% of each run, Pallas kernels for 34% -> 35%
where the time goes in v20:
time: 750 us; the launch traced here: 740 us
  Pallas kernels  293 us (39%)
  waiting for transfers between devices  180 us (24%)
  starting transfers between devices  137 us (18%)
  blocking collectives  52.2 us (7%)
  local copies, waits for them, and re-layouts  42.1 us (6%)
  other arithmetic  20.1 us (3%)
  between operations  15.9 us (2%)
    pallas_call x18, Pallas kernels, call(): pl.pallas_call(body, out_shape=[shape for shape, _ in outs], grid=grid, i...  231 us
    ppermute x46, waiting for transfers between devices, cross(): return lax.ppermute(a, axis, [(i, i ^ 1 << bit) for i in range(size)])  71.6 us
    ppermute x24, waiting for transfers between devices, swap_places(): got.append(lax.ppermute(chunks[k], ('clip', 'seq'), pairs))  53.6 us
    all_gather x2, blocking collectives, gather_slabs_later(): lax.all_gather(a, 'seq', axis=1, tiled=True)  52.2 us
    ppermute x24, starting transfers between devices, swap_places(): got.append(lax.ppermute(chunks[k], ('clip', 'seq'), pairs))  50.5 us
    ppermute x46, starting transfers between devices, cross(): return lax.ppermute(a, axis, [(i, i ^ 1 << bit) for i in range(size)])  45.9 us
    pallas_call x9, Pallas kernels, fold(): pl.pallas_call(body, out_shape=[jax.ShapeDtypeStruct(shape, BF16) for sha...  45.6 us
    all_to_all x1, waiting for transfers between devices, reduce_norms(): every = lax.all_to_all(a, ALL, split_axis=0, concat_axis=0, tiled=True)  29.3 us
  transfers between devices with their start and end apart: 90, of which 31 were waited for; matrix products, arithmetic and copies ran while one was open for 5% of the time, Pallas kernels for 35%

profile of v20, /device:TPU:0, one launch (start us, length us, event | category | flops | bytes accessed | tf_op | source)
XLA Modules:
  0.0 740.1 jit_solution(8404274451806189528)
XLA Ops:
  12.4 7.3 all-to-all-start
  33.0 8.0 %collective-permute-start.2 = (bf16[104,768]{1,0:T(8,128)(2,1)}, bf16[104,768]{1,0:T(8,128)(2,1)S(1)}, u32[]{:S(2)}, u32[]{:S(2)}) collective-permute-start(bf16[104,768]{1,0:T(8,128)(2,1)} %get-tuple-element.250), channel_id=1, source_target_pairs={{0,8},{2,10},{4,12},{6,14},{8,0},{10,2},{12,4},{14,6},{16,24},{18,... | collective-permute-start | bytes 479240 | tf_op jit(solution)/shard_map/ppermute | solution.py:809
  43.7 9.2 %collective-permute-start.6 = (bf16[8,48,384]{2,1,0:T(8,128)(2,1)S(1)}, bf16[8,48,384]{2,1,0:T(8,128)(2,1)S(1)}, u32[]{:S(2)}, u32[]{:S(2)}) collective-permute-start(bf16[8,48,384]{2,1,0:T(8,128)(2,1)S(1)} %pad_maximum_fusion.13), channel_id=1, source_target_pairs={{0,4},{2,6},{4,0},{6,2},{1,5},{3,7},{5,1},{7,3},{8,12},{10,14},{12... | collective-permute-start | bytes 884744 | tf_op jit(solution)/shard_map/ppermute | solution.py:854
  54.2 27.0 %collective-permute-done.3.refs_2_ = bf16[104,768]{1,0:T(8,128)(2,1)S(1)} collective-permute-done((bf16[104,768]{1,0:T(8,128)(2,1)}, bf16[104,768]{1,0:T(8,128)(2,1)S(1)}, u32[]{:S(2)}, u32[]{:S(2)}) %collective-permute-start.3) | collective-permute-done | bytes 159776 | tf_op jit(solution)/shard_map/ppermute | solution.py:809
  90.6 24.1 %all_gather.14 = bf16[4,192,384]{2,1,0:T(8,128)(2,1)S(1)} all-gather(bf16[4,48,384]{2,1,0:T(8,128)(2,1)S(1)} %split.7), channel_id=1, replica_groups=mesh['clip'=4,'seq'=4,'head'=2] {'seq'}, dimensions={1}, use_global_device_ids=true | all-gather | bytes 737280 | tf_op jit(solution)/shard_map/all_gather | solution.py:843
  114.7 28.1 %all_gather.13 = bf16[5,192,384]{2,1,0:T(8,128)(2,1)S(1)} all-gather(bf16[5,48,384]{2,1,0:T(8,128)(2,1)S(1)} %split.6), channel_id=1, replica_groups=mesh['clip'=4,'seq'=4,'head'=2] {'seq'}, dimensions={1}, use_global_device_ids=true | all-gather | bytes 921600 | tf_op jit(solution)/shard_map/all_gather | solution.py:843
  147.4 12.2 %shard_map.195 = (bf16[416,768]{1,0:T(8,128)(2,1)}, bf16[3,416,768]{2,1,0:T(8,128)(2,1)}, f32[2,3,2,416]{3,2,1,0:T(2,128)}, bf16[104,768]{1,0:T(8,128)(2,1)}, bf...) custom-call(bf16[104,768]{1,0:T(8,128)(2,1)} %get-tuple-element.254.refs_0_, ...), custom_call_target="tpu_custom_call" | custom-call | flops 1472200704 | bytes 14470656 | tf_op jit(solution)/shard_map/pallas_call | solution.py:212
  179.5 9.3 %shard_map.196 = (bf16[416,768]{1,0:T(8,128)(2,1)}, bf16[416,768]{1,0:T(8,128)(2,1)}, f32[416,768]{1,0:T(8,128)}, bf16[3,416,768]{2,1,0:T(8,128)(2,1)}) custom-call(s32[5]{0:T(128)} %stack.110.me_ref, bf16[104,768]{1,0:T(8,128)(2,1)} %get-tuple-element.270.refs_0_, bf16[104,768]{1,0:T(8,128)(2,1)} %copy-done.50, bf16[104,768]{1,0:T(8,128)(2,1)} %copy-done.52, ...), custom_call_target="tpu_custom_call" | custom-call | flops 2453667840 | bytes 28821524 | tf_op jit(solution)/shard_map/pallas_call | solution.py:212
  188.9 10.1 %shard_map.197 = (bf16[416,768]{1,0:T(8,128)(2,1)}, f32[416,768]{1,0:T(8,128)}, f32[2,3,2,2,208]{4,3,2,1,0:T(2,128)}) custom-call(bf16[3,416,768]{2,1,0:T(8,128)(2,1)} %get-tuple-element.274.qkv_ref, f32[416,768]{1,0:T(8,128)} %get-tuple-element.275.x1_ref, bf16[9,2,768,384]{3,2,1,0:T(8,128)(2,1)} %bitcast.201), custom_call_target="tpu_custom_call" | custom-call | flops 490733568 | bytes 15748608 | tf_op jit(solution)/shard_map/pallas_call | solution.py:212
  200.6 19.7 %collective-permute-done.17.refs_3_ = bf16[4,8,48,384]{3,2,1,0:T(8,128)(2,1)} collective-permute-done((bf16[4,8,48,384]{3,2,1,0:T(8,128)(2,1)S(1)}, bf16[4,8,48,384]{3,2,1,0:T(8,128)(2,1)}, u32[]{:S(2)}, u32[]{:S(2)}) %collective-permute-start.17) | collective-permute-done | bytes 1179680 | tf_op jit(solution)/shard_map/ppermute | solution.py:1054
  228.7 8.3 %shard_map.198 = bf16[8,2,16,48,384]{4,3,2,1,0:T(8,128)(2,1)} custom-call(s32[5]{0:T(128)} %stack.110.me_ref, bf16[4,8,48,384]{3,2,1,0:T(8,128)(2,1)} %copy-done.23, bf16[4,8,48,384]{3,2,1,0:T(8,128)(2,1)} %collective-permute-done.16.refs_1_, bf16[4,8,48,384]{3,2,1,0:T(8,128)(2,1)} %copy-done.24, bf16[4,8,48,384]{3,2,1,0:T(8,128)(2,1)} %collective-permute-done.17.refs_3_, ...), custom_call_target="tpu_custom_call" | custom-call | bytes 18874368 | tf_op jit(solution)/shard_map/pallas_call | solution.py:889
  236.9 13.2 %shard_map.199 = (f32[416,768]{1,0:T(8,128)}, bf16[104,768]{1,0:T(8,128)(2,1)}, bf16[104,768]{1,0:T(8,128)(2,1)}, bf16[104,768]{1,0:T(8,128)(2,1)}, bf16[104,768]{1,0:T(8,128)(2,1)}) custom-call(f32[416,768]{1,0:T(8,128)} %get-tuple-element.289.x2_ref, bf16[8,2,768,384]{3,2,1,0:T(8,128)(2,1)} %bitcast.214, bf16[8,2,768,384]{3,2,1,0:T(8,128)(2,1)} %bitcast.215, ...), custom_call_target="tpu_custom_call" | custom-call | flops 3925868544 | bytes 22106132 | tf_op jit(solution)/shard_map/pallas_call | solution.py:212
  262.9 12.2 %shard_map.200 = (bf16[416,768]{1,0:T(8,128)(2,1)}, bf16[3,416,768]{2,1,0:T(8,128)(2,1)}, f32[2,3,2,416]{3,2,1,0:T(2,128)}, bf16[104,768]{1,0:T(8,128)(2,1)}, bf...) custom-call(bf16[104,768]{1,0:T(8,128)(2,1)} %get-tuple-element.303.refs_0_, ...), custom_call_target="tpu_custom_call" | custom-call | flops 1472200704 | bytes 14470656 | tf_op jit(solution)/shard_map/pallas_call | solution.py:212
  296.9 9.3 %shard_map.201 = (bf16[416,768]{1,0:T(8,128)(2,1)}, bf16[416,768]{1,0:T(8,128)(2,1)}, f32[416,768]{1,0:T(8,128)}, bf16[3,416,768]{2,1,0:T(8,128)(2,1)}) custom-call(s32[5]{0:T(128)} %stack.110.me_ref, bf16[104,768]{1,0:T(8,128)(2,1)} %get-tuple-element.314.refs_0_, bf16[104,768]{1,0:T(8,128)(2,1)} %copy-done.54, ...), custom_call_target="tpu_custom_call" | custom-call | flops 2453667840 | bytes 28821524 | tf_op jit(solution)/shard_map/pallas_call | solution.py:212
  306.3 10.3 %shard_map.202 = (bf16[416,768]{1,0:T(8,128)(2,1)}, f32[416,768]{1,0:T(8,128)}, f32[2,3,2,2,208]{4,3,2,1,0:T(2,128)}) custom-call(bf16[3,416,768]{2,1,0:T(8,128)(2,1)} %get-tuple-element.319.qkv_ref, f32[416,768]{1,0:T(8,128)} %get-tuple-element.320.x1_ref, bf16[9,2,768,384]{3,2,1,0:T(8,128)(2,1)} %bitcast.209), custom_call_target="tpu_custom_call" | custom-call | flops 490733568 | bytes 15748608 | tf_op jit(solution)/shard_map/pallas_call | solution.py:212
  318.7 8.2 %shard_map.203 = bf16[8,2,16,48,384]{4,3,2,1,0:T(8,128)(2,1)} custom-call(s32[5]{0:T(128)} %stack.110.me_ref, bf16[4,8,48,384]{3,2,1,0:T(8,128)(2,1)} %copy-done.21, bf16[4,8,48,384]{3,2,1,0:T(8,128)(2,1)} %collective-permute-done.30.refs_1_, bf16[4,8,48,384]{3,2,1,0:T(8,128)(2,1)} %copy-done.22, bf16[4,8,48,384]{3,2,1,0:T(8,128)(2,1)} %copy-done.27, ...), custom_call_target="tpu_custom_call" | custom-call | bytes 18874368 | tf_op jit(solution)/shard_map/pallas_call | solution.py:889
  326.9 25.0 %shard_map.204 = (f32[416,768]{1,0:T(8,128)}, bf16[4,2,2,192,384]{4,3,2,1,0:T(8,128)(2,1)}, bf16[4,2,2,192,384]{4,3,2,1,0:T(8,128)(2,1)}, bf16[4,2,2,192,384]{4,...) custom-call(s32[5]{0:T(128)} %stack.110.me_ref, ...), custom_call_target="tpu_custom_call" | custom-call | flops 9814671360 | bytes 33447956 | tf_op jit(solution)/shard_map/pallas_call | solution.py:212
  351.9 9.9 %collective-permute-start.37 = (bf16[4,2,2,192,384]{4,3,2,1,0:T(8,128)(2,1)}, bf16[4,2,2,192,384]{4,3,2,1,0:T(8,128)(2,1)S(1)}, u32[]{:S(2)}, u32[]{:S(2)}) collective-permute-start(bf16[4,2,2,192,384]{4,3,2,1,0:T(8,128)(2,1)} %get-tuple-element.335), channel_id=1, source_target_pairs={{0,8},{8,0},{16,24},{24,16},{1,9},{9,1},{17,25},{25,17},{2,10},{10... | collective-permute-start | bytes 7077896 | tf_op jit(solution)/shard_map/ppermute | solution.py:1054
  361.9 21.5 %shard_map.205 = (f32[416,768]{1,0:T(8,128)}, bf16[4,2,2,192,384]{4,3,2,1,0:T(8,128)(2,1)}, bf16[4,2,2,192,384]{4,3,2,1,0:T(8,128)(2,1)}, f32[2,768]{1,0:T(2,128)}) custom-call(s32[5]{0:T(128)} %stack.110.me_ref, f32[416,768]{1,0:T(8,128)} %get-tuple-element.329.g_ref, f32[416,768]{1,0:T(8,128)} %get-tuple-element.320.x1_ref, ...), custom_call_target="tpu_custom_call" | custom-call | flops 3925868544 | bytes 32386580 | tf_op jit(solution)/shard_map/pallas_call | solution.py:212
  396.0 7.8 %shard_map.207 = (bf16[104,768]{1,0:T(8,128)(2,1)}, bf16[104,768]{1,0:T(8,128)(2,1)}, bf16[104,768]{1,0:T(8,128)(2,1)}, bf16[104,768]{1,0:T(8,128)(2,1)}, bf16[2...) custom-call(s32[5]{0:T(128)} %stack.110.me_ref, f32[416,768]{1,0:T(8,128)} %get-tuple-element.340.g_ref.refs_5_, ...), custom_call_target="tpu_custom_call" | custom-call | flops 1962934272 | bytes 17350676 | tf_op jit(solution)/shard_map/pallas_call | solution.py:212
  403.8 12.5 %collective-permute-start.39 = (bf16[104,768]{1,0:T(8,128)(2,1)}, bf16[104,768]{1,0:T(8,128)(2,1)S(1)}, u32[]{:S(2)}, u32[]{:S(2)}) collective-permute-start(bf16[104,768]{1,0:T(8,128)(2,1)} %get-tuple-element.344), channel_id=1, source_target_pairs={{0,8},{2,10},{4,12},{6,14},{8,0},{10,2},{12,4},{14,6},{16,24},{18,... | collective-permute-start | bytes 479240 | tf_op jit(solution)/shard_map/ppermute | solution.py:809
  431.6 18.1 %shard_map.209 = (bf16[104,768]{1,0:T(8,128)(2,1)}, bf16[104,768]{1,0:T(8,128)(2,1)}, bf16[104,768]{1,0:T(8,128)(2,1)}, bf16[104,768]{1,0:T(8,128)(2,1)}, bf16[1...) custom-call(s32[5]{0:T(128)} %stack.110.me_ref, ...), custom_call_target="tpu_custom_call" | custom-call | flops 2944401408 | bytes 18009620 | tf_op jit(solution)/shard_map/pallas_call | solution.py:212
  456.9 15.7 %collective-permute-start.48 = (bf16[104,768]{1,0:T(8,128)(2,1)}, bf16[104,768]{1,0:T(8,128)(2,1)S(1)}, u32[]{:S(2)}, u32[]{:S(2)}) collective-permute-start(bf16[104,768]{1,0:T(8,128)(2,1)} %get-tuple-element.368), channel_id=1, source_target_pairs={{0,2},{2,0},{4,6},{6,4},{8,10},{10,8},{12,14},{14,12},{16,18},{18,... | collective-permute-start | bytes 479240 | tf_op jit(solution)/shard_map/ppermute | solution.py:809
  486.6 22.3 %shard_map.212 = (f32[416,768]{1,0:T(8,128)}, bf16[4,2,2,192,384]{4,3,2,1,0:T(8,128)(2,1)}, bf16[4,2,2,192,384]{4,3,2,1,0:T(8,128)(2,1)}, bf16[4,2,2,192,384]{4,...) custom-call(s32[5]{0:T(128)} %stack.110.me_ref, f32[416,768]{1,0:T(8,128)} %get-tuple-element.387.g_ref, ...), custom_call_target="tpu_custom_call" | custom-call | flops 9814671360 | bytes 32170004 | tf_op jit(solution)/shard_map/pallas_call | solution.py:212
  515.1 21.5 %shard_map.214 = (f32[416,768]{1,0:T(8,128)}, bf16[4,2,2,192,384]{4,3,2,1,0:T(8,128)(2,1)}, bf16[4,2,2,192,384]{4,3,2,1,0:T(8,128)(2,1)}, f32[2,768]{1,0:T(2,128)}) custom-call(s32[5]{0:T(128)} %stack.110.me_ref, f32[416,768]{1,0:T(8,128)} %get-tuple-element.397.g_ref, f32[416,768]{1,0:T(8,128)} %get-tuple-element.275.x1_ref, ...), custom_call_target="tpu_custom_call" | custom-call | flops 3925868544 | bytes 32386580 | tf_op jit(solution)/shard_map/pallas_call | solution.py:212
  540.1 7.6 %collective-permute-done.57.refs_17_ = bf16[2,192,384]{2,1,0:T(8,128)(2,1)S(1)} collective-permute-done((bf16[2,192,384]{2,1,0:T(8,128)(2,1)S(1)}, bf16[2,192,384]{2,1,0:T(8,128)(2,1)S(1)}, u32[]{:S(2)}, u32[]{:S(2)}) %collective-permute-start.57) | collective-permute-done | bytes 294944 | tf_op jit(solution)/shard_map/ppermute | solution.py:1054
  557.2 7.8 %shard_map.216 = (bf16[104,768]{1,0:T(8,128)(2,1)}, bf16[104,768]{1,0:T(8,128)(2,1)}, bf16[104,768]{1,0:T(8,128)(2,1)}, bf16[104,768]{1,0:T(8,128)(2,1)}, bf16[2...) custom-call(s32[5]{0:T(128)} %stack.110.me_ref, f32[416,768]{1,0:T(8,128)} %get-tuple-element.412.g_ref.refs_5_, ...), custom_call_target="tpu_custom_call" | custom-call | flops 1962934272 | bytes 17350676 | tf_op jit(solution)/shard_map/pallas_call | solution.py:212
  566.8 15.3 %collective-permute-done.63.refs_2_ = bf16[8,192,384]{2,1,0:T(8,128)(2,1)S(1)} collective-permute-done((bf16[8,192,384]{2,1,0:T(8,128)(2,1)}, bf16[8,192,384]{2,1,0:T(8,128)(2,1)S(1)}, u32[]{:S(2)}, u32[]{:S(2)}) %collective-permute-start.63) | collective-permute-done | bytes 1179680 | tf_op jit(solution)/shard_map/ppermute | solution.py:1054
  592.7 18.3 %shard_map.218 = (bf16[104,768]{1,0:T(8,128)(2,1)}, bf16[104,768]{1,0:T(8,128)(2,1)}, bf16[104,768]{1,0:T(8,128)(2,1)}, bf16[104,768]{1,0:T(8,128)(2,1)}, bf16[1...) custom-call(s32[5]{0:T(128)} %stack.110.me_ref, ...), custom_call_target="tpu_custom_call" | custom-call | flops 2944401408 | bytes 18009620 | tf_op jit(solution)/shard_map/pallas_call | solution.py:212
  620.8 6.6 shard_map.219
  647.3 29.3 %all-to-all-done.1 = f32[32,1,384]{2,1,0:T(1,128)} async-done(((f32[32,1,384]{2,1,0:T(1,128)}), f32[32,1,384]{2,1,0:T(1,128)}, u32[]{:S(2)}, u32[]{:S(2)}) %all-to-all-start.1) | async-done | bytes 49184 | tf_op jit(solution)/shard_map/all_to_all | solution.py:1142
  716.5 13.3 %all-to-all-done.2 = bf16[4,5,48,384]{3,2,1,0:T(8,128)(2,1)S(1)} async-done(((bf16[4,5,48,384]{3,2,1,0:T(8,128)(2,1)}), bf16[4,5,48,384]{3,2,1,0:T(8,128)(2,1)S(1)}, u32[]{:S(2)}, u32[]{:S(2)}) %all-to-all-start.2) | async-done | bytes 737312 | tf_op jit(solution)/shard_map/all_to_all | solution.py:1080
  (473 shorter events, 255.2 us)
Async XLA Ops:
  7.2 140.1 %all-gather.3.cloned.1.call-start = ((), (), s32[]{:S(2)}) async-start(), calls=%async_computation.8 | async-start | bytes 10948608 | tf_op jit(solution)/shard_map/all_gather | solution.py:838
  19.7 243.2 %all-gather.5.cloned.1.call-start = ((), (), s32[]{:S(2)}) async-start(), calls=%async_computation.9 | async-start | bytes 11943936 | tf_op jit(solution)/shard_map/all_gather | solution.py:844
  41.0 43.5 %collective-permute-start.7 = (bf16[8,48,384]{2,1,0:T(8,128)(2,1)S(1)}, bf16[8,48,384]{2,1,0:T(8,128)(2,1)S(1)}, u32[]{:S(2)}, u32[]{:S(2)}) collective-permute-start(bf16[8,48,384]{2,1,0:T(8,128)(2,1)S(1)} %pad_maximum_fusion.13), channel_id=1, source_target_pairs={{0,6},{2,0},{4,2},{6,4},{1,7},{3,1},{5,3},{7,5},{8,14},{10,8},{12,... | collective-permute-start | bytes 884744 | tf_op jit(solution)/shard_map/ppermute | solution.py:854
  43.7 46.9 %collective-permute-start.6 = (bf16[8,48,384]{2,1,0:T(8,128)(2,1)S(1)}, bf16[8,48,384]{2,1,0:T(8,128)(2,1)S(1)}, u32[]{:S(2)}, u32[]{:S(2)}) collective-permute-start(bf16[8,48,384]{2,1,0:T(8,128)(2,1)S(1)} %pad_maximum_fusion.13), channel_id=1, source_target_pairs={{0,4},{2,6},{4,0},{6,2},{1,5},{3,7},{5,1},{7,3},{8,12},{10,14},{12... | collective-permute-start | bytes 884744 | tf_op jit(solution)/shard_map/ppermute | solution.py:854
  52.9 37.7 %collective-permute-start.5 = (bf16[8,48,384]{2,1,0:T(8,128)(2,1)S(1)}, bf16[8,48,384]{2,1,0:T(8,128)(2,1)S(1)}, u32[]{:S(2)}, u32[]{:S(2)}) collective-permute-start(bf16[8,48,384]{2,1,0:T(8,128)(2,1)S(1)} %pad_maximum_fusion.13), channel_id=1, source_target_pairs={{0,2},{2,4},{4,6},{6,0},{1,3},{3,5},{5,7},{7,1},{8,10},{10,12},{12... | collective-permute-start | bytes 884744 | tf_op jit(solution)/shard_map/ppermute | solution.py:854
  53.2 28.0 %collective-permute-start.3 = (bf16[104,768]{1,0:T(8,128)(2,1)}, bf16[104,768]{1,0:T(8,128)(2,1)S(1)}, u32[]{:S(2)}, u32[]{:S(2)}) collective-permute-start(bf16[104,768]{1,0:T(8,128)(2,1)} %get-tuple-element.251), channel_id=1, source_target_pairs={{0,2},{2,0},{4,6},{6,4},{8,10},{10,8},{12,14},{14,12},{16,18},{18,... | collective-permute-start | bytes 479240 | tf_op jit(solution)/shard_map/ppermute | solution.py:809
  53.4 31.0 %collective-permute-start.4 = (bf16[104,768]{1,0:T(8,128)(2,1)}, bf16[104,768]{1,0:T(8,128)(2,1)S(1)}, u32[]{:S(2)}, u32[]{:S(2)}) collective-permute-start(bf16[104,768]{1,0:T(8,128)(2,1)} %get-tuple-element.252), channel_id=1, source_target_pairs={{0,10},{2,8},{4,14},{6,12},{8,2},{10,0},{12,6},{14,4},{16,26},{18,... | collective-permute-start | bytes 479240 | tf_op jit(solution)/shard_map/ppermute | solution.py:809
  144.1 486.0 %reduce-scatter.7.cloned.1.call-start = ((), (), s32[]{:S(2)}) async-start(), calls=%async_computation.11 | async-start | bytes 737280 | tf_op jit(solution)/shard_map/reduce_scatter | solution.py:1083
  171.5 48.8 %collective-permute-start.17 = (bf16[4,8,48,384]{3,2,1,0:T(8,128)(2,1)S(1)}, bf16[4,8,48,384]{3,2,1,0:T(8,128)(2,1)}, u32[]{:S(2)}, u32[]{:S(2)}) collective-permute-start(bf16[4,8,48,384]{3,2,1,0:T(8,128)(2,1)S(1)} %pad_maximum_fusion.2.refs_2_), channel_id=1, source_target_pairs={{0,16},{8,24},{16,0},{24,8},{1,17},{9,25},{17,1},{25,9},{2,18},{10... | collective-permute-start | bytes 3538952 | tf_op jit(solution)/shard_map/ppermute | solution.py:1054
  172.1 49.0 %collective-permute-start.16 = (bf16[4,8,48,384]{3,2,1,0:T(8,128)(2,1)S(1)}, bf16[4,8,48,384]{3,2,1,0:T(8,128)(2,1)}, u32[]{:S(2)}, u32[]{:S(2)}) collective-permute-start(bf16[4,8,48,384]{3,2,1,0:T(8,128)(2,1)S(1)} %pad_maximum_fusion.1.refs_0_), channel_id=1, source_target_pairs={{0,1},{1,0},{2,3},{3,2},{4,5},{5,4},{6,7},{7,6},{8,9},{9,8},{10,11... | collective-permute-start | bytes 3538952 | tf_op jit(solution)/shard_map/ppermute | solution.py:1054
  226.4 33.5 %collective-permute-start.26 = (bf16[2,8,48,384]{3,2,1,0:T(8,128)(2,1)S(1)}, bf16[2,8,48,384]{3,2,1,0:T(8,128)(2,1)S(1)}, u32[]{:S(2)}, u32[]{:S(2)}) collective-permute-start(bf16[2,8,48,384]{3,2,1,0:T(8,128)(2,1)S(1)} %pad_maximum_fusion.8), channel_id=1, source_target_pairs={{0,1},{1,0},{2,3},{3,2},{4,5},{5,4},{6,7},{7,6},{8,9},{9,8},{10,11... | collective-permute-start | bytes 1769480 | tf_op jit(solution)/shard_map/ppermute | solution.py:1054
  227.4 32.5 %collective-permute-start.25 = (bf16[2,8,48,384]{3,2,1,0:T(8,128)(2,1)S(1)}, bf16[2,8,48,384]{3,2,1,0:T(8,128)(2,1)S(1)}, u32[]{:S(2)}, u32[]{:S(2)}) collective-permute-start(bf16[2,8,48,384]{3,2,1,0:T(8,128)(2,1)S(1)} %pad_maximum_fusion.7), channel_id=1, source_target_pairs={{0,16},{8,24},{16,0},{24,8},{1,17},{9,25},{17,1},{25,9},{2,18},{10... | collective-permute-start | bytes 1769480 | tf_op jit(solution)/shard_map/ppermute | solution.py:1054
  260.8 28.2 %collective-permute-start.31 = (bf16[4,8,48,384]{3,2,1,0:T(8,128)(2,1)S(1)}, bf16[4,8,48,384]{3,2,1,0:T(8,128)(2,1)S(1)}, u32[]{:S(2)}, u32[]{:S(2)}) collective-permute-start(bf16[4,8,48,384]{3,2,1,0:T(8,128)(2,1)S(1)} %pad_maximum_fusion.4.refs_2_), channel_id=1, source_target_pairs={{0,16},{8,24},{16,0},{24,8},{1,17},{9,25},{17,1},{25,9},{2,18},{10... | collective-permute-start | bytes 3538952 | tf_op jit(solution)/shard_map/ppermute | solution.py:1054
  261.8 28.0 %collective-permute-start.30 = (bf16[4,8,48,384]{3,2,1,0:T(8,128)(2,1)S(1)}, bf16[4,8,48,384]{3,2,1,0:T(8,128)(2,1)}, u32[]{:S(2)}, u32[]{:S(2)}) collective-permute-start(bf16[4,8,48,384]{3,2,1,0:T(8,128)(2,1)S(1)} %pad_maximum_fusion.3.refs_0_), channel_id=1, source_target_pairs={{0,1},{1,0},{2,3},{3,2},{4,5},{5,4},{6,7},{7,6},{8,9},{9,8},{10,11... | collective-permute-start | bytes 3538952 | tf_op jit(solution)/shard_map/ppermute | solution.py:1054
  277.1 39.5 %collective-permute-start.34 = (bf16[4,8,48,384]{3,2,1,0:T(8,128)(2,1)S(1)}, bf16[4,8,48,384]{3,2,1,0:T(8,128)(2,1)S(1)}, u32[]{:S(2)}, u32[]{:S(2)}) collective-permute-start(bf16[4,8,48,384]{3,2,1,0:T(8,128)(2,1)S(1)} %pad_maximum_fusion.4.refs_2_), channel_id=1, source_target_pairs={{0,8},{8,0},{16,24},{24,16},{1,9},{9,1},{17,25},{25,17},{2,10},{10... | collective-permute-start | bytes 3538952 | tf_op jit(solution)/shard_map/ppermute | solution.py:1054
  282.6 34.0 %collective-permute-start.32 = (bf16[4,8,48,384]{3,2,1,0:T(8,128)(2,1)S(1)}, bf16[4,8,48,384]{3,2,1,0:T(8,128)(2,1)S(1)}, u32[]{:S(2)}, u32[]{:S(2)}) collective-permute-start(bf16[4,8,48,384]{3,2,1,0:T(8,128)(2,1)S(1)} %pad_maximum_fusion.3.refs_0_), channel_id=1, source_target_pairs={{0,8},{8,0},{16,24},{24,16},{1,9},{9,1},{17,25},{25,17},{2,10},{10... | collective-permute-start | bytes 3538952 | tf_op jit(solution)/shard_map/ppermute | solution.py:1054
  351.9 34.6 %collective-permute-start.37 = (bf16[4,2,2,192,384]{4,3,2,1,0:T(8,128)(2,1)}, bf16[4,2,2,192,384]{4,3,2,1,0:T(8,128)(2,1)S(1)}, u32[]{:S(2)}, u32[]{:S(2)}) collective-permute-start(bf16[4,2,2,192,384]{4,3,2,1,0:T(8,128)(2,1)} %get-tuple-element.335), channel_id=1, source_target_pairs={{0,8},{8,0},{16,24},{24,16},{1,9},{9,1},{17,25},{25,17},{2,10},{10... | collective-permute-start | bytes 7077896 | tf_op jit(solution)/shard_map/ppermute | solution.py:1054
  383.4 35.8 %collective-permute-start.44 = (bf16[4,2,2,192,384]{4,3,2,1,0:T(8,128)(2,1)}, bf16[4,2,2,192,384]{4,3,2,1,0:T(8,128)(2,1)S(1)}, u32[]{:S(2)}, u32[]{:S(2)}) collective-permute-start(bf16[4,2,2,192,384]{4,3,2,1,0:T(8,128)(2,1)} %get-tuple-element.350), channel_id=1, source_target_pairs={{0,8},{8,0},{16,24},{24,16},{1,9},{9,1},{17,25},{25,17},{2,10},{10... | collective-permute-start | bytes 7077896 | tf_op jit(solution)/shard_map/ppermute | solution.py:1054
  428.0 28.2 %collective-permute-start.46 = (bf16[8,192,384]{2,1,0:T(8,128)(2,1)}, bf16[8,192,384]{2,1,0:T(8,128)(2,1)S(1)}, u32[]{:S(2)}, u32[]{:S(2)}) collective-permute-start(bf16[8,192,384]{2,1,0:T(8,128)(2,1)} %get-tuple-element.365), channel_id=1, source_target_pairs={{0,16},{8,24},{16,0},{24,8},{1,17},{9,25},{17,1},{25,9},{2,18},{10... | collective-permute-start | bytes 3538952 | tf_op jit(solution)/shard_map/ppermute | solution.py:1054
  428.8 28.0 %collective-permute-start.50 = (bf16[2,2,2,192,384]{4,3,2,1,0:T(8,128)(2,1)S(1)}, bf16[2,2,2,192,384]{4,3,2,1,0:T(8,128)(2,1)S(1)}, u32[]{:S(2)}, u32[]{:S(2)}) collective-permute-start(bf16[2,2,2,192,384]{4,3,2,1,0:T(8,128)(2,1)S(1)} %copy-done.83), channel_id=1, source_target_pairs={{0,8},{8,0},{16,24},{24,16},{1,9},{9,1},{17,25},{25,17},{2,10},{10... | collective-permute-start | bytes 3538952 | tf_op jit(solution)/shard_map/ppermute | solution.py:1054
  480.6 28.8 %collective-permute-start.54 = (bf16[6,192,384]{2,1,0:T(8,128)(2,1)}, bf16[6,192,384]{2,1,0:T(8,128)(2,1)S(1)}, u32[]{:S(2)}, u32[]{:S(2)}) collective-permute-start(bf16[6,192,384]{2,1,0:T(8,128)(2,1)} %get-tuple-element.389), channel_id=1, source_target_pairs={{0,1},{1,0},{2,3},{3,2},{4,5},{5,4},{6,7},{7,6},{8,9},{9,8},{10,11... | collective-permute-start | bytes 2654216 | tf_op jit(solution)/shard_map/ppermute | solution.py:1054
  481.3 28.2 %collective-permute-start.55 = (bf16[8,192,384]{2,1,0:T(8,128)(2,1)}, bf16[8,192,384]{2,1,0:T(8,128)(2,1)S(1)}, u32[]{:S(2)}, u32[]{:S(2)}) collective-permute-start(bf16[8,192,384]{2,1,0:T(8,128)(2,1)} %get-tuple-element.390), channel_id=1, source_target_pairs={{0,16},{8,24},{16,0},{24,8},{1,17},{9,25},{17,1},{25,9},{2,18},{10... | collective-permute-start | bytes 3538952 | tf_op jit(solution)/shard_map/ppermute | solution.py:1054
  508.9 40.8 %collective-permute-start.58 = (bf16[4,2,2,192,384]{4,3,2,1,0:T(8,128)(2,1)}, bf16[4,2,2,192,384]{4,3,2,1,0:T(8,128)(2,1)}, u32[]{:S(2)}, u32[]{:S(2)}) collective-permute-start(bf16[4,2,2,192,384]{4,3,2,1,0:T(8,128)(2,1)} %get-tuple-element.406), channel_id=1, source_target_pairs={{0,8},{8,0},{16,24},{24,16},{1,9},{9,1},{17,25},{25,17},{2,10},{10... | collective-permute-start | bytes 7077896 | tf_op jit(solution)/shard_map/ppermute | solution.py:1054
  509.0 40.8 %collective-permute-start.59 = (bf16[4,2,2,192,384]{4,3,2,1,0:T(8,128)(2,1)}, bf16[4,2,2,192,384]{4,3,2,1,0:T(8,128)(2,1)}, u32[]{:S(2)}, u32[]{:S(2)}) collective-permute-start(bf16[4,2,2,192,384]{4,3,2,1,0:T(8,128)(2,1)} %get-tuple-element.408), channel_id=1, source_target_pairs={{0,8},{8,0},{16,24},{24,16},{1,9},{9,1},{17,25},{25,17},{2,10},{10... | collective-permute-start | bytes 7077896 | tf_op jit(solution)/shard_map/ppermute | solution.py:1054
  515.0 131.3 %reduce-scatter.11.cloned.1.call-start = ((), (), s32[]{:S(2)}) async-start(), calls=%async_computation.13 | async-start | bytes 1474560 | tf_op jit(solution)/shard_map/reduce_scatter | solution.py:1083
  536.6 29.9 %collective-permute-start.65 = (bf16[4,2,2,192,384]{4,3,2,1,0:T(8,128)(2,1)}, bf16[4,2,2,192,384]{4,3,2,1,0:T(8,128)(2,1)S(1)}, u32[]{:S(2)}, u32[]{:S(2)}) collective-permute-start(bf16[4,2,2,192,384]{4,3,2,1,0:T(8,128)(2,1)} %get-tuple-element.422), channel_id=1, source_target_pairs={{0,8},{8,0},{16,24},{24,16},{1,9},{9,1},{17,25},{25,17},{2,10},{10... | collective-permute-start | bytes 7077896 | tf_op jit(solution)/shard_map/ppermute | solution.py:1054
  536.8 151.5 %reduce-scatter.5.cloned.1.call-start = ((), (), s32[]{:S(2)}) async-start(), calls=%async_computation.10 | async-start | bytes 921600 | tf_op jit(solution)/shard_map/reduce_scatter | solution.py:1083
  592.6 120.9 %reduce-scatter.9.cloned.1.call-start = ((), (), s32[]{:S(2)}) async-start(), calls=%async_computation.12 | async-start | bytes 1474560 | tf_op jit(solution)/shard_map/reduce_scatter | solution.py:1083
  627.5 50.8 %collective-permute-start.77 = (bf16[8,192,384]{2,1,0:T(8,128)(2,1)}, bf16[8,192,384]{2,1,0:T(8,128)(2,1)S(1)}, u32[]{:S(2)}, u32[]{:S(2)}) collective-permute-start(bf16[8,192,384]{2,1,0:T(8,128)(2,1)} %get-tuple-element.470), channel_id=1, source_target_pairs={{0,16},{8,24},{16,0},{24,8},{1,17},{9,25},{17,1},{25,9},{2,18},{10... | collective-permute-start | bytes 3538952 | tf_op jit(solution)/shard_map/ppermute | solution.py:1054
  628.5 49.7 %collective-permute-start.76 = (bf16[6,192,384]{2,1,0:T(8,128)(2,1)}, bf16[6,192,384]{2,1,0:T(8,128)(2,1)S(1)}, u32[]{:S(2)}, u32[]{:S(2)}) collective-permute-start(bf16[6,192,384]{2,1,0:T(8,128)(2,1)} %get-tuple-element.469), channel_id=1, source_target_pairs={{0,1},{1,0},{2,3},{3,2},{4,5},{5,4},{6,7},{7,6},{8,9},{9,8},{10,11... | collective-permute-start | bytes 2654216 | tf_op jit(solution)/shard_map/ppermute | solution.py:1054
  638.2 46.2 %collective-permute-start.75 = (bf16[1,2,196,768]{3,1,2,0:T(2,128)(2,1)}, bf16[1,2,196,768]{3,1,2,0:T(2,128)(2,1)S(1)}, u32[]{:S(2)}, u32[]{:S(2)}) collective-permute-start(bf16[1,2,196,768]{3,1,2,0:T(2,128)(2,1)} %bitcast.189), channel_id=1, source_target_pairs={{0,0},{8,2},{2,4},{10,6},{4,8},{12,10},{6,12},{14,14},{16,16},{24,... | collective-permute-start | bytes 1806344 | tf_op jit(solution)/shard_map/ppermute | solution.py:791
  642.7 34.0 %all-to-all-start.1 = ((f32[32,1,384]{2,1,0:T(1,128)}), f32[32,1,384]{2,1,0:T(1,128)}, u32[]{:S(2)}, u32[]{:S(2)}) async-start(f32[32,1,384]{2,1,0:T(1,128)} %copy.125), calls=%async_computation.1 | async-start | bytes 98304 | tf_op jit(solution)/shard_map/all_to_all | solution.py:1142
  (145 other events, 1586.7 us)
Sparse Core Ops, SparseCore 0:
  11.7 132.7 all-gather.2
  146.4 84.5 all-gather.4
  515.2 20.6 reduce-scatter.6
  538.0 27.4 reduce-scatter.10
  592.7 20.8 reduce-scatter.4
  640.1 34.2 reduce-scatter.8

commit v21 on v16

--- a/solution.py
+++ b/solution.py
@@ -1270,8 +1270,8 @@
     norm_sums = reduce_norms(jnp.concatenate(norm_rows, axis=0)).reshape(layers, 2, 3, -1)
     if quick:
         tokens_grad = go_back(from_rows(grad.astype(BF16)))
-        tokens_grad, norm_sums = move((tokens_grad, norm_sums), late, me, True)
-        move((), rest, me, True)
+        tokens_grad = move(tokens_grad, late, me)
+        norm_sums = move(norm_sums, rest, me, True)
         summed = [[p.result for p in some] for some in summed]
     cuts = (2 * g_ff[0][0].shape[0], g_space[0].shape[0], g_out[0].shape[0], len(g_time))
     results = []

time: 737 us -> 743 us (level)
  waiting for transfers between devices: 240 us -> 261 us
  starting transfers between devices: 126 us -> 118 us
  local copies, waits for them, and re-layouts: 38.9 us -> 31.4 us
    ppermute x46, waiting for transfers between devices: 72.7 us -> 97.2 us  [cross(): return lax.ppermute(a, axis, [(i, i ^ 1 << bit) for i in range(size)])]
    reduce_scatter x4 -> x5, waiting for transfers between devices: 0.06 us -> 21.5 us  [move(): own = lax.psum_scatter(array, 'seq', scatter_dimension=1, tiled=True)]
    all_to_all x1, waiting for transfers between devices: 28.3 us -> 7.25 us  [reduce_norms(): every = lax.all_to_all(a, ALL, split_axis=0, concat_axis=0, tiled=True)]
    all_to_all x2 -> x1, waiting for transfers between devices: 13.3 us -> 2.06 us  [move(): lax.all_to_all(array, 'seq', split_axis=0, concat_axis=0, tiled=True)]
    unnamed x173 -> x155, local copies, waits for them, and re-layouts: 23.5 us -> 19.4 us
  transfers between devices with their start and end apart: 90 -> 90, of which waited for: 30 -> 36; matrix products, arithmetic and copies ran while one was open for 5% -> 4% of each run, Pallas kernels for 33% -> 33%
where the time goes in v21:
time: 743 us; the launch traced here: 738 us
  Pallas kernels  293 us (39%)
  waiting for transfers between devices  261 us (35%)
  starting transfers between devices  118 us (16%)
  local copies, waits for them, and re-layouts  31.4 us (4%)
  other arithmetic  17.8 us (2%)
  between operations  16 us (2%)
    pallas_call x18, Pallas kernels, call(): pl.pallas_call(body, out_shape=[shape for shape, _ in outs], grid=grid, i...  231 us
    ppermute x46, waiting for transfers between devices, cross(): return lax.ppermute(a, axis, [(i, i ^ 1 << bit) for i in range(size)])  97.2 us
    ppermute x24, waiting for transfers between devices, swap_places(): got.append(lax.ppermute(chunks[k], ('clip', 'seq'), pairs))  67.5 us
    ppermute x24, starting transfers between devices, swap_places(): got.append(lax.ppermute(chunks[k], ('clip', 'seq'), pairs))  47.5 us
    pallas_call x9, Pallas kernels, fold(): pl.pallas_call(body, out_shape=[jax.ShapeDtypeStruct(shape, BF16) for sha...  45.3 us
    ppermute x6, waiting for transfers between devices, spread_steps(): lax.ppermute(pack, 'seq', [(i, (i + k) % ways) for i in range(ways)])  37.2 us
    ppermute x46, starting transfers between devices, cross(): return lax.ppermute(a, axis, [(i, i ^ 1 << bit) for i in range(size)])  36.9 us
    all_gather x2, waiting for transfers between devices, gather_slabs(): full = lax.all_gather(pack, ('head', 'clip', 'seq'), axis=1, tiled=True)  22.9 us
  transfers between devices with their start and end apart: 90, of which 36 were waited for; matrix products, arithmetic and copies ran while one was open for 4% of the time, Pallas kernels for 33%

profile of v21, /device:TPU:0, one launch (start us, length us, event | category | flops | bytes accessed | tf_op | source)
XLA Modules:
  0.0 737.6 jit_solution(10546184264358716748)
XLA Ops:
  33.3 8.0 %collective-permute-start.2 = (bf16[104,768]{1,0:T(8,128)(2,1)}, bf16[104,768]{1,0:T(8,128)(2,1)S(1)}, u32[]{:S(2)}, u32[]{:S(2)}) collective-permute-start(bf16[104,768]{1,0:T(8,128)(2,1)} %get-tuple-element.262), channel_id=1, source_target_pairs={{0,8},{2,10},{4,12},{6,14},{8,0},{10,2},{12,4},{14,6},{16,24},{18,... | collective-permute-start | bytes 479240 | tf_op jit(solution)/shard_map/ppermute | solution.py:809
  44.3 8.8 %collective-permute-start.6 = (bf16[8,48,384]{2,1,0:T(8,128)(2,1)S(1)}, bf16[8,48,384]{2,1,0:T(8,128)(2,1)S(1)}, u32[]{:S(2)}, u32[]{:S(2)}) collective-permute-start(bf16[8,48,384]{2,1,0:T(8,128)(2,1)S(1)} %pad_maximum_fusion.12), channel_id=1, source_target_pairs={{0,4},{2,6},{4,0},{6,2},{1,5},{3,7},{5,1},{7,3},{8,12},{10,14},{12... | collective-permute-start | bytes 884744 | tf_op jit(solution)/shard_map/ppermute | solution.py:848
  54.5 27.6 %collective-permute-done.3.refs_2_ = bf16[104,768]{1,0:T(8,128)(2,1)S(1)} collective-permute-done((bf16[104,768]{1,0:T(8,128)(2,1)}, bf16[104,768]{1,0:T(8,128)(2,1)S(1)}, u32[]{:S(2)}, u32[]{:S(2)}) %collective-permute-start.3) | collective-permute-done | bytes 159776 | tf_op jit(solution)/shard_map/ppermute | solution.py:809
  93.3 25.4 %collective-permute-done.9 = bf16[2,8,48,384]{3,2,1,0:T(8,128)(2,1)S(1)} collective-permute-done((bf16[2,8,48,384]{3,2,1,0:T(8,128)(2,1)S(1)}, bf16[2,8,48,384]{3,2,1,0:T(8,128)(2,1)S(1)}, u32[]{:S(2)}, u32[]{:S(2)}) %collective-permute-start.9) | collective-permute-done | bytes 589856 | tf_op jit(solution)/shard_map/ppermute | solution.py:1048
  126.6 13.0 %collective-permute-done.12 = bf16[8,48,384]{2,1,0:T(8,128)(2,1)S(1)} collective-permute-done((bf16[8,48,384]{2,1,0:T(8,128)(2,1)S(1)}, bf16[8,48,384]{2,1,0:T(8,128)(2,1)S(1)}, u32[]{:S(2)}, u32[]{:S(2)}) %collective-permute-start.12) | collective-permute-done | bytes 294944 | tf_op jit(solution)/shard_map/ppermute | solution.py:848
  139.6 19.2 %collective-permute-done.11 = bf16[8,48,384]{2,1,0:T(8,128)(2,1)S(1)} collective-permute-done((bf16[8,48,384]{2,1,0:T(8,128)(2,1)S(1)}, bf16[8,48,384]{2,1,0:T(8,128)(2,1)S(1)}, u32[]{:S(2)}, u32[]{:S(2)}) %collective-permute-start.11) | collective-permute-done | bytes 294944 | tf_op jit(solution)/shard_map/ppermute | solution.py:848
  159.5 12.8 %shard_map.195 = (bf16[416,768]{1,0:T(8,128)(2,1)}, bf16[3,416,768]{2,1,0:T(8,128)(2,1)}, f32[2,3,2,416]{3,2,1,0:T(2,128)}, bf16[104,768]{1,0:T(8,128)(2,1)}, bf...) custom-call(bf16[104,768]{1,0:T(8,128)(2,1)} %get-tuple-element.289.refs_0_, ...), custom_call_target="tpu_custom_call" | custom-call | flops 1472200704 | bytes 14470656 | tf_op jit(solution)/shard_map/pallas_call | solution.py:212
  174.2 7.6 %collective-permute-done.16.refs_2_ = bf16[104,768]{1,0:T(8,128)(2,1)S(1)} collective-permute-done((bf16[104,768]{1,0:T(8,128)(2,1)}, bf16[104,768]{1,0:T(8,128)(2,1)S(1)}, u32[]{:S(2)}, u32[]{:S(2)}) %collective-permute-start.16) | collective-permute-done | bytes 159776 | tf_op jit(solution)/shard_map/ppermute | solution.py:809
  191.8 9.4 %shard_map.196 = (bf16[416,768]{1,0:T(8,128)(2,1)}, bf16[416,768]{1,0:T(8,128)(2,1)}, f32[416,768]{1,0:T(8,128)}, bf16[3,416,768]{2,1,0:T(8,128)(2,1)}) custom-call(s32[5]{0:T(128)} %stack.110.me_ref, bf16[104,768]{1,0:T(8,128)(2,1)} %get-tuple-element.307.refs_0_, bf16[104,768]{1,0:T(8,128)(2,1)} %copy-done.37, bf16[104,768]{1,0:T(8,128)(2,1)} %copy-done.38, ...), custom_call_target="tpu_custom_call" | custom-call | flops 2453667840 | bytes 28821524 | tf_op jit(solution)/shard_map/pallas_call | solution.py:212
  201.1 9.9 %shard_map.197 = (bf16[416,768]{1,0:T(8,128)(2,1)}, f32[416,768]{1,0:T(8,128)}, f32[2,3,2,2,208]{4,3,2,1,0:T(2,128)}) custom-call(bf16[3,416,768]{2,1,0:T(8,128)(2,1)} %get-tuple-element.311.qkv_ref, f32[416,768]{1,0:T(8,128)} %get-tuple-element.312.x1_ref, bf16[9,2,768,384]{3,2,1,0:T(8,128)(2,1)} %bitcast.201), custom_call_target="tpu_custom_call" | custom-call | flops 490733568 | bytes 15748608 | tf_op jit(solution)/shard_map/pallas_call | solution.py:212
  213.1 9.0 %shard_map.198 = bf16[8,2,16,48,384]{4,3,2,1,0:T(8,128)(2,1)} custom-call(s32[5]{0:T(128)} %stack.110.me_ref, bf16[4,8,48,384]{3,2,1,0:T(8,128)(2,1)} %copy-done.20, bf16[4,8,48,384]{3,2,1,0:T(8,128)(2,1)} %collective-permute-done.13.refs_1_, bf16[4,8,48,384]{3,2,1,0:T(8,128)(2,1)} %copy-done.21, bf16[4,8,48,384]{3,2,1,0:T(8,128)(2,1)} %collective-permute-done.14.refs_3_, ...), custom_call_target="tpu_custom_call" | custom-call | bytes 18874368 | tf_op jit(solution)/shard_map/pallas_call | solution.py:883
  222.2 13.3 %shard_map.199 = (f32[416,768]{1,0:T(8,128)}, bf16[104,768]{1,0:T(8,128)(2,1)}, bf16[104,768]{1,0:T(8,128)(2,1)}, bf16[104,768]{1,0:T(8,128)(2,1)}, bf16[104,768]{1,0:T(8,128)(2,1)}) custom-call(f32[416,768]{1,0:T(8,128)} %get-tuple-element.318.x2_ref, bf16[8,2,768,384]{3,2,1,0:T(8,128)(2,1)} %bitcast.214, bf16[8,2,768,384]{3,2,1,0:T(8,128)(2,1)} %bitcast.215, ...), custom_call_target="tpu_custom_call" | custom-call | flops 3925868544 | bytes 22106132 | tf_op jit(solution)/shard_map/pallas_call | solution.py:212
  242.2 7.9 %collective-permute-done.26.refs_3_ = bf16[104,768]{1,0:T(8,128)(2,1)S(1)} collective-permute-done((bf16[104,768]{1,0:T(8,128)(2,1)}, bf16[104,768]{1,0:T(8,128)(2,1)S(1)}, u32[]{:S(2)}, u32[]{:S(2)}) %collective-permute-start.26) | collective-permute-done | bytes 159776 | tf_op jit(solution)/shard_map/ppermute | solution.py:809
  259.0 22.9 %all-gather.5.cloned.1.call-done = bf16[9,1536,384]{2,1,0:T(8,128)(2,1)} async-done(((bf16[9,48,384]{2,1,0:T(8,128)(2,1)}), bf16[9,1536,384]{2,1,0:T(8,128)(2,1)}) %all-gather.5.cloned.1.call-update) | async-done | bytes 10616848 | tf_op jit(solution)/shard_map/all_gather | solution.py:838
  281.9 12.4 %shard_map.200 = (bf16[416,768]{1,0:T(8,128)(2,1)}, bf16[3,416,768]{2,1,0:T(8,128)(2,1)}, f32[2,3,2,416]{3,2,1,0:T(2,128)}, bf16[104,768]{1,0:T(8,128)(2,1)}, bf...) custom-call(bf16[104,768]{1,0:T(8,128)(2,1)} %get-tuple-element.330.refs_0_, ...), custom_call_target="tpu_custom_call" | custom-call | flops 1472200704 | bytes 14470656 | tf_op jit(solution)/shard_map/pallas_call | solution.py:212
  306.1 9.3 %shard_map.201 = (bf16[416,768]{1,0:T(8,128)(2,1)}, bf16[416,768]{1,0:T(8,128)(2,1)}, f32[416,768]{1,0:T(8,128)}, bf16[3,416,768]{2,1,0:T(8,128)(2,1)}) custom-call(s32[5]{0:T(128)} %stack.110.me_ref, bf16[104,768]{1,0:T(8,128)(2,1)} %get-tuple-element.340.refs_0_, bf16[104,768]{1,0:T(8,128)(2,1)} %copy-done.39, bf16[104,768]{1,0:T(8,128)(2,1)} %copy-done.41, ...), custom_call_target="tpu_custom_call" | custom-call | flops 2453667840 | bytes 28821524 | tf_op jit(solution)/shard_map/pallas_call | solution.py:212
  315.4 9.9 %shard_map.202 = (bf16[416,768]{1,0:T(8,128)(2,1)}, f32[416,768]{1,0:T(8,128)}, f32[2,3,2,2,208]{4,3,2,1,0:T(2,128)}) custom-call(bf16[3,416,768]{2,1,0:T(8,128)(2,1)} %get-tuple-element.345.qkv_ref, f32[416,768]{1,0:T(8,128)} %get-tuple-element.346.x1_ref, bf16[9,2,768,384]{3,2,1,0:T(8,128)(2,1)} %bitcast.209), custom_call_target="tpu_custom_call" | custom-call | flops 490733568 | bytes 15748608 | tf_op jit(solution)/shard_map/pallas_call | solution.py:212
  325.3 8.2 %shard_map.203 = bf16[8,2,16,48,384]{4,3,2,1,0:T(8,128)(2,1)} custom-call(s32[5]{0:T(128)} %stack.110.me_ref, bf16[4,8,48,384]{3,2,1,0:T(8,128)(2,1)} %copy-done.22, bf16[4,8,48,384]{3,2,1,0:T(8,128)(2,1)} %collective-permute-done.27.refs_1_, bf16[4,8,48,384]{3,2,1,0:T(8,128)(2,1)} %copy-done.23, bf16[4,8,48,384]{3,2,1,0:T(8,128)(2,1)} %collective-permute-done.28.refs_3_, ...), custom_call_target="tpu_custom_call" | custom-call | bytes 18874368 | tf_op jit(solution)/shard_map/pallas_call | solution.py:883
  333.5 25.2 %shard_map.204 = (f32[416,768]{1,0:T(8,128)}, bf16[4,2,2,192,384]{4,3,2,1,0:T(8,128)(2,1)}, bf16[4,2,2,192,384]{4,3,2,1,0:T(8,128)(2,1)}, bf16[4,2,2,192,384]{4,...) custom-call(s32[5]{0:T(128)} %stack.110.me_ref, ...), custom_call_target="tpu_custom_call" | custom-call | flops 9814671360 | bytes 33447956 | tf_op jit(solution)/shard_map/pallas_call | solution.py:212
  359.3 21.5 %shard_map.205 = (f32[416,768]{1,0:T(8,128)}, bf16[4,2,2,192,384]{4,3,2,1,0:T(8,128)(2,1)}, bf16[4,2,2,192,384]{4,3,2,1,0:T(8,128)(2,1)}, f32[2,768]{1,0:T(2,128)}) custom-call(s32[5]{0:T(128)} %stack.110.me_ref, f32[416,768]{1,0:T(8,128)} %get-tuple-element.352.g_ref, f32[416,768]{1,0:T(8,128)} %get-tuple-element.346.x1_ref, ...), custom_call_target="tpu_custom_call" | custom-call | flops 3925868544 | bytes 32386580 | tf_op jit(solution)/shard_map/pallas_call | solution.py:212
  392.1 7.8 %shard_map.207 = (bf16[104,768]{1,0:T(8,128)(2,1)}, bf16[104,768]{1,0:T(8,128)(2,1)}, bf16[104,768]{1,0:T(8,128)(2,1)}, bf16[104,768]{1,0:T(8,128)(2,1)}, bf16[2...) custom-call(s32[5]{0:T(128)} %stack.110.me_ref, f32[416,768]{1,0:T(8,128)} %get-tuple-element.363.g_ref.refs_5_, ...), custom_call_target="tpu_custom_call" | custom-call | flops 1962934272 | bytes 17350676 | tf_op jit(solution)/shard_map/pallas_call | solution.py:212
  399.9 10.4 %collective-permute-start.39 = (bf16[104,768]{1,0:T(8,128)(2,1)}, bf16[104,768]{1,0:T(8,128)(2,1)S(1)}, u32[]{:S(2)}, u32[]{:S(2)}) collective-permute-start(bf16[104,768]{1,0:T(8,128)(2,1)} %get-tuple-element.367), channel_id=1, source_target_pairs={{0,8},{2,10},{4,12},{6,14},{8,0},{10,2},{12,4},{14,6},{16,24},{18,... | collective-permute-start | bytes 479240 | tf_op jit(solution)/shard_map/ppermute | solution.py:809
  427.8 18.1 %shard_map.209 = (bf16[104,768]{1,0:T(8,128)(2,1)}, bf16[104,768]{1,0:T(8,128)(2,1)}, bf16[104,768]{1,0:T(8,128)(2,1)}, bf16[104,768]{1,0:T(8,128)(2,1)}, bf16[1...) custom-call(s32[5]{0:T(128)} %stack.110.me_ref, ...), custom_call_target="tpu_custom_call" | custom-call | flops 2944401408 | bytes 18009620 | tf_op jit(solution)/shard_map/pallas_call | solution.py:212
  449.7 15.4 %collective-permute-start.48 = (bf16[104,768]{1,0:T(8,128)(2,1)}, bf16[104,768]{1,0:T(8,128)(2,1)S(1)}, u32[]{:S(2)}, u32[]{:S(2)}) collective-permute-start(bf16[104,768]{1,0:T(8,128)(2,1)} %get-tuple-element.391), channel_id=1, source_target_pairs={{0,2},{2,0},{4,6},{6,4},{8,10},{10,8},{12,14},{14,12},{16,18},{18,... | collective-permute-start | bytes 479240 | tf_op jit(solution)/shard_map/ppermute | solution.py:809
  479.6 22.1 %shard_map.212 = (f32[416,768]{1,0:T(8,128)}, bf16[4,2,2,192,384]{4,3,2,1,0:T(8,128)(2,1)}, bf16[4,2,2,192,384]{4,3,2,1,0:T(8,128)(2,1)}, bf16[4,2,2,192,384]{4,...) custom-call(s32[5]{0:T(128)} %stack.110.me_ref, f32[416,768]{1,0:T(8,128)} %get-tuple-element.410.g_ref, ...), custom_call_target="tpu_custom_call" | custom-call | flops 9814671360 | bytes 32170004 | tf_op jit(solution)/shard_map/pallas_call | solution.py:212
  507.7 21.5 %shard_map.214 = (f32[416,768]{1,0:T(8,128)}, bf16[4,2,2,192,384]{4,3,2,1,0:T(8,128)(2,1)}, bf16[4,2,2,192,384]{4,3,2,1,0:T(8,128)(2,1)}, f32[2,768]{1,0:T(2,128)}) custom-call(s32[5]{0:T(128)} %stack.110.me_ref, f32[416,768]{1,0:T(8,128)} %get-tuple-element.420.g_ref, f32[416,768]{1,0:T(8,128)} %get-tuple-element.312.x1_ref, ...), custom_call_target="tpu_custom_call" | custom-call | flops 3925868544 | bytes 32386580 | tf_op jit(solution)/shard_map/pallas_call | solution.py:212
  531.1 8.2 %collective-permute-done.57.refs_17_ = bf16[2,192,384]{2,1,0:T(8,128)(2,1)} collective-permute-done((bf16[2,192,384]{2,1,0:T(8,128)(2,1)S(1)}, bf16[2,192,384]{2,1,0:T(8,128)(2,1)}, u32[]{:S(2)}, u32[]{:S(2)}) %collective-permute-start.57) | collective-permute-done | bytes 294944 | tf_op jit(solution)/shard_map/ppermute | solution.py:1048
  548.9 7.8 %shard_map.216 = (bf16[104,768]{1,0:T(8,128)(2,1)}, bf16[104,768]{1,0:T(8,128)(2,1)}, bf16[104,768]{1,0:T(8,128)(2,1)}, bf16[104,768]{1,0:T(8,128)(2,1)}, bf16[2...) custom-call(s32[5]{0:T(128)} %stack.110.me_ref, f32[416,768]{1,0:T(8,128)} %get-tuple-element.435.g_ref.refs_5_, ...), custom_call_target="tpu_custom_call" | custom-call | flops 1962934272 | bytes 17350676 | tf_op jit(solution)/shard_map/pallas_call | solution.py:212
  558.6 16.1 %collective-permute-done.63.refs_2_ = bf16[8,192,384]{2,1,0:T(8,128)(2,1)S(1)} collective-permute-done((bf16[8,192,384]{2,1,0:T(8,128)(2,1)}, bf16[8,192,384]{2,1,0:T(8,128)(2,1)S(1)}, u32[]{:S(2)}, u32[]{:S(2)}) %collective-permute-start.63) | collective-permute-done | bytes 1179680 | tf_op jit(solution)/shard_map/ppermute | solution.py:1048
  584.7 18.1 %shard_map.218 = (bf16[104,768]{1,0:T(8,128)(2,1)}, bf16[104,768]{1,0:T(8,128)(2,1)}, bf16[104,768]{1,0:T(8,128)(2,1)}, bf16[104,768]{1,0:T(8,128)(2,1)}, bf16[1...) custom-call(s32[5]{0:T(128)} %stack.110.me_ref, ...), custom_call_target="tpu_custom_call" | custom-call | flops 2944401408 | bytes 18009620 | tf_op jit(solution)/shard_map/pallas_call | solution.py:212
  638.0 11.7 %collective-permute-done.76.refs_3_.refs_8_ = bf16[6,192,384]{2,1,0:T(8,128)(2,1)S(1)} collective-permute-done((bf16[6,192,384]{2,1,0:T(8,128)(2,1)}, bf16[6,192,384]{2,1,0:T(8,128)(2,1)S(1)}, u32[]{:S(2)}, u32[]{:S(2)}) %collective-permute-start.76) | collective-permute-done | bytes 884768 | tf_op jit(solution)/shard_map/ppermute | solution.py:1048
  700.8 21.4 %reduce-scatter.12.cloned.1.call-done = bf16[8,48,384]{2,1,0:T(8,128)(2,1)} async-done(((bf16[8,192,384]{2,1,0:T(8,128)(2,1)}), bf16[8,48,384]{2,1,0:T(8,128)(2,1)}) %reduce-scatter.12.cloned.1.call-update) | async-done | bytes 294928 | tf_op jit(solution)/shard_map/reduce_scatter | solution.py:1077
  (437 shorter events, 261.8 us)
Async XLA Ops:
  7.2 152.3 %all-gather.3.cloned.1.call-start = ((), (), s32[]{:S(2)}) async-start(), calls=%async_computation.8 | async-start | bytes 10948608 | tf_op jit(solution)/shard_map/all_gather | solution.py:838
  11.0 270.8 %all-gather.5.cloned.1.call-start = ((), (), s32[]{:S(2)}) async-start(), calls=%async_computation.9 | async-start | bytes 10948608 | tf_op jit(solution)/shard_map/all_gather | solution.py:838
  20.0 641.5 %reduce-scatter.10.cloned.1.call-start = ((), (), s32[]{:S(2)}) async-start(), calls=%async_computation.12 | async-start | bytes 737280 | tf_op jit(solution)/shard_map/reduce_scatter | solution.py:1077
  41.2 43.9 %collective-permute-start.7 = (bf16[8,48,384]{2,1,0:T(8,128)(2,1)S(1)}, bf16[8,48,384]{2,1,0:T(8,128)(2,1)S(1)}, u32[]{:S(2)}, u32[]{:S(2)}) collective-permute-start(bf16[8,48,384]{2,1,0:T(8,128)(2,1)S(1)} %pad_maximum_fusion.12), channel_id=1, source_target_pairs={{0,6},{2,0},{4,2},{6,4},{1,7},{3,1},{5,3},{7,5},{8,14},{10,8},{12,... | collective-permute-start | bytes 884744 | tf_op jit(solution)/shard_map/ppermute | solution.py:848
  44.3 45.7 %collective-permute-start.6 = (bf16[8,48,384]{2,1,0:T(8,128)(2,1)S(1)}, bf16[8,48,384]{2,1,0:T(8,128)(2,1)S(1)}, u32[]{:S(2)}, u32[]{:S(2)}) collective-permute-start(bf16[8,48,384]{2,1,0:T(8,128)(2,1)S(1)} %pad_maximum_fusion.12), channel_id=1, source_target_pairs={{0,4},{2,6},{4,0},{6,2},{1,5},{3,7},{5,1},{7,3},{8,12},{10,14},{12... | collective-permute-start | bytes 884744 | tf_op jit(solution)/shard_map/ppermute | solution.py:848
  53.2 36.9 %collective-permute-start.5 = (bf16[8,48,384]{2,1,0:T(8,128)(2,1)S(1)}, bf16[8,48,384]{2,1,0:T(8,128)(2,1)S(1)}, u32[]{:S(2)}, u32[]{:S(2)}) collective-permute-start(bf16[8,48,384]{2,1,0:T(8,128)(2,1)S(1)} %pad_maximum_fusion.12), channel_id=1, source_target_pairs={{0,2},{2,4},{4,6},{6,0},{1,3},{3,5},{5,7},{7,1},{8,10},{10,12},{12... | collective-permute-start | bytes 884744 | tf_op jit(solution)/shard_map/ppermute | solution.py:848
  53.2 28.8 %collective-permute-start.3 = (bf16[104,768]{1,0:T(8,128)(2,1)}, bf16[104,768]{1,0:T(8,128)(2,1)S(1)}, u32[]{:S(2)}, u32[]{:S(2)}) collective-permute-start(bf16[104,768]{1,0:T(8,128)(2,1)} %get-tuple-element.263), channel_id=1, source_target_pairs={{0,2},{2,0},{4,6},{6,4},{8,10},{10,8},{12,14},{14,12},{16,18},{18,... | collective-permute-start | bytes 479240 | tf_op jit(solution)/shard_map/ppermute | solution.py:809
  53.7 31.3 %collective-permute-start.4 = (bf16[104,768]{1,0:T(8,128)(2,1)}, bf16[104,768]{1,0:T(8,128)(2,1)S(1)}, u32[]{:S(2)}, u32[]{:S(2)}) collective-permute-start(bf16[104,768]{1,0:T(8,128)(2,1)} %get-tuple-element.264), channel_id=1, source_target_pairs={{0,10},{2,8},{4,14},{6,12},{8,2},{10,0},{12,6},{14,4},{16,26},{18,... | collective-permute-start | bytes 479240 | tf_op jit(solution)/shard_map/ppermute | solution.py:809
  90.1 28.6 %collective-permute-start.9 = (bf16[2,8,48,384]{3,2,1,0:T(8,128)(2,1)S(1)}, bf16[2,8,48,384]{3,2,1,0:T(8,128)(2,1)S(1)}, u32[]{:S(2)}, u32[]{:S(2)}) collective-permute-start(bf16[2,8,48,384]{3,2,1,0:T(8,128)(2,1)S(1)} %pad_maximum_fusion.5), channel_id=1, source_target_pairs={{0,1},{1,0},{2,3},{3,2},{4,5},{5,4},{6,7},{7,6},{8,9},{9,8},{10,11... | collective-permute-start | bytes 1769480 | tf_op jit(solution)/shard_map/ppermute | solution.py:1048
  120.5 38.3 %collective-permute-start.14 = (bf16[4,8,48,384]{3,2,1,0:T(8,128)(2,1)S(1)}, bf16[4,8,48,384]{3,2,1,0:T(8,128)(2,1)}, u32[]{:S(2)}, u32[]{:S(2)}) collective-permute-start(bf16[4,8,48,384]{3,2,1,0:T(8,128)(2,1)S(1)} %pad_maximum_fusion.1.refs_2_), channel_id=1, source_target_pairs={{0,16},{8,24},{16,0},{24,8},{1,17},{9,25},{17,1},{25,9},{2,18},{10... | collective-permute-start | bytes 3538952 | tf_op jit(solution)/shard_map/ppermute | solution.py:1048
  122.1 36.8 %collective-permute-start.13 = (bf16[4,8,48,384]{3,2,1,0:T(8,128)(2,1)S(1)}, bf16[4,8,48,384]{3,2,1,0:T(8,128)(2,1)}, u32[]{:S(2)}, u32[]{:S(2)}) collective-permute-start(bf16[4,8,48,384]{3,2,1,0:T(8,128)(2,1)S(1)} %pad_maximum_fusion.refs_0_), channel_id=1, source_target_pairs={{0,1},{1,0},{2,3},{3,2},{4,5},{5,4},{6,7},{7,6},{8,9},{9,8},{10,11... | collective-permute-start | bytes 3538952 | tf_op jit(solution)/shard_map/ppermute | solution.py:1048
  123.8 35.1 %collective-permute-start.11 = (bf16[8,48,384]{2,1,0:T(8,128)(2,1)S(1)}, bf16[8,48,384]{2,1,0:T(8,128)(2,1)S(1)}, u32[]{:S(2)}, u32[]{:S(2)}) collective-permute-start(bf16[8,48,384]{2,1,0:T(8,128)(2,1)S(1)} %pad_maximum_fusion.13), channel_id=1, source_target_pairs={{0,4},{2,6},{4,0},{6,2},{1,5},{3,7},{5,1},{7,3},{8,12},{10,14},{12... | collective-permute-start | bytes 884744 | tf_op jit(solution)/shard_map/ppermute | solution.py:848
  124.6 34.2 %collective-permute-start.10 = (bf16[8,48,384]{2,1,0:T(8,128)(2,1)S(1)}, bf16[8,48,384]{2,1,0:T(8,128)(2,1)S(1)}, u32[]{:S(2)}, u32[]{:S(2)}) collective-permute-start(bf16[8,48,384]{2,1,0:T(8,128)(2,1)S(1)} %pad_maximum_fusion.13), channel_id=1, source_target_pairs={{0,2},{2,4},{4,6},{6,0},{1,3},{3,5},{5,7},{7,1},{8,10},{10,12},{12... | collective-permute-start | bytes 884744 | tf_op jit(solution)/shard_map/ppermute | solution.py:848
  139.6 33.1 %collective-permute-start.20 = (bf16[4,8,48,384]{3,2,1,0:T(8,128)(2,1)S(1)}, bf16[4,8,48,384]{3,2,1,0:T(8,128)(2,1)}, u32[]{:S(2)}, u32[]{:S(2)}) collective-permute-start(bf16[4,8,48,384]{3,2,1,0:T(8,128)(2,1)S(1)} %pad_maximum_fusion.1.refs_2_), channel_id=1, source_target_pairs={{0,8},{8,0},{16,24},{24,16},{1,9},{9,1},{17,25},{25,17},{2,10},{10... | collective-permute-start | bytes 3538952 | tf_op jit(solution)/shard_map/ppermute | solution.py:1048
  211.4 45.5 %collective-permute-start.28 = (bf16[4,8,48,384]{3,2,1,0:T(8,128)(2,1)S(1)}, bf16[4,8,48,384]{3,2,1,0:T(8,128)(2,1)}, u32[]{:S(2)}, u32[]{:S(2)}) collective-permute-start(bf16[4,8,48,384]{3,2,1,0:T(8,128)(2,1)S(1)} %pad_maximum_fusion.3.refs_2_), channel_id=1, source_target_pairs={{0,16},{8,24},{16,0},{24,8},{1,17},{9,25},{17,1},{25,9},{2,18},{10... | collective-permute-start | bytes 3538952 | tf_op jit(solution)/shard_map/ppermute | solution.py:1048
  211.9 45.7 %collective-permute-start.27 = (bf16[4,8,48,384]{3,2,1,0:T(8,128)(2,1)S(1)}, bf16[4,8,48,384]{3,2,1,0:T(8,128)(2,1)}, u32[]{:S(2)}, u32[]{:S(2)}) collective-permute-start(bf16[4,8,48,384]{3,2,1,0:T(8,128)(2,1)S(1)} %pad_maximum_fusion.2.refs_0_), channel_id=1, source_target_pairs={{0,1},{1,0},{2,3},{3,2},{4,5},{5,4},{6,7},{7,6},{8,9},{9,8},{10,11... | collective-permute-start | bytes 3538952 | tf_op jit(solution)/shard_map/ppermute | solution.py:1048
  236.1 58.5 %collective-permute-start.34 = (bf16[4,8,48,384]{3,2,1,0:T(8,128)(2,1)S(1)}, bf16[4,8,48,384]{3,2,1,0:T(8,128)(2,1)}, u32[]{:S(2)}, u32[]{:S(2)}) collective-permute-start(bf16[4,8,48,384]{3,2,1,0:T(8,128)(2,1)S(1)} %pad_maximum_fusion.3.refs_2_), channel_id=1, source_target_pairs={{0,8},{8,0},{16,24},{24,16},{1,9},{9,1},{17,25},{25,17},{2,10},{10... | collective-permute-start | bytes 3538952 | tf_op jit(solution)/shard_map/ppermute | solution.py:1048
  237.1 60.3 %collective-permute-start.32 = (bf16[4,8,48,384]{3,2,1,0:T(8,128)(2,1)S(1)}, bf16[4,8,48,384]{3,2,1,0:T(8,128)(2,1)}, u32[]{:S(2)}, u32[]{:S(2)}) collective-permute-start(bf16[4,8,48,384]{3,2,1,0:T(8,128)(2,1)S(1)} %pad_maximum_fusion.2.refs_0_), channel_id=1, source_target_pairs={{0,8},{8,0},{16,24},{24,16},{1,9},{9,1},{17,25},{25,17},{2,10},{10... | collective-permute-start | bytes 3538952 | tf_op jit(solution)/shard_map/ppermute | solution.py:1048
  257.6 47.8 %collective-permute-start.33 = (bf16[4,8,48,384]{3,2,1,0:T(8,128)(2,1)}, bf16[4,8,48,384]{3,2,1,0:T(8,128)(2,1)}, u32[]{:S(2)}, u32[]{:S(2)}) collective-permute-start(bf16[4,8,48,384]{3,2,1,0:T(8,128)(2,1)} %collective-permute-done.27.refs_1_), channel_id=1, source_target_pairs={{0,8},{8,0},{16,24},{24,16},{1,9},{9,1},{17,25},{25,17},{2,10},{10... | collective-permute-start | bytes 3538952 | tf_op jit(solution)/shard_map/ppermute | solution.py:1048
  257.6 47.8 %collective-permute-start.35 = (bf16[4,8,48,384]{3,2,1,0:T(8,128)(2,1)}, bf16[4,8,48,384]{3,2,1,0:T(8,128)(2,1)}, u32[]{:S(2)}, u32[]{:S(2)}) collective-permute-start(bf16[4,8,48,384]{3,2,1,0:T(8,128)(2,1)} %collective-permute-done.28.refs_3_), channel_id=1, source_target_pairs={{0,8},{8,0},{16,24},{24,16},{1,9},{9,1},{17,25},{25,17},{2,10},{10... | collective-permute-start | bytes 3538952 | tf_op jit(solution)/shard_map/ppermute | solution.py:1048
  380.8 29.6 %collective-permute-start.44 = (bf16[4,2,2,192,384]{4,3,2,1,0:T(8,128)(2,1)}, bf16[4,2,2,192,384]{4,3,2,1,0:T(8,128)(2,1)S(1)}, u32[]{:S(2)}, u32[]{:S(2)}) collective-permute-start(bf16[4,2,2,192,384]{4,3,2,1,0:T(8,128)(2,1)} %get-tuple-element.373), channel_id=1, source_target_pairs={{0,8},{8,0},{16,24},{24,16},{1,9},{9,1},{17,25},{25,17},{2,10},{10... | collective-permute-start | bytes 7077896 | tf_op jit(solution)/shard_map/ppermute | solution.py:1048
  472.7 29.5 %collective-permute-start.54 = (bf16[6,192,384]{2,1,0:T(8,128)(2,1)}, bf16[6,192,384]{2,1,0:T(8,128)(2,1)S(1)}, u32[]{:S(2)}, u32[]{:S(2)}) collective-permute-start(bf16[6,192,384]{2,1,0:T(8,128)(2,1)} %get-tuple-element.412), channel_id=1, source_target_pairs={{0,1},{1,0},{2,3},{3,2},{4,5},{5,4},{6,7},{7,6},{8,9},{9,8},{10,11... | collective-permute-start | bytes 2654216 | tf_op jit(solution)/shard_map/ppermute | solution.py:1048
  501.6 40.5 %collective-permute-start.58 = (bf16[4,2,2,192,384]{4,3,2,1,0:T(8,128)(2,1)}, bf16[4,2,2,192,384]{4,3,2,1,0:T(8,128)(2,1)}, u32[]{:S(2)}, u32[]{:S(2)}) collective-permute-start(bf16[4,2,2,192,384]{4,3,2,1,0:T(8,128)(2,1)} %get-tuple-element.429), channel_id=1, source_target_pairs={{0,8},{8,0},{16,24},{24,16},{1,9},{9,1},{17,25},{25,17},{2,10},{10... | collective-permute-start | bytes 7077896 | tf_op jit(solution)/shard_map/ppermute | solution.py:1048
  501.7 40.4 %collective-permute-start.59 = (bf16[4,2,2,192,384]{4,3,2,1,0:T(8,128)(2,1)}, bf16[4,2,2,192,384]{4,3,2,1,0:T(8,128)(2,1)}, u32[]{:S(2)}, u32[]{:S(2)}) collective-permute-start(bf16[4,2,2,192,384]{4,3,2,1,0:T(8,128)(2,1)} %get-tuple-element.431), channel_id=1, source_target_pairs={{0,8},{8,0},{16,24},{24,16},{1,9},{9,1},{17,25},{25,17},{2,10},{10... | collective-permute-start | bytes 7077896 | tf_op jit(solution)/shard_map/ppermute | solution.py:1048
  529.2 29.1 %collective-permute-start.65 = (bf16[4,2,2,192,384]{4,3,2,1,0:T(8,128)(2,1)}, bf16[4,2,2,192,384]{4,3,2,1,0:T(8,128)(2,1)S(1)}, u32[]{:S(2)}, u32[]{:S(2)}) collective-permute-start(bf16[4,2,2,192,384]{4,3,2,1,0:T(8,128)(2,1)} %get-tuple-element.445), channel_id=1, source_target_pairs={{0,8},{8,0},{16,24},{24,16},{1,9},{9,1},{17,25},{25,17},{2,10},{10... | collective-permute-start | bytes 7077896 | tf_op jit(solution)/shard_map/ppermute | solution.py:1048
  529.3 133.1 %reduce-scatter.14.cloned.1.call-start = ((), (), s32[]{:S(2)}) async-start(), calls=%async_computation.14 | async-start | bytes 1474560 | tf_op jit(solution)/shard_map/reduce_scatter | solution.py:1077
  548.7 127.0 %reduce-scatter.6.cloned.1.call-start = ((), (), s32[]{:S(2)}) async-start(), calls=%async_computation.10 | async-start | bytes 921600 | tf_op jit(solution)/shard_map/reduce_scatter | solution.py:1077
  582.3 28.5 %collective-permute-start.66 = (bf16[8,192,384]{2,1,0:T(8,128)(2,1)}, bf16[8,192,384]{2,1,0:T(8,128)(2,1)S(1)}, u32[]{:S(2)}, u32[]{:S(2)}) collective-permute-start(bf16[8,192,384]{2,1,0:T(8,128)(2,1)} %get-tuple-element.462), channel_id=1, source_target_pairs={{0,1},{1,0},{2,3},{3,2},{4,5},{5,4},{6,7},{7,6},{8,9},{9,8},{10,11... | collective-permute-start | bytes 3538952 | tf_op jit(solution)/shard_map/ppermute | solution.py:1048
  584.0 28.5 %collective-permute-start.71 = (bf16[2,2,2,192,384]{4,3,2,1,0:T(8,128)(2,1)}, bf16[2,2,2,192,384]{4,3,2,1,0:T(8,128)(2,1)S(1)}, u32[]{:S(2)}, u32[]{:S(2)}) collective-permute-start(bf16[2,2,2,192,384]{4,3,2,1,0:T(8,128)(2,1)} %get-tuple-element.471), channel_id=1, source_target_pairs={{0,8},{8,0},{16,24},{24,16},{1,9},{9,1},{17,25},{25,17},{2,10},{10... | collective-permute-start | bytes 3538952 | tf_op jit(solution)/shard_map/ppermute | solution.py:1048
  611.9 86.4 %reduce-scatter.8.cloned.1.call-start = ((), (), s32[]{:S(2)}) async-start(), calls=%async_computation.11 | async-start | bytes 737280 | tf_op jit(solution)/shard_map/reduce_scatter | solution.py:1077
  661.3 60.9 %reduce-scatter.12.cloned.1.call-start = ((), (), s32[]{:S(2)}) async-start(), calls=%async_computation.13 | async-start | bytes 1474560 | tf_op jit(solution)/shard_map/reduce_scatter | solution.py:1077
  694.8 32.5 %all-to-all-start.2 = ((bf16[4,5,48,384]{3,2,1,0:T(8,128)(2,1)}), bf16[4,5,48,384]{3,2,1,0:T(8,128)(2,1)S(1)}, u32[]{:S(2)}, u32[]{:S(2)}) async-start(bf16[4,5,48,384]{3,2,1,0:T(8,128)(2,1)} %shard_map.222), calls=%async_computation.2 | async-start | bytes 1474560 | tf_op jit(solution)/shard_map/all_to_all | solution.py:1074
  (129 other events, 1650.7 us)
Sparse Core Ops, SparseCore 0:
  11.7 144.1 all-gather.2
  159.5 122.2 all-gather.4
  529.5 20.1 reduce-scatter.9
  551.8 33.1 reduce-scatter.13
  612.0 24.6 reduce-scatter.5
  661.4 20.9 reduce-scatter.7
  684.7 37.4 reduce-scatter.11

commit v22 on v21

--- a/solution.py
+++ b/solution.py
@@ -1270,7 +1270,7 @@
     norm_sums = reduce_norms(jnp.concatenate(norm_rows, axis=0)).reshape(layers, 2, 3, -1)
     if quick:
         tokens_grad = go_back(from_rows(grad.astype(BF16)))
-        tokens_grad = move(tokens_grad, late, me)
+        tokens_grad = move(tokens_grad, late, me, True)
         norm_sums = move(norm_sums, rest, me, True)
         summed = [[p.result for p in some] for some in summed]
     cuts = (2 * g_ff[0][0].shape[0], g_space[0].shape[0], g_out[0].shape[0], len(g_time))

time: 743 us -> 731 us (0.984)
  waiting for transfers between devices: 261 us -> 236 us
  starting transfers between devices: 118 us -> 126 us
    reduce_scatter x5 -> x4, waiting for transfers between devices: 21.5 us -> 0.06 us  [move(): own = lax.psum_scatter(array, 'seq', scatter_dimension=1, tiled=True)]
    ppermute x46, waiting for transfers between devices: 97.2 us -> 83.3 us  [cross(): return lax.ppermute(a, axis, [(i, i ^ 1 << bit) for i in range(size)])]
    all_to_all x1 -> x2, waiting for transfers between devices: 2.06 us -> 13.2 us  [move(): lax.all_to_all(array, 'seq', split_axis=0, concat_axis=0, tiled=True)]
    ppermute x24, waiting for transfers between devices: 67.5 us -> 59.8 us  [swap_places(): got.append(lax.ppermute(chunks[k], ('clip', 'seq'), pairs))]
    unnamed x155 -> x167, local copies, waits for them, and re-layouts: 19.4 us -> 21.7 us
  transfers between devices with their start and end apart: 90 -> 90, of which waited for: 36 -> 32; matrix products, arithmetic and copies ran while one was open for 4% -> 5% of each run, Pallas kernels for 33% -> 33%
where the time goes in v22:
time: 731 us; the launch traced here: 726 us
  Pallas kernels  294 us (40%)
  waiting for transfers between devices  236 us (32%)
  starting transfers between devices  126 us (17%)
  local copies, waits for them, and re-layouts  36.5 us (5%)
  other arithmetic  17.8 us (2%)
  between operations  15.9 us (2%)
    pallas_call x18, Pallas kernels, call(): pl.pallas_call(body, out_shape=[shape for shape, _ in outs], grid=grid, i...  231 us
    ppermute x46, waiting for transfers between devices, cross(): return lax.ppermute(a, axis, [(i, i ^ 1 << bit) for i in range(size)])  83.3 us
    ppermute x24, waiting for transfers between devices, swap_places(): got.append(lax.ppermute(chunks[k], ('clip', 'seq'), pairs))  59.8 us
    ppermute x24, starting transfers between devices, swap_places(): got.append(lax.ppermute(chunks[k], ('clip', 'seq'), pairs))  47.3 us
    pallas_call x9, Pallas kernels, fold(): pl.pallas_call(body, out_shape=[jax.ShapeDtypeStruct(shape, BF16) for sha...  45.3 us
    ppermute x46, starting transfers between devices, cross(): return lax.ppermute(a, axis, [(i, i ^ 1 << bit) for i in range(size)])  39.2 us
    ppermute x6, waiting for transfers between devices, spread_steps(): lax.ppermute(pack, 'seq', [(i, (i + k) % ways) for i in range(ways)])  37.2 us
    all_gather x2, waiting for transfers between devices, gather_slabs(): full = lax.all_gather(pack, ('head', 'clip', 'seq'), axis=1, tiled=True)  22.6 us
  transfers between devices with their start and end apart: 90, of which 32 were waited for; matrix products, arithmetic and copies ran while one was open for 5% of the time, Pallas kernels for 33%

profile of v22, /device:TPU:0, one launch (start us, length us, event | category | flops | bytes accessed | tf_op | source)
XLA Modules:
  0.0 725.5 jit_solution(10659979304626805450)
XLA Ops:
  33.3 8.0 %collective-permute-start.2 = (bf16[104,768]{1,0:T(8,128)(2,1)}, bf16[104,768]{1,0:T(8,128)(2,1)S(1)}, u32[]{:S(2)}, u32[]{:S(2)}) collective-permute-start(bf16[104,768]{1,0:T(8,128)(2,1)} %get-tuple-element.262), channel_id=1, source_target_pairs={{0,8},{2,10},{4,12},{6,14},{8,0},{10,2},{12,4},{14,6},{16,24},{18,... | collective-permute-start | bytes 479240 | tf_op jit(solution)/shard_map/ppermute | solution.py:809
  44.3 8.8 %collective-permute-start.6 = (bf16[8,48,384]{2,1,0:T(8,128)(2,1)S(1)}, bf16[8,48,384]{2,1,0:T(8,128)(2,1)S(1)}, u32[]{:S(2)}, u32[]{:S(2)}) collective-permute-start(bf16[8,48,384]{2,1,0:T(8,128)(2,1)S(1)} %pad_maximum_fusion.12), channel_id=1, source_target_pairs={{0,4},{2,6},{4,0},{6,2},{1,5},{3,7},{5,1},{7,3},{8,12},{10,14},{12... | collective-permute-start | bytes 884744 | tf_op jit(solution)/shard_map/ppermute | solution.py:848
  54.5 27.6 %collective-permute-done.3.refs_2_ = bf16[104,768]{1,0:T(8,128)(2,1)S(1)} collective-permute-done((bf16[104,768]{1,0:T(8,128)(2,1)}, bf16[104,768]{1,0:T(8,128)(2,1)S(1)}, u32[]{:S(2)}, u32[]{:S(2)}) %collective-permute-start.3) | collective-permute-done | bytes 159776 | tf_op jit(solution)/shard_map/ppermute | solution.py:809
  93.3 25.4 %collective-permute-done.9 = bf16[2,8,48,384]{3,2,1,0:T(8,128)(2,1)S(1)} collective-permute-done((bf16[2,8,48,384]{3,2,1,0:T(8,128)(2,1)S(1)}, bf16[2,8,48,384]{3,2,1,0:T(8,128)(2,1)S(1)}, u32[]{:S(2)}, u32[]{:S(2)}) %collective-permute-start.9) | collective-permute-done | bytes 589856 | tf_op jit(solution)/shard_map/ppermute | solution.py:1048
  126.6 13.0 %collective-permute-done.12 = bf16[8,48,384]{2,1,0:T(8,128)(2,1)S(1)} collective-permute-done((bf16[8,48,384]{2,1,0:T(8,128)(2,1)S(1)}, bf16[8,48,384]{2,1,0:T(8,128)(2,1)S(1)}, u32[]{:S(2)}, u32[]{:S(2)}) %collective-permute-start.12) | collective-permute-done | bytes 294944 | tf_op jit(solution)/shard_map/ppermute | solution.py:848
  139.6 19.2 %collective-permute-done.11 = bf16[8,48,384]{2,1,0:T(8,128)(2,1)S(1)} collective-permute-done((bf16[8,48,384]{2,1,0:T(8,128)(2,1)S(1)}, bf16[8,48,384]{2,1,0:T(8,128)(2,1)S(1)}, u32[]{:S(2)}, u32[]{:S(2)}) %collective-permute-start.11) | collective-permute-done | bytes 294944 | tf_op jit(solution)/shard_map/ppermute | solution.py:848
  159.5 12.4 %shard_map.195 = (bf16[416,768]{1,0:T(8,128)(2,1)}, bf16[3,416,768]{2,1,0:T(8,128)(2,1)}, f32[2,3,2,416]{3,2,1,0:T(2,128)}, bf16[104,768]{1,0:T(8,128)(2,1)}, bf...) custom-call(bf16[104,768]{1,0:T(8,128)(2,1)} %get-tuple-element.289.refs_0_, ...), custom_call_target="tpu_custom_call" | custom-call | flops 1472200704 | bytes 14470656 | tf_op jit(solution)/shard_map/pallas_call | solution.py:212
  173.8 7.8 %collective-permute-done.16.refs_2_ = bf16[104,768]{1,0:T(8,128)(2,1)S(1)} collective-permute-done((bf16[104,768]{1,0:T(8,128)(2,1)}, bf16[104,768]{1,0:T(8,128)(2,1)S(1)}, u32[]{:S(2)}, u32[]{:S(2)}) %collective-permute-start.16) | collective-permute-done | bytes 159776 | tf_op jit(solution)/shard_map/ppermute | solution.py:809
  191.6 9.3 %shard_map.196 = (bf16[416,768]{1,0:T(8,128)(2,1)}, bf16[416,768]{1,0:T(8,128)(2,1)}, f32[416,768]{1,0:T(8,128)}, bf16[3,416,768]{2,1,0:T(8,128)(2,1)}) custom-call(s32[5]{0:T(128)} %stack.110.me_ref, bf16[104,768]{1,0:T(8,128)(2,1)} %get-tuple-element.307.refs_0_, bf16[104,768]{1,0:T(8,128)(2,1)} %copy-done.44, bf16[104,768]{1,0:T(8,128)(2,1)} %copy-done.45, ...), custom_call_target="tpu_custom_call" | custom-call | flops 2453667840 | bytes 28821524 | tf_op jit(solution)/shard_map/pallas_call | solution.py:212
  201.0 9.9 %shard_map.197 = (bf16[416,768]{1,0:T(8,128)(2,1)}, f32[416,768]{1,0:T(8,128)}, f32[2,3,2,2,208]{4,3,2,1,0:T(2,128)}) custom-call(bf16[3,416,768]{2,1,0:T(8,128)(2,1)} %get-tuple-element.311.qkv_ref, f32[416,768]{1,0:T(8,128)} %get-tuple-element.312.x1_ref, bf16[9,2,768,384]{3,2,1,0:T(8,128)(2,1)} %bitcast.201), custom_call_target="tpu_custom_call" | custom-call | flops 490733568 | bytes 15748608 | tf_op jit(solution)/shard_map/pallas_call | solution.py:212
  213.6 8.9 %shard_map.198 = bf16[8,2,16,48,384]{4,3,2,1,0:T(8,128)(2,1)} custom-call(s32[5]{0:T(128)} %stack.110.me_ref, bf16[4,8,48,384]{3,2,1,0:T(8,128)(2,1)} %copy-done.21, bf16[4,8,48,384]{3,2,1,0:T(8,128)(2,1)} %collective-permute-done.13.refs_1_, bf16[4,8,48,384]{3,2,1,0:T(8,128)(2,1)} %copy-done.22, bf16[4,8,48,384]{3,2,1,0:T(8,128)(2,1)} %collective-permute-done.14.refs_3_, ...), custom_call_target="tpu_custom_call" | custom-call | bytes 18874368 | tf_op jit(solution)/shard_map/pallas_call | solution.py:883
  222.6 13.3 %shard_map.199 = (f32[416,768]{1,0:T(8,128)}, bf16[104,768]{1,0:T(8,128)(2,1)}, bf16[104,768]{1,0:T(8,128)(2,1)}, bf16[104,768]{1,0:T(8,128)(2,1)}, bf16[104,768]{1,0:T(8,128)(2,1)}) custom-call(f32[416,768]{1,0:T(8,128)} %get-tuple-element.318.x2_ref, bf16[8,2,768,384]{3,2,1,0:T(8,128)(2,1)} %bitcast.214, bf16[8,2,768,384]{3,2,1,0:T(8,128)(2,1)} %bitcast.215, ...), custom_call_target="tpu_custom_call" | custom-call | flops 3925868544 | bytes 22106132 | tf_op jit(solution)/shard_map/pallas_call | solution.py:212
  242.6 8.0 %collective-permute-done.26.refs_3_ = bf16[104,768]{1,0:T(8,128)(2,1)S(1)} collective-permute-done((bf16[104,768]{1,0:T(8,128)(2,1)}, bf16[104,768]{1,0:T(8,128)(2,1)S(1)}, u32[]{:S(2)}, u32[]{:S(2)}) %collective-permute-start.26) | collective-permute-done | bytes 159776 | tf_op jit(solution)/shard_map/ppermute | solution.py:809
  259.0 22.6 %all-gather.5.cloned.1.call-done = bf16[9,1536,384]{2,1,0:T(8,128)(2,1)} async-done(((bf16[9,48,384]{2,1,0:T(8,128)(2,1)}), bf16[9,1536,384]{2,1,0:T(8,128)(2,1)}) %all-gather.5.cloned.1.call-update) | async-done | bytes 10616848 | tf_op jit(solution)/shard_map/all_gather | solution.py:838
  281.6 12.5 %shard_map.200 = (bf16[416,768]{1,0:T(8,128)(2,1)}, bf16[3,416,768]{2,1,0:T(8,128)(2,1)}, f32[2,3,2,416]{3,2,1,0:T(2,128)}, bf16[104,768]{1,0:T(8,128)(2,1)}, bf...) custom-call(bf16[104,768]{1,0:T(8,128)(2,1)} %get-tuple-element.330.refs_0_, ...), custom_call_target="tpu_custom_call" | custom-call | flops 1472200704 | bytes 14470656 | tf_op jit(solution)/shard_map/pallas_call | solution.py:212
  305.9 9.4 %shard_map.201 = (bf16[416,768]{1,0:T(8,128)(2,1)}, bf16[416,768]{1,0:T(8,128)(2,1)}, f32[416,768]{1,0:T(8,128)}, bf16[3,416,768]{2,1,0:T(8,128)(2,1)}) custom-call(s32[5]{0:T(128)} %stack.110.me_ref, bf16[104,768]{1,0:T(8,128)(2,1)} %get-tuple-element.340.refs_0_, bf16[104,768]{1,0:T(8,128)(2,1)} %copy-done.46, bf16[104,768]{1,0:T(8,128)(2,1)} %copy-done.48, ...), custom_call_target="tpu_custom_call" | custom-call | flops 2453667840 | bytes 28821524 | tf_op jit(solution)/shard_map/pallas_call | solution.py:212
  315.3 9.9 %shard_map.202 = (bf16[416,768]{1,0:T(8,128)(2,1)}, f32[416,768]{1,0:T(8,128)}, f32[2,3,2,2,208]{4,3,2,1,0:T(2,128)}) custom-call(bf16[3,416,768]{2,1,0:T(8,128)(2,1)} %get-tuple-element.345.qkv_ref, f32[416,768]{1,0:T(8,128)} %get-tuple-element.346.x1_ref, bf16[9,2,768,384]{3,2,1,0:T(8,128)(2,1)} %bitcast.209), custom_call_target="tpu_custom_call" | custom-call | flops 490733568 | bytes 15748608 | tf_op jit(solution)/shard_map/pallas_call | solution.py:212
  325.2 8.2 %shard_map.203 = bf16[8,2,16,48,384]{4,3,2,1,0:T(8,128)(2,1)} custom-call(s32[5]{0:T(128)} %stack.110.me_ref, bf16[4,8,48,384]{3,2,1,0:T(8,128)(2,1)} %copy-done.23, bf16[4,8,48,384]{3,2,1,0:T(8,128)(2,1)} %collective-permute-done.27.refs_1_, bf16[4,8,48,384]{3,2,1,0:T(8,128)(2,1)} %copy-done.24, bf16[4,8,48,384]{3,2,1,0:T(8,128)(2,1)} %collective-permute-done.28.refs_3_, ...), custom_call_target="tpu_custom_call" | custom-call | bytes 18874368 | tf_op jit(solution)/shard_map/pallas_call | solution.py:883
  333.4 25.4 %shard_map.204 = (f32[416,768]{1,0:T(8,128)}, bf16[4,2,2,192,384]{4,3,2,1,0:T(8,128)(2,1)}, bf16[4,2,2,192,384]{4,3,2,1,0:T(8,128)(2,1)}, bf16[4,2,2,192,384]{4,...) custom-call(s32[5]{0:T(128)} %stack.110.me_ref, ...), custom_call_target="tpu_custom_call" | custom-call | flops 9814671360 | bytes 33447956 | tf_op jit(solution)/shard_map/pallas_call | solution.py:212
  359.4 21.6 %shard_map.205 = (f32[416,768]{1,0:T(8,128)}, bf16[4,2,2,192,384]{4,3,2,1,0:T(8,128)(2,1)}, bf16[4,2,2,192,384]{4,3,2,1,0:T(8,128)(2,1)}, f32[2,768]{1,0:T(2,128)}) custom-call(s32[5]{0:T(128)} %stack.110.me_ref, f32[416,768]{1,0:T(8,128)} %get-tuple-element.352.g_ref, f32[416,768]{1,0:T(8,128)} %get-tuple-element.346.x1_ref, ...), custom_call_target="tpu_custom_call" | custom-call | flops 3925868544 | bytes 32386580 | tf_op jit(solution)/shard_map/pallas_call | solution.py:212
  392.4 7.8 %shard_map.207 = (bf16[104,768]{1,0:T(8,128)(2,1)}, bf16[104,768]{1,0:T(8,128)(2,1)}, bf16[104,768]{1,0:T(8,128)(2,1)}, bf16[104,768]{1,0:T(8,128)(2,1)}, bf16[2...) custom-call(s32[5]{0:T(128)} %stack.110.me_ref, f32[416,768]{1,0:T(8,128)} %get-tuple-element.363.g_ref.refs_5_, ...), custom_call_target="tpu_custom_call" | custom-call | flops 1962934272 | bytes 17350676 | tf_op jit(solution)/shard_map/pallas_call | solution.py:212
  400.1 10.4 %collective-permute-start.39 = (bf16[104,768]{1,0:T(8,128)(2,1)}, bf16[104,768]{1,0:T(8,128)(2,1)S(1)}, u32[]{:S(2)}, u32[]{:S(2)}) collective-permute-start(bf16[104,768]{1,0:T(8,128)(2,1)} %get-tuple-element.367), channel_id=1, source_target_pairs={{0,8},{2,10},{4,12},{6,14},{8,0},{10,2},{12,4},{14,6},{16,24},{18,... | collective-permute-start | bytes 479240 | tf_op jit(solution)/shard_map/ppermute | solution.py:809
  428.2 18.1 %shard_map.209 = (bf16[104,768]{1,0:T(8,128)(2,1)}, bf16[104,768]{1,0:T(8,128)(2,1)}, bf16[104,768]{1,0:T(8,128)(2,1)}, bf16[104,768]{1,0:T(8,128)(2,1)}, bf16[1...) custom-call(s32[5]{0:T(128)} %stack.110.me_ref, ...), custom_call_target="tpu_custom_call" | custom-call | flops 2944401408 | bytes 18009620 | tf_op jit(solution)/shard_map/pallas_call | solution.py:212
  449.7 15.4 %collective-permute-start.48 = (bf16[104,768]{1,0:T(8,128)(2,1)}, bf16[104,768]{1,0:T(8,128)(2,1)S(1)}, u32[]{:S(2)}, u32[]{:S(2)}) collective-permute-start(bf16[104,768]{1,0:T(8,128)(2,1)} %get-tuple-element.391), channel_id=1, source_target_pairs={{0,2},{2,0},{4,6},{6,4},{8,10},{10,8},{12,14},{14,12},{16,18},{18,... | collective-permute-start | bytes 479240 | tf_op jit(solution)/shard_map/ppermute | solution.py:809
  479.7 22.3 %shard_map.212 = (f32[416,768]{1,0:T(8,128)}, bf16[4,2,2,192,384]{4,3,2,1,0:T(8,128)(2,1)}, bf16[4,2,2,192,384]{4,3,2,1,0:T(8,128)(2,1)}, bf16[4,2,2,192,384]{4,...) custom-call(s32[5]{0:T(128)} %stack.110.me_ref, f32[416,768]{1,0:T(8,128)} %get-tuple-element.410.g_ref, ...), custom_call_target="tpu_custom_call" | custom-call | flops 9814671360 | bytes 32170004 | tf_op jit(solution)/shard_map/pallas_call | solution.py:212
  508.1 21.5 %shard_map.214 = (f32[416,768]{1,0:T(8,128)}, bf16[4,2,2,192,384]{4,3,2,1,0:T(8,128)(2,1)}, bf16[4,2,2,192,384]{4,3,2,1,0:T(8,128)(2,1)}, f32[2,768]{1,0:T(2,128)}) custom-call(s32[5]{0:T(128)} %stack.110.me_ref, f32[416,768]{1,0:T(8,128)} %get-tuple-element.420.g_ref, f32[416,768]{1,0:T(8,128)} %get-tuple-element.312.x1_ref, ...), custom_call_target="tpu_custom_call" | custom-call | flops 3925868544 | bytes 32386580 | tf_op jit(solution)/shard_map/pallas_call | solution.py:212
  532.3 8.0 %collective-permute-done.57.refs_17_ = bf16[2,192,384]{2,1,0:T(8,128)(2,1)S(1)} collective-permute-done((bf16[2,192,384]{2,1,0:T(8,128)(2,1)S(1)}, bf16[2,192,384]{2,1,0:T(8,128)(2,1)S(1)}, u32[]{:S(2)}, u32[]{:S(2)}) %collective-permute-start.57) | collective-permute-done | bytes 294944 | tf_op jit(solution)/shard_map/ppermute | solution.py:1048
  549.4 7.8 %shard_map.216 = (bf16[104,768]{1,0:T(8,128)(2,1)}, bf16[104,768]{1,0:T(8,128)(2,1)}, bf16[104,768]{1,0:T(8,128)(2,1)}, bf16[104,768]{1,0:T(8,128)(2,1)}, bf16[2...) custom-call(s32[5]{0:T(128)} %stack.110.me_ref, f32[416,768]{1,0:T(8,128)} %get-tuple-element.435.g_ref.refs_5_, ...), custom_call_target="tpu_custom_call" | custom-call | flops 1962934272 | bytes 17350676 | tf_op jit(solution)/shard_map/pallas_call | solution.py:212
  559.0 16.2 %collective-permute-done.63.refs_2_ = bf16[8,192,384]{2,1,0:T(8,128)(2,1)S(1)} collective-permute-done((bf16[8,192,384]{2,1,0:T(8,128)(2,1)}, bf16[8,192,384]{2,1,0:T(8,128)(2,1)S(1)}, u32[]{:S(2)}, u32[]{:S(2)}) %collective-permute-start.63) | collective-permute-done | bytes 1179680 | tf_op jit(solution)/shard_map/ppermute | solution.py:1048
  585.3 18.3 %shard_map.218 = (bf16[104,768]{1,0:T(8,128)(2,1)}, bf16[104,768]{1,0:T(8,128)(2,1)}, bf16[104,768]{1,0:T(8,128)(2,1)}, bf16[104,768]{1,0:T(8,128)(2,1)}, bf16[1...) custom-call(s32[5]{0:T(128)} %stack.110.me_ref, ...), custom_call_target="tpu_custom_call" | custom-call | flops 2944401408 | bytes 18009620 | tf_op jit(solution)/shard_map/pallas_call | solution.py:212
  654.7 13.9 %all-to-all-done.1 = f32[32,1,384]{2,1,0:T(1,128)} async-done(((f32[32,1,384]{2,1,0:T(1,128)}), f32[32,1,384]{2,1,0:T(1,128)}, u32[]{:S(2)}, u32[]{:S(2)}) %all-to-all-start.1) | async-done | bytes 49184 | tf_op jit(solution)/shard_map/all_to_all | solution.py:1136
  702.0 13.2 %all-to-all-done.2 = bf16[4,5,48,384]{3,2,1,0:T(8,128)(2,1)S(1)} async-done(((bf16[4,5,48,384]{3,2,1,0:T(8,128)(2,1)}), bf16[4,5,48,384]{3,2,1,0:T(8,128)(2,1)S(1)}, u32[]{:S(2)}, u32[]{:S(2)}) %all-to-all-start.2) | async-done | bytes 737312 | tf_op jit(solution)/shard_map/all_to_all | solution.py:1074
  (448 shorter events, 255.7 us)
Async XLA Ops:
  7.2 152.3 %all-gather.3.cloned.1.call-start = ((), (), s32[]{:S(2)}) async-start(), calls=%async_computation.8 | async-start | bytes 10948608 | tf_op jit(solution)/shard_map/all_gather | solution.py:838
  11.0 270.6 %all-gather.5.cloned.1.call-start = ((), (), s32[]{:S(2)}) async-start(), calls=%async_computation.9 | async-start | bytes 10948608 | tf_op jit(solution)/shard_map/all_gather | solution.py:838
  20.0 602.6 %reduce-scatter.7.cloned.1.call-start = ((), (), s32[]{:S(2)}) async-start(), calls=%async_computation.11 | async-start | bytes 737280 | tf_op jit(solution)/shard_map/reduce_scatter | solution.py:1077
  41.2 43.9 %collective-permute-start.7 = (bf16[8,48,384]{2,1,0:T(8,128)(2,1)S(1)}, bf16[8,48,384]{2,1,0:T(8,128)(2,1)S(1)}, u32[]{:S(2)}, u32[]{:S(2)}) collective-permute-start(bf16[8,48,384]{2,1,0:T(8,128)(2,1)S(1)} %pad_maximum_fusion.12), channel_id=1, source_target_pairs={{0,6},{2,0},{4,2},{6,4},{1,7},{3,1},{5,3},{7,5},{8,14},{10,8},{12,... | collective-permute-start | bytes 884744 | tf_op jit(solution)/shard_map/ppermute | solution.py:848
  44.3 45.7 %collective-permute-start.6 = (bf16[8,48,384]{2,1,0:T(8,128)(2,1)S(1)}, bf16[8,48,384]{2,1,0:T(8,128)(2,1)S(1)}, u32[]{:S(2)}, u32[]{:S(2)}) collective-permute-start(bf16[8,48,384]{2,1,0:T(8,128)(2,1)S(1)} %pad_maximum_fusion.12), channel_id=1, source_target_pairs={{0,4},{2,6},{4,0},{6,2},{1,5},{3,7},{5,1},{7,3},{8,12},{10,14},{12... | collective-permute-start | bytes 884744 | tf_op jit(solution)/shard_map/ppermute | solution.py:848
  53.2 36.9 %collective-permute-start.5 = (bf16[8,48,384]{2,1,0:T(8,128)(2,1)S(1)}, bf16[8,48,384]{2,1,0:T(8,128)(2,1)S(1)}, u32[]{:S(2)}, u32[]{:S(2)}) collective-permute-start(bf16[8,48,384]{2,1,0:T(8,128)(2,1)S(1)} %pad_maximum_fusion.12), channel_id=1, source_target_pairs={{0,2},{2,4},{4,6},{6,0},{1,3},{3,5},{5,7},{7,1},{8,10},{10,12},{12... | collective-permute-start | bytes 884744 | tf_op jit(solution)/shard_map/ppermute | solution.py:848
  53.2 28.8 %collective-permute-start.3 = (bf16[104,768]{1,0:T(8,128)(2,1)}, bf16[104,768]{1,0:T(8,128)(2,1)S(1)}, u32[]{:S(2)}, u32[]{:S(2)}) collective-permute-start(bf16[104,768]{1,0:T(8,128)(2,1)} %get-tuple-element.263), channel_id=1, source_target_pairs={{0,2},{2,0},{4,6},{6,4},{8,10},{10,8},{12,14},{14,12},{16,18},{18,... | collective-permute-start | bytes 479240 | tf_op jit(solution)/shard_map/ppermute | solution.py:809
  53.7 31.3 %collective-permute-start.4 = (bf16[104,768]{1,0:T(8,128)(2,1)}, bf16[104,768]{1,0:T(8,128)(2,1)S(1)}, u32[]{:S(2)}, u32[]{:S(2)}) collective-permute-start(bf16[104,768]{1,0:T(8,128)(2,1)} %get-tuple-element.264), channel_id=1, source_target_pairs={{0,10},{2,8},{4,14},{6,12},{8,2},{10,0},{12,6},{14,4},{16,26},{18,... | collective-permute-start | bytes 479240 | tf_op jit(solution)/shard_map/ppermute | solution.py:809
  90.1 28.6 %collective-permute-start.9 = (bf16[2,8,48,384]{3,2,1,0:T(8,128)(2,1)S(1)}, bf16[2,8,48,384]{3,2,1,0:T(8,128)(2,1)S(1)}, u32[]{:S(2)}, u32[]{:S(2)}) collective-permute-start(bf16[2,8,48,384]{3,2,1,0:T(8,128)(2,1)S(1)} %pad_maximum_fusion.5), channel_id=1, source_target_pairs={{0,1},{1,0},{2,3},{3,2},{4,5},{5,4},{6,7},{7,6},{8,9},{9,8},{10,11... | collective-permute-start | bytes 1769480 | tf_op jit(solution)/shard_map/ppermute | solution.py:1048
  91.7 28.5 %collective-permute-start.8 = (bf16[2,8,48,384]{3,2,1,0:T(8,128)(2,1)S(1)}, bf16[2,8,48,384]{3,2,1,0:T(8,128)(2,1)S(1)}, u32[]{:S(2)}, u32[]{:S(2)}) collective-permute-start(bf16[2,8,48,384]{3,2,1,0:T(8,128)(2,1)S(1)} %pad_maximum_fusion.4), channel_id=1, source_target_pairs={{0,16},{8,24},{16,0},{24,8},{1,17},{9,25},{17,1},{25,9},{2,18},{10... | collective-permute-start | bytes 1769480 | tf_op jit(solution)/shard_map/ppermute | solution.py:1048
  120.5 38.3 %collective-permute-start.14 = (bf16[4,8,48,384]{3,2,1,0:T(8,128)(2,1)S(1)}, bf16[4,8,48,384]{3,2,1,0:T(8,128)(2,1)}, u32[]{:S(2)}, u32[]{:S(2)}) collective-permute-start(bf16[4,8,48,384]{3,2,1,0:T(8,128)(2,1)S(1)} %pad_maximum_fusion.1.refs_2_), channel_id=1, source_target_pairs={{0,16},{8,24},{16,0},{24,8},{1,17},{9,25},{17,1},{25,9},{2,18},{10... | collective-permute-start | bytes 3538952 | tf_op jit(solution)/shard_map/ppermute | solution.py:1048
  122.1 36.8 %collective-permute-start.13 = (bf16[4,8,48,384]{3,2,1,0:T(8,128)(2,1)S(1)}, bf16[4,8,48,384]{3,2,1,0:T(8,128)(2,1)}, u32[]{:S(2)}, u32[]{:S(2)}) collective-permute-start(bf16[4,8,48,384]{3,2,1,0:T(8,128)(2,1)S(1)} %pad_maximum_fusion.refs_0_), channel_id=1, source_target_pairs={{0,1},{1,0},{2,3},{3,2},{4,5},{5,4},{6,7},{7,6},{8,9},{9,8},{10,11... | collective-permute-start | bytes 3538952 | tf_op jit(solution)/shard_map/ppermute | solution.py:1048
  123.8 35.1 %collective-permute-start.11 = (bf16[8,48,384]{2,1,0:T(8,128)(2,1)S(1)}, bf16[8,48,384]{2,1,0:T(8,128)(2,1)S(1)}, u32[]{:S(2)}, u32[]{:S(2)}) collective-permute-start(bf16[8,48,384]{2,1,0:T(8,128)(2,1)S(1)} %pad_maximum_fusion.13), channel_id=1, source_target_pairs={{0,4},{2,6},{4,0},{6,2},{1,5},{3,7},{5,1},{7,3},{8,12},{10,14},{12... | collective-permute-start | bytes 884744 | tf_op jit(solution)/shard_map/ppermute | solution.py:848
  124.6 34.2 %collective-permute-start.10 = (bf16[8,48,384]{2,1,0:T(8,128)(2,1)S(1)}, bf16[8,48,384]{2,1,0:T(8,128)(2,1)S(1)}, u32[]{:S(2)}, u32[]{:S(2)}) collective-permute-start(bf16[8,48,384]{2,1,0:T(8,128)(2,1)S(1)} %pad_maximum_fusion.13), channel_id=1, source_target_pairs={{0,2},{2,4},{4,6},{6,0},{1,3},{3,5},{5,7},{7,1},{8,10},{10,12},{12... | collective-permute-start | bytes 884744 | tf_op jit(solution)/shard_map/ppermute | solution.py:848
  139.6 32.8 %collective-permute-start.20 = (bf16[4,8,48,384]{3,2,1,0:T(8,128)(2,1)S(1)}, bf16[4,8,48,384]{3,2,1,0:T(8,128)(2,1)}, u32[]{:S(2)}, u32[]{:S(2)}) collective-permute-start(bf16[4,8,48,384]{3,2,1,0:T(8,128)(2,1)S(1)} %pad_maximum_fusion.1.refs_2_), channel_id=1, source_target_pairs={{0,8},{8,0},{16,24},{24,16},{1,9},{9,1},{17,25},{25,17},{2,10},{10... | collective-permute-start | bytes 3538952 | tf_op jit(solution)/shard_map/ppermute | solution.py:1048
  211.4 45.3 %collective-permute-start.28 = (bf16[4,8,48,384]{3,2,1,0:T(8,128)(2,1)S(1)}, bf16[4,8,48,384]{3,2,1,0:T(8,128)(2,1)}, u32[]{:S(2)}, u32[]{:S(2)}) collective-permute-start(bf16[4,8,48,384]{3,2,1,0:T(8,128)(2,1)S(1)} %pad_maximum_fusion.3.refs_2_), channel_id=1, source_target_pairs={{0,16},{8,24},{16,0},{24,8},{1,17},{9,25},{17,1},{25,9},{2,18},{10... | collective-permute-start | bytes 3538952 | tf_op jit(solution)/shard_map/ppermute | solution.py:1048
  211.9 45.7 %collective-permute-start.27 = (bf16[4,8,48,384]{3,2,1,0:T(8,128)(2,1)S(1)}, bf16[4,8,48,384]{3,2,1,0:T(8,128)(2,1)}, u32[]{:S(2)}, u32[]{:S(2)}) collective-permute-start(bf16[4,8,48,384]{3,2,1,0:T(8,128)(2,1)S(1)} %pad_maximum_fusion.2.refs_0_), channel_id=1, source_target_pairs={{0,1},{1,0},{2,3},{3,2},{4,5},{5,4},{6,7},{7,6},{8,9},{9,8},{10,11... | collective-permute-start | bytes 3538952 | tf_op jit(solution)/shard_map/ppermute | solution.py:1048
  236.1 58.3 %collective-permute-start.34 = (bf16[4,8,48,384]{3,2,1,0:T(8,128)(2,1)S(1)}, bf16[4,8,48,384]{3,2,1,0:T(8,128)(2,1)}, u32[]{:S(2)}, u32[]{:S(2)}) collective-permute-start(bf16[4,8,48,384]{3,2,1,0:T(8,128)(2,1)S(1)} %pad_maximum_fusion.3.refs_2_), channel_id=1, source_target_pairs={{0,8},{8,0},{16,24},{24,16},{1,9},{9,1},{17,25},{25,17},{2,10},{10... | collective-permute-start | bytes 3538952 | tf_op jit(solution)/shard_map/ppermute | solution.py:1048
  237.5 59.7 %collective-permute-start.32 = (bf16[4,8,48,384]{3,2,1,0:T(8,128)(2,1)S(1)}, bf16[4,8,48,384]{3,2,1,0:T(8,128)(2,1)}, u32[]{:S(2)}, u32[]{:S(2)}) collective-permute-start(bf16[4,8,48,384]{3,2,1,0:T(8,128)(2,1)S(1)} %pad_maximum_fusion.2.refs_0_), channel_id=1, source_target_pairs={{0,8},{8,0},{16,24},{24,16},{1,9},{9,1},{17,25},{25,17},{2,10},{10... | collective-permute-start | bytes 3538952 | tf_op jit(solution)/shard_map/ppermute | solution.py:1048
  257.6 47.6 %collective-permute-start.33 = (bf16[4,8,48,384]{3,2,1,0:T(8,128)(2,1)}, bf16[4,8,48,384]{3,2,1,0:T(8,128)(2,1)}, u32[]{:S(2)}, u32[]{:S(2)}) collective-permute-start(bf16[4,8,48,384]{3,2,1,0:T(8,128)(2,1)} %collective-permute-done.27.refs_1_), channel_id=1, source_target_pairs={{0,8},{8,0},{16,24},{24,16},{1,9},{9,1},{17,25},{25,17},{2,10},{10... | collective-permute-start | bytes 3538952 | tf_op jit(solution)/shard_map/ppermute | solution.py:1048
  257.6 47.6 %collective-permute-start.35 = (bf16[4,8,48,384]{3,2,1,0:T(8,128)(2,1)}, bf16[4,8,48,384]{3,2,1,0:T(8,128)(2,1)}, u32[]{:S(2)}, u32[]{:S(2)}) collective-permute-start(bf16[4,8,48,384]{3,2,1,0:T(8,128)(2,1)} %collective-permute-done.28.refs_3_), channel_id=1, source_target_pairs={{0,8},{8,0},{16,24},{24,16},{1,9},{9,1},{17,25},{25,17},{2,10},{10... | collective-permute-start | bytes 3538952 | tf_op jit(solution)/shard_map/ppermute | solution.py:1048
  381.0 29.7 %collective-permute-start.44 = (bf16[4,2,2,192,384]{4,3,2,1,0:T(8,128)(2,1)}, bf16[4,2,2,192,384]{4,3,2,1,0:T(8,128)(2,1)S(1)}, u32[]{:S(2)}, u32[]{:S(2)}) collective-permute-start(bf16[4,2,2,192,384]{4,3,2,1,0:T(8,128)(2,1)} %get-tuple-element.373), channel_id=1, source_target_pairs={{0,8},{8,0},{16,24},{24,16},{1,9},{9,1},{17,25},{25,17},{2,10},{10... | collective-permute-start | bytes 7077896 | tf_op jit(solution)/shard_map/ppermute | solution.py:1048
  472.9 29.7 %collective-permute-start.54 = (bf16[6,192,384]{2,1,0:T(8,128)(2,1)}, bf16[6,192,384]{2,1,0:T(8,128)(2,1)S(1)}, u32[]{:S(2)}, u32[]{:S(2)}) collective-permute-start(bf16[6,192,384]{2,1,0:T(8,128)(2,1)} %get-tuple-element.412), channel_id=1, source_target_pairs={{0,1},{1,0},{2,3},{3,2},{4,5},{5,4},{6,7},{7,6},{8,9},{9,8},{10,11... | collective-permute-start | bytes 2654216 | tf_op jit(solution)/shard_map/ppermute | solution.py:1048
  474.4 28.2 %collective-permute-start.55 = (bf16[8,192,384]{2,1,0:T(8,128)(2,1)}, bf16[8,192,384]{2,1,0:T(8,128)(2,1)S(1)}, u32[]{:S(2)}, u32[]{:S(2)}) collective-permute-start(bf16[8,192,384]{2,1,0:T(8,128)(2,1)} %get-tuple-element.413), channel_id=1, source_target_pairs={{0,16},{8,24},{16,0},{24,8},{1,17},{9,25},{17,1},{25,9},{2,18},{10... | collective-permute-start | bytes 3538952 | tf_op jit(solution)/shard_map/ppermute | solution.py:1048
  502.0 40.8 %collective-permute-start.58 = (bf16[4,2,2,192,384]{4,3,2,1,0:T(8,128)(2,1)}, bf16[4,2,2,192,384]{4,3,2,1,0:T(8,128)(2,1)}, u32[]{:S(2)}, u32[]{:S(2)}) collective-permute-start(bf16[4,2,2,192,384]{4,3,2,1,0:T(8,128)(2,1)} %get-tuple-element.429), channel_id=1, source_target_pairs={{0,8},{8,0},{16,24},{24,16},{1,9},{9,1},{17,25},{25,17},{2,10},{10... | collective-permute-start | bytes 7077896 | tf_op jit(solution)/shard_map/ppermute | solution.py:1048
  502.1 40.7 %collective-permute-start.59 = (bf16[4,2,2,192,384]{4,3,2,1,0:T(8,128)(2,1)}, bf16[4,2,2,192,384]{4,3,2,1,0:T(8,128)(2,1)}, u32[]{:S(2)}, u32[]{:S(2)}) collective-permute-start(bf16[4,2,2,192,384]{4,3,2,1,0:T(8,128)(2,1)} %get-tuple-element.431), channel_id=1, source_target_pairs={{0,8},{8,0},{16,24},{24,16},{1,9},{9,1},{17,25},{25,17},{2,10},{10... | collective-permute-start | bytes 7077896 | tf_op jit(solution)/shard_map/ppermute | solution.py:1048
  508.1 131.3 %reduce-scatter.11.cloned.1.call-start = ((), (), s32[]{:S(2)}) async-start(), calls=%async_computation.13 | async-start | bytes 1474560 | tf_op jit(solution)/shard_map/reduce_scatter | solution.py:1077
  529.7 28.9 %collective-permute-start.65 = (bf16[4,2,2,192,384]{4,3,2,1,0:T(8,128)(2,1)}, bf16[4,2,2,192,384]{4,3,2,1,0:T(8,128)(2,1)S(1)}, u32[]{:S(2)}, u32[]{:S(2)}) collective-permute-start(bf16[4,2,2,192,384]{4,3,2,1,0:T(8,128)(2,1)} %get-tuple-element.445), channel_id=1, source_target_pairs={{0,8},{8,0},{16,24},{24,16},{1,9},{9,1},{17,25},{25,17},{2,10},{10... | collective-permute-start | bytes 7077896 | tf_op jit(solution)/shard_map/ppermute | solution.py:1048
  529.8 143.5 %reduce-scatter.5.cloned.1.call-start = ((), (), s32[]{:S(2)}) async-start(), calls=%async_computation.10 | async-start | bytes 921600 | tf_op jit(solution)/shard_map/reduce_scatter | solution.py:1077
  585.2 113.8 %reduce-scatter.9.cloned.1.call-start = ((), (), s32[]{:S(2)}) async-start(), calls=%async_computation.12 | async-start | bytes 1474560 | tf_op jit(solution)/shard_map/reduce_scatter | solution.py:1077
  620.6 28.9 %collective-permute-start.77 = (bf16[8,192,384]{2,1,0:T(8,128)(2,1)}, bf16[8,192,384]{2,1,0:T(8,128)(2,1)S(1)}, u32[]{:S(2)}, u32[]{:S(2)}) collective-permute-start(bf16[8,192,384]{2,1,0:T(8,128)(2,1)} %get-tuple-element.487), channel_id=1, source_target_pairs={{0,16},{8,24},{16,0},{24,8},{1,17},{9,25},{17,1},{25,9},{2,18},{10... | collective-permute-start | bytes 3538952 | tf_op jit(solution)/shard_map/ppermute | solution.py:1048
  635.1 33.5 %all-to-all-start.1 = ((f32[32,1,384]{2,1,0:T(1,128)}), f32[32,1,384]{2,1,0:T(1,128)}, u32[]{:S(2)}, u32[]{:S(2)}) async-start(f32[32,1,384]{2,1,0:T(1,128)} %copy.125), calls=%async_computation.1 | async-start | bytes 98304 | tf_op jit(solution)/shard_map/all_to_all | solution.py:1136
  (135 other events, 1560.8 us)
Sparse Core Ops, SparseCore 0:
  11.7 144.2 all-gather.2
  159.6 121.9 all-gather.4
  508.2 19.7 reduce-scatter.6
  530.2 27.6 reduce-scatter.10
  585.3 21.4 reduce-scatter.4
  632.5 34.9 reduce-scatter.8

commit v23 on v22

--- a/solution.py
+++ b/solution.py
@@ -1270,8 +1270,8 @@
     norm_sums = reduce_norms(jnp.concatenate(norm_rows, axis=0)).reshape(layers, 2, 3, -1)
     if quick:
         tokens_grad = go_back(from_rows(grad.astype(BF16)))
-        tokens_grad = move(tokens_grad, late, me, True)
-        norm_sums = move(norm_sums, rest, me, True)
+        tokens_grad = move(tokens_grad, rest, me, True)
+        norm_sums = move(norm_sums, space + rest, me, True)
         summed = [[p.result for p in some] for some in summed]
     cuts = (2 * g_ff[0][0].shape[0], g_space[0].shape[0], g_out[0].shape[0], len(g_time))
     results = []

time: 731 us -> 743 us (1.016)
  waiting for transfers between devices: 236 us -> 251 us
    all_to_all x2 -> x1, waiting for transfers between devices: 13.2 us -> 22.2 us  [move(): lax.all_to_all(array, 'seq', split_axis=0, concat_axis=0, tiled=True)]
    all_to_all x1, waiting for transfers between devices: 13.9 us -> 6.27 us  [reduce_norms(): every = lax.all_to_all(a, ALL, split_axis=0, concat_axis=0, tiled=True)]
    unnamed x167 -> x165, local copies, waits for them, and re-layouts: 21.7 us -> 20.4 us
  transfers between devices with their start and end apart: 90 -> 89, of which waited for: 32 -> 32; matrix products, arithmetic and copies ran while one was open for 5% -> 4% of each run, Pallas kernels for 33% -> 33%
where the time goes in v23:
time: 743 us; the launch traced here: 737 us
  Pallas kernels  293 us (39%)
  waiting for transfers between devices  251 us (34%)
  starting transfers between devices  126 us (17%)
  local copies, waits for them, and re-layouts  32.4 us (4%)
  other arithmetic  18.1 us (2%)
  between operations  16.1 us (2%)
    pallas_call x18, Pallas kernels, call(): pl.pallas_call(body, out_shape=[shape for shape, _ in outs], grid=grid, i...  231 us
    ppermute x46, waiting for transfers between devices, cross(): return lax.ppermute(a, axis, [(i, i ^ 1 << bit) for i in range(size)])  90.1 us
    ppermute x24, waiting for transfers between devices, swap_places(): got.append(lax.ppermute(chunks[k], ('clip', 'seq'), pairs))  67 us
    ppermute x24, starting transfers between devices, swap_places(): got.append(lax.ppermute(chunks[k], ('clip', 'seq'), pairs))  47.2 us
    pallas_call x9, Pallas kernels, fold(): pl.pallas_call(body, out_shape=[jax.ShapeDtypeStruct(shape, BF16) for sha...  45.4 us
    ppermute x46, starting transfers between devices, cross(): return lax.ppermute(a, axis, [(i, i ^ 1 << bit) for i in range(size)])  39.1 us
    ppermute x6, waiting for transfers between devices, spread_steps(): lax.ppermute(pack, 'seq', [(i, (i + k) % ways) for i in range(ways)])  37.2 us
    all_gather x2, waiting for transfers between devices, gather_slabs(): full = lax.all_gather(pack, ('head', 'clip', 'seq'), axis=1, tiled=True)  22.7 us
  transfers between devices with their start and end apart: 89, of which 32 were waited for; matrix products, arithmetic and copies ran while one was open for 4% of the time, Pallas kernels for 33%

profile of v23, /device:TPU:0, one launch (start us, length us, event | category | flops | bytes accessed | tf_op | source)
XLA Modules:
  0.0 737.4 jit_solution(636400910433974160)
XLA Ops:
  33.3 8.0 %collective-permute-start.2 = (bf16[104,768]{1,0:T(8,128)(2,1)}, bf16[104,768]{1,0:T(8,128)(2,1)S(1)}, u32[]{:S(2)}, u32[]{:S(2)}) collective-permute-start(bf16[104,768]{1,0:T(8,128)(2,1)} %get-tuple-element.260), channel_id=1, source_target_pairs={{0,8},{2,10},{4,12},{6,14},{8,0},{10,2},{12,4},{14,6},{16,24},{18,... | collective-permute-start | bytes 479240 | tf_op jit(solution)/shard_map/ppermute | solution.py:809
  44.4 8.8 %collective-permute-start.6 = (bf16[8,48,384]{2,1,0:T(8,128)(2,1)S(1)}, bf16[8,48,384]{2,1,0:T(8,128)(2,1)S(1)}, u32[]{:S(2)}, u32[]{:S(2)}) collective-permute-start(bf16[8,48,384]{2,1,0:T(8,128)(2,1)S(1)} %pad_maximum_fusion.12), channel_id=1, source_target_pairs={{0,4},{2,6},{4,0},{6,2},{1,5},{3,7},{5,1},{7,3},{8,12},{10,14},{12... | collective-permute-start | bytes 884744 | tf_op jit(solution)/shard_map/ppermute | solution.py:848
  54.5 27.6 %collective-permute-done.3.refs_2_ = bf16[104,768]{1,0:T(8,128)(2,1)S(1)} collective-permute-done((bf16[104,768]{1,0:T(8,128)(2,1)}, bf16[104,768]{1,0:T(8,128)(2,1)S(1)}, u32[]{:S(2)}, u32[]{:S(2)}) %collective-permute-start.3) | collective-permute-done | bytes 159776 | tf_op jit(solution)/shard_map/ppermute | solution.py:809
  93.3 25.4 %collective-permute-done.9 = bf16[2,8,48,384]{3,2,1,0:T(8,128)(2,1)S(1)} collective-permute-done((bf16[2,8,48,384]{3,2,1,0:T(8,128)(2,1)S(1)}, bf16[2,8,48,384]{3,2,1,0:T(8,128)(2,1)S(1)}, u32[]{:S(2)}, u32[]{:S(2)}) %collective-permute-start.9) | collective-permute-done | bytes 589856 | tf_op jit(solution)/shard_map/ppermute | solution.py:1048
  126.6 13.1 %collective-permute-done.12 = bf16[8,48,384]{2,1,0:T(8,128)(2,1)S(1)} collective-permute-done((bf16[8,48,384]{2,1,0:T(8,128)(2,1)S(1)}, bf16[8,48,384]{2,1,0:T(8,128)(2,1)S(1)}, u32[]{:S(2)}, u32[]{:S(2)}) %collective-permute-start.12) | collective-permute-done | bytes 294944 | tf_op jit(solution)/shard_map/ppermute | solution.py:848
  139.6 19.2 %collective-permute-done.11 = bf16[8,48,384]{2,1,0:T(8,128)(2,1)S(1)} collective-permute-done((bf16[8,48,384]{2,1,0:T(8,128)(2,1)S(1)}, bf16[8,48,384]{2,1,0:T(8,128)(2,1)S(1)}, u32[]{:S(2)}, u32[]{:S(2)}) %collective-permute-start.11) | collective-permute-done | bytes 294944 | tf_op jit(solution)/shard_map/ppermute | solution.py:848
  159.5 12.7 %shard_map.195 = (bf16[416,768]{1,0:T(8,128)(2,1)}, bf16[3,416,768]{2,1,0:T(8,128)(2,1)}, f32[2,3,2,416]{3,2,1,0:T(2,128)}, bf16[104,768]{1,0:T(8,128)(2,1)}, bf...) custom-call(bf16[104,768]{1,0:T(8,128)(2,1)} %get-tuple-element.287.refs_0_, ...), custom_call_target="tpu_custom_call" | custom-call | flops 1472200704 | bytes 14470656 | tf_op jit(solution)/shard_map/pallas_call | solution.py:212
  191.8 9.4 %shard_map.196 = (bf16[416,768]{1,0:T(8,128)(2,1)}, bf16[416,768]{1,0:T(8,128)(2,1)}, f32[416,768]{1,0:T(8,128)}, bf16[3,416,768]{2,1,0:T(8,128)(2,1)}) custom-call(s32[5]{0:T(128)} %stack.110.me_ref, bf16[104,768]{1,0:T(8,128)(2,1)} %get-tuple-element.305.refs_0_, bf16[104,768]{1,0:T(8,128)(2,1)} %copy-done.44, bf16[104,768]{1,0:T(8,128)(2,1)} %copy-done.45, ...), custom_call_target="tpu_custom_call" | custom-call | flops 2453667840 | bytes 28821524 | tf_op jit(solution)/shard_map/pallas_call | solution.py:212
  201.2 9.9 %shard_map.197 = (bf16[416,768]{1,0:T(8,128)(2,1)}, f32[416,768]{1,0:T(8,128)}, f32[2,3,2,2,208]{4,3,2,1,0:T(2,128)}) custom-call(bf16[3,416,768]{2,1,0:T(8,128)(2,1)} %get-tuple-element.309.qkv_ref, f32[416,768]{1,0:T(8,128)} %get-tuple-element.310.x1_ref, bf16[9,2,768,384]{3,2,1,0:T(8,128)(2,1)} %bitcast.201), custom_call_target="tpu_custom_call" | custom-call | flops 490733568 | bytes 15748608 | tf_op jit(solution)/shard_map/pallas_call | solution.py:212
  213.3 9.0 %shard_map.198 = bf16[8,2,16,48,384]{4,3,2,1,0:T(8,128)(2,1)} custom-call(s32[5]{0:T(128)} %stack.110.me_ref, bf16[4,8,48,384]{3,2,1,0:T(8,128)(2,1)} %copy-done.21, bf16[4,8,48,384]{3,2,1,0:T(8,128)(2,1)} %collective-permute-done.13.refs_1_, bf16[4,8,48,384]{3,2,1,0:T(8,128)(2,1)} %copy-done.22, bf16[4,8,48,384]{3,2,1,0:T(8,128)(2,1)} %collective-permute-done.14.refs_3_, ...), custom_call_target="tpu_custom_call" | custom-call | bytes 18874368 | tf_op jit(solution)/shard_map/pallas_call | solution.py:883
  222.3 13.3 %shard_map.199 = (f32[416,768]{1,0:T(8,128)}, bf16[104,768]{1,0:T(8,128)(2,1)}, bf16[104,768]{1,0:T(8,128)(2,1)}, bf16[104,768]{1,0:T(8,128)(2,1)}, bf16[104,768]{1,0:T(8,128)(2,1)}) custom-call(f32[416,768]{1,0:T(8,128)} %get-tuple-element.316.x2_ref, bf16[8,2,768,384]{3,2,1,0:T(8,128)(2,1)} %bitcast.214, bf16[8,2,768,384]{3,2,1,0:T(8,128)(2,1)} %bitcast.215, ...), custom_call_target="tpu_custom_call" | custom-call | flops 3925868544 | bytes 22106132 | tf_op jit(solution)/shard_map/pallas_call | solution.py:212
  242.3 7.9 %collective-permute-done.26.refs_3_ = bf16[104,768]{1,0:T(8,128)(2,1)S(1)} collective-permute-done((bf16[104,768]{1,0:T(8,128)(2,1)}, bf16[104,768]{1,0:T(8,128)(2,1)S(1)}, u32[]{:S(2)}, u32[]{:S(2)}) %collective-permute-start.26) | collective-permute-done | bytes 159776 | tf_op jit(solution)/shard_map/ppermute | solution.py:809
  259.1 22.7 %all-gather.5.cloned.1.call-done = bf16[9,1536,384]{2,1,0:T(8,128)(2,1)} async-done(((bf16[9,48,384]{2,1,0:T(8,128)(2,1)}), bf16[9,1536,384]{2,1,0:T(8,128)(2,1)}) %all-gather.5.cloned.1.call-update) | async-done | bytes 10616848 | tf_op jit(solution)/shard_map/all_gather | solution.py:838
  281.8 12.4 %shard_map.200 = (bf16[416,768]{1,0:T(8,128)(2,1)}, bf16[3,416,768]{2,1,0:T(8,128)(2,1)}, f32[2,3,2,416]{3,2,1,0:T(2,128)}, bf16[104,768]{1,0:T(8,128)(2,1)}, bf...) custom-call(bf16[104,768]{1,0:T(8,128)(2,1)} %get-tuple-element.328.refs_0_, ...), custom_call_target="tpu_custom_call" | custom-call | flops 1472200704 | bytes 14470656 | tf_op jit(solution)/shard_map/pallas_call | solution.py:212
  306.0 9.4 %shard_map.201 = (bf16[416,768]{1,0:T(8,128)(2,1)}, bf16[416,768]{1,0:T(8,128)(2,1)}, f32[416,768]{1,0:T(8,128)}, bf16[3,416,768]{2,1,0:T(8,128)(2,1)}) custom-call(s32[5]{0:T(128)} %stack.110.me_ref, bf16[104,768]{1,0:T(8,128)(2,1)} %get-tuple-element.338.refs_0_, bf16[104,768]{1,0:T(8,128)(2,1)} %copy-done.46, bf16[104,768]{1,0:T(8,128)(2,1)} %copy-done.48, ...), custom_call_target="tpu_custom_call" | custom-call | flops 2453667840 | bytes 28821524 | tf_op jit(solution)/shard_map/pallas_call | solution.py:212
  315.4 9.9 %shard_map.202 = (bf16[416,768]{1,0:T(8,128)(2,1)}, f32[416,768]{1,0:T(8,128)}, f32[2,3,2,2,208]{4,3,2,1,0:T(2,128)}) custom-call(bf16[3,416,768]{2,1,0:T(8,128)(2,1)} %get-tuple-element.343.qkv_ref, f32[416,768]{1,0:T(8,128)} %get-tuple-element.344.x1_ref, bf16[9,2,768,384]{3,2,1,0:T(8,128)(2,1)} %bitcast.209), custom_call_target="tpu_custom_call" | custom-call | flops 490733568 | bytes 15748608 | tf_op jit(solution)/shard_map/pallas_call | solution.py:212
  325.3 8.3 %shard_map.203 = bf16[8,2,16,48,384]{4,3,2,1,0:T(8,128)(2,1)} custom-call(s32[5]{0:T(128)} %stack.110.me_ref, bf16[4,8,48,384]{3,2,1,0:T(8,128)(2,1)} %copy-done.23, bf16[4,8,48,384]{3,2,1,0:T(8,128)(2,1)} %collective-permute-done.27.refs_1_, bf16[4,8,48,384]{3,2,1,0:T(8,128)(2,1)} %copy-done.24, bf16[4,8,48,384]{3,2,1,0:T(8,128)(2,1)} %collective-permute-done.28.refs_3_, ...), custom_call_target="tpu_custom_call" | custom-call | bytes 18874368 | tf_op jit(solution)/shard_map/pallas_call | solution.py:883
  333.5 25.1 %shard_map.204 = (f32[416,768]{1,0:T(8,128)}, bf16[4,2,2,192,384]{4,3,2,1,0:T(8,128)(2,1)}, bf16[4,2,2,192,384]{4,3,2,1,0:T(8,128)(2,1)}, bf16[4,2,2,192,384]{4,...) custom-call(s32[5]{0:T(128)} %stack.110.me_ref, ...), custom_call_target="tpu_custom_call" | custom-call | flops 9814671360 | bytes 33447956 | tf_op jit(solution)/shard_map/pallas_call | solution.py:212
  359.3 21.6 %shard_map.205 = (f32[416,768]{1,0:T(8,128)}, bf16[4,2,2,192,384]{4,3,2,1,0:T(8,128)(2,1)}, bf16[4,2,2,192,384]{4,3,2,1,0:T(8,128)(2,1)}, f32[2,768]{1,0:T(2,128)}) custom-call(s32[5]{0:T(128)} %stack.110.me_ref, f32[416,768]{1,0:T(8,128)} %get-tuple-element.350.g_ref, f32[416,768]{1,0:T(8,128)} %get-tuple-element.344.x1_ref, ...), custom_call_target="tpu_custom_call" | custom-call | flops 3925868544 | bytes 32386580 | tf_op jit(solution)/shard_map/pallas_call | solution.py:212
  392.3 7.8 %shard_map.207 = (bf16[104,768]{1,0:T(8,128)(2,1)}, bf16[104,768]{1,0:T(8,128)(2,1)}, bf16[104,768]{1,0:T(8,128)(2,1)}, bf16[104,768]{1,0:T(8,128)(2,1)}, bf16[2...) custom-call(s32[5]{0:T(128)} %stack.110.me_ref, f32[416,768]{1,0:T(8,128)} %get-tuple-element.361.g_ref.refs_5_, ...), custom_call_target="tpu_custom_call" | custom-call | flops 1962934272 | bytes 17350676 | tf_op jit(solution)/shard_map/pallas_call | solution.py:212
  400.0 10.3 %collective-permute-start.39 = (bf16[104,768]{1,0:T(8,128)(2,1)}, bf16[104,768]{1,0:T(8,128)(2,1)S(1)}, u32[]{:S(2)}, u32[]{:S(2)}) collective-permute-start(bf16[104,768]{1,0:T(8,128)(2,1)} %get-tuple-element.365), channel_id=1, source_target_pairs={{0,8},{2,10},{4,12},{6,14},{8,0},{10,2},{12,4},{14,6},{16,24},{18,... | collective-permute-start | bytes 479240 | tf_op jit(solution)/shard_map/ppermute | solution.py:809
  427.9 18.1 %shard_map.209 = (bf16[104,768]{1,0:T(8,128)(2,1)}, bf16[104,768]{1,0:T(8,128)(2,1)}, bf16[104,768]{1,0:T(8,128)(2,1)}, bf16[104,768]{1,0:T(8,128)(2,1)}, bf16[1...) custom-call(s32[5]{0:T(128)} %stack.110.me_ref, ...), custom_call_target="tpu_custom_call" | custom-call | flops 2944401408 | bytes 18009620 | tf_op jit(solution)/shard_map/pallas_call | solution.py:212
  449.6 15.3 %collective-permute-start.48 = (bf16[104,768]{1,0:T(8,128)(2,1)}, bf16[104,768]{1,0:T(8,128)(2,1)S(1)}, u32[]{:S(2)}, u32[]{:S(2)}) collective-permute-start(bf16[104,768]{1,0:T(8,128)(2,1)} %get-tuple-element.389), channel_id=1, source_target_pairs={{0,2},{2,0},{4,6},{6,4},{8,10},{10,8},{12,14},{14,12},{16,18},{18,... | collective-permute-start | bytes 479240 | tf_op jit(solution)/shard_map/ppermute | solution.py:809
  479.5 22.1 %shard_map.212 = (f32[416,768]{1,0:T(8,128)}, bf16[4,2,2,192,384]{4,3,2,1,0:T(8,128)(2,1)}, bf16[4,2,2,192,384]{4,3,2,1,0:T(8,128)(2,1)}, bf16[4,2,2,192,384]{4,...) custom-call(s32[5]{0:T(128)} %stack.110.me_ref, f32[416,768]{1,0:T(8,128)} %get-tuple-element.408.g_ref, ...), custom_call_target="tpu_custom_call" | custom-call | flops 9814671360 | bytes 32170004 | tf_op jit(solution)/shard_map/pallas_call | solution.py:212
  507.7 21.5 %shard_map.214 = (f32[416,768]{1,0:T(8,128)}, bf16[4,2,2,192,384]{4,3,2,1,0:T(8,128)(2,1)}, bf16[4,2,2,192,384]{4,3,2,1,0:T(8,128)(2,1)}, f32[2,768]{1,0:T(2,128)}) custom-call(s32[5]{0:T(128)} %stack.110.me_ref, f32[416,768]{1,0:T(8,128)} %get-tuple-element.418.g_ref, f32[416,768]{1,0:T(8,128)} %get-tuple-element.310.x1_ref, ...), custom_call_target="tpu_custom_call" | custom-call | flops 3925868544 | bytes 32386580 | tf_op jit(solution)/shard_map/pallas_call | solution.py:212
  531.2 8.3 %collective-permute-done.57.refs_17_ = bf16[2,192,384]{2,1,0:T(8,128)(2,1)S(1)} collective-permute-done((bf16[2,192,384]{2,1,0:T(8,128)(2,1)}, bf16[2,192,384]{2,1,0:T(8,128)(2,1)S(1)}, u32[]{:S(2)}, u32[]{:S(2)}) %collective-permute-start.57) | collective-permute-done | bytes 294944 | tf_op jit(solution)/shard_map/ppermute | solution.py:1048
  548.6 7.8 %shard_map.216 = (bf16[104,768]{1,0:T(8,128)(2,1)}, bf16[104,768]{1,0:T(8,128)(2,1)}, bf16[104,768]{1,0:T(8,128)(2,1)}, bf16[104,768]{1,0:T(8,128)(2,1)}, bf16[2...) custom-call(s32[5]{0:T(128)} %stack.110.me_ref, f32[416,768]{1,0:T(8,128)} %get-tuple-element.433.g_ref.refs_5_, ...), custom_call_target="tpu_custom_call" | custom-call | flops 1962934272 | bytes 17350676 | tf_op jit(solution)/shard_map/pallas_call | solution.py:212
  558.2 16.6 %collective-permute-done.63.refs_2_ = bf16[8,192,384]{2,1,0:T(8,128)(2,1)S(1)} collective-permute-done((bf16[8,192,384]{2,1,0:T(8,128)(2,1)}, bf16[8,192,384]{2,1,0:T(8,128)(2,1)S(1)}, u32[]{:S(2)}, u32[]{:S(2)}) %collective-permute-start.63) | collective-permute-done | bytes 1179680 | tf_op jit(solution)/shard_map/ppermute | solution.py:1048
  584.6 18.1 %shard_map.218 = (bf16[104,768]{1,0:T(8,128)(2,1)}, bf16[104,768]{1,0:T(8,128)(2,1)}, bf16[104,768]{1,0:T(8,128)(2,1)}, bf16[104,768]{1,0:T(8,128)(2,1)}, bf16[1...) custom-call(s32[5]{0:T(128)} %stack.110.me_ref, ...), custom_call_target="tpu_custom_call" | custom-call | flops 2944401408 | bytes 18009620 | tf_op jit(solution)/shard_map/pallas_call | solution.py:212
  639.2 13.7 %collective-permute-done.77.refs_7_.refs_3_ = bf16[6,192,384]{2,1,0:T(8,128)(2,1)S(1)} collective-permute-done((bf16[6,192,384]{2,1,0:T(8,128)(2,1)}, bf16[6,192,384]{2,1,0:T(8,128)(2,1)S(1)}, u32[]{:S(2)}, u32[]{:S(2)}) %collective-permute-start.77) | collective-permute-done | bytes 884768 | tf_op jit(solution)/shard_map/ppermute | solution.py:1048
  666.0 10.3 %all-to-all-start.1 = ((f32[32,1,384]{2,1,0:T(1,128)}), f32[32,1,384]{2,1,0:T(1,128)S(1)}, u32[]{:S(2)}, u32[]{:S(2)}) async-start(f32[32,1,384]{2,1,0:T(1,128)} %copy.125), calls=%async_computation.1 | async-start | bytes 98304 | tf_op jit(solution)/shard_map/all_to_all | solution.py:1136
  703.3 22.2 %all-to-all-done.2 = bf16[4,9,48,384]{3,2,1,0:T(8,128)(2,1)S(1)} async-done(((bf16[4,9,48,384]{3,2,1,0:T(8,128)(2,1)}), bf16[4,9,48,384]{3,2,1,0:T(8,128)(2,1)S(1)}, u32[]{:S(2)}, u32[]{:S(2)}) %all-to-all-start.2) | async-done | bytes 1327136 | tf_op jit(solution)/shard_map/all_to_all | solution.py:1074
  (441 shorter events, 255.6 us)
Async XLA Ops:
  7.2 152.3 %all-gather.3.cloned.1.call-start = ((), (), s32[]{:S(2)}) async-start(), calls=%async_computation.7 | async-start | bytes 10948608 | tf_op jit(solution)/shard_map/all_gather | solution.py:838
  11.0 270.8 %all-gather.5.cloned.1.call-start = ((), (), s32[]{:S(2)}) async-start(), calls=%async_computation.8 | async-start | bytes 10948608 | tf_op jit(solution)/shard_map/all_gather | solution.py:838
  20.0 656.3 %reduce-scatter.7.cloned.1.call-start = ((), (), s32[]{:S(2)}) async-start(), calls=%async_computation.10 | async-start | bytes 737280 | tf_op jit(solution)/shard_map/reduce_scatter | solution.py:1077
  41.3 43.9 %collective-permute-start.7 = (bf16[8,48,384]{2,1,0:T(8,128)(2,1)S(1)}, bf16[8,48,384]{2,1,0:T(8,128)(2,1)S(1)}, u32[]{:S(2)}, u32[]{:S(2)}) collective-permute-start(bf16[8,48,384]{2,1,0:T(8,128)(2,1)S(1)} %pad_maximum_fusion.12), channel_id=1, source_target_pairs={{0,6},{2,0},{4,2},{6,4},{1,7},{3,1},{5,3},{7,5},{8,14},{10,8},{12,... | collective-permute-start | bytes 884744 | tf_op jit(solution)/shard_map/ppermute | solution.py:848
  44.4 45.7 %collective-permute-start.6 = (bf16[8,48,384]{2,1,0:T(8,128)(2,1)S(1)}, bf16[8,48,384]{2,1,0:T(8,128)(2,1)S(1)}, u32[]{:S(2)}, u32[]{:S(2)}) collective-permute-start(bf16[8,48,384]{2,1,0:T(8,128)(2,1)S(1)} %pad_maximum_fusion.12), channel_id=1, source_target_pairs={{0,4},{2,6},{4,0},{6,2},{1,5},{3,7},{5,1},{7,3},{8,12},{10,14},{12... | collective-permute-start | bytes 884744 | tf_op jit(solution)/shard_map/ppermute | solution.py:848
  53.2 36.9 %collective-permute-start.5 = (bf16[8,48,384]{2,1,0:T(8,128)(2,1)S(1)}, bf16[8,48,384]{2,1,0:T(8,128)(2,1)S(1)}, u32[]{:S(2)}, u32[]{:S(2)}) collective-permute-start(bf16[8,48,384]{2,1,0:T(8,128)(2,1)S(1)} %pad_maximum_fusion.12), channel_id=1, source_target_pairs={{0,2},{2,4},{4,6},{6,0},{1,3},{3,5},{5,7},{7,1},{8,10},{10,12},{12... | collective-permute-start | bytes 884744 | tf_op jit(solution)/shard_map/ppermute | solution.py:848
  53.2 28.8 %collective-permute-start.3 = (bf16[104,768]{1,0:T(8,128)(2,1)}, bf16[104,768]{1,0:T(8,128)(2,1)S(1)}, u32[]{:S(2)}, u32[]{:S(2)}) collective-permute-start(bf16[104,768]{1,0:T(8,128)(2,1)} %get-tuple-element.261), channel_id=1, source_target_pairs={{0,2},{2,0},{4,6},{6,4},{8,10},{10,8},{12,14},{14,12},{16,18},{18,... | collective-permute-start | bytes 479240 | tf_op jit(solution)/shard_map/ppermute | solution.py:809
  53.8 31.3 %collective-permute-start.4 = (bf16[104,768]{1,0:T(8,128)(2,1)}, bf16[104,768]{1,0:T(8,128)(2,1)S(1)}, u32[]{:S(2)}, u32[]{:S(2)}) collective-permute-start(bf16[104,768]{1,0:T(8,128)(2,1)} %get-tuple-element.262), channel_id=1, source_target_pairs={{0,10},{2,8},{4,14},{6,12},{8,2},{10,0},{12,6},{14,4},{16,26},{18,... | collective-permute-start | bytes 479240 | tf_op jit(solution)/shard_map/ppermute | solution.py:809
  90.1 28.6 %collective-permute-start.9 = (bf16[2,8,48,384]{3,2,1,0:T(8,128)(2,1)S(1)}, bf16[2,8,48,384]{3,2,1,0:T(8,128)(2,1)S(1)}, u32[]{:S(2)}, u32[]{:S(2)}) collective-permute-start(bf16[2,8,48,384]{3,2,1,0:T(8,128)(2,1)S(1)} %pad_maximum_fusion.5), channel_id=1, source_target_pairs={{0,1},{1,0},{2,3},{3,2},{4,5},{5,4},{6,7},{7,6},{8,9},{9,8},{10,11... | collective-permute-start | bytes 1769480 | tf_op jit(solution)/shard_map/ppermute | solution.py:1048
  91.7 28.5 %collective-permute-start.8 = (bf16[2,8,48,384]{3,2,1,0:T(8,128)(2,1)S(1)}, bf16[2,8,48,384]{3,2,1,0:T(8,128)(2,1)S(1)}, u32[]{:S(2)}, u32[]{:S(2)}) collective-permute-start(bf16[2,8,48,384]{3,2,1,0:T(8,128)(2,1)S(1)} %pad_maximum_fusion.4), channel_id=1, source_target_pairs={{0,16},{8,24},{16,0},{24,8},{1,17},{9,25},{17,1},{25,9},{2,18},{10... | collective-permute-start | bytes 1769480 | tf_op jit(solution)/shard_map/ppermute | solution.py:1048
  120.5 38.3 %collective-permute-start.14 = (bf16[4,8,48,384]{3,2,1,0:T(8,128)(2,1)S(1)}, bf16[4,8,48,384]{3,2,1,0:T(8,128)(2,1)}, u32[]{:S(2)}, u32[]{:S(2)}) collective-permute-start(bf16[4,8,48,384]{3,2,1,0:T(8,128)(2,1)S(1)} %pad_maximum_fusion.1.refs_2_), channel_id=1, source_target_pairs={{0,16},{8,24},{16,0},{24,8},{1,17},{9,25},{17,1},{25,9},{2,18},{10... | collective-permute-start | bytes 3538952 | tf_op jit(solution)/shard_map/ppermute | solution.py:1048
  122.1 36.8 %collective-permute-start.13 = (bf16[4,8,48,384]{3,2,1,0:T(8,128)(2,1)S(1)}, bf16[4,8,48,384]{3,2,1,0:T(8,128)(2,1)}, u32[]{:S(2)}, u32[]{:S(2)}) collective-permute-start(bf16[4,8,48,384]{3,2,1,0:T(8,128)(2,1)S(1)} %pad_maximum_fusion.refs_0_), channel_id=1, source_target_pairs={{0,1},{1,0},{2,3},{3,2},{4,5},{5,4},{6,7},{7,6},{8,9},{9,8},{10,11... | collective-permute-start | bytes 3538952 | tf_op jit(solution)/shard_map/ppermute | solution.py:1048
  123.8 35.1 %collective-permute-start.11 = (bf16[8,48,384]{2,1,0:T(8,128)(2,1)S(1)}, bf16[8,48,384]{2,1,0:T(8,128)(2,1)S(1)}, u32[]{:S(2)}, u32[]{:S(2)}) collective-permute-start(bf16[8,48,384]{2,1,0:T(8,128)(2,1)S(1)} %pad_maximum_fusion.13), channel_id=1, source_target_pairs={{0,4},{2,6},{4,0},{6,2},{1,5},{3,7},{5,1},{7,3},{8,12},{10,14},{12... | collective-permute-start | bytes 884744 | tf_op jit(solution)/shard_map/ppermute | solution.py:848
  124.6 34.2 %collective-permute-start.10 = (bf16[8,48,384]{2,1,0:T(8,128)(2,1)S(1)}, bf16[8,48,384]{2,1,0:T(8,128)(2,1)S(1)}, u32[]{:S(2)}, u32[]{:S(2)}) collective-permute-start(bf16[8,48,384]{2,1,0:T(8,128)(2,1)S(1)} %pad_maximum_fusion.13), channel_id=1, source_target_pairs={{0,2},{2,4},{4,6},{6,0},{1,3},{3,5},{5,7},{7,1},{8,10},{10,12},{12... | collective-permute-start | bytes 884744 | tf_op jit(solution)/shard_map/ppermute | solution.py:848
  139.6 33.1 %collective-permute-start.20 = (bf16[4,8,48,384]{3,2,1,0:T(8,128)(2,1)S(1)}, bf16[4,8,48,384]{3,2,1,0:T(8,128)(2,1)}, u32[]{:S(2)}, u32[]{:S(2)}) collective-permute-start(bf16[4,8,48,384]{3,2,1,0:T(8,128)(2,1)S(1)} %pad_maximum_fusion.1.refs_2_), channel_id=1, source_target_pairs={{0,8},{8,0},{16,24},{24,16},{1,9},{9,1},{17,25},{25,17},{2,10},{10... | collective-permute-start | bytes 3538952 | tf_op jit(solution)/shard_map/ppermute | solution.py:1048
  211.4 45.4 %collective-permute-start.28 = (bf16[4,8,48,384]{3,2,1,0:T(8,128)(2,1)S(1)}, bf16[4,8,48,384]{3,2,1,0:T(8,128)(2,1)}, u32[]{:S(2)}, u32[]{:S(2)}) collective-permute-start(bf16[4,8,48,384]{3,2,1,0:T(8,128)(2,1)S(1)} %pad_maximum_fusion.3.refs_2_), channel_id=1, source_target_pairs={{0,16},{8,24},{16,0},{24,8},{1,17},{9,25},{17,1},{25,9},{2,18},{10... | collective-permute-start | bytes 3538952 | tf_op jit(solution)/shard_map/ppermute | solution.py:1048
  212.0 45.7 %collective-permute-start.27 = (bf16[4,8,48,384]{3,2,1,0:T(8,128)(2,1)S(1)}, bf16[4,8,48,384]{3,2,1,0:T(8,128)(2,1)}, u32[]{:S(2)}, u32[]{:S(2)}) collective-permute-start(bf16[4,8,48,384]{3,2,1,0:T(8,128)(2,1)S(1)} %pad_maximum_fusion.2.refs_0_), channel_id=1, source_target_pairs={{0,1},{1,0},{2,3},{3,2},{4,5},{5,4},{6,7},{7,6},{8,9},{9,8},{10,11... | collective-permute-start | bytes 3538952 | tf_op jit(solution)/shard_map/ppermute | solution.py:1048
  236.1 58.4 %collective-permute-start.34 = (bf16[4,8,48,384]{3,2,1,0:T(8,128)(2,1)S(1)}, bf16[4,8,48,384]{3,2,1,0:T(8,128)(2,1)}, u32[]{:S(2)}, u32[]{:S(2)}) collective-permute-start(bf16[4,8,48,384]{3,2,1,0:T(8,128)(2,1)S(1)} %pad_maximum_fusion.3.refs_2_), channel_id=1, source_target_pairs={{0,8},{8,0},{16,24},{24,16},{1,9},{9,1},{17,25},{25,17},{2,10},{10... | collective-permute-start | bytes 3538952 | tf_op jit(solution)/shard_map/ppermute | solution.py:1048
  237.2 60.1 %collective-permute-start.32 = (bf16[4,8,48,384]{3,2,1,0:T(8,128)(2,1)S(1)}, bf16[4,8,48,384]{3,2,1,0:T(8,128)(2,1)}, u32[]{:S(2)}, u32[]{:S(2)}) collective-permute-start(bf16[4,8,48,384]{3,2,1,0:T(8,128)(2,1)S(1)} %pad_maximum_fusion.2.refs_0_), channel_id=1, source_target_pairs={{0,8},{8,0},{16,24},{24,16},{1,9},{9,1},{17,25},{25,17},{2,10},{10... | collective-permute-start | bytes 3538952 | tf_op jit(solution)/shard_map/ppermute | solution.py:1048
  257.7 47.7 %collective-permute-start.33 = (bf16[4,8,48,384]{3,2,1,0:T(8,128)(2,1)}, bf16[4,8,48,384]{3,2,1,0:T(8,128)(2,1)}, u32[]{:S(2)}, u32[]{:S(2)}) collective-permute-start(bf16[4,8,48,384]{3,2,1,0:T(8,128)(2,1)} %collective-permute-done.27.refs_1_), channel_id=1, source_target_pairs={{0,8},{8,0},{16,24},{24,16},{1,9},{9,1},{17,25},{25,17},{2,10},{10... | collective-permute-start | bytes 3538952 | tf_op jit(solution)/shard_map/ppermute | solution.py:1048
  257.7 47.7 %collective-permute-start.35 = (bf16[4,8,48,384]{3,2,1,0:T(8,128)(2,1)}, bf16[4,8,48,384]{3,2,1,0:T(8,128)(2,1)}, u32[]{:S(2)}, u32[]{:S(2)}) collective-permute-start(bf16[4,8,48,384]{3,2,1,0:T(8,128)(2,1)} %collective-permute-done.28.refs_3_), channel_id=1, source_target_pairs={{0,8},{8,0},{16,24},{24,16},{1,9},{9,1},{17,25},{25,17},{2,10},{10... | collective-permute-start | bytes 3538952 | tf_op jit(solution)/shard_map/ppermute | solution.py:1048
  380.8 29.7 %collective-permute-start.44 = (bf16[4,2,2,192,384]{4,3,2,1,0:T(8,128)(2,1)}, bf16[4,2,2,192,384]{4,3,2,1,0:T(8,128)(2,1)S(1)}, u32[]{:S(2)}, u32[]{:S(2)}) collective-permute-start(bf16[4,2,2,192,384]{4,3,2,1,0:T(8,128)(2,1)} %get-tuple-element.371), channel_id=1, source_target_pairs={{0,8},{8,0},{16,24},{24,16},{1,9},{9,1},{17,25},{25,17},{2,10},{10... | collective-permute-start | bytes 7077896 | tf_op jit(solution)/shard_map/ppermute | solution.py:1048
  472.7 29.6 %collective-permute-start.54 = (bf16[6,192,384]{2,1,0:T(8,128)(2,1)}, bf16[6,192,384]{2,1,0:T(8,128)(2,1)S(1)}, u32[]{:S(2)}, u32[]{:S(2)}) collective-permute-start(bf16[6,192,384]{2,1,0:T(8,128)(2,1)} %get-tuple-element.410), channel_id=1, source_target_pairs={{0,1},{1,0},{2,3},{3,2},{4,5},{5,4},{6,7},{7,6},{8,9},{9,8},{10,11... | collective-permute-start | bytes 2654216 | tf_op jit(solution)/shard_map/ppermute | solution.py:1048
  501.7 40.4 %collective-permute-start.58 = (bf16[4,2,2,192,384]{4,3,2,1,0:T(8,128)(2,1)}, bf16[4,2,2,192,384]{4,3,2,1,0:T(8,128)(2,1)}, u32[]{:S(2)}, u32[]{:S(2)}) collective-permute-start(bf16[4,2,2,192,384]{4,3,2,1,0:T(8,128)(2,1)} %get-tuple-element.427), channel_id=1, source_target_pairs={{0,8},{8,0},{16,24},{24,16},{1,9},{9,1},{17,25},{25,17},{2,10},{10... | collective-permute-start | bytes 7077896 | tf_op jit(solution)/shard_map/ppermute | solution.py:1048
  501.7 40.4 %collective-permute-start.59 = (bf16[4,2,2,192,384]{4,3,2,1,0:T(8,128)(2,1)}, bf16[4,2,2,192,384]{4,3,2,1,0:T(8,128)(2,1)}, u32[]{:S(2)}, u32[]{:S(2)}) collective-permute-start(bf16[4,2,2,192,384]{4,3,2,1,0:T(8,128)(2,1)} %get-tuple-element.429), channel_id=1, source_target_pairs={{0,8},{8,0},{16,24},{24,16},{1,9},{9,1},{17,25},{25,17},{2,10},{10... | collective-permute-start | bytes 7077896 | tf_op jit(solution)/shard_map/ppermute | solution.py:1048
  529.3 28.5 %collective-permute-start.65 = (bf16[4,2,2,192,384]{4,3,2,1,0:T(8,128)(2,1)}, bf16[4,2,2,192,384]{4,3,2,1,0:T(8,128)(2,1)S(1)}, u32[]{:S(2)}, u32[]{:S(2)}) collective-permute-start(bf16[4,2,2,192,384]{4,3,2,1,0:T(8,128)(2,1)} %get-tuple-element.443), channel_id=1, source_target_pairs={{0,8},{8,0},{16,24},{24,16},{1,9},{9,1},{17,25},{25,17},{2,10},{10... | collective-permute-start | bytes 7077896 | tf_op jit(solution)/shard_map/ppermute | solution.py:1048
  529.4 163.9 %reduce-scatter.11.cloned.1.call-start = ((), (), s32[]{:S(2)}) async-start(), calls=%async_computation.12 | async-start | bytes 1474560 | tf_op jit(solution)/shard_map/reduce_scatter | solution.py:1077
  531.1 163.6 %reduce-scatter.5.cloned.1.call-start = ((), (), s32[]{:S(2)}) async-start(), calls=%async_computation.9 | async-start | bytes 921600 | tf_op jit(solution)/shard_map/reduce_scatter | solution.py:1077
  583.5 28.5 %collective-permute-start.67 = (bf16[8,192,384]{2,1,0:T(8,128)(2,1)}, bf16[8,192,384]{2,1,0:T(8,128)(2,1)}, u32[]{:S(2)}, u32[]{:S(2)}) collective-permute-start(bf16[8,192,384]{2,1,0:T(8,128)(2,1)} %get-tuple-element.461), channel_id=1, source_target_pairs={{0,16},{8,24},{16,0},{24,8},{1,17},{9,25},{17,1},{25,9},{2,18},{10... | collective-permute-start | bytes 3538952 | tf_op jit(solution)/shard_map/ppermute | solution.py:1048
  603.3 96.9 %reduce-scatter.9.cloned.1.call-start = ((), (), s32[]{:S(2)}) async-start(), calls=%async_computation.11 | async-start | bytes 1474560 | tf_op jit(solution)/shard_map/reduce_scatter | solution.py:1077
  629.2 28.6 %collective-permute-start.76 = (bf16[8,192,384]{2,1,0:T(8,128)(2,1)}, bf16[8,192,384]{2,1,0:T(8,128)(2,1)S(1)}, u32[]{:S(2)}, u32[]{:S(2)}) collective-permute-start(bf16[8,192,384]{2,1,0:T(8,128)(2,1)} %get-tuple-element.484), channel_id=1, source_target_pairs={{0,16},{8,24},{16,0},{24,8},{1,17},{9,25},{17,1},{25,9},{2,18},{10... | collective-permute-start | bytes 3538952 | tf_op jit(solution)/shard_map/ppermute | solution.py:1048
  689.7 35.8 %all-to-all-start.2 = ((bf16[4,9,48,384]{3,2,1,0:T(8,128)(2,1)}), bf16[4,9,48,384]{3,2,1,0:T(8,128)(2,1)S(1)}, u32[]{:S(2)}, u32[]{:S(2)}) async-start(bf16[4,9,48,384]{3,2,1,0:T(8,128)(2,1)} %shard_map.222), calls=%async_computation.2 | async-start | bytes 2654208 | tf_op jit(solution)/shard_map/all_to_all | solution.py:1074
  (133 other events, 1606.4 us)
Sparse Core Ops, SparseCore 0:
  11.7 144.2 all-gather.2
  159.6 122.2 all-gather.4
  529.5 20.0 reduce-scatter.6
  551.8 33.0 reduce-scatter.10
  603.4 27.7 reduce-scatter.4
  639.3 32.7 reduce-scatter.8
